TPU v7x, 32 devices: a whole 2x2x4 slice. The times are simulated.
32 devices in a mesh: dp: 32 (over z, y, x, core).
Axes of the slice: x: 2, y: 2, z: 4, core: 2. Of those that a mesh axis runs over, the one named last changes fastest.
Arguments:
- tokens: bfloat16 [8192, 1536], P('dp'), may hold values from -6 to 6
- teacher: bfloat16 [8192, 1536], P('dp'), may hold values from -6 to 6
- valid_mask: int32 [8192], P('dp'), may hold values from 0 to 1, as said below
- w_query: bfloat16 [1536, 1536], P('dp'), may hold values from -0.15625 to 0.15625
- key_weight_matrix: bfloat16 [1536, 768], P('dp'), may hold values from -0.15625 to 0.15625
- value_weight_matrix: bfloat16 [1536, 768], P('dp'), may hold values from -0.15625 to 0.15625
- w_output: bfloat16 [1536, 1536], P('dp'), may hold values from -1.25 to 1.25
- w_gate: bfloat16 [1536, 4096], P('dp'), may hold values from -0.15625 to 0.15625
- w_up: bfloat16 [1536, 4096], P('dp'), may hold values from -0.15625 to 0.15625
- w_down: bfloat16 [4096, 1536], P('dp'), may hold values from -0.09375 to 0.09375
- attn_gain: bfloat16 [1536], P('dp'), may hold values from 0.5 to 1.5
- ffn_gain: bfloat16 [1536], P('dp'), may hold values from 0.5 to 1.5
Outputs:
- out_act: bfloat16 [8192, 1536], P('dp')
- loss: float32 [], replicated
- input_grad: bfloat16 [8192, 1536], P('dp')
- grad_w_query: float32 [1536, 1536], P('dp')
- grad_w_key: float32 [1536, 768], P('dp')
- grad_w_value: float32 [1536, 768], P('dp')
- grad_w_output: float32 [1536, 1536], P('dp')
- grad_w_gate: float32 [1536, 4096], P('dp')
- grad_w_up: float32 [1536, 4096], P('dp')
- grad_w_down: float32 [4096, 1536], P('dp')
- grad_attn_gain: float32 [1536], P('dp')
- grad_ffn_gain: float32 [1536], P('dp')
Inputs may be any that keep to these rules, and one draw needn't show every extreme that they name: The first token of every sequence (rows that are multiples of 128) has valid_mask 1.
All inputs are finite; a program needn't handle non-finite values.
Results may differ from a plain program's by a relative error of at most 0.012.
Values may be sent and summed in bfloat16 or wider, within the bound.
No kernel may reach another device: no remote copies, remote signals or barrier semaphores. Data moves between devices by JAX's collectives and lax.ppermute only.
A program may use at most 320 MiB of HBM per device.

v0:
```python
import math

import jax
import jax.numpy as jnp
from jax import lax
from jax.sharding import PartitionSpec as P

MODEL_WIDTH = 1536
QUERY_HEAD_COUNT = 16
KEY_VALUE_HEADS = 8
HEAD_SIZE = 96
SEQ = 128
MB = 2


EPSILON = 1e-05
ROPE_BASE = 100000.0
MASK_FILL = -1e30


def shortened(value):
    return jax.tree.map(lambda a: a.astype(jnp.bfloat16) if a.dtype == jnp.float32 else a, value)


def from_partner(value, axis, apart):
    mask = 2**apart
    pairs = [(source, source ^ mask) for source in range(lax.axis_size(axis))]
    return lax.ppermute(value, axis, pairs)


def rotation_tables(length, width):
    half_width = width // 2
    position = jnp.arange(length, dtype=jnp.float32)[:, None]
    freq_rate = ROPE_BASE ** (-2.0 * jnp.arange(half_width, dtype=jnp.float32) / width)
    angle_table = position * freq_rate[None, :]
    return (jnp.cos(angle_table)[:, None, :], jnp.sin(angle_table)[:, None, :])


def apply_rotary(heads_in, cosine_lookup, sine_lookup):
    half_width = heads_in.shape[-1] // 2
    left_part = heads_in[..., :half_width]
    right_part = heads_in[..., half_width:]
    return jnp.concatenate(
        [
            left_part * cosine_lookup - right_part * sine_lookup,
            right_part * cosine_lookup + left_part * sine_lookup,
        ],
        axis=-1,
    )


def unturn(heads_in, cosine_lookup, sine_lookup):
    half_width = heads_in.shape[-1] // 2
    left_part = heads_in[..., :half_width]
    right_part = heads_in[..., half_width:]
    return jnp.concatenate(
        [
            left_part * cosine_lookup + right_part * sine_lookup,
            right_part * cosine_lookup - left_part * sine_lookup,
        ],
        axis=-1,
    )


def norm_rows(field_in, gain_vec):
    inv_scale = lax.rsqrt(jnp.mean(field_in * field_in, axis=-1, keepdims=True) + EPSILON)
    return (field_in * inv_scale * gain_vec, inv_scale)


def norm_back(upstream, field_in, inv_scale, gain_vec):
    gain_grad = jnp.sum(upstream * field_in * inv_scale, axis=0)
    scaled_up = upstream * gain_vec
    field_grad = inv_scale * scaled_up - field_in * inv_scale**3 * jnp.mean(
        scaled_up * field_in, axis=-1, keepdims=True
    )
    return (gain_grad, field_grad)


def attend_scores(query_head_rows, key_head_rows):
    total_row_count = query_head_rows.shape[0]
    score_scale = 1.0 / math.sqrt(HEAD_SIZE)
    raw_scores = (
        jnp.einsum(
            "qhrd,khd->hrqk", query_head_rows, key_head_rows, preferred_element_type=jnp.float32
        )
        * score_scale
    )
    causal = jnp.arange(total_row_count)[:, None] >= jnp.arange(total_row_count)[None, :]
    return jnp.where(causal, raw_scores, MASK_FILL)


def forward_pass(inputs_f, weight_set, cosine_lookup, sine_lookup):
    (
        w_query,
        key_weight_matrix,
        value_weight_matrix,
        w_output,
        w_gate,
        w_up,
        w_down,
        attn_gain,
        ffn_gain,
    ) = weight_set
    total_row_count = inputs_f.shape[0]
    head_groups = QUERY_HEAD_COUNT // KEY_VALUE_HEADS
    normed, inv_attn = norm_rows(inputs_f, attn_gain.astype(jnp.float32))
    normed_in = normed.astype(jnp.bfloat16)
    query_raw = jnp.dot(normed_in, w_query, preferred_element_type=jnp.float32)
    unrotated_keys = jnp.dot(normed_in, key_weight_matrix, preferred_element_type=jnp.float32)
    value_rows = jnp.dot(normed_in, value_weight_matrix, preferred_element_type=jnp.float32).astype(
        jnp.bfloat16
    )
    value_rows = value_rows.reshape(total_row_count, KEY_VALUE_HEADS, HEAD_SIZE)
    query_head_rows = apply_rotary(
        query_raw.reshape(total_row_count, QUERY_HEAD_COUNT, HEAD_SIZE), cosine_lookup, sine_lookup
    ).astype(jnp.bfloat16)
    query_head_rows = query_head_rows.reshape(
        total_row_count, KEY_VALUE_HEADS, head_groups, HEAD_SIZE
    )
    key_head_rows = apply_rotary(
        unrotated_keys.reshape(total_row_count, KEY_VALUE_HEADS, HEAD_SIZE),
        cosine_lookup,
        sine_lookup,
    ).astype(jnp.bfloat16)
    scores = attend_scores(query_head_rows, key_head_rows)
    row_max = jnp.max(scores, axis=-1, keepdims=True)
    log_total = row_max + jnp.log(jnp.sum(jnp.exp(scores - row_max), axis=-1, keepdims=True))
    attn_probs = jnp.exp(scores - log_total)
    mixed_heads = jnp.einsum(
        "hrqk,khd->qhrd",
        attn_probs.astype(jnp.bfloat16),
        value_rows,
        preferred_element_type=jnp.float32,
    )
    mixed_heads = mixed_heads.reshape(total_row_count, MODEL_WIDTH).astype(jnp.bfloat16)
    hidden_res = inputs_f + jnp.dot(mixed_heads, w_output, preferred_element_type=jnp.float32)
    normed_two, inv_ffn = norm_rows(hidden_res, ffn_gain.astype(jnp.float32))
    normed_mid = normed_two.astype(jnp.bfloat16)
    gate_pre = jnp.dot(normed_mid, w_gate, preferred_element_type=jnp.float32)
    up_pre = jnp.dot(normed_mid, w_up, preferred_element_type=jnp.float32)
    hidden_act = (jax.nn.silu(gate_pre) * up_pre).astype(jnp.bfloat16)
    result = hidden_res + jnp.dot(hidden_act, w_down, preferred_element_type=jnp.float32)
    saved_state = (
        inputs_f,
        inv_attn,
        normed_in,
        query_head_rows,
        key_head_rows,
        value_rows,
        log_total,
        mixed_heads,
        hidden_res,
        inv_ffn,
        normed_mid,
        gate_pre,
        up_pre,
        hidden_act,
    )
    return (result, saved_state)


def backward_pass(grad_out, saved_state, weight_set, cosine_lookup, sine_lookup):
    (
        w_query,
        key_weight_matrix,
        value_weight_matrix,
        w_output,
        w_gate,
        w_up,
        w_down,
        attn_gain,
        ffn_gain,
    ) = weight_set
    (
        inputs_f,
        inv_attn,
        normed_in,
        query_head_rows,
        key_head_rows,
        value_rows,
        log_total,
        mixed_heads,
        hidden_res,
        inv_ffn,
        normed_mid,
        gate_pre,
        up_pre,
        hidden_act,
    ) = saved_state
    total_row_count = inputs_f.shape[0]
    head_groups = QUERY_HEAD_COUNT // KEY_VALUE_HEADS
    score_scale = 1.0 / math.sqrt(HEAD_SIZE)
    grad_low = grad_out.astype(jnp.bfloat16)
    grad_down = jnp.einsum("sf,sd->fd", hidden_act, grad_low, preferred_element_type=jnp.float32)
    grad_hidden = jnp.einsum("sd,fd->sf", grad_low, w_down, preferred_element_type=jnp.float32)
    gate_sigmoid = jax.nn.sigmoid(gate_pre)
    grad_gate_in = (
        grad_hidden * up_pre * gate_sigmoid * (1.0 + gate_pre * (1.0 - gate_sigmoid))
    ).astype(jnp.bfloat16)
    grad_up_in = (grad_hidden * gate_pre * gate_sigmoid).astype(jnp.bfloat16)
    grad_gate = jnp.einsum(
        "sd,sf->df", normed_mid, grad_gate_in, preferred_element_type=jnp.float32
    )
    grad_up = jnp.einsum("sd,sf->df", normed_mid, grad_up_in, preferred_element_type=jnp.float32)
    grad_mid = jnp.einsum(
        "sf,df->sd", grad_gate_in, w_gate, preferred_element_type=jnp.float32
    ) + jnp.einsum("sf,df->sd", grad_up_in, w_up, preferred_element_type=jnp.float32)
    grad_ffn, grad_res = norm_back(grad_mid, hidden_res, inv_ffn, ffn_gain.astype(jnp.float32))
    grad_res = grad_out + grad_res
    res_low = grad_res.astype(jnp.bfloat16)
    grad_output = jnp.einsum("sd,se->de", mixed_heads, res_low, preferred_element_type=jnp.float32)
    gradient_mixed_heads = jnp.einsum(
        "se,de->sd", res_low, w_output, preferred_element_type=jnp.float32
    )
    gradient_mixed_heads = gradient_mixed_heads.astype(jnp.bfloat16).reshape(
        total_row_count, KEY_VALUE_HEADS, head_groups, HEAD_SIZE
    )
    scores = attend_scores(query_head_rows, key_head_rows)
    attn_probs = jnp.exp(scores - log_total)
    grad_probs = jnp.einsum(
        "qhrd,khd->hrqk", gradient_mixed_heads, value_rows, preferred_element_type=jnp.float32
    )
    grad_scores = attn_probs * (
        grad_probs - jnp.sum(attn_probs * grad_probs, axis=-1, keepdims=True)
    )
    grad_scores = grad_scores.astype(jnp.bfloat16)
    grad_query = (
        jnp.einsum("hrqk,khd->qhrd", grad_scores, key_head_rows, preferred_element_type=jnp.float32)
        * score_scale
    )
    grad_keys = (
        jnp.einsum(
            "hrqk,qhrd->khd", grad_scores, query_head_rows, preferred_element_type=jnp.float32
        )
        * score_scale
    )
    value_gradient = jnp.einsum(
        "hrqk,qhrd->khd",
        attn_probs.astype(jnp.bfloat16),
        gradient_mixed_heads,
        preferred_element_type=jnp.float32,
    )
    query_back = unturn(
        grad_query.reshape(total_row_count, QUERY_HEAD_COUNT, HEAD_SIZE), cosine_lookup, sine_lookup
    )
    query_back = query_back.reshape(total_row_count, MODEL_WIDTH).astype(jnp.bfloat16)
    key_back = (
        unturn(grad_keys, cosine_lookup, sine_lookup)
        .reshape(total_row_count, KEY_VALUE_HEADS * HEAD_SIZE)
        .astype(jnp.bfloat16)
    )
    value_pullback = value_gradient.reshape(total_row_count, KEY_VALUE_HEADS * HEAD_SIZE).astype(
        jnp.bfloat16
    )
    grad_query_w = jnp.einsum(
        "sd,se->de", normed_in, query_back, preferred_element_type=jnp.float32
    )
    grad_key_w = jnp.einsum("sd,se->de", normed_in, key_back, preferred_element_type=jnp.float32)
    grad_value_w = jnp.einsum(
        "sd,se->de", normed_in, value_pullback, preferred_element_type=jnp.float32
    )
    grad_in_norm = (
        jnp.einsum("se,de->sd", query_back, w_query, preferred_element_type=jnp.float32)
        + jnp.einsum("se,de->sd", key_back, key_weight_matrix, preferred_element_type=jnp.float32)
        + jnp.einsum(
            "se,de->sd", value_pullback, value_weight_matrix, preferred_element_type=jnp.float32
        )
    )
    grad_attn, grad_input = norm_back(
        grad_in_norm, inputs_f, inv_attn, attn_gain.astype(jnp.float32)
    )
    grad_terms = (
        grad_query_w,
        grad_key_w,
        grad_value_w,
        grad_output,
        grad_gate,
        grad_up,
        grad_down,
        grad_attn,
        grad_ffn,
    )
    return (grad_res + grad_input, grad_terms)


def halving_sum(partial_terms):
    position = lax.axis_index("dp")
    levels = lax.axis_size("dp").bit_length() - 1
    current = partial_terms
    for bit_number in reversed(range(levels)):
        upper_flag = position // 2**bit_number % 2 == 1
        kept_list = []
        sent_list = []
        for term_rows in current:
            half_rows = term_rows.shape[0] // 2
            lower_rows = term_rows[:half_rows]
            higher_rows = term_rows[half_rows:]
            kept_list.append(jnp.where(upper_flag, higher_rows, lower_rows))
            sent_list.append(jnp.where(upper_flag, lower_rows, higher_rows))
        received = from_partner(
            (
                shortened(sent_list[0]),
                shortened(sent_list[1]),
                shortened(sent_list[2]),
                shortened(sent_list[3]),
                shortened(sent_list[4]),
                shortened(sent_list[5]),
                shortened(sent_list[6]),
                shortened(sent_list[7]),
                shortened(sent_list[8]),
            ),
            "dp",
            bit_number,
        )
        current = tuple(
            (kept_part + came_part for kept_part, came_part in zip(kept_list, received))
        )
    return current


def body(
    tokens,
    teacher,
    valid_mask,
    w_query,
    key_weight_matrix,
    value_weight_matrix,
    w_output,
    w_gate,
    w_up,
    w_down,
    attn_gain,
    ffn_gain,
):
    shards = (
        w_query,
        key_weight_matrix,
        value_weight_matrix,
        w_output,
        w_gate,
        w_up,
        w_down,
        attn_gain,
        ffn_gain,
    )
    devices = lax.axis_size("dp")
    cosine_lookup, sine_lookup = rotation_tables(SEQ, HEAD_SIZE)
    summed = tuple(
        (
            jnp.zeros((shard_piece.shape[0] * devices,) + shard_piece.shape[1:], jnp.float32)
            for shard_piece in shards
        )
    )
    outputs = []
    input_parts = []
    loss_total = jnp.zeros((), jnp.float32)
    for batch_index in range(MB):
        first_row = batch_index * SEQ
        inputs_f = tokens[first_row : first_row + SEQ].astype(jnp.float32)
        forward_set = (
            lax.all_gather(w_query, "dp", axis=0, tiled=True),
            lax.all_gather(key_weight_matrix, "dp", axis=0, tiled=True),
            lax.all_gather(value_weight_matrix, "dp", axis=0, tiled=True),
            lax.all_gather(w_output, "dp", axis=0, tiled=True),
            lax.all_gather(w_gate, "dp", axis=0, tiled=True),
            lax.all_gather(w_up, "dp", axis=0, tiled=True),
            lax.all_gather(w_down, "dp", axis=0, tiled=True),
            lax.all_gather(attn_gain, "dp", axis=0, tiled=True),
            lax.all_gather(ffn_gain, "dp", axis=0, tiled=True),
        )
        result, saved_state = forward_pass(inputs_f, forward_set, cosine_lookup, sine_lookup)
        outputs.append(result.astype(jnp.bfloat16))
        target_f = teacher[first_row : first_row + SEQ].astype(jnp.float32)
        mask_f = valid_mask[first_row : first_row + SEQ].astype(jnp.float32)
        grad_out = (result - target_f) * mask_f[:, None]
        loss_total = loss_total + jnp.sum(grad_out * grad_out)
        backward_set = (
            lax.all_gather(w_query, "dp", axis=0, tiled=True),
            lax.all_gather(key_weight_matrix, "dp", axis=0, tiled=True),
            lax.all_gather(value_weight_matrix, "dp", axis=0, tiled=True),
            lax.all_gather(w_output, "dp", axis=0, tiled=True),
            lax.all_gather(w_gate, "dp", axis=0, tiled=True),
            lax.all_gather(w_up, "dp", axis=0, tiled=True),
            lax.all_gather(w_down, "dp", axis=0, tiled=True),
            lax.all_gather(attn_gain, "dp", axis=0, tiled=True),
            lax.all_gather(ffn_gain, "dp", axis=0, tiled=True),
        )
        grad_input, grad_terms = backward_pass(
            grad_out, saved_state, backward_set, cosine_lookup, sine_lookup
        )
        input_parts.append(grad_input.astype(jnp.bfloat16))
        summed = tuple((acc_part + new_part for acc_part, new_part in zip(summed, grad_terms)))
    summed = halving_sum(summed)
    valid_count = jnp.sum(valid_mask).astype(jnp.float32)
    loss_sum, count_sum = lax.psum((loss_total, valid_count), "dp")
    loss = loss_sum / (count_sum * MODEL_WIDTH)
    return (
        jnp.concatenate(outputs, axis=0),
        loss,
        jnp.concatenate(input_parts, axis=0),
        summed[0],
        summed[1],
        summed[2],
        summed[3],
        summed[4],
        summed[5],
        summed[6],
        summed[7],
        summed[8],
    )


def solution(mesh):
    in_specs = (
        P("dp", None),
        P("dp", None),
        P("dp"),
        P("dp", None),
        P("dp", None),
        P("dp", None),
        P("dp", None),
        P("dp", None),
        P("dp", None),
        P("dp", None),
        P("dp"),
        P("dp"),
    )
    out_specs = (
        P("dp", None),
        P(),
        P("dp", None),
        P("dp", None),
        P("dp", None),
        P("dp", None),
        P("dp", None),
        P("dp", None),
        P("dp", None),
        P("dp", None),
        P("dp"),
        P("dp"),
    )
    return jax.shard_map(body, mesh=mesh, in_specs=in_specs, out_specs=out_specs, check_vma=False)
```

profile of v0, /device:TPU:0, one launch (start us, length us, event | category | flops | bytes accessed | tf_op | source)
XLA Modules:
  0.0 2158.9 jit_solution(6979843510940930265)
XLA Ops:
  13.7 42.1 %all-reduce.3 = (bf16[1536]{0:T(1024)(128)(2,1)S(1)}, bf16[1536]{0:T(1024)(128)(2,1)S(1)}) all-reduce(bf16[1536]{0:T(1024)(128)(2,1)S(1)} %dynamic-update-slice, bf16[1536]{0:T(1024)(128)(2,1)S(1)} %dynamic-update-slice.1), channel_id=1, replica_groups=mesh['dp'=32] {'dp'}, use_global_device_ids=true, to_apply=%add | all-reduce | flops 3072 | bytes 12288
  61.2 9.7 all-gather.8.cloned.1.call-done
  77.5 52.5 %all-gather.10.cloned.1.call-done = bf16[1536,768]{1,0:T(8,128)(2,1)} async-done(((bf16[48,768]{1,0:T(8,128)(2,1)}), bf16[1536,768]{1,0:T(8,128)(2,1)}) %all-gather.10.cloned.1.call-update) | async-done | bytes 2359312 | tf_op jit(solution)/shard_map/all_gather | solution.py:362
  134.2 61.3 %all-gather.12.cloned.1.call-done = bf16[1536,1536]{1,0:T(8,128)(2,1)} async-done(((bf16[48,1536]{1,0:T(8,128)(2,1)}), bf16[1536,1536]{1,0:T(8,128)(2,1)}) %all-gather.12.cloned.1.call-update) | async-done | bytes 4718608 | tf_op jit(solution)/shard_map/all_gather | solution.py:361
  195.5 4.5 fusion.78
  205.3 55.5 %all-gather.14.cloned.1.call-done = bf16[1536,1536]{1,0:T(8,128)(2,1)} async-done(((bf16[48,1536]{1,0:T(8,128)(2,1)}), bf16[1536,1536]{1,0:T(8,128)(2,1)}) %all-gather.14.cloned.1.call-update) | async-done | bytes 4718608 | tf_op jit(solution)/shard_map/all_gather | solution.py:364
  267.5 90.8 %all-gather.16.cloned.1.call-done = bf16[1536,4096]{1,0:T(8,128)(2,1)} async-done(((bf16[48,4096]{1,0:T(8,128)(2,1)}), bf16[1536,4096]{1,0:T(8,128)(2,1)}) %all-gather.16.cloned.1.call-update) | async-done | bytes 12582928 | tf_op jit(solution)/shard_map/all_gather | solution.py:365
  358.3 8.1 fusion.85
  366.4 88.8 %all-gather.18.cloned.1.call-done = bf16[1536,4096]{1,0:T(8,128)(2,1)} async-done(((bf16[48,4096]{1,0:T(8,128)(2,1)}), bf16[1536,4096]{1,0:T(8,128)(2,1)}) %all-gather.18.cloned.1.call-update) | async-done | bytes 12582928 | tf_op jit(solution)/shard_map/all_gather | solution.py:366
  455.3 8.6 multiply_convert_fusion.5
  463.9 88.5 %all-gather.20.cloned.1.call-done = bf16[4096,1536]{1,0:T(8,128)(2,1)} async-done(((bf16[128,1536]{1,0:T(8,128)(2,1)}), bf16[4096,1536]{1,0:T(8,128)(2,1)}) %all-gather.20.cloned.1.call-update) | async-done | bytes 12582928 | tf_op jit(solution)/shard_map/all_gather | solution.py:367
  552.4 6.5 convolution_add_fusion.16
  558.9 11.4 multiply_convert_fusion.2
  570.3 10.1 fusion.87
  580.4 11.6 multiply_reduce_fusion.3
  595.1 9.7 multiply_convert_fusion.4
  606.9 9.6 multiply_convert_fusion
  616.6 10.0 fusion.89
  626.7 9.7 multiply_reduce_fusion.2
  650.9 5.0 fusion.37
  656.0 10.3 fusion.91
  666.3 10.1 fusion.92
  676.4 10.6 fusion.40
  725.6 3.7 copy-done.5
  732.5 16.4 convolution_add_fusion.2
  748.9 11.7 select_convert_fusion.2
  760.7 16.3 convolution_add_fusion.1
  777.0 11.8 select_convert_fusion.1
  788.8 16.8 convolution_add_fusion
  805.7 11.9 select_convert_fusion
  823.9 211.0 %all-reduce.2 = (f32[]{:T(128)}, f32[]{:T(128)}) all-reduce(f32[]{:T(128)S(6)} %add.347, f32[]{:T(128)S(6)} %convert_element_type.467), channel_id=1, replica_groups=mesh['dp'=32] {'dp'}, use_global_device_ids=true, to_apply=%region_10.11 | all-reduce | flops 2 | bytes 16 | tf_op jit(solution)/shard_map/psum | solution.py:395
  1037.1 3.7 collective-permute-done.40
  1040.8 3.5 collective-permute-done.36
  1044.4 3.5 collective-permute-done.41
  1073.3 139.9 %collective-permute-done.6 = bf16[384,768]{1,0:T(8,128)(2,1)S(1)} collective-permute-done((bf16[384,768]{1,0:T(8,128)(2,1)S(1)}, bf16[384,768]{1,0:T(8,128)(2,1)S(1)}, u32[]{:S(2)}, u32[]{:S(2)}) %collective-permute-start.6) | collective-permute-done | bytes 589856 | tf_op jit(solution)/shard_map/ppermute | solution.py:28
  1216.0 9.9 collective-permute-done.11
  1228.2 5.6 collective-permute-done.7
  1235.6 5.2 collective-permute-done.12
  1242.2 4.6 collective-permute-done.8
  1248.4 3.5 collective-permute-done.13
  1262.8 5.4 convert_add_fusion.6
  1273.6 247.3 %collective-permute-done.1 = bf16[384,1536]{1,0:T(8,128)(2,1)} collective-permute-done((bf16[384,1536]{1,0:T(8,128)(2,1)}, bf16[384,1536]{1,0:T(8,128)(2,1)}, u32[]{:S(2)}, u32[]{:S(2)}) %collective-permute-start.1) | collective-permute-done | bytes 1179680 | tf_op jit(solution)/shard_map/ppermute | solution.py:28
  1526.5 18.9 collective-permute-done.16
  1550.0 11.0 collective-permute-done.17
  1563.2 6.0 collective-permute-done.18
  1571.5 35.2 %collective-permute-done.20 = bf16[768,4096]{1,0:T(8,128)(2,1)} collective-permute-done((bf16[768,4096]{1,0:T(8,128)(2,1)}, bf16[768,4096]{1,0:T(8,128)(2,1)}, u32[]{:S(2)}, u32[]{:S(2)}) %collective-permute-start.20) | collective-permute-done | bytes 6291488 | tf_op jit(solution)/shard_map/ppermute | solution.py:28
  1606.7 9.4 convert_add_fusion.2
  1616.1 6.9 select_convert_fusion.5
  1623.0 118.6 %collective-permute-done.25 = bf16[768,4096]{1,0:T(8,128)(2,1)} collective-permute-done((bf16[768,4096]{1,0:T(8,128)(2,1)}, bf16[768,4096]{1,0:T(8,128)(2,1)}, u32[]{:S(2)}, u32[]{:S(2)}) %collective-permute-start.25) | collective-permute-done | bytes 6291488 | tf_op jit(solution)/shard_map/ppermute | solution.py:28
  1741.6 11.2 convert_add_fusion.1
  1758.3 118.1 %collective-permute-done.30 = bf16[2048,1536]{1,0:T(8,128)(2,1)} collective-permute-done((bf16[2048,1536]{1,0:T(8,128)(2,1)}, bf16[2048,1536]{1,0:T(8,128)(2,1)}, u32[]{:S(2)}, u32[]{:S(2)}) %collective-permute-start.30) | collective-permute-done | bytes 6291488 | tf_op jit(solution)/shard_map/ppermute | solution.py:28
  1876.4 11.7 convert_add_fusion
  1890.2 53.5 %collective-permute-done.21 = bf16[384,4096]{1,0:T(8,128)(2,1)} collective-permute-done((bf16[384,4096]{1,0:T(8,128)(2,1)}, bf16[384,4096]{1,0:T(8,128)(2,1)}, u32[]{:S(2)}, u32[]{:S(2)}) %collective-permute-start.21) | collective-permute-done | bytes 3145760 | tf_op jit(solution)/shard_map/ppermute | solution.py:28
  1943.8 10.3 convert_add_fusion.5
  1954.0 4.3 select_convert_fusion.10
  1960.3 50.9 %collective-permute-done.26 = bf16[384,4096]{1,0:T(8,128)(2,1)} collective-permute-done((bf16[384,4096]{1,0:T(8,128)(2,1)}, bf16[384,4096]{1,0:T(8,128)(2,1)}, u32[]{:S(2)}, u32[]{:S(2)}) %collective-permute-start.26) | collective-permute-done | bytes 3145760 | tf_op jit(solution)/shard_map/ppermute | solution.py:28
  2011.2 10.3 convert_add_fusion.4
  2021.4 4.3 select_convert_fusion.9
  2027.8 50.7 %collective-permute-done.31 = bf16[1024,1536]{1,0:T(8,128)(2,1)} collective-permute-done((bf16[1024,1536]{1,0:T(8,128)(2,1)}, bf16[1024,1536]{1,0:T(8,128)(2,1)}, u32[]{:S(2)}, u32[]{:S(2)}) %collective-permute-start.31) | collective-permute-done | bytes 3145760 | tf_op jit(solution)/shard_map/ppermute | solution.py:28
  2078.5 6.3 convert_add_fusion.3
  2090.1 3.9 convert_add_fusion.10
  2099.2 25.5 %collective-permute-done.32 = bf16[512,1536]{1,0:T(8,128)(2,1)S(1)} collective-permute-done((bf16[512,1536]{1,0:T(8,128)(2,1)S(1)}, bf16[512,1536]{1,0:T(8,128)(2,1)S(1)}, u32[]{:S(2)}, u32[]{:S(2)}) %collective-permute-start.32) | collective-permute-done | bytes 1572896 | tf_op jit(solution)/shard_map/ppermute | solution.py:28
  2127.7 3.9 collective-permute-done.28
  2132.0 15.2 collective-permute-done.33
  (508 shorter events, 195.1 us)
Async XLA Ops:
  7.2 63.8 %all-gather.8.cloned.1.call-start = ((), (), s32[]{:S(2)}) async-start(), calls=%async_computation | async-start | bytes 2433024 | tf_op jit(solution)/shard_map/all_gather | solution.py:363
  7.9 122.1 %all-gather.10.cloned.1.call-start = ((), (), s32[]{:S(2)}) async-start(), calls=%async_computation.1 | async-start | bytes 2433024 | tf_op jit(solution)/shard_map/all_gather | solution.py:362
  8.7 186.9 %all-gather.12.cloned.1.call-start = ((), (), s32[]{:S(2)}) async-start(), calls=%async_computation.2 | async-start | bytes 4866048 | tf_op jit(solution)/shard_map/all_gather | solution.py:361
  9.4 251.4 %all-gather.14.cloned.1.call-start = ((), (), s32[]{:S(2)}) async-start(), calls=%async_computation.3 | async-start | bytes 4866048 | tf_op jit(solution)/shard_map/all_gather | solution.py:364
  10.0 348.3 %all-gather.16.cloned.1.call-start = ((), (), s32[]{:S(2)}) async-start(), calls=%async_computation.4 | async-start | bytes 12976128 | tf_op jit(solution)/shard_map/all_gather | solution.py:365
  10.6 444.7 %all-gather.18.cloned.1.call-start = ((), (), s32[]{:S(2)}) async-start(), calls=%async_computation.5 | async-start | bytes 12976128 | tf_op jit(solution)/shard_map/all_gather | solution.py:366
  11.1 541.2 %all-gather.20.cloned.1.call-start = ((), (), s32[]{:S(2)}) async-start(), calls=%async_computation.6 | async-start | bytes 12976128 | tf_op jit(solution)/shard_map/all_gather | solution.py:367
  57.9 144.4 %copy-start.84 = (pred[128,128]{0,1:T(8,128)(4,1)}, pred[128,128]{0,1:T(8,128)(4,1)S(1)}, u32[]{:S(2)}) copy-start(pred[128,128]{0,1:T(8,128)(4,1)S(1)} %iota_compare_fusion) | copy-start | bytes 49156
  75.2 189.6 %copy-start.59 = (bf16[128,768]{0,1:T(8,128)(2,1)}, bf16[128,768]{0,1:T(8,128)(2,1)S(1)}, u32[]{:S(2)}) copy-start(bf16[128,768]{0,1:T(8,128)(2,1)S(1)} %copy.57) | copy-start | bytes 589828
  77.5 126.7 %copy-start.61 = (bf16[128,768]{0,1:T(8,128)(2,1)}, bf16[128,768]{0,1:T(8,128)(2,1)S(1)}, u32[]{:S(2)}) copy-start(bf16[128,768]{0,1:T(8,128)(2,1)S(1)} %copy.53) | copy-start | bytes 589828
  264.2 288.2 %copy-start.17 = (f32[128,1536]{1,0:T(8,128)}, f32[128,1536]{1,0:T(8,128)S(1)}, u32[]{:S(2)}) copy-start(f32[128,1536]{1,0:T(8,128)S(1)} %get-tuple-element.82) | copy-start | bytes 2359300
  267.5 187.8 %copy-start.28 = (bf16[128,1536]{1,0:T(8,128)(2,1)}, bf16[128,1536]{1,0:T(8,128)(2,1)S(1)}, u32[]{:S(2)}) copy-start(bf16[128,1536]{1,0:T(8,128)(2,1)S(1)} %multiply_convert_fusion.9) | copy-start | bytes 1179652
  708.1 548.8 %collective-permute-start = (bf16[768,1536]{1,0:T(8,128)(2,1)}, bf16[768,1536]{1,0:T(8,128)(2,1)}, u32[]{:S(2)}, u32[]{:S(2)}) collective-permute-start(bf16[768,1536]{1,0:T(8,128)(2,1)} %select_convert_fusion.7), channel_id=1, source_target_pairs={{0,16},{1,17},{2,18},{3,19},{4,20},{5,21},{6,22},{7,23},{8,24},{9,... | collective-permute-start | bytes 7077896 | tf_op jit(solution)/shard_map/ppermute | solution.py:28
  716.4 348.6 %collective-permute-start.5 = (bf16[768,768]{1,0:T(8,128)(2,1)}, bf16[768,768]{1,0:T(8,128)(2,1)}, u32[]{:S(2)}, u32[]{:S(2)}) collective-permute-start(bf16[768,768]{1,0:T(8,128)(2,1)} %select_convert_fusion.13), channel_id=1, source_target_pairs={{0,16},{1,17},{2,18},{3,19},{4,20},{5,21},{6,22},{7,23},{8,24},{9,... | collective-permute-start | bytes 3538952 | tf_op jit(solution)/shard_map/ppermute | solution.py:28
  722.6 346.0 %collective-permute-start.10 = (bf16[768,768]{1,0:T(8,128)(2,1)}, bf16[768,768]{1,0:T(8,128)(2,1)}, u32[]{:S(2)}, u32[]{:S(2)}) collective-permute-start(bf16[768,768]{1,0:T(8,128)(2,1)} %select_convert_fusion.12), channel_id=1, source_target_pairs={{0,16},{1,17},{2,18},{3,19},{4,20},{5,21},{6,22},{7,23},{8,24},{9,... | collective-permute-start | bytes 3538952 | tf_op jit(solution)/shard_map/ppermute | solution.py:28
  731.1 530.5 %collective-permute-start.15 = (bf16[768,1536]{1,0:T(8,128)(2,1)}, bf16[768,1536]{1,0:T(8,128)(2,1)}, u32[]{:S(2)}, u32[]{:S(2)}) collective-permute-start(bf16[768,1536]{1,0:T(8,128)(2,1)} %select_convert_fusion.6), channel_id=1, source_target_pairs={{0,16},{1,17},{2,18},{3,19},{4,20},{5,21},{6,22},{7,23},{8,24},{9,... | collective-permute-start | bytes 7077896 | tf_op jit(solution)/shard_map/ppermute | solution.py:28
  817.6 218.6 %collective-permute-start.35 = (bf16[768]{0:T(1024)(128)(2,1)S(1)}, bf16[768]{0:T(1024)(128)(2,1)S(1)}, u32[]{:S(2)}, u32[]{:S(2)}) collective-permute-start(bf16[768]{0:T(1024)(128)(2,1)S(1)} %select_convert_fusion.36), channel_id=1, source_target_pairs={{0,16},{1,17},{2,18},{3,19},{4,20},{5,21},{6,22},{7,23},{8,24},{9,... | collective-permute-start | bytes 4616 | tf_op jit(solution)/shard_map/ppermute | solution.py:28
  1036.2 4.5 collective-permute-start.40
  1040.8 3.6 collective-permute-start.36
  1044.3 3.6 collective-permute-start.41
  1047.9 4.0 collective-permute-start.37
  1051.9 3.5 collective-permute-start.42
  1055.4 3.5 collective-permute-start.38
  1059.0 3.5 collective-permute-start.43
  1062.5 1.1 collective-permute-start.39
  1063.6 543.1 %collective-permute-start.20 = (bf16[768,4096]{1,0:T(8,128)(2,1)}, bf16[768,4096]{1,0:T(8,128)(2,1)}, u32[]{:S(2)}, u32[]{:S(2)}) collective-permute-start(bf16[768,4096]{1,0:T(8,128)(2,1)} %select_convert_fusion.2), channel_id=1, source_target_pairs={{0,16},{1,17},{2,18},{3,19},{4,20},{5,21},{6,22},{7,23},{8,24},{9,... | collective-permute-start | bytes 18874376 | tf_op jit(solution)/shard_map/ppermute | solution.py:28
  1065.1 7.6 collective-permute-start.44
  1068.6 144.6 %collective-permute-start.6 = (bf16[384,768]{1,0:T(8,128)(2,1)S(1)}, bf16[384,768]{1,0:T(8,128)(2,1)S(1)}, u32[]{:S(2)}, u32[]{:S(2)}) collective-permute-start(bf16[384,768]{1,0:T(8,128)(2,1)S(1)} %select_convert_fusion.20), channel_id=1, source_target_pairs={{0,8},{1,9},{2,10},{3,11},{4,12},{5,13},{6,14},{7,15},{8,0},{9,1},... | collective-permute-start | bytes 1769480 | tf_op jit(solution)/shard_map/ppermute | solution.py:28
  1070.7 186.2 %slice-start.21 = ((s8[9437184]{0:T(1024)(128)(4,1)}), s8[4194304]{0:T(1024)(128)(4,1)S(1)}, s32[]{:S(2)}) async-start(s8[9437184]{0:T(1024)(128)(4,1)} %bitcast.194), calls=%async_computation.28 | async-start | bytes 8388608
  1072.5 184.4 %slice-start.22 = ((s8[9437184]{0:T(1024)(128)(4,1)}), s8[4194304]{0:T(1024)(128)(4,1)S(1)}, s32[]{:S(2)}) async-start(s8[9437184]{0:T(1024)(128)(4,1)} %bitcast.194), calls=%async_computation.29 | async-start | bytes 8388608
  1072.7 153.2 %collective-permute-start.11 = (bf16[384,768]{1,0:T(8,128)(2,1)S(1)}, bf16[384,768]{1,0:T(8,128)(2,1)S(1)}, u32[]{:S(2)}, u32[]{:S(2)}) collective-permute-start(bf16[384,768]{1,0:T(8,128)(2,1)S(1)} %select_convert_fusion.19), channel_id=1, source_target_pairs={{0,8},{1,9},{2,10},{3,11},{4,12},{5,13},{6,14},{7,15},{8,0},{9,1},... | collective-permute-start | bytes 1769480 | tf_op jit(solution)/shard_map/ppermute | solution.py:28
  1213.3 528.4 %collective-permute-start.25 = (bf16[768,4096]{1,0:T(8,128)(2,1)}, bf16[768,4096]{1,0:T(8,128)(2,1)}, u32[]{:S(2)}, u32[]{:S(2)}) collective-permute-start(bf16[768,4096]{1,0:T(8,128)(2,1)} %select_convert_fusion.1), channel_id=1, source_target_pairs={{0,16},{1,17},{2,18},{3,19},{4,20},{5,21},{6,22},{7,23},{8,24},{9,... | collective-permute-start | bytes 18874376 | tf_op jit(solution)/shard_map/ppermute | solution.py:28
  1225.9 7.9 collective-permute-start.7
  1233.8 7.0 collective-permute-start.12
  1240.8 6.0 collective-permute-start.8
  1246.8 5.1 collective-permute-start.13
  1252.0 1.3 collective-permute-start.9
  1253.2 623.1 %collective-permute-start.30 = (bf16[2048,1536]{1,0:T(8,128)(2,1)}, bf16[2048,1536]{1,0:T(8,128)(2,1)}, u32[]{:S(2)}, u32[]{:S(2)}) collective-permute-start(bf16[2048,1536]{1,0:T(8,128)(2,1)} %select_convert_fusion), channel_id=1, source_target_pairs={{0,16},{1,17},{2,18},{3,19},{4,20},{5,21},{6,22},{7,23},{8,24},{9,... | collective-permute-start | bytes 18874376 | tf_op jit(solution)/shard_map/ppermute | solution.py:28
  1256.9 14.0 collective-permute-start.14
  1262.7 258.2 %collective-permute-start.1 = (bf16[384,1536]{1,0:T(8,128)(2,1)}, bf16[384,1536]{1,0:T(8,128)(2,1)}, u32[]{:S(2)}, u32[]{:S(2)}) collective-permute-start(bf16[384,1536]{1,0:T(8,128)(2,1)} %select_convert_fusion.14), channel_id=1, source_target_pairs={{0,8},{1,9},{2,10},{3,11},{4,12},{5,13},{6,14},{7,15},{8,0},{9,1},... | collective-permute-start | bytes 3538952 | tf_op jit(solution)/shard_map/ppermute | solution.py:28
  1262.8 343.9 %slice-start.3 = ((s8[25165824]{0:T(1024)(128)(4,1)}), s8[4194304]{0:T(1024)(128)(4,1)S(1)}, s32[]{:S(2)}) async-start(s8[25165824]{0:T(1024)(128)(4,1)} %bitcast.182), calls=%async_computation.10 | async-start | bytes 8388608
  1262.8 343.9 %slice-start.4 = ((s8[25165824]{0:T(1024)(128)(4,1)}), s8[4194304]{0:T(1024)(128)(4,1)S(1)}, s32[]{:S(2)}) async-start(s8[25165824]{0:T(1024)(128)(4,1)} %bitcast.182), calls=%async_computation.11 | async-start | bytes 8388608
  1268.1 338.6 %slice-start.5 = ((s8[25165824]{0:T(1024)(128)(4,1)}), s8[4194304]{0:T(1024)(128)(4,1)S(1)}, s32[]{:S(2)}) async-start(s8[25165824]{0:T(1024)(128)(4,1)} %bitcast.182), calls=%async_computation.12 | async-start | bytes 8388608
  1270.9 274.5 %collective-permute-start.16 = (bf16[384,1536]{1,0:T(8,128)(2,1)S(1)}, bf16[384,1536]{1,0:T(8,128)(2,1)S(1)}, u32[]{:S(2)}, u32[]{:S(2)}) collective-permute-start(bf16[384,1536]{1,0:T(8,128)(2,1)S(1)} %select_convert_fusion.11), channel_id=1, source_target_pairs={{0,8},{1,9},{2,10},{3,11},{4,12},{5,13},{6,14},{7,15},{8,0},{9,1},... | collective-permute-start | bytes 3538952 | tf_op jit(solution)/shard_map/ppermute | solution.py:28
  1273.0 272.5 %slice-start.31 = ((s8[4718592]{0:T(1024)(128)(4,1)}), s8[4194304]{0:T(1024)(128)(4,1)S(1)}, s32[]{:S(2)}) async-start(s8[4718592]{0:T(1024)(128)(4,1)} %bitcast.202), calls=%async_computation.38 | async-start | bytes 8388608
  1273.6 271.8 %slice-start.32 = ((s8[4718592]{0:T(1024)(128)(4,1)}), s8[524288]{0:T(1024)(128)(4,1)S(1)}, s32[]{:S(2)}) async-start(s8[4718592]{0:T(1024)(128)(4,1)} %bitcast.202), calls=%async_computation.39 | async-start | bytes 1048576
  1524.4 23.8 %collective-permute-start.2 = (bf16[192,1536]{1,0:T(8,128)(2,1)S(1)}, bf16[192,1536]{1,0:T(8,128)(2,1)S(1)}, u32[]{:S(2)}, u32[]{:S(2)}) collective-permute-start(bf16[192,1536]{1,0:T(8,128)(2,1)S(1)} %select_convert_fusion.21), channel_id=1, source_target_pairs={{0,4},{1,5},{2,6},{3,7},{4,0},{5,1},{6,2},{7,3},{8,12},{9,13},{10,... | collective-permute-start | bytes 1769480 | tf_op jit(solution)/shard_map/ppermute | solution.py:28
  1546.1 15.0 collective-permute-start.17
  1548.5 14.5 collective-permute-start.3
  1561.4 7.9 collective-permute-start.18
  1563.1 6.3 collective-permute-start.4
  1569.3 1.4 collective-permute-start.19
  1623.0 320.8 %collective-permute-start.21 = (bf16[384,4096]{1,0:T(8,128)(2,1)}, bf16[384,4096]{1,0:T(8,128)(2,1)}, u32[]{:S(2)}, u32[]{:S(2)}) collective-permute-start(bf16[384,4096]{1,0:T(8,128)(2,1)} %select_convert_fusion.5), channel_id=1, source_target_pairs={{0,8},{1,9},{2,10},{3,11},{4,12},{5,13},{6,14},{7,15},{8,0},{9,1},... | collective-permute-start | bytes 9437192 | tf_op jit(solution)/shard_map/ppermute | solution.py:28
  1755.5 255.7 %collective-permute-start.26 = (bf16[384,4096]{1,0:T(8,128)(2,1)}, bf16[384,4096]{1,0:T(8,128)(2,1)}, u32[]{:S(2)}, u32[]{:S(2)}) collective-permute-start(bf16[384,4096]{1,0:T(8,128)(2,1)} %select_convert_fusion.4), channel_id=1, source_target_pairs={{0,8},{1,9},{2,10},{3,11},{4,12},{5,13},{6,14},{7,15},{8,0},{9,1},... | collective-permute-start | bytes 9437192 | tf_op jit(solution)/shard_map/ppermute | solution.py:28
  1890.2 188.3 %collective-permute-start.31 = (bf16[1024,1536]{1,0:T(8,128)(2,1)}, bf16[1024,1536]{1,0:T(8,128)(2,1)}, u32[]{:S(2)}, u32[]{:S(2)}) collective-permute-start(bf16[1024,1536]{1,0:T(8,128)(2,1)} %select_convert_fusion.3), channel_id=1, source_target_pairs={{0,8},{1,9},{2,10},{3,11},{4,12},{5,13},{6,14},{7,15},{8,0},{9,1},... | collective-permute-start | bytes 9437192 | tf_op jit(solution)/shard_map/ppermute | solution.py:28
  1958.3 131.8 %collective-permute-start.22 = (bf16[192,4096]{1,0:T(8,128)(2,1)}, bf16[192,4096]{1,0:T(8,128)(2,1)}, u32[]{:S(2)}, u32[]{:S(2)}) collective-permute-start(bf16[192,4096]{1,0:T(8,128)(2,1)} %select_convert_fusion.10), channel_id=1, source_target_pairs={{0,4},{1,5},{2,6},{3,7},{4,0},{5,1},{6,2},{7,3},{8,12},{9,13},{10,... | collective-permute-start | bytes 4718600 | tf_op jit(solution)/shard_map/ppermute | solution.py:28
  2025.7 70.0 %collective-permute-start.27 = (bf16[192,4096]{1,0:T(8,128)(2,1)}, bf16[192,4096]{1,0:T(8,128)(2,1)}, u32[]{:S(2)}, u32[]{:S(2)}) collective-permute-start(bf16[192,4096]{1,0:T(8,128)(2,1)} %select_convert_fusion.9), channel_id=1, source_target_pairs={{0,4},{1,5},{2,6},{3,7},{4,0},{5,1},{6,2},{7,3},{8,12},{9,13},{10,... | collective-permute-start | bytes 4718600 | tf_op jit(solution)/shard_map/ppermute | solution.py:28
  2088.0 36.7 %collective-permute-start.32 = (bf16[512,1536]{1,0:T(8,128)(2,1)S(1)}, bf16[512,1536]{1,0:T(8,128)(2,1)S(1)}, u32[]{:S(2)}, u32[]{:S(2)}) collective-permute-start(bf16[512,1536]{1,0:T(8,128)(2,1)S(1)} %select_convert_fusion.8), channel_id=1, source_target_pairs={{0,4},{1,5},{2,6},{3,7},{4,0},{5,1},{6,2},{7,3},{8,12},{9,13},{10,... | collective-permute-start | bytes 4718600 | tf_op jit(solution)/shard_map/ppermute | solution.py:28
  2094.2 33.0 %collective-permute-start.23 = (bf16[96,4096]{1,0:T(8,128)(2,1)S(1)}, bf16[96,4096]{1,0:T(8,128)(2,1)S(1)}, u32[]{:S(2)}, u32[]{:S(2)}) collective-permute-start(bf16[96,4096]{1,0:T(8,128)(2,1)S(1)} %select_convert_fusion.17), channel_id=1, source_target_pairs={{0,2},{1,3},{2,0},{3,1},{4,6},{5,7},{6,4},{7,5},{8,10},{9,11},{10,... | collective-permute-start | bytes 2359304 | tf_op jit(solution)/shard_map/ppermute | solution.py:28
  2098.3 33.3 %collective-permute-start.28 = (bf16[96,4096]{1,0:T(8,128)(2,1)S(1)}, bf16[96,4096]{1,0:T(8,128)(2,1)S(1)}, u32[]{:S(2)}, u32[]{:S(2)}) collective-permute-start(bf16[96,4096]{1,0:T(8,128)(2,1)S(1)} %select_convert_fusion.16), channel_id=1, source_target_pairs={{0,2},{1,3},{2,0},{3,1},{4,6},{5,7},{6,4},{7,5},{8,10},{9,11},{10,... | collective-permute-start | bytes 2359304 | tf_op jit(solution)/shard_map/ppermute | solution.py:28
  2125.7 21.5 collective-permute-start.33
  2127.6 20.1 collective-permute-start.24
  2131.9 16.8 collective-permute-start.29
  2147.6 2.1 collective-permute-start.34
  (117 other events, 1639.4 us)
Sparse Core Ops, SparseCore 0:
  10.9 60.0 all-gather.7
  73.9 56.1 all-gather.9
  133.0 62.5 all-gather.11
  198.3 62.4 all-gather.13
  263.5 94.7 all-gather.15
  361.0 94.2 all-gather.17
  458.1 94.2 all-gather.19
where the time goes:
time: 2170 us; the launch traced here: 2160 us
  waiting for transfers between devices  1390 us (64%)
  blocking collectives  253 us (12%)
  matrix products  240 us (11%)
  other arithmetic  180 us (8%)
  starting transfers between devices  51.8 us (2%)
    ppermute x45, waiting for transfers between devices, from_partner(): return lax.ppermute(value, axis, pairs)  943 us
    psum x1, blocking collectives, body(): loss_sum, count_sum = lax.psum((loss_total, valid_count), 'dp')  211 us
    add x45, other arithmetic, halving_sum(): kept_part + came_part  93 us
    all_gather x1, waiting for transfers between devices, body(): lax.all_gather(w_gate, 'dp', axis=0, tiled=True)  90.8 us
    all_gather x1, waiting for transfers between devices, body(): lax.all_gather(w_up, 'dp', axis=0, tiled=True)  88.8 us
    all_gather x1, waiting for transfers between devices, body(): lax.all_gather(w_down, 'dp', axis=0, tiled=True)  88.5 us
    convert_element_type x45, other arithmetic, shortened(): a.astype(jnp.bfloat16)  72 us
    all_gather x1, waiting for transfers between devices, body(): lax.all_gather(w_query, 'dp', axis=0, tiled=True)  61.3 us
  transfers between devices with their start and end apart: 52, of which 36 were waited for; matrix products, arithmetic and copies ran while one was open for 13% of the time, Pallas kernels for 0%

commit v1 on v0

v1 whole, which is shorter than its diff:
```python
import math

import jax
import jax.numpy as jnp
from jax import lax
from jax.sharding import PartitionSpec as P

QUERY_HEAD_COUNT = 16
KEY_VALUE_HEADS = 8
HEAD_SIZE = 96
SEQ = 128
EPSILON = 1e-05
ROPE_BASE = 100000.0
MASK_FILL = -1e30
LANES = 128
LONGEST_LINE = 8

BF = jnp.bfloat16
F32 = jnp.float32


def dot(a, b, dims):
    return lax.dot_general(a, b, (dims, ((), ())), preferred_element_type=F32)


def mm(a, b):
    return dot(a, b, ((1,), (0,)))


def mm_t(a, b):
    return dot(a, b, ((1,), (1,)))


def t_mm(a, b):
    return dot(a, b, ((0,), (0,)))


def swap(value, mask):
    n = lax.axis_size("dp")
    return lax.ppermute(value, "dp", [(i, i ^ mask) for i in range(n)])


def shift(value, step, direction):
    n = lax.axis_size("dp")
    planes = n // 8
    if direction > 0:
        pairs = [(i, i + 8) for i in range(n) if i // 8 >= step - 1 and i + 8 < n]
    else:
        pairs = [(i, i - 8) for i in range(n) if i // 8 <= planes - step and i >= 8]
    return lax.ppermute(value, "dp", pairs)


def collect_shift(value, step, direction):
    n = lax.axis_size("dp")
    planes = n // 8
    far = planes - step
    if direction > 0:
        pairs = [(i, i + 8) for i in range(n) if i + 8 * far < n and i + 8 < n]
    else:
        pairs = [(i, i - 8) for i in range(n) if i - 8 * far >= 0 and i >= 8]
    return lax.ppermute(value, "dp", pairs)


def column_groups(with_core):
    n = lax.axis_size("dp")
    planes = n // 8
    if with_core:
        return [[8 * z + 2 * p + c for z in range(planes) for c in range(2)] for p in range(4)]
    return [[8 * z + 2 * p + c for z in range(planes)] for p in range(4) for c in range(2)]


def z_gather(value, z):
    planes = lax.axis_size("dp") // 8
    if planes > LONGEST_LINE:
        return lax.all_gather(value, "dp", axis_index_groups=column_groups(False), axis=0)
    below, above = [], []
    up = down = value
    for step in range(1, planes):
        up = shift(up, step, 1)
        down = shift(down, step, -1)
        below.append(up)
        above.append(down)
    line = jnp.stack(below[::-1] + [value] + above)
    return lax.dynamic_slice_in_dim(line, planes - 1 - z, planes)


def z_reduce(parts, z):
    planes = lax.axis_size("dp") // 8
    if planes > LONGEST_LINE:
        return lax.psum_scatter(
            parts.astype(BF), "dp", axis_index_groups=column_groups(False), scatter_dimension=0
        ).astype(F32)

    def entry(k):
        return lax.dynamic_index_in_dim(parts, k, 0, keepdims=False)

    up = down = None
    for step in range(1, planes):
        far = planes - step
        send_up, send_down = entry(z + far), entry(z - far)
        if step > 1:
            send_up = send_up + up.astype(F32)
            send_down = send_down + down.astype(F32)
        up = collect_shift(send_up.astype(BF), step, 1)
        down = collect_shift(send_down.astype(BF), step, -1)
    own = entry(z)
    if planes > 1:
        own = own + up.astype(F32) + down.astype(F32)
    return own


def place(out, piece, where):
    return lax.dynamic_update_slice(out, piece, where)


def gather_rows(value, place_bits):
    z, y, x, c = place_bits
    planes = lax.axis_size("dp") // 8
    rows, columns = value.shape
    half = planes // 2
    own = z_gather(value, z)
    a, b = own[:half], own[half:]
    a_x = swap(a, 2)
    b_y = swap(b, 4)
    a_far = swap(jnp.stack([a, a_x]), 4)
    b_far = swap(jnp.stack([b, b_y]), 2)
    out = jnp.zeros((planes, 2, 2, 2, rows, columns), value.dtype)
    for core, move in ((c, lambda v: v), (1 - c, lambda v: swap(v, 1))):
        for piece, start, at_y, at_x in (
            (own, 0, y, x),
            (a_x, 0, y, 1 - x),
            (b_y, half, 1 - y, x),
        ):
            piece = move(piece)
            out = place(out, piece[:, None, None, None], (start, at_y, at_x, core, 0, 0))
        a_core, b_core = move(a_far), move(b_far)
        out = place(out, a_core[0][:, None, None, None], (0, 1 - y, x, core, 0, 0))
        out = place(out, a_core[1][:, None, None, None], (0, 1 - y, 1 - x, core, 0, 0))
        out = place(out, b_core[0][:, None, None, None], (half, y, 1 - x, core, 0, 0))
        out = place(out, b_core[1][:, None, None, None], (half, 1 - y, 1 - x, core, 0, 0))
    return out.reshape(planes * 8 * rows, columns)


def pick(parts, index, axis):
    return lax.dynamic_index_in_dim(parts, index, axis, keepdims=False)


def scatter_rows(partial, place_bits):
    z, y, x, c = place_bits
    planes = lax.axis_size("dp") // 8
    columns = partial.shape[1]
    parts = partial.reshape(planes, 2, 2, 2, -1, columns)
    half = planes // 2
    came = swap(pick(parts, 1 - c, 3).astype(BF), 1)
    parts = pick(parts, c, 3) + came.astype(F32)
    a, b = parts[:half], parts[half:]
    came_a = swap(pick(a, 1 - y, 1).astype(BF), 4)
    came_b = swap(pick(b, 1 - x, 2).astype(BF), 2)
    a = pick(a, y, 1) + came_a.astype(F32)
    b = pick(b, x, 2) + came_b.astype(F32)
    came_a = swap(pick(a, 1 - x, 1).astype(BF), 2)
    came_b = swap(pick(b, 1 - y, 1).astype(BF), 4)
    a = pick(a, x, 1) + came_a.astype(F32)
    b = pick(b, y, 1) + came_b.astype(F32)
    return z_reduce(jnp.concatenate([a, b]), z)


def split_gather(rows):
    half = rows.shape[0] // 2
    a, b = rows[:half], rows[half:]
    a_x = swap(a, 2)
    b_y = swap(b, 4)
    a_far = swap(jnp.concatenate([a, a_x]), 4)
    b_far = swap(jnp.concatenate([b, b_y]), 2)
    return (jnp.concatenate([a, a_x, b, b_y]), jnp.concatenate([a_far, b_far]))


def split_reduce(near, far):
    two = far.shape[0] // 2
    one = two // 2
    low = far.astype(BF)
    came_a = swap(low[:two], 4)
    came_b = swap(low[two:], 2)
    a = near[:two] + came_a.astype(F32)
    b = near[two:] + came_b.astype(F32)
    came_a = swap(a[one:].astype(BF), 2)
    came_b = swap(b[one:].astype(BF), 4)
    return jnp.concatenate([a[:one] + came_a.astype(F32), b[:one] + came_b.astype(F32)])


def total_of(value):
    n = lax.axis_size("dp")
    mask = 1
    while mask < n:
        value = value + swap(value, mask)
        mask *= 2
    return value


def rotation_tables(length, width):
    half_width = width // 2
    position = jnp.arange(length, dtype=F32)[:, None]
    freq_rate = ROPE_BASE ** (-2.0 * jnp.arange(half_width, dtype=F32) / width)
    angle_table = position * freq_rate[None, :]
    return (jnp.cos(angle_table)[:, None, :], jnp.sin(angle_table)[:, None, :])


def turn(heads_in, cosine_lookup, sine_lookup):
    half_width = heads_in.shape[-1] // 2
    left_part = heads_in[..., :half_width]
    right_part = heads_in[..., half_width:]
    return jnp.concatenate(
        [
            left_part * cosine_lookup - right_part * sine_lookup,
            right_part * cosine_lookup + left_part * sine_lookup,
        ],
        axis=-1,
    )


def norm_rows(field_in, gain_vec):
    inv_scale = lax.rsqrt(jnp.mean(field_in * field_in, axis=-1, keepdims=True) + EPSILON)
    return (field_in * inv_scale * gain_vec, inv_scale)


def norm_back(upstream, field_in, inv_scale, gain_vec):
    gain_grad = jnp.sum(upstream * field_in * inv_scale, axis=0)
    scaled_up = upstream * gain_vec
    field_grad = inv_scale * scaled_up - field_in * inv_scale**3 * jnp.mean(
        scaled_up * field_in, axis=-1, keepdims=True
    )
    return (gain_grad, field_grad)


def probabilities(query_heads, key_heads):
    score_scale = 1.0 / math.sqrt(HEAD_SIZE)
    raw_scores = (
        jnp.einsum("bqhrd,bkhd->bhrqk", query_heads, key_heads, preferred_element_type=F32)
        * score_scale
    )
    causal = jnp.arange(SEQ)[:, None] >= jnp.arange(SEQ)[None, :]
    scores = jnp.where(causal, raw_scores, MASK_FILL)
    row_max = jnp.max(scores, axis=-1, keepdims=True)
    weights = jnp.exp(scores - row_max)
    return weights / jnp.sum(weights, axis=-1, keepdims=True)


def ffn_forward(rows, w_gate, w_up, w_down):
    gate_pre = mm(rows, w_gate)
    up_pre = mm(rows, w_up)
    hidden = (jax.nn.silu(gate_pre) * up_pre).astype(BF)
    return (mm(hidden, w_down), gate_pre, up_pre, hidden)


def ffn_backward(grad_low, gate_pre, up_pre, w_gate, w_up, w_down):
    grad_hidden = mm_t(grad_low, w_down)
    gate_sigmoid = jax.nn.sigmoid(gate_pre)
    grad_gate = (
        grad_hidden * up_pre * gate_sigmoid * (1.0 + gate_pre * (1.0 - gate_sigmoid))
    ).astype(BF)
    grad_up = (grad_hidden * gate_pre * gate_sigmoid).astype(BF)
    return (mm_t(grad_gate, w_gate) + mm_t(grad_up, w_up), grad_gate, grad_up)


def body(
    tokens,
    teacher,
    valid_mask,
    w_query,
    key_weight_matrix,
    value_weight_matrix,
    w_output,
    w_gate,
    w_up,
    w_down,
    attn_gain,
    ffn_gain,
):
    n = lax.axis_size("dp")
    planes = n // 8
    position = lax.axis_index("dp")
    c, x, y, z = position % 2, position // 2 % 2, position // 4 % 2, position // 8
    bits = (z, y, x, c)
    p = position // 2 % 4
    rows = w_query.shape[0]
    width = w_query.shape[1]
    kv_width = key_weight_matrix.shape[1]
    ff_rows = w_down.shape[0]
    ff = w_gate.shape[1]
    count = tokens.shape[0]
    sequences = count // SEQ
    groups = QUERY_HEAD_COUNT // KEY_VALUE_HEADS
    score_scale = 1.0 / math.sqrt(HEAD_SIZE)
    cosine_lookup, sine_lookup = rotation_tables(SEQ, HEAD_SIZE)

    with jax.named_scope("ffn_weights_to_columns"):
        both = jnp.stack([w_gate, w_up]).reshape(2, rows, planes, 4, 2 * ff_rows)

        def columns_for(r):
            return pick(both, p ^ r, 3).reshape(2, rows, ff // 4)

        by_source = jnp.zeros((2, 4, rows, ff // 4), BF)
        for r in range(4):
            piece = columns_for(r)
            if r:
                piece = swap(piece, r << 1)
            by_source = place(by_source, piece[:, None], (0, p ^ r, 0, 0))

    with jax.named_scope("attention_weights"):
        gains = jnp.stack([attn_gain, ffn_gain], axis=1)
        gains = jnp.pad(gains, ((0, 0), (0, LANES - 2)))
        qkv_local = jnp.concatenate(
            [w_query, key_weight_matrix, value_weight_matrix, gains], axis=1
        )
        qkv = gather_rows(qkv_local, bits)
        wo = gather_rows(w_output, bits)

    with jax.named_scope("ffn_weights_along_z"):
        column = z_gather(by_source, z)
        other = swap(column, 1)
        gate_up = jnp.zeros((2, planes, 4, 2, rows, ff // 4), BF)
        gate_up = place(gate_up, jnp.swapaxes(column, 0, 1)[:, :, :, None], (0, 0, 0, c, 0, 0))
        gate_up = place(gate_up, jnp.swapaxes(other, 0, 1)[:, :, :, None], (0, 0, 0, 1 - c, 0, 0))
        gate_up = gate_up.reshape(2, n * rows, ff // 4)
        wg, wu = gate_up[0], gate_up[1]
        wd = lax.all_gather(
            w_down, "dp", axis_index_groups=column_groups(True), axis=0, tiled=True
        )

    with jax.named_scope("attention_forward"):
        wq = qkv[:, :width]
        wk = qkv[:, width : width + kv_width]
        wv = qkv[:, width + kv_width : width + 2 * kv_width]
        gain_in = qkv[:, width + 2 * kv_width].astype(F32)
        gain_mid = qkv[:, width + 2 * kv_width + 1].astype(F32)
        inputs_f = tokens.astype(F32)
        normed, inv_attn = norm_rows(inputs_f, gain_in)
        normed_in = normed.astype(BF)
        heads = (sequences, SEQ, QUERY_HEAD_COUNT, HEAD_SIZE)
        kv_heads = (sequences, SEQ, KEY_VALUE_HEADS, HEAD_SIZE)
        grouped = (sequences, SEQ, KEY_VALUE_HEADS, groups, HEAD_SIZE)
        query = turn(mm(normed_in, wq).reshape(heads), cosine_lookup, sine_lookup)
        query = query.astype(BF).reshape(grouped)
        key = turn(mm(normed_in, wk).reshape(kv_heads), cosine_lookup, sine_lookup).astype(BF)
        value = mm(normed_in, wv).astype(BF).reshape(kv_heads)
        probs = probabilities(query, key)
        probs_low = probs.astype(BF)
        mixed = jnp.einsum("bhrqk,bkhd->bqhrd", probs_low, value, preferred_element_type=F32)
        mixed = mixed.reshape(count, width).astype(BF)
        hidden_res = inputs_f + mm(mixed, wo)
        normed_two, inv_ffn = norm_rows(hidden_res, gain_mid)
        normed_mid = normed_two.astype(BF)

    with jax.named_scope("ffn_forward"):
        near, far = split_gather(normed_mid)
        y_near, gate_near, up_near, hid_near = ffn_forward(near, wg, wu, wd)
        y_far, gate_far, up_far, hid_far = ffn_forward(far, wg, wu, wd)
        result = hidden_res + split_reduce(y_near, y_far)
        out_act = result.astype(BF)

    with jax.named_scope("loss"):
        mask_f = valid_mask.astype(F32)
        grad_out = (result - teacher.astype(F32)) * mask_f[:, None]
        sums = jnp.stack([jnp.sum(grad_out * grad_out), jnp.sum(mask_f)])
        sums = total_of(jnp.broadcast_to(sums[:, None], (2, LANES)))
        loss = sums[0, 0] / (sums[1, 0] * width)

    with jax.named_scope("ffn_backward"):
        grad_low = grad_out.astype(BF)
        d_near, d_far = split_gather(grad_low)
        m_near, dg_near, du_near = ffn_backward(d_near, gate_near, up_near, wg, wu, wd)
        m_far, dg_far, du_far = ffn_backward(d_far, gate_far, up_far, wg, wu, wd)
        grad_mid = split_reduce(m_near, m_far)

    with jax.named_scope("ffn_weight_gradients"):
        hid = jnp.concatenate([hid_near, hid_far])
        d_all = jnp.concatenate([d_near, d_far])
        mid_all = jnp.concatenate([near, far])
        dg_all = jnp.concatenate([dg_near, dg_far])
        du_all = jnp.concatenate([du_near, du_far])
        grad_down = t_mm(hid, d_all).astype(BF)
        grad_down = lax.psum_scatter(
            grad_down,
            "dp",
            axis_index_groups=column_groups(True),
            scatter_dimension=0,
            tiled=True,
        ).astype(F32)
        shape = (planes, 4, 2, rows, ff // 4)
        order = (0, 2, 1, 3, 4)
        g_gate = t_mm(mid_all, dg_all).astype(BF).reshape(shape).transpose(order)
        g_up = t_mm(mid_all, du_all).astype(BF).reshape(shape).transpose(order)
        both = jnp.stack([g_gate, g_up], axis=2).reshape(n * 2 * rows, ff // 4)
        both = lax.psum_scatter(
            both, "dp", axis_index_groups=column_groups(True), scatter_dimension=0, tiled=True
        ).reshape(2, 4, rows, ff // 4)
        spread = jnp.zeros((2, rows, planes, 4, 2 * ff_rows), BF)
        for r in range(4):
            piece = pick(both, p ^ r, 1)
            if r:
                piece = swap(piece, r << 1)
            piece = piece.reshape(2, rows, planes, 1, 2 * ff_rows)
            spread = place(spread, piece, (0, 0, 0, p ^ r, 0))
        spread = spread.reshape(2, rows, ff).astype(F32)
        grad_gate, grad_up = spread[0], spread[1]

    with jax.named_scope("attention_backward"):
        grad_gain_mid, grad_res = norm_back(grad_mid, hidden_res, inv_ffn, gain_mid)
        grad_res = grad_out + grad_res
        res_low = grad_res.astype(BF)
        g_wo = t_mm(mixed, res_low)
        grad_mixed = mm_t(res_low, wo).astype(BF).reshape(grouped)
        grad_probs = jnp.einsum(
            "bqhrd,bkhd->bhrqk", grad_mixed, value, preferred_element_type=F32
        )
        grad_scores = probs * (grad_probs - jnp.sum(probs * grad_probs, axis=-1, keepdims=True))
        grad_scores = grad_scores.astype(BF)
        grad_query = score_scale * jnp.einsum(
            "bhrqk,bkhd->bqhrd", grad_scores, key, preferred_element_type=F32
        )
        grad_key = score_scale * jnp.einsum(
            "bhrqk,bqhrd->bkhd", grad_scores, query, preferred_element_type=F32
        )
        grad_value = jnp.einsum(
            "bhrqk,bqhrd->bkhd", probs_low, grad_mixed, preferred_element_type=F32
        )
        query_back = turn(grad_query.reshape(heads), cosine_lookup, -sine_lookup)
        query_back = query_back.reshape(count, width).astype(BF)
        key_back = turn(grad_key, cosine_lookup, -sine_lookup).reshape(count, kv_width).astype(BF)
        value_back = grad_value.reshape(count, kv_width).astype(BF)
        grad_in = mm_t(query_back, wq) + mm_t(key_back, wk) + mm_t(value_back, wv)
        grad_gain_in, grad_tokens = norm_back(grad_in, inputs_f, inv_attn, gain_in)
        input_grad = (grad_res + grad_tokens).astype(BF)

    with jax.named_scope("attention_weight_gradients"):
        g_wo = scatter_rows(g_wo, bits)
        g_gains = jnp.stack([grad_gain_in, grad_gain_mid], axis=1)
        g_gains = jnp.pad(g_gains, ((0, 0), (0, LANES - 2)))
        g_qkv = jnp.concatenate(
            [
                t_mm(normed_in, query_back),
                t_mm(normed_in, key_back),
                t_mm(normed_in, value_back),
                g_gains,
            ],
            axis=1,
        )
        g_qkv = scatter_rows(g_qkv, bits)
        g_wq = g_qkv[:, :width]
        g_wk = g_qkv[:, width : width + kv_width]
        g_wv = g_qkv[:, width + kv_width : width + 2 * kv_width]
        g_gain_in = g_qkv[:, width + 2 * kv_width]
        g_gain_mid = g_qkv[:, width + 2 * kv_width + 1]

    return (
        out_act,
        loss,
        input_grad,
        g_wq,
        g_wk,
        g_wv,
        g_wo,
        grad_gate,
        grad_up,
        grad_down,
        g_gain_in,
        g_gain_mid,
    )


def solution(mesh):
    wide, flat = P("dp", None), P("dp")
    in_specs = (wide, wide, flat) + (wide,) * 7 + (flat, flat)
    out_specs = (wide, P(), wide) + (wide,) * 7 + (flat, flat)
    return jax.shard_map(body, mesh=mesh, in_specs=in_specs, out_specs=out_specs, check_vma=False)
```

time: 2170 us -> 624 us (0.29)
  waiting for transfers between devices: 1390 us -> 220 us
  blocking collectives: 253 us -> 0 us
  matrix products: 240 us -> 80.1 us
  other arithmetic: 180 us -> 59.2 us
  local copies, waits for them, and re-layouts: 18.9 us -> 127 us
  starting transfers between devices: 51.8 us -> 110 us
    ppermute x45 -> x86, waiting for transfers between devices: 943 us -> 220 us  [the longest x56 152 us: swap(): return lax.ppermute(value, 'dp', [(i, i ^ mask) for i in range(n)])]
    all_gather x7 -> x1, waiting for transfers between devices: 447 us -> 0.01 us  [body(): lax.all_gather(w_down, 'dp', axis_index_groups=column_groups(True), axis=...]
    psum x1 -> x0, blocking collectives: 211 us -> none  [body(): loss_sum, count_sum = lax.psum((loss_total, valid_count), 'dp')]
    dot_general x54 -> x32, matrix products: 240 us -> 77.9 us  [the longest x27 72.1 us: dot(): return lax.dot_general(a, b, (dims, ((), ())), preferred_element_type=F32)]
    add x49 -> x24, other arithmetic: 93.1 us -> 21.8 us  [the longest x2 14.3 us: scatter_rows(): parts = pick(parts, c, 3) + came.astype(F32)]
    convert_element_type x52 -> x13, other arithmetic: 75.5 us -> 7.3 us  [the longest x1 1.95 us: body(): grad_down = lax.psum_scatter(grad_down, 'dp', axis_index_groups=column_gr...]
    ppermute x45 -> x86, starting transfers between devices: 51.6 us -> 110 us  [the longest x56 51.6 us: swap(): return lax.ppermute(value, 'dp', [(i, i ^ mask) for i in range(n)])]
    unnamed x1 -> x0, blocking collectives: 42.1 us -> none
  transfers between devices with their start and end apart: 52 -> 89, of which waited for: 36 -> 36; matrix products, arithmetic and copies ran while one was open for 13% -> 37% of each run, Pallas kernels for 0% -> 0%
where the time goes in v1:
time: 624 us; the launch traced here: 615 us
  waiting for transfers between devices  220 us (35%)
  local copies, waits for them, and re-layouts  127 us (20%)
  starting transfers between devices  110 us (18%)
  matrix products  80.1 us (13%)
  other arithmetic  59.2 us (9%)
  between operations  19.2 us (3%)
    ppermute x56, waiting for transfers between devices, swap(): return lax.ppermute(value, 'dp', [(i, i ^ mask) for i in range(n)])  152 us
    dot_general x27, matrix products, dot(): return lax.dot_general(a, b, (dims, ((), ())), preferred_element_type=F32)  72.1 us
    ppermute x18, waiting for transfers between devices, shift(): return lax.ppermute(value, 'dp', pairs)  60.5 us
    ppermute x56, starting transfers between devices, swap(): return lax.ppermute(value, 'dp', [(i, i ^ mask) for i in range(n)])  51.6 us
    dynamic_update_slice x38, local copies, waits for them, and re-layouts, place(): return lax.dynamic_update_slice(out, piece, where)  38.5 us
    ppermute x18, starting transfers between devices, shift(): return lax.ppermute(value, 'dp', pairs)  33 us
    ppermute x12, starting transfers between devices, collect_shift(): return lax.ppermute(value, 'dp', pairs)  25.4 us
    unnamed x206, local copies, waits for them, and re-layouts  23.2 us
  transfers between devices with their start and end apart: 89, of which 36 were waited for; matrix products, arithmetic and copies ran while one was open for 37% of the time, Pallas kernels for 0%

profile of v1, /device:TPU:0, one launch (start us, length us, event | category | flops | bytes accessed | tf_op | source)
XLA Modules:
  0.0 615.3 jit_solution(3143944979508603208)
XLA Ops:
  7.2 5.7 collective-permute-start.15
  17.3 5.9 collective-permute-start
  32.3 2.5 collective-permute-start.34
  34.8 5.1 collective-permute-done.33
  42.0 10.5 %collective-permute-done.19 = bf16[48,1536]{1,0:T(8,128)(2,1)S(1)} collective-permute-done((bf16[48,1536]{1,0:T(8,128)(2,1)}, bf16[48,1536]{1,0:T(8,128)(2,1)S(1)}, u32[]{:S(2)}, u32[]{:S(2)}) %collective-permute-start.19) | collective-permute-done | bytes 147488 | tf_op jit(solution)/shard_map/attention_weights/ppermute | solution.py:50
  55.7 9.7 %collective-permute-done.20 = bf16[48,1536]{1,0:T(8,128)(2,1)S(1)} collective-permute-done((bf16[48,1536]{1,0:T(8,128)(2,1)S(1)}, bf16[48,1536]{1,0:T(8,128)(2,1)S(1)}, u32[]{:S(2)}, u32[]{:S(2)}) %collective-permute-start.20) | collective-permute-done | bytes 147488 | tf_op jit(solution)/shard_map/attention_weights/ppermute | solution.py:50
  68.3 5.5 collective-permute-start.35
  78.7 15.7 %collective-permute-done.4 = bf16[48,3200]{1,0:T(8,128)(2,1)S(1)} collective-permute-done((bf16[48,3200]{1,0:T(8,128)(2,1)}, bf16[48,3200]{1,0:T(8,128)(2,1)S(1)}, u32[]{:S(2)}, u32[]{:S(2)}) %collective-permute-start.4) | collective-permute-done | bytes 307232 | tf_op jit(solution)/shard_map/attention_weights/ppermute | solution.py:50
  101.6 4.4 collective-permute-done.5
  109.5 2.6 bitcast_dynamic-update-slice_fusion.3
  116.3 5.1 collective-permute-done.24
  128.7 13.2 %collective-permute-done.6 = bf16[2,48,3200]{2,1,0:T(8,128)(2,1)S(1)} collective-permute-done((bf16[2,48,3200]{2,1,0:T(8,128)(2,1)S(1)}, bf16[2,48,3200]{2,1,0:T(8,128)(2,1)S(1)}, u32[]{:S(2)}, u32[]{:S(2)}) %collective-permute-start.6) | collective-permute-done | bytes 614432 | tf_op jit(solution)/shard_map/attention_weights/ppermute | solution.py:40
  152.8 18.6 %collective-permute-done.40 = bf16[2,4,48,1024]{3,2,1,0:T(8,128)(2,1)S(1)} collective-permute-done((bf16[2,4,48,1024]{3,2,1,0:T(8,128)(2,1)S(1)}, bf16[2,4,48,1024]{3,2,1,0:T(8,128)(2,1)S(1)}, u32[]{:S(2)}, u32[]{:S(2)}) %collective-permute-start.40) | collective-permute-done | bytes 786464 | tf_op jit(solution)/shard_map/ffn_weights_along_z/ppermute | solution.py:50
  180.1 3.5 collective-permute-done.13
  187.8 3.2 fusion.4
  193.4 2.5 reshape.262
  197.9 2.3 fusion.206
  203.0 4.1 multiply_reduce_fusion.3
  209.0 10.8 %collective-permute-done.30 = bf16[128,1536]{1,0:T(8,128)(2,1)S(1)} collective-permute-done((bf16[128,1536]{1,0:T(8,128)(2,1)S(1)}, bf16[128,1536]{1,0:T(8,128)(2,1)S(1)}, u32[]{:S(2)}, u32[]{:S(2)}) %collective-permute-start.30) | collective-permute-done | bytes 393248 | tf_op jit(solution)/shard_map/ffn_forward/ppermute | solution.py:40
  222.1 9.9 %collective-permute-done.31 = bf16[128,1536]{1,0:T(8,128)(2,1)S(1)} collective-permute-done((bf16[128,1536]{1,0:T(8,128)(2,1)S(1)}, bf16[128,1536]{1,0:T(8,128)(2,1)S(1)}, u32[]{:S(2)}, u32[]{:S(2)}) %collective-permute-start.31) | collective-permute-done | bytes 393248 | tf_op jit(solution)/shard_map/ffn_forward/ppermute | solution.py:40
  232.7 14.6 %collective-permute-done.42 = bf16[256,1536]{1,0:T(8,128)(2,1)S(1)} collective-permute-done((bf16[256,1536]{1,0:T(8,128)(2,1)S(1)}, bf16[256,1536]{1,0:T(8,128)(2,1)S(1)}, u32[]{:S(2)}, u32[]{:S(2)}) %collective-permute-start.42) | collective-permute-done | bytes 786464 | tf_op jit(solution)/shard_map/ffn_forward/ppermute | solution.py:40
  248.9 3.5 bitcast_dynamic-update-slice_fusion
  256.9 3.5 multiply_convert_fusion.4
  260.4 4.1 convolution_convert_fusion.3
  268.3 3.5 multiply_convert_fusion.5
  273.6 8.0 %collective-permute-done.44 = bf16[256,1536]{1,0:T(8,128)(2,1)S(1)} collective-permute-done((bf16[256,1536]{1,0:T(8,128)(2,1)S(1)}, bf16[256,1536]{1,0:T(8,128)(2,1)S(1)}, u32[]{:S(2)}, u32[]{:S(2)}) %collective-permute-start.44) | collective-permute-done | bytes 786464 | tf_op jit(solution)/shard_map/ffn_forward/ppermute | solution.py:40
  284.6 5.8 collective-permute-done.47
  294.7 7.2 %collective-permute-done.53 = bf16[128,1536]{1,0:T(8,128)(2,1)S(1)} collective-permute-done((bf16[128,1536]{1,0:T(8,128)(2,1)S(1)}, bf16[128,1536]{1,0:T(8,128)(2,1)S(1)}, u32[]{:S(2)}, u32[]{:S(2)}) %collective-permute-start.53) | collective-permute-done | bytes 393248 | tf_op jit(solution)/shard_map/ffn_backward/ppermute | solution.py:40
  310.3 6.4 %collective-permute-done.54 = bf16[128,1536]{1,0:T(8,128)(2,1)} collective-permute-done((bf16[128,1536]{1,0:T(8,128)(2,1)}, bf16[128,1536]{1,0:T(8,128)(2,1)}, u32[]{:S(2)}, u32[]{:S(2)}) %collective-permute-start.54) | collective-permute-done | bytes 393248 | tf_op jit(solution)/shard_map/ffn_backward/ppermute | solution.py:40
  318.6 5.0 multiply_convert_fusion.3
  327.3 3.6 convolution_add_fusion.1
  330.9 2.4 multiply_convert_fusion.1
  341.0 4.9 convolution_convert_fusion
  346.0 7.7 %convolution_convert_fusion.2 = bf16[1536,1024]{1,0:T(8,128)(2,1)} fusion(bf16[1024,1536]{1,0:T(8,128)(2,1)} %copy-done.51, bf16[512,1024]{1,0:T(8,128)(2,1)} %copy-done.80, bf16[512,1024]{1,0:T(8,128)(2,1)} %copy-done.76), kind=kOutput, calls=%fused_computation.28 | convolution fusion | flops 3226992640 | bytes 8388608 | tf_op jit(solution)/shard_map/ffn_weight_gradients/dot_general | solution.py:23
  358.5 4.9 convolution_convert_fusion.1
  365.3 6.0 collective-permute-done.58
  374.9 2.3 convolution_convert_fusion.4
  377.2 4.0 reshape.291
  383.5 2.5 fusion.63
  408.5 7.8 %pad_maximum_fusion = f32[1536,3200]{0,1:T(8,128)} fusion(f32[1536,128]{0,1:T(8,128)S(1)} %select_maximum_fusion, f32[1536,768]{0,1:T(8,128)S(1)} %fusion.116, f32[1536,768]{0,1:T(8,128)S(1)} %fusion.119, f32[1536,1536]{0,1:T(8,128)S(1)} %fusion.68), kind=kLoop, calls=%fused_computation.1 | loop fusion | flops 14745600 | bytes 39321600 | tf_op jit(solution)/shard_map/attention_weight_gradients/concatenate | solution.py:439
  416.3 20.1 %copy.104 = f32[1536,3200]{1,0:T(8,128)} copy(f32[1536,3200]{0,1:T(8,128)} %pad_maximum_fusion) | data formatting | bytes 39321600 | tf_op jit(solution)/shard_map/attention_weight_gradients/concatenate | solution.py:439
  436.4 6.7 %fusion.1 = bf16[4,2,2,48,3200]{4,3,2,1,0:T(8,128)(2,1)} fusion(f32[4,2,2,2,48,3200]{5,4,3,2,1,0:T(8,128)} %bitcast.512, s32[]{:T(128)S(6)} %select_n.233), kind=kLoop, calls=%fused_computation.19 | loop fusion | bytes 9830404 | tf_op jit(solution)/shard_map/attention_weight_gradients/convert_element_type | solution.py:154
  448.4 3.3 pad_maximum_fusion.1
  452.6 2.8 collective-permute-done.51
  455.4 3.8 collective-permute-start.52
  459.2 4.2 bitcast_add_fusion.1
  469.6 6.5 %collective-permute-done.73 = bf16[2,2,48,1536]{3,2,0,1:T(8,128)(2,1)S(1)} collective-permute-done((bf16[2,2,48,1536]{3,2,0,1:T(8,128)(2,1)S(1)}, bf16[2,2,48,1536]{3,2,0,1:T(8,128)(2,1)S(1)}, u32[]{:S(2)}, u32[]{:S(2)}) %collective-permute-start.73) | collective-permute-done | bytes 589856 | tf_op jit(solution)/shard_map/attention_weight_gradients/ppermute | solution.py:40
  477.7 5.9 collective-permute-done.75
  485.0 10.1 %bitcast_add_fusion = f32[4,2,2,48,3200]{4,3,2,1,0:T(8,128)} fusion(bf16[4,2,2,48,3200]{4,3,2,1,0:T(8,128)(2,1)} %collective-permute-done.61, f32[4,2,2,2,48,3200]{5,4,3,2,1,0:T(8,128)} %bitcast.513, s32[]{:T(128)S(6)} %select_n.230), kind=kLoop, calls=%fused_computation.2 | loop fusion | flops 4915200 | bytes 24576004 | tf_op jit(solution)/shard_map/attention_weight_gradients/add | solution.py:155
  495.1 4.7 fusion.196
  501.1 3.7 collective-permute-start.77
  507.1 15.5 %collective-permute-done.62 = bf16[2,2,48,3200]{3,2,0,1:T(8,128)(2,1)S(1)} collective-permute-done((bf16[2,2,48,3200]{3,2,0,1:T(8,128)(2,1)S(1)}, bf16[2,2,48,3200]{3,2,0,1:T(8,128)(2,1)S(1)}, u32[]{:S(2)}, u32[]{:S(2)}) %collective-permute-start.62) | collective-permute-done | bytes 1228832 | tf_op jit(solution)/shard_map/attention_weight_gradients/ppermute | solution.py:40
  525.0 8.2 %collective-permute-done.64 = bf16[2,2,48,3200]{3,2,1,0:T(8,128)(2,1)S(1)} collective-permute-done((bf16[2,2,48,3200]{3,2,1,0:T(8,128)(2,1)S(1)}, bf16[2,2,48,3200]{3,2,1,0:T(8,128)(2,1)S(1)}, u32[]{:S(2)}, u32[]{:S(2)}) %collective-permute-start.64) | collective-permute-done | bytes 1228832 | tf_op jit(solution)/shard_map/attention_weight_gradients/ppermute | solution.py:40
  534.7 5.2 collective-permute-done.63
  540.0 3.9 collective-permute-done.65
  548.6 2.3 collective-permute-done.66
  551.1 4.4 collective-permute-start.67
  556.4 2.8 collective-permute-start.79
  561.1 6.0 collective-permute-start.68
  571.4 4.5 collective-permute-done.71
  584.4 4.8 dynamic_update_slice.148
  589.4 4.8 dynamic_update_slice.149
  594.4 4.8 dynamic_update_slice.150
  599.4 4.8 dynamic_update_slice.151
  (534 shorter events, 204.0 us)
Async XLA Ops:
  7.2 253.2 %all-gather.2.cloned.1.call-start = ((), (), s32[]{:S(2)}) async-start(), calls=%async_computation.2 | async-start | bytes 3538944 | tf_op jit(solution)/shard_map/ffn_weights_along_z/all_gather | solution.py:326
  7.2 22.9 %collective-permute-start.15 = (bf16[48,1536]{1,0:T(8,128)(2,1)}, bf16[48,1536]{1,0:T(8,128)(2,1)}, u32[]{:S(2)}, u32[]{:S(2)}) collective-permute-start(bf16[48,1536]{1,0:T(8,128)(2,1)} %param.18), channel_id=1, source_target_pairs={{0,8},{1,9},{2,10},{3,11},{4,12},{5,13},{6,14},{7,15},{8,16},{9,17... | collective-permute-start | bytes 442376 | tf_op jit(solution)/shard_map/attention_weights/ppermute | solution.py:50
  13.0 19.4 %collective-permute-start.18 = (bf16[48,1536]{1,0:T(8,128)(2,1)}, bf16[48,1536]{1,0:T(8,128)(2,1)}, u32[]{:S(2)}, u32[]{:S(2)}) collective-permute-start(bf16[48,1536]{1,0:T(8,128)(2,1)} %param.18), channel_id=1, source_target_pairs={{8,0},{9,1},{10,2},{11,3},{12,4},{13,5},{14,6},{15,7},{16,8},{17,9... | collective-permute-start | bytes 442376 | tf_op jit(solution)/shard_map/attention_weights/ppermute | solution.py:50
  16.0 57.7 %collective-permute-start.3 = (bf16[48,3200]{1,0:T(8,128)(2,1)S(1)}, bf16[48,3200]{1,0:T(8,128)(2,1)}, u32[]{:S(2)}, u32[]{:S(2)}) collective-permute-start(bf16[48,3200]{1,0:T(8,128)(2,1)S(1)} %fusion.131), channel_id=1, source_target_pairs={{8,0},{9,1},{10,2},{11,3},{12,4},{13,5},{14,6},{15,7},{16,8},{17,9... | collective-permute-start | bytes 921608 | tf_op jit(solution)/shard_map/attention_weights/ppermute | solution.py:50
  17.3 57.7 %collective-permute-start = (bf16[48,3200]{1,0:T(8,128)(2,1)S(1)}, bf16[48,3200]{1,0:T(8,128)(2,1)}, u32[]{:S(2)}, u32[]{:S(2)}) collective-permute-start(bf16[48,3200]{1,0:T(8,128)(2,1)S(1)} %fusion.131), channel_id=1, source_target_pairs={{0,8},{1,9},{2,10},{3,11},{4,12},{5,13},{6,14},{7,15},{8,16},{9,17... | collective-permute-start | bytes 921608 | tf_op jit(solution)/shard_map/attention_weights/ppermute | solution.py:50
  23.3 545.9 %reduce-scatter.5.cloned.1.call-start = ((), (), s32[]{:S(2)}) async-start(), calls=%async_computation.4 | async-start | bytes 3538944 | tf_op jit(solution)/shard_map/ffn_weight_gradients/reduce_scatter | solution.py:382
  30.1 9.9 %collective-permute-start.33 = (bf16[2,48,1024]{2,1,0:T(8,128)(2,1)S(1)}, bf16[2,48,1024]{2,1,0:T(8,128)(2,1)S(1)}, u32[]{:S(2)}, u32[]{:S(2)}) collective-permute-start(bf16[2,48,1024]{2,1,0:T(8,128)(2,1)S(1)} %reshape.266), channel_id=1, source_target_pairs={{0,4},{1,5},{2,6},{3,7},{4,0},{5,1},{6,2},{7,3},{8,12},{9,13},{10,... | collective-permute-start | bytes 589832 | tf_op jit(solution)/shard_map/ffn_weights_to_columns/ppermute | solution.py:40
  31.6 9.6 %collective-permute-start.16 = (bf16[48,1536]{1,0:T(8,128)(2,1)}, bf16[48,1536]{1,0:T(8,128)(2,1)S(1)}, u32[]{:S(2)}, u32[]{:S(2)}) collective-permute-start(bf16[48,1536]{1,0:T(8,128)(2,1)} %collective-permute-done.15), channel_id=1, source_target_pairs={{8,16},{9,17},{10,18},{11,19},{12,20},{13,21},{14,22},{15,23},{16,... | collective-permute-start | bytes 442376 | tf_op jit(solution)/shard_map/attention_weights/ppermute | solution.py:50
  32.3 34.7 %collective-permute-start.34 = (bf16[2,48,1024]{2,1,0:T(8,128)(2,1)S(1)}, bf16[2,48,1024]{2,1,0:T(8,128)(2,1)S(1)}, u32[]{:S(2)}, u32[]{:S(2)}) collective-permute-start(bf16[2,48,1024]{2,1,0:T(8,128)(2,1)S(1)} %reshape.267), channel_id=1, source_target_pairs={{0,6},{1,7},{2,4},{3,5},{4,2},{5,3},{6,0},{7,1},{8,14},{9,15},{10,... | collective-permute-start | bytes 589832 | tf_op jit(solution)/shard_map/ffn_weights_to_columns/ppermute | solution.py:40
  40.0 12.5 %collective-permute-start.19 = (bf16[48,1536]{1,0:T(8,128)(2,1)}, bf16[48,1536]{1,0:T(8,128)(2,1)S(1)}, u32[]{:S(2)}, u32[]{:S(2)}) collective-permute-start(bf16[48,1536]{1,0:T(8,128)(2,1)} %collective-permute-done.18), channel_id=1, source_target_pairs={{8,0},{9,1},{10,2},{11,3},{12,4},{13,5},{14,6},{15,7},{16,8},{17,9... | collective-permute-start | bytes 442376 | tf_op jit(solution)/shard_map/attention_weights/ppermute | solution.py:50
  41.3 12.4 %collective-permute-start.17 = (bf16[48,1536]{1,0:T(8,128)(2,1)S(1)}, bf16[48,1536]{1,0:T(8,128)(2,1)S(1)}, u32[]{:S(2)}, u32[]{:S(2)}) collective-permute-start(bf16[48,1536]{1,0:T(8,128)(2,1)S(1)} %collective-permute-done.16), channel_id=1, source_target_pairs={{16,24},{17,25},{18,26},{19,27},{20,28},{21,29},{22,30},{23,31}} | collective-permute-start | bytes 442376 | tf_op jit(solution)/shard_map/attention_weights/ppermute | solution.py:50
  52.4 12.9 %collective-permute-start.20 = (bf16[48,1536]{1,0:T(8,128)(2,1)S(1)}, bf16[48,1536]{1,0:T(8,128)(2,1)S(1)}, u32[]{:S(2)}, u32[]{:S(2)}) collective-permute-start(bf16[48,1536]{1,0:T(8,128)(2,1)S(1)} %collective-permute-done.19), channel_id=1, source_target_pairs={{8,0},{9,1},{10,2},{11,3},{12,4},{13,5},{14,6},{15,7}} | collective-permute-start | bytes 442376 | tf_op jit(solution)/shard_map/attention_weights/ppermute | solution.py:50
  65.5 11.7 %collective-permute-start.21 = (bf16[2,48,1536]{2,1,0:T(8,128)(2,1)S(1)}, bf16[2,48,1536]{2,1,0:T(8,128)(2,1)S(1)}, u32[]{:S(2)}, u32[]{:S(2)}) collective-permute-start(bf16[2,48,1536]{2,1,0:T(8,128)(2,1)S(1)} %get-tuple-element.70), channel_id=1, source_target_pairs={{0,2},{1,3},{2,0},{3,1},{4,6},{5,7},{6,4},{7,5},{8,10},{9,11},{10,... | collective-permute-start | bytes 884744 | tf_op jit(solution)/shard_map/attention_weights/ppermute | solution.py:40
  67.0 59.5 %collective-permute-start.38 = (bf16[2,4,48,1024]{3,2,1,0:T(8,128)(2,1)S(1)}, bf16[2,4,48,1024]{3,2,1,0:T(8,128)(2,1)}, u32[]{:S(2)}, u32[]{:S(2)}) collective-permute-start(bf16[2,4,48,1024]{3,2,1,0:T(8,128)(2,1)S(1)} %bitcast_dynamic-update-slice_fusion.28), channel_id=1, source_target_pairs={{8,0},{9,1},{10,2},{11,3},{12,4},{13,5},{14,6},{15,7},{16,8},{17,9... | collective-permute-start | bytes 2359304 | tf_op jit(solution)/shard_map/ffn_weights_along_z/ppermute | solution.py:50
  68.3 58.3 %collective-permute-start.35 = (bf16[2,4,48,1024]{3,2,1,0:T(8,128)(2,1)S(1)}, bf16[2,4,48,1024]{3,2,1,0:T(8,128)(2,1)}, u32[]{:S(2)}, u32[]{:S(2)}) collective-permute-start(bf16[2,4,48,1024]{3,2,1,0:T(8,128)(2,1)S(1)} %bitcast_dynamic-update-slice_fusion.28), channel_id=1, source_target_pairs={{0,8},{1,9},{2,10},{3,11},{4,12},{5,13},{6,14},{7,15},{8,16},{9,17... | collective-permute-start | bytes 2359304 | tf_op jit(solution)/shard_map/ffn_weights_along_z/ppermute | solution.py:50
  73.8 20.6 %collective-permute-start.4 = (bf16[48,3200]{1,0:T(8,128)(2,1)}, bf16[48,3200]{1,0:T(8,128)(2,1)S(1)}, u32[]{:S(2)}, u32[]{:S(2)}) collective-permute-start(bf16[48,3200]{1,0:T(8,128)(2,1)} %collective-permute-done.3), channel_id=1, source_target_pairs={{8,0},{9,1},{10,2},{11,3},{12,4},{13,5},{14,6},{15,7},{16,8},{17,9... | collective-permute-start | bytes 921608 | tf_op jit(solution)/shard_map/attention_weights/ppermute | solution.py:50
  75.1 19.3 %collective-permute-start.1 = (bf16[48,3200]{1,0:T(8,128)(2,1)}, bf16[48,3200]{1,0:T(8,128)(2,1)S(1)}, u32[]{:S(2)}, u32[]{:S(2)}) collective-permute-start(bf16[48,3200]{1,0:T(8,128)(2,1)} %collective-permute-done), channel_id=1, source_target_pairs={{8,16},{9,17},{10,18},{11,19},{12,20},{13,21},{14,22},{15,23},{16,... | collective-permute-start | bytes 921608 | tf_op jit(solution)/shard_map/attention_weights/ppermute | solution.py:50
  77.2 18.5 %collective-permute-start.22 = (bf16[2,48,1536]{2,1,0:T(8,128)(2,1)S(1)}, bf16[2,48,1536]{2,1,0:T(8,128)(2,1)S(1)}, u32[]{:S(2)}, u32[]{:S(2)}) collective-permute-start(bf16[2,48,1536]{2,1,0:T(8,128)(2,1)S(1)} %get-tuple-element.69), channel_id=1, source_target_pairs={{0,4},{1,5},{2,6},{3,7},{4,0},{5,1},{6,2},{7,3},{8,12},{9,13},{10,... | collective-permute-start | bytes 884744 | tf_op jit(solution)/shard_map/attention_weights/ppermute | solution.py:40
  94.4 28.9 %collective-permute-start.25 = (bf16[4,48,1536]{2,1,0:T(8,128)(2,1)}, bf16[4,48,1536]{2,1,0:T(8,128)(2,1)}, u32[]{:S(2)}, u32[]{:S(2)}) collective-permute-start(bf16[4,48,1536]{2,1,0:T(8,128)(2,1)} %get-tuple-element.27), channel_id=1, source_target_pairs={{0,1},{1,0},{2,3},{3,2},{4,5},{5,4},{6,7},{7,6},{8,9},{9,8},{10,11... | collective-permute-start | bytes 1769480 | tf_op jit(solution)/shard_map/attention_weights/ppermute | solution.py:40
  94.4 11.6 %collective-permute-start.5 = (bf16[48,3200]{1,0:T(8,128)(2,1)S(1)}, bf16[48,3200]{1,0:T(8,128)(2,1)S(1)}, u32[]{:S(2)}, u32[]{:S(2)}) collective-permute-start(bf16[48,3200]{1,0:T(8,128)(2,1)S(1)} %collective-permute-done.4), channel_id=1, source_target_pairs={{8,0},{9,1},{10,2},{11,3},{12,4},{13,5},{14,6},{15,7}} | collective-permute-start | bytes 921608 | tf_op jit(solution)/shard_map/attention_weights/ppermute | solution.py:50
  98.2 16.1 %collective-permute-start.23 = (bf16[2,2,48,1536]{3,2,1,0:T(8,128)(2,1)}, bf16[2,2,48,1536]{3,2,1,0:T(8,128)(2,1)}, u32[]{:S(2)}, u32[]{:S(2)}) collective-permute-start(bf16[2,2,48,1536]{3,2,1,0:T(8,128)(2,1)} %pad_maximum_fusion.12), channel_id=1, source_target_pairs={{0,4},{1,5},{2,6},{3,7},{4,0},{5,1},{6,2},{7,3},{8,12},{9,13},{10,... | collective-permute-start | bytes 1769480 | tf_op jit(solution)/shard_map/attention_weights/ppermute | solution.py:40
  106.0 15.4 %collective-permute-start.24 = (bf16[2,2,48,1536]{3,2,1,0:T(8,128)(2,1)}, bf16[2,2,48,1536]{3,2,1,0:T(8,128)(2,1)}, u32[]{:S(2)}, u32[]{:S(2)}) collective-permute-start(bf16[2,2,48,1536]{3,2,1,0:T(8,128)(2,1)} %pad_maximum_fusion.13), channel_id=1, source_target_pairs={{0,2},{1,3},{2,0},{3,1},{4,6},{5,7},{6,4},{7,5},{8,10},{9,11},{10,... | collective-permute-start | bytes 1769480 | tf_op jit(solution)/shard_map/attention_weights/ppermute | solution.py:40
  114.3 13.6 %collective-permute-start.27 = (bf16[2,48,1536]{2,1,0:T(8,128)(2,1)S(1)}, bf16[2,48,1536]{2,1,0:T(8,128)(2,1)S(1)}, u32[]{:S(2)}, u32[]{:S(2)}) collective-permute-start(bf16[2,48,1536]{2,1,0:T(8,128)(2,1)S(1)} %collective-permute-done.22), channel_id=1, source_target_pairs={{0,1},{1,0},{2,3},{3,2},{4,5},{5,4},{6,7},{7,6},{8,9},{9,8},{10,11... | collective-permute-start | bytes 884744 | tf_op jit(solution)/shard_map/attention_weights/ppermute | solution.py:40
  123.4 18.6 %collective-permute-start.7 = (bf16[2,48,3200]{2,1,0:T(8,128)(2,1)S(1)}, bf16[2,48,3200]{2,1,0:T(8,128)(2,1)S(1)}, u32[]{:S(2)}, u32[]{:S(2)}) collective-permute-start(bf16[2,48,3200]{2,1,0:T(8,128)(2,1)S(1)} %copy-done.19), channel_id=1, source_target_pairs={{0,4},{1,5},{2,6},{3,7},{4,0},{5,1},{6,2},{7,3},{8,12},{9,13},{10,... | collective-permute-start | bytes 1843208 | tf_op jit(solution)/shard_map/attention_weights/ppermute | solution.py:40
  125.8 16.1 %collective-permute-start.6 = (bf16[2,48,3200]{2,1,0:T(8,128)(2,1)S(1)}, bf16[2,48,3200]{2,1,0:T(8,128)(2,1)S(1)}, u32[]{:S(2)}, u32[]{:S(2)}) collective-permute-start(bf16[2,48,3200]{2,1,0:T(8,128)(2,1)S(1)} %get-tuple-element.50), channel_id=1, source_target_pairs={{0,2},{1,3},{2,0},{3,1},{4,6},{5,7},{6,4},{7,5},{8,10},{9,11},{10,... | collective-permute-start | bytes 1843208 | tf_op jit(solution)/shard_map/attention_weights/ppermute | solution.py:40
  126.5 51.4 %collective-permute-start.10 = (bf16[4,48,3200]{2,1,0:T(8,128)(2,1)}, bf16[4,48,3200]{2,1,0:T(8,128)(2,1)}, u32[]{:S(2)}, u32[]{:S(2)}) collective-permute-start(bf16[4,48,3200]{2,1,0:T(8,128)(2,1)} %get-tuple-element.25), channel_id=1, source_target_pairs={{0,1},{1,0},{2,3},{3,2},{4,5},{5,4},{6,7},{7,6},{8,9},{9,8},{10,11... | collective-permute-start | bytes 3686408 | tf_op jit(solution)/shard_map/attention_weights/ppermute | solution.py:40
  126.6 22.0 %collective-permute-start.39 = (bf16[2,4,48,1024]{3,2,1,0:T(8,128)(2,1)}, bf16[2,4,48,1024]{3,2,1,0:T(8,128)(2,1)S(1)}, u32[]{:S(2)}, u32[]{:S(2)}) collective-permute-start(bf16[2,4,48,1024]{3,2,1,0:T(8,128)(2,1)} %collective-permute-done.38), channel_id=1, source_target_pairs={{8,0},{9,1},{10,2},{11,3},{12,4},{13,5},{14,6},{15,7},{16,8},{17,9... | collective-permute-start | bytes 2359304 | tf_op jit(solution)/shard_map/ffn_weights_along_z/ppermute | solution.py:50
  127.9 17.9 %collective-permute-start.36 = (bf16[2,4,48,1024]{3,2,1,0:T(8,128)(2,1)}, bf16[2,4,48,1024]{3,2,1,0:T(8,128)(2,1)S(1)}, u32[]{:S(2)}, u32[]{:S(2)}) collective-permute-start(bf16[2,4,48,1024]{3,2,1,0:T(8,128)(2,1)} %collective-permute-done.35), channel_id=1, source_target_pairs={{8,16},{9,17},{10,18},{11,19},{12,20},{13,21},{14,22},{15,23},{16,... | collective-permute-start | bytes 2359304 | tf_op jit(solution)/shard_map/ffn_weights_along_z/ppermute | solution.py:50
  144.9 29.5 %collective-permute-start.8 = (bf16[2,2,48,3200]{3,2,1,0:T(8,128)(2,1)}, bf16[2,2,48,3200]{3,2,1,0:T(8,128)(2,1)S(1)}, u32[]{:S(2)}, u32[]{:S(2)}) collective-permute-start(bf16[2,2,48,3200]{3,2,1,0:T(8,128)(2,1)} %pad_maximum_fusion.4), channel_id=1, source_target_pairs={{0,4},{1,5},{2,6},{3,7},{4,0},{5,1},{6,2},{7,3},{8,12},{9,13},{10,... | collective-permute-start | bytes 3686408 | tf_op jit(solution)/shard_map/attention_weights/ppermute | solution.py:40
  145.8 29.3 %collective-permute-start.9 = (bf16[2,2,48,3200]{3,2,1,0:T(8,128)(2,1)}, bf16[2,2,48,3200]{3,2,1,0:T(8,128)(2,1)}, u32[]{:S(2)}, u32[]{:S(2)}) collective-permute-start(bf16[2,2,48,3200]{3,2,1,0:T(8,128)(2,1)} %pad_maximum_fusion.5), channel_id=1, source_target_pairs={{0,2},{1,3},{2,0},{3,1},{4,6},{5,7},{6,4},{7,5},{8,10},{9,11},{10,... | collective-permute-start | bytes 3686408 | tf_op jit(solution)/shard_map/attention_weights/ppermute | solution.py:40
  148.6 31.4 %collective-permute-start.12 = (bf16[2,48,3200]{2,1,0:T(8,128)(2,1)S(1)}, bf16[2,48,3200]{2,1,0:T(8,128)(2,1)S(1)}, u32[]{:S(2)}, u32[]{:S(2)}) collective-permute-start(bf16[2,48,3200]{2,1,0:T(8,128)(2,1)S(1)} %collective-permute-done.7), channel_id=1, source_target_pairs={{0,1},{1,0},{2,3},{3,2},{4,5},{5,4},{6,7},{7,6},{8,9},{9,8},{10,11... | collective-permute-start | bytes 1843208 | tf_op jit(solution)/shard_map/attention_weights/ppermute | solution.py:40
  148.6 22.7 %collective-permute-start.40 = (bf16[2,4,48,1024]{3,2,1,0:T(8,128)(2,1)S(1)}, bf16[2,4,48,1024]{3,2,1,0:T(8,128)(2,1)S(1)}, u32[]{:S(2)}, u32[]{:S(2)}) collective-permute-start(bf16[2,4,48,1024]{3,2,1,0:T(8,128)(2,1)S(1)} %collective-permute-done.39), channel_id=1, source_target_pairs={{8,0},{9,1},{10,2},{11,3},{12,4},{13,5},{14,6},{15,7}} | collective-permute-start | bytes 2359304 | tf_op jit(solution)/shard_map/ffn_weights_along_z/ppermute | solution.py:50
  174.4 74.5 %collective-permute-start.41 = (bf16[4,2,4,48,1024]{4,3,2,0,1:T(8,128)(2,1)}, bf16[4,2,4,48,1024]{4,3,2,0,1:T(8,128)(2,1)}, u32[]{:S(2)}, u32[]{:S(2)}) collective-permute-start(bf16[4,2,4,48,1024]{4,3,2,0,1:T(8,128)(2,1)} %get-tuple-element.23), channel_id=1, source_target_pairs={{0,1},{1,0},{2,3},{3,2},{4,5},{5,4},{6,7},{7,6},{8,9},{9,8},{10,11... | collective-permute-start | bytes 9437192 | tf_op jit(solution)/shard_map/ffn_weights_along_z/ppermute | solution.py:40
  208.3 11.4 %collective-permute-start.30 = (bf16[128,1536]{1,0:T(8,128)(2,1)S(1)}, bf16[128,1536]{1,0:T(8,128)(2,1)S(1)}, u32[]{:S(2)}, u32[]{:S(2)}) collective-permute-start(bf16[128,1536]{1,0:T(8,128)(2,1)S(1)} %get-tuple-element.92), channel_id=1, source_target_pairs={{0,2},{1,3},{2,0},{3,1},{4,6},{5,7},{6,4},{7,5},{8,10},{9,11},{10,... | collective-permute-start | bytes 1179656 | tf_op jit(solution)/shard_map/ffn_forward/ppermute | solution.py:40
  219.8 12.1 %collective-permute-start.31 = (bf16[128,1536]{1,0:T(8,128)(2,1)S(1)}, bf16[128,1536]{1,0:T(8,128)(2,1)S(1)}, u32[]{:S(2)}, u32[]{:S(2)}) collective-permute-start(bf16[128,1536]{1,0:T(8,128)(2,1)S(1)} %get-tuple-element.90), channel_id=1, source_target_pairs={{0,4},{1,5},{2,6},{3,7},{4,0},{5,1},{6,2},{7,3},{8,12},{9,13},{10,... | collective-permute-start | bytes 1179656 | tf_op jit(solution)/shard_map/ffn_forward/ppermute | solution.py:40
  220.8 26.6 %collective-permute-start.42 = (bf16[256,1536]{1,0:T(8,128)(2,1)S(1)}, bf16[256,1536]{1,0:T(8,128)(2,1)S(1)}, u32[]{:S(2)}, u32[]{:S(2)}) collective-permute-start(bf16[256,1536]{1,0:T(8,128)(2,1)S(1)} %pad_maximum_fusion.7), channel_id=1, source_target_pairs={{0,4},{1,5},{2,6},{3,7},{4,0},{5,1},{6,2},{7,3},{8,12},{9,13},{10,... | collective-permute-start | bytes 2359304 | tf_op jit(solution)/shard_map/ffn_forward/ppermute | solution.py:40
  232.0 16.7 %collective-permute-start.43 = (bf16[256,1536]{1,0:T(8,128)(2,1)S(1)}, bf16[256,1536]{1,0:T(8,128)(2,1)S(1)}, u32[]{:S(2)}, u32[]{:S(2)}) collective-permute-start(bf16[256,1536]{1,0:T(8,128)(2,1)S(1)} %pad_maximum_fusion.8), channel_id=1, source_target_pairs={{0,2},{1,3},{2,0},{3,1},{4,6},{5,7},{6,4},{7,5},{8,10},{9,11},{10,... | collective-permute-start | bytes 2359304 | tf_op jit(solution)/shard_map/ffn_forward/ppermute | solution.py:40
  264.6 16.9 %collective-permute-start.44 = (bf16[256,1536]{1,0:T(8,128)(2,1)S(1)}, bf16[256,1536]{1,0:T(8,128)(2,1)S(1)}, u32[]{:S(2)}, u32[]{:S(2)}) collective-permute-start(bf16[256,1536]{1,0:T(8,128)(2,1)S(1)} %get-tuple-element.61), channel_id=1, source_target_pairs={{0,4},{1,5},{2,6},{3,7},{4,0},{5,1},{6,2},{7,3},{8,12},{9,13},{10,... | collective-permute-start | bytes 2359304 | tf_op jit(solution)/shard_map/ffn_forward/ppermute | solution.py:40
  265.5 16.6 %collective-permute-start.46 = (bf16[256,1536]{1,0:T(8,128)(2,1)S(1)}, bf16[256,1536]{1,0:T(8,128)(2,1)S(1)}, u32[]{:S(2)}, u32[]{:S(2)}) collective-permute-start(bf16[256,1536]{1,0:T(8,128)(2,1)S(1)} %get-tuple-element.62), channel_id=1, source_target_pairs={{0,2},{1,3},{2,0},{3,1},{4,6},{5,7},{6,4},{7,5},{8,10},{9,11},{10,... | collective-permute-start | bytes 2359304 | tf_op jit(solution)/shard_map/ffn_forward/ppermute | solution.py:40
  304.4 12.4 %collective-permute-start.54 = (bf16[128,1536]{1,0:T(8,128)(2,1)}, bf16[128,1536]{1,0:T(8,128)(2,1)}, u32[]{:S(2)}, u32[]{:S(2)}) collective-permute-start(bf16[128,1536]{1,0:T(8,128)(2,1)} %get-tuple-element.76), channel_id=1, source_target_pairs={{0,4},{1,5},{2,6},{3,7},{4,0},{5,1},{6,2},{7,3},{8,12},{9,13},{10,... | collective-permute-start | bytes 1179656 | tf_op jit(solution)/shard_map/ffn_backward/ppermute | solution.py:40
  309.0 21.8 %collective-permute-start.55 = (bf16[256,1536]{1,0:T(8,128)(2,1)S(1)}, bf16[256,1536]{1,0:T(8,128)(2,1)S(1)}, u32[]{:S(2)}, u32[]{:S(2)}) collective-permute-start(bf16[256,1536]{1,0:T(8,128)(2,1)S(1)} %pad_maximum_fusion.9), channel_id=1, source_target_pairs={{0,4},{1,5},{2,6},{3,7},{4,0},{5,1},{6,2},{7,3},{8,12},{9,13},{10,... | collective-permute-start | bytes 2359304 | tf_op jit(solution)/shard_map/ffn_backward/ppermute | solution.py:40
  317.9 13.0 %collective-permute-start.56 = (bf16[256,1536]{1,0:T(8,128)(2,1)S(1)}, bf16[256,1536]{1,0:T(8,128)(2,1)S(1)}, u32[]{:S(2)}, u32[]{:S(2)}) collective-permute-start(bf16[256,1536]{1,0:T(8,128)(2,1)S(1)} %pad_maximum_fusion.10), channel_id=1, source_target_pairs={{0,2},{1,3},{2,0},{3,1},{4,6},{5,7},{6,4},{7,5},{8,10},{9,11},{10,... | collective-permute-start | bytes 2359304 | tf_op jit(solution)/shard_map/ffn_backward/ppermute | solution.py:40
  338.7 16.3 %collective-permute-start.57 = (bf16[256,1536]{1,0:T(8,128)(2,1)}, bf16[256,1536]{1,0:T(8,128)(2,1)}, u32[]{:S(2)}, u32[]{:S(2)}) collective-permute-start(bf16[256,1536]{1,0:T(8,128)(2,1)} %get-tuple-element.59), channel_id=1, source_target_pairs={{0,4},{1,5},{2,6},{3,7},{4,0},{5,1},{6,2},{7,3},{8,12},{9,13},{10,... | collective-permute-start | bytes 2359304 | tf_op jit(solution)/shard_map/ffn_backward/ppermute | solution.py:40
  339.5 15.6 %collective-permute-start.59 = (bf16[256,1536]{1,0:T(8,128)(2,1)}, bf16[256,1536]{1,0:T(8,128)(2,1)}, u32[]{:S(2)}, u32[]{:S(2)}) collective-permute-start(bf16[256,1536]{1,0:T(8,128)(2,1)} %get-tuple-element.60), channel_id=1, source_target_pairs={{0,2},{1,3},{2,0},{3,1},{4,6},{5,7},{6,4},{7,5},{8,10},{9,11},{10,... | collective-permute-start | bytes 2359304 | tf_op jit(solution)/shard_map/ffn_backward/ppermute | solution.py:40
  346.0 232.5 %reduce-scatter.3.cloned.1.call-start = ((), (), s32[]{:S(2)}) async-start(), calls=%async_computation.3 | async-start | bytes 7077888 | tf_op jit(solution)/shard_map/ffn_weight_gradients/reduce_scatter | solution.py:394
  392.0 51.7 %collective-permute-start.48 = (f32[2,128]{1,0:T(2,128)S(1)}, f32[2,128]{1,0:T(2,128)S(1)}, u32[]{:S(2)}, u32[]{:S(2)}) collective-permute-start(f32[2,128]{1,0:T(2,128)S(1)} %broadcast_in_dim.124), channel_id=1, source_target_pairs={{0,1},{1,0},{2,3},{3,2},{4,5},{5,4},{6,7},{7,6},{8,9},{9,8},{10,11... | collective-permute-start | bytes 3080 | tf_op jit(solution)/shard_map/loss/ppermute | solution.py:40
  403.4 55.8 %collective-permute-start.72 = (bf16[4,2,2,48,1536]{4,3,2,1,0:T(8,128)(2,1)}, bf16[4,2,2,48,1536]{4,3,2,1,0:T(8,128)(2,1)}, u32[]{:S(2)}, u32[]{:S(2)}) collective-permute-start(bf16[4,2,2,48,1536]{4,3,2,1,0:T(8,128)(2,1)} %fusion.11), channel_id=1, source_target_pairs={{0,1},{1,0},{2,3},{3,2},{4,5},{5,4},{6,7},{7,6},{8,9},{9,8},{10,11... | collective-permute-start | bytes 7077896 | tf_op jit(solution)/shard_map/attention_weight_gradients/ppermute | solution.py:40
  443.2 41.8 %collective-permute-start.61 = (bf16[4,2,2,48,3200]{4,3,2,1,0:T(8,128)(2,1)}, bf16[4,2,2,48,3200]{4,3,2,1,0:T(8,128)(2,1)}, u32[]{:S(2)}, u32[]{:S(2)}) collective-permute-start(bf16[4,2,2,48,3200]{4,3,2,1,0:T(8,128)(2,1)} %fusion.1), channel_id=1, source_target_pairs={{0,1},{1,0},{2,3},{3,2},{4,5},{5,4},{6,7},{7,6},{8,9},{9,8},{10,11... | collective-permute-start | bytes 14745608 | tf_op jit(solution)/shard_map/attention_weight_gradients/ppermute | solution.py:40
  455.4 10.8 %collective-permute-start.52 = (f32[2,128]{1,0:T(2,128)S(1)}, f32[2,128]{1,0:T(2,128)S(1)}, u32[]{:S(2)}, u32[]{:S(2)}) collective-permute-start(f32[2,128]{1,0:T(2,128)S(1)} %add.444), channel_id=1, source_target_pairs={{0,16},{1,17},{2,18},{3,19},{4,20},{5,21},{6,22},{7,23},{8,24},{9,... | collective-permute-start | bytes 3080 | tf_op jit(solution)/shard_map/loss/ppermute | solution.py:40
  463.8 12.3 %collective-permute-start.73 = (bf16[2,2,48,1536]{3,2,0,1:T(8,128)(2,1)S(1)}, bf16[2,2,48,1536]{3,2,0,1:T(8,128)(2,1)S(1)}, u32[]{:S(2)}, u32[]{:S(2)}) collective-permute-start(bf16[2,2,48,1536]{3,2,0,1:T(8,128)(2,1)S(1)} %fusion.111), channel_id=1, source_target_pairs={{0,4},{1,5},{2,6},{3,7},{4,0},{5,1},{6,2},{7,3},{8,12},{9,13},{10,... | collective-permute-start | bytes 1769480 | tf_op jit(solution)/shard_map/attention_weight_gradients/ppermute | solution.py:40
  468.1 15.5 %collective-permute-start.75 = (bf16[2,2,48,1536]{3,2,1,0:T(8,128)(2,1)S(1)}, bf16[2,2,48,1536]{3,2,1,0:T(8,128)(2,1)S(1)}, u32[]{:S(2)}, u32[]{:S(2)}) collective-permute-start(bf16[2,2,48,1536]{3,2,1,0:T(8,128)(2,1)S(1)} %fusion.110), channel_id=1, source_target_pairs={{0,2},{1,3},{2,0},{3,1},{4,6},{5,7},{6,4},{7,5},{8,10},{9,11},{10,... | collective-permute-start | bytes 1769480 | tf_op jit(solution)/shard_map/attention_weight_gradients/ppermute | solution.py:40
  476.3 24.6 %collective-permute-start.74 = (bf16[2,48,1536]{2,1,0:T(8,128)(2,1)S(1)}, bf16[2,48,1536]{2,1,0:T(8,128)(2,1)S(1)}, u32[]{:S(2)}, u32[]{:S(2)}) collective-permute-start(bf16[2,48,1536]{2,1,0:T(8,128)(2,1)S(1)} %fusion.134), channel_id=1, source_target_pairs={{0,2},{1,3},{2,0},{3,1},{4,6},{5,7},{6,4},{7,5},{8,10},{9,11},{10,... | collective-permute-start | bytes 884744 | tf_op jit(solution)/shard_map/attention_weight_gradients/ppermute | solution.py:40
  483.8 17.2 %collective-permute-start.76 = (bf16[2,48,1536]{2,1,0:T(8,128)(2,1)S(1)}, bf16[2,48,1536]{2,1,0:T(8,128)(2,1)S(1)}, u32[]{:S(2)}, u32[]{:S(2)}) collective-permute-start(bf16[2,48,1536]{2,1,0:T(8,128)(2,1)S(1)} %fusion.135), channel_id=1, source_target_pairs={{0,4},{1,5},{2,6},{3,7},{4,0},{5,1},{6,2},{7,3},{8,12},{9,13},{10,... | collective-permute-start | bytes 884744 | tf_op jit(solution)/shard_map/attention_weight_gradients/ppermute | solution.py:40
  500.0 22.6 %collective-permute-start.62 = (bf16[2,2,48,3200]{3,2,0,1:T(8,128)(2,1)S(1)}, bf16[2,2,48,3200]{3,2,0,1:T(8,128)(2,1)S(1)}, u32[]{:S(2)}, u32[]{:S(2)}) collective-permute-start(bf16[2,2,48,3200]{3,2,0,1:T(8,128)(2,1)S(1)} %fusion.62), channel_id=1, source_target_pairs={{0,4},{1,5},{2,6},{3,7},{4,0},{5,1},{6,2},{7,3},{8,12},{9,13},{10,... | collective-permute-start | bytes 3686408 | tf_op jit(solution)/shard_map/attention_weight_gradients/ppermute | solution.py:40
  501.1 45.3 %collective-permute-start.77 = (bf16[48,1536]{1,0:T(8,128)(2,1)S(1)}, bf16[48,1536]{1,0:T(8,128)(2,1)S(1)}, u32[]{:S(2)}, u32[]{:S(2)}) collective-permute-start(bf16[48,1536]{1,0:T(8,128)(2,1)S(1)} %get-tuple-element.67), channel_id=1, source_target_pairs={{0,8},{1,9},{2,10},{3,11},{4,12},{5,13},{6,14},{7,15}} | collective-permute-start | bytes 442376 | tf_op jit(solution)/shard_map/attention_weight_gradients/ppermute | solution.py:61
  504.8 41.6 %collective-permute-start.80 = (bf16[48,1536]{1,0:T(8,128)(2,1)S(1)}, bf16[48,1536]{1,0:T(8,128)(2,1)S(1)}, u32[]{:S(2)}, u32[]{:S(2)}) collective-permute-start(bf16[48,1536]{1,0:T(8,128)(2,1)S(1)} %get-tuple-element.68), channel_id=1, source_target_pairs={{24,16},{25,17},{26,18},{27,19},{28,20},{29,21},{30,22},{31,23}} | collective-permute-start | bytes 442376 | tf_op jit(solution)/shard_map/attention_weight_gradients/ppermute | solution.py:61
  505.7 27.6 %collective-permute-start.64 = (bf16[2,2,48,3200]{3,2,1,0:T(8,128)(2,1)S(1)}, bf16[2,2,48,3200]{3,2,1,0:T(8,128)(2,1)S(1)}, u32[]{:S(2)}, u32[]{:S(2)}) collective-permute-start(bf16[2,2,48,3200]{3,2,1,0:T(8,128)(2,1)S(1)} %fusion.61), channel_id=1, source_target_pairs={{0,2},{1,3},{2,0},{3,1},{4,6},{5,7},{6,4},{7,5},{8,10},{9,11},{10,... | collective-permute-start | bytes 3686408 | tf_op jit(solution)/shard_map/attention_weight_gradients/ppermute | solution.py:40
  522.8 17.0 %collective-permute-start.63 = (bf16[2,48,3200]{2,1,0:T(8,128)(2,1)S(1)}, bf16[2,48,3200]{2,1,0:T(8,128)(2,1)S(1)}, u32[]{:S(2)}, u32[]{:S(2)}) collective-permute-start(bf16[2,48,3200]{2,1,0:T(8,128)(2,1)S(1)} %fusion.75), channel_id=1, source_target_pairs={{0,2},{1,3},{2,0},{3,1},{4,6},{5,7},{6,4},{7,5},{8,10},{9,11},{10,... | collective-permute-start | bytes 1843208 | tf_op jit(solution)/shard_map/attention_weight_gradients/ppermute | solution.py:40
  533.6 10.2 %collective-permute-start.65 = (bf16[2,48,3200]{2,1,0:T(8,128)(2,1)S(1)}, bf16[2,48,3200]{2,1,0:T(8,128)(2,1)S(1)}, u32[]{:S(2)}, u32[]{:S(2)}) collective-permute-start(bf16[2,48,3200]{2,1,0:T(8,128)(2,1)S(1)} %fusion.76), channel_id=1, source_target_pairs={{0,4},{1,5},{2,6},{3,7},{4,0},{5,1},{6,2},{7,3},{8,12},{9,13},{10,... | collective-permute-start | bytes 1843208 | tf_op jit(solution)/shard_map/attention_weight_gradients/ppermute | solution.py:40
  551.1 9.7 %collective-permute-start.67 = (bf16[48,3200]{1,0:T(8,128)(2,1)S(1)}, bf16[48,3200]{1,0:T(8,128)(2,1)S(1)}, u32[]{:S(2)}, u32[]{:S(2)}) collective-permute-start(bf16[48,3200]{1,0:T(8,128)(2,1)S(1)} %get-tuple-element.45), channel_id=1, source_target_pairs={{0,8},{1,9},{2,10},{3,11},{4,12},{5,13},{6,14},{7,15},{8,16},{9,17... | collective-permute-start | bytes 921608 | tf_op jit(solution)/shard_map/attention_weight_gradients/ppermute | solution.py:61
  556.4 12.0 %collective-permute-start.79 = (bf16[48,1536]{1,0:T(8,128)(2,1)S(1)}, bf16[48,1536]{1,0:T(8,128)(2,1)S(1)}, u32[]{:S(2)}, u32[]{:S(2)}) collective-permute-start(bf16[48,1536]{1,0:T(8,128)(2,1)S(1)} %get-tuple-element.63), channel_id=1, source_target_pairs={{0,8},{1,9},{2,10},{3,11},{4,12},{5,13},{6,14},{7,15},{8,16},{9,17... | collective-permute-start | bytes 442376 | tf_op jit(solution)/shard_map/attention_weight_gradients/ppermute | solution.py:61
  561.1 10.3 %collective-permute-start.68 = (bf16[48,3200]{1,0:T(8,128)(2,1)S(1)}, bf16[48,3200]{1,0:T(8,128)(2,1)S(1)}, u32[]{:S(2)}, u32[]{:S(2)}) collective-permute-start(bf16[48,3200]{1,0:T(8,128)(2,1)S(1)} %get-tuple-element.43), channel_id=1, source_target_pairs={{0,8},{1,9},{2,10},{3,11},{4,12},{5,13},{6,14},{7,15},{8,16},{9,17... | collective-permute-start | bytes 921608 | tf_op jit(solution)/shard_map/attention_weight_gradients/ppermute | solution.py:61
  579.8 19.4 %collective-permute-start.85 = (bf16[2,48,1024]{2,1,0:T(8,128)(2,1)S(1)}, bf16[2,48,1024]{2,1,0:T(8,128)(2,1)S(1)}, u32[]{:S(2)}, u32[]{:S(2)}) collective-permute-start(bf16[2,48,1024]{2,1,0:T(8,128)(2,1)S(1)} %get-tuple-element.81), channel_id=1, source_target_pairs={{0,6},{1,7},{2,4},{3,5},{4,2},{5,3},{6,0},{7,1},{8,14},{9,15},{10,... | collective-permute-start | bytes 589832 | tf_op jit(solution)/shard_map/ffn_weight_gradients/ppermute | solution.py:40
  581.8 12.4 %collective-permute-start.84 = (bf16[2,48,1024]{2,1,0:T(8,128)(2,1)S(1)}, bf16[2,48,1024]{2,1,0:T(8,128)(2,1)S(1)}, u32[]{:S(2)}, u32[]{:S(2)}) collective-permute-start(bf16[2,48,1024]{2,1,0:T(8,128)(2,1)S(1)} %get-tuple-element.82), channel_id=1, source_target_pairs={{0,4},{1,5},{2,6},{3,7},{4,0},{5,1},{6,2},{7,3},{8,12},{9,13},{10,... | collective-permute-start | bytes 589832 | tf_op jit(solution)/shard_map/ffn_weight_gradients/ppermute | solution.py:40
  (113 other events, 1198.9 us)
Sparse Core Ops, SparseCore 0:
  23.4 42.1 all-gather.1
  346.1 42.3 reduce-scatter.4
  451.8 75.0 reduce-scatter.2

commit v2 on v1

v2 whole, which is shorter than its diff:
```python
import math

import jax
import jax.numpy as jnp
from jax import lax
from jax.sharding import PartitionSpec as P

QUERY_HEAD_COUNT = 16
KEY_VALUE_HEADS = 8
HEAD_SIZE = 96
SEQ = 128
EPSILON = 1e-05
ROPE_BASE = 100000.0
MASK_FILL = -1e30
LANES = 128

BF = jnp.bfloat16
F32 = jnp.float32


def dot(a, b, dims):
    return lax.dot_general(a, b, (dims, ((), ())), preferred_element_type=F32)


def mm(a, b):
    return dot(a, b, ((1,), (0,)))


def mm_t(a, b):
    return dot(a, b, ((1,), (1,)))


def t_mm(a, b):
    return dot(a, b, ((0,), (0,)))


def swap(value, mask):
    n = lax.axis_size("dp")
    return lax.ppermute(value, "dp", [(i, i ^ mask) for i in range(n)])


def column_groups():
    n = lax.axis_size("dp")
    return [[8 * z + 2 * p + c for z in range(n // 8)] for p in range(4) for c in range(2)]


def z_pieces(value, z):
    planes = lax.axis_size("dp") // 8
    if planes != 4:
        whole = lax.all_gather(value, "dp", axis_index_groups=column_groups(), axis=0)
        return [(whole, 0)]
    return [(value[None], z)] + [(swap(value, 8 * k)[None], z ^ k) for k in (1, 2, 3)]


def z_reduce(parts, z):
    planes = lax.axis_size("dp") // 8
    if planes != 4:
        return lax.psum_scatter(
            parts.astype(BF), "dp", axis_index_groups=column_groups(), scatter_dimension=0
        ).astype(F32)
    came = [swap(pick(parts, z ^ k, 0).astype(BF), 8 * k) for k in (3, 2, 1)]
    own = pick(parts, z, 0)
    for piece in came:
        own = own + piece.astype(F32)
    return own


def place(out, piece, where):
    return lax.dynamic_update_slice(out, piece, where)


def pick(parts, index, axis):
    return lax.dynamic_index_in_dim(parts, index, axis, keepdims=False)


def both(first, second):
    return lax.optimization_barrier((first, second))


def plane_reduce(parts, place_bits):
    z, y, x, c = place_bits
    half = parts.shape[0] // 2
    a, b = parts[:half], parts[half:]
    came_a, came_b = both(
        swap(pick(a, 1 - y, 1).astype(BF), 4), swap(pick(b, 1 - x, 2).astype(BF), 2)
    )
    a = pick(a, y, 1) + came_a.astype(F32)
    b = pick(b, x, 2) + came_b.astype(F32)
    came_a, came_b = both(
        swap(pick(a, 1 - x, 1).astype(BF), 2), swap(pick(b, 1 - y, 1).astype(BF), 4)
    )
    a = pick(a, x, 1) + came_a.astype(F32)
    b = pick(b, y, 1) + came_b.astype(F32)
    return z_reduce(jnp.concatenate([a, b]), z)


def core_first(count, rows):
    order = jnp.arange(count)
    per_core = count // 2
    core, rest = order // per_core, order % per_core
    source = (rest // rows * 2 + core) * rows + rest % rows
    return (jnp.arange(count)[:, None] == source[None, :]).astype(BF)


def core_halves(values, c):
    width = values.shape[1] // 2
    return (
        lax.dynamic_slice_in_dim(values, c * width, width, 1),
        lax.dynamic_slice_in_dim(values, (1 - c) * width, width, 1),
    )


def core_gradient(features, grads, c):
    mine, theirs = core_halves(features, c)
    came = swap(t_mm(theirs, grads).astype(BF), 1)
    return t_mm(mine, grads) + came.astype(F32)


def split_gather(rows):
    half = rows.shape[0] // 2
    a, b = rows[:half], rows[half:]
    a_x, b_y = both(swap(a, 2), swap(b, 4))
    a_far, b_far = both(
        swap(jnp.concatenate([a, a_x]), 4), swap(jnp.concatenate([b, b_y]), 2)
    )
    return (jnp.concatenate([a, a_x, b, b_y]), jnp.concatenate([a_far, b_far]))


def split_reduce(near, far):
    two = far.shape[0] // 2
    one = two // 2
    low = far.astype(BF)
    came_a, came_b = both(swap(low[:two], 4), swap(low[two:], 2))
    a = near[:two] + came_a.astype(F32)
    b = near[two:] + came_b.astype(F32)
    came_a, came_b = both(swap(a[one:].astype(BF), 2), swap(b[one:].astype(BF), 4))
    return jnp.concatenate([a[:one] + came_a.astype(F32), b[:one] + came_b.astype(F32)])


def total_of(value):
    n = lax.axis_size("dp")
    mask = 1
    while mask < n:
        value = value + swap(value, mask)
        mask *= 2
    return value


def scatter_gains(partial, position):
    n = lax.axis_size("dp")
    rows = partial.shape[1] // n
    return lax.dynamic_slice_in_dim(total_of(partial), position * rows, rows, 1)


def rotation_tables(length, width):
    half_width = width // 2
    position = jnp.arange(length, dtype=F32)[:, None]
    freq_rate = ROPE_BASE ** (-2.0 * jnp.arange(half_width, dtype=F32) / width)
    angle_table = position * freq_rate[None, :]
    return (jnp.cos(angle_table)[:, None, :], jnp.sin(angle_table)[:, None, :])


def turn(heads_in, cosine_lookup, sine_lookup):
    half_width = heads_in.shape[-1] // 2
    left_part = heads_in[..., :half_width]
    right_part = heads_in[..., half_width:]
    return jnp.concatenate(
        [
            left_part * cosine_lookup - right_part * sine_lookup,
            right_part * cosine_lookup + left_part * sine_lookup,
        ],
        axis=-1,
    )


def norm_rows(field_in, gain_vec):
    inv_scale = lax.rsqrt(jnp.mean(field_in * field_in, axis=-1, keepdims=True) + EPSILON)
    return (field_in * inv_scale * gain_vec, inv_scale)


def norm_back(upstream, field_in, inv_scale, gain_vec):
    gain_grad = jnp.sum(upstream * field_in * inv_scale, axis=0)
    scaled_up = upstream * gain_vec
    field_grad = inv_scale * scaled_up - field_in * inv_scale**3 * jnp.mean(
        scaled_up * field_in, axis=-1, keepdims=True
    )
    return (gain_grad, field_grad)


def probabilities(query_heads, key_heads):
    score_scale = 1.0 / math.sqrt(HEAD_SIZE)
    raw_scores = (
        jnp.einsum("bqhrd,bkhd->bhrqk", query_heads, key_heads, preferred_element_type=F32)
        * score_scale
    )
    causal = jnp.arange(SEQ)[:, None] >= jnp.arange(SEQ)[None, :]
    scores = jnp.where(causal, raw_scores, MASK_FILL)
    row_max = jnp.max(scores, axis=-1, keepdims=True)
    weights = jnp.exp(scores - row_max)
    return weights / jnp.sum(weights, axis=-1, keepdims=True)


def ffn_forward(rows, w_both, w_down):
    pre = mm(rows, w_both)
    units = pre.shape[1] // 2
    hidden = (jax.nn.silu(pre[:, :units]) * pre[:, units:]).astype(BF)
    return (mm(hidden, w_down), pre, hidden)


def ffn_backward(grad_low, pre, w_both, w_down):
    grad_hidden = mm_t(grad_low, w_down)
    units = pre.shape[1] // 2
    gate_pre, up_pre = pre[:, :units], pre[:, units:]
    gate_sigmoid = jax.nn.sigmoid(gate_pre)
    grad_gate = grad_hidden * up_pre * gate_sigmoid * (1.0 + gate_pre * (1.0 - gate_sigmoid))
    grad_up = grad_hidden * gate_pre * gate_sigmoid
    grads = jnp.concatenate([grad_gate.astype(BF), grad_up.astype(BF)], axis=1)
    return (mm_t(grads, w_both), grads)


def body(
    tokens,
    teacher,
    valid_mask,
    w_query,
    key_weight_matrix,
    value_weight_matrix,
    w_output,
    w_gate,
    w_up,
    w_down,
    attn_gain,
    ffn_gain,
):
    n = lax.axis_size("dp")
    planes = n // 8
    position = lax.axis_index("dp")
    c, x, y, z = position % 2, position // 2 % 2, position // 4 % 2, position // 8
    bits = (z, y, x, c)
    p = position // 2 % 4
    rows = w_query.shape[0]
    width = w_query.shape[1]
    kv_width = key_weight_matrix.shape[1]
    ff_rows = w_down.shape[0]
    ff = w_gate.shape[1]
    count = tokens.shape[0]
    sequences = count // SEQ
    groups = QUERY_HEAD_COUNT // KEY_VALUE_HEADS
    score_scale = 1.0 / math.sqrt(HEAD_SIZE)
    cosine_lookup, sine_lookup = rotation_tables(SEQ, HEAD_SIZE)

    with jax.named_scope("attention_weights"):
        gains = jnp.stack([attn_gain, ffn_gain], axis=1)
        gains = jnp.pad(gains, ((0, 0), (0, LANES - 2)))
        local = jnp.concatenate(
            [w_query, key_weight_matrix, value_weight_matrix, w_output, gains], axis=1
        )
        gathered = lax.all_gather(local, "dp", axis=0, tiled=True)

    part = 2 * ff_rows
    units = planes * part

    with jax.named_scope("ffn_weights_to_columns"):
        gate_cut = w_gate.reshape(rows, planes, 4, part)
        up_cut = w_up.reshape(rows, planes, 4, part)

        def columns_for(r):
            gate = pick(gate_cut, p ^ r, 2).reshape(rows, units)
            up = pick(up_cut, p ^ r, 2).reshape(rows, units)
            return jnp.concatenate([gate, up], axis=1)

        by_source = jnp.zeros((4, rows, 2 * units), BF)
        for r in (3, 1, 2, 0):
            piece = columns_for(r)
            if r:
                piece = swap(piece, r << 1)
            by_source = place(by_source, piece[None], (p ^ r, 0, 0))

    with jax.named_scope("ffn_weights_along_z"):
        wb = jnp.zeros((planes, 4, 2, rows, 2 * units), BF)
        for piece, at in z_pieces(by_source, z):
            other = swap(piece, 1)
            wb = place(wb, piece[:, :, None], (at, 0, c, 0, 0))
            wb = place(wb, other[:, :, None], (at, 0, 1 - c, 0, 0))
        wb = wb.reshape(n * rows, 2 * units)
        wd = jnp.zeros((planes, 2, ff_rows, width), BF)
        for piece, at in z_pieces(w_down, z):
            other = swap(piece, 1)
            wd = place(wd, piece[:, None], (at, c, 0, 0))
            wd = place(wd, other[:, None], (at, 1 - c, 0, 0))
        wd = wd.reshape(units, width)

    with jax.named_scope("attention_forward"):
        wide = width + 2 * kv_width
        wqkv = gathered[:, :wide]
        wo = gathered[:, wide : wide + width]
        gain_in = gathered[:, wide + width].astype(F32)
        gain_mid = gathered[:, wide + width + 1].astype(F32)
        inputs_f = tokens.astype(F32)
        normed, inv_attn = norm_rows(inputs_f, gain_in)
        normed_in = normed.astype(BF)
        heads = (sequences, SEQ, QUERY_HEAD_COUNT, HEAD_SIZE)
        kv_heads = (sequences, SEQ, KEY_VALUE_HEADS, HEAD_SIZE)
        grouped = (sequences, SEQ, KEY_VALUE_HEADS, groups, HEAD_SIZE)
        raw = mm(normed_in, wqkv)
        query = turn(raw[:, :width].reshape(heads), cosine_lookup, sine_lookup)
        query = query.astype(BF).reshape(grouped)
        key = raw[:, width : width + kv_width].reshape(kv_heads)
        key = turn(key, cosine_lookup, sine_lookup).astype(BF)
        value = raw[:, width + kv_width :].astype(BF).reshape(kv_heads)
        probs = probabilities(query, key)
        probs_low = probs.astype(BF)
        mixed = jnp.einsum("bhrqk,bkhd->bqhrd", probs_low, value, preferred_element_type=F32)
        mixed = mixed.reshape(count, width).astype(BF)
        hidden_res = inputs_f + mm(mixed, wo)
        normed_two, inv_ffn = norm_rows(hidden_res, gain_mid)
        normed_mid = normed_two.astype(BF)

    with jax.named_scope("ffn_forward"):
        near, far = split_gather(normed_mid)
        y_near, pre_near, hid_near = ffn_forward(near, wb, wd)
        y_far, pre_far, hid_far = ffn_forward(far, wb, wd)
        result = hidden_res + split_reduce(y_near, y_far)
        out_act = result.astype(BF)

    with jax.named_scope("loss"):
        mask_f = valid_mask.astype(F32)
        grad_out = (result - teacher.astype(F32)) * mask_f[:, None]
        sums = jnp.stack([jnp.sum(grad_out * grad_out), jnp.sum(mask_f)])
        sums = total_of(jnp.broadcast_to(sums[:, None], (2, LANES)))
        loss = sums[0, 0] / (sums[1, 0] * width)

    with jax.named_scope("ffn_backward"):
        grad_low = grad_out.astype(BF)
        d_near, d_far = split_gather(grad_low)
        m_near, g_near = ffn_backward(d_near, pre_near, wb, wd)
        m_far, g_far = ffn_backward(d_far, pre_far, wb, wd)
        grad_mid = split_reduce(m_near, m_far)

    with jax.named_scope("ffn_weight_gradients"):
        by_core = core_first(width, rows)
        hid = jnp.concatenate([hid_near, hid_far])
        d_all = jnp.concatenate([d_near, d_far])
        grad_down = t_mm(hid, d_all).reshape(planes, 2, ff_rows, width)
        came = swap(pick(grad_down, 1 - c, 1).astype(BF), 1)
        grad_down = z_reduce(pick(grad_down, c, 1) + came.astype(F32), z)
        mid_all = mm(jnp.concatenate([near, far]), by_core).astype(BF)
        g_all = jnp.concatenate([g_near, g_far])
        g_both = core_gradient(mid_all, g_all, c)
        g_both = z_reduce(g_both.reshape(planes, 4, rows, 2 * units), z).astype(BF)
        came = [pick(g_both, p, 0)]
        for r in (1, 2, 3):
            came.append(swap(pick(g_both, p ^ r, 0), r << 1))
        natural = []
        for q in range(4):
            piece = came[3]
            for r in (0, 1, 2):
                piece = jnp.where(p == (q ^ r), came[r], piece)
            natural.append(piece.astype(F32))
        grad_gate = jnp.concatenate(
            [natural[q][:, k * part : (k + 1) * part] for k in range(planes) for q in range(4)],
            axis=1,
        )
        grad_up = jnp.concatenate(
            [
                natural[q][:, units + k * part : units + (k + 1) * part]
                for k in range(planes)
                for q in range(4)
            ],
            axis=1,
        )

    with jax.named_scope("attention_backward"):
        grad_gain_mid, grad_res = norm_back(grad_mid, hidden_res, inv_ffn, gain_mid)
        grad_res = grad_out + grad_res
        res_low = grad_res.astype(BF)
        grad_mixed = mm_t(res_low, wo).astype(BF).reshape(grouped)
        grad_probs = jnp.einsum(
            "bqhrd,bkhd->bhrqk", grad_mixed, value, preferred_element_type=F32
        )
        grad_scores = probs * (grad_probs - jnp.sum(probs * grad_probs, axis=-1, keepdims=True))
        grad_scores = grad_scores.astype(BF)
        grad_query = score_scale * jnp.einsum(
            "bhrqk,bkhd->bqhrd", grad_scores, key, preferred_element_type=F32
        )
        grad_key = score_scale * jnp.einsum(
            "bhrqk,bqhrd->bkhd", grad_scores, query, preferred_element_type=F32
        )
        grad_value = jnp.einsum(
            "bhrqk,bqhrd->bkhd", probs_low, grad_mixed, preferred_element_type=F32
        )
        query_back = turn(grad_query.reshape(heads), cosine_lookup, -sine_lookup)
        query_back = query_back.reshape(count, width).astype(BF)
        key_back = turn(grad_key, cosine_lookup, -sine_lookup).reshape(count, kv_width).astype(BF)
        value_back = grad_value.reshape(count, kv_width).astype(BF)
        grad_raw = jnp.concatenate([query_back, key_back, value_back], axis=1)
        grad_in = mm_t(grad_raw, wqkv)
        grad_gain_in, grad_tokens = norm_back(grad_in, inputs_f, inv_attn, gain_in)
        input_grad = (grad_res + grad_tokens).astype(BF)

    with jax.named_scope("attention_weight_gradients"):
        shape = (planes, 2, 2, rows, -1)
        mixed_by_core = mm(mixed, by_core).astype(BF)
        g_wo = core_gradient(mixed_by_core, res_low, c)
        g_wo = plane_reduce(g_wo.reshape(shape), bits)
        normed_by_core = mm(normed_in, by_core).astype(BF)
        g_raw = core_gradient(normed_by_core, grad_raw, c)
        g_raw = plane_reduce(g_raw.reshape(shape), bits)
        g_wq = g_raw[:, :width]
        g_wk = g_raw[:, width : width + kv_width]
        g_wv = g_raw[:, width + kv_width :]

    with jax.named_scope("gain_gradients"):
        g_gains = jnp.stack([grad_gain_in, grad_gain_mid])
        g_gains = scatter_gains(g_gains, position)

    return (
        out_act,
        loss,
        input_grad,
        g_wq,
        g_wk,
        g_wv,
        g_wo,
        grad_gate,
        grad_up,
        grad_down,
        g_gains[0],
        g_gains[1],
    )


def solution(mesh):
    wide, flat = P("dp", None), P("dp")
    in_specs = (wide, wide, flat) + (wide,) * 7 + (flat, flat)
    out_specs = (wide, P(), wide) + (wide,) * 7 + (flat, flat)
    return jax.shard_map(body, mesh=mesh, in_specs=in_specs, out_specs=out_specs, check_vma=False)
```

time: 624 us -> 625 us (level)
  waiting for transfers between devices: 220 us -> 332 us
  local copies, waits for them, and re-layouts: 127 us -> 56.2 us
  starting transfers between devices: 110 us -> 73.7 us
  other arithmetic: 59.2 us -> 28.4 us
  matrix products: 80.1 us -> 108 us
    ppermute x56 -> x70, waiting for transfers between devices: 152 us -> 319 us  [swap(): return lax.ppermute(value, 'dp', [(i, i ^ mask) for i in range(n)])]
    ppermute x30 -> x0, waiting for transfers between devices: 67.6 us -> none  [the longest x18 60.5 us: shift(): return lax.ppermute(value, 'dp', pairs)]
    ppermute x30 -> x0, starting transfers between devices: 58.3 us -> none  [the longest x18 33 us: shift(): return lax.ppermute(value, 'dp', pairs)]
    dynamic_update_slice x38 -> x19, local copies, waits for them, and re-layouts: 38.5 us -> 8.05 us  [place(): return lax.dynamic_update_slice(out, piece, where)]
    dot_general x27 -> x22, matrix products: 72.1 us -> 100 us  [dot(): return lax.dot_general(a, b, (dims, ((), ())), preferred_element_type=F32)]
    ppermute x56 -> x70, starting transfers between devices: 51.6 us -> 73.6 us  [swap(): return lax.ppermute(value, 'dp', [(i, i ^ mask) for i in range(n)])]
    concatenate x2 -> x4, local copies, waits for them, and re-layouts: 20.3 us -> 0.76 us  [the longest x1 0.64 us: body(): jnp.concatenate([natural[q][:, units + k * part:units + (k + 1) * part] f...]
    all_gather x1, waiting for transfers between devices: 0.01 us -> 12.8 us  [body(): gathered = lax.all_gather(local, 'dp', axis=0, tiled=True)]
  transfers between devices with their start and end apart: 89 -> 71, of which waited for: 36 -> 39; matrix products, arithmetic and copies ran while one was open for 37% -> 22% of each run, Pallas kernels for 0% -> 0%
where the time goes in v2:
time: 625 us; the launch traced here: 617 us
  waiting for transfers between devices  332 us (53%)
  matrix products  108 us (17%)
  starting transfers between devices  73.7 us (12%)
  local copies, waits for them, and re-layouts  56.2 us (9%)
  other arithmetic  28.4 us (5%)
  between operations  18.7 us (3%)
    ppermute x70, waiting for transfers between devices, swap(): return lax.ppermute(value, 'dp', [(i, i ^ mask) for i in range(n)])  319 us
    dot_general x22, matrix products, dot(): return lax.dot_general(a, b, (dims, ((), ())), preferred_element_type=F32)  100 us
    ppermute x70, starting transfers between devices, swap(): return lax.ppermute(value, 'dp', [(i, i ^ mask) for i in range(n)])  73.6 us
    unnamed x150, local copies, waits for them, and re-layouts  15.4 us
    all_gather x1, waiting for transfers between devices, body(): gathered = lax.all_gather(local, 'dp', axis=0, tiled=True)  12.8 us
  transfers between devices with their start and end apart: 71, of which 39 were waited for; matrix products, arithmetic and copies ran while one was open for 22% of the time, Pallas kernels for 0%

profile of v2, /device:TPU:0, one launch (start us, length us, event | category | flops | bytes accessed | tf_op | source)
XLA Modules:
  0.0 616.7 jit_solution(9327427217987128407)
XLA Ops:
  12.5 3.1 collective-permute-start.13
  15.6 2.5 collective-permute-start.17
  19.8 4.9 dynamic-slice_reduce_fusion
  33.1 2.0 collective-permute-done.2
  35.7 5.2 collective-permute-done.3
  41.1 3.6 collective-permute-start.10
  44.7 3.4 broadcast_in_dim.132
  49.4 47.7 %collective-permute-done.15 = bf16[128,1536]{1,0:T(8,128)(2,1)S(1)} collective-permute-done((bf16[128,1536]{1,0:T(8,128)(2,1)}, bf16[128,1536]{1,0:T(8,128)(2,1)S(1)}, u32[]{:S(2)}, u32[]{:S(2)}) %collective-permute-start.15) | collective-permute-done | bytes 393248 | tf_op jit(solution)/shard_map/ffn_weights_along_z/ppermute | solution.py:39
  101.1 70.2 %collective-permute-done.8 = bf16[4,48,2048]{2,1,0:T(8,128)(2,1)S(1)} collective-permute-done((bf16[4,48,2048]{2,1,0:T(8,128)(2,1)S(1)}, bf16[4,48,2048]{2,1,0:T(8,128)(2,1)S(1)}, u32[]{:S(2)}, u32[]{:S(2)}) %collective-permute-start.8) | collective-permute-done | bytes 786464 | tf_op jit(solution)/shard_map/ffn_weights_along_z/ppermute | solution.py:39
  179.5 12.8 %all-gather.2.cloned.1.call-done = bf16[1536,4736]{1,0:T(8,128)(2,1)} async-done(((bf16[48,4736]{1,0:T(8,128)(2,1)}), bf16[1536,4736]{1,0:T(8,128)(2,1)}) %all-gather.2.cloned.1.call-update) | async-done | bytes 14549008 | tf_op jit(solution)/shard_map/attention_weights/all_gather | solution.py:258
  193.9 5.7 fusion.6
  206.7 2.0 fusion.227
  208.8 1.7 fusion.81
  211.4 3.8 multiply_reduce_fusion.3
  218.6 3.0 fusion.19
  221.6 3.0 fusion.18
  224.6 2.3 collective-permute-done.1
  230.4 5.7 fusion.49
  236.0 11.0 %collective-permute-done.20 = bf16[256,1536]{1,0:T(8,128)(2,1)S(1)} collective-permute-done((bf16[256,1536]{1,0:T(8,128)(2,1)S(1)}, bf16[256,1536]{1,0:T(8,128)(2,1)S(1)}, u32[]{:S(2)}, u32[]{:S(2)}) %collective-permute-start.20) | collective-permute-done | bytes 786464 | tf_op jit(solution)/shard_map/ffn_forward/ppermute | solution.py:39
  248.1 5.6 fusion.57
  255.7 1.8 convolution_convert_fusion.4
  259.5 1.8 fusion.228
  261.3 13.7 %collective-permute-done.22 = bf16[256,1536]{1,0:T(8,128)(2,1)S(1)} collective-permute-done((bf16[256,1536]{1,0:T(8,128)(2,1)S(1)}, bf16[256,1536]{1,0:T(8,128)(2,1)S(1)}, u32[]{:S(2)}, u32[]{:S(2)}) %collective-permute-start.22) | collective-permute-done | bytes 786464 | tf_op jit(solution)/shard_map/ffn_forward/ppermute | solution.py:39
  278.3 5.5 collective-permute-done.24
  288.8 6.5 %fusion.15 = bf16[1024,1536]{1,0:T(8,128)(2,1)} fusion(bf16[1024,1536]{1,0:T(8,128)(2,1)S(1)} %constant_dynamic-update-slice_fusion.5, s32[1536]{0:T(1024)S(1)} %copy-done.38), kind=kOutput, calls=%fused_computation.21 | convolution fusion | flops 4835770368 | bytes 6297600 | tf_op jit(solution)/shard_map/ffn_weight_gradients/dot_general | solution.py:22
  295.4 3.4 multiply_convert_fusion.3
  301.1 5.8 fusion.23
  306.8 6.7 %collective-permute-done.32 = bf16[256,1536]{1,0:T(8,128)(2,1)S(1)} collective-permute-done((bf16[256,1536]{1,0:T(8,128)(2,1)S(1)}, bf16[256,1536]{1,0:T(8,128)(2,1)S(1)}, u32[]{:S(2)}, u32[]{:S(2)}) %collective-permute-start.32) | collective-permute-done | bytes 786464 | tf_op jit(solution)/shard_map/ffn_backward/ppermute | solution.py:39
  314.1 2.3 multiply_convert_fusion.1
  316.6 6.9 %convolution_convert_fusion.3 = bf16[512,1536]{1,0:T(8,128)(2,1)S(1)} fusion(bf16[1536,2048]{1,0:T(8,128)(2,1)} %bitcast.32, bf16[512,1024]{1,0:T(8,128)(2,1)S(1)} %get-tuple-element.82, bf16[512,1024]{1,0:T(8,128)(2,1)S(1)} %get-tuple-element.81), kind=kOutput, calls=%fused_computation.40 | convolution fusion | flops 3226206208 | bytes 9961472 | tf_op jit(solution)/shard_map/ffn_backward/dot_general | solution.py:22
  325.5 3.6 fusion.30
  330.6 8.4 %collective-permute-done.35 = bf16[256,1536]{1,0:T(8,128)(2,1)S(1)} collective-permute-done((bf16[256,1536]{1,0:T(8,128)(2,1)S(1)}, bf16[256,1536]{1,0:T(8,128)(2,1)S(1)}, u32[]{:S(2)}, u32[]{:S(2)}) %collective-permute-start.35) | collective-permute-done | bytes 786464 | tf_op jit(solution)/shard_map/ffn_backward/ppermute | solution.py:39
  341.7 2.0 collective-permute-start.36
  343.8 19.3 %convolution_convert_fusion.1 = bf16[768,2048]{1,0:T(8,128)(2,1)} fusion(bf16[1024,1536]{1,0:T(8,128)(2,1)S(1)} %copy-done.46, s32[]{:T(128)S(6)} %select_n.298, bf16[512,1024]{1,0:T(8,128)(2,1)S(1)} %get-tuple-element.82, bf16[512,1024]{1,0:T(8,128)(2,1)S(1)} %get-tuple-element.81, bf16[512,1024]{1,0:T(8,128)(2,1)S(1)} %get-tuple-element.84, ...), kind=kOutput, calls=%fused_computation.36 | convolution fusion | flops 3239575552 | bytes 8912900 | tf_op jit(solution)/shard_map/ffn_weight_gradients/dot_general | solution.py:22
  365.1 4.6 fusion.20
  369.7 4.2 reshape.313
  373.9 2.0 copy.79
  375.9 2.5 fusion.85
  387.3 5.8 fusion.48
  393.4 3.5 collective-permute-done.26
  405.7 1.8 collective-permute-start.68
  409.5 1.8 collective-permute-start.69
  411.2 1.9 bitcast_add_fusion
  413.3 2.5 collective-permute-start.62
  415.8 1.9 collective-permute-start.63
  420.3 7.0 %collective-permute-done.62 = bf16[128,1536]{1,0:T(8,128)(2,1)S(1)} collective-permute-done((bf16[128,1536]{1,0:T(8,128)(2,1)S(1)}, bf16[128,1536]{1,0:T(8,128)(2,1)S(1)}, u32[]{:S(2)}, u32[]{:S(2)}) %collective-permute-start.62) | collective-permute-done | bytes 393248 | tf_op jit(solution)/shard_map/ffn_weight_gradients/ppermute | solution.py:39
  427.3 5.3 collective-permute-done.64
  432.7 13.2 %collective-permute-done.63 = bf16[128,1536]{1,0:T(8,128)(2,1)S(1)} collective-permute-done((bf16[128,1536]{1,0:T(8,128)(2,1)S(1)}, bf16[128,1536]{1,0:T(8,128)(2,1)S(1)}, u32[]{:S(2)}, u32[]{:S(2)}) %collective-permute-start.63) | collective-permute-done | bytes 393248 | tf_op jit(solution)/shard_map/ffn_weight_gradients/ppermute | solution.py:39
  447.0 7.0 %convert_add_fusion.1 = f32[768,2048]{1,0:T(8,128)S(1)} fusion(bf16[768,2048]{1,0:T(8,128)(2,1)} %collective-permute-done.54, bf16[1024,1536]{1,0:T(8,128)(2,1)} %fusion.15, s32[]{:T(128)S(6)} %select_n.297, bf16[512,1024]{1,0:T(8,128)(2,1)} %copy-done.51, bf16[512,1024]{1,0:T(8,128)(2,1)} %copy-done.50, bf16[512,1024]{1,0:T(8,128)(2,1)} %copy-done.49, ...), kind=kOutput, calls=%fused_computation.10 | convolution fusion | flops 3241148416 | bytes 15204356 | tf_op jit(solution)/shard_map/ffn_weight_gradients/dot_general | solution.py:22
  454.3 2.0 collective-permute-start.55
  456.3 2.4 collective-permute-start.56
  461.2 15.4 %collective-permute-done.55 = bf16[4,48,2048]{2,1,0:T(8,128)(2,1)S(1)} collective-permute-done((bf16[4,48,2048]{2,1,0:T(8,128)(2,1)S(1)}, bf16[4,48,2048]{2,1,0:T(8,128)(2,1)S(1)}, u32[]{:S(2)}, u32[]{:S(2)}) %collective-permute-start.55) | collective-permute-done | bytes 786464 | tf_op jit(solution)/shard_map/ffn_weight_gradients/ppermute | solution.py:39
  477.3 17.0 %collective-permute-done.57 = bf16[4,48,2048]{2,1,0:T(8,128)(2,1)S(1)} collective-permute-done((bf16[4,48,2048]{2,1,0:T(8,128)(2,1)S(1)}, bf16[4,48,2048]{2,1,0:T(8,128)(2,1)S(1)}, u32[]{:S(2)}, u32[]{:S(2)}) %collective-permute-start.57) | collective-permute-done | bytes 786464 | tf_op jit(solution)/shard_map/ffn_weight_gradients/ppermute | solution.py:39
  494.3 26.7 %collective-permute-done.56 = bf16[4,48,2048]{2,1,0:T(8,128)(2,1)S(1)} collective-permute-done((bf16[4,48,2048]{2,1,0:T(8,128)(2,1)S(1)}, bf16[4,48,2048]{2,1,0:T(8,128)(2,1)S(1)}, u32[]{:S(2)}, u32[]{:S(2)}) %collective-permute-start.56) | collective-permute-done | bytes 786464 | tf_op jit(solution)/shard_map/ffn_weight_gradients/ppermute | solution.py:39
  521.5 2.2 collective-permute-start.60
  530.3 2.9 collective-permute-start.49
  536.3 1.7 convert_add_fusion
  540.6 2.4 collective-permute-start.39
  549.1 16.0 %collective-permute-done.40 = bf16[2,2,48,3072]{3,2,0,1:T(8,128)(2,1)S(1)} collective-permute-done((bf16[2,2,48,3072]{3,2,0,1:T(8,128)(2,1)S(1)}, bf16[2,2,48,3072]{3,2,0,1:T(8,128)(2,1)S(1)}, u32[]{:S(2)}, u32[]{:S(2)}) %collective-permute-start.40) | collective-permute-done | bytes 1179680 | tf_op jit(solution)/shard_map/attention_weight_gradients/ppermute | solution.py:39
  570.6 3.5 collective-permute-start.53
  574.1 5.3 collective-permute-done.42
  580.7 3.8 collective-permute-start.45
  584.6 9.3 %collective-permute-done.52 = bf16[48,1536]{1,0:T(8,128)(2,1)S(1)} collective-permute-done((bf16[48,1536]{1,0:T(8,128)(2,1)S(1)}, bf16[48,1536]{1,0:T(8,128)(2,1)S(1)}, u32[]{:S(2)}, u32[]{:S(2)}) %collective-permute-start.52) | collective-permute-done | bytes 147488 | tf_op jit(solution)/shard_map/attention_weight_gradients/ppermute | solution.py:39
  594.7 11.9 %collective-permute-done.44 = bf16[48,3072]{1,0:T(8,128)(2,1)S(1)} collective-permute-done((bf16[48,3072]{1,0:T(8,128)(2,1)S(1)}, bf16[48,3072]{1,0:T(8,128)(2,1)S(1)}, u32[]{:S(2)}, u32[]{:S(2)}) %collective-permute-start.44) | collective-permute-done | bytes 294944 | tf_op jit(solution)/shard_map/attention_weight_gradients/ppermute | solution.py:39
  (401 shorter events, 123.4 us)
Async XLA Ops:
  7.2 185.1 %all-gather.2.cloned.1.call-start = ((), (), s32[]{:S(2)}) async-start(), calls=%async_computation | async-start | bytes 15003648 | tf_op jit(solution)/shard_map/attention_weights/all_gather | solution.py:258
  12.5 36.6 %collective-permute-start.13 = (bf16[128,1536]{1,0:T(8,128)(2,1)}, bf16[128,1536]{1,0:T(8,128)(2,1)S(1)}, u32[]{:S(2)}, u32[]{:S(2)}) collective-permute-start(bf16[128,1536]{1,0:T(8,128)(2,1)} %param.21), channel_id=1, source_target_pairs={{0,8},{1,9},{2,10},{3,11},{4,12},{5,13},{6,14},{7,15},{8,0},{9,1},... | collective-permute-start | bytes 1179656 | tf_op jit(solution)/shard_map/ffn_weights_along_z/ppermute | solution.py:39
  15.6 81.8 %collective-permute-start.17 = (bf16[128,1536]{1,0:T(8,128)(2,1)}, bf16[128,1536]{1,0:T(8,128)(2,1)S(1)}, u32[]{:S(2)}, u32[]{:S(2)}) collective-permute-start(bf16[128,1536]{1,0:T(8,128)(2,1)} %param.21), channel_id=1, source_target_pairs={{0,24},{1,25},{2,26},{3,27},{4,28},{5,29},{6,30},{7,31},{8,16},{9,... | collective-permute-start | bytes 1179656 | tf_op jit(solution)/shard_map/ffn_weights_along_z/ppermute | solution.py:39
  18.1 79.1 %collective-permute-start.15 = (bf16[128,1536]{1,0:T(8,128)(2,1)}, bf16[128,1536]{1,0:T(8,128)(2,1)S(1)}, u32[]{:S(2)}, u32[]{:S(2)}) collective-permute-start(bf16[128,1536]{1,0:T(8,128)(2,1)} %param.21), channel_id=1, source_target_pairs={{0,16},{1,17},{2,18},{3,19},{4,20},{5,21},{6,22},{7,23},{8,24},{9,... | collective-permute-start | bytes 1179656 | tf_op jit(solution)/shard_map/ffn_weights_along_z/ppermute | solution.py:39
  24.8 16.2 %collective-permute-start.4 = (bf16[48,2048]{1,0:T(8,128)(2,1)S(1)}, bf16[48,2048]{1,0:T(8,128)(2,1)S(1)}, u32[]{:S(2)}, u32[]{:S(2)}) collective-permute-start(bf16[48,2048]{1,0:T(8,128)(2,1)S(1)} %pad_maximum_fusion.16), channel_id=1, source_target_pairs={{0,4},{1,5},{2,6},{3,7},{4,0},{5,1},{6,2},{7,3},{8,12},{9,13},{10,... | collective-permute-start | bytes 589832 | tf_op jit(solution)/shard_map/ffn_weights_to_columns/ppermute | solution.py:39
  27.1 7.9 %collective-permute-start.2 = (bf16[48,2048]{1,0:T(8,128)(2,1)}, bf16[48,2048]{1,0:T(8,128)(2,1)S(1)}, u32[]{:S(2)}, u32[]{:S(2)}) collective-permute-start(bf16[48,2048]{1,0:T(8,128)(2,1)} %pad_maximum_fusion.14), channel_id=1, source_target_pairs={{0,6},{1,7},{2,4},{3,5},{4,2},{5,3},{6,0},{7,1},{8,14},{9,15},{10,... | collective-permute-start | bytes 589832 | tf_op jit(solution)/shard_map/ffn_weights_to_columns/ppermute | solution.py:39
  35.1 5.9 collective-permute-start.3
  41.0 8.1 %collective-permute-start.12 = (bf16[1,128,1536]{2,1,0:T(8,128)(2,1)S(1)}, bf16[1,128,1536]{2,1,0:T(8,128)(2,1)S(1)}, u32[]{:S(2)}, u32[]{:S(2)}) collective-permute-start(bf16[1,128,1536]{2,1,0:T(8,128)(2,1)S(1)} %bitcast.367), channel_id=1, source_target_pairs={{0,1},{1,0},{2,3},{3,2},{4,5},{5,4},{6,7},{7,6},{8,9},{9,8},{10,11... | collective-permute-start | bytes 1179656 | tf_op jit(solution)/shard_map/ffn_weights_along_z/ppermute | solution.py:39
  41.1 59.8 %collective-permute-start.10 = (bf16[4,48,2048]{2,1,0:T(8,128)(2,1)S(1)}, bf16[4,48,2048]{2,1,0:T(8,128)(2,1)S(1)}, u32[]{:S(2)}, u32[]{:S(2)}) collective-permute-start(bf16[4,48,2048]{2,1,0:T(8,128)(2,1)S(1)} %fusion.153), channel_id=1, source_target_pairs={{0,24},{1,25},{2,26},{3,27},{4,28},{5,29},{6,30},{7,31},{8,16},{9,... | collective-permute-start | bytes 2359304 | tf_op jit(solution)/shard_map/ffn_weights_along_z/ppermute | solution.py:39
  49.1 122.2 %collective-permute-start.8 = (bf16[4,48,2048]{2,1,0:T(8,128)(2,1)S(1)}, bf16[4,48,2048]{2,1,0:T(8,128)(2,1)S(1)}, u32[]{:S(2)}, u32[]{:S(2)}) collective-permute-start(bf16[4,48,2048]{2,1,0:T(8,128)(2,1)S(1)} %fusion.153), channel_id=1, source_target_pairs={{0,16},{1,17},{2,18},{3,19},{4,20},{5,21},{6,22},{7,23},{8,24},{9,... | collective-permute-start | bytes 2359304 | tf_op jit(solution)/shard_map/ffn_weights_along_z/ppermute | solution.py:39
  49.1 48.3 %collective-permute-start.14 = (bf16[1,128,1536]{2,1,0:T(8,128)(2,1)S(1)}, bf16[1,128,1536]{2,1,0:T(8,128)(2,1)S(1)}, u32[]{:S(2)}, u32[]{:S(2)}) collective-permute-start(bf16[1,128,1536]{2,1,0:T(8,128)(2,1)S(1)} %bitcast.370), channel_id=1, source_target_pairs={{0,1},{1,0},{2,3},{3,2},{4,5},{5,4},{6,7},{7,6},{8,9},{9,8},{10,11... | collective-permute-start | bytes 1179656 | tf_op jit(solution)/shard_map/ffn_weights_along_z/ppermute | solution.py:39
  97.1 74.2 %collective-permute-start.6 = (bf16[4,48,2048]{2,1,0:T(8,128)(2,1)S(1)}, bf16[4,48,2048]{2,1,0:T(8,128)(2,1)S(1)}, u32[]{:S(2)}, u32[]{:S(2)}) collective-permute-start(bf16[4,48,2048]{2,1,0:T(8,128)(2,1)S(1)} %fusion.153), channel_id=1, source_target_pairs={{0,8},{1,9},{2,10},{3,11},{4,12},{5,13},{6,14},{7,15},{8,0},{9,1},... | collective-permute-start | bytes 2359304 | tf_op jit(solution)/shard_map/ffn_weights_along_z/ppermute | solution.py:39
  97.4 74.4 %collective-permute-start.5 = (bf16[1,4,48,2048]{3,2,1,0:T(8,128)(2,1)S(1)}, bf16[1,4,48,2048]{3,2,1,0:T(8,128)(2,1)S(1)}, u32[]{:S(2)}, u32[]{:S(2)}) collective-permute-start(bf16[1,4,48,2048]{3,2,1,0:T(8,128)(2,1)S(1)} %bitcast.353), channel_id=1, source_target_pairs={{0,1},{1,0},{2,3},{3,2},{4,5},{5,4},{6,7},{7,6},{8,9},{9,8},{10,11... | collective-permute-start | bytes 2359304 | tf_op jit(solution)/shard_map/ffn_weights_along_z/ppermute | solution.py:39
  100.9 77.7 %collective-permute-start.11 = (bf16[1,4,48,2048]{3,2,1,0:T(8,128)(2,1)S(1)}, bf16[1,4,48,2048]{3,2,1,0:T(8,128)(2,1)S(1)}, u32[]{:S(2)}, u32[]{:S(2)}) collective-permute-start(bf16[1,4,48,2048]{3,2,1,0:T(8,128)(2,1)S(1)} %bitcast.364), channel_id=1, source_target_pairs={{0,1},{1,0},{2,3},{3,2},{4,5},{5,4},{6,7},{7,6},{8,9},{9,8},{10,11... | collective-permute-start | bytes 2359304 | tf_op jit(solution)/shard_map/ffn_weights_along_z/ppermute | solution.py:39
  171.3 5.4 collective-permute-start.9
  215.5 11.3 %collective-permute-start.1 = (bf16[128,1536]{1,0:T(8,128)(2,1)S(1)}, bf16[128,1536]{1,0:T(8,128)(2,1)S(1)}, u32[]{:S(2)}, u32[]{:S(2)}) collective-permute-start(bf16[128,1536]{1,0:T(8,128)(2,1)S(1)} %get-tuple-element.130), channel_id=1, source_target_pairs={{0,4},{1,5},{2,6},{3,7},{4,0},{5,1},{6,2},{7,3},{8,12},{9,13},{10,... | collective-permute-start | bytes 1179656 | tf_op jit(solution)/shard_map/ffn_forward/ppermute | solution.py:39
  217.1 11.0 %collective-permute-start = (bf16[128,1536]{1,0:T(8,128)(2,1)S(1)}, bf16[128,1536]{1,0:T(8,128)(2,1)S(1)}, u32[]{:S(2)}, u32[]{:S(2)}) collective-permute-start(bf16[128,1536]{1,0:T(8,128)(2,1)S(1)} %get-tuple-element.131), channel_id=1, source_target_pairs={{0,2},{1,3},{2,0},{3,1},{4,6},{5,7},{6,4},{7,5},{8,10},{9,11},{10,... | collective-permute-start | bytes 1179656 | tf_op jit(solution)/shard_map/ffn_forward/ppermute | solution.py:39
  228.3 18.7 %collective-permute-start.20 = (bf16[256,1536]{1,0:T(8,128)(2,1)S(1)}, bf16[256,1536]{1,0:T(8,128)(2,1)S(1)}, u32[]{:S(2)}, u32[]{:S(2)}) collective-permute-start(bf16[256,1536]{1,0:T(8,128)(2,1)S(1)} %pad_maximum_fusion.3), channel_id=1, source_target_pairs={{0,2},{1,3},{2,0},{3,1},{4,6},{5,7},{6,4},{7,5},{8,10},{9,11},{10,... | collective-permute-start | bytes 2359304 | tf_op jit(solution)/shard_map/ffn_forward/ppermute | solution.py:39
  229.9 18.3 %collective-permute-start.19 = (bf16[256,1536]{1,0:T(8,128)(2,1)S(1)}, bf16[256,1536]{1,0:T(8,128)(2,1)S(1)}, u32[]{:S(2)}, u32[]{:S(2)}) collective-permute-start(bf16[256,1536]{1,0:T(8,128)(2,1)S(1)} %pad_maximum_fusion.2), channel_id=1, source_target_pairs={{0,4},{1,5},{2,6},{3,7},{4,0},{5,1},{6,2},{7,3},{8,12},{9,13},{10,... | collective-permute-start | bytes 2359304 | tf_op jit(solution)/shard_map/ffn_forward/ppermute | solution.py:39
  257.6 17.4 %collective-permute-start.22 = (bf16[256,1536]{1,0:T(8,128)(2,1)S(1)}, bf16[256,1536]{1,0:T(8,128)(2,1)S(1)}, u32[]{:S(2)}, u32[]{:S(2)}) collective-permute-start(bf16[256,1536]{1,0:T(8,128)(2,1)S(1)} %get-tuple-element.108), channel_id=1, source_target_pairs={{0,2},{1,3},{2,0},{3,1},{4,6},{5,7},{6,4},{7,5},{8,10},{9,11},{10,... | collective-permute-start | bytes 2359304 | tf_op jit(solution)/shard_map/ffn_forward/ppermute | solution.py:39
  258.2 17.1 %collective-permute-start.21 = (bf16[256,1536]{1,0:T(8,128)(2,1)S(1)}, bf16[256,1536]{1,0:T(8,128)(2,1)S(1)}, u32[]{:S(2)}, u32[]{:S(2)}) collective-permute-start(bf16[256,1536]{1,0:T(8,128)(2,1)S(1)} %get-tuple-element.109), channel_id=1, source_target_pairs={{0,4},{1,5},{2,6},{3,7},{4,0},{5,1},{6,2},{7,3},{8,12},{9,13},{10,... | collective-permute-start | bytes 2359304 | tf_op jit(solution)/shard_map/ffn_forward/ppermute | solution.py:39
  276.0 7.8 %collective-permute-start.24 = (bf16[128,1536]{1,0:T(8,128)(2,1)S(1)}, bf16[128,1536]{1,0:T(8,128)(2,1)S(1)}, u32[]{:S(2)}, u32[]{:S(2)}) collective-permute-start(bf16[128,1536]{1,0:T(8,128)(2,1)S(1)} %slice.516), channel_id=1, source_target_pairs={{0,4},{1,5},{2,6},{3,7},{4,0},{5,1},{6,2},{7,3},{8,12},{9,13},{10,... | collective-permute-start | bytes 1179656 | tf_op jit(solution)/shard_map/ffn_forward/ppermute | solution.py:39
  276.8 7.8 %collective-permute-start.23 = (bf16[128,1536]{1,0:T(8,128)(2,1)S(1)}, bf16[128,1536]{1,0:T(8,128)(2,1)S(1)}, u32[]{:S(2)}, u32[]{:S(2)}) collective-permute-start(bf16[128,1536]{1,0:T(8,128)(2,1)S(1)} %slice.517), channel_id=1, source_target_pairs={{0,2},{1,3},{2,0},{3,1},{4,6},{5,7},{6,4},{7,5},{8,10},{9,11},{10,... | collective-permute-start | bytes 1179656 | tf_op jit(solution)/shard_map/ffn_forward/ppermute | solution.py:39
  286.1 9.3 %collective-permute-start.31 = (bf16[128,1536]{1,0:T(8,128)(2,1)S(1)}, bf16[128,1536]{1,0:T(8,128)(2,1)S(1)}, u32[]{:S(2)}, u32[]{:S(2)}) collective-permute-start(bf16[128,1536]{1,0:T(8,128)(2,1)S(1)} %get-tuple-element.124), channel_id=1, source_target_pairs={{0,4},{1,5},{2,6},{3,7},{4,0},{5,1},{6,2},{7,3},{8,12},{9,13},{10,... | collective-permute-start | bytes 1179656 | tf_op jit(solution)/shard_map/ffn_backward/ppermute | solution.py:39
  287.4 8.0 %collective-permute-start.30 = (bf16[128,1536]{1,0:T(8,128)(2,1)S(1)}, bf16[128,1536]{1,0:T(8,128)(2,1)S(1)}, u32[]{:S(2)}, u32[]{:S(2)}) collective-permute-start(bf16[128,1536]{1,0:T(8,128)(2,1)S(1)} %get-tuple-element.125), channel_id=1, source_target_pairs={{0,2},{1,3},{2,0},{3,1},{4,6},{5,7},{6,4},{7,5},{8,10},{9,11},{10,... | collective-permute-start | bytes 1179656 | tf_op jit(solution)/shard_map/ffn_backward/ppermute | solution.py:39
  299.1 14.5 %collective-permute-start.32 = (bf16[256,1536]{1,0:T(8,128)(2,1)S(1)}, bf16[256,1536]{1,0:T(8,128)(2,1)S(1)}, u32[]{:S(2)}, u32[]{:S(2)}) collective-permute-start(bf16[256,1536]{1,0:T(8,128)(2,1)S(1)} %pad_maximum_fusion.4), channel_id=1, source_target_pairs={{0,4},{1,5},{2,6},{3,7},{4,0},{5,1},{6,2},{7,3},{8,12},{9,13},{10,... | collective-permute-start | bytes 2359304 | tf_op jit(solution)/shard_map/ffn_backward/ppermute | solution.py:39
  299.8 14.3 %collective-permute-start.33 = (bf16[256,1536]{1,0:T(8,128)(2,1)S(1)}, bf16[256,1536]{1,0:T(8,128)(2,1)S(1)}, u32[]{:S(2)}, u32[]{:S(2)}) collective-permute-start(bf16[256,1536]{1,0:T(8,128)(2,1)S(1)} %pad_maximum_fusion.5), channel_id=1, source_target_pairs={{0,2},{1,3},{2,0},{3,1},{4,6},{5,7},{6,4},{7,5},{8,10},{9,11},{10,... | collective-permute-start | bytes 2359304 | tf_op jit(solution)/shard_map/ffn_backward/ppermute | solution.py:39
  323.6 15.4 %collective-permute-start.35 = (bf16[256,1536]{1,0:T(8,128)(2,1)S(1)}, bf16[256,1536]{1,0:T(8,128)(2,1)S(1)}, u32[]{:S(2)}, u32[]{:S(2)}) collective-permute-start(bf16[256,1536]{1,0:T(8,128)(2,1)S(1)} %get-tuple-element.106), channel_id=1, source_target_pairs={{0,2},{1,3},{2,0},{3,1},{4,6},{5,7},{6,4},{7,5},{8,10},{9,11},{10,... | collective-permute-start | bytes 2359304 | tf_op jit(solution)/shard_map/ffn_backward/ppermute | solution.py:39
  324.4 15.4 %collective-permute-start.34 = (bf16[256,1536]{1,0:T(8,128)(2,1)S(1)}, bf16[256,1536]{1,0:T(8,128)(2,1)S(1)}, u32[]{:S(2)}, u32[]{:S(2)}) collective-permute-start(bf16[256,1536]{1,0:T(8,128)(2,1)S(1)} %get-tuple-element.107), channel_id=1, source_target_pairs={{0,4},{1,5},{2,6},{3,7},{4,0},{5,1},{6,2},{7,3},{8,12},{9,13},{10,... | collective-permute-start | bytes 2359304 | tf_op jit(solution)/shard_map/ffn_backward/ppermute | solution.py:39
  330.6 80.6 %collective-permute-start.61 = (bf16[4,128,1536]{2,1,0:T(8,128)(2,1)}, bf16[4,128,1536]{2,1,0:T(8,128)(2,1)}, u32[]{:S(2)}, u32[]{:S(2)}) collective-permute-start(bf16[4,128,1536]{2,1,0:T(8,128)(2,1)} %fusion.38), channel_id=1, source_target_pairs={{0,1},{1,0},{2,3},{3,2},{4,5},{5,4},{6,7},{7,6},{8,9},{9,8},{10,11... | collective-permute-start | bytes 4718600 | tf_op jit(solution)/shard_map/ffn_weight_gradients/ppermute | solution.py:39
  340.3 22.8 %collective-permute-start.37 = (bf16[128,1536]{1,0:T(8,128)(2,1)S(1)}, bf16[128,1536]{1,0:T(8,128)(2,1)S(1)}, u32[]{:S(2)}, u32[]{:S(2)}) collective-permute-start(bf16[128,1536]{1,0:T(8,128)(2,1)S(1)} %slice.514), channel_id=1, source_target_pairs={{0,4},{1,5},{2,6},{3,7},{4,0},{5,1},{6,2},{7,3},{8,12},{9,13},{10,... | collective-permute-start | bytes 1179656 | tf_op jit(solution)/shard_map/ffn_backward/ppermute | solution.py:39
  341.7 21.4 %collective-permute-start.36 = (bf16[128,1536]{1,0:T(8,128)(2,1)S(1)}, bf16[128,1536]{1,0:T(8,128)(2,1)S(1)}, u32[]{:S(2)}, u32[]{:S(2)}) collective-permute-start(bf16[128,1536]{1,0:T(8,128)(2,1)S(1)} %slice.515), channel_id=1, source_target_pairs={{0,2},{1,3},{2,0},{3,1},{4,6},{5,7},{6,4},{7,5},{8,10},{9,11},{10,... | collective-permute-start | bytes 1179656 | tf_op jit(solution)/shard_map/ffn_backward/ppermute | solution.py:39
  363.1 83.9 %collective-permute-start.54 = (bf16[768,2048]{1,0:T(8,128)(2,1)}, bf16[768,2048]{1,0:T(8,128)(2,1)}, u32[]{:S(2)}, u32[]{:S(2)}) collective-permute-start(bf16[768,2048]{1,0:T(8,128)(2,1)} %convolution_convert_fusion.1), channel_id=1, source_target_pairs={{0,1},{1,0},{2,3},{3,2},{4,5},{5,4},{6,7},{7,6},{8,9},{9,8},{10,11... | collective-permute-start | bytes 9437192 | tf_op jit(solution)/shard_map/ffn_weight_gradients/ppermute | solution.py:39
  383.2 10.0 %collective-permute-start.25 = (f32[2,128]{1,0:T(2,128)S(1)}, f32[2,128]{1,0:T(2,128)S(1)}, u32[]{:S(2)}, u32[]{:S(2)}) collective-permute-start(f32[2,128]{1,0:T(2,128)S(1)} %broadcast_in_dim.163), channel_id=1, source_target_pairs={{0,1},{1,0},{2,3},{3,2},{4,5},{5,4},{6,7},{7,6},{8,9},{9,8},{10,11... | collective-permute-start | bytes 3080 | tf_op jit(solution)/shard_map/loss/ppermute | solution.py:39
  393.3 4.3 collective-permute-start.65
  400.5 3.8 collective-permute-start.28
  401.4 4.3 collective-permute-start.67
  404.3 4.5 collective-permute-start.29
  409.5 10.1 %collective-permute-start.69 = (f32[2,1536]{1,0:T(2,128)S(1)}, f32[2,1536]{1,0:T(2,128)S(1)}, u32[]{:S(2)}, u32[]{:S(2)}) collective-permute-start(f32[2,1536]{1,0:T(2,128)S(1)} %add.480), channel_id=1, source_target_pairs={{0,16},{1,17},{2,18},{3,19},{4,20},{5,21},{6,22},{7,23},{8,24},{9,... | collective-permute-start | bytes 36872 | tf_op jit(solution)/shard_map/gain_gradients/ppermute | solution.py:39
  413.3 14.0 %collective-permute-start.62 = (bf16[128,1536]{1,0:T(8,128)(2,1)S(1)}, bf16[128,1536]{1,0:T(8,128)(2,1)S(1)}, u32[]{:S(2)}, u32[]{:S(2)}) collective-permute-start(bf16[128,1536]{1,0:T(8,128)(2,1)S(1)} %get-tuple-element.87), channel_id=1, source_target_pairs={{0,24},{1,25},{2,26},{3,27},{4,28},{5,29},{6,30},{7,31},{8,16},{9,... | collective-permute-start | bytes 1179656 | tf_op jit(solution)/shard_map/ffn_weight_gradients/ppermute | solution.py:39
  415.8 16.8 %collective-permute-start.64 = (bf16[128,1536]{1,0:T(8,128)(2,1)S(1)}, bf16[128,1536]{1,0:T(8,128)(2,1)S(1)}, u32[]{:S(2)}, u32[]{:S(2)}) collective-permute-start(bf16[128,1536]{1,0:T(8,128)(2,1)S(1)} %get-tuple-element.88), channel_id=1, source_target_pairs={{0,8},{1,9},{2,10},{3,11},{4,12},{5,13},{6,14},{7,15},{8,0},{9,1},... | collective-permute-start | bytes 1179656 | tf_op jit(solution)/shard_map/ffn_weight_gradients/ppermute | solution.py:39
  415.8 30.0 %collective-permute-start.63 = (bf16[128,1536]{1,0:T(8,128)(2,1)S(1)}, bf16[128,1536]{1,0:T(8,128)(2,1)S(1)}, u32[]{:S(2)}, u32[]{:S(2)}) collective-permute-start(bf16[128,1536]{1,0:T(8,128)(2,1)S(1)} %get-tuple-element.89), channel_id=1, source_target_pairs={{0,16},{1,17},{2,18},{3,19},{4,20},{5,21},{6,22},{7,23},{8,24},{9,... | collective-permute-start | bytes 1179656 | tf_op jit(solution)/shard_map/ffn_weight_gradients/ppermute | solution.py:39
  419.6 39.1 %collective-permute-start.46 = (bf16[768,1536]{1,0:T(8,128)(2,1)S(1)}, bf16[768,1536]{1,0:T(8,128)(2,1)S(1)}, u32[]{:S(2)}, u32[]{:S(2)}) collective-permute-start(bf16[768,1536]{1,0:T(8,128)(2,1)S(1)} %convolution_convert_fusion.2), channel_id=1, source_target_pairs={{0,1},{1,0},{2,3},{3,2},{4,5},{5,4},{6,7},{7,6},{8,9},{9,8},{10,11... | collective-permute-start | bytes 7077896 | tf_op jit(solution)/shard_map/attention_weight_gradients/ppermute | solution.py:39
  427.3 107.7 %collective-permute-start.38 = (bf16[768,3072]{1,0:T(8,128)(2,1)S(1)}, bf16[768,3072]{1,0:T(8,128)(2,1)S(1)}, u32[]{:S(2)}, u32[]{:S(2)}) collective-permute-start(bf16[768,3072]{1,0:T(8,128)(2,1)S(1)} %convolution_convert_fusion), channel_id=1, source_target_pairs={{0,1},{1,0},{2,3},{3,2},{4,5},{5,4},{6,7},{7,6},{8,9},{9,8},{10,11... | collective-permute-start | bytes 14155784 | tf_op jit(solution)/shard_map/attention_weight_gradients/ppermute | solution.py:39
  454.3 22.3 %collective-permute-start.55 = (bf16[4,48,2048]{2,1,0:T(8,128)(2,1)S(1)}, bf16[4,48,2048]{2,1,0:T(8,128)(2,1)S(1)}, u32[]{:S(2)}, u32[]{:S(2)}) collective-permute-start(bf16[4,48,2048]{2,1,0:T(8,128)(2,1)S(1)} %get-tuple-element.78), channel_id=1, source_target_pairs={{0,24},{1,25},{2,26},{3,27},{4,28},{5,29},{6,30},{7,31},{8,16},{9,... | collective-permute-start | bytes 2359304 | tf_op jit(solution)/shard_map/ffn_weight_gradients/ppermute | solution.py:39
  456.3 38.0 %collective-permute-start.57 = (bf16[4,48,2048]{2,1,0:T(8,128)(2,1)S(1)}, bf16[4,48,2048]{2,1,0:T(8,128)(2,1)S(1)}, u32[]{:S(2)}, u32[]{:S(2)}) collective-permute-start(bf16[4,48,2048]{2,1,0:T(8,128)(2,1)S(1)} %get-tuple-element.79), channel_id=1, source_target_pairs={{0,8},{1,9},{2,10},{3,11},{4,12},{5,13},{6,14},{7,15},{8,0},{9,1},... | collective-permute-start | bytes 2359304 | tf_op jit(solution)/shard_map/ffn_weight_gradients/ppermute | solution.py:39
  456.3 64.7 %collective-permute-start.56 = (bf16[4,48,2048]{2,1,0:T(8,128)(2,1)S(1)}, bf16[4,48,2048]{2,1,0:T(8,128)(2,1)S(1)}, u32[]{:S(2)}, u32[]{:S(2)}) collective-permute-start(bf16[4,48,2048]{2,1,0:T(8,128)(2,1)S(1)} %get-tuple-element.80), channel_id=1, source_target_pairs={{0,16},{1,17},{2,18},{3,19},{4,20},{5,21},{6,22},{7,23},{8,24},{9,... | collective-permute-start | bytes 2359304 | tf_op jit(solution)/shard_map/ffn_weight_gradients/ppermute | solution.py:39
  460.0 65.1 %collective-permute-start.48 = (bf16[2,2,48,1536]{3,2,0,1:T(8,128)(2,1)S(1)}, bf16[2,2,48,1536]{3,2,0,1:T(8,128)(2,1)S(1)}, u32[]{:S(2)}, u32[]{:S(2)}) collective-permute-start(bf16[2,2,48,1536]{3,2,0,1:T(8,128)(2,1)S(1)} %fusion.103), channel_id=1, source_target_pairs={{0,2},{1,3},{2,0},{3,1},{4,6},{5,7},{6,4},{7,5},{8,10},{9,11},{10,... | collective-permute-start | bytes 1769480 | tf_op jit(solution)/shard_map/attention_weight_gradients/ppermute | solution.py:39
  476.6 49.3 %collective-permute-start.47 = (bf16[2,2,48,1536]{3,2,0,1:T(8,128)(2,1)S(1)}, bf16[2,2,48,1536]{3,2,0,1:T(8,128)(2,1)S(1)}, u32[]{:S(2)}, u32[]{:S(2)}) collective-permute-start(bf16[2,2,48,1536]{3,2,0,1:T(8,128)(2,1)S(1)} %fusion.102), channel_id=1, source_target_pairs={{0,4},{1,5},{2,6},{3,7},{4,0},{5,1},{6,2},{7,3},{8,12},{9,13},{10,... | collective-permute-start | bytes 1769480 | tf_op jit(solution)/shard_map/attention_weight_gradients/ppermute | solution.py:39
  521.5 8.7 %collective-permute-start.60 = (bf16[48,2048]{1,0:T(8,128)(2,1)S(1)}, bf16[48,2048]{1,0:T(8,128)(2,1)S(1)}, u32[]{:S(2)}, u32[]{:S(2)}) collective-permute-start(bf16[48,2048]{1,0:T(8,128)(2,1)S(1)} %get-tuple-element.126), channel_id=1, source_target_pairs={{0,6},{1,7},{2,4},{3,5},{4,2},{5,3},{6,0},{7,1},{8,14},{9,15},{10,... | collective-permute-start | bytes 589832 | tf_op jit(solution)/shard_map/ffn_weight_gradients/ppermute | solution.py:39
  523.8 10.9 %collective-permute-start.59 = (bf16[48,2048]{1,0:T(8,128)(2,1)S(1)}, bf16[48,2048]{1,0:T(8,128)(2,1)S(1)}, u32[]{:S(2)}, u32[]{:S(2)}) collective-permute-start(bf16[48,2048]{1,0:T(8,128)(2,1)S(1)} %get-tuple-element.127), channel_id=1, source_target_pairs={{0,2},{1,3},{2,0},{3,1},{4,6},{5,7},{6,4},{7,5},{8,10},{9,11},{10,... | collective-permute-start | bytes 589832 | tf_op jit(solution)/shard_map/ffn_weight_gradients/ppermute | solution.py:39
  525.1 9.6 %collective-permute-start.58 = (bf16[48,2048]{1,0:T(8,128)(2,1)S(1)}, bf16[48,2048]{1,0:T(8,128)(2,1)S(1)}, u32[]{:S(2)}, u32[]{:S(2)}) collective-permute-start(bf16[48,2048]{1,0:T(8,128)(2,1)S(1)} %get-tuple-element.128), channel_id=1, source_target_pairs={{0,4},{1,5},{2,6},{3,7},{4,0},{5,1},{6,2},{7,3},{8,12},{9,13},{10,... | collective-permute-start | bytes 589832 | tf_op jit(solution)/shard_map/ffn_weight_gradients/ppermute | solution.py:39
  527.2 20.8 %collective-permute-start.50 = (bf16[2,48,1536]{2,1,0:T(8,128)(2,1)}, bf16[2,48,1536]{2,1,0:T(8,128)(2,1)}, u32[]{:S(2)}, u32[]{:S(2)}) collective-permute-start(bf16[2,48,1536]{2,1,0:T(8,128)(2,1)} %fusion.136), channel_id=1, source_target_pairs={{0,4},{1,5},{2,6},{3,7},{4,0},{5,1},{6,2},{7,3},{8,12},{9,13},{10,... | collective-permute-start | bytes 884744 | tf_op jit(solution)/shard_map/attention_weight_gradients/ppermute | solution.py:39
  530.3 17.7 %collective-permute-start.49 = (bf16[2,48,1536]{2,1,0:T(8,128)(2,1)}, bf16[2,48,1536]{2,1,0:T(8,128)(2,1)}, u32[]{:S(2)}, u32[]{:S(2)}) collective-permute-start(bf16[2,48,1536]{2,1,0:T(8,128)(2,1)} %fusion.135), channel_id=1, source_target_pairs={{0,2},{1,3},{2,0},{3,1},{4,6},{5,7},{6,4},{7,5},{8,10},{9,11},{10,... | collective-permute-start | bytes 884744 | tf_op jit(solution)/shard_map/attention_weight_gradients/ppermute | solution.py:39
  539.6 25.4 %collective-permute-start.40 = (bf16[2,2,48,3072]{3,2,0,1:T(8,128)(2,1)S(1)}, bf16[2,2,48,3072]{3,2,0,1:T(8,128)(2,1)S(1)}, u32[]{:S(2)}, u32[]{:S(2)}) collective-permute-start(bf16[2,2,48,3072]{3,2,0,1:T(8,128)(2,1)S(1)} %fusion.87), channel_id=1, source_target_pairs={{0,2},{1,3},{2,0},{3,1},{4,6},{5,7},{6,4},{7,5},{8,10},{9,11},{10,... | collective-permute-start | bytes 3538952 | tf_op jit(solution)/shard_map/attention_weight_gradients/ppermute | solution.py:39
  540.6 25.9 %collective-permute-start.39 = (bf16[2,2,48,3072]{3,2,0,1:T(8,128)(2,1)S(1)}, bf16[2,2,48,3072]{3,2,0,1:T(8,128)(2,1)S(1)}, u32[]{:S(2)}, u32[]{:S(2)}) collective-permute-start(bf16[2,2,48,3072]{3,2,0,1:T(8,128)(2,1)S(1)} %fusion.86), channel_id=1, source_target_pairs={{0,4},{1,5},{2,6},{3,7},{4,0},{5,1},{6,2},{7,3},{8,12},{9,13},{10,... | collective-permute-start | bytes 3538952 | tf_op jit(solution)/shard_map/attention_weight_gradients/ppermute | solution.py:39
  567.4 12.0 %collective-permute-start.42 = (bf16[2,48,3072]{2,1,0:T(8,128)(2,1)S(1)}, bf16[2,48,3072]{2,1,0:T(8,128)(2,1)S(1)}, u32[]{:S(2)}, u32[]{:S(2)}) collective-permute-start(bf16[2,48,3072]{2,1,0:T(8,128)(2,1)S(1)} %fusion.101), channel_id=1, source_target_pairs={{0,4},{1,5},{2,6},{3,7},{4,0},{5,1},{6,2},{7,3},{8,12},{9,13},{10,... | collective-permute-start | bytes 1769480 | tf_op jit(solution)/shard_map/attention_weight_gradients/ppermute | solution.py:39
  567.7 11.8 %collective-permute-start.41 = (bf16[2,48,3072]{2,1,0:T(8,128)(2,1)S(1)}, bf16[2,48,3072]{2,1,0:T(8,128)(2,1)S(1)}, u32[]{:S(2)}, u32[]{:S(2)}) collective-permute-start(bf16[2,48,3072]{2,1,0:T(8,128)(2,1)S(1)} %fusion.100), channel_id=1, source_target_pairs={{0,2},{1,3},{2,0},{3,1},{4,6},{5,7},{6,4},{7,5},{8,10},{9,11},{10,... | collective-permute-start | bytes 1769480 | tf_op jit(solution)/shard_map/attention_weight_gradients/ppermute | solution.py:39
  569.7 11.0 %collective-permute-start.51 = (bf16[48,1536]{1,0:T(8,128)(2,1)S(1)}, bf16[48,1536]{1,0:T(8,128)(2,1)S(1)}, u32[]{:S(2)}, u32[]{:S(2)}) collective-permute-start(bf16[48,1536]{1,0:T(8,128)(2,1)S(1)} %get-tuple-element.114), channel_id=1, source_target_pairs={{0,24},{1,25},{2,26},{3,27},{4,28},{5,29},{6,30},{7,31},{8,16},{9,... | collective-permute-start | bytes 442376 | tf_op jit(solution)/shard_map/attention_weight_gradients/ppermute | solution.py:39
  570.6 23.3 %collective-permute-start.52 = (bf16[48,1536]{1,0:T(8,128)(2,1)S(1)}, bf16[48,1536]{1,0:T(8,128)(2,1)S(1)}, u32[]{:S(2)}, u32[]{:S(2)}) collective-permute-start(bf16[48,1536]{1,0:T(8,128)(2,1)S(1)} %get-tuple-element.115), channel_id=1, source_target_pairs={{0,16},{1,17},{2,18},{3,19},{4,20},{5,21},{6,22},{7,23},{8,24},{9,... | collective-permute-start | bytes 442376 | tf_op jit(solution)/shard_map/attention_weight_gradients/ppermute | solution.py:39
  570.6 23.3 %collective-permute-start.53 = (bf16[48,1536]{1,0:T(8,128)(2,1)S(1)}, bf16[48,1536]{1,0:T(8,128)(2,1)S(1)}, u32[]{:S(2)}, u32[]{:S(2)}) collective-permute-start(bf16[48,1536]{1,0:T(8,128)(2,1)S(1)} %get-tuple-element.116), channel_id=1, source_target_pairs={{0,8},{1,9},{2,10},{3,11},{4,12},{5,13},{6,14},{7,15},{8,0},{9,1},... | collective-permute-start | bytes 442376 | tf_op jit(solution)/shard_map/attention_weight_gradients/ppermute | solution.py:39
  580.1 14.6 %collective-permute-start.43 = (bf16[48,3072]{1,0:T(8,128)(2,1)S(1)}, bf16[48,3072]{1,0:T(8,128)(2,1)S(1)}, u32[]{:S(2)}, u32[]{:S(2)}) collective-permute-start(bf16[48,3072]{1,0:T(8,128)(2,1)S(1)} %get-tuple-element.95), channel_id=1, source_target_pairs={{0,24},{1,25},{2,26},{3,27},{4,28},{5,29},{6,30},{7,31},{8,16},{9,... | collective-permute-start | bytes 884744 | tf_op jit(solution)/shard_map/attention_weight_gradients/ppermute | solution.py:39
  580.7 25.9 %collective-permute-start.44 = (bf16[48,3072]{1,0:T(8,128)(2,1)S(1)}, bf16[48,3072]{1,0:T(8,128)(2,1)S(1)}, u32[]{:S(2)}, u32[]{:S(2)}) collective-permute-start(bf16[48,3072]{1,0:T(8,128)(2,1)S(1)} %get-tuple-element.96), channel_id=1, source_target_pairs={{0,16},{1,17},{2,18},{3,19},{4,20},{5,21},{6,22},{7,23},{8,24},{9,... | collective-permute-start | bytes 884744 | tf_op jit(solution)/shard_map/attention_weight_gradients/ppermute | solution.py:39
  580.7 25.9 %collective-permute-start.45 = (bf16[48,3072]{1,0:T(8,128)(2,1)S(1)}, bf16[48,3072]{1,0:T(8,128)(2,1)S(1)}, u32[]{:S(2)}, u32[]{:S(2)}) collective-permute-start(bf16[48,3072]{1,0:T(8,128)(2,1)S(1)} %get-tuple-element.97), channel_id=1, source_target_pairs={{0,8},{1,9},{2,10},{3,11},{4,12},{5,13},{6,14},{7,15},{8,0},{9,1},... | collective-permute-start | bytes 884744 | tf_op jit(solution)/shard_map/attention_weight_gradients/ppermute | solution.py:39
  (61 other events, 966.1 us)
Sparse Core Ops, SparseCore 0:
  12.6 179.6 all-gather.1

commit v3 on v2

--- a/solution.py
+++ b/solution.py
@@ -3,6 +3,8 @@
 import jax
 import jax.numpy as jnp
 from jax import lax
+from jax.experimental import pallas as pl
+from jax.experimental.pallas import tpu as pltpu
 from jax.sharding import PartitionSpec as P
 
 QUERY_HEAD_COUNT = 16
@@ -39,24 +41,18 @@
     return lax.ppermute(value, "dp", [(i, i ^ mask) for i in range(n)])
 
 
-def column_groups():
+def column_groups(with_core):
     n = lax.axis_size("dp")
-    return [[8 * z + 2 * p + c for z in range(n // 8)] for p in range(4) for c in range(2)]
-
-
-def z_pieces(value, z):
-    planes = lax.axis_size("dp") // 8
-    if planes != 4:
-        whole = lax.all_gather(value, "dp", axis_index_groups=column_groups(), axis=0)
-        return [(whole, 0)]
-    return [(value[None], z)] + [(swap(value, 8 * k)[None], z ^ k) for k in (1, 2, 3)]
+    planes = range(n // 8)
+    if with_core:
+        return [[8 * z + 2 * p + c for z in planes for c in range(2)] for p in range(4)]
+    return [[8 * z + 2 * p + c for z in planes] for p in range(4) for c in range(2)]
 
 
 def z_reduce(parts, z):
-    planes = lax.axis_size("dp") // 8
-    if planes != 4:
+    if parts.shape[0] != 4:
         return lax.psum_scatter(
-            parts.astype(BF), "dp", axis_index_groups=column_groups(), scatter_dimension=0
+            parts.astype(BF), "dp", axis_index_groups=column_groups(False), scatter_dimension=0
         ).astype(F32)
     came = [swap(pick(parts, z ^ k, 0).astype(BF), 8 * k) for k in (3, 2, 1)]
     own = pick(parts, z, 0)
@@ -65,6 +61,43 @@
     return own
 
 
+def walk_start(parts, z):
+    payload = jnp.stack(
+        [pick(parts, jnp.where(z == 0, 2, 1), 0), pick(parts, jnp.where(z == 0, 3, 0), 0)]
+    )
+    return along_z(payload.astype(BF), [(0, 1), (3, 2)])
+
+
+def walk_end(parts, came, z):
+    came = came.astype(F32)
+    across = pick(parts, 3 - z, 0) + came[0]
+    far = pick(parts, jnp.where(z == 1, 3, 0), 0) + came[1]
+    up = jnp.where(z == 1, across, pick(parts, jnp.minimum(z + 1, 3), 0))
+    down = jnp.where(z == 2, across, pick(parts, jnp.maximum(z - 1, 0), 0))
+    return (
+        along_z(up.astype(BF), [(0, 1), (1, 2), (2, 3)]),
+        along_z(down.astype(BF), [(1, 0), (2, 1), (3, 2)]),
+        along_z(far.astype(BF), [(2, 0), (1, 3)]),
+    )
+
+
+def owned(parts, came, z):
+    own = pick(parts, z, 0)
+    for piece in came:
+        own = own + piece.astype(F32)
+    return own
+
+
+def along_z(value, pairs):
+    return lax.ppermute(
+        value, "dp", [(8 * a + i, 8 * b + i) for a, b in pairs for i in range(8)]
+    )
+
+
+def tied(*values):
+    return lax.optimization_barrier(values)
+
+
 def place(out, piece, where):
     return lax.dynamic_update_slice(out, piece, where)
 
@@ -73,25 +106,241 @@
     return lax.dynamic_index_in_dim(parts, index, axis, keepdims=False)
 
 
-def both(first, second):
-    return lax.optimization_barrier((first, second))
+def column_cuts(w_gate, w_up, p, part):
+    rows = w_gate.shape[0]
+    gate_cut = w_gate.reshape(rows, -1, 4, part)
+    up_cut = w_up.reshape(rows, -1, 4, part)
+    cuts = []
+    for r in range(4):
+        gate = pick(gate_cut, p ^ r, 2).reshape(rows, -1)
+        up = pick(up_cut, p ^ r, 2).reshape(rows, -1)
+        cuts.append(jnp.concatenate([gate, up], axis=1))
+    return cuts
+
+
+def by_source(came, p):
+    out = jnp.zeros((4,) + came[0].shape, BF)
+    for r in range(4):
+        out = place(out, came[r][None], (p ^ r, 0, 0))
+    return out
+
+
+def gather_columns(mine, rows):
+    n = lax.axis_size("dp")
+    columns = mine.shape[2]
+    whole = lax.all_gather(
+        mine.reshape(4 * rows, columns),
+        "dp",
+        axis_index_groups=column_groups(True),
+        axis=0,
+        tiled=True,
+    )
+    whole = whole.reshape(n // 8, 2, 4, rows, columns).transpose(0, 2, 1, 3, 4)
+    return whole.reshape(n * rows, columns)
+
+
+def gather_weights_plainly(local, w_gate, w_up, w_down, p):
+    rows = local.shape[0]
+    gathered = lax.all_gather(local, "dp", axis=0, tiled=True)
+    cuts = column_cuts(w_gate, w_up, p, 2 * w_down.shape[0])
+    came = [cuts[0]] + [swap(cuts[r], r << 1) for r in (1, 2, 3)]
+    wb = gather_columns(by_source(came, p), rows)
+    wd = lax.all_gather(
+        w_down, "dp", axis_index_groups=column_groups(True), axis=0, tiled=True
+    )
+    return gathered, wb, wd
+
+
+def unset(shape, dtype):
+    return pl.pallas_call(
+        lambda out: None,
+        out_shape=jax.ShapeDtypeStruct(shape, dtype),
+        out_specs=pl.BlockSpec(memory_space=pl.ANY),
+        name="unset",
+    )()
+
+
+def packed(pieces):
+    widths = [piece.shape[1] for piece in pieces]
+    rows = pieces[0].shape[0]
+
+    def kernel(*refs):
+        out = refs[-1]
+        at = 0
+        for ref, size in zip(refs[:-1], widths):
+            out[:, at : at + size] = ref[...]
+            at += size
+
+    return pl.pallas_call(
+        kernel,
+        out_shape=jax.ShapeDtypeStruct((rows, sum(widths)), pieces[0].dtype),
+        name="packed",
+    )(*pieces)
+
+
+def column_cuts_kernel(w_gate, w_up, p, part):
+    rows, ff = w_gate.shape
+    planes = ff // (4 * part)
+    units = planes * part
+
+    def kernel(p_ref, gate, up, *outs):
+        for r, out in enumerate(outs):
+            q = p_ref[0] ^ r
+            for k in range(planes):
+                start = pl.multiple_of((4 * k + q) * part, LANES)
+                out[:, k * part : (k + 1) * part] = gate[:, pl.ds(start, part)]
+                out[:, units + k * part : units + (k + 1) * part] = up[:, pl.ds(start, part)]
+
+    shape = jax.ShapeDtypeStruct((rows, 2 * units), w_gate.dtype)
+    return pl.pallas_call(
+        kernel,
+        out_shape=[shape] * 4,
+        in_specs=[pl.BlockSpec(memory_space=pltpu.SMEM)]
+        + [pl.BlockSpec(memory_space=pltpu.VMEM)] * 2,
+        name="column_cuts",
+    )(p[None], w_gate, w_up)
+
+
+def gather_weights(local, w_gate, w_up, w_down, place_bits):
+    z, y, x, c = place_bits
+    p = 2 * y + x
+    rows, columns = local.shape
+    ff_rows, width = w_down.shape
+    end = (z == 0) | (z == 3)
+    up_pairs = [(0, 1), (1, 2), (2, 3)]
+    down_pairs = [(1, 0), (2, 1), (3, 2)]
+    far_pairs = [(0, 2), (3, 1)]
+    out_pairs = [(1, 0), (2, 3)]
+    z_b = jnp.where(z == 0, 1, z - 1)
+    z_c = jnp.where(z < 2, 2, jnp.where(z == 2, 3, 1))
+    z_d = jnp.where(z < 2, 3, 0)
+    out = unset((4, 2, 2, 2, rows, columns), BF)
+
+    def near_side(up, down):
+        return jnp.where(z == 0, down, up)
+
+    def to_pass_on(up, down):
+        return jnp.where(z == 1, down, up)
+
+    def put_x(out, piece, z_k, at_y, core):
+        return place(out, piece[None, None, :, None], (z_k, at_y, 0, core, 0, 0))
+
+    def put_y(out, piece, z_k, at_x, core):
+        return place(out, piece[None, :, None, None], (z_k, 0, at_x, core, 0, 0))
+
+    def in_order(bit, mine, theirs):
+        return jnp.stack([jnp.where(bit == 0, mine, theirs), jnp.where(bit == 0, theirs, mine)])
+
+    with jax.named_scope("phase_0"):
+        cuts = column_cuts_kernel(w_gate, w_up, p, 2 * ff_rows)
+        up, down, came_x, came_y, came_xy = tied(
+            along_z(local, up_pairs),
+            along_z(local, down_pairs),
+            swap(cuts[1], 2),
+            swap(cuts[2], 4),
+            swap(cuts[3], 6),
+        )
+    with jax.named_scope("phase_1"):
+        a, b = local, near_side(up, down)
+        a_x, b_y, far, first = tied(
+            swap(a, 2),
+            swap(b, 4),
+            along_z(tied(local, up, down)[0], far_pairs),
+            along_z(to_pass_on(up, down), out_pairs),
+        )
+        gu = unset((4, rows, cuts[0].shape[1]), BF)
+        for r, piece in enumerate((cuts[0], came_x, came_y, came_xy)):
+            gu = place(gu, piece[None], (p ^ r, 0, 0))
+        a2, b2 = in_order(x, a, a_x), in_order(y, b, b_y)
+    with jax.named_scope("phase_2"):
+        a_far, b_far = tied(swap(a2, 4), swap(b2, 2))
+        second, a2_core, b2_core = tied(along_z(far, out_pairs), swap(a2, 1), swap(b2, 1))
+        gu_in = tied(gu, second)[0]
+        g_up, g_down = along_z(gu_in, up_pairs), along_z(gu_in, down_pairs)
+        out = put_x(out, a2, z, y, c)
+        out = put_y(out, b2, z_b, x, c)
+        out = put_x(out, a2_core, z, y, 1 - c)
+        out = put_y(out, b2_core, z_b, x, 1 - c)
+    with jax.named_scope("phase_3"):
+        a, b = jnp.where(end, first, down), jnp.where(end, second, far)
+        a, b, a_far, b_far = tied(a, b, a_far, b_far)
+        a_x, b_y, g_up, g_down = tied(swap(a, 2), swap(b, 4), g_up, g_down)
+        a_core, b_core = swap(a_far, 1), swap(b_far, 1)
+        out = put_x(out, a_far, z, 1 - y, c)
+        out = put_y(out, b_far, z_b, 1 - x, c)
+        out = put_x(out, a_core, z, 1 - y, 1 - c)
+        out = put_y(out, b_core, z_b, 1 - x, 1 - c)
+        a2, b2 = in_order(x, a, a_x), in_order(y, b, b_y)
+    with jax.named_scope("phase_4"):
+        g_far = along_z(tied(gu, g_up)[0], far_pairs)
+        g_first = along_z(to_pass_on(g_up, g_down), out_pairs)
+        a_far, b_far = tied(swap(a2, 4), swap(b2, 2))
+        a2_core, b2_core = swap(a2, 1), swap(b2, 1)
+        out = put_x(out, a2, z_c, y, c)
+        out = put_y(out, b2, z_d, x, c)
+        out = put_x(out, a2_core, z_c, y, 1 - c)
+        out = put_y(out, b2_core, z_d, x, 1 - c)
+    with jax.named_scope("phase_5"):
+        a_core, b_core, g_far, g_first = tied(swap(a_far, 1), swap(b_far, 1), g_far, g_first)
+        out = put_x(out, a_far, z_c, 1 - y, c)
+        out = put_y(out, b_far, z_d, 1 - x, c)
+        out = put_x(out, a_core, z_c, 1 - y, 1 - c)
+        out = put_y(out, b_core, z_d, 1 - x, 1 - c)
+        gathered = out.reshape(32 * rows, columns)
+        g_second = along_z(g_far, out_pairs)
+
+
+    def step_1(beside):
+        d_in, *pieces = tied(w_down, gu, near_side(g_up, g_down), jnp.where(end, g_first, g_down), beside)[:4]
+        return (
+            tied(along_z(d_in, up_pairs), along_z(d_in, down_pairs)),
+            pieces,
+            [swap(piece, 1) for piece in pieces],
+        )
+
+    def step_2(state, beside):
+        (d_up, d_down), pieces, others = state
+        d_up, d_down, last, beside = tied(d_up, d_down, jnp.where(end, g_second, g_far), beside)
+        d_far = along_z(tied(w_down, d_up)[0], far_pairs)
+        d_first = along_z(to_pass_on(d_up, d_down), out_pairs)
+        wb = unset((4, 4, 2) + gu.shape[1:], BF)
+        for piece, other, z_k in zip(pieces + [last], others + [swap(last, 1)], (z, z_b, z_c, z_d)):
+            wb = place(wb, piece[None, :, None], (z_k, 0, c, 0, 0))
+            wb = place(wb, other[None, :, None], (z_k, 0, 1 - c, 0, 0))
+        return beside, (d_up, d_down, d_far, d_first), wb.reshape(32 * rows, -1)
+
+    def step_3(state):
+        d_up, d_down, d_far, d_first = state
+        d_second = along_z(d_far, out_pairs)
+        wd = unset((4, 2, ff_rows, width), BF)
+        for piece, z_k in (
+            (w_down, z),
+            (near_side(d_up, d_down), z_b),
+            (jnp.where(end, d_first, d_down), z_c),
+            (jnp.where(end, d_second, d_far), z_d),
+        ):
+            wd = place(wd, piece[None, None], (z_k, c, 0, 0))
+            wd = place(wd, swap(piece, 1)[None, None], (z_k, 1 - c, 0, 0))
+        return wd.reshape(8 * ff_rows, width)
+
+    return gathered, step_1, step_2, step_3
 
 
 def plane_reduce(parts, place_bits):
     z, y, x, c = place_bits
     half = parts.shape[0] // 2
     a, b = parts[:half], parts[half:]
-    came_a, came_b = both(
+    came_a, came_b = tied(
         swap(pick(a, 1 - y, 1).astype(BF), 4), swap(pick(b, 1 - x, 2).astype(BF), 2)
     )
     a = pick(a, y, 1) + came_a.astype(F32)
     b = pick(b, x, 2) + came_b.astype(F32)
-    came_a, came_b = both(
+    came_a, came_b = tied(
         swap(pick(a, 1 - x, 1).astype(BF), 2), swap(pick(b, 1 - y, 1).astype(BF), 4)
     )
     a = pick(a, x, 1) + came_a.astype(F32)
     b = pick(b, y, 1) + came_b.astype(F32)
-    return z_reduce(jnp.concatenate([a, b]), z)
+    return jnp.concatenate([a, b])
 
 
 def core_first(count, rows):
@@ -110,31 +359,47 @@
     )
 
 
-def core_gradient(features, grads, c):
-    mine, theirs = core_halves(features, c)
-    came = swap(t_mm(theirs, grads).astype(BF), 1)
-    return t_mm(mine, grads) + came.astype(F32)
-
-
-def split_gather(rows):
+def split_gather(rows, beside=()):
     half = rows.shape[0] // 2
     a, b = rows[:half], rows[half:]
-    a_x, b_y = both(swap(a, 2), swap(b, 4))
-    a_far, b_far = both(
-        swap(jnp.concatenate([a, a_x]), 4), swap(jnp.concatenate([b, b_y]), 2)
-    )
-    return (jnp.concatenate([a, a_x, b, b_y]), jnp.concatenate([a_far, b_far]))
-
-
-def split_reduce(near, far):
+    a_x, b_y, *beside = tied(swap(a, 2), swap(b, 4), *beside)
+    a_far, b_far = tied(swap(jnp.concatenate([a, a_x]), 4), swap(jnp.concatenate([b, b_y]), 2))
+    return (jnp.concatenate([a, a_x, b, b_y]), jnp.concatenate([a_far, b_far]), beside)
+
+
+def split_reduce(near, far, beside=lambda: (), later=lambda *values: ()):
     two = far.shape[0] // 2
     one = two // 2
     low = far.astype(BF)
-    came_a, came_b = both(swap(low[:two], 4), swap(low[two:], 2))
+    came_a, came_b, *done = tied(swap(low[:two], 4), swap(low[two:], 2), *beside())
     a = near[:two] + came_a.astype(F32)
     b = near[two:] + came_b.astype(F32)
-    came_a, came_b = both(swap(a[one:].astype(BF), 2), swap(b[one:].astype(BF), 4))
-    return jnp.concatenate([a[:one] + came_a.astype(F32), b[:one] + came_b.astype(F32)])
+    came_a, came_b, *done = tied(
+        swap(a[one:].astype(BF), 2), swap(b[one:].astype(BF), 4), *later(*done)
+    )
+    own = jnp.concatenate([a[:one] + came_a.astype(F32), b[:one] + came_b.astype(F32)])
+    return (own, *done)
+
+
+def spread_columns(came, p, part):
+    units = came[0].shape[1] // 2
+    natural = []
+    for q in range(4):
+        piece = came[3]
+        for r in (0, 1, 2):
+            piece = jnp.where(p == (q ^ r), came[r], piece)
+        natural.append(piece.astype(F32))
+    return tuple(
+        jnp.concatenate(
+            [
+                natural[q][:, start + k * part : start + (k + 1) * part]
+                for k in range(units // part)
+                for q in range(4)
+            ],
+            axis=1,
+        )
+        for start in (0, units)
+    )
 
 
 def total_of(value):
@@ -249,46 +514,15 @@
     score_scale = 1.0 / math.sqrt(HEAD_SIZE)
     cosine_lookup, sine_lookup = rotation_tables(SEQ, HEAD_SIZE)
 
-    with jax.named_scope("attention_weights"):
-        gains = jnp.stack([attn_gain, ffn_gain], axis=1)
-        gains = jnp.pad(gains, ((0, 0), (0, LANES - 2)))
-        local = jnp.concatenate(
-            [w_query, key_weight_matrix, value_weight_matrix, w_output, gains], axis=1
-        )
-        gathered = lax.all_gather(local, "dp", axis=0, tiled=True)
-
     part = 2 * ff_rows
     units = planes * part
-
-    with jax.named_scope("ffn_weights_to_columns"):
-        gate_cut = w_gate.reshape(rows, planes, 4, part)
-        up_cut = w_up.reshape(rows, planes, 4, part)
-
-        def columns_for(r):
-            gate = pick(gate_cut, p ^ r, 2).reshape(rows, units)
-            up = pick(up_cut, p ^ r, 2).reshape(rows, units)
-            return jnp.concatenate([gate, up], axis=1)
-
-        by_source = jnp.zeros((4, rows, 2 * units), BF)
-        for r in (3, 1, 2, 0):
-            piece = columns_for(r)
-            if r:
-                piece = swap(piece, r << 1)
-            by_source = place(by_source, piece[None], (p ^ r, 0, 0))
-
-    with jax.named_scope("ffn_weights_along_z"):
-        wb = jnp.zeros((planes, 4, 2, rows, 2 * units), BF)
-        for piece, at in z_pieces(by_source, z):
-            other = swap(piece, 1)
-            wb = place(wb, piece[:, :, None], (at, 0, c, 0, 0))
-            wb = place(wb, other[:, :, None], (at, 0, 1 - c, 0, 0))
-        wb = wb.reshape(n * rows, 2 * units)
-        wd = jnp.zeros((planes, 2, ff_rows, width), BF)
-        for piece, at in z_pieces(w_down, z):
-            other = swap(piece, 1)
-            wd = place(wd, piece[:, None], (at, c, 0, 0))
-            wd = place(wd, other[:, None], (at, 1 - c, 0, 0))
-        wd = wd.reshape(units, width)
+    gains = jnp.stack([attn_gain, ffn_gain], axis=1)
+    gains = jnp.pad(gains, ((0, 0), (0, LANES - 2)))
+    local = packed([w_query, key_weight_matrix, value_weight_matrix, w_output, gains])
+    if planes == 4:
+        gathered, step_1, step_2, step_3 = gather_weights(local, w_gate, w_up, w_down, bits)
+    else:
+        gathered, wb, wd = gather_weights_plainly(local, w_gate, w_up, w_down, p)
 
     with jax.named_scope("attention_forward"):
         wide = width + 2 * kv_width
@@ -303,6 +537,8 @@
         kv_heads = (sequences, SEQ, KEY_VALUE_HEADS, HEAD_SIZE)
         grouped = (sequences, SEQ, KEY_VALUE_HEADS, groups, HEAD_SIZE)
         raw = mm(normed_in, wqkv)
+        if planes == 4:
+            moving = step_1(raw)
         query = turn(raw[:, :width].reshape(heads), cosine_lookup, sine_lookup)
         query = query.astype(BF).reshape(grouped)
         key = raw[:, width : width + kv_width].reshape(kv_heads)
@@ -312,15 +548,21 @@
         probs_low = probs.astype(BF)
         mixed = jnp.einsum("bhrqk,bkhd->bqhrd", probs_low, value, preferred_element_type=F32)
         mixed = mixed.reshape(count, width).astype(BF)
+        if planes == 4:
+            mixed, moving, wb = step_2(moving, mixed)
         hidden_res = inputs_f + mm(mixed, wo)
         normed_two, inv_ffn = norm_rows(hidden_res, gain_mid)
         normed_mid = normed_two.astype(BF)
 
     with jax.named_scope("ffn_forward"):
-        near, far = split_gather(normed_mid)
+        if planes == 4:
+            near, far, moving = split_gather(normed_mid, moving)
+            wd = step_3(moving)
+        else:
+            near, far, moving = split_gather(normed_mid)
         y_near, pre_near, hid_near = ffn_forward(near, wb, wd)
         y_far, pre_far, hid_far = ffn_forward(far, wb, wd)
-        result = hidden_res + split_reduce(y_near, y_far)
+        result = hidden_res + split_reduce(y_near, y_far)[0]
         out_act = result.astype(BF)
 
     with jax.named_scope("loss"):
@@ -332,48 +574,41 @@
 
     with jax.named_scope("ffn_backward"):
         grad_low = grad_out.astype(BF)
-        d_near, d_far = split_gather(grad_low)
+        d_near, d_far, _ = split_gather(grad_low)
         m_near, g_near = ffn_backward(d_near, pre_near, wb, wd)
         m_far, g_far = ffn_backward(d_far, pre_far, wb, wd)
-        grad_mid = split_reduce(m_near, m_far)
-
-    with jax.named_scope("ffn_weight_gradients"):
         by_core = core_first(width, rows)
         hid = jnp.concatenate([hid_near, hid_far])
         d_all = jnp.concatenate([d_near, d_far])
-        grad_down = t_mm(hid, d_all).reshape(planes, 2, ff_rows, width)
-        came = swap(pick(grad_down, 1 - c, 1).astype(BF), 1)
-        grad_down = z_reduce(pick(grad_down, c, 1) + came.astype(F32), z)
         mid_all = mm(jnp.concatenate([near, far]), by_core).astype(BF)
         g_all = jnp.concatenate([g_near, g_far])
-        g_both = core_gradient(mid_all, g_all, c)
-        g_both = z_reduce(g_both.reshape(planes, 4, rows, 2 * units), z).astype(BF)
-        came = [pick(g_both, p, 0)]
-        for r in (1, 2, 3):
-            came.append(swap(pick(g_both, p ^ r, 0), r << 1))
-        natural = []
-        for q in range(4):
-            piece = came[3]
-            for r in (0, 1, 2):
-                piece = jnp.where(p == (q ^ r), came[r], piece)
-            natural.append(piece.astype(F32))
-        grad_gate = jnp.concatenate(
-            [natural[q][:, k * part : (k + 1) * part] for k in range(planes) for q in range(4)],
-            axis=1,
-        )
-        grad_up = jnp.concatenate(
-            [
-                natural[q][:, units + k * part : units + (k + 1) * part]
-                for k in range(planes)
-                for q in range(4)
-            ],
-            axis=1,
-        )
+        mid_mine, mid_theirs = core_halves(mid_all, c)
+
+        def beside():
+            g_down = t_mm(hid, d_all).reshape(planes, 2, ff_rows, width)
+            came = swap(pick(g_down, 1 - c, 1).astype(BF), 1)
+            return (pick(g_down, c, 1), came, t_mm(mid_theirs, g_all).astype(BF))
+
+        def later(own, came, theirs):
+            g_down = own + came.astype(F32)
+            started = (walk_start(g_down, z),) if planes == 4 else ()
+            return (t_mm(mid_mine, g_all), swap(theirs, 1), g_down, *started)
+
+        grad_mid, g_both, came, g_down, *moving_down = split_reduce(m_near, m_far, beside, later)
+        g_both = (g_both + came.astype(F32)).reshape(planes, 4, rows, 2 * units)
+        if planes == 4:
+            moving_both = walk_start(g_both, z)
+            moving_down = walk_end(g_down, moving_down[0], z)
 
     with jax.named_scope("attention_backward"):
         grad_gain_mid, grad_res = norm_back(grad_mid, hidden_res, inv_ffn, gain_mid)
         grad_res = grad_out + grad_res
         res_low = grad_res.astype(BF)
+        mixed_mine, mixed_theirs = core_halves(mm(mixed, by_core).astype(BF), c)
+        wo_came = swap(t_mm(mixed_theirs, res_low).astype(BF), 1)
+        g_wo = t_mm(mixed_mine, res_low) + wo_came.astype(F32)
+        shape = (planes, 2, 2, rows, -1)
+        g_wo = plane_reduce(g_wo.reshape(shape), bits)
         grad_mixed = mm_t(res_low, wo).astype(BF).reshape(grouped)
         grad_probs = jnp.einsum(
             "bqhrd,bkhd->bhrqk", grad_mixed, value, preferred_element_type=F32
@@ -394,21 +629,38 @@
         key_back = turn(grad_key, cosine_lookup, -sine_lookup).reshape(count, kv_width).astype(BF)
         value_back = grad_value.reshape(count, kv_width).astype(BF)
         grad_raw = jnp.concatenate([query_back, key_back, value_back], axis=1)
+        normed_mine, normed_theirs = core_halves(mm(normed_in, by_core).astype(BF), c)
+        if planes == 4:
+            grad_raw, moving_both, g_wo, *moving_down = tied(
+                grad_raw, moving_both, g_wo, *moving_down
+            )
+            moving_both = walk_end(g_both, moving_both, z)
+            g_down = owned(g_down, moving_down, z)
+        else:
+            g_down = z_reduce(g_down, z)
+        q_came = swap(t_mm(normed_theirs, grad_raw[:, :width]).astype(BF), 1)
+        kv_came = swap(t_mm(normed_theirs, grad_raw[:, width:]).astype(BF), 1)
+        g_q = t_mm(normed_mine, grad_raw[:, :width]) + q_came.astype(F32)
+        g_kv = t_mm(normed_mine, grad_raw[:, width:]) + kv_came.astype(F32)
         grad_in = mm_t(grad_raw, wqkv)
         grad_gain_in, grad_tokens = norm_back(grad_in, inputs_f, inv_attn, gain_in)
         input_grad = (grad_res + grad_tokens).astype(BF)
 
-    with jax.named_scope("attention_weight_gradients"):
-        shape = (planes, 2, 2, rows, -1)
-        mixed_by_core = mm(mixed, by_core).astype(BF)
-        g_wo = core_gradient(mixed_by_core, res_low, c)
-        g_wo = plane_reduce(g_wo.reshape(shape), bits)
-        normed_by_core = mm(normed_in, by_core).astype(BF)
-        g_raw = core_gradient(normed_by_core, grad_raw, c)
-        g_raw = plane_reduce(g_raw.reshape(shape), bits)
-        g_wq = g_raw[:, :width]
-        g_wk = g_raw[:, width : width + kv_width]
-        g_wv = g_raw[:, width + kv_width :]
+    with jax.named_scope("weight_gradients_to_owners"):
+        if planes == 4:
+            g_both = owned(g_both, moving_both, z).astype(BF)
+        else:
+            g_both = z_reduce(g_both, z).astype(BF)
+        g_q = plane_reduce(g_q.reshape(shape), bits)
+        came = [pick(g_both, p, 0)]
+        for r in (1, 2, 3):
+            came.append(swap(pick(g_both, p ^ r, 0), r << 1))
+        grad_gate, grad_up = spread_columns(came, p, part)
+        g_kv = plane_reduce(g_kv.reshape(shape), bits)
+        g_wo = z_reduce(g_wo, z)
+        g_wq = z_reduce(g_q, z)
+        g_kv = z_reduce(g_kv, z)
+        g_wk, g_wv = g_kv[:, :kv_width], g_kv[:, kv_width:]
 
     with jax.named_scope("gain_gradients"):
         g_gains = jnp.stack([grad_gain_in, grad_gain_mid])
@@ -424,7 +676,7 @@
         g_wo,
         grad_gate,
         grad_up,
-        grad_down,
+        g_down,
         g_gains[0],
         g_gains[1],
     )

time: 625 us -> 571 us (0.914)
  waiting for transfers between devices: 332 us -> 233 us
  starting transfers between devices: 73.7 us -> 130 us
  other arithmetic: 28.4 us -> 43.1 us
  matrix products: 108 us -> 94.8 us
  between operations: 18.7 us -> 5.64 us
    ppermute x70 -> x82, waiting for transfers between devices: 319 us -> 172 us  [swap(): return lax.ppermute(value, 'dp', [(i, i ^ mask) for i in range(n)])]
    ppermute x0 -> x23, waiting for transfers between devices: none -> 61.4 us  [along_z(): lax.ppermute(value, 'dp', [(8 * a + i, 8 * b + i) for a, b in pairs for i...]
    ppermute x0 -> x23, starting transfers between devices: none -> 55.2 us  [along_z(): lax.ppermute(value, 'dp', [(8 * a + i, 8 * b + i) for a, b in pairs for i...]
    dot_general x22 -> x24, matrix products: 100 us -> 87.2 us  [dot(): return lax.dot_general(a, b, (dims, ((), ())), preferred_element_type=F32)]
    all_gather x1 -> x0, waiting for transfers between devices: 12.8 us -> none  [body(): gathered = lax.all_gather(local, 'dp', axis=0, tiled=True)]
    dynamic_update_slice x19 -> x28, local copies, waits for them, and re-layouts: 8.05 us -> 18.4 us  [place(): return lax.dynamic_update_slice(out, piece, where)]
    ppermute x70 -> x82, starting transfers between devices: 73.6 us -> 75.3 us  [swap(): return lax.ppermute(value, 'dp', [(i, i ^ mask) for i in range(n)])]
    unnamed x150 -> x153, local copies, waits for them, and re-layouts: 15.4 us -> 16.8 us
  transfers between devices with their start and end apart: 71 -> 105, of which waited for: 39 -> 50; matrix products, arithmetic and copies ran while one was open for 22% -> 26% of each run, Pallas kernels for 0% -> 0%
where the time goes in v3:
time: 571 us; the launch traced here: 564 us
  waiting for transfers between devices  233 us (41%)
  starting transfers between devices  130 us (23%)
  matrix products  94.8 us (17%)
  local copies, waits for them, and re-layouts  54.8 us (10%)
  other arithmetic  43.1 us (8%)
    ppermute x82, waiting for transfers between devices, swap(): return lax.ppermute(value, 'dp', [(i, i ^ mask) for i in range(n)])  172 us
    dot_general x24, matrix products, dot(): return lax.dot_general(a, b, (dims, ((), ())), preferred_element_type=F32)  87.2 us
    ppermute x82, starting transfers between devices, swap(): return lax.ppermute(value, 'dp', [(i, i ^ mask) for i in range(n)])  75.3 us
    ppermute x23, waiting for transfers between devices, along_z(): lax.ppermute(value, 'dp', [(8 * a + i, 8 * b + i) for a, b in pairs for i...  61.4 us
    ppermute x23, starting transfers between devices, along_z(): lax.ppermute(value, 'dp', [(8 * a + i, 8 * b + i) for a, b in pairs for i...  55.2 us
    dynamic_update_slice x28, local copies, waits for them, and re-layouts, place(): return lax.dynamic_update_slice(out, piece, where)  18.4 us
    unnamed x153, local copies, waits for them, and re-layouts  16.8 us
  transfers between devices with their start and end apart: 105, of which 50 were waited for; matrix products, arithmetic and copies ran while one was open for 26% of the time, Pallas kernels for 0%

profile of v3, /device:TPU:0, one launch (start us, length us, event | category | flops | bytes accessed | tf_op | source)
XLA Modules:
  0.0 564.1 jit_solution(18253968859062043616)
XLA Ops:
  4.0 4.9 collective-permute-start
  23.6 6.0 %collective-permute-done.4 = bf16[48,2048]{1,0:T(8,128)(2,1)S(1)} collective-permute-done((bf16[48,2048]{1,0:T(8,128)(2,1)}, bf16[48,2048]{1,0:T(8,128)(2,1)S(1)}, u32[]{:S(2)}, u32[]{:S(2)}) %collective-permute-start.4) | collective-permute-done | bytes 196640 | tf_op jit(solution)/shard_map/phase_0/ppermute | solution.py:41
  29.8 5.5 collective-permute-start.7
  38.2 6.3 %collective-permute-done.7 = bf16[48,4736]{1,0:T(8,128)(2,1)S(1)} collective-permute-done((bf16[48,4736]{1,0:T(8,128)(2,1)S(1)}, bf16[48,4736]{1,0:T(8,128)(2,1)S(1)}, u32[]{:S(2)}, u32[]{:S(2)}) %collective-permute-start.7) | collective-permute-done | bytes 454688 | tf_op jit(solution)/shard_map/phase_1/ppermute | solution.py:92
  44.5 2.3 collective-permute-done.6
  46.8 2.1 collective-permute-done.8
  55.1 10.9 %collective-permute-done.9 = bf16[48,4736]{1,0:T(8,128)(2,1)S(1)} collective-permute-done((bf16[48,4736]{1,0:T(8,128)(2,1)S(1)}, bf16[48,4736]{1,0:T(8,128)(2,1)S(1)}, u32[]{:S(2)}, u32[]{:S(2)}) %collective-permute-start.9) | collective-permute-done | bytes 454688 | tf_op jit(solution)/shard_map/phase_2/ppermute | solution.py:92
  68.9 3.0 collective-permute-done.13
  79.7 5.8 %collective-permute-done.14 = bf16[48,4736]{1,0:T(8,128)(2,1)S(1)} collective-permute-done((bf16[48,4736]{1,0:T(8,128)(2,1)S(1)}, bf16[48,4736]{1,0:T(8,128)(2,1)S(1)}, u32[]{:S(2)}, u32[]{:S(2)}) %collective-permute-start.14) | collective-permute-done | bytes 454688 | tf_op jit(solution)/shard_map/phase_3/ppermute | solution.py:41
  92.7 4.1 collective-permute-start.22
  99.8 11.0 %collective-permute-done.19 = bf16[2,48,4736]{2,1,0:T(8,128)(2,1)S(1)} collective-permute-done((bf16[2,48,4736]{2,1,0:T(8,128)(2,1)S(1)}, bf16[2,48,4736]{2,1,0:T(8,128)(2,1)S(1)}, u32[]{:S(2)}, u32[]{:S(2)}) %collective-permute-start.19) | collective-permute-done | bytes 909344 | tf_op jit(solution)/shard_map/phase_4/ppermute | solution.py:41
  118.1 13.6 %collective-permute-done.23 = bf16[4,48,2048]{2,1,0:T(8,128)(2,1)S(1)} collective-permute-done((bf16[4,48,2048]{2,1,0:T(8,128)(2,1)S(1)}, bf16[4,48,2048]{2,1,0:T(8,128)(2,1)S(1)}, u32[]{:S(2)}, u32[]{:S(2)}) %collective-permute-start.23) | collective-permute-done | bytes 786464 | tf_op jit(solution)/shard_map/phase_4/ppermute | solution.py:92
  133.8 2.1 fusion.233
  136.1 5.2 fusion.6
  144.9 2.2 collective-permute-start.28
  150.4 2.4 copy.215
  163.4 2.2 fusion.243
  169.1 3.0 fusion.19
  172.3 7.5 %collective-permute-done.30 = bf16[4,48,2048]{2,1,0:T(8,128)(2,1)} collective-permute-done((bf16[4,48,2048]{2,1,0:T(8,128)(2,1)}, bf16[4,48,2048]{2,1,0:T(8,128)(2,1)}, u32[]{:S(2)}, u32[]{:S(2)}) %collective-permute-start.30) | collective-permute-done | bytes 786464 | tf_op jit(solution)/shard_map/phase_5/ppermute | solution.py:92
  183.7 3.8 multiply_reduce_fusion.3
  191.2 6.9 %collective-permute-start.33 = (bf16[128,1536]{1,0:T(8,128)(2,1)}, bf16[128,1536]{1,0:T(8,128)(2,1)S(1)}, u32[]{:S(2)}, u32[]{:S(2)}) collective-permute-start(bf16[128,1536]{1,0:T(8,128)(2,1)} %param.21), channel_id=1, source_target_pairs={{0,16},{1,17},{2,18},{3,19},{4,20},{5,21},{6,22},{7,23},{24,8},{25... | collective-permute-start | bytes 1179656 | tf_op jit(solution)/shard_map/attention_forward/ppermute | solution.py:92
  200.5 2.8 collective-permute-done.33
  207.2 3.4 fusion.50
  211.3 9.3 %collective-permute-done.45 = bf16[256,1536]{1,0:T(8,128)(2,1)S(1)} collective-permute-done((bf16[256,1536]{1,0:T(8,128)(2,1)S(1)}, bf16[256,1536]{1,0:T(8,128)(2,1)S(1)}, u32[]{:S(2)}, u32[]{:S(2)}) %collective-permute-start.45) | collective-permute-done | bytes 786464 | tf_op jit(solution)/shard_map/ffn_forward/ppermute | solution.py:41
  220.8 3.4 fusion.58
  233.7 14.1 %collective-permute-done.46 = bf16[256,1536]{1,0:T(8,128)(2,1)S(1)} collective-permute-done((bf16[256,1536]{1,0:T(8,128)(2,1)S(1)}, bf16[256,1536]{1,0:T(8,128)(2,1)S(1)}, u32[]{:S(2)}, u32[]{:S(2)}) %collective-permute-start.46) | collective-permute-done | bytes 786464 | tf_op jit(solution)/shard_map/ffn_forward/ppermute | solution.py:41
  252.0 7.7 %collective-permute-done.48 = bf16[128,1536]{1,0:T(8,128)(2,1)S(1)} collective-permute-done((bf16[128,1536]{1,0:T(8,128)(2,1)S(1)}, bf16[128,1536]{1,0:T(8,128)(2,1)S(1)}, u32[]{:S(2)}, u32[]{:S(2)}) %collective-permute-start.48) | collective-permute-done | bytes 393248 | tf_op jit(solution)/shard_map/ffn_forward/ppermute | solution.py:41
  264.4 6.8 %fusion.15 = bf16[1024,1536]{1,0:T(8,128)(2,1)} fusion(bf16[1024,1536]{1,0:T(8,128)(2,1)S(1)} %constant_dynamic-update-slice_fusion.6, s32[1536]{0:T(1024)S(1)} %copy-done.42), kind=kOutput, calls=%fused_computation.21 | convolution fusion | flops 4835770368 | bytes 6297600 | tf_op jit(solution)/shard_map/ffn_backward/dot_general | solution.py:24
  277.2 4.2 multiply_convert_fusion.3
  281.4 7.5 %collective-permute-done.58 = bf16[256,1536]{1,0:T(8,128)(2,1)S(1)} collective-permute-done((bf16[256,1536]{1,0:T(8,128)(2,1)S(1)}, bf16[256,1536]{1,0:T(8,128)(2,1)S(1)}, u32[]{:S(2)}, u32[]{:S(2)}) %collective-permute-start.58) | collective-permute-done | bytes 786464 | tf_op jit(solution)/shard_map/ffn_backward/ppermute | solution.py:41
  289.8 3.3 multiply_convert_fusion.1
  295.1 5.4 fusion.30
  301.7 3.4 convolution_convert_fusion.4
  308.1 5.3 convolution_convert_fusion.3
  313.5 10.9 %collective-permute-done.59 = bf16[256,1536]{1,0:T(8,128)(2,1)S(1)} collective-permute-done((bf16[256,1536]{1,0:T(8,128)(2,1)S(1)}, bf16[256,1536]{1,0:T(8,128)(2,1)S(1)}, u32[]{:S(2)}, u32[]{:S(2)}) %collective-permute-start.59) | collective-permute-done | bytes 786464 | tf_op jit(solution)/shard_map/ffn_backward/ppermute | solution.py:41
  325.0 5.1 fusion.23
  330.7 2.2 collective-permute-start.65
  335.5 12.0 %fusion.77 = f32[768,2048]{1,0:T(8,128)S(1)} fusion(bf16[1024,1536]{1,0:T(8,128)(2,1)S(1)} %copy-done.52, s32[]{:T(128)S(6)} %select_n.573, bf16[512,1024]{1,0:T(8,128)(2,1)} %get-tuple-element.222, bf16[512,1024]{1,0:T(8,128)(2,1)} %copy-done.54, bf16[512,1024]{1,0:T(8,128)(2,1)S(1)} %copy-done.53, bf16[512,1024]{1,0:T(8,128)(2,1)S(1)} %get-tuple-element.223), kind=kOutput, calls=%fused_computation.140 | convolution fusion | flops 3238002688 | bytes 12058628 | tf_op jit(solution)/shard_map/ffn_backward/dot_general | solution.py:24
  347.5 2.9 collective-permute-done.65
  351.8 5.3 collective-permute-start.72
  359.1 3.7 fusion.20
  362.9 2.2 convolution_convert_fusion.2
  369.7 4.0 collective-permute-start.66
  375.6 2.4 fusion.34
  385.0 2.5 convert_add_fusion.3
  392.7 11.8 %collective-permute-done.52 = f32[2,128]{1,0:T(2,128)S(1)} collective-permute-done((f32[2,128]{1,0:T(2,128)S(1)}, f32[2,128]{1,0:T(2,128)S(1)}, u32[]{:S(2)}, u32[]{:S(2)}) %collective-permute-start.52) | collective-permute-done | bytes 1056 | tf_op jit(solution)/shard_map/loss/ppermute | solution.py:41
  405.6 2.5 collective-permute-done.53
  415.7 2.1 collective-permute-done.71
  419.5 5.6 collective-permute-done.73
  425.2 8.3 %collective-permute-done.74 = bf16[128,1536]{1,0:T(8,128)(2,1)S(1)} collective-permute-done((bf16[128,1536]{1,0:T(8,128)(2,1)S(1)}, bf16[128,1536]{1,0:T(8,128)(2,1)S(1)}, u32[]{:S(2)}, u32[]{:S(2)}) %collective-permute-start.74) | collective-permute-done | bytes 393248 | tf_op jit(solution)/shard_map/ffn_backward/ppermute | solution.py:92
  433.5 5.6 fusion.48
  448.2 2.3 fusion.93
  455.0 4.1 collective-permute-start.103
  459.9 23.9 %collective-permute-done.103 = f32[2,1536]{1,0:T(2,128)S(1)} collective-permute-done((f32[2,1536]{1,0:T(2,128)S(1)}, f32[2,1536]{1,0:T(2,128)S(1)}, u32[]{:S(2)}, u32[]{:S(2)}) %collective-permute-start.103) | collective-permute-done | bytes 12320 | tf_op jit(solution)/shard_map/gain_gradients/ppermute | solution.py:41
  485.7 3.0 collective-permute-done.104
  493.0 2.3 collective-permute-done.92
  501.0 2.7 collective-permute-done.99
  511.3 10.6 %collective-permute-done.85 = bf16[2,2,48,1536]{3,2,0,1:T(8,128)(2,1)S(1)} collective-permute-done((bf16[2,2,48,1536]{3,2,0,1:T(8,128)(2,1)S(1)}, bf16[2,2,48,1536]{3,2,0,1:T(8,128)(2,1)S(1)}, u32[]{:S(2)}, u32[]{:S(2)}) %collective-permute-start.85) | collective-permute-done | bytes 589856 | tf_op jit(solution)/shard_map/weight_gradients_to_owners/ppermute | solution.py:41
  525.5 9.0 %collective-permute-done.77 = bf16[2,2,48,1536]{3,2,0,1:T(8,128)(2,1)S(1)} collective-permute-done((bf16[2,2,48,1536]{3,2,0,1:T(8,128)(2,1)S(1)}, bf16[2,2,48,1536]{3,2,0,1:T(8,128)(2,1)S(1)}, u32[]{:S(2)}, u32[]{:S(2)}) %collective-permute-start.77) | collective-permute-done | bytes 589856 | tf_op jit(solution)/shard_map/weight_gradients_to_owners/ppermute | solution.py:41
  538.8 5.3 collective-permute-start.88
  545.0 3.8 collective-permute-start.80
  548.8 4.8 collective-permute-start.82
  553.6 5.1 collective-permute-done.89
  559.6 2.3 collective-permute-done.81
  (524 shorter events, 202.6 us)
Async XLA Ops:
  4.0 25.7 %collective-permute-start = (bf16[48,4736]{1,0:T(8,128)(2,1)}, bf16[48,4736]{1,0:T(8,128)(2,1)S(1)}, u32[]{:S(2)}, u32[]{:S(2)}) collective-permute-start(bf16[48,4736]{1,0:T(8,128)(2,1)} %packed.1), channel_id=1, source_target_pairs={{0,8},{1,9},{2,10},{3,11},{4,12},{5,13},{6,14},{7,15},{8,16},{9,17... | collective-permute-start | bytes 1363976 | tf_op jit(solution)/shard_map/phase_0/ppermute | solution.py:92
  8.9 20.7 %collective-permute-start.1 = (bf16[48,4736]{1,0:T(8,128)(2,1)}, bf16[48,4736]{1,0:T(8,128)(2,1)S(1)}, u32[]{:S(2)}, u32[]{:S(2)}) collective-permute-start(bf16[48,4736]{1,0:T(8,128)(2,1)} %packed.1), channel_id=1, source_target_pairs={{8,0},{9,1},{10,2},{11,3},{12,4},{13,5},{14,6},{15,7},{16,8},{17,9... | collective-permute-start | bytes 1363976 | tf_op jit(solution)/shard_map/phase_0/ppermute | solution.py:92
  22.1 16.1 %collective-permute-start.5 = (bf16[48,4736]{1,0:T(8,128)(2,1)S(1)}, bf16[48,4736]{1,0:T(8,128)(2,1)S(1)}, u32[]{:S(2)}, u32[]{:S(2)}) collective-permute-start(bf16[48,4736]{1,0:T(8,128)(2,1)S(1)} %copy-done.15), channel_id=1, source_target_pairs={{0,2},{1,3},{2,0},{3,1},{4,6},{5,7},{6,4},{7,5},{8,10},{9,11},{10,... | collective-permute-start | bytes 1363976 | tf_op jit(solution)/shard_map/phase_1/ppermute | solution.py:41
  29.8 14.7 %collective-permute-start.7 = (bf16[48,4736]{1,0:T(8,128)(2,1)S(1)}, bf16[48,4736]{1,0:T(8,128)(2,1)S(1)}, u32[]{:S(2)}, u32[]{:S(2)}) collective-permute-start(bf16[48,4736]{1,0:T(8,128)(2,1)S(1)} %copy-done.15), channel_id=1, source_target_pairs={{0,16},{1,17},{2,18},{3,19},{4,20},{5,21},{6,22},{7,23},{24,8},{25... | collective-permute-start | bytes 1363976 | tf_op jit(solution)/shard_map/phase_1/ppermute | solution.py:92
  49.2 16.8 %collective-permute-start.11 = (bf16[2,48,4736]{2,1,0:T(8,128)(2,1)S(1)}, bf16[2,48,4736]{2,1,0:T(8,128)(2,1)S(1)}, u32[]{:S(2)}, u32[]{:S(2)}) collective-permute-start(bf16[2,48,4736]{2,1,0:T(8,128)(2,1)S(1)} %pad_maximum_fusion.5), channel_id=1, source_target_pairs={{0,1},{1,0},{2,3},{3,2},{4,5},{5,4},{6,7},{7,6},{8,9},{9,8},{10,11... | collective-permute-start | bytes 2727944 | tf_op jit(solution)/shard_map/phase_2/ppermute | solution.py:41
  49.3 22.6 %collective-permute-start.13 = (bf16[2,48,4736]{2,1,0:T(8,128)(2,1)S(1)}, bf16[2,48,4736]{2,1,0:T(8,128)(2,1)S(1)}, u32[]{:S(2)}, u32[]{:S(2)}) collective-permute-start(bf16[2,48,4736]{2,1,0:T(8,128)(2,1)S(1)} %pad_maximum_fusion.5), channel_id=1, source_target_pairs={{0,2},{1,3},{2,0},{3,1},{4,6},{5,7},{6,4},{7,5},{8,10},{9,11},{10,... | collective-permute-start | bytes 2727944 | tf_op jit(solution)/shard_map/phase_2/ppermute | solution.py:41
  50.0 16.0 %collective-permute-start.10 = (bf16[2,48,4736]{2,1,0:T(8,128)(2,1)S(1)}, bf16[2,48,4736]{2,1,0:T(8,128)(2,1)S(1)}, u32[]{:S(2)}, u32[]{:S(2)}) collective-permute-start(bf16[2,48,4736]{2,1,0:T(8,128)(2,1)S(1)} %pad_maximum_fusion.4), channel_id=1, source_target_pairs={{0,1},{1,0},{2,3},{3,2},{4,5},{5,4},{6,7},{7,6},{8,9},{9,8},{10,11... | collective-permute-start | bytes 2727944 | tf_op jit(solution)/shard_map/phase_2/ppermute | solution.py:41
  50.2 22.4 %collective-permute-start.12 = (bf16[2,48,4736]{2,1,0:T(8,128)(2,1)S(1)}, bf16[2,48,4736]{2,1,0:T(8,128)(2,1)S(1)}, u32[]{:S(2)}, u32[]{:S(2)}) collective-permute-start(bf16[2,48,4736]{2,1,0:T(8,128)(2,1)S(1)} %pad_maximum_fusion.4), channel_id=1, source_target_pairs={{0,4},{1,5},{2,6},{3,7},{4,0},{5,1},{6,2},{7,3},{8,12},{9,13},{10,... | collective-permute-start | bytes 2727944 | tf_op jit(solution)/shard_map/phase_2/ppermute | solution.py:41
  51.7 14.3 %collective-permute-start.9 = (bf16[48,4736]{1,0:T(8,128)(2,1)S(1)}, bf16[48,4736]{1,0:T(8,128)(2,1)S(1)}, u32[]{:S(2)}, u32[]{:S(2)}) collective-permute-start(bf16[48,4736]{1,0:T(8,128)(2,1)S(1)} %collective-permute-done.7), channel_id=1, source_target_pairs={{8,0},{9,1},{10,2},{11,3},{12,4},{13,5},{14,6},{15,7},{16,24},{17,... | collective-permute-start | bytes 1363976 | tf_op jit(solution)/shard_map/phase_2/ppermute | solution.py:92
  66.0 20.7 %collective-permute-start.16 = (bf16[4,48,2048]{2,1,0:T(8,128)(2,1)S(1)}, bf16[4,48,2048]{2,1,0:T(8,128)(2,1)S(1)}, u32[]{:S(2)}, u32[]{:S(2)}) collective-permute-start(bf16[4,48,2048]{2,1,0:T(8,128)(2,1)S(1)} %bitcast_dynamic-update-slice_fusion.32), channel_id=1, source_target_pairs={{0,8},{1,9},{2,10},{3,11},{4,12},{5,13},{6,14},{7,15},{8,16},{9,17... | collective-permute-start | bytes 2359304 | tf_op jit(solution)/shard_map/phase_2/ppermute | solution.py:92
  67.5 20.4 %collective-permute-start.17 = (bf16[4,48,2048]{2,1,0:T(8,128)(2,1)S(1)}, bf16[4,48,2048]{2,1,0:T(8,128)(2,1)S(1)}, u32[]{:S(2)}, u32[]{:S(2)}) collective-permute-start(bf16[4,48,2048]{2,1,0:T(8,128)(2,1)S(1)} %bitcast_dynamic-update-slice_fusion.32), channel_id=1, source_target_pairs={{8,0},{9,1},{10,2},{11,3},{12,4},{13,5},{14,6},{15,7},{16,8},{17,9... | collective-permute-start | bytes 2359304 | tf_op jit(solution)/shard_map/phase_2/ppermute | solution.py:92
  72.6 18.5 %collective-permute-start.24 = (bf16[2,48,4736]{2,1,0:T(8,128)(2,1)S(1)}, bf16[2,48,4736]{2,1,0:T(8,128)(2,1)S(1)}, u32[]{:S(2)}, u32[]{:S(2)}) collective-permute-start(bf16[2,48,4736]{2,1,0:T(8,128)(2,1)S(1)} %collective-permute-done.12), channel_id=1, source_target_pairs={{0,1},{1,0},{2,3},{3,2},{4,5},{5,4},{6,7},{7,6},{8,9},{9,8},{10,11... | collective-permute-start | bytes 2727944 | tf_op jit(solution)/shard_map/phase_3/ppermute | solution.py:41
  88.1 26.5 %collective-permute-start.27 = (bf16[2,48,4736]{2,1,0:T(8,128)(2,1)S(1)}, bf16[2,48,4736]{2,1,0:T(8,128)(2,1)S(1)}, u32[]{:S(2)}, u32[]{:S(2)}) collective-permute-start(bf16[2,48,4736]{2,1,0:T(8,128)(2,1)S(1)} %pad_maximum_fusion.7), channel_id=1, source_target_pairs={{0,1},{1,0},{2,3},{3,2},{4,5},{5,4},{6,7},{7,6},{8,9},{9,8},{10,11... | collective-permute-start | bytes 2727944 | tf_op jit(solution)/shard_map/phase_4/ppermute | solution.py:41
  88.2 22.6 %collective-permute-start.19 = (bf16[2,48,4736]{2,1,0:T(8,128)(2,1)S(1)}, bf16[2,48,4736]{2,1,0:T(8,128)(2,1)S(1)}, u32[]{:S(2)}, u32[]{:S(2)}) collective-permute-start(bf16[2,48,4736]{2,1,0:T(8,128)(2,1)S(1)} %pad_maximum_fusion.7), channel_id=1, source_target_pairs={{0,2},{1,3},{2,0},{3,1},{4,6},{5,7},{6,4},{7,5},{8,10},{9,11},{10,... | collective-permute-start | bytes 2727944 | tf_op jit(solution)/shard_map/phase_4/ppermute | solution.py:41
  89.9 23.7 %collective-permute-start.26 = (bf16[2,48,4736]{2,1,0:T(8,128)(2,1)S(1)}, bf16[2,48,4736]{2,1,0:T(8,128)(2,1)S(1)}, u32[]{:S(2)}, u32[]{:S(2)}) collective-permute-start(bf16[2,48,4736]{2,1,0:T(8,128)(2,1)S(1)} %pad_maximum_fusion.6), channel_id=1, source_target_pairs={{0,1},{1,0},{2,3},{3,2},{4,5},{5,4},{6,7},{7,6},{8,9},{9,8},{10,11... | collective-permute-start | bytes 2727944 | tf_op jit(solution)/shard_map/phase_4/ppermute | solution.py:41
  91.2 22.4 %collective-permute-start.18 = (bf16[2,48,4736]{2,1,0:T(8,128)(2,1)S(1)}, bf16[2,48,4736]{2,1,0:T(8,128)(2,1)S(1)}, u32[]{:S(2)}, u32[]{:S(2)}) collective-permute-start(bf16[2,48,4736]{2,1,0:T(8,128)(2,1)S(1)} %pad_maximum_fusion.6), channel_id=1, source_target_pairs={{0,4},{1,5},{2,6},{3,7},{4,0},{5,1},{6,2},{7,3},{8,12},{9,13},{10,... | collective-permute-start | bytes 2727944 | tf_op jit(solution)/shard_map/phase_4/ppermute | solution.py:41
  92.7 25.4 %collective-permute-start.22 = (bf16[4,48,2048]{2,1,0:T(8,128)(2,1)S(1)}, bf16[4,48,2048]{2,1,0:T(8,128)(2,1)S(1)}, u32[]{:S(2)}, u32[]{:S(2)}) collective-permute-start(bf16[4,48,2048]{2,1,0:T(8,128)(2,1)S(1)} %bitcast_dynamic-update-slice_fusion.32), channel_id=1, source_target_pairs={{0,16},{1,17},{2,18},{3,19},{4,20},{5,21},{6,22},{7,23},{24,8},{25... | collective-permute-start | bytes 2359304 | tf_op jit(solution)/shard_map/phase_4/ppermute | solution.py:92
  110.8 21.0 %collective-permute-start.23 = (bf16[4,48,2048]{2,1,0:T(8,128)(2,1)S(1)}, bf16[4,48,2048]{2,1,0:T(8,128)(2,1)S(1)}, u32[]{:S(2)}, u32[]{:S(2)}) collective-permute-start(bf16[4,48,2048]{2,1,0:T(8,128)(2,1)S(1)} %get-tuple-element.253), channel_id=1, source_target_pairs={{8,0},{9,1},{10,2},{11,3},{12,4},{13,5},{14,6},{15,7},{16,24},{17,... | collective-permute-start | bytes 2359304 | tf_op jit(solution)/shard_map/phase_4/ppermute | solution.py:92
  113.6 18.2 %collective-permute-start.20 = (bf16[2,48,4736]{2,1,0:T(8,128)(2,1)S(1)}, bf16[2,48,4736]{2,1,0:T(8,128)(2,1)S(1)}, u32[]{:S(2)}, u32[]{:S(2)}) collective-permute-start(bf16[2,48,4736]{2,1,0:T(8,128)(2,1)S(1)} %collective-permute-done.18), channel_id=1, source_target_pairs={{0,1},{1,0},{2,3},{3,2},{4,5},{5,4},{6,7},{7,6},{8,9},{9,8},{10,11... | collective-permute-start | bytes 2727944 | tf_op jit(solution)/shard_map/phase_5/ppermute | solution.py:41
  116.6 15.1 %collective-permute-start.21 = (bf16[2,48,4736]{2,1,0:T(8,128)(2,1)S(1)}, bf16[2,48,4736]{2,1,0:T(8,128)(2,1)S(1)}, u32[]{:S(2)}, u32[]{:S(2)}) collective-permute-start(bf16[2,48,4736]{2,1,0:T(8,128)(2,1)S(1)} %collective-permute-done.19), channel_id=1, source_target_pairs={{0,1},{1,0},{2,3},{3,2},{4,5},{5,4},{6,7},{7,6},{8,9},{9,8},{10,11... | collective-permute-start | bytes 2727944 | tf_op jit(solution)/shard_map/phase_5/ppermute | solution.py:41
  144.9 27.2 %collective-permute-start.28 = (bf16[128,1536]{1,0:T(8,128)(2,1)}, bf16[128,1536]{1,0:T(8,128)(2,1)}, u32[]{:S(2)}, u32[]{:S(2)}) collective-permute-start(bf16[128,1536]{1,0:T(8,128)(2,1)} %param.21), channel_id=1, source_target_pairs={{0,8},{1,9},{2,10},{3,11},{4,12},{5,13},{6,14},{7,15},{8,16},{9,17... | collective-permute-start | bytes 1179656 | tf_op jit(solution)/shard_map/attention_forward/ppermute | solution.py:92
  147.1 25.2 %collective-permute-start.29 = (bf16[128,1536]{1,0:T(8,128)(2,1)}, bf16[128,1536]{1,0:T(8,128)(2,1)S(1)}, u32[]{:S(2)}, u32[]{:S(2)}) collective-permute-start(bf16[128,1536]{1,0:T(8,128)(2,1)} %param.21), channel_id=1, source_target_pairs={{8,0},{9,1},{10,2},{11,3},{12,4},{13,5},{14,6},{15,7},{16,8},{17,9... | collective-permute-start | bytes 1179656 | tf_op jit(solution)/shard_map/attention_forward/ppermute | solution.py:92
  159.5 20.3 %collective-permute-start.30 = (bf16[4,48,2048]{2,1,0:T(8,128)(2,1)}, bf16[4,48,2048]{2,1,0:T(8,128)(2,1)}, u32[]{:S(2)}, u32[]{:S(2)}) collective-permute-start(bf16[4,48,2048]{2,1,0:T(8,128)(2,1)} %copy-done.24), channel_id=1, source_target_pairs={{8,0},{9,1},{10,2},{11,3},{12,4},{13,5},{14,6},{15,7},{16,24},{17,... | collective-permute-start | bytes 2359304 | tf_op jit(solution)/shard_map/phase_5/ppermute | solution.py:92
  161.6 27.8 %collective-permute-start.35 = (bf16[4,48,2048]{2,1,0:T(8,128)(2,1)S(1)}, bf16[4,48,2048]{2,1,0:T(8,128)(2,1)}, u32[]{:S(2)}, u32[]{:S(2)}) collective-permute-start(bf16[4,48,2048]{2,1,0:T(8,128)(2,1)S(1)} %copy-done.11), channel_id=1, source_target_pairs={{0,1},{1,0},{2,3},{3,2},{4,5},{5,4},{6,7},{7,6},{8,9},{9,8},{10,11... | collective-permute-start | bytes 2359304 | tf_op jit(solution)/shard_map/attention_forward/ppermute | solution.py:41
  168.6 22.6 %collective-permute-start.36 = (bf16[4,48,2048]{2,1,0:T(8,128)(2,1)S(1)}, bf16[4,48,2048]{2,1,0:T(8,128)(2,1)S(1)}, u32[]{:S(2)}, u32[]{:S(2)}) collective-permute-start(bf16[4,48,2048]{2,1,0:T(8,128)(2,1)S(1)} %copy-done.12), channel_id=1, source_target_pairs={{0,1},{1,0},{2,3},{3,2},{4,5},{5,4},{6,7},{7,6},{8,9},{9,8},{10,11... | collective-permute-start | bytes 2359304 | tf_op jit(solution)/shard_map/attention_forward/ppermute | solution.py:41
  172.1 26.2 %collective-permute-start.37 = (bf16[4,48,2048]{2,1,0:T(8,128)(2,1)S(1)}, bf16[4,48,2048]{2,1,0:T(8,128)(2,1)S(1)}, u32[]{:S(2)}, u32[]{:S(2)}) collective-permute-start(bf16[4,48,2048]{2,1,0:T(8,128)(2,1)S(1)} %copy-done.8), channel_id=1, source_target_pairs={{0,1},{1,0},{2,3},{3,2},{4,5},{5,4},{6,7},{7,6},{8,9},{9,8},{10,11... | collective-permute-start | bytes 2359304 | tf_op jit(solution)/shard_map/attention_forward/ppermute | solution.py:41
  182.3 18.2 %collective-permute-start.34 = (bf16[128,1536]{1,0:T(8,128)(2,1)S(1)}, bf16[128,1536]{1,0:T(8,128)(2,1)S(1)}, u32[]{:S(2)}, u32[]{:S(2)}) collective-permute-start(bf16[128,1536]{1,0:T(8,128)(2,1)S(1)} %broadcast_select_fusion.11), channel_id=1, source_target_pairs={{8,0},{9,1},{10,2},{11,3},{12,4},{13,5},{14,6},{15,7},{16,24},{17,... | collective-permute-start | bytes 1179656 | tf_op jit(solution)/shard_map/attention_forward/ppermute | solution.py:92
  203.4 17.2 %collective-permute-start.45 = (bf16[256,1536]{1,0:T(8,128)(2,1)S(1)}, bf16[256,1536]{1,0:T(8,128)(2,1)S(1)}, u32[]{:S(2)}, u32[]{:S(2)}) collective-permute-start(bf16[256,1536]{1,0:T(8,128)(2,1)S(1)} %pad_maximum_fusion.10), channel_id=1, source_target_pairs={{0,2},{1,3},{2,0},{3,1},{4,6},{5,7},{6,4},{7,5},{8,10},{9,11},{10,... | collective-permute-start | bytes 2359304 | tf_op jit(solution)/shard_map/ffn_forward/ppermute | solution.py:41
  204.0 16.9 %collective-permute-start.44 = (bf16[256,1536]{1,0:T(8,128)(2,1)S(1)}, bf16[256,1536]{1,0:T(8,128)(2,1)S(1)}, u32[]{:S(2)}, u32[]{:S(2)}) collective-permute-start(bf16[256,1536]{1,0:T(8,128)(2,1)S(1)} %pad_maximum_fusion.9), channel_id=1, source_target_pairs={{0,4},{1,5},{2,6},{3,7},{4,0},{5,1},{6,2},{7,3},{8,12},{9,13},{10,... | collective-permute-start | bytes 2359304 | tf_op jit(solution)/shard_map/ffn_forward/ppermute | solution.py:41
  205.7 18.6 %collective-permute-start.42 = (bf16[128,1536]{1,0:T(8,128)(2,1)S(1)}, bf16[128,1536]{1,0:T(8,128)(2,1)S(1)}, u32[]{:S(2)}, u32[]{:S(2)}) collective-permute-start(bf16[128,1536]{1,0:T(8,128)(2,1)S(1)} %collective-permute-done.33), channel_id=1, source_target_pairs={{8,0},{9,1},{10,2},{11,3},{12,4},{13,5},{14,6},{15,7},{16,24},{17,... | collective-permute-start | bytes 1179656 | tf_op jit(solution)/shard_map/ffn_forward/ppermute | solution.py:92
  210.8 13.5 %collective-permute-start.41 = (bf16[128,1536]{1,0:T(8,128)(2,1)S(1)}, bf16[128,1536]{1,0:T(8,128)(2,1)S(1)}, u32[]{:S(2)}, u32[]{:S(2)}) collective-permute-start(bf16[128,1536]{1,0:T(8,128)(2,1)S(1)} %get-tuple-element.211), channel_id=1, source_target_pairs={{0,1},{1,0},{2,3},{3,2},{4,5},{5,4},{6,7},{7,6},{8,9},{9,8},{10,11... | collective-permute-start | bytes 1179656 | tf_op jit(solution)/shard_map/ffn_forward/ppermute | solution.py:41
  228.2 19.6 %collective-permute-start.46 = (bf16[256,1536]{1,0:T(8,128)(2,1)S(1)}, bf16[256,1536]{1,0:T(8,128)(2,1)S(1)}, u32[]{:S(2)}, u32[]{:S(2)}) collective-permute-start(bf16[256,1536]{1,0:T(8,128)(2,1)S(1)} %get-tuple-element.252), channel_id=1, source_target_pairs={{0,4},{1,5},{2,6},{3,7},{4,0},{5,1},{6,2},{7,3},{8,12},{9,13},{10,... | collective-permute-start | bytes 2359304 | tf_op jit(solution)/shard_map/ffn_forward/ppermute | solution.py:41
  229.8 19.3 %collective-permute-start.47 = (bf16[256,1536]{1,0:T(8,128)(2,1)S(1)}, bf16[256,1536]{1,0:T(8,128)(2,1)S(1)}, u32[]{:S(2)}, u32[]{:S(2)}) collective-permute-start(bf16[256,1536]{1,0:T(8,128)(2,1)S(1)} %get-tuple-element.251), channel_id=1, source_target_pairs={{0,2},{1,3},{2,0},{3,1},{4,6},{5,7},{6,4},{7,5},{8,10},{9,11},{10,... | collective-permute-start | bytes 2359304 | tf_op jit(solution)/shard_map/ffn_forward/ppermute | solution.py:41
  272.5 16.4 %collective-permute-start.58 = (bf16[256,1536]{1,0:T(8,128)(2,1)S(1)}, bf16[256,1536]{1,0:T(8,128)(2,1)S(1)}, u32[]{:S(2)}, u32[]{:S(2)}) collective-permute-start(bf16[256,1536]{1,0:T(8,128)(2,1)S(1)} %pad_maximum_fusion.12), channel_id=1, source_target_pairs={{0,2},{1,3},{2,0},{3,1},{4,6},{5,7},{6,4},{7,5},{8,10},{9,11},{10,... | collective-permute-start | bytes 2359304 | tf_op jit(solution)/shard_map/ffn_backward/ppermute | solution.py:41
  274.2 15.6 %collective-permute-start.57 = (bf16[256,1536]{1,0:T(8,128)(2,1)S(1)}, bf16[256,1536]{1,0:T(8,128)(2,1)S(1)}, u32[]{:S(2)}, u32[]{:S(2)}) collective-permute-start(bf16[256,1536]{1,0:T(8,128)(2,1)S(1)} %pad_maximum_fusion.11), channel_id=1, source_target_pairs={{0,4},{1,5},{2,6},{3,7},{4,0},{5,1},{6,2},{7,3},{8,12},{9,13},{10,... | collective-permute-start | bytes 2359304 | tf_op jit(solution)/shard_map/ffn_backward/ppermute | solution.py:41
  300.7 24.3 %collective-permute-start.61 = (bf16[4,128,1536]{2,1,0:T(8,128)(2,1)S(1)}, bf16[4,128,1536]{2,1,0:T(8,128)(2,1)S(1)}, u32[]{:S(2)}, u32[]{:S(2)}) collective-permute-start(bf16[4,128,1536]{2,1,0:T(8,128)(2,1)S(1)} %fusion.38), channel_id=1, source_target_pairs={{0,1},{1,0},{2,3},{3,2},{4,5},{5,4},{6,7},{7,6},{8,9},{9,8},{10,11... | collective-permute-start | bytes 4718600 | tf_op jit(solution)/shard_map/ffn_backward/ppermute | solution.py:41
  305.3 19.1 %collective-permute-start.59 = (bf16[256,1536]{1,0:T(8,128)(2,1)S(1)}, bf16[256,1536]{1,0:T(8,128)(2,1)S(1)}, u32[]{:S(2)}, u32[]{:S(2)}) collective-permute-start(bf16[256,1536]{1,0:T(8,128)(2,1)S(1)} %get-tuple-element.250), channel_id=1, source_target_pairs={{0,4},{1,5},{2,6},{3,7},{4,0},{5,1},{6,2},{7,3},{8,12},{9,13},{10,... | collective-permute-start | bytes 2359304 | tf_op jit(solution)/shard_map/ffn_backward/ppermute | solution.py:41
  306.2 18.7 %collective-permute-start.60 = (bf16[256,1536]{1,0:T(8,128)(2,1)S(1)}, bf16[256,1536]{1,0:T(8,128)(2,1)S(1)}, u32[]{:S(2)}, u32[]{:S(2)}) collective-permute-start(bf16[256,1536]{1,0:T(8,128)(2,1)S(1)} %get-tuple-element.249), channel_id=1, source_target_pairs={{0,2},{1,3},{2,0},{3,1},{4,6},{5,7},{6,4},{7,5},{8,10},{9,11},{10,... | collective-permute-start | bytes 2359304 | tf_op jit(solution)/shard_map/ffn_backward/ppermute | solution.py:41
  325.0 25.4 %collective-permute-start.64 = (bf16[768,2048]{1,0:T(8,128)(2,1)S(1)}, bf16[768,2048]{1,0:T(8,128)(2,1)S(1)}, u32[]{:S(2)}, u32[]{:S(2)}) collective-permute-start(bf16[768,2048]{1,0:T(8,128)(2,1)S(1)} %convolution_convert_fusion.3), channel_id=1, source_target_pairs={{0,1},{1,0},{2,3},{3,2},{4,5},{5,4},{6,7},{7,6},{8,9},{9,8},{10,11... | collective-permute-start | bytes 9437192 | tf_op jit(solution)/shard_map/ffn_backward/ppermute | solution.py:41
  330.7 19.7 %collective-permute-start.65 = (bf16[2,128,1536]{2,1,0:T(8,128)(2,1)S(1)}, bf16[2,128,1536]{2,1,0:T(8,128)(2,1)S(1)}, u32[]{:S(2)}, u32[]{:S(2)}) collective-permute-start(bf16[2,128,1536]{2,1,0:T(8,128)(2,1)S(1)} %pad_maximum_fusion.13), channel_id=1, source_target_pairs={{0,8},{1,9},{2,10},{3,11},{4,12},{5,13},{6,14},{7,15},{24,16},{25,... | collective-permute-start | bytes 2359304 | tf_op jit(solution)/shard_map/ffn_backward/ppermute | solution.py:92
  333.4 14.1 %collective-permute-start.62 = (bf16[128,1536]{1,0:T(8,128)(2,1)S(1)}, bf16[128,1536]{1,0:T(8,128)(2,1)S(1)}, u32[]{:S(2)}, u32[]{:S(2)}) collective-permute-start(bf16[128,1536]{1,0:T(8,128)(2,1)S(1)} %slice.584), channel_id=1, source_target_pairs={{0,2},{1,3},{2,0},{3,1},{4,6},{5,7},{6,4},{7,5},{8,10},{9,11},{10,... | collective-permute-start | bytes 1179656 | tf_op jit(solution)/shard_map/ffn_backward/ppermute | solution.py:41
  334.2 13.3 %collective-permute-start.63 = (bf16[128,1536]{1,0:T(8,128)(2,1)S(1)}, bf16[128,1536]{1,0:T(8,128)(2,1)S(1)}, u32[]{:S(2)}, u32[]{:S(2)}) collective-permute-start(bf16[128,1536]{1,0:T(8,128)(2,1)S(1)} %slice.583), channel_id=1, source_target_pairs={{0,4},{1,5},{2,6},{3,7},{4,0},{5,1},{6,2},{7,3},{8,12},{9,13},{10,... | collective-permute-start | bytes 1179656 | tf_op jit(solution)/shard_map/ffn_backward/ppermute | solution.py:41
  351.8 67.7 %collective-permute-start.72 = (bf16[128,1536]{1,0:T(8,128)(2,1)}, bf16[128,1536]{1,0:T(8,128)(2,1)}, u32[]{:S(2)}, u32[]{:S(2)}) collective-permute-start(bf16[128,1536]{1,0:T(8,128)(2,1)} %get-tuple-element.231), channel_id=1, source_target_pairs={{0,8},{1,9},{2,10},{3,11},{4,12},{5,13},{6,14},{7,15},{8,16},{9,17... | collective-permute-start | bytes 1179656 | tf_op jit(solution)/shard_map/ffn_backward/ppermute | solution.py:92
  365.1 19.9 %collective-permute-start.67 = (bf16[768,1536]{1,0:T(8,128)(2,1)}, bf16[768,1536]{1,0:T(8,128)(2,1)}, u32[]{:S(2)}, u32[]{:S(2)}) collective-permute-start(bf16[768,1536]{1,0:T(8,128)(2,1)} %convolution_convert_fusion.2), channel_id=1, source_target_pairs={{0,1},{1,0},{2,3},{3,2},{4,5},{5,4},{6,7},{7,6},{8,9},{9,8},{10,11... | collective-permute-start | bytes 7077896 | tf_op jit(solution)/shard_map/attention_backward/ppermute | solution.py:41
  369.7 63.7 %collective-permute-start.66 = (bf16[2,4,48,2048]{3,2,1,0:T(8,128)(2,1)}, bf16[2,4,48,2048]{3,2,1,0:T(8,128)(2,1)}, u32[]{:S(2)}, u32[]{:S(2)}) collective-permute-start(bf16[2,4,48,2048]{3,2,1,0:T(8,128)(2,1)} %pad_maximum_fusion.2), channel_id=1, source_target_pairs={{0,8},{1,9},{2,10},{3,11},{4,12},{5,13},{6,14},{7,15},{24,16},{25,... | collective-permute-start | bytes 4718600 | tf_op jit(solution)/shard_map/ffn_backward/ppermute | solution.py:92
  387.9 21.2 %collective-permute-start.69 = (bf16[2,2,48,1536]{3,2,0,1:T(8,128)(2,1)S(1)}, bf16[2,2,48,1536]{3,2,0,1:T(8,128)(2,1)S(1)}, u32[]{:S(2)}, u32[]{:S(2)}) collective-permute-start(bf16[2,2,48,1536]{3,2,0,1:T(8,128)(2,1)S(1)} %fusion.99), channel_id=1, source_target_pairs={{0,2},{1,3},{2,0},{3,1},{4,6},{5,7},{6,4},{7,5},{8,10},{9,11},{10,... | collective-permute-start | bytes 1769480 | tf_op jit(solution)/shard_map/attention_backward/ppermute | solution.py:41
  389.4 19.7 %collective-permute-start.68 = (bf16[2,2,48,1536]{3,2,0,1:T(8,128)(2,1)S(1)}, bf16[2,2,48,1536]{3,2,0,1:T(8,128)(2,1)S(1)}, u32[]{:S(2)}, u32[]{:S(2)}) collective-permute-start(bf16[2,2,48,1536]{3,2,0,1:T(8,128)(2,1)S(1)} %fusion.98), channel_id=1, source_target_pairs={{0,4},{1,5},{2,6},{3,7},{4,0},{5,1},{6,2},{7,3},{8,12},{9,13},{10,... | collective-permute-start | bytes 1769480 | tf_op jit(solution)/shard_map/attention_backward/ppermute | solution.py:41
  390.8 13.7 %collective-permute-start.52 = (f32[2,128]{1,0:T(2,128)S(1)}, f32[2,128]{1,0:T(2,128)S(1)}, u32[]{:S(2)}, u32[]{:S(2)}) collective-permute-start(f32[2,128]{1,0:T(2,128)S(1)} %fusion.265), channel_id=1, source_target_pairs={{0,4},{1,5},{2,6},{3,7},{4,0},{5,1},{6,2},{7,3},{8,12},{9,13},{10,... | collective-permute-start | bytes 3080 | tf_op jit(solution)/shard_map/loss/ppermute | solution.py:41
  417.8 15.7 %collective-permute-start.74 = (bf16[128,1536]{1,0:T(8,128)(2,1)S(1)}, bf16[128,1536]{1,0:T(8,128)(2,1)S(1)}, u32[]{:S(2)}, u32[]{:S(2)}) collective-permute-start(bf16[128,1536]{1,0:T(8,128)(2,1)S(1)} %copy-done.31), channel_id=1, source_target_pairs={{16,0},{17,1},{18,2},{19,3},{20,4},{21,5},{22,6},{23,7},{8,24},{9,... | collective-permute-start | bytes 1179656 | tf_op jit(solution)/shard_map/ffn_backward/ppermute | solution.py:92
  442.1 47.2 %collective-permute-start.94 = (bf16[4,48,2048]{2,1,0:T(8,128)(2,1)S(1)}, bf16[4,48,2048]{2,1,0:T(8,128)(2,1)S(1)}, u32[]{:S(2)}, u32[]{:S(2)}) collective-permute-start(bf16[4,48,2048]{2,1,0:T(8,128)(2,1)S(1)} %get-tuple-element.216), channel_id=1, source_target_pairs={{0,8},{1,9},{2,10},{3,11},{4,12},{5,13},{6,14},{7,15},{8,16},{9,17... | collective-permute-start | bytes 2359304 | tf_op jit(solution)/shard_map/attention_backward/ppermute | solution.py:92
  443.4 45.9 %collective-permute-start.95 = (bf16[4,48,2048]{2,1,0:T(8,128)(2,1)S(1)}, bf16[4,48,2048]{2,1,0:T(8,128)(2,1)S(1)}, u32[]{:S(2)}, u32[]{:S(2)}) collective-permute-start(bf16[4,48,2048]{2,1,0:T(8,128)(2,1)S(1)} %get-tuple-element.217), channel_id=1, source_target_pairs={{8,0},{9,1},{10,2},{11,3},{12,4},{13,5},{14,6},{15,7},{16,8},{17,9... | collective-permute-start | bytes 2359304 | tf_op jit(solution)/shard_map/attention_backward/ppermute | solution.py:92
  444.7 44.6 %collective-permute-start.96 = (bf16[4,48,2048]{2,1,0:T(8,128)(2,1)S(1)}, bf16[4,48,2048]{2,1,0:T(8,128)(2,1)S(1)}, u32[]{:S(2)}, u32[]{:S(2)}) collective-permute-start(bf16[4,48,2048]{2,1,0:T(8,128)(2,1)S(1)} %get-tuple-element.218), channel_id=1, source_target_pairs={{16,0},{17,1},{18,2},{19,3},{20,4},{21,5},{22,6},{23,7},{8,24},{9,... | collective-permute-start | bytes 2359304 | tf_op jit(solution)/shard_map/attention_backward/ppermute | solution.py:92
  455.0 28.8 %collective-permute-start.103 = (f32[2,1536]{1,0:T(2,128)S(1)}, f32[2,1536]{1,0:T(2,128)S(1)}, u32[]{:S(2)}, u32[]{:S(2)}) collective-permute-start(f32[2,1536]{1,0:T(2,128)S(1)} %add.618), channel_id=1, source_target_pairs={{0,8},{1,9},{2,10},{3,11},{4,12},{5,13},{6,14},{7,15},{8,0},{9,1},... | collective-permute-start | bytes 36872 | tf_op jit(solution)/shard_map/gain_gradients/ppermute | solution.py:41
  489.3 14.8 %collective-permute-start.83 = (bf16[768,1536]{1,0:T(8,128)(2,1)S(1)}, bf16[768,1536]{1,0:T(8,128)(2,1)S(1)}, u32[]{:S(2)}, u32[]{:S(2)}) collective-permute-start(bf16[768,1536]{1,0:T(8,128)(2,1)S(1)} %convolution_convert_fusion), channel_id=1, source_target_pairs={{0,1},{1,0},{2,3},{3,2},{4,5},{5,4},{6,7},{7,6},{8,9},{9,8},{10,11... | collective-permute-start | bytes 7077896 | tf_op jit(solution)/shard_map/attention_backward/ppermute | solution.py:41
  489.4 18.0 %collective-permute-start.75 = (bf16[768,1536]{1,0:T(8,128)(2,1)S(1)}, bf16[768,1536]{1,0:T(8,128)(2,1)S(1)}, u32[]{:S(2)}, u32[]{:S(2)}) collective-permute-start(bf16[768,1536]{1,0:T(8,128)(2,1)S(1)} %convolution_convert_fusion.1), channel_id=1, source_target_pairs={{0,1},{1,0},{2,3},{3,2},{4,5},{5,4},{6,7},{7,6},{8,9},{9,8},{10,11... | collective-permute-start | bytes 7077896 | tf_op jit(solution)/shard_map/attention_backward/ppermute | solution.py:41
  505.6 16.3 %collective-permute-start.85 = (bf16[2,2,48,1536]{3,2,0,1:T(8,128)(2,1)S(1)}, bf16[2,2,48,1536]{3,2,0,1:T(8,128)(2,1)S(1)}, u32[]{:S(2)}, u32[]{:S(2)}) collective-permute-start(bf16[2,2,48,1536]{3,2,0,1:T(8,128)(2,1)S(1)} %fusion.103), channel_id=1, source_target_pairs={{0,2},{1,3},{2,0},{3,1},{4,6},{5,7},{6,4},{7,5},{8,10},{9,11},{10,... | collective-permute-start | bytes 1769480 | tf_op jit(solution)/shard_map/weight_gradients_to_owners/ppermute | solution.py:41
  506.6 16.3 %collective-permute-start.84 = (bf16[2,2,48,1536]{3,2,0,1:T(8,128)(2,1)S(1)}, bf16[2,2,48,1536]{3,2,0,1:T(8,128)(2,1)S(1)}, u32[]{:S(2)}, u32[]{:S(2)}) collective-permute-start(bf16[2,2,48,1536]{3,2,0,1:T(8,128)(2,1)S(1)} %fusion.102), channel_id=1, source_target_pairs={{0,4},{1,5},{2,6},{3,7},{4,0},{5,1},{6,2},{7,3},{8,12},{9,13},{10,... | collective-permute-start | bytes 1769480 | tf_op jit(solution)/shard_map/weight_gradients_to_owners/ppermute | solution.py:41
  508.7 25.9 %collective-permute-start.77 = (bf16[2,2,48,1536]{3,2,0,1:T(8,128)(2,1)S(1)}, bf16[2,2,48,1536]{3,2,0,1:T(8,128)(2,1)S(1)}, u32[]{:S(2)}, u32[]{:S(2)}) collective-permute-start(bf16[2,2,48,1536]{3,2,0,1:T(8,128)(2,1)S(1)} %fusion.101), channel_id=1, source_target_pairs={{0,2},{1,3},{2,0},{3,1},{4,6},{5,7},{6,4},{7,5},{8,10},{9,11},{10,... | collective-permute-start | bytes 1769480 | tf_op jit(solution)/shard_map/weight_gradients_to_owners/ppermute | solution.py:41
  510.2 25.2 %collective-permute-start.76 = (bf16[2,2,48,1536]{3,2,0,1:T(8,128)(2,1)S(1)}, bf16[2,2,48,1536]{3,2,0,1:T(8,128)(2,1)S(1)}, u32[]{:S(2)}, u32[]{:S(2)}) collective-permute-start(bf16[2,2,48,1536]{3,2,0,1:T(8,128)(2,1)S(1)} %fusion.100), channel_id=1, source_target_pairs={{0,4},{1,5},{2,6},{3,7},{4,0},{5,1},{6,2},{7,3},{8,12},{9,13},{10,... | collective-permute-start | bytes 1769480 | tf_op jit(solution)/shard_map/weight_gradients_to_owners/ppermute | solution.py:41
  523.1 15.4 %collective-permute-start.87 = (bf16[2,48,1536]{2,1,0:T(8,128)(2,1)S(1)}, bf16[2,48,1536]{2,1,0:T(8,128)(2,1)S(1)}, u32[]{:S(2)}, u32[]{:S(2)}) collective-permute-start(bf16[2,48,1536]{2,1,0:T(8,128)(2,1)S(1)} %fusion.128), channel_id=1, source_target_pairs={{0,4},{1,5},{2,6},{3,7},{4,0},{5,1},{6,2},{7,3},{8,12},{9,13},{10,... | collective-permute-start | bytes 884744 | tf_op jit(solution)/shard_map/weight_gradients_to_owners/ppermute | solution.py:41
  524.1 14.4 %collective-permute-start.86 = (bf16[2,48,1536]{2,1,0:T(8,128)(2,1)S(1)}, bf16[2,48,1536]{2,1,0:T(8,128)(2,1)S(1)}, u32[]{:S(2)}, u32[]{:S(2)}) collective-permute-start(bf16[2,48,1536]{2,1,0:T(8,128)(2,1)S(1)} %fusion.127), channel_id=1, source_target_pairs={{0,2},{1,3},{2,0},{3,1},{4,6},{5,7},{6,4},{7,5},{8,10},{9,11},{10,... | collective-permute-start | bytes 884744 | tf_op jit(solution)/shard_map/weight_gradients_to_owners/ppermute | solution.py:41
  544.0 14.7 %collective-permute-start.89 = (bf16[48,1536]{1,0:T(8,128)(2,1)S(1)}, bf16[48,1536]{1,0:T(8,128)(2,1)S(1)}, u32[]{:S(2)}, u32[]{:S(2)}) collective-permute-start(bf16[48,1536]{1,0:T(8,128)(2,1)S(1)} %get-tuple-element.263), channel_id=1, source_target_pairs={{0,16},{1,17},{2,18},{3,19},{4,20},{5,21},{6,22},{7,23},{8,24},{9,... | collective-permute-start | bytes 442376 | tf_op jit(solution)/shard_map/weight_gradients_to_owners/ppermute | solution.py:41
  544.0 14.7 %collective-permute-start.90 = (bf16[48,1536]{1,0:T(8,128)(2,1)S(1)}, bf16[48,1536]{1,0:T(8,128)(2,1)S(1)}, u32[]{:S(2)}, u32[]{:S(2)}) collective-permute-start(bf16[48,1536]{1,0:T(8,128)(2,1)S(1)} %get-tuple-element.264), channel_id=1, source_target_pairs={{0,8},{1,9},{2,10},{3,11},{4,12},{5,13},{6,14},{7,15},{8,0},{9,1},... | collective-permute-start | bytes 442376 | tf_op jit(solution)/shard_map/weight_gradients_to_owners/ppermute | solution.py:41
  545.0 14.6 %collective-permute-start.80 = (bf16[48,1536]{1,0:T(8,128)(2,1)S(1)}, bf16[48,1536]{1,0:T(8,128)(2,1)S(1)}, u32[]{:S(2)}, u32[]{:S(2)}) collective-permute-start(bf16[48,1536]{1,0:T(8,128)(2,1)S(1)} %get-tuple-element.265), channel_id=1, source_target_pairs={{0,24},{1,25},{2,26},{3,27},{4,28},{5,29},{6,30},{7,31},{8,16},{9,... | collective-permute-start | bytes 442376 | tf_op jit(solution)/shard_map/weight_gradients_to_owners/ppermute | solution.py:41
  (103 other events, 1056.0 us)

commit v4 on v3

--- a/solution.py
+++ b/solution.py
@@ -231,6 +231,10 @@
     def in_order(bit, mine, theirs):
         return jnp.stack([jnp.where(bit == 0, mine, theirs), jnp.where(bit == 0, theirs, mine)])
 
+    def put(out, pair, z_a, z_b, at_y, at_x, core):
+        out = put_x(out, pair[0], z_a, at_y, core)
+        return put_y(out, pair[1], z_b, at_x, core)
+
     with jax.named_scope("phase_0"):
         cuts = column_cuts_kernel(w_gate, w_up, p, 2 * ff_rows)
         up, down, came_x, came_y, came_xy = tied(
@@ -241,105 +245,112 @@
             swap(cuts[3], 6),
         )
     with jax.named_scope("phase_1"):
-        a, b = local, near_side(up, down)
+        b = near_side(up, down)
+        a, b, passing = tied(local, b, to_pass_on(up, down))
         a_x, b_y, far, first = tied(
-            swap(a, 2),
-            swap(b, 4),
-            along_z(tied(local, up, down)[0], far_pairs),
-            along_z(to_pass_on(up, down), out_pairs),
+            swap(a, 2), swap(b, 4), along_z(a, far_pairs), along_z(passing, out_pairs)
         )
         gu = unset((4, rows, cuts[0].shape[1]), BF)
         for r, piece in enumerate((cuts[0], came_x, came_y, came_xy)):
             gu = place(gu, piece[None], (p ^ r, 0, 0))
-        a2, b2 = in_order(x, a, a_x), in_order(y, b, b_y)
     with jax.named_scope("phase_2"):
-        a_far, b_far = tied(swap(a2, 4), swap(b2, 2))
-        second, a2_core, b2_core = tied(along_z(far, out_pairs), swap(a2, 1), swap(b2, 1))
-        gu_in = tied(gu, second)[0]
-        g_up, g_down = along_z(gu_in, up_pairs), along_z(gu_in, down_pairs)
-        out = put_x(out, a2, z, y, c)
-        out = put_y(out, b2, z_b, x, c)
-        out = put_x(out, a2_core, z, y, 1 - c)
-        out = put_y(out, b2_core, z_b, x, 1 - c)
+        a2, b2, far, gu = tied(in_order(x, a, a_x), in_order(y, b, b_y), far, gu)
+        g_up, g_down = along_z(gu, up_pairs), along_z(gu, down_pairs)
+        a_far, b_far, second = tied(swap(a2, 4), swap(b2, 2), along_z(far, out_pairs))
+        near_1 = jnp.stack([a2, b2])
+        out = put(out, near_1, z, z_b, y, x, c)
     with jax.named_scope("phase_3"):
         a, b = jnp.where(end, first, down), jnp.where(end, second, far)
-        a, b, a_far, b_far = tied(a, b, a_far, b_far)
-        a_x, b_y, g_up, g_down = tied(swap(a, 2), swap(b, 4), g_up, g_down)
-        a_core, b_core = swap(a_far, 1), swap(b_far, 1)
-        out = put_x(out, a_far, z, 1 - y, c)
-        out = put_y(out, b_far, z_b, 1 - x, c)
-        out = put_x(out, a_core, z, 1 - y, 1 - c)
-        out = put_y(out, b_core, z_b, 1 - x, 1 - c)
-        a2, b2 = in_order(x, a, a_x), in_order(y, b, b_y)
+        a, b, near_1 = tied(a, b, near_1)
+        a_x, b_y, g_up, g_down, core_1 = tied(
+            swap(a, 2), swap(b, 4), g_up, g_down, swap(near_1, 1)
+        )
+        out = put(out, jnp.stack([a_far, b_far]), z, z_b, 1 - y, 1 - x, c)
     with jax.named_scope("phase_4"):
-        g_far = along_z(tied(gu, g_up)[0], far_pairs)
-        g_first = along_z(to_pass_on(g_up, g_down), out_pairs)
-        a_far, b_far = tied(swap(a2, 4), swap(b2, 2))
-        a2_core, b2_core = swap(a2, 1), swap(b2, 1)
-        out = put_x(out, a2, z_c, y, c)
-        out = put_y(out, b2, z_d, x, c)
-        out = put_x(out, a2_core, z_c, y, 1 - c)
-        out = put_y(out, b2_core, z_d, x, 1 - c)
+        a2, b2, gu, passing, far_1 = tied(
+            in_order(x, a, a_x),
+            in_order(y, b, b_y),
+            gu,
+            to_pass_on(g_up, g_down),
+            jnp.stack([a_far, b_far]),
+        )
+        g_far, g_first = along_z(gu, far_pairs), along_z(passing, out_pairs)
+        a_far, b_far, core_2 = tied(swap(a2, 4), swap(b2, 2), swap(far_1, 1))
+        out = put(out, core_1, z, z_b, y, x, 1 - c)
+        near_2 = jnp.stack([a2, b2])
+        out = put(out, near_2, z_c, z_d, y, x, c)
     with jax.named_scope("phase_5"):
-        a_core, b_core, g_far, g_first = tied(swap(a_far, 1), swap(b_far, 1), g_far, g_first)
-        out = put_x(out, a_far, z_c, 1 - y, c)
-        out = put_y(out, b_far, z_d, 1 - x, c)
-        out = put_x(out, a_core, z_c, 1 - y, 1 - c)
-        out = put_y(out, b_core, z_d, 1 - x, 1 - c)
+        near_2, far_2 = tied(near_2, jnp.stack([a_far, b_far]))
+        core_3, core_4 = tied(swap(near_2, 1), swap(far_2, 1))
+        out = put(out, core_2, z, z_b, 1 - y, 1 - x, 1 - c)
+        out = put(out, far_2, z_c, z_d, 1 - y, 1 - x, c)
+        out = put(out, core_3, z_c, z_d, y, x, 1 - c)
+        out = put(out, core_4, z_c, z_d, 1 - y, 1 - x, 1 - c)
         gathered = out.reshape(32 * rows, columns)
-        g_second = along_z(g_far, out_pairs)
 
 
     def step_1(beside):
-        d_in, *pieces = tied(w_down, gu, near_side(g_up, g_down), jnp.where(end, g_first, g_down), beside)[:4]
-        return (
-            tied(along_z(d_in, up_pairs), along_z(d_in, down_pairs)),
-            pieces,
-            [swap(piece, 1) for piece in pieces],
-        )
+        g_in, f_in, d_in, beside = tied(g_far, g_first, w_down, beside)
+        g_second = along_z(g_in, out_pairs)
+        return beside, (g_in, f_in, g_second, along_z(d_in, up_pairs), along_z(d_in, down_pairs))
 
     def step_2(state, beside):
-        (d_up, d_down), pieces, others = state
-        d_up, d_down, last, beside = tied(d_up, d_down, jnp.where(end, g_second, g_far), beside)
-        d_far = along_z(tied(w_down, d_up)[0], far_pairs)
-        d_first = along_z(to_pass_on(d_up, d_down), out_pairs)
-        wb = unset((4, 4, 2) + gu.shape[1:], BF)
-        for piece, other, z_k in zip(pieces + [last], others + [swap(last, 1)], (z, z_b, z_c, z_d)):
-            wb = place(wb, piece[None, :, None], (z_k, 0, c, 0, 0))
-            wb = place(wb, other[None, :, None], (z_k, 0, 1 - c, 0, 0))
-        return beside, (d_up, d_down, d_far, d_first), wb.reshape(32 * rows, -1)
-
-    def step_3(state):
-        d_up, d_down, d_far, d_first = state
-        d_second = along_z(d_far, out_pairs)
-        wd = unset((4, 2, ff_rows, width), BF)
-        for piece, z_k in (
-            (w_down, z),
-            (near_side(d_up, d_down), z_b),
-            (jnp.where(end, d_first, d_down), z_c),
-            (jnp.where(end, d_second, d_far), z_d),
-        ):
-            wd = place(wd, piece[None, None], (z_k, c, 0, 0))
-            wd = place(wd, swap(piece, 1)[None, None], (z_k, 1 - c, 0, 0))
-        return wd.reshape(8 * ff_rows, width)
-
-    return gathered, step_1, step_2, step_3
-
-
-def plane_reduce(parts, place_bits):
+        g_in, f_in, g_second, d_up, d_down = state
+        pieces = jnp.stack(
+            [gu, near_side(g_up, g_down), jnp.where(end, f_in, g_down), jnp.where(end, g_second, g_in)]
+        )
+        pieces, d_in, d_pass, d_up, d_down, beside = tied(
+            pieces, w_down, to_pass_on(d_up, d_down), d_up, d_down, beside
+        )
+        moving = (swap(pieces, 1), along_z(d_in, far_pairs), along_z(d_pass, out_pairs))
+
+        def step_3(others, d_far, d_first):
+            d_second = along_z(d_far, out_pairs)
+            wb = unset((4, 4, 2) + gu.shape[1:], BF)
+            places = (z, z_b, z_c, z_d)
+            for k in range(4):
+                wb = place(wb, pieces[k][None, :, None], (places[k], 0, c, 0, 0))
+                wb = place(wb, others[k][None, :, None], (places[k], 0, 1 - c, 0, 0))
+            d_all = jnp.stack(
+                [
+                    w_down,
+                    near_side(d_up, d_down),
+                    jnp.where(end, d_first, d_down),
+                    jnp.where(end, d_second, d_far),
+                ]
+            )
+            d_others = swap(d_all, 1)
+            wd = unset((4, 2, ff_rows, width), BF)
+            for k in range(4):
+                wd = place(wd, d_all[k][None, None], (places[k], c, 0, 0))
+                wd = place(wd, d_others[k][None, None], (places[k], 1 - c, 0, 0))
+            return wb.reshape(32 * rows, -1), wd.reshape(8 * ff_rows, width)
+
+        return beside, moving, step_3
+
+    return gathered, step_1, step_2
+
+
+def plane_step_1(parts, place_bits):
     z, y, x, c = place_bits
     half = parts.shape[0] // 2
     a, b = parts[:half], parts[half:]
-    came_a, came_b = tied(
-        swap(pick(a, 1 - y, 1).astype(BF), 4), swap(pick(b, 1 - x, 2).astype(BF), 2)
-    )
-    a = pick(a, y, 1) + came_a.astype(F32)
-    b = pick(b, x, 2) + came_b.astype(F32)
-    came_a, came_b = tied(
-        swap(pick(a, 1 - x, 1).astype(BF), 2), swap(pick(b, 1 - y, 1).astype(BF), 4)
-    )
-    a = pick(a, x, 1) + came_a.astype(F32)
-    b = pick(b, y, 1) + came_b.astype(F32)
+    return (swap(pick(a, 1 - y, 1).astype(BF), 4), swap(pick(b, 1 - x, 2).astype(BF), 2))
+
+
+def plane_step_2(parts, came, place_bits):
+    z, y, x, c = place_bits
+    half = parts.shape[0] // 2
+    a = pick(parts[:half], y, 1) + came[0].astype(F32)
+    b = pick(parts[half:], x, 2) + came[1].astype(F32)
+    moving = (swap(pick(a, 1 - x, 1).astype(BF), 2), swap(pick(b, 1 - y, 1).astype(BF), 4))
+    return (a, b), moving
+
+
+def plane_step_3(sums, came, place_bits):
+    z, y, x, c = place_bits
+    a = pick(sums[0], x, 1) + came[0].astype(F32)
+    b = pick(sums[1], y, 1) + came[1].astype(F32)
     return jnp.concatenate([a, b])
 
 
@@ -359,26 +370,29 @@
     )
 
 
-def split_gather(rows, beside=()):
+def split_gather(rows, beside=(), then=lambda *values: values):
     half = rows.shape[0] // 2
     a, b = rows[:half], rows[half:]
     a_x, b_y, *beside = tied(swap(a, 2), swap(b, 4), *beside)
-    a_far, b_far = tied(swap(jnp.concatenate([a, a_x]), 4), swap(jnp.concatenate([b, b_y]), 2))
-    return (jnp.concatenate([a, a_x, b, b_y]), jnp.concatenate([a_far, b_far]), beside)
-
-
-def split_reduce(near, far, beside=lambda: (), later=lambda *values: ()):
+    a2, b2 = tied(jnp.concatenate([a, a_x]), jnp.concatenate([b, b_y]))
+    a_far, b_far = swap(a2, 4), swap(b2, 2)
+    beside = then(*beside)
+    a_far, b_far = tied(a_far, b_far)
+    return (jnp.concatenate([a2, b2]), jnp.concatenate([a_far, b_far]), beside)
+
+
+def split_reduce(near, far, beside=(), later=lambda *values: values):
     two = far.shape[0] // 2
     one = two // 2
     low = far.astype(BF)
-    came_a, came_b, *done = tied(swap(low[:two], 4), swap(low[two:], 2), *beside())
+    came_a, came_b, *beside = tied(swap(low[:two], 4), swap(low[two:], 2), *beside)
     a = near[:two] + came_a.astype(F32)
     b = near[two:] + came_b.astype(F32)
-    came_a, came_b, *done = tied(
-        swap(a[one:].astype(BF), 2), swap(b[one:].astype(BF), 4), *later(*done)
+    came_a, came_b, *beside = tied(
+        swap(a[one:].astype(BF), 2), swap(b[one:].astype(BF), 4), *later(*beside)
     )
     own = jnp.concatenate([a[:one] + came_a.astype(F32), b[:one] + came_b.astype(F32)])
-    return (own, *done)
+    return (own, *beside)
 
 
 def spread_columns(came, p, part):
@@ -400,21 +414,6 @@
         )
         for start in (0, units)
     )
-
-
-def total_of(value):
-    n = lax.axis_size("dp")
-    mask = 1
-    while mask < n:
-        value = value + swap(value, mask)
-        mask *= 2
-    return value
-
-
-def scatter_gains(partial, position):
-    n = lax.axis_size("dp")
-    rows = partial.shape[1] // n
-    return lax.dynamic_slice_in_dim(total_of(partial), position * rows, rows, 1)
 
 
 def rotation_tables(length, width):
@@ -520,7 +519,7 @@
     gains = jnp.pad(gains, ((0, 0), (0, LANES - 2)))
     local = packed([w_query, key_weight_matrix, value_weight_matrix, w_output, gains])
     if planes == 4:
-        gathered, step_1, step_2, step_3 = gather_weights(local, w_gate, w_up, w_down, bits)
+        gathered, step_1, step_2 = gather_weights(local, w_gate, w_up, w_down, bits)
     else:
         gathered, wb, wd = gather_weights_plainly(local, w_gate, w_up, w_down, p)
 
@@ -538,7 +537,7 @@
         grouped = (sequences, SEQ, KEY_VALUE_HEADS, groups, HEAD_SIZE)
         raw = mm(normed_in, wqkv)
         if planes == 4:
-            moving = step_1(raw)
+            raw, moving = step_1(raw)
         query = turn(raw[:, :width].reshape(heads), cosine_lookup, sine_lookup)
         query = query.astype(BF).reshape(grouped)
         key = raw[:, width : width + kv_width].reshape(kv_heads)
@@ -548,16 +547,15 @@
         probs_low = probs.astype(BF)
         mixed = jnp.einsum("bhrqk,bkhd->bqhrd", probs_low, value, preferred_element_type=F32)
         mixed = mixed.reshape(count, width).astype(BF)
-        if planes == 4:
-            mixed, moving, wb = step_2(moving, mixed)
         hidden_res = inputs_f + mm(mixed, wo)
         normed_two, inv_ffn = norm_rows(hidden_res, gain_mid)
         normed_mid = normed_two.astype(BF)
 
     with jax.named_scope("ffn_forward"):
         if planes == 4:
+            normed_mid, moving, step_3 = step_2(moving, normed_mid)
             near, far, moving = split_gather(normed_mid, moving)
-            wd = step_3(moving)
+            wb, wd = step_3(*moving)
         else:
             near, far, moving = split_gather(normed_mid)
         y_near, pre_near, hid_near = ffn_forward(near, wb, wd)
@@ -569,52 +567,88 @@
         mask_f = valid_mask.astype(F32)
         grad_out = (result - teacher.astype(F32)) * mask_f[:, None]
         sums = jnp.stack([jnp.sum(grad_out * grad_out), jnp.sum(mask_f)])
-        sums = total_of(jnp.broadcast_to(sums[:, None], (2, LANES)))
-        loss = sums[0, 0] / (sums[1, 0] * width)
+        sums = jnp.broadcast_to(sums[:, None], (2, LANES))
+
+    high = n // 2
+    rest = [1 << k for k in range(4, n.bit_length() - 2)]
 
     with jax.named_scope("ffn_backward"):
-        grad_low = grad_out.astype(BF)
-        d_near, d_far, _ = split_gather(grad_low)
+        grad_low, sums = tied(grad_out.astype(BF), sums)
+
+        def sums_further(*came):
+            value = sums + came[0]
+            for mask in rest:
+                value = value + swap(value, mask)
+            return (value, swap(value, 8))
+
+        d_near, d_far, (sums, sums_came) = split_gather(grad_low, (swap(sums, 1),), sums_further)
         m_near, g_near = ffn_backward(d_near, pre_near, wb, wd)
         m_far, g_far = ffn_backward(d_far, pre_far, wb, wd)
+        m_near, m_far, sums, sums_came = tied(m_near, m_far, sums, sums_came)
+        sums = sums + sums_came
         by_core = core_first(width, rows)
         hid = jnp.concatenate([hid_near, hid_far])
         d_all = jnp.concatenate([d_near, d_far])
         mid_all = mm(jnp.concatenate([near, far]), by_core).astype(BF)
         g_all = jnp.concatenate([g_near, g_far])
         mid_mine, mid_theirs = core_halves(mid_all, c)
-
-        def beside():
-            g_down = t_mm(hid, d_all).reshape(planes, 2, ff_rows, width)
-            came = swap(pick(g_down, 1 - c, 1).astype(BF), 1)
-            return (pick(g_down, c, 1), came, t_mm(mid_theirs, g_all).astype(BF))
-
-        def later(own, came, theirs):
+        g_down = t_mm(hid, d_all).reshape(planes, 2, ff_rows, width)
+        beside = (
+            swap(pick(g_down, 1 - c, 1).astype(BF), 1),
+            pick(g_down, c, 1),
+            t_mm(mid_theirs, g_all).astype(BF),
+            sums,
+            swap(sums, high),
+        )
+
+        def later(came, own, theirs, sums, sums_came):
             g_down = own + came.astype(F32)
+            sums = sums + sums_came
             started = (walk_start(g_down, z),) if planes == 4 else ()
-            return (t_mm(mid_mine, g_all), swap(theirs, 1), g_down, *started)
-
-        grad_mid, g_both, came, g_down, *moving_down = split_reduce(m_near, m_far, beside, later)
-        g_both = (g_both + came.astype(F32)).reshape(planes, 4, rows, 2 * units)
-        if planes == 4:
-            moving_both = walk_start(g_both, z)
-            moving_down = walk_end(g_down, moving_down[0], z)
+            return (swap(theirs, 1), sums, swap(sums, 2), g_down, started)
+
+        def later_flat(*values):
+            theirs_came, sums, sums_came, g_down, started = later(*values)
+            moving.extend(started)
+            return (theirs_came, sums, sums_came, g_down)
+
+        moving = []
+        grad_mid, both_came, sums, sums_came, g_down = split_reduce(
+            m_near, m_far, beside, later_flat
+        )
+        sums = sums + sums_came
+        g_both = t_mm(mid_mine, g_all) + both_came.astype(F32)
+        g_both = g_both.reshape(planes, 4, rows, 2 * units)
 
     with jax.named_scope("attention_backward"):
         grad_gain_mid, grad_res = norm_back(grad_mid, hidden_res, inv_ffn, gain_mid)
         grad_res = grad_out + grad_res
         res_low = grad_res.astype(BF)
         mixed_mine, mixed_theirs = core_halves(mm(mixed, by_core).astype(BF), c)
-        wo_came = swap(t_mm(mixed_theirs, res_low).astype(BF), 1)
-        g_wo = t_mm(mixed_mine, res_low) + wo_came.astype(F32)
+        wo_came, sums_came = tied(swap(t_mm(mixed_theirs, res_low).astype(BF), 1), swap(sums, 4))
+        sums = sums + sums_came
+        loss = sums[0, 0] / (sums[1, 0] * width)
         shape = (planes, 2, 2, rows, -1)
-        g_wo = plane_reduce(g_wo.reshape(shape), bits)
+        g_wo = (t_mm(mixed_mine, res_low) + wo_came.astype(F32)).reshape(shape)
+        if planes == 4:
+            g_wo, down_came, g_down = tied(g_wo, moving[0], g_down)
+            down_moving = walk_end(g_down, down_came, z)
+        wo_moving = plane_step_1(g_wo, bits)
         grad_mixed = mm_t(res_low, wo).astype(BF).reshape(grouped)
         grad_probs = jnp.einsum(
             "bqhrd,bkhd->bhrqk", grad_mixed, value, preferred_element_type=F32
         )
         grad_scores = probs * (grad_probs - jnp.sum(probs * grad_probs, axis=-1, keepdims=True))
         grad_scores = grad_scores.astype(BF)
+        if planes == 4:
+            grad_scores, g_both, *came = tied(grad_scores, g_both, *wo_moving, *down_moving)
+            wo_came, down_came = came[:2], came[2:]
+            g_down = owned(g_down, down_came, z)
+            both_moving = walk_start(g_both, z)
+        else:
+            wo_came = wo_moving
+            g_down = z_reduce(g_down, z)
+        g_wo, wo_moving = plane_step_2(g_wo, wo_came, bits)
         grad_query = score_scale * jnp.einsum(
             "bhrqk,bkhd->bqhrd", grad_scores, key, preferred_element_type=F32
         )
@@ -630,41 +664,64 @@
         value_back = grad_value.reshape(count, kv_width).astype(BF)
         grad_raw = jnp.concatenate([query_back, key_back, value_back], axis=1)
         normed_mine, normed_theirs = core_halves(mm(normed_in, by_core).astype(BF), c)
-        if planes == 4:
-            grad_raw, moving_both, g_wo, *moving_down = tied(
-                grad_raw, moving_both, g_wo, *moving_down
-            )
-            moving_both = walk_end(g_both, moving_both, z)
-            g_down = owned(g_down, moving_down, z)
-        else:
-            g_down = z_reduce(g_down, z)
-        q_came = swap(t_mm(normed_theirs, grad_raw[:, :width]).astype(BF), 1)
-        kv_came = swap(t_mm(normed_theirs, grad_raw[:, width:]).astype(BF), 1)
-        g_q = t_mm(normed_mine, grad_raw[:, :width]) + q_came.astype(F32)
-        g_kv = t_mm(normed_mine, grad_raw[:, width:]) + kv_came.astype(F32)
+        grad_raw, *wo_came = tied(grad_raw, *wo_moving)
+        g_wo = plane_step_3(g_wo, wo_came, bits)
+
+    with jax.named_scope("input_gradient"):
+        qkv_came = swap(t_mm(normed_theirs, grad_raw).astype(BF), 1)
+        g_qkv = t_mm(normed_mine, grad_raw) + qkv_came.astype(F32)
         grad_in = mm_t(grad_raw, wqkv)
         grad_gain_in, grad_tokens = norm_back(grad_in, inputs_f, inv_attn, gain_in)
         input_grad = (grad_res + grad_tokens).astype(BF)
+        gains = jnp.stack([grad_gain_in, grad_gain_mid])
 
     with jax.named_scope("weight_gradients_to_owners"):
+        g_qkv = g_qkv.reshape(shape)
+        g_qkv, gains = tied(g_qkv, gains)
+        qkv_came = tied(*plane_step_1(g_qkv, bits), swap(gains, 1))
+        gains = gains + qkv_came[2]
         if planes == 4:
-            g_both = owned(g_both, moving_both, z).astype(BF)
+            g_both, both_came, *qkv_came = tied(g_both, both_moving, *qkv_came[:2])
+            both_moving = walk_end(g_both, both_came, z)
         else:
-            g_both = z_reduce(g_both, z).astype(BF)
-        g_q = plane_reduce(g_q.reshape(shape), bits)
-        came = [pick(g_both, p, 0)]
-        for r in (1, 2, 3):
-            came.append(swap(pick(g_both, p ^ r, 0), r << 1))
-        grad_gate, grad_up = spread_columns(came, p, part)
-        g_kv = plane_reduce(g_kv.reshape(shape), bits)
-        g_wo = z_reduce(g_wo, z)
-        g_wq = z_reduce(g_q, z)
-        g_kv = z_reduce(g_kv, z)
-        g_wk, g_wv = g_kv[:, :kv_width], g_kv[:, kv_width:]
-
-    with jax.named_scope("gain_gradients"):
-        g_gains = jnp.stack([grad_gain_in, grad_gain_mid])
-        g_gains = scatter_gains(g_gains, position)
+            g_both = z_reduce(g_both, z)
+        g_qkv, qkv_moving = plane_step_2(g_qkv, qkv_came[:2], bits)
+        if planes == 4:
+            *qkv_came, both_0, both_1, both_2 = tied(*qkv_moving, *both_moving)
+            g_both = owned(g_both, (both_0, both_1, both_2), z)
+        else:
+            qkv_came = qkv_moving
+        g_qkv = plane_step_3(g_qkv, qkv_came, bits)
+        g_both = g_both.astype(BF)
+        g_all = jnp.concatenate([g_qkv, g_wo], axis=2)
+        gains, g_all, g_both = tied(gains, g_all, g_both)
+        if planes == 4:
+            all_moving = walk_start(g_all, z)
+        came = [pick(g_both, p ^ r, 0) for r in range(4)]
+        gains_came, *moved = tied(
+            swap(gains, 2), *[swap(came[r], r << 1) for r in (1, 2, 3)]
+        )
+        gains = gains + gains_came
+        for mask in rest:
+            gains = gains + swap(gains, mask)
+        grad_gate, grad_up = spread_columns([came[0]] + moved, p, part)
+        gains_came = swap(gains, 4)
+        if planes == 4:
+            g_all, all_came, gains_came = tied(g_all, all_moving, gains_came)
+            gains = gains + gains_came
+            all_0, all_1, all_2, gains_came = tied(*walk_end(g_all, all_came, z), swap(gains, 8))
+            g_all = owned(g_all, (all_0, all_1, all_2), z)
+        else:
+            gains = gains + gains_came
+            gains_came = swap(gains, 8)
+            g_all = z_reduce(g_all, z)
+        gains = gains + gains_came
+        gains = gains + swap(gains, high)
+        g_gains = lax.dynamic_slice_in_dim(gains, position * rows, rows, 1)
+        g_wq = g_all[:, :width]
+        g_wk = g_all[:, width : width + kv_width]
+        g_wv = g_all[:, width + kv_width : wide]
+        g_wo = g_all[:, wide:]
 
     return (
         out_act,

time: 571 us -> 634 us (1.11)
  local copies, waits for them, and re-layouts: 54.8 us -> 91.5 us
  starting transfers between devices: 130 us -> 114 us
  waiting for transfers between devices: 233 us -> 247 us
  other arithmetic: 43.1 us -> 56.9 us
  matrix products: 94.8 us -> 108 us
    ppermute x23 -> x27, waiting for transfers between devices: 61.4 us -> 93.6 us  [along_z(): lax.ppermute(value, 'dp', [(8 * a + i, 8 * b + i) for a, b in pairs for i...]
    ppermute x82 -> x58, starting transfers between devices: 75.3 us -> 53.8 us  [swap(): return lax.ppermute(value, 'dp', [(i, i ^ mask) for i in range(n)])]
    ppermute x82 -> x58, waiting for transfers between devices: 172 us -> 154 us  [swap(): return lax.ppermute(value, 'dp', [(i, i ^ mask) for i in range(n)])]
    dynamic_update_slice x28 -> x32, local copies, waits for them, and re-layouts: 18.4 us -> 34.9 us  [place(): return lax.dynamic_update_slice(out, piece, where)]
    dot_general x24 -> x22, matrix products: 87.2 us -> 102 us  [dot(): return lax.dot_general(a, b, (dims, ((), ())), preferred_element_type=F32)]
    optimization_barrier x0 -> x4, local copies, waits for them, and re-layouts: none -> 9.25 us  [tied(): return lax.optimization_barrier(values)]
    another operation x5 -> x16, other arithmetic: 3.81 us -> 11.1 us  [the longest x4 4.63 us: step_2(): jnp.stack([gu, near_side(g_up, g_down), jnp.where(end, f_in, g_down), jnp...]
    add x26 -> x21, other arithmetic: 4.62 us -> 11.7 us  [the longest x1 6.92 us: body(): g_both = t_mm(mid_mine, g_all) + both_came.astype(F32)]
  transfers between devices with their start and end apart: 105 -> 85, of which waited for: 50 -> 43; matrix products, arithmetic and copies ran while one was open for 26% -> 35% of each run, Pallas kernels for 0% -> 0%
where the time goes in v4:
time: 634 us; the launch traced here: 626 us
  waiting for transfers between devices  247 us (39%)
  starting transfers between devices  114 us (18%)
  matrix products  108 us (17%)
  local copies, waits for them, and re-layouts  91.5 us (14%)
  other arithmetic  56.9 us (9%)
  between operations  6.49 us (1%)
    ppermute x58, waiting for transfers between devices, swap(): return lax.ppermute(value, 'dp', [(i, i ^ mask) for i in range(n)])  154 us
    dot_general x22, matrix products, dot(): return lax.dot_general(a, b, (dims, ((), ())), preferred_element_type=F32)  102 us
    ppermute x27, waiting for transfers between devices, along_z(): lax.ppermute(value, 'dp', [(8 * a + i, 8 * b + i) for a, b in pairs for i...  93.6 us
    ppermute x27, starting transfers between devices, along_z(): lax.ppermute(value, 'dp', [(8 * a + i, 8 * b + i) for a, b in pairs for i...  60.2 us
    ppermute x58, starting transfers between devices, swap(): return lax.ppermute(value, 'dp', [(i, i ^ mask) for i in range(n)])  53.8 us
    dynamic_update_slice x32, local copies, waits for them, and re-layouts, place(): return lax.dynamic_update_slice(out, piece, where)  34.9 us
    unnamed x244, local copies, waits for them, and re-layouts  17.5 us
  transfers between devices with their start and end apart: 85, of which 43 were waited for; matrix products, arithmetic and copies ran while one was open for 35% of the time, Pallas kernels for 0%

profile of v4, /device:TPU:0, one launch (start us, length us, event | category | flops | bytes accessed | tf_op | source)
XLA Modules:
  0.0 625.9 jit_solution(6033126582404321516)
XLA Ops:
  4.1 4.9 collective-permute-start
  19.4 4.0 collective-permute-done.3
  24.7 5.3 collective-permute-start.7
  34.3 5.9 collective-permute-done.6
  40.2 2.5 collective-permute-done.8
  51.2 21.1 %collective-permute-done.11 = bf16[48,4736]{1,0:T(8,128)(2,1)S(1)} collective-permute-done((bf16[48,4736]{1,0:T(8,128)(2,1)S(1)}, bf16[48,4736]{1,0:T(8,128)(2,1)S(1)}, u32[]{:S(2)}, u32[]{:S(2)}) %collective-permute-start.11) | collective-permute-done | bytes 454688 | tf_op jit(solution)/shard_map/phase_2/ppermute | solution.py:92
  76.0 9.3 %collective-permute-done.12 = bf16[48,4736]{1,0:T(8,128)(2,1)S(1)} collective-permute-done((bf16[48,4736]{1,0:T(8,128)(2,1)S(1)}, bf16[48,4736]{1,0:T(8,128)(2,1)S(1)}, u32[]{:S(2)}, u32[]{:S(2)}) %collective-permute-start.12) | collective-permute-done | bytes 454688 | tf_op jit(solution)/shard_map/phase_3/ppermute | solution.py:41
  96.6 13.0 %collective-permute-done.19 = bf16[2,48,4736]{2,1,0:T(8,128)(2,1)S(1)} collective-permute-done((bf16[2,48,4736]{2,1,0:T(8,128)(2,1)S(1)}, bf16[2,48,4736]{2,1,0:T(8,128)(2,1)S(1)}, u32[]{:S(2)}, u32[]{:S(2)}) %collective-permute-start.19) | collective-permute-done | bytes 909344 | tf_op jit(solution)/shard_map/phase_4/ppermute | solution.py:41
  120.9 2.2 fusion.210
  123.3 5.2 fusion.7
  132.8 5.5 collective-permute-start.26
  140.1 2.4 copy.191
  148.9 2.2 fusion.220
  155.5 3.8 multiply_reduce_fusion.3
  166.8 15.5 %collective-permute-done.24 = bf16[4,48,2048]{2,1,0:T(8,128)(2,1)S(1)} collective-permute-done((bf16[4,48,2048]{2,1,0:T(8,128)(2,1)}, bf16[4,48,2048]{2,1,0:T(8,128)(2,1)S(1)}, u32[]{:S(2)}, u32[]{:S(2)}) %collective-permute-start.24) | collective-permute-done | bytes 786464 | tf_op jit(solution)/shard_map/attention_forward/ppermute | solution.py:92
  194.5 4.0 collective-permute-done.27
  200.1 3.8 collective-permute-done.31
  219.4 2.2 bitcast_dynamic-update-slice_fusion.23
  221.6 8.1 %collective-permute-done.32 = bf16[128,1536]{1,0:T(8,128)(2,1)S(1)} collective-permute-done((bf16[128,1536]{1,0:T(8,128)(2,1)S(1)}, bf16[128,1536]{1,0:T(8,128)(2,1)S(1)}, u32[]{:S(2)}, u32[]{:S(2)}) %collective-permute-start.32) | collective-permute-done | bytes 393248 | tf_op jit(solution)/shard_map/ffn_forward/ppermute | solution.py:92
  231.2 6.1 fusion.65
  237.4 3.4 fusion.69
  252.2 14.9 %collective-permute-done.36 = bf16[256,1536]{1,0:T(8,128)(2,1)S(1)} collective-permute-done((bf16[256,1536]{1,0:T(8,128)(2,1)S(1)}, bf16[256,1536]{1,0:T(8,128)(2,1)S(1)}, u32[]{:S(2)}, u32[]{:S(2)}) %collective-permute-start.36) | collective-permute-done | bytes 786464 | tf_op jit(solution)/shard_map/ffn_forward/ppermute | solution.py:41
  274.0 4.3 fusion.35
  280.1 2.3 collective-permute-done.39
  290.0 9.2 %fusion.16 = bf16[1024,1536]{1,0:T(8,128)(2,1)} fusion(s32[1536]{0:T(1024)S(1)} %copy-done.78, bf16[256,1536]{1,0:T(8,128)(2,1)S(1)} %copy-done.91, bf16[256,1536]{1,0:T(8,128)(2,1)S(1)} %copy-done.89, bf16[256,1536]{1,0:T(8,128)(2,1)S(1)} %copy-done.57, bf16[256,1536]{1,0:T(8,128)(2,1)S(1)} %copy-done.59), kind=kOutput, calls=%fused_computation.22 | convolution fusion | flops 4848353280 | bytes 6297600 | tf_op jit(solution)/shard_map/ffn_backward/dot_general | solution.py:24
  302.1 2.4 multiply_convert_fusion.3
  305.9 3.4 fusion.39
  309.4 10.0 %collective-permute-done.43 = bf16[256,1536]{1,0:T(8,128)(2,1)S(1)} collective-permute-done((bf16[256,1536]{1,0:T(8,128)(2,1)S(1)}, bf16[256,1536]{1,0:T(8,128)(2,1)S(1)}, u32[]{:S(2)}, u32[]{:S(2)}) %collective-permute-start.43) | collective-permute-done | bytes 786464 | tf_op jit(solution)/shard_map/ffn_backward/ppermute | solution.py:41
  320.2 2.3 multiply_convert_fusion.1
  322.6 3.5 fusion.17
  326.1 3.7 fusion.43
  333.9 5.2 convolution_convert_fusion.2
  339.3 11.9 %collective-permute-done.46 = bf16[256,1536]{1,0:T(8,128)(2,1)S(1)} collective-permute-done((bf16[256,1536]{1,0:T(8,128)(2,1)S(1)}, bf16[256,1536]{1,0:T(8,128)(2,1)S(1)}, u32[]{:S(2)}, u32[]{:S(2)}) %collective-permute-start.46) | collective-permute-done | bytes 786464 | tf_op jit(solution)/shard_map/ffn_backward/ppermute | solution.py:41
  354.1 19.8 %fusion.84 = f32[768,2048]{1,0:T(8,128)} fusion(bf16[1024,1536]{1,0:T(8,128)(2,1)S(1)} %copy-done.93, s32[]{:T(128)S(6)} %select_n.577, bf16[512,1024]{1,0:T(8,128)(2,1)S(1)} %copy-done.102, bf16[512,1024]{1,0:T(8,128)(2,1)S(1)} %copy-done.100, bf16[512,1024]{1,0:T(8,128)(2,1)S(1)} %copy-done.97, bf16[512,1024]{1,0:T(8,128)(2,1)S(1)} %copy-done.95), kind=kOutput, calls=%fused_computation.135 | convolution fusion | flops 3238002688 | bytes 12058628 | tf_op jit(solution)/shard_map/ffn_backward/dot_general | solution.py:24
  379.3 5.5 collective-permute-start.56
  384.8 2.5 collective-permute-done.50
  389.8 2.3 convolution_convert_fusion.1
  393.2 4.6 fusion.36
  397.8 4.0 reshape.286
  407.8 6.9 %convert_add_fusion.1 = f32[768,2048]{1,0:T(8,128)} fusion(f32[768,2048]{1,0:T(8,128)} %fusion.84, bf16[768,2048]{1,0:T(8,128)(2,1)S(1)} %copy-done.29), kind=kLoop, calls=%fused_computation.11 | loop fusion | flops 3145728 | bytes 15728640 | tf_op jit(solution)/shard_map/ffn_backward/add | solution.py:620
  415.7 2.3 convert_add_fusion.2
  421.0 4.4 collective-permute-start.59
  434.1 12.6 %collective-permute-done.60 = bf16[128,1536]{1,0:T(8,128)(2,1)S(1)} collective-permute-done((bf16[128,1536]{1,0:T(8,128)(2,1)S(1)}, bf16[128,1536]{1,0:T(8,128)(2,1)S(1)}, u32[]{:S(2)}, u32[]{:S(2)}) %collective-permute-start.60) | collective-permute-done | bytes 393248 | tf_op jit(solution)/shard_map/attention_backward/ppermute | solution.py:92
  456.9 3.6 convolution_convert_fusion
  466.5 3.8 collective-permute-start.68
  470.3 2.2 fusion.108
  472.5 7.7 %fusion.63 = (f32[1536]{0:T(1024)S(1)}, f32[256]{0:T(256)S(1)}, f32[256,1536]{1,0:T(8,128)}) fusion(bf16[256,1536]{1,0:T(8,128)(2,1)S(1)} %copy-done.15, f32[256]{0:T(256)S(1)} %copy-done.80, f32[1536]{0:T(1024)S(1)} %convert_reduce_fusion.1, bf16[256,3072]{0,1:T(8,128)(2,1)S(1)} %pad_maximum_fusion.7, bf16[1536,4736]{1,0:T(8,128)(2,1)} %bitcast.416), kind=kOutput, calls=%fused_computation.99 | convolution fusion | flops 2418669824 | bytes 13383680 | tf_op jit(solution)/shard_map/input_gradient/dot_general | solution.py:24
  480.2 3.9 convert_add_fusion
  484.0 4.2 copy.172
  488.2 2.6 slice.497
  492.1 4.2 copy.171
  496.8 2.8 slice.496
  502.6 21.9 %collective-permute-done.66 = bf16[2,2,48,3072]{3,2,0,1:T(8,128)(2,1)S(1)} collective-permute-done((bf16[2,2,48,3072]{3,2,0,1:T(8,128)(2,1)}, bf16[2,2,48,3072]{3,2,0,1:T(8,128)(2,1)S(1)}, u32[]{:S(2)}, u32[]{:S(2)}) %collective-permute-start.66) | collective-permute-done | bytes 1179680 | tf_op jit(solution)/shard_map/weight_gradients_to_owners/ppermute | solution.py:41
  524.5 3.4 collective-permute-done.65
  539.1 10.6 %collective-permute-done.70 = bf16[2,48,3072]{2,1,0:T(8,128)(2,1)S(1)} collective-permute-done((bf16[2,48,3072]{2,1,0:T(8,128)(2,1)S(1)}, bf16[2,48,3072]{2,1,0:T(8,128)(2,1)S(1)}, u32[]{:S(2)}, u32[]{:S(2)}) %collective-permute-start.70) | collective-permute-done | bytes 589856 | tf_op jit(solution)/shard_map/weight_gradients_to_owners/ppermute | solution.py:41
  550.9 3.2 collective-permute-done.72
  554.0 16.2 %collective-permute-done.73 = bf16[4,48,2048]{2,1,0:T(8,128)(2,1)S(1)} collective-permute-done((bf16[4,48,2048]{2,1,0:T(8,128)(2,1)S(1)}, bf16[4,48,2048]{2,1,0:T(8,128)(2,1)S(1)}, u32[]{:S(2)}, u32[]{:S(2)}) %collective-permute-start.73) | collective-permute-done | bytes 786464 | tf_op jit(solution)/shard_map/weight_gradients_to_owners/ppermute | solution.py:92
  578.0 3.2 collective-permute-done.75
  583.6 2.3 collective-permute-done.79
  585.9 8.4 %collective-permute-done.74 = bf16[2,48,4608]{2,1,0:T(8,128)(2,1)S(1)} collective-permute-done((bf16[2,48,4608]{2,1,0:T(8,128)(2,1)S(1)}, bf16[2,48,4608]{2,1,0:T(8,128)(2,1)S(1)}, u32[]{:S(2)}, u32[]{:S(2)}) %collective-permute-start.74) | collective-permute-done | bytes 884768 | tf_op jit(solution)/shard_map/weight_gradients_to_owners/ppermute | solution.py:92
  594.8 4.4 collective-permute-start.80
  601.8 3.2 collective-permute-start.83
  605.1 14.0 %collective-permute-done.83 = f32[2,1536]{1,0:T(2,128)S(1)} collective-permute-done((f32[2,1536]{1,0:T(2,128)S(1)}, f32[2,1536]{1,0:T(2,128)S(1)}, u32[]{:S(2)}, u32[]{:S(2)}) %collective-permute-start.83) | collective-permute-done | bytes 12320 | tf_op jit(solution)/shard_map/weight_gradients_to_owners/ppermute | solution.py:41
  621.0 2.8 collective-permute-done.84
  (580 shorter events, 222.6 us)
Async XLA Ops:
  4.1 19.3 %collective-permute-start = (bf16[48,4736]{1,0:T(8,128)(2,1)}, bf16[48,4736]{1,0:T(8,128)(2,1)S(1)}, u32[]{:S(2)}, u32[]{:S(2)}) collective-permute-start(bf16[48,4736]{1,0:T(8,128)(2,1)} %packed.1), channel_id=1, source_target_pairs={{0,8},{1,9},{2,10},{3,11},{4,12},{5,13},{6,14},{7,15},{8,16},{9,17... | collective-permute-start | bytes 1363976 | tf_op jit(solution)/shard_map/phase_0/ppermute | solution.py:92
  9.0 14.3 %collective-permute-start.1 = (bf16[48,4736]{1,0:T(8,128)(2,1)}, bf16[48,4736]{1,0:T(8,128)(2,1)S(1)}, u32[]{:S(2)}, u32[]{:S(2)}) collective-permute-start(bf16[48,4736]{1,0:T(8,128)(2,1)} %packed.1), channel_id=1, source_target_pairs={{8,0},{9,1},{10,2},{11,3},{12,4},{13,5},{14,6},{15,7},{16,8},{17,9... | collective-permute-start | bytes 1363976 | tf_op jit(solution)/shard_map/phase_0/ppermute | solution.py:92
  23.4 10.8 %collective-permute-start.5 = (bf16[48,4736]{1,0:T(8,128)(2,1)S(1)}, bf16[48,4736]{1,0:T(8,128)(2,1)S(1)}, u32[]{:S(2)}, u32[]{:S(2)}) collective-permute-start(bf16[48,4736]{1,0:T(8,128)(2,1)S(1)} %copy-done.30), channel_id=1, source_target_pairs={{0,2},{1,3},{2,0},{3,1},{4,6},{5,7},{6,4},{7,5},{8,10},{9,11},{10,... | collective-permute-start | bytes 1363976 | tf_op jit(solution)/shard_map/phase_1/ppermute | solution.py:41
  24.7 15.5 %collective-permute-start.7 = (bf16[48,4736]{1,0:T(8,128)(2,1)S(1)}, bf16[48,4736]{1,0:T(8,128)(2,1)S(1)}, u32[]{:S(2)}, u32[]{:S(2)}) collective-permute-start(bf16[48,4736]{1,0:T(8,128)(2,1)S(1)} %copy-done.30), channel_id=1, source_target_pairs={{0,16},{1,17},{2,18},{3,19},{4,20},{5,21},{6,22},{7,23},{24,8},{25... | collective-permute-start | bytes 1363976 | tf_op jit(solution)/shard_map/phase_1/ppermute | solution.py:92
  30.9 11.9 %collective-permute-start.8 = (bf16[48,4736]{1,0:T(8,128)(2,1)S(1)}, bf16[48,4736]{1,0:T(8,128)(2,1)S(1)}, u32[]{:S(2)}, u32[]{:S(2)}) collective-permute-start(bf16[48,4736]{1,0:T(8,128)(2,1)S(1)} %get-tuple-element.154), channel_id=1, source_target_pairs={{8,0},{9,1},{10,2},{11,3},{12,4},{13,5},{14,6},{15,7},{16,24},{17,... | collective-permute-start | bytes 1363976 | tf_op jit(solution)/shard_map/phase_1/ppermute | solution.py:92
  43.2 32.9 %collective-permute-start.14 = (bf16[4,48,2048]{2,1,0:T(8,128)(2,1)S(1)}, bf16[4,48,2048]{2,1,0:T(8,128)(2,1)S(1)}, u32[]{:S(2)}, u32[]{:S(2)}) collective-permute-start(bf16[4,48,2048]{2,1,0:T(8,128)(2,1)S(1)} %bitcast_dynamic-update-slice_fusion.28), channel_id=1, source_target_pairs={{0,8},{1,9},{2,10},{3,11},{4,12},{5,13},{6,14},{7,15},{8,16},{9,17... | collective-permute-start | bytes 2359304 | tf_op jit(solution)/shard_map/phase_2/ppermute | solution.py:92
  44.7 31.4 %collective-permute-start.15 = (bf16[4,48,2048]{2,1,0:T(8,128)(2,1)S(1)}, bf16[4,48,2048]{2,1,0:T(8,128)(2,1)S(1)}, u32[]{:S(2)}, u32[]{:S(2)}) collective-permute-start(bf16[4,48,2048]{2,1,0:T(8,128)(2,1)S(1)} %bitcast_dynamic-update-slice_fusion.28), channel_id=1, source_target_pairs={{8,0},{9,1},{10,2},{11,3},{12,4},{13,5},{14,6},{15,7},{16,8},{17,9... | collective-permute-start | bytes 2359304 | tf_op jit(solution)/shard_map/phase_2/ppermute | solution.py:92
  46.0 26.3 %collective-permute-start.10 = (bf16[2,48,4736]{2,1,0:T(8,128)(2,1)S(1)}, bf16[2,48,4736]{2,1,0:T(8,128)(2,1)S(1)}, u32[]{:S(2)}, u32[]{:S(2)}) collective-permute-start(bf16[2,48,4736]{2,1,0:T(8,128)(2,1)S(1)} %pad_maximum_fusion.10), channel_id=1, source_target_pairs={{0,2},{1,3},{2,0},{3,1},{4,6},{5,7},{6,4},{7,5},{8,10},{9,11},{10,... | collective-permute-start | bytes 2727944 | tf_op jit(solution)/shard_map/phase_2/ppermute | solution.py:41
  46.6 25.7 %collective-permute-start.9 = (bf16[2,48,4736]{2,1,0:T(8,128)(2,1)S(1)}, bf16[2,48,4736]{2,1,0:T(8,128)(2,1)S(1)}, u32[]{:S(2)}, u32[]{:S(2)}) collective-permute-start(bf16[2,48,4736]{2,1,0:T(8,128)(2,1)S(1)} %pad_maximum_fusion.9), channel_id=1, source_target_pairs={{0,4},{1,5},{2,6},{3,7},{4,0},{5,1},{6,2},{7,3},{8,12},{9,13},{10,... | collective-permute-start | bytes 2727944 | tf_op jit(solution)/shard_map/phase_2/ppermute | solution.py:41
  47.6 24.7 %collective-permute-start.11 = (bf16[48,4736]{1,0:T(8,128)(2,1)S(1)}, bf16[48,4736]{1,0:T(8,128)(2,1)S(1)}, u32[]{:S(2)}, u32[]{:S(2)}) collective-permute-start(bf16[48,4736]{1,0:T(8,128)(2,1)S(1)} %collective-permute-done.7), channel_id=1, source_target_pairs={{8,0},{9,1},{10,2},{11,3},{12,4},{13,5},{14,6},{15,7},{16,24},{17,... | collective-permute-start | bytes 1363976 | tf_op jit(solution)/shard_map/phase_2/ppermute | solution.py:92
  72.4 12.9 %collective-permute-start.16 = (bf16[2,2,48,4736]{3,2,1,0:T(8,128)(2,1)S(1)}, bf16[2,2,48,4736]{3,2,1,0:T(8,128)(2,1)S(1)}, u32[]{:S(2)}, u32[]{:S(2)}) collective-permute-start(bf16[2,2,48,4736]{3,2,1,0:T(8,128)(2,1)S(1)} %pad_maximum_fusion.1), channel_id=1, source_target_pairs={{0,1},{1,0},{2,3},{3,2},{4,5},{5,4},{6,7},{7,6},{8,9},{9,8},{10,11... | collective-permute-start | bytes 5455880 | tf_op jit(solution)/shard_map/phase_3/ppermute | solution.py:41
  72.5 12.8 %collective-permute-start.12 = (bf16[48,4736]{1,0:T(8,128)(2,1)S(1)}, bf16[48,4736]{1,0:T(8,128)(2,1)S(1)}, u32[]{:S(2)}, u32[]{:S(2)}) collective-permute-start(bf16[48,4736]{1,0:T(8,128)(2,1)S(1)} %broadcast_select_fusion.4), channel_id=1, source_target_pairs={{0,2},{1,3},{2,0},{3,1},{4,6},{5,7},{6,4},{7,5},{8,10},{9,11},{10,... | collective-permute-start | bytes 1363976 | tf_op jit(solution)/shard_map/phase_3/ppermute | solution.py:41
  72.5 12.8 %collective-permute-start.13 = (bf16[48,4736]{1,0:T(8,128)(2,1)S(1)}, bf16[48,4736]{1,0:T(8,128)(2,1)S(1)}, u32[]{:S(2)}, u32[]{:S(2)}) collective-permute-start(bf16[48,4736]{1,0:T(8,128)(2,1)S(1)} %broadcast_select_fusion.3), channel_id=1, source_target_pairs={{0,4},{1,5},{2,6},{3,7},{4,0},{5,1},{6,2},{7,3},{8,12},{9,13},{10,... | collective-permute-start | bytes 1363976 | tf_op jit(solution)/shard_map/phase_3/ppermute | solution.py:41
  87.0 23.3 %collective-permute-start.21 = (bf16[2,2,48,4736]{3,2,1,0:T(8,128)(2,1)S(1)}, bf16[2,2,48,4736]{3,2,1,0:T(8,128)(2,1)S(1)}, u32[]{:S(2)}, u32[]{:S(2)}) collective-permute-start(bf16[2,2,48,4736]{3,2,1,0:T(8,128)(2,1)S(1)} %pad_maximum_fusion.2), channel_id=1, source_target_pairs={{0,1},{1,0},{2,3},{3,2},{4,5},{5,4},{6,7},{7,6},{8,9},{9,8},{10,11... | collective-permute-start | bytes 5455880 | tf_op jit(solution)/shard_map/phase_4/ppermute | solution.py:41
  87.0 22.6 %collective-permute-start.19 = (bf16[2,48,4736]{2,1,0:T(8,128)(2,1)S(1)}, bf16[2,48,4736]{2,1,0:T(8,128)(2,1)S(1)}, u32[]{:S(2)}, u32[]{:S(2)}) collective-permute-start(bf16[2,48,4736]{2,1,0:T(8,128)(2,1)S(1)} %pad_maximum_fusion.11), channel_id=1, source_target_pairs={{0,4},{1,5},{2,6},{3,7},{4,0},{5,1},{6,2},{7,3},{8,12},{9,13},{10,... | collective-permute-start | bytes 2727944 | tf_op jit(solution)/shard_map/phase_4/ppermute | solution.py:41
  88.1 22.2 %collective-permute-start.20 = (bf16[2,48,4736]{2,1,0:T(8,128)(2,1)S(1)}, bf16[2,48,4736]{2,1,0:T(8,128)(2,1)S(1)}, u32[]{:S(2)}, u32[]{:S(2)}) collective-permute-start(bf16[2,48,4736]{2,1,0:T(8,128)(2,1)S(1)} %pad_maximum_fusion.12), channel_id=1, source_target_pairs={{0,2},{1,3},{2,0},{3,1},{4,6},{5,7},{6,4},{7,5},{8,10},{9,11},{10,... | collective-permute-start | bytes 2727944 | tf_op jit(solution)/shard_map/phase_4/ppermute | solution.py:41
  91.8 36.8 %collective-permute-start.17 = (bf16[4,48,2048]{2,1,0:T(8,128)(2,1)S(1)}, bf16[4,48,2048]{2,1,0:T(8,128)(2,1)S(1)}, u32[]{:S(2)}, u32[]{:S(2)}) collective-permute-start(bf16[4,48,2048]{2,1,0:T(8,128)(2,1)S(1)} %bitcast_dynamic-update-slice_fusion.28), channel_id=1, source_target_pairs={{0,16},{1,17},{2,18},{3,19},{4,20},{5,21},{6,22},{7,23},{24,8},{25... | collective-permute-start | bytes 2359304 | tf_op jit(solution)/shard_map/phase_4/ppermute | solution.py:92
  93.1 35.4 %collective-permute-start.18 = (bf16[4,48,2048]{2,1,0:T(8,128)(2,1)}, bf16[4,48,2048]{2,1,0:T(8,128)(2,1)S(1)}, u32[]{:S(2)}, u32[]{:S(2)}) collective-permute-start(bf16[4,48,2048]{2,1,0:T(8,128)(2,1)} %get-tuple-element.178), channel_id=1, source_target_pairs={{8,0},{9,1},{10,2},{11,3},{12,4},{13,5},{14,6},{15,7},{16,24},{17,... | collective-permute-start | bytes 2359304 | tf_op jit(solution)/shard_map/phase_4/ppermute | solution.py:92
  131.5 33.4 %collective-permute-start.25 = (bf16[128,1536]{1,0:T(8,128)(2,1)}, bf16[128,1536]{1,0:T(8,128)(2,1)S(1)}, u32[]{:S(2)}, u32[]{:S(2)}) collective-permute-start(bf16[128,1536]{1,0:T(8,128)(2,1)} %param.21), channel_id=1, source_target_pairs={{8,0},{9,1},{10,2},{11,3},{12,4},{13,5},{14,6},{15,7},{16,8},{17,9... | collective-permute-start | bytes 1179656 | tf_op jit(solution)/shard_map/attention_forward/ppermute | solution.py:92
  132.8 32.1 %collective-permute-start.26 = (bf16[128,1536]{1,0:T(8,128)(2,1)}, bf16[128,1536]{1,0:T(8,128)(2,1)}, u32[]{:S(2)}, u32[]{:S(2)}) collective-permute-start(bf16[128,1536]{1,0:T(8,128)(2,1)} %param.21), channel_id=1, source_target_pairs={{0,8},{1,9},{2,10},{3,11},{4,12},{5,13},{6,14},{7,15},{8,16},{9,17... | collective-permute-start | bytes 1179656 | tf_op jit(solution)/shard_map/attention_forward/ppermute | solution.py:92
  161.2 21.2 %collective-permute-start.24 = (bf16[4,48,2048]{2,1,0:T(8,128)(2,1)}, bf16[4,48,2048]{2,1,0:T(8,128)(2,1)S(1)}, u32[]{:S(2)}, u32[]{:S(2)}) collective-permute-start(bf16[4,48,2048]{2,1,0:T(8,128)(2,1)} %copy-done.47), channel_id=1, source_target_pairs={{8,0},{9,1},{10,2},{11,3},{12,4},{13,5},{14,6},{15,7},{16,24},{17,... | collective-permute-start | bytes 2359304 | tf_op jit(solution)/shard_map/attention_forward/ppermute | solution.py:92
  184.4 19.5 %collective-permute-start.29 = (bf16[4,4,48,2048]{3,2,1,0:T(8,128)(2,1)}, bf16[4,4,48,2048]{3,2,1,0:T(8,128)(2,1)}, u32[]{:S(2)}, u32[]{:S(2)}) collective-permute-start(bf16[4,4,48,2048]{3,2,1,0:T(8,128)(2,1)} %pad_maximum_fusion), channel_id=1, source_target_pairs={{0,1},{1,0},{2,3},{3,2},{4,5},{5,4},{6,7},{7,6},{8,9},{9,8},{10,11... | collective-permute-start | bytes 9437192 | tf_op jit(solution)/shard_map/ffn_forward/ppermute | solution.py:41
  186.9 11.6 %collective-permute-start.27 = (bf16[128,1536]{1,0:T(8,128)(2,1)S(1)}, bf16[128,1536]{1,0:T(8,128)(2,1)S(1)}, u32[]{:S(2)}, u32[]{:S(2)}) collective-permute-start(bf16[128,1536]{1,0:T(8,128)(2,1)S(1)} %get-tuple-element.364), channel_id=1, source_target_pairs={{0,2},{1,3},{2,0},{3,1},{4,6},{5,7},{6,4},{7,5},{8,10},{9,11},{10,... | collective-permute-start | bytes 1179656 | tf_op jit(solution)/shard_map/ffn_forward/ppermute | solution.py:41
  188.7 11.2 %collective-permute-start.28 = (bf16[128,1536]{1,0:T(8,128)(2,1)S(1)}, bf16[128,1536]{1,0:T(8,128)(2,1)S(1)}, u32[]{:S(2)}, u32[]{:S(2)}) collective-permute-start(bf16[128,1536]{1,0:T(8,128)(2,1)S(1)} %get-tuple-element.363), channel_id=1, source_target_pairs={{0,4},{1,5},{2,6},{3,7},{4,0},{5,1},{6,2},{7,3},{8,12},{9,13},{10,... | collective-permute-start | bytes 1179656 | tf_op jit(solution)/shard_map/ffn_forward/ppermute | solution.py:41
  191.1 12.9 %collective-permute-start.31 = (bf16[128,1536]{1,0:T(8,128)(2,1)S(1)}, bf16[128,1536]{1,0:T(8,128)(2,1)S(1)}, u32[]{:S(2)}, u32[]{:S(2)}) collective-permute-start(bf16[128,1536]{1,0:T(8,128)(2,1)S(1)} %copy-done.64), channel_id=1, source_target_pairs={{8,0},{9,1},{10,2},{11,3},{12,4},{13,5},{14,6},{15,7},{16,24},{17,... | collective-permute-start | bytes 1179656 | tf_op jit(solution)/shard_map/ffn_forward/ppermute | solution.py:92
  204.1 33.2 %collective-permute-start.34 = (bf16[256,1536]{1,0:T(8,128)(2,1)S(1)}, bf16[256,1536]{1,0:T(8,128)(2,1)S(1)}, u32[]{:S(2)}, u32[]{:S(2)}) collective-permute-start(bf16[256,1536]{1,0:T(8,128)(2,1)S(1)} %pad_maximum_fusion.15), channel_id=1, source_target_pairs={{0,4},{1,5},{2,6},{3,7},{4,0},{5,1},{6,2},{7,3},{8,12},{9,13},{10,... | collective-permute-start | bytes 2359304 | tf_op jit(solution)/shard_map/ffn_forward/ppermute | solution.py:41
  205.1 32.2 %collective-permute-start.35 = (bf16[256,1536]{1,0:T(8,128)(2,1)S(1)}, bf16[256,1536]{1,0:T(8,128)(2,1)S(1)}, u32[]{:S(2)}, u32[]{:S(2)}) collective-permute-start(bf16[256,1536]{1,0:T(8,128)(2,1)S(1)} %pad_maximum_fusion.16), channel_id=1, source_target_pairs={{0,2},{1,3},{2,0},{3,1},{4,6},{5,7},{6,4},{7,5},{8,10},{9,11},{10,... | collective-permute-start | bytes 2359304 | tf_op jit(solution)/shard_map/ffn_forward/ppermute | solution.py:41
  218.1 11.6 %collective-permute-start.32 = (bf16[128,1536]{1,0:T(8,128)(2,1)S(1)}, bf16[128,1536]{1,0:T(8,128)(2,1)S(1)}, u32[]{:S(2)}, u32[]{:S(2)}) collective-permute-start(bf16[128,1536]{1,0:T(8,128)(2,1)S(1)} %collective-permute-done.30), channel_id=1, source_target_pairs={{8,0},{9,1},{10,2},{11,3},{12,4},{13,5},{14,6},{15,7},{16,24},{17,... | collective-permute-start | bytes 1179656 | tf_op jit(solution)/shard_map/ffn_forward/ppermute | solution.py:92
  231.1 11.9 %collective-permute-start.33 = (bf16[4,128,1536]{2,1,0:T(8,128)(2,1)S(1)}, bf16[4,128,1536]{2,1,0:T(8,128)(2,1)S(1)}, u32[]{:S(2)}, u32[]{:S(2)}) collective-permute-start(bf16[4,128,1536]{2,1,0:T(8,128)(2,1)S(1)} %pad_maximum_fusion.5), channel_id=1, source_target_pairs={{0,1},{1,0},{2,3},{3,2},{4,5},{5,4},{6,7},{7,6},{8,9},{9,8},{10,11... | collective-permute-start | bytes 4718600 | tf_op jit(solution)/shard_map/ffn_forward/ppermute | solution.py:41
  247.0 20.0 %collective-permute-start.36 = (bf16[256,1536]{1,0:T(8,128)(2,1)S(1)}, bf16[256,1536]{1,0:T(8,128)(2,1)S(1)}, u32[]{:S(2)}, u32[]{:S(2)}) collective-permute-start(bf16[256,1536]{1,0:T(8,128)(2,1)S(1)} %get-tuple-element.331), channel_id=1, source_target_pairs={{0,4},{1,5},{2,6},{3,7},{4,0},{5,1},{6,2},{7,3},{8,12},{9,13},{10,... | collective-permute-start | bytes 2359304 | tf_op jit(solution)/shard_map/ffn_forward/ppermute | solution.py:41
  248.1 19.7 %collective-permute-start.37 = (bf16[256,1536]{1,0:T(8,128)(2,1)S(1)}, bf16[256,1536]{1,0:T(8,128)(2,1)S(1)}, u32[]{:S(2)}, u32[]{:S(2)}) collective-permute-start(bf16[256,1536]{1,0:T(8,128)(2,1)S(1)} %get-tuple-element.330), channel_id=1, source_target_pairs={{0,2},{1,3},{2,0},{3,1},{4,6},{5,7},{6,4},{7,5},{8,10},{9,11},{10,... | collective-permute-start | bytes 2359304 | tf_op jit(solution)/shard_map/ffn_forward/ppermute | solution.py:41
  288.5 10.7 %collective-permute-start.40 = (bf16[128,1536]{1,0:T(8,128)(2,1)S(1)}, bf16[128,1536]{1,0:T(8,128)(2,1)S(1)}, u32[]{:S(2)}, u32[]{:S(2)}) collective-permute-start(bf16[128,1536]{1,0:T(8,128)(2,1)S(1)} %get-tuple-element.362), channel_id=1, source_target_pairs={{0,2},{1,3},{2,0},{3,1},{4,6},{5,7},{6,4},{7,5},{8,10},{9,11},{10,... | collective-permute-start | bytes 1179656 | tf_op jit(solution)/shard_map/ffn_backward/ppermute | solution.py:41
  299.4 20.0 %collective-permute-start.43 = (bf16[256,1536]{1,0:T(8,128)(2,1)S(1)}, bf16[256,1536]{1,0:T(8,128)(2,1)S(1)}, u32[]{:S(2)}, u32[]{:S(2)}) collective-permute-start(bf16[256,1536]{1,0:T(8,128)(2,1)S(1)} %pad_maximum_fusion.17), channel_id=1, source_target_pairs={{0,4},{1,5},{2,6},{3,7},{4,0},{5,1},{6,2},{7,3},{8,12},{9,13},{10,... | collective-permute-start | bytes 2359304 | tf_op jit(solution)/shard_map/ffn_backward/ppermute | solution.py:41
  300.5 19.7 %collective-permute-start.44 = (bf16[256,1536]{1,0:T(8,128)(2,1)S(1)}, bf16[256,1536]{1,0:T(8,128)(2,1)S(1)}, u32[]{:S(2)}, u32[]{:S(2)}) collective-permute-start(bf16[256,1536]{1,0:T(8,128)(2,1)S(1)} %pad_maximum_fusion.18), channel_id=1, source_target_pairs={{0,2},{1,3},{2,0},{3,1},{4,6},{5,7},{6,4},{7,5},{8,10},{9,11},{10,... | collective-permute-start | bytes 2359304 | tf_op jit(solution)/shard_map/ffn_backward/ppermute | solution.py:41
  304.5 25.3 %collective-permute-start.45 = (f32[2,128]{1,0:T(2,128)S(1)}, f32[2,128]{1,0:T(2,128)S(1)}, u32[]{:S(2)}, u32[]{:S(2)}) collective-permute-start(f32[2,128]{1,0:T(2,128)S(1)} %add.511), channel_id=1, source_target_pairs={{0,8},{1,9},{2,10},{3,11},{4,12},{5,13},{6,14},{7,15},{8,0},{9,1},... | collective-permute-start | bytes 3080 | tf_op jit(solution)/shard_map/ffn_backward/ppermute | solution.py:41
  331.1 20.9 %collective-permute-start.48 = (bf16[4,128,1536]{2,1,0:T(8,128)(2,1)S(1)}, bf16[4,128,1536]{2,1,0:T(8,128)(2,1)S(1)}, u32[]{:S(2)}, u32[]{:S(2)}) collective-permute-start(bf16[4,128,1536]{2,1,0:T(8,128)(2,1)S(1)} %fusion.53), channel_id=1, source_target_pairs={{0,1},{1,0},{2,3},{3,2},{4,5},{5,4},{6,7},{7,6},{8,9},{9,8},{10,11... | collective-permute-start | bytes 4718600 | tf_op jit(solution)/shard_map/ffn_backward/ppermute | solution.py:41
  331.3 20.0 %collective-permute-start.46 = (bf16[256,1536]{1,0:T(8,128)(2,1)S(1)}, bf16[256,1536]{1,0:T(8,128)(2,1)S(1)}, u32[]{:S(2)}, u32[]{:S(2)}) collective-permute-start(bf16[256,1536]{1,0:T(8,128)(2,1)S(1)} %get-tuple-element.329), channel_id=1, source_target_pairs={{0,4},{1,5},{2,6},{3,7},{4,0},{5,1},{6,2},{7,3},{8,12},{9,13},{10,... | collective-permute-start | bytes 2359304 | tf_op jit(solution)/shard_map/ffn_backward/ppermute | solution.py:41
  332.3 19.7 %collective-permute-start.47 = (bf16[256,1536]{1,0:T(8,128)(2,1)S(1)}, bf16[256,1536]{1,0:T(8,128)(2,1)S(1)}, u32[]{:S(2)}, u32[]{:S(2)}) collective-permute-start(bf16[256,1536]{1,0:T(8,128)(2,1)S(1)} %get-tuple-element.328), channel_id=1, source_target_pairs={{0,2},{1,3},{2,0},{3,1},{4,6},{5,7},{6,4},{7,5},{8,10},{9,11},{10,... | collective-permute-start | bytes 2359304 | tf_op jit(solution)/shard_map/ffn_backward/ppermute | solution.py:41
  352.0 35.6 %collective-permute-start.52 = (bf16[768,2048]{1,0:T(8,128)(2,1)S(1)}, bf16[768,2048]{1,0:T(8,128)(2,1)S(1)}, u32[]{:S(2)}, u32[]{:S(2)}) collective-permute-start(bf16[768,2048]{1,0:T(8,128)(2,1)S(1)} %convolution_convert_fusion.2), channel_id=1, source_target_pairs={{0,1},{1,0},{2,3},{3,2},{4,5},{5,4},{6,7},{7,6},{8,9},{9,8},{10,11... | collective-permute-start | bytes 9437192 | tf_op jit(solution)/shard_map/ffn_backward/ppermute | solution.py:41
  373.9 10.9 %collective-permute-start.53 = (f32[2,128]{1,0:T(2,128)S(1)}, f32[2,128]{1,0:T(2,128)S(1)}, u32[]{:S(2)}, u32[]{:S(2)}) collective-permute-start(f32[2,128]{1,0:T(2,128)S(1)} %add.520), channel_id=1, source_target_pairs={{0,2},{1,3},{2,0},{3,1},{4,6},{5,7},{6,4},{7,5},{8,10},{9,11},{10,... | collective-permute-start | bytes 3080 | tf_op jit(solution)/shard_map/ffn_backward/ppermute | solution.py:41
  376.0 11.3 %collective-permute-start.50 = (bf16[128,1536]{1,0:T(8,128)(2,1)S(1)}, bf16[128,1536]{1,0:T(8,128)(2,1)S(1)}, u32[]{:S(2)}, u32[]{:S(2)}) collective-permute-start(bf16[128,1536]{1,0:T(8,128)(2,1)S(1)} %slice.676), channel_id=1, source_target_pairs={{0,2},{1,3},{2,0},{3,1},{4,6},{5,7},{6,4},{7,5},{8,10},{9,11},{10,... | collective-permute-start | bytes 1179656 | tf_op jit(solution)/shard_map/ffn_backward/ppermute | solution.py:41
  376.5 11.1 %collective-permute-start.51 = (bf16[128,1536]{1,0:T(8,128)(2,1)S(1)}, bf16[128,1536]{1,0:T(8,128)(2,1)S(1)}, u32[]{:S(2)}, u32[]{:S(2)}) collective-permute-start(bf16[128,1536]{1,0:T(8,128)(2,1)S(1)} %slice.675), channel_id=1, source_target_pairs={{0,4},{1,5},{2,6},{3,7},{4,0},{5,1},{6,2},{7,3},{8,12},{9,13},{10,... | collective-permute-start | bytes 1179656 | tf_op jit(solution)/shard_map/ffn_backward/ppermute | solution.py:41
  379.3 38.8 %collective-permute-start.56 = (bf16[2,128,1536]{2,1,0:T(8,128)(2,1)}, bf16[2,128,1536]{2,1,0:T(8,128)(2,1)}, u32[]{:S(2)}, u32[]{:S(2)}) collective-permute-start(bf16[2,128,1536]{2,1,0:T(8,128)(2,1)} %pad_maximum_fusion.19), channel_id=1, source_target_pairs={{0,8},{1,9},{2,10},{3,11},{4,12},{5,13},{6,14},{7,15},{24,16},{25,... | collective-permute-start | bytes 2359304 | tf_op jit(solution)/shard_map/ffn_backward/ppermute | solution.py:92
  392.1 23.6 %collective-permute-start.54 = (bf16[768,1536]{1,0:T(8,128)(2,1)}, bf16[768,1536]{1,0:T(8,128)(2,1)}, u32[]{:S(2)}, u32[]{:S(2)}) collective-permute-start(bf16[768,1536]{1,0:T(8,128)(2,1)} %convolution_convert_fusion.1), channel_id=1, source_target_pairs={{0,1},{1,0},{2,3},{3,2},{4,5},{5,4},{6,7},{7,6},{8,9},{9,8},{10,11... | collective-permute-start | bytes 7077896 | tf_op jit(solution)/shard_map/attention_backward/ppermute | solution.py:41
  392.1 23.6 %collective-permute-start.55 = (f32[2,128]{1,0:T(2,128)S(1)}, f32[2,128]{1,0:T(2,128)S(1)}, u32[]{:S(2)}, u32[]{:S(2)}) collective-permute-start(f32[2,128]{1,0:T(2,128)S(1)} %add.522), channel_id=1, source_target_pairs={{0,4},{1,5},{2,6},{3,7},{4,0},{5,1},{6,2},{7,3},{8,12},{9,13},{10,... | collective-permute-start | bytes 3080 | tf_op jit(solution)/shard_map/attention_backward/ppermute | solution.py:41
  421.0 13.1 %collective-permute-start.59 = (bf16[128,1536]{1,0:T(8,128)(2,1)S(1)}, bf16[128,1536]{1,0:T(8,128)(2,1)S(1)}, u32[]{:S(2)}, u32[]{:S(2)}) collective-permute-start(bf16[128,1536]{1,0:T(8,128)(2,1)S(1)} %get-tuple-element.312), channel_id=1, source_target_pairs={{0,8},{1,9},{2,10},{3,11},{4,12},{5,13},{6,14},{7,15},{8,16},{9,17... | collective-permute-start | bytes 1179656 | tf_op jit(solution)/shard_map/attention_backward/ppermute | solution.py:92
  425.4 21.2 %collective-permute-start.60 = (bf16[128,1536]{1,0:T(8,128)(2,1)S(1)}, bf16[128,1536]{1,0:T(8,128)(2,1)S(1)}, u32[]{:S(2)}, u32[]{:S(2)}) collective-permute-start(bf16[128,1536]{1,0:T(8,128)(2,1)S(1)} %get-tuple-element.311), channel_id=1, source_target_pairs={{8,0},{9,1},{10,2},{11,3},{12,4},{13,5},{14,6},{15,7},{16,8},{17,9... | collective-permute-start | bytes 1179656 | tf_op jit(solution)/shard_map/attention_backward/ppermute | solution.py:92
  426.7 19.9 %collective-permute-start.61 = (bf16[128,1536]{1,0:T(8,128)(2,1)S(1)}, bf16[128,1536]{1,0:T(8,128)(2,1)S(1)}, u32[]{:S(2)}, u32[]{:S(2)}) collective-permute-start(bf16[128,1536]{1,0:T(8,128)(2,1)S(1)} %get-tuple-element.310), channel_id=1, source_target_pairs={{16,0},{17,1},{18,2},{19,3},{20,4},{21,5},{22,6},{23,7},{8,24},{9,... | collective-permute-start | bytes 1179656 | tf_op jit(solution)/shard_map/attention_backward/ppermute | solution.py:92
  428.5 18.2 %collective-permute-start.58 = (bf16[2,2,48,1536]{3,2,0,1:T(8,128)(2,1)S(1)}, bf16[2,2,48,1536]{3,2,0,1:T(8,128)(2,1)S(1)}, u32[]{:S(2)}, u32[]{:S(2)}) collective-permute-start(bf16[2,2,48,1536]{3,2,0,1:T(8,128)(2,1)S(1)} %fusion.112), channel_id=1, source_target_pairs={{0,2},{1,3},{2,0},{3,1},{4,6},{5,7},{6,4},{7,5},{8,10},{9,11},{10,... | collective-permute-start | bytes 1769480 | tf_op jit(solution)/shard_map/attention_backward/ppermute | solution.py:41
  430.4 16.3 %collective-permute-start.57 = (bf16[2,2,48,1536]{3,2,0,1:T(8,128)(2,1)S(1)}, bf16[2,2,48,1536]{3,2,0,1:T(8,128)(2,1)S(1)}, u32[]{:S(2)}, u32[]{:S(2)}) collective-permute-start(bf16[2,2,48,1536]{3,2,0,1:T(8,128)(2,1)S(1)} %fusion.111), channel_id=1, source_target_pairs={{0,4},{1,5},{2,6},{3,7},{4,0},{5,1},{6,2},{7,3},{8,12},{9,13},{10,... | collective-permute-start | bytes 1769480 | tf_op jit(solution)/shard_map/attention_backward/ppermute | solution.py:41
  460.5 19.7 %collective-permute-start.64 = (bf16[768,3072]{1,0:T(8,128)(2,1)}, bf16[768,3072]{1,0:T(8,128)(2,1)}, u32[]{:S(2)}, u32[]{:S(2)}) collective-permute-start(bf16[768,3072]{1,0:T(8,128)(2,1)} %convolution_convert_fusion), channel_id=1, source_target_pairs={{0,1},{1,0},{2,3},{3,2},{4,5},{5,4},{6,7},{7,6},{8,9},{9,8},{10,11... | collective-permute-start | bytes 14155784 | tf_op jit(solution)/shard_map/input_gradient/ppermute | solution.py:41
  466.5 61.5 %collective-permute-start.68 = (bf16[2,4,48,2048]{3,2,1,0:T(8,128)(2,1)}, bf16[2,4,48,2048]{3,2,1,0:T(8,128)(2,1)}, u32[]{:S(2)}, u32[]{:S(2)}) collective-permute-start(bf16[2,4,48,2048]{3,2,1,0:T(8,128)(2,1)} %pad_maximum_fusion.8), channel_id=1, source_target_pairs={{0,8},{1,9},{2,10},{3,11},{4,12},{5,13},{6,14},{7,15},{24,16},{25,... | collective-permute-start | bytes 4718600 | tf_op jit(solution)/shard_map/attention_backward/ppermute | solution.py:92
  496.2 28.2 %collective-permute-start.66 = (bf16[2,2,48,3072]{3,2,0,1:T(8,128)(2,1)}, bf16[2,2,48,3072]{3,2,0,1:T(8,128)(2,1)S(1)}, u32[]{:S(2)}, u32[]{:S(2)}) collective-permute-start(bf16[2,2,48,3072]{3,2,0,1:T(8,128)(2,1)} %fusion.93), channel_id=1, source_target_pairs={{0,2},{1,3},{2,0},{3,1},{4,6},{5,7},{6,4},{7,5},{8,10},{9,11},{10,... | collective-permute-start | bytes 3538952 | tf_op jit(solution)/shard_map/weight_gradients_to_owners/ppermute | solution.py:41
  499.8 28.1 %collective-permute-start.65 = (bf16[2,2,48,3072]{3,2,0,1:T(8,128)(2,1)S(1)}, bf16[2,2,48,3072]{3,2,0,1:T(8,128)(2,1)S(1)}, u32[]{:S(2)}, u32[]{:S(2)}) collective-permute-start(bf16[2,2,48,3072]{3,2,0,1:T(8,128)(2,1)S(1)} %fusion.92), channel_id=1, source_target_pairs={{0,4},{1,5},{2,6},{3,7},{4,0},{5,1},{6,2},{7,3},{8,12},{9,13},{10,... | collective-permute-start | bytes 3538952 | tf_op jit(solution)/shard_map/weight_gradients_to_owners/ppermute | solution.py:41
  530.7 20.2 %collective-permute-start.71 = (bf16[4,48,2048]{2,1,0:T(8,128)(2,1)S(1)}, bf16[4,48,2048]{2,1,0:T(8,128)(2,1)S(1)}, u32[]{:S(2)}, u32[]{:S(2)}) collective-permute-start(bf16[4,48,2048]{2,1,0:T(8,128)(2,1)S(1)} %get-tuple-element.300), channel_id=1, source_target_pairs={{0,8},{1,9},{2,10},{3,11},{4,12},{5,13},{6,14},{7,15},{8,16},{9,17... | collective-permute-start | bytes 2359304 | tf_op jit(solution)/shard_map/weight_gradients_to_owners/ppermute | solution.py:92
  532.0 22.0 %collective-permute-start.72 = (bf16[4,48,2048]{2,1,0:T(8,128)(2,1)S(1)}, bf16[4,48,2048]{2,1,0:T(8,128)(2,1)S(1)}, u32[]{:S(2)}, u32[]{:S(2)}) collective-permute-start(bf16[4,48,2048]{2,1,0:T(8,128)(2,1)S(1)} %get-tuple-element.299), channel_id=1, source_target_pairs={{8,0},{9,1},{10,2},{11,3},{12,4},{13,5},{14,6},{15,7},{16,8},{17,9... | collective-permute-start | bytes 2359304 | tf_op jit(solution)/shard_map/weight_gradients_to_owners/ppermute | solution.py:92
  533.3 36.9 %collective-permute-start.73 = (bf16[4,48,2048]{2,1,0:T(8,128)(2,1)S(1)}, bf16[4,48,2048]{2,1,0:T(8,128)(2,1)S(1)}, u32[]{:S(2)}, u32[]{:S(2)}) collective-permute-start(bf16[4,48,2048]{2,1,0:T(8,128)(2,1)S(1)} %get-tuple-element.298), channel_id=1, source_target_pairs={{16,0},{17,1},{18,2},{19,3},{20,4},{21,5},{22,6},{23,7},{8,24},{9,... | collective-permute-start | bytes 2359304 | tf_op jit(solution)/shard_map/weight_gradients_to_owners/ppermute | solution.py:92
  535.1 14.6 %collective-permute-start.70 = (bf16[2,48,3072]{2,1,0:T(8,128)(2,1)S(1)}, bf16[2,48,3072]{2,1,0:T(8,128)(2,1)S(1)}, u32[]{:S(2)}, u32[]{:S(2)}) collective-permute-start(bf16[2,48,3072]{2,1,0:T(8,128)(2,1)S(1)} %fusion.114), channel_id=1, source_target_pairs={{0,4},{1,5},{2,6},{3,7},{4,0},{5,1},{6,2},{7,3},{8,12},{9,13},{10,... | collective-permute-start | bytes 1769480 | tf_op jit(solution)/shard_map/weight_gradients_to_owners/ppermute | solution.py:41
  536.5 14.3 %collective-permute-start.69 = (bf16[2,48,3072]{2,1,0:T(8,128)(2,1)S(1)}, bf16[2,48,3072]{2,1,0:T(8,128)(2,1)S(1)}, u32[]{:S(2)}, u32[]{:S(2)}) collective-permute-start(bf16[2,48,3072]{2,1,0:T(8,128)(2,1)S(1)} %fusion.113), channel_id=1, source_target_pairs={{0,2},{1,3},{2,0},{3,1},{4,6},{5,7},{6,4},{7,5},{8,10},{9,11},{10,... | collective-permute-start | bytes 1769480 | tf_op jit(solution)/shard_map/weight_gradients_to_owners/ppermute | solution.py:41
  576.6 17.6 %collective-permute-start.74 = (bf16[2,48,4608]{2,1,0:T(8,128)(2,1)S(1)}, bf16[2,48,4608]{2,1,0:T(8,128)(2,1)S(1)}, u32[]{:S(2)}, u32[]{:S(2)}) collective-permute-start(bf16[2,48,4608]{2,1,0:T(8,128)(2,1)S(1)} %pad_maximum_fusion.13), channel_id=1, source_target_pairs={{0,8},{1,9},{2,10},{3,11},{4,12},{5,13},{6,14},{7,15},{24,16},{25,... | collective-permute-start | bytes 2654216 | tf_op jit(solution)/shard_map/weight_gradients_to_owners/ppermute | solution.py:92
  594.8 24.3 %collective-permute-start.80 = (bf16[48,4608]{1,0:T(8,128)(2,1)S(1)}, bf16[48,4608]{1,0:T(8,128)(2,1)S(1)}, u32[]{:S(2)}, u32[]{:S(2)}) collective-permute-start(bf16[48,4608]{1,0:T(8,128)(2,1)S(1)} %get-tuple-element.309), channel_id=1, source_target_pairs={{0,8},{1,9},{2,10},{3,11},{4,12},{5,13},{6,14},{7,15},{8,16},{9,17... | collective-permute-start | bytes 1327112 | tf_op jit(solution)/shard_map/weight_gradients_to_owners/ppermute | solution.py:92
  599.2 19.9 %collective-permute-start.81 = (bf16[48,4608]{1,0:T(8,128)(2,1)S(1)}, bf16[48,4608]{1,0:T(8,128)(2,1)S(1)}, u32[]{:S(2)}, u32[]{:S(2)}) collective-permute-start(bf16[48,4608]{1,0:T(8,128)(2,1)S(1)} %get-tuple-element.308), channel_id=1, source_target_pairs={{8,0},{9,1},{10,2},{11,3},{12,4},{13,5},{14,6},{15,7},{16,8},{17,9... | collective-permute-start | bytes 1327112 | tf_op jit(solution)/shard_map/weight_gradients_to_owners/ppermute | solution.py:92
  600.5 18.6 %collective-permute-start.82 = (bf16[48,4608]{1,0:T(8,128)(2,1)S(1)}, bf16[48,4608]{1,0:T(8,128)(2,1)S(1)}, u32[]{:S(2)}, u32[]{:S(2)}) collective-permute-start(bf16[48,4608]{1,0:T(8,128)(2,1)S(1)} %get-tuple-element.307), channel_id=1, source_target_pairs={{16,0},{17,1},{18,2},{19,3},{20,4},{21,5},{22,6},{23,7},{8,24},{9,... | collective-permute-start | bytes 1327112 | tf_op jit(solution)/shard_map/weight_gradients_to_owners/ppermute | solution.py:92
  601.8 17.3 %collective-permute-start.83 = (f32[2,1536]{1,0:T(2,128)S(1)}, f32[2,1536]{1,0:T(2,128)S(1)}, u32[]{:S(2)}, u32[]{:S(2)}) collective-permute-start(f32[2,1536]{1,0:T(2,128)S(1)} %add.560), channel_id=1, source_target_pairs={{0,8},{1,9},{2,10},{3,11},{4,12},{5,13},{6,14},{7,15},{8,0},{9,1},... | collective-permute-start | bytes 36872 | tf_op jit(solution)/shard_map/weight_gradients_to_owners/ppermute | solution.py:41
  (133 other events, 1029.5 us)

commit v5 on v4

--- a/solution.py
+++ b/solution.py
@@ -49,43 +49,54 @@
     return [[8 * z + 2 * p + c for z in planes] for p in range(4) for c in range(2)]
 
 
-def z_reduce(parts, z):
-    if parts.shape[0] != 4:
-        return lax.psum_scatter(
-            parts.astype(BF), "dp", axis_index_groups=column_groups(False), scatter_dimension=0
-        ).astype(F32)
-    came = [swap(pick(parts, z ^ k, 0).astype(BF), 8 * k) for k in (3, 2, 1)]
-    own = pick(parts, z, 0)
+def z_reduce(parts):
+    total = sum(part.astype(F32) for part in parts)
+    return lax.psum_scatter(
+        total.astype(BF), "dp", axis_index_groups=column_groups(False), scatter_dimension=0
+    ).astype(F32)
+
+
+def summed(parts, index, axis):
+    total = pick(parts[0], index, axis).astype(F32)
+    for part in parts[1:]:
+        total = total + pick(part, index, axis).astype(F32)
+    return total
+
+
+def walk_1(parts, z):
+    return along_z(summed(parts, 3 - z, 0).astype(BF), [(0, 1), (3, 2)])
+
+
+def walk_2(parts, came, z):
+    across = summed(parts, jnp.where(z == 0, 2, 1), 0)
+    far = summed(parts, jnp.where(z == 1, 3, 0), 0) + came.astype(F32)
+    return (
+        along_z(across.astype(BF), [(0, 1), (3, 2)]),
+        along_z(far.astype(BF), [(1, 3), (2, 0)]),
+    )
+
+
+def walk_3(parts, came, z):
+    up = summed(parts, jnp.minimum(z + 1, 3), 0)
+    down = summed(parts, jnp.maximum(z - 1, 0), 0)
+    came = came.astype(F32)
+    up = jnp.where(z == 1, up + came, up)
+    down = jnp.where(z == 2, down + came, down)
+    return (
+        along_z(up.astype(BF), [(0, 1), (1, 2), (2, 3)]),
+        along_z(down.astype(BF), [(1, 0), (2, 1), (3, 2)]),
+    )
+
+
+def owned(parts, came, z):
+    own = summed(parts, z, 0)
     for piece in came:
         own = own + piece.astype(F32)
     return own
 
 
-def walk_start(parts, z):
-    payload = jnp.stack(
-        [pick(parts, jnp.where(z == 0, 2, 1), 0), pick(parts, jnp.where(z == 0, 3, 0), 0)]
-    )
-    return along_z(payload.astype(BF), [(0, 1), (3, 2)])
-
-
-def walk_end(parts, came, z):
-    came = came.astype(F32)
-    across = pick(parts, 3 - z, 0) + came[0]
-    far = pick(parts, jnp.where(z == 1, 3, 0), 0) + came[1]
-    up = jnp.where(z == 1, across, pick(parts, jnp.minimum(z + 1, 3), 0))
-    down = jnp.where(z == 2, across, pick(parts, jnp.maximum(z - 1, 0), 0))
-    return (
-        along_z(up.astype(BF), [(0, 1), (1, 2), (2, 3)]),
-        along_z(down.astype(BF), [(1, 0), (2, 1), (3, 2)]),
-        along_z(far.astype(BF), [(2, 0), (1, 3)]),
-    )
-
-
-def owned(parts, came, z):
-    own = pick(parts, z, 0)
-    for piece in came:
-        own = own + piece.astype(F32)
-    return own
+def direct(parts, z):
+    return [swap(summed(parts, z ^ k, 0).astype(BF), 8 * k) for k in (3, 2, 1)]
 
 
 def along_z(value, pairs):
@@ -199,6 +210,38 @@
         + [pl.BlockSpec(memory_space=pltpu.VMEM)] * 2,
         name="column_cuts",
     )(p[None], w_gate, w_up)
+
+
+def assembled(pieces, places):
+    blocks, rows, columns = pieces[0].shape
+    count = len(pieces)
+
+    def kernel(at, *refs):
+        out, sems = refs[count], refs[count + 1]
+        copies = []
+        for i in range(count):
+            for j in range(blocks):
+                start = pl.multiple_of(at[i, j], 16)
+                copy = pltpu.make_async_copy(
+                    refs[i].at[j], out.at[pl.ds(start, rows)], sems.at[i, j]
+                )
+                copy.start()
+                copies.append(copy)
+        for copy in copies:
+            copy.wait()
+
+    size = count * blocks * rows * columns * 2
+    return pl.pallas_call(
+        kernel,
+        out_shape=jax.ShapeDtypeStruct((count * blocks * rows, columns), pieces[0].dtype),
+        in_specs=[pl.BlockSpec(memory_space=pltpu.SMEM)]
+        + [pl.BlockSpec(memory_space=pl.ANY)] * count,
+        out_specs=pl.BlockSpec(memory_space=pltpu.VMEM),
+        scratch_shapes=[pltpu.SemaphoreType.DMA((count, blocks))],
+        compiler_params=pltpu.CompilerParams(vmem_limit_bytes=16 * 2**20),
+        cost_estimate=pl.CostEstimate(flops=0, bytes_accessed=2 * size, transcendentals=0),
+        name="assembled",
+    )(places, *pieces)
 
 
 def gather_weights(local, w_gate, w_up, w_down, place_bits):
@@ -280,7 +323,10 @@
         near_2 = jnp.stack([a2, b2])
         out = put(out, near_2, z_c, z_d, y, x, c)
     with jax.named_scope("phase_5"):
-        near_2, far_2 = tied(near_2, jnp.stack([a_far, b_far]))
+        near_2, far_2, g_far, g_first = tied(
+            near_2, jnp.stack([a_far, b_far]), g_far, g_first
+        )
+        g_second = along_z(g_far, out_pairs)
         core_3, core_4 = tied(swap(near_2, 1), swap(far_2, 1))
         out = put(out, core_2, z, z_b, 1 - y, 1 - x, 1 - c)
         out = put(out, far_2, z_c, z_d, 1 - y, 1 - x, c)
@@ -290,27 +336,32 @@
 
 
     def step_1(beside):
-        g_in, f_in, d_in, beside = tied(g_far, g_first, w_down, beside)
-        g_second = along_z(g_in, out_pairs)
-        return beside, (g_in, f_in, g_second, along_z(d_in, up_pairs), along_z(d_in, down_pairs))
+        last, d_in, beside = tied(g_second, w_down, beside)
+        return beside, (last, along_z(d_in, up_pairs), along_z(d_in, down_pairs))
 
     def step_2(state, beside):
-        g_in, f_in, g_second, d_up, d_down = state
-        pieces = jnp.stack(
-            [gu, near_side(g_up, g_down), jnp.where(end, f_in, g_down), jnp.where(end, g_second, g_in)]
-        )
-        pieces, d_in, d_pass, d_up, d_down, beside = tied(
-            pieces, w_down, to_pass_on(d_up, d_down), d_up, d_down, beside
-        )
-        moving = (swap(pieces, 1), along_z(d_in, far_pairs), along_z(d_pass, out_pairs))
-
-        def step_3(others, d_far, d_first):
-            d_second = along_z(d_far, out_pairs)
-            wb = unset((4, 4, 2) + gu.shape[1:], BF)
-            places = (z, z_b, z_c, z_d)
-            for k in range(4):
-                wb = place(wb, pieces[k][None, :, None], (places[k], 0, c, 0, 0))
-                wb = place(wb, others[k][None, :, None], (places[k], 0, 1 - c, 0, 0))
+        last, d_up, d_down, beside = tied(*state, beside)
+        pieces = tied(
+            gu,
+            near_side(g_up, g_down),
+            jnp.where(end, g_first, g_down),
+            jnp.where(end, last, g_far),
+        )
+        d_in, d_pass = tied(w_down, to_pass_on(d_up, d_down))
+        moving = (along_z(d_in, far_pairs), along_z(d_pass, out_pairs))
+        return beside, (pieces, d_up, d_down, swap(jnp.stack(pieces), 1), *moving)
+
+    def step_3(state, beside):
+        pieces, d_up, d_down, *state = state
+        others, d_far, d_first, beside = tied(*state, beside)
+        moving = (along_z(d_far, out_pairs),)
+        along = jnp.stack([z, z_b, z_c, z_d])
+
+        def step_4(d_second):
+            mine = 8 * along[:, None] + 2 * jnp.arange(4)[None, :] + c
+            theirs = 8 * along[:, None] + 2 * jnp.arange(4)[None, :] + 1 - c
+            places = jnp.concatenate([mine, theirs]) * rows
+            wb = assembled(list(pieces) + [others[k] for k in range(4)], places.astype(jnp.int32))
             d_all = jnp.stack(
                 [
                     w_down,
@@ -320,45 +371,52 @@
                 ]
             )
             d_others = swap(d_all, 1)
-            wd = unset((4, 2, ff_rows, width), BF)
-            for k in range(4):
-                wd = place(wd, d_all[k][None, None], (places[k], c, 0, 0))
-                wd = place(wd, d_others[k][None, None], (places[k], 1 - c, 0, 0))
-            return wb.reshape(32 * rows, -1), wd.reshape(8 * ff_rows, width)
-
-        return beside, moving, step_3
-
-    return gathered, step_1, step_2
+            places = jnp.stack([2 * along + c, 2 * along + 1 - c]) * ff_rows
+            wd = assembled([d_all, d_others], places.astype(jnp.int32))
+            return wb, wd
+
+        return beside, moving, step_4
+
+    return gathered, step_1, step_2, step_3
+
+
+def halves(parts):
+    half = parts[0].shape[2] // 2
+    return [part[:, :, :half] for part in parts], [part[:, :, half:] for part in parts]
 
 
 def plane_step_1(parts, place_bits):
     z, y, x, c = place_bits
-    half = parts.shape[0] // 2
-    a, b = parts[:half], parts[half:]
-    return (swap(pick(a, 1 - y, 1).astype(BF), 4), swap(pick(b, 1 - x, 2).astype(BF), 2))
+    a, b = halves(parts)
+    return (swap(summed(a, 1 - y, 1).astype(BF), 4), swap(summed(b, 1 - x, 0).astype(BF), 2))
 
 
 def plane_step_2(parts, came, place_bits):
     z, y, x, c = place_bits
-    half = parts.shape[0] // 2
-    a = pick(parts[:half], y, 1) + came[0].astype(F32)
-    b = pick(parts[half:], x, 2) + came[1].astype(F32)
-    moving = (swap(pick(a, 1 - x, 1).astype(BF), 2), swap(pick(b, 1 - y, 1).astype(BF), 4))
+    a, b = halves(parts)
+    a = [summed(a, y, 1), came[0]]
+    b = [summed(b, x, 0), came[1]]
+    moving = (swap(summed(a, 1 - x, 0).astype(BF), 2), swap(summed(b, 1 - y, 0).astype(BF), 4))
     return (a, b), moving
 
 
 def plane_step_3(sums, came, place_bits):
     z, y, x, c = place_bits
-    a = pick(sums[0], x, 1) + came[0].astype(F32)
-    b = pick(sums[1], y, 1) + came[1].astype(F32)
+    a = summed(sums[0], x, 0) + came[0].astype(F32)
+    b = summed(sums[1], y, 0) + came[1].astype(F32)
     return jnp.concatenate([a, b])
 
 
-def core_first(count, rows):
+def core_first(count, rows, chip_order):
     order = jnp.arange(count)
-    per_core = count // 2
-    core, rest = order // per_core, order % per_core
-    source = (rest // rows * 2 + core) * rows + rest % rows
+    row, place_of = order % rows, order // rows
+    chips = count // rows // 2
+    core, chip = place_of // chips, place_of % chips
+    if chip_order == "xyz":
+        planes = chips // 4
+        x, y, z = chip // (2 * planes), chip // planes % 2, chip % planes
+        chip = 4 * z + 2 * y + x
+    source = (2 * chip + core) * rows + row
     return (jnp.arange(count)[:, None] == source[None, :]).astype(BF)
 
 
@@ -519,7 +577,7 @@
     gains = jnp.pad(gains, ((0, 0), (0, LANES - 2)))
     local = packed([w_query, key_weight_matrix, value_weight_matrix, w_output, gains])
     if planes == 4:
-        gathered, step_1, step_2 = gather_weights(local, w_gate, w_up, w_down, bits)
+        gathered, step_1, step_2, step_3 = gather_weights(local, w_gate, w_up, w_down, bits)
     else:
         gathered, wb, wd = gather_weights_plainly(local, w_gate, w_up, w_down, p)
 
@@ -544,6 +602,8 @@
         key = turn(key, cosine_lookup, sine_lookup).astype(BF)
         value = raw[:, width + kv_width :].astype(BF).reshape(kv_heads)
         probs = probabilities(query, key)
+        if planes == 4:
+            probs, moving = step_2(moving, probs)
         probs_low = probs.astype(BF)
         mixed = jnp.einsum("bhrqk,bkhd->bqhrd", probs_low, value, preferred_element_type=F32)
         mixed = mixed.reshape(count, width).astype(BF)
@@ -553,14 +613,25 @@
 
     with jax.named_scope("ffn_forward"):
         if planes == 4:
-            normed_mid, moving, step_3 = step_2(moving, normed_mid)
+            normed_mid, moving, step_4 = step_3(moving, normed_mid)
             near, far, moving = split_gather(normed_mid, moving)
-            wb, wd = step_3(*moving)
+            wb, wd = step_4(*moving)
         else:
             near, far, moving = split_gather(normed_mid)
         y_near, pre_near, hid_near = ffn_forward(near, wb, wd)
         y_far, pre_far, hid_far = ffn_forward(far, wb, wd)
-        result = hidden_res + split_reduce(y_near, y_far)[0]
+        by_plane = core_first(width, rows, "zyx")
+        by_side = core_first(width, rows, "xyz")
+        beside = (
+            *core_halves(mm(near, by_plane).astype(BF), c),
+            *core_halves(mm(far, by_plane).astype(BF), c),
+            *core_halves(mm(mixed, by_side).astype(BF), c),
+            *core_halves(mm(normed_in, by_side).astype(BF), c),
+        )
+        result, *halves = split_reduce(y_near, y_far, beside)
+        near_mine, near_theirs, far_mine, far_theirs = halves[:4]
+        mixed_mine, mixed_theirs, normed_mine, normed_theirs = halves[4:]
+        result = hidden_res + result
         out_act = result.astype(BF)
 
     with jax.named_scope("loss"):
@@ -586,53 +657,38 @@
         m_far, g_far = ffn_backward(d_far, pre_far, wb, wd)
         m_near, m_far, sums, sums_came = tied(m_near, m_far, sums, sums_came)
         sums = sums + sums_came
-        by_core = core_first(width, rows)
-        hid = jnp.concatenate([hid_near, hid_far])
-        d_all = jnp.concatenate([d_near, d_far])
-        mid_all = mm(jnp.concatenate([near, far]), by_core).astype(BF)
-        g_all = jnp.concatenate([g_near, g_far])
-        mid_mine, mid_theirs = core_halves(mid_all, c)
-        g_down = t_mm(hid, d_all).reshape(planes, 2, ff_rows, width)
+        g_down = (t_mm(hid_near, d_near) + t_mm(hid_far, d_far)).reshape(planes, 2, ff_rows, width)
         beside = (
             swap(pick(g_down, 1 - c, 1).astype(BF), 1),
             pick(g_down, c, 1),
-            t_mm(mid_theirs, g_all).astype(BF),
+            (t_mm(near_theirs, g_near) + t_mm(far_theirs, g_far)).astype(BF),
             sums,
             swap(sums, high),
         )
 
         def later(came, own, theirs, sums, sums_came):
-            g_down = own + came.astype(F32)
             sums = sums + sums_came
-            started = (walk_start(g_down, z),) if planes == 4 else ()
-            return (swap(theirs, 1), sums, swap(sums, 2), g_down, started)
-
-        def later_flat(*values):
-            theirs_came, sums, sums_came, g_down, started = later(*values)
-            moving.extend(started)
-            return (theirs_came, sums, sums_came, g_down)
-
-        moving = []
-        grad_mid, both_came, sums, sums_came, g_down = split_reduce(
-            m_near, m_far, beside, later_flat
-        )
+            started = (walk_1((own, came), z),) if planes == 4 else ()
+            return (swap(theirs, 1), sums, swap(sums, 2), own, came, *started)
+
+        grad_mid, both_came, sums, sums_came, *down, = split_reduce(m_near, m_far, beside, later)
         sums = sums + sums_came
-        g_both = t_mm(mid_mine, g_all) + both_came.astype(F32)
-        g_both = g_both.reshape(planes, 4, rows, 2 * units)
+        down, moving = down[:2], down[2:]
+        g_both = (t_mm(near_mine, g_near) + t_mm(far_mine, g_far), both_came)
+        g_both = [part.reshape(planes, 4, rows, 2 * units) for part in g_both]
 
     with jax.named_scope("attention_backward"):
         grad_gain_mid, grad_res = norm_back(grad_mid, hidden_res, inv_ffn, gain_mid)
         grad_res = grad_out + grad_res
         res_low = grad_res.astype(BF)
-        mixed_mine, mixed_theirs = core_halves(mm(mixed, by_core).astype(BF), c)
+        if planes == 4:
+            res_low, moving = tied(res_low, *moving)
+            moving, down_far = walk_2(down, moving, z)
         wo_came, sums_came = tied(swap(t_mm(mixed_theirs, res_low).astype(BF), 1), swap(sums, 4))
         sums = sums + sums_came
         loss = sums[0, 0] / (sums[1, 0] * width)
-        shape = (planes, 2, 2, rows, -1)
-        g_wo = (t_mm(mixed_mine, res_low) + wo_came.astype(F32)).reshape(shape)
-        if planes == 4:
-            g_wo, down_came, g_down = tied(g_wo, moving[0], g_down)
-            down_moving = walk_end(g_down, down_came, z)
+        shape = (2, 2, planes, rows, -1)
+        g_wo = [t_mm(mixed_mine, res_low).reshape(shape), wo_came.reshape(shape)]
         wo_moving = plane_step_1(g_wo, bits)
         grad_mixed = mm_t(res_low, wo).astype(BF).reshape(grouped)
         grad_probs = jnp.einsum(
@@ -641,13 +697,14 @@
         grad_scores = probs * (grad_probs - jnp.sum(probs * grad_probs, axis=-1, keepdims=True))
         grad_scores = grad_scores.astype(BF)
         if planes == 4:
-            grad_scores, g_both, *came = tied(grad_scores, g_both, *wo_moving, *down_moving)
-            wo_came, down_came = came[:2], came[2:]
-            g_down = owned(g_down, down_came, z)
-            both_moving = walk_start(g_both, z)
+            wo_0, wo_1, moving, down_far, grad_scores = tied(
+                *wo_moving, moving, down_far, grad_scores
+            )
+            moving = walk_3(down, moving, z)
+            wo_came = (wo_0, wo_1)
         else:
             wo_came = wo_moving
-            g_down = z_reduce(g_down, z)
+            g_down = z_reduce(down)
         g_wo, wo_moving = plane_step_2(g_wo, wo_came, bits)
         grad_query = score_scale * jnp.einsum(
             "bhrqk,bkhd->bqhrd", grad_scores, key, preferred_element_type=F32
@@ -663,65 +720,73 @@
         key_back = turn(grad_key, cosine_lookup, -sine_lookup).reshape(count, kv_width).astype(BF)
         value_back = grad_value.reshape(count, kv_width).astype(BF)
         grad_raw = jnp.concatenate([query_back, key_back, value_back], axis=1)
-        normed_mine, normed_theirs = core_halves(mm(normed_in, by_core).astype(BF), c)
-        grad_raw, *wo_came = tied(grad_raw, *wo_moving)
+        if planes == 4:
+            grad_raw, wo_0, wo_1, down_0, down_1 = tied(grad_raw, *wo_moving, *moving)
+            wo_came = (wo_0, wo_1)
+            g_down = owned(down, (down_far, down_0, down_1), z)
+            moving = walk_1(g_both, z)
+        else:
+            wo_came = wo_moving
         g_wo = plane_step_3(g_wo, wo_came, bits)
 
+    with jax.named_scope("q_k_v_weight_gradients"):
+        qkv_came = swap(t_mm(normed_theirs, grad_raw).astype(BF), 1)
+        g_qkv = t_mm(normed_mine, grad_raw)
+        if planes == 4:
+            qkv_came, g_qkv, moving = tied(qkv_came, g_qkv, moving)
+            moving, both_far = walk_2(g_both, moving, z)
+        g_qkv = [g_qkv.reshape(shape), qkv_came.reshape(shape)]
+        qkv_moving = plane_step_1(g_qkv, bits)
+
     with jax.named_scope("input_gradient"):
-        qkv_came = swap(t_mm(normed_theirs, grad_raw).astype(BF), 1)
-        g_qkv = t_mm(normed_mine, grad_raw) + qkv_came.astype(F32)
         grad_in = mm_t(grad_raw, wqkv)
         grad_gain_in, grad_tokens = norm_back(grad_in, inputs_f, inv_attn, gain_in)
         input_grad = (grad_res + grad_tokens).astype(BF)
         gains = jnp.stack([grad_gain_in, grad_gain_mid])
+        gains_came = swap(gains, 1)
 
     with jax.named_scope("weight_gradients_to_owners"):
-        g_qkv = g_qkv.reshape(shape)
-        g_qkv, gains = tied(g_qkv, gains)
-        qkv_came = tied(*plane_step_1(g_qkv, bits), swap(gains, 1))
-        gains = gains + qkv_came[2]
-        if planes == 4:
-            g_both, both_came, *qkv_came = tied(g_both, both_moving, *qkv_came[:2])
-            both_moving = walk_end(g_both, both_came, z)
-        else:
-            g_both = z_reduce(g_both, z)
-        g_qkv, qkv_moving = plane_step_2(g_qkv, qkv_came[:2], bits)
-        if planes == 4:
-            *qkv_came, both_0, both_1, both_2 = tied(*qkv_moving, *both_moving)
-            g_both = owned(g_both, (both_0, both_1, both_2), z)
+        if planes == 4:
+            *qkv_came, moving, both_far, gains_came, gains = tied(
+                *qkv_moving, moving, both_far, gains_came, gains
+            )
+            moving = walk_3(g_both, moving, z)
         else:
             qkv_came = qkv_moving
+            both = z_reduce(g_both)
+        gains = gains + gains_came
+        g_qkv, qkv_moving = plane_step_2(g_qkv, qkv_came, bits)
+        gains_came = swap(gains, 8)
+        if planes == 4:
+            qkv_0, qkv_1, both_0, both_1, gains_came = tied(*qkv_moving, *moving, gains_came)
+            qkv_came = (qkv_0, qkv_1)
+            both = owned(g_both, (both_far, both_0, both_1), z)
+        else:
+            qkv_came = qkv_moving
+        gains = gains + gains_came
         g_qkv = plane_step_3(g_qkv, qkv_came, bits)
-        g_both = g_both.astype(BF)
-        g_all = jnp.concatenate([g_qkv, g_wo], axis=2)
-        gains, g_all, g_both = tied(gains, g_all, g_both)
-        if planes == 4:
-            all_moving = walk_start(g_all, z)
-        came = [pick(g_both, p ^ r, 0) for r in range(4)]
-        gains_came, *moved = tied(
-            swap(gains, 2), *[swap(came[r], r << 1) for r in (1, 2, 3)]
-        )
+        both = both.astype(BF)
+        if planes == 4:
+            moving = direct([g_qkv], z) + direct([g_wo], z)
+        gains_came = swap(gains, high)
+        gains, gains_came, both = tied(gains, gains_came, both)
+        gains = gains + gains_came
+        came = [pick(both, p ^ r, 0) for r in range(4)]
+        gains_came, *moved = tied(swap(gains, 2), *[swap(came[r], r << 1) for r in (1, 2, 3)])
         gains = gains + gains_came
         for mask in rest:
             gains = gains + swap(gains, mask)
         grad_gate, grad_up = spread_columns([came[0]] + moved, p, part)
-        gains_came = swap(gains, 4)
-        if planes == 4:
-            g_all, all_came, gains_came = tied(g_all, all_moving, gains_came)
-            gains = gains + gains_came
-            all_0, all_1, all_2, gains_came = tied(*walk_end(g_all, all_came, z), swap(gains, 8))
-            g_all = owned(g_all, (all_0, all_1, all_2), z)
+        gains = gains + swap(gains, 4)
+        g_gains = lax.dynamic_slice_in_dim(gains, position * rows, rows, 1)
+        if planes == 4:
+            g_qkv = owned([g_qkv], moving[:3], z)
+            g_wo = owned([g_wo], moving[3:], z)
         else:
-            gains = gains + gains_came
-            gains_came = swap(gains, 8)
-            g_all = z_reduce(g_all, z)
-        gains = gains + gains_came
-        gains = gains + swap(gains, high)
-        g_gains = lax.dynamic_slice_in_dim(gains, position * rows, rows, 1)
-        g_wq = g_all[:, :width]
-        g_wk = g_all[:, width : width + kv_width]
-        g_wv = g_all[:, width + kv_width : wide]
-        g_wo = g_all[:, wide:]
+            g_qkv, g_wo = z_reduce([g_qkv]), z_reduce([g_wo])
+        g_wq = g_qkv[:, :width]
+        g_wk = g_qkv[:, width : width + kv_width]
+        g_wv = g_qkv[:, width + kv_width :]
 
     return (
         out_act,

time: 634 us -> 560 us (0.88)
  waiting for transfers between devices: 247 us -> 185 us
  matrix products: 108 us -> 84 us
  local copies, waits for them, and re-layouts: 91.5 us -> 76.2 us
  starting transfers between devices: 114 us -> 129 us
  Pallas kernels: 1.86 us -> 13.4 us
    ppermute x27 -> x25, waiting for transfers between devices: 93.6 us -> 59.2 us  [along_z(): lax.ppermute(value, 'dp', [(8 * a + i, 8 * b + i) for a, b in pairs for i...]
    ppermute x58 -> x64, waiting for transfers between devices: 154 us -> 126 us  [swap(): return lax.ppermute(value, 'dp', [(i, i ^ mask) for i in range(n)])]
    dot_general x22 -> x26, matrix products: 102 us -> 78.3 us  [dot(): return lax.dot_general(a, b, (dims, ((), ())), preferred_element_type=F32)]
    dynamic_update_slice x32 -> x19, local copies, waits for them, and re-layouts: 34.9 us -> 16.2 us  [place(): return lax.dynamic_update_slice(out, piece, where)]
    ppermute x58 -> x64, starting transfers between devices: 53.8 us -> 69.1 us  [swap(): return lax.ppermute(value, 'dp', [(i, i ^ mask) for i in range(n)])]
    convert_element_type x7 -> x16, other arithmetic: 5.65 us -> 18.3 us  [the longest x2 4.3 us: walk_2(): across.astype(BF)]
    pallas_call x0 -> x2, Pallas kernels: none -> 11.5 us  [assembled(): pl.pallas_call(kernel, out_shape=jax.ShapeDtypeStruct((count * blocks * r...]
    optimization_barrier x4 -> x0, local copies, waits for them, and re-layouts: 9.25 us -> none  [tied(): return lax.optimization_barrier(values)]
  transfers between devices with their start and end apart: 85 -> 89, of which waited for: 43 -> 40; matrix products, arithmetic and copies ran while one was open for 35% -> 33% of each run, Pallas kernels for 0% -> 2%
where the time goes in v5:
time: 560 us; the launch traced here: 552 us
  waiting for transfers between devices  185 us (33%)
  starting transfers between devices  129 us (23%)
  matrix products  84 us (15%)
  local copies, waits for them, and re-layouts  76.2 us (14%)
  other arithmetic  57.6 us (10%)
  Pallas kernels  13.4 us (2%)
  between operations  6.29 us (1%)
    ppermute x64, waiting for transfers between devices, swap(): return lax.ppermute(value, 'dp', [(i, i ^ mask) for i in range(n)])  126 us
    dot_general x26, matrix products, dot(): return lax.dot_general(a, b, (dims, ((), ())), preferred_element_type=F32)  78.3 us
    ppermute x64, starting transfers between devices, swap(): return lax.ppermute(value, 'dp', [(i, i ^ mask) for i in range(n)])  69.1 us
    ppermute x25, starting transfers between devices, along_z(): lax.ppermute(value, 'dp', [(8 * a + i, 8 * b + i) for a, b in pairs for i...  60 us
    ppermute x25, waiting for transfers between devices, along_z(): lax.ppermute(value, 'dp', [(8 * a + i, 8 * b + i) for a, b in pairs for i...  59.2 us
    dynamic_update_slice x19, local copies, waits for them, and re-layouts, place(): return lax.dynamic_update_slice(out, piece, where)  16.2 us
    unnamed x234, local copies, waits for them, and re-layouts  12.3 us
    pallas_call x2, Pallas kernels, assembled(): pl.pallas_call(kernel, out_shape=jax.ShapeDtypeStruct((count * blocks * r...  11.5 us
  transfers between devices with their start and end apart: 89, of which 40 were waited for; matrix products, arithmetic and copies ran while one was open for 33% of the time, Pallas kernels for 2%

profile of v5, /device:TPU:0, one launch (start us, length us, event | category | flops | bytes accessed | tf_op | source)
XLA Modules:
  0.0 552.0 jit_solution(1244200260251739165)
XLA Ops:
  4.1 4.9 collective-permute-start
  19.4 4.0 collective-permute-done.3
  26.5 5.3 collective-permute-start.7
  36.1 5.9 %collective-permute-done.6 = bf16[48,4736]{1,0:T(8,128)(2,1)S(1)} collective-permute-done((bf16[48,4736]{1,0:T(8,128)(2,1)S(1)}, bf16[48,4736]{1,0:T(8,128)(2,1)S(1)}, u32[]{:S(2)}, u32[]{:S(2)}) %collective-permute-start.6) | collective-permute-done | bytes 454688 | tf_op jit(solution)/shard_map/phase_1/ppermute | solution.py:41
  53.0 20.2 %collective-permute-done.11 = bf16[48,4736]{1,0:T(8,128)(2,1)S(1)} collective-permute-done((bf16[48,4736]{1,0:T(8,128)(2,1)S(1)}, bf16[48,4736]{1,0:T(8,128)(2,1)S(1)}, u32[]{:S(2)}, u32[]{:S(2)}) %collective-permute-start.11) | collective-permute-done | bytes 454688 | tf_op jit(solution)/shard_map/phase_2/ppermute | solution.py:103
  77.8 8.5 %collective-permute-done.12 = bf16[48,4736]{1,0:T(8,128)(2,1)S(1)} collective-permute-done((bf16[48,4736]{1,0:T(8,128)(2,1)S(1)}, bf16[48,4736]{1,0:T(8,128)(2,1)S(1)}, u32[]{:S(2)}, u32[]{:S(2)}) %collective-permute-start.12) | collective-permute-done | bytes 454688 | tf_op jit(solution)/shard_map/phase_3/ppermute | solution.py:41
  90.5 2.2 collective-permute-start.20
  98.2 11.3 %collective-permute-done.17 = bf16[2,48,4736]{2,1,0:T(8,128)(2,1)S(1)} collective-permute-done((bf16[2,48,4736]{2,1,0:T(8,128)(2,1)S(1)}, bf16[2,48,4736]{2,1,0:T(8,128)(2,1)S(1)}, u32[]{:S(2)}, u32[]{:S(2)}) %collective-permute-start.17) | collective-permute-done | bytes 909344 | tf_op jit(solution)/shard_map/phase_4/ppermute | solution.py:41
  111.2 2.7 collective-permute-done.21
  124.3 2.1 fusion.184
  127.9 5.2 fusion.9
  133.2 5.9 %collective-permute-done.22 = bf16[4,48,2048]{2,1,0:T(8,128)(2,1)} collective-permute-done((bf16[4,48,2048]{2,1,0:T(8,128)(2,1)}, bf16[4,48,2048]{2,1,0:T(8,128)(2,1)}, u32[]{:S(2)}, u32[]{:S(2)}) %collective-permute-start.22) | collective-permute-done | bytes 786464 | tf_op jit(solution)/shard_map/phase_5/ppermute | solution.py:103
  141.3 2.2 collective-permute-start.25
  148.2 2.4 copy.157
  151.7 3.0 copy.120
  154.7 3.0 reshape.529
  157.8 2.2 subtract_convert_fusion.1
  166.2 3.5 fusion.31
  177.5 5.1 collective-permute-start.28
  187.0 3.8 multiply_reduce_fusion.3
  191.6 3.6 collective-permute-done.29
  198.0 9.2 %assembled.2 = bf16[1536,2048]{1,0:T(8,128)(2,1)S(1)} custom-call(s32[8,4]{1,0:T(8,128)S(1)} %add_multiply_fusion.at, bf16[4,48,2048]{2,1,0:T(8,128)(2,1)S(1)} %bitcast_dynamic-update-slice_fusion.16.refs_0_, bf16[4,48,2048]{2,1,0:T(8,128)(2,1)S(1)} %get-tuple-element.215.refs_1_, bf16[4,48,2048]{2,1,0:T(8,128)(2,1)S(1)} %broadcast_select_fusion.1.refs_2_, ...), custom_call_target="tpu_custom_call" | custom-call | bytes 12582912 | tf_op jit(solution)/shard_map/ffn_forward/assembled/pallas_call | solution.py:234
  212.4 3.4 fusion.197
  215.8 2.7 fusion.19
  220.4 4.9 collective-permute-done.34
  226.9 3.5 fusion.199
  231.0 2.3 assembled.3
  237.4 2.7 fusion.20
  243.1 8.8 %collective-permute-done.36 = bf16[256,1536]{1,0:T(8,128)(2,1)S(1)} collective-permute-done((bf16[256,1536]{1,0:T(8,128)(2,1)S(1)}, bf16[256,1536]{1,0:T(8,128)(2,1)S(1)}, u32[]{:S(2)}, u32[]{:S(2)}) %collective-permute-start.36) | collective-permute-done | bytes 786464 | tf_op jit(solution)/shard_map/ffn_forward/ppermute | solution.py:41
  257.5 3.7 collective-permute-done.38
  270.2 5.9 %collective-permute-done.40 = bf16[128,1536]{1,0:T(8,128)(2,1)S(1)} collective-permute-done((bf16[128,1536]{1,0:T(8,128)(2,1)S(1)}, bf16[128,1536]{1,0:T(8,128)(2,1)S(1)}, u32[]{:S(2)}, u32[]{:S(2)}) %collective-permute-start.40) | collective-permute-done | bytes 393248 | tf_op jit(solution)/shard_map/ffn_backward/ppermute | solution.py:41
  277.8 2.5 collective-permute-start.43
  282.2 2.4 multiply_convert_fusion.3
  286.4 3.4 collective-permute-start.45
  289.9 5.6 %fusion.76 = f32[512,1536]{1,0:T(8,128)} fusion(bf16[1536,2048]{1,0:T(8,128)(2,1)S(1)} %assembled.2, bf16[512,1024]{1,0:T(8,128)(2,1)S(1)} %get-tuple-element.349, bf16[512,1024]{1,0:T(8,128)(2,1)S(1)} %get-tuple-element.348), kind=kOutput, calls=%fused_computation.216 | convolution fusion | flops 3225419776 | bytes 11534336 | tf_op jit(solution)/shard_map/ffn_backward/dot_general | solution.py:24
  295.6 2.3 multiply_convert_fusion.1
  298.0 3.4 fusion.75
  309.3 3.7 add_convert_fusion
  313.4 11.1 %collective-permute-done.46 = bf16[256,1536]{1,0:T(8,128)(2,1)S(1)} collective-permute-done((bf16[256,1536]{1,0:T(8,128)(2,1)S(1)}, bf16[256,1536]{1,0:T(8,128)(2,1)S(1)}, u32[]{:S(2)}, u32[]{:S(2)}) %collective-permute-start.46) | collective-permute-done | bytes 786464 | tf_op jit(solution)/shard_map/ffn_backward/ppermute | solution.py:41
  328.3 3.8 collective-permute-start.54
  332.1 2.4 convert_add_fusion.3
  338.3 7.6 %collective-permute-done.53 = f32[2,128]{1,0:T(2,128)S(1)} collective-permute-done((f32[2,128]{1,0:T(2,128)S(1)}, f32[2,128]{1,0:T(2,128)S(1)}, u32[]{:S(2)}, u32[]{:S(2)}) %collective-permute-start.53) | collective-permute-done | bytes 1056 | tf_op jit(solution)/shard_map/ffn_backward/ppermute | solution.py:41
  352.7 2.2 convolution_convert_fusion.1
  355.0 4.6 fusion.25
  359.6 4.9 reshape.547
  364.5 3.6 copy.130
  371.9 5.1 collective-permute-start.59
  386.9 12.0 %collective-permute-done.58 = bf16[2,2,48,1536]{3,2,1,0:T(8,128)(2,1)S(1)} collective-permute-done((bf16[2,2,48,1536]{3,2,1,0:T(8,128)(2,1)S(1)}, bf16[2,2,48,1536]{3,2,1,0:T(8,128)(2,1)S(1)}, u32[]{:S(2)}, u32[]{:S(2)}) %collective-permute-start.58) | collective-permute-done | bytes 589856 | tf_op jit(solution)/shard_map/attention_backward/ppermute | solution.py:41
  414.7 3.7 convolution_convert_fusion
  418.5 3.8 fusion.73
  424.3 3.2 fusion.65
  427.5 4.1 collective-permute-start.66
  431.6 2.4 collective-permute-start.69
  436.0 7.8 %fusion.44 = (f32[1536]{0:T(1024)S(1)}, f32[256]{0:T(256)S(1)}, f32[256,1536]{1,0:T(8,128)}) fusion(bf16[256,1536]{1,0:T(8,128)(2,1)S(1)} %copy-done.28, f32[256]{0:T(256)S(1)} %copy-done.85, f32[1536]{0:T(1024)S(1)} %copy-done.78, bf16[256,3072]{0,1:T(8,128)(2,1)S(1)} %copy-done.10, bf16[1536,4736]{1,0:T(8,128)(2,1)} %bitcast.464), kind=kOutput, calls=%fused_computation.97 | convolution fusion | flops 2418669824 | bytes 13383680 | tf_op jit(solution)/shard_map/input_gradient/dot_general | solution.py:24
  448.9 4.2 fusion.185
  453.1 2.9 fusion.186
  465.8 2.5 collective-permute-start.80
  468.3 2.7 collective-permute-start.81
  471.0 21.6 %collective-permute-done.70 = bf16[4,48,2048]{2,1,0:T(8,128)(2,1)S(1)} collective-permute-done((bf16[4,48,2048]{2,1,0:T(8,128)(2,1)S(1)}, bf16[4,48,2048]{2,1,0:T(8,128)(2,1)S(1)}, u32[]{:S(2)}, u32[]{:S(2)}) %collective-permute-start.70) | collective-permute-done | bytes 786464 | tf_op jit(solution)/shard_map/q_k_v_weight_gradients/ppermute | solution.py:103
  492.6 2.3 fusion.33
  495.0 4.0 collective-permute-start.74
  504.9 2.7 collective-permute-start.76
  508.4 7.0 %collective-permute-done.76 = f32[2,1536]{1,0:T(2,128)S(1)} collective-permute-done((f32[2,1536]{1,0:T(2,128)S(1)}, f32[2,1536]{1,0:T(2,128)S(1)}, u32[]{:S(2)}, u32[]{:S(2)}) %collective-permute-start.76) | collective-permute-done | bytes 12320 | tf_op jit(solution)/shard_map/weight_gradients_to_owners/ppermute | solution.py:41
  536.8 11.8 %collective-permute-done.78 = bf16[48,3072]{1,0:T(8,128)(2,1)S(1)} collective-permute-done((bf16[48,3072]{1,0:T(8,128)(2,1)S(1)}, bf16[48,3072]{1,0:T(8,128)(2,1)S(1)}, u32[]{:S(2)}, u32[]{:S(2)}) %collective-permute-start.78) | collective-permute-done | bytes 294944 | tf_op jit(solution)/shard_map/weight_gradients_to_owners/ppermute | solution.py:41
  (565 shorter events, 224.2 us)
Async XLA Ops:
  4.1 19.3 %collective-permute-start = (bf16[48,4736]{1,0:T(8,128)(2,1)}, bf16[48,4736]{1,0:T(8,128)(2,1)S(1)}, u32[]{:S(2)}, u32[]{:S(2)}) collective-permute-start(bf16[48,4736]{1,0:T(8,128)(2,1)} %packed.1), channel_id=1, source_target_pairs={{0,8},{1,9},{2,10},{3,11},{4,12},{5,13},{6,14},{7,15},{8,16},{9,17... | collective-permute-start | bytes 1363976 | tf_op jit(solution)/shard_map/phase_0/ppermute | solution.py:103
  9.0 15.1 %collective-permute-start.1 = (bf16[48,4736]{1,0:T(8,128)(2,1)}, bf16[48,4736]{1,0:T(8,128)(2,1)S(1)}, u32[]{:S(2)}, u32[]{:S(2)}) collective-permute-start(bf16[48,4736]{1,0:T(8,128)(2,1)} %packed.1), channel_id=1, source_target_pairs={{8,0},{9,1},{10,2},{11,3},{12,4},{13,5},{14,6},{15,7},{16,8},{17,9... | collective-permute-start | bytes 1363976 | tf_op jit(solution)/shard_map/phase_0/ppermute | solution.py:103
  26.5 15.5 %collective-permute-start.7 = (bf16[48,4736]{1,0:T(8,128)(2,1)S(1)}, bf16[48,4736]{1,0:T(8,128)(2,1)S(1)}, u32[]{:S(2)}, u32[]{:S(2)}) collective-permute-start(bf16[48,4736]{1,0:T(8,128)(2,1)S(1)} %copy-done.35), channel_id=1, source_target_pairs={{0,16},{1,17},{2,18},{3,19},{4,20},{5,21},{6,22},{7,23},{24,8},{25... | collective-permute-start | bytes 1363976 | tf_op jit(solution)/shard_map/phase_1/ppermute | solution.py:103
  32.7 11.4 %collective-permute-start.8 = (bf16[48,4736]{1,0:T(8,128)(2,1)S(1)}, bf16[48,4736]{1,0:T(8,128)(2,1)S(1)}, u32[]{:S(2)}, u32[]{:S(2)}) collective-permute-start(bf16[48,4736]{1,0:T(8,128)(2,1)S(1)} %get-tuple-element.171), channel_id=1, source_target_pairs={{8,0},{9,1},{10,2},{11,3},{12,4},{13,5},{14,6},{15,7},{16,24},{17,... | collective-permute-start | bytes 1363976 | tf_op jit(solution)/shard_map/phase_1/ppermute | solution.py:103
  44.5 33.2 %collective-permute-start.14 = (bf16[4,48,2048]{2,1,0:T(8,128)(2,1)S(1)}, bf16[4,48,2048]{2,1,0:T(8,128)(2,1)S(1)}, u32[]{:S(2)}, u32[]{:S(2)}) collective-permute-start(bf16[4,48,2048]{2,1,0:T(8,128)(2,1)S(1)} %bitcast_dynamic-update-slice_fusion.16.refs_0_), channel_id=1, source_target_pairs={{0,8},{1,9},{2,10},{3,11},{4,12},{5,13},{6,14},{7,15},{8,16},{9,17... | collective-permute-start | bytes 2359304 | tf_op jit(solution)/shard_map/phase_2/ppermute | solution.py:103
  46.0 31.7 %collective-permute-start.15 = (bf16[4,48,2048]{2,1,0:T(8,128)(2,1)S(1)}, bf16[4,48,2048]{2,1,0:T(8,128)(2,1)S(1)}, u32[]{:S(2)}, u32[]{:S(2)}) collective-permute-start(bf16[4,48,2048]{2,1,0:T(8,128)(2,1)S(1)} %bitcast_dynamic-update-slice_fusion.16.refs_0_), channel_id=1, source_target_pairs={{8,0},{9,1},{10,2},{11,3},{12,4},{13,5},{14,6},{15,7},{16,8},{17,9... | collective-permute-start | bytes 2359304 | tf_op jit(solution)/shard_map/phase_2/ppermute | solution.py:103
  47.3 25.9 %collective-permute-start.10 = (bf16[2,48,4736]{2,1,0:T(8,128)(2,1)S(1)}, bf16[2,48,4736]{2,1,0:T(8,128)(2,1)S(1)}, u32[]{:S(2)}, u32[]{:S(2)}) collective-permute-start(bf16[2,48,4736]{2,1,0:T(8,128)(2,1)S(1)} %pad_maximum_fusion.11), channel_id=1, source_target_pairs={{0,2},{1,3},{2,0},{3,1},{4,6},{5,7},{6,4},{7,5},{8,10},{9,11},{10,... | collective-permute-start | bytes 2727944 | tf_op jit(solution)/shard_map/phase_2/ppermute | solution.py:41
  47.9 25.3 %collective-permute-start.9 = (bf16[2,48,4736]{2,1,0:T(8,128)(2,1)S(1)}, bf16[2,48,4736]{2,1,0:T(8,128)(2,1)S(1)}, u32[]{:S(2)}, u32[]{:S(2)}) collective-permute-start(bf16[2,48,4736]{2,1,0:T(8,128)(2,1)S(1)} %pad_maximum_fusion.10), channel_id=1, source_target_pairs={{0,4},{1,5},{2,6},{3,7},{4,0},{5,1},{6,2},{7,3},{8,12},{9,13},{10,... | collective-permute-start | bytes 2727944 | tf_op jit(solution)/shard_map/phase_2/ppermute | solution.py:41
  49.4 23.8 %collective-permute-start.11 = (bf16[48,4736]{1,0:T(8,128)(2,1)S(1)}, bf16[48,4736]{1,0:T(8,128)(2,1)S(1)}, u32[]{:S(2)}, u32[]{:S(2)}) collective-permute-start(bf16[48,4736]{1,0:T(8,128)(2,1)S(1)} %collective-permute-done.7), channel_id=1, source_target_pairs={{8,0},{9,1},{10,2},{11,3},{12,4},{13,5},{14,6},{15,7},{16,24},{17,... | collective-permute-start | bytes 1363976 | tf_op jit(solution)/shard_map/phase_2/ppermute | solution.py:103
  73.3 13.0 %collective-permute-start.16 = (bf16[2,2,48,4736]{3,2,1,0:T(8,128)(2,1)S(1)}, bf16[2,2,48,4736]{3,2,1,0:T(8,128)(2,1)S(1)}, u32[]{:S(2)}, u32[]{:S(2)}) collective-permute-start(bf16[2,2,48,4736]{3,2,1,0:T(8,128)(2,1)S(1)} %pad_maximum_fusion.3), channel_id=1, source_target_pairs={{0,1},{1,0},{2,3},{3,2},{4,5},{5,4},{6,7},{7,6},{8,9},{9,8},{10,11... | collective-permute-start | bytes 5455880 | tf_op jit(solution)/shard_map/phase_3/ppermute | solution.py:41
  73.4 12.8 %collective-permute-start.12 = (bf16[48,4736]{1,0:T(8,128)(2,1)S(1)}, bf16[48,4736]{1,0:T(8,128)(2,1)S(1)}, u32[]{:S(2)}, u32[]{:S(2)}) collective-permute-start(bf16[48,4736]{1,0:T(8,128)(2,1)S(1)} %broadcast_select_fusion.7), channel_id=1, source_target_pairs={{0,2},{1,3},{2,0},{3,1},{4,6},{5,7},{6,4},{7,5},{8,10},{9,11},{10,... | collective-permute-start | bytes 1363976 | tf_op jit(solution)/shard_map/phase_3/ppermute | solution.py:41
  73.4 12.9 %collective-permute-start.13 = (bf16[48,4736]{1,0:T(8,128)(2,1)S(1)}, bf16[48,4736]{1,0:T(8,128)(2,1)S(1)}, u32[]{:S(2)}, u32[]{:S(2)}) collective-permute-start(bf16[48,4736]{1,0:T(8,128)(2,1)S(1)} %broadcast_select_fusion.6), channel_id=1, source_target_pairs={{0,4},{1,5},{2,6},{3,7},{4,0},{5,1},{6,2},{7,3},{8,12},{9,13},{10,... | collective-permute-start | bytes 1363976 | tf_op jit(solution)/shard_map/phase_3/ppermute | solution.py:41
  86.8 24.1 %collective-permute-start.19 = (bf16[2,2,48,4736]{3,2,1,0:T(8,128)(2,1)S(1)}, bf16[2,2,48,4736]{3,2,1,0:T(8,128)(2,1)S(1)}, u32[]{:S(2)}, u32[]{:S(2)}) collective-permute-start(bf16[2,2,48,4736]{3,2,1,0:T(8,128)(2,1)S(1)} %pad_maximum_fusion.4), channel_id=1, source_target_pairs={{0,1},{1,0},{2,3},{3,2},{4,5},{5,4},{6,7},{7,6},{8,9},{9,8},{10,11... | collective-permute-start | bytes 5455880 | tf_op jit(solution)/shard_map/phase_4/ppermute | solution.py:41
  86.9 22.6 %collective-permute-start.17 = (bf16[2,48,4736]{2,1,0:T(8,128)(2,1)S(1)}, bf16[2,48,4736]{2,1,0:T(8,128)(2,1)S(1)}, u32[]{:S(2)}, u32[]{:S(2)}) collective-permute-start(bf16[2,48,4736]{2,1,0:T(8,128)(2,1)S(1)} %pad_maximum_fusion.12), channel_id=1, source_target_pairs={{0,4},{1,5},{2,6},{3,7},{4,0},{5,1},{6,2},{7,3},{8,12},{9,13},{10,... | collective-permute-start | bytes 2727944 | tf_op jit(solution)/shard_map/phase_4/ppermute | solution.py:41
  88.7 22.2 %collective-permute-start.18 = (bf16[2,48,4736]{2,1,0:T(8,128)(2,1)S(1)}, bf16[2,48,4736]{2,1,0:T(8,128)(2,1)S(1)}, u32[]{:S(2)}, u32[]{:S(2)}) collective-permute-start(bf16[2,48,4736]{2,1,0:T(8,128)(2,1)S(1)} %pad_maximum_fusion.13), channel_id=1, source_target_pairs={{0,2},{1,3},{2,0},{3,1},{4,6},{5,7},{6,4},{7,5},{8,10},{9,11},{10,... | collective-permute-start | bytes 2727944 | tf_op jit(solution)/shard_map/phase_4/ppermute | solution.py:41
  90.5 20.7 %collective-permute-start.20 = (bf16[4,48,2048]{2,1,0:T(8,128)(2,1)S(1)}, bf16[4,48,2048]{2,1,0:T(8,128)(2,1)}, u32[]{:S(2)}, u32[]{:S(2)}) collective-permute-start(bf16[4,48,2048]{2,1,0:T(8,128)(2,1)S(1)} %bitcast_dynamic-update-slice_fusion.16.refs_0_), channel_id=1, source_target_pairs={{0,16},{1,17},{2,18},{3,19},{4,20},{5,21},{6,22},{7,23},{24,8},{25... | collective-permute-start | bytes 2359304 | tf_op jit(solution)/shard_map/phase_4/ppermute | solution.py:103
  92.7 21.2 %collective-permute-start.21 = (bf16[4,48,2048]{2,1,0:T(8,128)(2,1)S(1)}, bf16[4,48,2048]{2,1,0:T(8,128)(2,1)S(1)}, u32[]{:S(2)}, u32[]{:S(2)}) collective-permute-start(bf16[4,48,2048]{2,1,0:T(8,128)(2,1)S(1)} %get-tuple-element.200), channel_id=1, source_target_pairs={{8,0},{9,1},{10,2},{11,3},{12,4},{13,5},{14,6},{15,7},{16,24},{17,... | collective-permute-start | bytes 2359304 | tf_op jit(solution)/shard_map/phase_4/ppermute | solution.py:103
  117.5 21.6 %collective-permute-start.22 = (bf16[4,48,2048]{2,1,0:T(8,128)(2,1)}, bf16[4,48,2048]{2,1,0:T(8,128)(2,1)}, u32[]{:S(2)}, u32[]{:S(2)}) collective-permute-start(bf16[4,48,2048]{2,1,0:T(8,128)(2,1)} %collective-permute-done.20), channel_id=1, source_target_pairs={{8,0},{9,1},{10,2},{11,3},{12,4},{13,5},{14,6},{15,7},{16,24},{17,... | collective-permute-start | bytes 2359304 | tf_op jit(solution)/shard_map/phase_5/ppermute | solution.py:103
  141.3 28.4 %collective-permute-start.25 = (bf16[128,1536]{1,0:T(8,128)(2,1)}, bf16[128,1536]{1,0:T(8,128)(2,1)}, u32[]{:S(2)}, u32[]{:S(2)}) collective-permute-start(bf16[128,1536]{1,0:T(8,128)(2,1)} %param.21), channel_id=1, source_target_pairs={{0,8},{1,9},{2,10},{3,11},{4,12},{5,13},{6,14},{7,15},{8,16},{9,17... | collective-permute-start | bytes 1179656 | tf_op jit(solution)/shard_map/attention_forward/ppermute | solution.py:103
  143.5 26.2 %collective-permute-start.26 = (bf16[128,1536]{1,0:T(8,128)(2,1)}, bf16[128,1536]{1,0:T(8,128)(2,1)}, u32[]{:S(2)}, u32[]{:S(2)}) collective-permute-start(bf16[128,1536]{1,0:T(8,128)(2,1)} %param.21), channel_id=1, source_target_pairs={{8,0},{9,1},{10,2},{11,3},{12,4},{13,5},{14,6},{15,7},{16,8},{17,9... | collective-permute-start | bytes 1179656 | tf_op jit(solution)/shard_map/attention_forward/ppermute | solution.py:103
  171.4 23.8 %collective-permute-start.27 = (bf16[4,4,48,2048]{3,2,1,0:T(8,128)(2,1)S(1)}, bf16[4,4,48,2048]{3,2,1,0:T(8,128)(2,1)S(1)}, u32[]{:S(2)}, u32[]{:S(2)}) collective-permute-start(bf16[4,4,48,2048]{3,2,1,0:T(8,128)(2,1)S(1)} %pad_maximum_fusion), channel_id=1, source_target_pairs={{0,1},{1,0},{2,3},{3,2},{4,5},{5,4},{6,7},{7,6},{8,9},{9,8},{10,11... | collective-permute-start | bytes 9437192 | tf_op jit(solution)/shard_map/attention_forward/ppermute | solution.py:41
  177.5 14.1 %collective-permute-start.28 = (bf16[128,1536]{1,0:T(8,128)(2,1)}, bf16[128,1536]{1,0:T(8,128)(2,1)S(1)}, u32[]{:S(2)}, u32[]{:S(2)}) collective-permute-start(bf16[128,1536]{1,0:T(8,128)(2,1)} %param.21), channel_id=1, source_target_pairs={{0,16},{1,17},{2,18},{3,19},{4,20},{5,21},{6,22},{7,23},{24,8},{25... | collective-permute-start | bytes 1179656 | tf_op jit(solution)/shard_map/attention_forward/ppermute | solution.py:103
  182.6 12.6 %collective-permute-start.29 = (bf16[128,1536]{1,0:T(8,128)(2,1)S(1)}, bf16[128,1536]{1,0:T(8,128)(2,1)S(1)}, u32[]{:S(2)}, u32[]{:S(2)}) collective-permute-start(bf16[128,1536]{1,0:T(8,128)(2,1)S(1)} %get-tuple-element.221), channel_id=1, source_target_pairs={{8,0},{9,1},{10,2},{11,3},{12,4},{13,5},{14,6},{15,7},{16,24},{17,... | collective-permute-start | bytes 1179656 | tf_op jit(solution)/shard_map/attention_forward/ppermute | solution.py:103
  195.3 12.0 %collective-permute-start.30 = (bf16[128,1536]{1,0:T(8,128)(2,1)S(1)}, bf16[128,1536]{1,0:T(8,128)(2,1)S(1)}, u32[]{:S(2)}, u32[]{:S(2)}) collective-permute-start(bf16[128,1536]{1,0:T(8,128)(2,1)S(1)} %get-tuple-element.425), channel_id=1, source_target_pairs={{0,2},{1,3},{2,0},{3,1},{4,6},{5,7},{6,4},{7,5},{8,10},{9,11},{10,... | collective-permute-start | bytes 1179656 | tf_op jit(solution)/shard_map/ffn_forward/ppermute | solution.py:41
  195.6 11.6 %collective-permute-start.31 = (bf16[128,1536]{1,0:T(8,128)(2,1)S(1)}, bf16[128,1536]{1,0:T(8,128)(2,1)S(1)}, u32[]{:S(2)}, u32[]{:S(2)}) collective-permute-start(bf16[128,1536]{1,0:T(8,128)(2,1)S(1)} %get-tuple-element.424), channel_id=1, source_target_pairs={{0,4},{1,5},{2,6},{3,7},{4,0},{5,1},{6,2},{7,3},{8,12},{9,13},{10,... | collective-permute-start | bytes 1179656 | tf_op jit(solution)/shard_map/ffn_forward/ppermute | solution.py:41
  196.0 11.3 %collective-permute-start.32 = (bf16[128,1536]{1,0:T(8,128)(2,1)S(1)}, bf16[128,1536]{1,0:T(8,128)(2,1)S(1)}, u32[]{:S(2)}, u32[]{:S(2)}) collective-permute-start(bf16[128,1536]{1,0:T(8,128)(2,1)S(1)} %collective-permute-done.28), channel_id=1, source_target_pairs={{8,0},{9,1},{10,2},{11,3},{12,4},{13,5},{14,6},{15,7},{16,24},{17,... | collective-permute-start | bytes 1179656 | tf_op jit(solution)/shard_map/ffn_forward/ppermute | solution.py:103
  207.4 17.8 %collective-permute-start.34 = (bf16[256,1536]{1,0:T(8,128)(2,1)S(1)}, bf16[256,1536]{1,0:T(8,128)(2,1)S(1)}, u32[]{:S(2)}, u32[]{:S(2)}) collective-permute-start(bf16[256,1536]{1,0:T(8,128)(2,1)S(1)} %pad_maximum_fusion.15), channel_id=1, source_target_pairs={{0,4},{1,5},{2,6},{3,7},{4,0},{5,1},{6,2},{7,3},{8,12},{9,13},{10,... | collective-permute-start | bytes 2359304 | tf_op jit(solution)/shard_map/ffn_forward/ppermute | solution.py:41
  209.2 17.5 %collective-permute-start.35 = (bf16[256,1536]{1,0:T(8,128)(2,1)S(1)}, bf16[256,1536]{1,0:T(8,128)(2,1)S(1)}, u32[]{:S(2)}, u32[]{:S(2)}) collective-permute-start(bf16[256,1536]{1,0:T(8,128)(2,1)S(1)} %pad_maximum_fusion.16), channel_id=1, source_target_pairs={{0,2},{1,3},{2,0},{3,1},{4,6},{5,7},{6,4},{7,5},{8,10},{9,11},{10,... | collective-permute-start | bytes 2359304 | tf_op jit(solution)/shard_map/ffn_forward/ppermute | solution.py:41
  212.3 18.8 %collective-permute-start.33 = (bf16[4,128,1536]{2,1,0:T(8,128)(2,1)S(1)}, bf16[4,128,1536]{2,1,0:T(8,128)(2,1)S(1)}, u32[]{:S(2)}, u32[]{:S(2)}) collective-permute-start(bf16[4,128,1536]{2,1,0:T(8,128)(2,1)S(1)} %pad_maximum_fusion.7.refs_0_), channel_id=1, source_target_pairs={{0,1},{1,0},{2,3},{3,2},{4,5},{5,4},{6,7},{7,6},{8,9},{9,8},{10,11... | collective-permute-start | bytes 4718600 | tf_op jit(solution)/shard_map/ffn_forward/ppermute | solution.py:41
  235.3 16.6 %collective-permute-start.36 = (bf16[256,1536]{1,0:T(8,128)(2,1)S(1)}, bf16[256,1536]{1,0:T(8,128)(2,1)S(1)}, u32[]{:S(2)}, u32[]{:S(2)}) collective-permute-start(bf16[256,1536]{1,0:T(8,128)(2,1)S(1)} %get-tuple-element.387), channel_id=1, source_target_pairs={{0,4},{1,5},{2,6},{3,7},{4,0},{5,1},{6,2},{7,3},{8,12},{9,13},{10,... | collective-permute-start | bytes 2359304 | tf_op jit(solution)/shard_map/ffn_forward/ppermute | solution.py:41
  235.7 17.1 %collective-permute-start.37 = (bf16[256,1536]{1,0:T(8,128)(2,1)S(1)}, bf16[256,1536]{1,0:T(8,128)(2,1)S(1)}, u32[]{:S(2)}, u32[]{:S(2)}) collective-permute-start(bf16[256,1536]{1,0:T(8,128)(2,1)S(1)} %get-tuple-element.386), channel_id=1, source_target_pairs={{0,2},{1,3},{2,0},{3,1},{4,6},{5,7},{6,4},{7,5},{8,10},{9,11},{10,... | collective-permute-start | bytes 2359304 | tf_op jit(solution)/shard_map/ffn_forward/ppermute | solution.py:41
  277.8 17.7 %collective-permute-start.43 = (bf16[256,1536]{1,0:T(8,128)(2,1)S(1)}, bf16[256,1536]{1,0:T(8,128)(2,1)S(1)}, u32[]{:S(2)}, u32[]{:S(2)}) collective-permute-start(bf16[256,1536]{1,0:T(8,128)(2,1)S(1)} %pad_maximum_fusion.17), channel_id=1, source_target_pairs={{0,4},{1,5},{2,6},{3,7},{4,0},{5,1},{6,2},{7,3},{8,12},{9,13},{10,... | collective-permute-start | bytes 2359304 | tf_op jit(solution)/shard_map/ffn_backward/ppermute | solution.py:41
  280.4 15.1 %collective-permute-start.44 = (bf16[256,1536]{1,0:T(8,128)(2,1)S(1)}, bf16[256,1536]{1,0:T(8,128)(2,1)S(1)}, u32[]{:S(2)}, u32[]{:S(2)}) collective-permute-start(bf16[256,1536]{1,0:T(8,128)(2,1)S(1)} %pad_maximum_fusion.18), channel_id=1, source_target_pairs={{0,2},{1,3},{2,0},{3,1},{4,6},{5,7},{6,4},{7,5},{8,10},{9,11},{10,... | collective-permute-start | bytes 2359304 | tf_op jit(solution)/shard_map/ffn_backward/ppermute | solution.py:41
  286.4 15.0 %collective-permute-start.45 = (f32[2,128]{1,0:T(2,128)S(1)}, f32[2,128]{1,0:T(2,128)S(1)}, u32[]{:S(2)}, u32[]{:S(2)}) collective-permute-start(f32[2,128]{1,0:T(2,128)S(1)} %add.802), channel_id=1, source_target_pairs={{0,8},{1,9},{2,10},{3,11},{4,12},{5,13},{6,14},{7,15},{8,0},{9,1},... | collective-permute-start | bytes 3080 | tf_op jit(solution)/shard_map/ffn_backward/ppermute | solution.py:41
  301.4 12.0 %collective-permute-start.49 = (f32[2,128]{1,0:T(2,128)S(1)}, f32[2,128]{1,0:T(2,128)S(1)}, u32[]{:S(2)}, u32[]{:S(2)}) collective-permute-start(f32[2,128]{1,0:T(2,128)S(1)} %add.805), channel_id=1, source_target_pairs={{0,16},{1,17},{2,18},{3,19},{4,20},{5,21},{6,22},{7,23},{8,24},{9,... | collective-permute-start | bytes 3080 | tf_op jit(solution)/shard_map/ffn_backward/ppermute | solution.py:41
  304.3 21.1 %collective-permute-start.48 = (bf16[4,128,1536]{2,1,0:T(8,128)(2,1)S(1)}, bf16[4,128,1536]{2,1,0:T(8,128)(2,1)}, u32[]{:S(2)}, u32[]{:S(2)}) collective-permute-start(bf16[4,128,1536]{2,1,0:T(8,128)(2,1)S(1)} %fusion.34), channel_id=1, source_target_pairs={{0,1},{1,0},{2,3},{3,2},{4,5},{5,4},{6,7},{7,6},{8,9},{9,8},{10,11... | collective-permute-start | bytes 4718600 | tf_op jit(solution)/shard_map/ffn_backward/ppermute | solution.py:41
  304.5 20.0 %collective-permute-start.46 = (bf16[256,1536]{1,0:T(8,128)(2,1)S(1)}, bf16[256,1536]{1,0:T(8,128)(2,1)S(1)}, u32[]{:S(2)}, u32[]{:S(2)}) collective-permute-start(bf16[256,1536]{1,0:T(8,128)(2,1)S(1)} %get-tuple-element.381), channel_id=1, source_target_pairs={{0,4},{1,5},{2,6},{3,7},{4,0},{5,1},{6,2},{7,3},{8,12},{9,13},{10,... | collective-permute-start | bytes 2359304 | tf_op jit(solution)/shard_map/ffn_backward/ppermute | solution.py:41
  305.8 19.7 %collective-permute-start.47 = (bf16[256,1536]{1,0:T(8,128)(2,1)S(1)}, bf16[256,1536]{1,0:T(8,128)(2,1)S(1)}, u32[]{:S(2)}, u32[]{:S(2)}) collective-permute-start(bf16[256,1536]{1,0:T(8,128)(2,1)S(1)} %get-tuple-element.380), channel_id=1, source_target_pairs={{0,2},{1,3},{2,0},{3,1},{4,6},{5,7},{6,4},{7,5},{8,10},{9,11},{10,... | collective-permute-start | bytes 2359304 | tf_op jit(solution)/shard_map/ffn_backward/ppermute | solution.py:41
  326.3 21.2 %collective-permute-start.52 = (bf16[768,2048]{1,0:T(8,128)(2,1)}, bf16[768,2048]{1,0:T(8,128)(2,1)}, u32[]{:S(2)}, u32[]{:S(2)}) collective-permute-start(bf16[768,2048]{1,0:T(8,128)(2,1)} %add_convert_fusion), channel_id=1, source_target_pairs={{0,1},{1,0},{2,3},{3,2},{4,5},{5,4},{6,7},{7,6},{8,9},{9,8},{10,11... | collective-permute-start | bytes 9437192 | tf_op jit(solution)/shard_map/ffn_backward/ppermute | solution.py:41
  328.3 17.7 %collective-permute-start.54 = (bf16[128,1536]{1,0:T(8,128)(2,1)}, bf16[128,1536]{1,0:T(8,128)(2,1)}, u32[]{:S(2)}, u32[]{:S(2)}) collective-permute-start(bf16[128,1536]{1,0:T(8,128)(2,1)} %fusion.98), channel_id=1, source_target_pairs={{0,8},{1,9},{2,10},{3,11},{4,12},{5,13},{6,14},{7,15},{24,16},{25,... | collective-permute-start | bytes 1179656 | tf_op jit(solution)/shard_map/ffn_backward/ppermute | solution.py:103
  334.5 11.4 %collective-permute-start.50 = (bf16[128,1536]{1,0:T(8,128)(2,1)S(1)}, bf16[128,1536]{1,0:T(8,128)(2,1)S(1)}, u32[]{:S(2)}, u32[]{:S(2)}) collective-permute-start(bf16[128,1536]{1,0:T(8,128)(2,1)S(1)} %slice.583), channel_id=1, source_target_pairs={{0,2},{1,3},{2,0},{3,1},{4,6},{5,7},{6,4},{7,5},{8,10},{9,11},{10,... | collective-permute-start | bytes 1179656 | tf_op jit(solution)/shard_map/ffn_backward/ppermute | solution.py:41
  355.0 26.6 %collective-permute-start.55 = (bf16[768,1536]{1,0:T(8,128)(2,1)}, bf16[768,1536]{1,0:T(8,128)(2,1)}, u32[]{:S(2)}, u32[]{:S(2)}) collective-permute-start(bf16[768,1536]{1,0:T(8,128)(2,1)} %convolution_convert_fusion.1), channel_id=1, source_target_pairs={{0,1},{1,0},{2,3},{3,2},{4,5},{5,4},{6,7},{7,6},{8,9},{9,8},{10,11... | collective-permute-start | bytes 7077896 | tf_op jit(solution)/shard_map/attention_backward/ppermute | solution.py:41
  369.5 17.3 %collective-permute-start.60 = (bf16[128,1536]{1,0:T(8,128)(2,1)S(1)}, bf16[128,1536]{1,0:T(8,128)(2,1)S(1)}, u32[]{:S(2)}, u32[]{:S(2)}) collective-permute-start(bf16[128,1536]{1,0:T(8,128)(2,1)S(1)} %fusion.70), channel_id=1, source_target_pairs={{8,24},{9,25},{10,26},{11,27},{12,28},{13,29},{14,30},{15,31},{16,... | collective-permute-start | bytes 1179656 | tf_op jit(solution)/shard_map/attention_backward/ppermute | solution.py:103
  371.9 15.0 %collective-permute-start.59 = (bf16[128,1536]{1,0:T(8,128)(2,1)S(1)}, bf16[128,1536]{1,0:T(8,128)(2,1)S(1)}, u32[]{:S(2)}, u32[]{:S(2)}) collective-permute-start(bf16[128,1536]{1,0:T(8,128)(2,1)S(1)} %fusion.99), channel_id=1, source_target_pairs={{0,8},{1,9},{2,10},{3,11},{4,12},{5,13},{6,14},{7,15},{24,16},{25,... | collective-permute-start | bytes 1179656 | tf_op jit(solution)/shard_map/attention_backward/ppermute | solution.py:103
  383.9 15.0 %collective-permute-start.58 = (bf16[2,2,48,1536]{3,2,1,0:T(8,128)(2,1)S(1)}, bf16[2,2,48,1536]{3,2,1,0:T(8,128)(2,1)S(1)}, u32[]{:S(2)}, u32[]{:S(2)}) collective-permute-start(bf16[2,2,48,1536]{3,2,1,0:T(8,128)(2,1)S(1)} %get-tuple-element.357), channel_id=1, source_target_pairs={{0,2},{1,3},{2,0},{3,1},{4,6},{5,7},{6,4},{7,5},{8,10},{9,11},{10,... | collective-permute-start | bytes 1769480 | tf_op jit(solution)/shard_map/attention_backward/ppermute | solution.py:41
  384.7 14.7 %collective-permute-start.57 = (bf16[2,2,48,1536]{3,2,1,0:T(8,128)(2,1)S(1)}, bf16[2,2,48,1536]{3,2,1,0:T(8,128)(2,1)S(1)}, u32[]{:S(2)}, u32[]{:S(2)}) collective-permute-start(bf16[2,2,48,1536]{3,2,1,0:T(8,128)(2,1)S(1)} %get-tuple-element.359), channel_id=1, source_target_pairs={{0,4},{1,5},{2,6},{3,7},{4,0},{5,1},{6,2},{7,3},{8,12},{9,13},{10,... | collective-permute-start | bytes 1769480 | tf_op jit(solution)/shard_map/attention_backward/ppermute | solution.py:41
  403.3 11.4 %collective-permute-start.64 = (bf16[128,1536]{1,0:T(8,128)(2,1)S(1)}, bf16[128,1536]{1,0:T(8,128)(2,1)S(1)}, u32[]{:S(2)}, u32[]{:S(2)}) collective-permute-start(bf16[128,1536]{1,0:T(8,128)(2,1)S(1)} %get-tuple-element.350), channel_id=1, source_target_pairs={{8,0},{9,1},{10,2},{11,3},{12,4},{13,5},{14,6},{15,7},{16,8},{17,9... | collective-permute-start | bytes 1179656 | tf_op jit(solution)/shard_map/attention_backward/ppermute | solution.py:103
  418.3 30.5 %collective-permute-start.65 = (bf16[768,3072]{1,0:T(8,128)(2,1)}, bf16[768,3072]{1,0:T(8,128)(2,1)}, u32[]{:S(2)}, u32[]{:S(2)}) collective-permute-start(bf16[768,3072]{1,0:T(8,128)(2,1)} %convolution_convert_fusion), channel_id=1, source_target_pairs={{0,1},{1,0},{2,3},{3,2},{4,5},{5,4},{6,7},{7,6},{8,9},{9,8},{10,11... | collective-permute-start | bytes 14155784 | tf_op jit(solution)/shard_map/q_k_v_weight_gradients/ppermute | solution.py:41
  427.5 21.4 %collective-permute-start.66 = (bf16[4,48,2048]{2,1,0:T(8,128)(2,1)}, bf16[4,48,2048]{2,1,0:T(8,128)(2,1)}, u32[]{:S(2)}, u32[]{:S(2)}) collective-permute-start(bf16[4,48,2048]{2,1,0:T(8,128)(2,1)} %get-tuple-element.339), channel_id=1, source_target_pairs={{0,8},{1,9},{2,10},{3,11},{4,12},{5,13},{6,14},{7,15},{24,16},{25,... | collective-permute-start | bytes 2359304 | tf_op jit(solution)/shard_map/attention_backward/ppermute | solution.py:103
  431.6 34.2 %collective-permute-start.69 = (bf16[4,48,2048]{2,1,0:T(8,128)(2,1)}, bf16[4,48,2048]{2,1,0:T(8,128)(2,1)}, u32[]{:S(2)}, u32[]{:S(2)}) collective-permute-start(bf16[4,48,2048]{2,1,0:T(8,128)(2,1)} %get-tuple-element.338), channel_id=1, source_target_pairs={{0,8},{1,9},{2,10},{3,11},{4,12},{5,13},{6,14},{7,15},{24,16},{25,... | collective-permute-start | bytes 2359304 | tf_op jit(solution)/shard_map/q_k_v_weight_gradients/ppermute | solution.py:103
  443.8 24.5 %collective-permute-start.71 = (f32[2,1536]{1,0:T(2,128)S(1)}, f32[2,1536]{1,0:T(2,128)S(1)}, u32[]{:S(2)}, u32[]{:S(2)}) collective-permute-start(f32[2,1536]{1,0:T(2,128)S(1)} %pad_maximum_fusion.33), channel_id=1, source_target_pairs={{0,1},{1,0},{2,3},{3,2},{4,5},{5,4},{6,7},{7,6},{8,9},{9,8},{10,11... | collective-permute-start | bytes 36872 | tf_op jit(solution)/shard_map/input_gradient/ppermute | solution.py:41
  457.6 35.1 %collective-permute-start.68 = (bf16[2,2,48,3072]{3,2,1,0:T(8,128)(2,1)S(1)}, bf16[2,2,48,3072]{3,2,1,0:T(8,128)(2,1)S(1)}, u32[]{:S(2)}, u32[]{:S(2)}) collective-permute-start(bf16[2,2,48,3072]{3,2,1,0:T(8,128)(2,1)S(1)} %get-tuple-element.343), channel_id=1, source_target_pairs={{0,2},{1,3},{2,0},{3,1},{4,6},{5,7},{6,4},{7,5},{8,10},{9,11},{10,... | collective-permute-start | bytes 3538952 | tf_op jit(solution)/shard_map/q_k_v_weight_gradients/ppermute | solution.py:41
  460.1 32.5 %collective-permute-start.67 = (bf16[2,2,48,3072]{3,2,1,0:T(8,128)(2,1)S(1)}, bf16[2,2,48,3072]{3,2,1,0:T(8,128)(2,1)S(1)}, u32[]{:S(2)}, u32[]{:S(2)}) collective-permute-start(bf16[2,2,48,3072]{3,2,1,0:T(8,128)(2,1)S(1)} %get-tuple-element.344), channel_id=1, source_target_pairs={{0,4},{1,5},{2,6},{3,7},{4,0},{5,1},{6,2},{7,3},{8,12},{9,13},{10,... | collective-permute-start | bytes 3538952 | tf_op jit(solution)/shard_map/q_k_v_weight_gradients/ppermute | solution.py:41
  462.9 29.7 %collective-permute-start.70 = (bf16[4,48,2048]{2,1,0:T(8,128)(2,1)S(1)}, bf16[4,48,2048]{2,1,0:T(8,128)(2,1)S(1)}, u32[]{:S(2)}, u32[]{:S(2)}) collective-permute-start(bf16[4,48,2048]{2,1,0:T(8,128)(2,1)S(1)} %fusion.48), channel_id=1, source_target_pairs={{8,24},{9,25},{10,26},{11,27},{12,28},{13,29},{14,30},{15,31},{16,... | collective-permute-start | bytes 2359304 | tf_op jit(solution)/shard_map/q_k_v_weight_gradients/ppermute | solution.py:103
  465.8 35.0 %collective-permute-start.80 = (bf16[48,1536]{1,0:T(8,128)(2,1)S(1)}, bf16[48,1536]{1,0:T(8,128)(2,1)S(1)}, u32[]{:S(2)}, u32[]{:S(2)}) collective-permute-start(bf16[48,1536]{1,0:T(8,128)(2,1)S(1)} %get-tuple-element.394), channel_id=1, source_target_pairs={{0,24},{1,25},{2,26},{3,27},{4,28},{5,29},{6,30},{7,31},{8,16},{9,... | collective-permute-start | bytes 442376 | tf_op jit(solution)/shard_map/weight_gradients_to_owners/ppermute | solution.py:41
  468.3 33.4 %collective-permute-start.81 = (bf16[48,1536]{1,0:T(8,128)(2,1)S(1)}, bf16[48,1536]{1,0:T(8,128)(2,1)S(1)}, u32[]{:S(2)}, u32[]{:S(2)}) collective-permute-start(bf16[48,1536]{1,0:T(8,128)(2,1)S(1)} %get-tuple-element.395), channel_id=1, source_target_pairs={{0,16},{1,17},{2,18},{3,19},{4,20},{5,21},{6,22},{7,23},{8,24},{9,... | collective-permute-start | bytes 442376 | tf_op jit(solution)/shard_map/weight_gradients_to_owners/ppermute | solution.py:41
  492.6 12.3 %collective-permute-start.82 = (bf16[48,1536]{1,0:T(8,128)(2,1)S(1)}, bf16[48,1536]{1,0:T(8,128)(2,1)S(1)}, u32[]{:S(2)}, u32[]{:S(2)}) collective-permute-start(bf16[48,1536]{1,0:T(8,128)(2,1)S(1)} %get-tuple-element.396), channel_id=1, source_target_pairs={{0,8},{1,9},{2,10},{3,11},{4,12},{5,13},{6,14},{7,15},{8,0},{9,1},... | collective-permute-start | bytes 442376 | tf_op jit(solution)/shard_map/weight_gradients_to_owners/ppermute | solution.py:41
  495.0 20.5 %collective-permute-start.74 = (bf16[4,48,2048]{2,1,0:T(8,128)(2,1)S(1)}, bf16[4,48,2048]{2,1,0:T(8,128)(2,1)S(1)}, u32[]{:S(2)}, u32[]{:S(2)}) collective-permute-start(bf16[4,48,2048]{2,1,0:T(8,128)(2,1)S(1)} %get-tuple-element.337), channel_id=1, source_target_pairs={{0,8},{1,9},{2,10},{3,11},{4,12},{5,13},{6,14},{7,15},{8,16},{9,17... | collective-permute-start | bytes 2359304 | tf_op jit(solution)/shard_map/weight_gradients_to_owners/ppermute | solution.py:103
  498.9 16.5 %collective-permute-start.75 = (bf16[4,48,2048]{2,1,0:T(8,128)(2,1)S(1)}, bf16[4,48,2048]{2,1,0:T(8,128)(2,1)S(1)}, u32[]{:S(2)}, u32[]{:S(2)}) collective-permute-start(bf16[4,48,2048]{2,1,0:T(8,128)(2,1)S(1)} %get-tuple-element.336), channel_id=1, source_target_pairs={{8,0},{9,1},{10,2},{11,3},{12,4},{13,5},{14,6},{15,7},{16,8},{17,9... | collective-permute-start | bytes 2359304 | tf_op jit(solution)/shard_map/weight_gradients_to_owners/ppermute | solution.py:103
  500.8 14.6 %collective-permute-start.73 = (bf16[2,48,3072]{2,1,0:T(8,128)(2,1)S(1)}, bf16[2,48,3072]{2,1,0:T(8,128)(2,1)S(1)}, u32[]{:S(2)}, u32[]{:S(2)}) collective-permute-start(bf16[2,48,3072]{2,1,0:T(8,128)(2,1)S(1)} %fusion.80), channel_id=1, source_target_pairs={{0,4},{1,5},{2,6},{3,7},{4,0},{5,1},{6,2},{7,3},{8,12},{9,13},{10,... | collective-permute-start | bytes 1769480 | tf_op jit(solution)/shard_map/weight_gradients_to_owners/ppermute | solution.py:41
  501.7 13.7 %collective-permute-start.72 = (bf16[2,48,3072]{2,1,0:T(8,128)(2,1)S(1)}, bf16[2,48,3072]{2,1,0:T(8,128)(2,1)S(1)}, u32[]{:S(2)}, u32[]{:S(2)}) collective-permute-start(bf16[2,48,3072]{2,1,0:T(8,128)(2,1)S(1)} %fusion.79), channel_id=1, source_target_pairs={{0,2},{1,3},{2,0},{3,1},{4,6},{5,7},{6,4},{7,5},{8,10},{9,11},{10,... | collective-permute-start | bytes 1769480 | tf_op jit(solution)/shard_map/weight_gradients_to_owners/ppermute | solution.py:41
  525.4 11.5 %collective-permute-start.77 = (bf16[48,3072]{1,0:T(8,128)(2,1)S(1)}, bf16[48,3072]{1,0:T(8,128)(2,1)S(1)}, u32[]{:S(2)}, u32[]{:S(2)}) collective-permute-start(bf16[48,3072]{1,0:T(8,128)(2,1)S(1)} %get-tuple-element.369), channel_id=1, source_target_pairs={{0,24},{1,25},{2,26},{3,27},{4,28},{5,29},{6,30},{7,31},{8,16},{9,... | collective-permute-start | bytes 884744 | tf_op jit(solution)/shard_map/weight_gradients_to_owners/ppermute | solution.py:41
  528.8 19.8 %collective-permute-start.78 = (bf16[48,3072]{1,0:T(8,128)(2,1)S(1)}, bf16[48,3072]{1,0:T(8,128)(2,1)S(1)}, u32[]{:S(2)}, u32[]{:S(2)}) collective-permute-start(bf16[48,3072]{1,0:T(8,128)(2,1)S(1)} %get-tuple-element.370), channel_id=1, source_target_pairs={{0,16},{1,17},{2,18},{3,19},{4,20},{5,21},{6,22},{7,23},{8,24},{9,... | collective-permute-start | bytes 884744 | tf_op jit(solution)/shard_map/weight_gradients_to_owners/ppermute | solution.py:41
  529.5 19.1 %collective-permute-start.79 = (bf16[48,3072]{1,0:T(8,128)(2,1)S(1)}, bf16[48,3072]{1,0:T(8,128)(2,1)S(1)}, u32[]{:S(2)}, u32[]{:S(2)}) collective-permute-start(bf16[48,3072]{1,0:T(8,128)(2,1)S(1)} %get-tuple-element.371), channel_id=1, source_target_pairs={{0,8},{1,9},{2,10},{3,11},{4,12},{5,13},{6,14},{7,15},{8,0},{9,1},... | collective-permute-start | bytes 884744 | tf_op jit(solution)/shard_map/weight_gradients_to_owners/ppermute | solution.py:41
  (129 other events, 985.4 us)

commit v6 on v5

v6 whole, which is shorter than its diff:
```python
import math

import jax
import jax.numpy as jnp
from jax import lax
from jax.experimental import pallas as pl
from jax.experimental.pallas import tpu as pltpu
from jax.sharding import PartitionSpec as P

HEAD_SIZE = 96
SEQ = 128
EPSILON = 1e-05
ROPE_BASE = 100000.0
MASK_FILL = -1e30
LANES = 128

BF = jnp.bfloat16
F32 = jnp.float32
NO_COST = pl.CostEstimate(flops=1, bytes_accessed=1, transcendentals=0)


def dot(a, b, dims):
    return lax.dot_general(a, b, (dims, ((), ())), preferred_element_type=F32)


def mm(a, b):
    return dot(a, b, ((1,), (0,)))


def mm_t(a, b):
    return dot(a, b, ((1,), (1,)))


def t_mm(a, b):
    return dot(a, b, ((0,), (0,)))


def swap(value, mask):
    n = lax.axis_size("dp")
    return lax.ppermute(value, "dp", [(i, i ^ mask) for i in range(n)])


def column_groups(with_core):
    n = lax.axis_size("dp")
    planes = range(n // 8)
    if with_core:
        return [[8 * z + 2 * p + c for z in planes for c in range(2)] for p in range(4)]
    return [[8 * z + 2 * p + c for z in planes] for p in range(4) for c in range(2)]


def z_reduce(parts):
    total = sum(part.astype(F32) for part in parts)
    return lax.psum_scatter(
        total.astype(BF), "dp", axis_index_groups=column_groups(False), scatter_dimension=0
    ).astype(F32)


def summed(parts, index, axis):
    total = pick(parts[0], index, axis).astype(F32)
    for part in parts[1:]:
        total = total + pick(part, index, axis).astype(F32)
    return total


def owned(parts, came, z):
    own = summed(parts, z, 0)
    for piece in came:
        own = own + piece.astype(F32)
    return own


def direct(parts, z):
    return [swap(summed(parts, z ^ k, 0).astype(BF), 8 * k) for k in (3, 2, 1)]


def along_z(value, pairs):
    return lax.ppermute(
        value, "dp", [(8 * a + i, 8 * b + i) for a, b in pairs for i in range(8)]
    )


def tied(*values):
    return lax.optimization_barrier(values)


def place(out, piece, where):
    return lax.dynamic_update_slice(out, piece, where)


def pick(parts, index, axis):
    return lax.dynamic_index_in_dim(parts, index, axis, keepdims=False)


def column_cuts(w_gate, w_up, p, part):
    rows = w_gate.shape[0]
    gate_cut = w_gate.reshape(rows, -1, 4, part)
    up_cut = w_up.reshape(rows, -1, 4, part)
    cuts = []
    for r in range(4):
        gate = pick(gate_cut, p ^ r, 2).reshape(rows, -1)
        up = pick(up_cut, p ^ r, 2).reshape(rows, -1)
        cuts.append(jnp.concatenate([gate, up], axis=1))
    return cuts


def by_source(came, p):
    out = jnp.zeros((4,) + came[0].shape, BF)
    for r in range(4):
        out = place(out, came[r][None], (p ^ r, 0, 0))
    return out


def along_column(value):
    return lax.all_gather(
        value, "dp", axis_index_groups=column_groups(True), axis=0, tiled=True
    )


def sum_to_owners(partial):
    return lax.psum_scatter(
        partial, "dp", axis_index_groups=column_groups(True), scatter_dimension=0, tiled=True
    )


def gather_weights_plainly(local, w_gate, w_up, w_down, p):
    gathered = lax.all_gather(local, "dp", axis=0, tiled=True)
    cuts = column_cuts(w_gate, w_up, p, 2 * w_down.shape[0])
    came = [cuts[0]] + [swap(cuts[r], r << 1) for r in (1, 2, 3)]
    mine = by_source(came, p)
    wb = along_column(mine.reshape(-1, mine.shape[2]))
    return gathered, wb, along_column(w_down)


def merged(came, w_down, p):
    rows, columns = came[0].shape
    ff_rows, width = w_down.shape
    tall = 4 * rows
    side = width * ff_rows // tall
    rest = width - side
    low = tall - ff_rows

    def kernel(p_ref, *refs):
        wd, out = refs[4:]
        for r in range(4):
            start = pl.multiple_of((p_ref[0] ^ r) * rows, 16)
            out[pl.ds(start, rows), :columns] = refs[r][...]
        out[:ff_rows, columns:] = wd[:, :side]
        for k in range(ff_rows // low):
            at = columns + k * rest
            out[ff_rows:, at : at + rest] = wd[k * low : (k + 1) * low, side:]

    return pl.pallas_call(
        kernel,
        out_shape=jax.ShapeDtypeStruct((tall, columns + side), w_down.dtype),
        in_specs=[pl.BlockSpec(memory_space=pltpu.SMEM)]
        + [pl.BlockSpec(memory_space=pltpu.VMEM)] * 5,
        cost_estimate=NO_COST,
        name="merged",
    )(p[None], *came, w_down)


def w_down_from(whole, ff_rows, columns, width):
    side = whole.shape[1] - columns
    rest = width - side
    tall = width * ff_rows // side
    low = tall - ff_rows
    devices = whole.shape[0] // tall

    def kernel(ref, out, sem):
        copies = []
        for i in range(devices):
            top, to = i * tall, i * ff_rows
            pairs = [
                (
                    ref.at[pl.ds(top, ff_rows), pl.ds(columns, side)],
                    out.at[pl.ds(to, ff_rows), pl.ds(0, side)],
                )
            ]
            for k in range(ff_rows // low):
                pairs.append(
                    (
                        ref.at[pl.ds(top + ff_rows, low), pl.ds(columns + k * rest, rest)],
                        out.at[pl.ds(to + k * low, low), pl.ds(side, rest)],
                    )
                )
            for k, (source, target) in enumerate(pairs):
                copies.append(pltpu.make_async_copy(source, target, sem.at[i, k]))
        for copy in copies:
            copy.start()
        for copy in copies:
            copy.wait()

    return pl.pallas_call(
        kernel,
        out_shape=jax.ShapeDtypeStruct((devices * ff_rows, width), whole.dtype),
        in_specs=[pl.BlockSpec(memory_space=pl.ANY)],
        out_specs=pl.BlockSpec(memory_space=pltpu.VMEM),
        scratch_shapes=[pltpu.SemaphoreType.DMA((devices, 1 + ff_rows // low))],
        cost_estimate=NO_COST,
        name="w_down_from",
    )(whole)


def unset(shape, dtype):
    return pl.pallas_call(
        lambda out: None,
        out_shape=jax.ShapeDtypeStruct(shape, dtype),
        out_specs=pl.BlockSpec(memory_space=pl.ANY),
        name="unset",
    )()


def packed(pieces):
    widths = [piece.shape[1] for piece in pieces]
    rows = pieces[0].shape[0]

    def kernel(*refs):
        out = refs[-1]
        at = 0
        for ref, size in zip(refs[:-1], widths):
            out[:, at : at + size] = ref[...]
            at += size

    return pl.pallas_call(
        kernel,
        out_shape=jax.ShapeDtypeStruct((rows, sum(widths)), pieces[0].dtype),
        name="packed",
    )(*pieces)


def column_cuts_kernel(w_gate, w_up, p, part):
    rows, ff = w_gate.shape
    planes = ff // (4 * part)
    units = planes * part

    def kernel(p_ref, gate, up, *outs):
        for r, out in enumerate(outs):
            q = p_ref[0] ^ r
            for k in range(planes):
                start = pl.multiple_of((4 * k + q) * part, LANES)
                out[:, k * part : (k + 1) * part] = gate[:, pl.ds(start, part)]
                out[:, units + k * part : units + (k + 1) * part] = up[:, pl.ds(start, part)]

    shape = jax.ShapeDtypeStruct((rows, 2 * units), w_gate.dtype)
    return pl.pallas_call(
        kernel,
        out_shape=[shape] * 4,
        in_specs=[pl.BlockSpec(memory_space=pltpu.SMEM)]
        + [pl.BlockSpec(memory_space=pltpu.VMEM)] * 2,
        name="column_cuts",
    )(p[None], w_gate, w_up)


def gather_weights(local, w_gate, w_up, w_down, place_bits):
    z, y, x, c = place_bits
    p = 2 * y + x
    rows, columns = local.shape
    ff_rows, width = w_down.shape
    end = (z == 0) | (z == 3)
    up_pairs = [(0, 1), (1, 2), (2, 3)]
    down_pairs = [(1, 0), (2, 1), (3, 2)]
    far_pairs = [(0, 2), (3, 1)]
    out_pairs = [(1, 0), (2, 3)]
    z_b = jnp.where(z == 0, 1, z - 1)
    z_c = jnp.where(z < 2, 2, jnp.where(z == 2, 3, 1))
    z_d = jnp.where(z < 2, 3, 0)
    out = unset((4, 2, 2, 2, rows, columns), BF)

    def near_side(up, down):
        return jnp.where(z == 0, down, up)

    def to_pass_on(up, down):
        return jnp.where(z == 1, down, up)

    def put_x(out, piece, z_k, at_y, core):
        return place(out, piece[None, None, :, None], (z_k, at_y, 0, core, 0, 0))

    def put_y(out, piece, z_k, at_x, core):
        return place(out, piece[None, :, None, None], (z_k, 0, at_x, core, 0, 0))

    def in_order(bit, mine, theirs):
        return jnp.stack([jnp.where(bit == 0, mine, theirs), jnp.where(bit == 0, theirs, mine)])

    def put(out, pair, z_a, z_b, at_y, at_x, core):
        out = put_x(out, pair[0], z_a, at_y, core)
        return put_y(out, pair[1], z_b, at_x, core)

    with jax.named_scope("phase_0"):
        cuts = column_cuts_kernel(w_gate, w_up, p, 2 * ff_rows)
        up, down, came_x, came_y, came_xy = tied(
            along_z(local, up_pairs),
            along_z(local, down_pairs),
            swap(cuts[1], 2),
            swap(cuts[2], 4),
            swap(cuts[3], 6),
        )
    with jax.named_scope("phase_1"):
        b = near_side(up, down)
        a, b, passing = tied(local, b, to_pass_on(up, down))
        a_x, b_y, far, first = tied(
            swap(a, 2), swap(b, 4), along_z(a, far_pairs), along_z(passing, out_pairs)
        )
        ffn = merged((cuts[0], came_x, came_y, came_xy), w_down, p)
    with jax.named_scope("phase_2"):
        a2, b2, far = tied(in_order(x, a, a_x), in_order(y, b, b_y), far)
        near_1 = jnp.stack([a2, b2])
        a_far, b_far, second = tied(swap(a2, 4), swap(b2, 2), along_z(far, out_pairs))
        out = put(out, near_1, z, z_b, y, x, c)
    with jax.named_scope("ffn_weights"):
        ffn = along_column(tied(ffn, second)[0])
    with jax.named_scope("phase_3"):
        a, b = jnp.where(end, first, down), jnp.where(end, second, far)
        a, b, near_1 = tied(a, b, near_1)
        a_x, b_y, core_1 = tied(swap(a, 2), swap(b, 4), swap(near_1, 1))
        far_1 = jnp.stack([a_far, b_far])
        out = put(out, far_1, z, z_b, 1 - y, 1 - x, c)
    with jax.named_scope("phase_4"):
        a2, b2, far_1 = tied(in_order(x, a, a_x), in_order(y, b, b_y), far_1)
        a_far, b_far, core_2 = tied(swap(a2, 4), swap(b2, 2), swap(far_1, 1))
        out = put(out, core_1, z, z_b, y, x, 1 - c)
        near_2 = jnp.stack([a2, b2])
        out = put(out, near_2, z_c, z_d, y, x, c)
    with jax.named_scope("phase_5"):
        near_2, far_2 = tied(near_2, jnp.stack([a_far, b_far]))
        core_3, core_4 = tied(swap(near_2, 1), swap(far_2, 1))
        out = put(out, core_2, z, z_b, 1 - y, 1 - x, 1 - c)
        out = put(out, far_2, z_c, z_d, 1 - y, 1 - x, c)
        out = put(out, core_3, z_c, z_d, y, x, 1 - c)
        out = put(out, core_4, z_c, z_d, 1 - y, 1 - x, 1 - c)
        gathered = out.reshape(32 * rows, columns)
    return gathered, ffn


def halves(parts):
    half = parts[0].shape[2] // 2
    return [part[:, :, :half] for part in parts], [part[:, :, half:] for part in parts]


def plane_step_1(parts, place_bits):
    z, y, x, c = place_bits
    a, b = halves(parts)
    return (swap(summed(a, 1 - y, 1).astype(BF), 4), swap(summed(b, 1 - x, 0).astype(BF), 2))


def plane_step_2(parts, came, place_bits):
    z, y, x, c = place_bits
    a, b = halves(parts)
    a = [summed(a, y, 1), came[0]]
    b = [summed(b, x, 0), came[1]]
    moving = (swap(summed(a, 1 - x, 0).astype(BF), 2), swap(summed(b, 1 - y, 0).astype(BF), 4))
    return (a, b), moving


def plane_step_3(sums, came, place_bits):
    z, y, x, c = place_bits
    a = summed(sums[0], x, 0) + came[0].astype(F32)
    b = summed(sums[1], y, 0) + came[1].astype(F32)
    return jnp.concatenate([a, b])


def reordered(count, rows, order):
    place_of, row = jnp.arange(count) // rows, jnp.arange(count) % rows
    planes = count // rows // 8
    if order == "cxyz":
        core, chip = place_of // (4 * planes), place_of % (4 * planes)
        x, y, z = chip // (2 * planes), chip // planes % 2, chip % planes
    else:
        z, core, y, x = place_of // 8, place_of // 4 % 2, place_of // 2 % 2, place_of % 2
    source = (8 * z + 4 * y + 2 * x + core) * rows + row
    return (jnp.arange(count)[:, None] == source[None, :]).astype(BF)


def core_halves(values, c):
    width = values.shape[1] // 2
    return (
        lax.dynamic_slice_in_dim(values, c * width, width, 1),
        lax.dynamic_slice_in_dim(values, (1 - c) * width, width, 1),
    )


def split_gather(rows, beside=(), then=lambda pieces, *values: values):
    half = rows.shape[0] // 2
    a, b = rows[:half], rows[half:]
    a_x, b_y, *beside = tied(swap(a, 2), swap(b, 4), *beside)
    a2, b2 = tied(jnp.concatenate([a, a_x]), jnp.concatenate([b, b_y]))
    a_far, b_far, *beside = tied(swap(a2, 4), swap(b2, 2), *then((a2, b2), *beside))
    return (jnp.concatenate([a_far, b_far]), *beside)


def split_reduce(near, low, beside=(), later=lambda *values: values):
    two = low.shape[0] // 2
    one = two // 2
    came_a, came_b, *beside = tied(swap(low[:two], 4), swap(low[two:], 2), *beside)
    a = near[:two] + came_a.astype(F32)
    b = near[two:] + came_b.astype(F32)
    came_a, came_b, *beside = tied(
        swap(a[one:].astype(BF), 2), swap(b[one:].astype(BF), 4), *later(*beside)
    )
    own = jnp.concatenate([a[:one] + came_a.astype(F32), b[:one] + came_b.astype(F32)])
    return (own, *beside)


def spread_columns(came, p, part):
    units = came[0].shape[1] // 2
    natural = []
    for q in range(4):
        piece = came[3]
        for r in (0, 1, 2):
            piece = jnp.where(p == (q ^ r), came[r], piece)
        natural.append(piece.astype(F32))
    return tuple(
        jnp.concatenate(
            [
                natural[q][:, start + k * part : start + (k + 1) * part]
                for k in range(units // part)
                for q in range(4)
            ],
            axis=1,
        )
        for start in (0, units)
    )


def rotation_tables(length, width):
    half_width = width // 2
    position = jnp.arange(length, dtype=F32)[:, None]
    freq_rate = ROPE_BASE ** (-2.0 * jnp.arange(half_width, dtype=F32) / width)
    angle_table = position * freq_rate[None, :]
    return (jnp.cos(angle_table)[:, None, :], jnp.sin(angle_table)[:, None, :])


HEADS_AT_ONCE = 8


def rotation_lanes():
    cosine, sine = rotation_tables(SEQ, HEAD_SIZE)
    lanes = HEADS_AT_ONCE * 2
    return (jnp.tile(cosine[:, 0], (1, lanes)), jnp.tile(sine[:, 0], (1, lanes)))


def turned(value, cosine, sine, back):
    size = value.shape[1]
    half = HEAD_SIZE // 2
    lane = lax.broadcasted_iota(jnp.int32, value.shape, 1)
    right = pltpu.roll(value, size - half, 1)
    left = pltpu.roll(value, half, 1)
    first = lane % HEAD_SIZE < half
    other = jnp.where(first, right, -left) if back else jnp.where(first, -right, left)
    return value * cosine + other * sine


def head_of(value, i):
    size = value.shape[1]
    period = 3 * LANES
    group = value[:, i // 4 * period : (i // 4 + 1) * period]
    if i % 4:
        group = pltpu.roll(group, period - i % 4 * HEAD_SIZE, 1)
    head = group[:, :LANES]
    lane = lax.broadcasted_iota(jnp.int32, head.shape, 1)
    return jnp.where(lane < HEAD_SIZE, head, 0.0)


def side_by_side(heads):
    rows = heads[0].shape[0]
    total = None
    for i, head in enumerate(heads):
        wide = jnp.concatenate([head, jnp.zeros((rows, 2 * LANES), head.dtype)], axis=1)
        if i:
            wide = pltpu.roll(wide, i * HEAD_SIZE, 1)
        total = wide if total is None else total + wide
    return total


def row_softmax(query, key):
    scores = lax.dot_general(
        query, key, (((1,), (1,)), ((), ())), preferred_element_type=F32
    ) * (1.0 / math.sqrt(HEAD_SIZE))
    row = lax.broadcasted_iota(jnp.int32, scores.shape, 0)
    column = lax.broadcasted_iota(jnp.int32, scores.shape, 1)
    scores = jnp.where(row >= column, scores, MASK_FILL)
    weights = jnp.exp(scores - jnp.max(scores, axis=1, keepdims=True))
    return weights * (1.0 / jnp.sum(weights, axis=1, keepdims=True))


def attention_blocks(width, kv_width):
    q_size = HEADS_AT_ONCE * HEAD_SIZE
    kv_size = q_size * kv_width // width
    return q_size, kv_size


def attention_forward(raw, cosine, sine, width, kv_width):
    count = raw.shape[0]
    q_size, kv_size = attention_blocks(width, kv_width)
    steps = width // q_size
    per_kv = width // kv_width

    def kernel(q_raw, k_raw, v_raw, cosine, sine, q_out, k_out, v_out, mixed):
        q = turned(q_raw[...], cosine[...], sine[...], False).astype(BF)
        k = turned(k_raw[...], cosine[:, :kv_size], sine[:, :kv_size], False).astype(BF)
        v = v_raw[...].astype(BF)
        q_out[...] = q
        k_out[...] = k
        v_out[...] = v
        q, k, v = q.astype(F32), k.astype(F32), v.astype(F32)
        for group in range(HEADS_AT_ONCE // 4):
            outs = []
            for i in range(4 * group, 4 * group + 4):
                if i % per_kv == 0:
                    key = head_of(k, i // per_kv).astype(BF)
                    value = head_of(v, i // per_kv).astype(BF)
                probs = row_softmax(head_of(q, i).astype(BF), key)
                outs.append(jnp.dot(probs.astype(BF), value, preferred_element_type=F32))
            mixed[:, 384 * group : 384 * group + 384] = side_by_side(outs).astype(BF)

    def block(size, at):
        return pl.BlockSpec((SEQ, size), lambda s, j: (s, at // size + j))

    table = pl.BlockSpec((SEQ, q_size), lambda s, j: (0, 0))
    return pl.pallas_call(
        kernel,
        grid=(count // SEQ, steps),
        out_shape=[
            jax.ShapeDtypeStruct((count, width), BF),
            jax.ShapeDtypeStruct((count, kv_width), BF),
            jax.ShapeDtypeStruct((count, kv_width), BF),
            jax.ShapeDtypeStruct((count, width), BF),
        ],
        in_specs=[
            block(q_size, 0),
            block(kv_size, width),
            block(kv_size, width + kv_width),
            table,
            table,
        ],
        out_specs=[block(q_size, 0), block(kv_size, 0), block(kv_size, 0), block(q_size, 0)],
        cost_estimate=NO_COST,
        name="attention_forward",
    )(raw, raw, raw, cosine, sine)


def attention_backward(grad_mixed, q, k, v, cosine, sine):
    count, width = q.shape
    kv_width = k.shape[1]
    q_size, kv_size = attention_blocks(width, kv_width)
    steps = width // q_size
    per_kv = width // kv_width
    scale = 1.0 / math.sqrt(HEAD_SIZE)
    rows_rows = (((0,), (0,)), ((), ()))
    lanes_lanes = (((1,), (1,)), ((), ()))

    def kernel(d_ref, q_ref, k_ref, v_ref, cosine, sine, out):
        d, q = d_ref[...].astype(F32), q_ref[...].astype(F32)
        k, v = k_ref[...].astype(F32), v_ref[...].astype(F32)
        d_q, d_k, d_v = [], [], []
        for i in range(HEADS_AT_ONCE):
            if i % per_kv == 0:
                key = head_of(k, i // per_kv).astype(BF)
                value = head_of(v, i // per_kv).astype(BF)
            query, upstream = head_of(q, i).astype(BF), head_of(d, i).astype(BF)
            probs = row_softmax(query, key)
            d_probs = lax.dot_general(upstream, value, lanes_lanes, preferred_element_type=F32)
            d_scores = probs * (d_probs - jnp.sum(probs * d_probs, axis=1, keepdims=True))
            d_scores = d_scores.astype(BF)
            d_q.append(jnp.dot(d_scores, key, preferred_element_type=F32) * scale)
            part_k = lax.dot_general(d_scores, query, rows_rows, preferred_element_type=F32)
            part_v = lax.dot_general(
                probs.astype(BF), upstream, rows_rows, preferred_element_type=F32
            )
            if i % per_kv == 0:
                d_k.append(part_k)
                d_v.append(part_v)
            else:
                d_k[-1] += part_k
                d_v[-1] += part_v
        d_q = jnp.concatenate([side_by_side(d_q[g : g + 4]) for g in range(0, len(d_q), 4)], axis=1)
        d_q = turned(d_q, cosine[...], sine[...], True).astype(BF)
        d_k = side_by_side([part * scale for part in d_k])
        d_k = turned(d_k, cosine[:, :kv_size], sine[:, :kv_size], True).astype(BF)
        j = pl.program_id(1)
        out[:, pl.ds(pl.multiple_of(j * q_size, LANES), q_size)] = d_q
        at = pl.multiple_of(width + j * kv_size, LANES)
        out[:, pl.ds(at, kv_size)] = d_k
        at = pl.multiple_of(width + kv_width + j * kv_size, LANES)
        out[:, pl.ds(at, kv_size)] = side_by_side(d_v).astype(BF)

    def block(size):
        return pl.BlockSpec((SEQ, size), lambda s, j: (s, j))

    table = pl.BlockSpec((SEQ, q_size), lambda s, j: (0, 0))
    return pl.pallas_call(
        kernel,
        grid=(count // SEQ, steps),
        out_shape=jax.ShapeDtypeStruct((count, width + 2 * kv_width), BF),
        in_specs=[block(q_size), block(q_size), block(kv_size), block(kv_size), table, table],
        out_specs=pl.BlockSpec((SEQ, width + 2 * kv_width), lambda s, j: (s, 0)),
        cost_estimate=NO_COST,
        name="attention_backward",
    )(grad_mixed, q, k, v, cosine, sine)


def norm_rows(field_in, gain_vec):
    inv_scale = lax.rsqrt(jnp.mean(field_in * field_in, axis=-1, keepdims=True) + EPSILON)
    return (field_in * inv_scale * gain_vec, inv_scale)


def norm_back(upstream, field_in, inv_scale, gain_vec):
    gain_grad = jnp.sum(upstream * field_in * inv_scale, axis=0)
    scaled_up = upstream * gain_vec
    field_grad = inv_scale * scaled_up - field_in * inv_scale**3 * jnp.mean(
        scaled_up * field_in, axis=-1, keepdims=True
    )
    return (gain_grad, field_grad)


def ffn_forward(rows, w_both, w_down):
    units = w_down.shape[0]
    pre = mm(rows, w_both[:, : 2 * units])
    hidden = (jax.nn.silu(pre[:, :units]) * pre[:, units:]).astype(BF)
    return (mm(hidden, w_down), pre, hidden)


def ffn_backward(grad_low, pre, w_both, w_down):
    grad_hidden = mm_t(grad_low, w_down)
    units = w_down.shape[0]
    gate_pre, up_pre = pre[:, :units], pre[:, units:]
    gate_sigmoid = jax.nn.sigmoid(gate_pre)
    grad_gate = grad_hidden * up_pre * gate_sigmoid * (1.0 + gate_pre * (1.0 - gate_sigmoid))
    grad_up = grad_hidden * gate_pre * gate_sigmoid
    grads = jnp.concatenate([grad_gate.astype(BF), grad_up.astype(BF)], axis=1)
    return (mm_t(grads, w_both[:, : 2 * units]), grads)


FFN_TILE = 256
FFN_VMEM = 48 * 2**20


def tiles_of(w_both, w_down, units):
    width = w_down.shape[1]
    steps = units // FFN_TILE
    return [
        pl.BlockSpec((width, FFN_TILE), lambda j: (0, j)),
        pl.BlockSpec((width, FFN_TILE), lambda j: (0, j + steps)),
        pl.BlockSpec((FFN_TILE, width), lambda j: (j, 0)),
    ]


def whole(array):
    return pl.BlockSpec(array.shape, lambda j: (0,) * array.ndim)


def sigmoid(value):
    return 1.0 / (1.0 + jnp.exp(-value))


def ffn_forward_beside(pieces, w_both, w_down):
    units, width = w_down.shape
    steps = units // FFN_TILE
    sizes = [piece.shape[0] for piece in pieces]
    count = sum(sizes)
    kinds = ((width, BF), (units, BF), (units, F32), (units, F32))
    kept_specs = [
        pl.BlockSpec((count, width), lambda j: (0, 0)),
        pl.BlockSpec((count, FFN_TILE), lambda j: (0, j)),
        pl.BlockSpec((count, FFN_TILE), lambda j: (0, j)),
        pl.BlockSpec((count, FFN_TILE), lambda j: (0, j)),
    ]
    first = len(pieces) + 3

    def kernel(*refs):
        w_gate, w_up, w_low = refs[len(pieces) : first]
        y, rows, hidden, gate, up, total = refs[-6:]
        j = pl.program_id(0)

        @pl.when(j == 0)
        def _():
            at = 0
            for ref, size in zip(refs, sizes):
                rows[at : at + size] = ref[...]
                at += size

        gate_pre = jnp.dot(rows[...], w_gate[...], preferred_element_type=F32)
        up_pre = jnp.dot(rows[...], w_up[...], preferred_element_type=F32)
        gate[...] = gate_pre
        up[...] = up_pre
        hid = (gate_pre * sigmoid(gate_pre) * up_pre).astype(BF)
        hidden[...] = hid
        part = jnp.dot(hid, w_low[...], preferred_element_type=F32)

        @pl.when(j == 0)
        def _():
            total[...] = part

        @pl.when(j > 0)
        def _():
            total[...] += part

        @pl.when(j == steps - 1)
        def _():
            y[...] = total[...].astype(y.dtype)

    y_shape = jax.ShapeDtypeStruct((count, width), F32)
    outs = pl.pallas_call(
        kernel,
        grid=(steps,),
        out_shape=[y_shape] + [jax.ShapeDtypeStruct((count, w), t) for w, t in kinds],
        in_specs=[whole(piece) for piece in pieces]
        + tiles_of(w_both, w_down, units),
        out_specs=[whole(y_shape)] + kept_specs,
        scratch_shapes=[pltpu.VMEM((count, width), F32)],
        compiler_params=pltpu.CompilerParams(vmem_limit_bytes=FFN_VMEM),
        cost_estimate=NO_COST,
        name="ffn_forward_beside",
    )(*pieces, w_both, w_both, w_down)
    return tuple(outs)


def ffn_backward_beside(pieces, gate_pre, up_pre, w_both, w_down):
    units, width = w_down.shape
    steps = units // FFN_TILE
    sizes = [piece.shape[0] for piece in pieces]
    count = sum(sizes)
    kinds = ((width, BF), (2 * units, BF))
    kept_specs = [
        pl.BlockSpec((count, width), lambda j: (0, 0)),
        pl.BlockSpec((count, 2 * units), lambda j: (0, 0)),
    ]
    pre_spec = pl.BlockSpec((count, FFN_TILE), lambda j: (0, j))
    first = len(pieces) + 5
    dims = (((1,), (1,)), ((), ()))

    def kernel(*refs):
        gate, up, w_gate, w_up, w_low = refs[len(pieces) : first]
        m, rows, grads, total = refs[-4:]
        j = pl.program_id(0)

        @pl.when(j == 0)
        def _():
            at = 0
            for ref, size in zip(refs, sizes):
                rows[at : at + size] = ref[...]
                at += size

        grad_hidden = lax.dot_general(rows[...], w_low[...], dims, preferred_element_type=F32)
        g = gate[...]
        s = sigmoid(g)
        grad_gate = (grad_hidden * up[...] * s * (1.0 + g * (1.0 - s))).astype(BF)
        grad_up = (grad_hidden * g * s).astype(BF)
        start = pl.multiple_of(j * FFN_TILE, LANES)
        grads[:, pl.ds(start, FFN_TILE)] = grad_gate
        grads[:, pl.ds(start + units, FFN_TILE)] = grad_up
        part = lax.dot_general(grad_gate, w_gate[...], dims, preferred_element_type=F32)
        part += lax.dot_general(grad_up, w_up[...], dims, preferred_element_type=F32)

        @pl.when(j == 0)
        def _():
            total[...] = part

        @pl.when(j > 0)
        def _():
            total[...] += part

        @pl.when(j == steps - 1)
        def _():
            m[...] = total[...].astype(m.dtype)

    m_shape = jax.ShapeDtypeStruct((count, width), F32)
    outs = pl.pallas_call(
        kernel,
        grid=(steps,),
        out_shape=[m_shape] + [jax.ShapeDtypeStruct((count, w), t) for w, t in kinds],
        in_specs=[whole(piece) for piece in pieces]
        + [pre_spec] * 2
        + tiles_of(w_both, w_down, units),
        out_specs=[whole(m_shape)] + kept_specs,
        scratch_shapes=[pltpu.VMEM((count, width), F32)],
        compiler_params=pltpu.CompilerParams(vmem_limit_bytes=FFN_VMEM),
        cost_estimate=NO_COST,
        name="ffn_backward_beside",
    )(*pieces, gate_pre, up_pre, w_both, w_both, w_down)
    return tuple(outs)


def products(pairs, dtype):
    tokens, rows = pairs[0][0].shape
    columns = pairs[0][1].shape[1]
    tile = columns // 4

    def kernel(*refs):
        total = None
        for i in range(len(pairs)):
            part = lax.dot_general(
                refs[2 * i][...],
                refs[2 * i + 1][...],
                (((0,), (0,)), ((), ())),
                preferred_element_type=F32,
            )
            total = part if total is None else total + part
        refs[-1][...] = total.astype(dtype)

    specs = [
        pl.BlockSpec((tokens, rows), lambda j: (0, 0)),
        pl.BlockSpec((tokens, tile), lambda j: (0, j)),
    ]
    return pl.pallas_call(
        kernel,
        grid=(columns // tile,),
        out_shape=jax.ShapeDtypeStruct((rows, columns), dtype),
        in_specs=specs * len(pairs),
        out_specs=pl.BlockSpec((rows, tile), lambda j: (0, j)),
        compiler_params=pltpu.CompilerParams(vmem_limit_bytes=FFN_VMEM),
        cost_estimate=NO_COST,
        name="products",
    )(*[array for pair in pairs for array in pair])


def body(
    tokens,
    teacher,
    valid_mask,
    w_query,
    key_weight_matrix,
    value_weight_matrix,
    w_output,
    w_gate,
    w_up,
    w_down,
    attn_gain,
    ffn_gain,
):
    n = lax.axis_size("dp")
    planes = n // 8
    position = lax.axis_index("dp")
    c, x, y, z = position % 2, position // 2 % 2, position // 4 % 2, position // 8
    bits = (z, y, x, c)
    p = position // 2 % 4
    rows = w_query.shape[0]
    width = w_query.shape[1]
    kv_width = key_weight_matrix.shape[1]
    ff_rows = w_down.shape[0]
    ff = w_gate.shape[1]
    count = tokens.shape[0]
    cosine, sine = rotation_lanes()

    part = 2 * ff_rows
    units = planes * part
    gains = jnp.stack([attn_gain, ffn_gain], axis=1)
    gains = jnp.pad(gains, ((0, 0), (0, LANES - 2)))
    local = packed([w_query, key_weight_matrix, value_weight_matrix, w_output, gains])
    if planes == 4:
        gathered, wb = gather_weights(local, w_gate, w_up, w_down, bits)
        wd = w_down_from(wb, ff_rows, 2 * units, width)
    else:
        gathered, wb, wd = gather_weights_plainly(local, w_gate, w_up, w_down, p)

    with jax.named_scope("attention_forward"):
        wide = width + 2 * kv_width
        wqkv = gathered[:, :wide]
        wo = gathered[:, wide : wide + width]
        gain_in = gathered[:, wide + width].astype(F32)
        gain_mid = gathered[:, wide + width + 1].astype(F32)
        inputs_f = tokens.astype(F32)
        normed, inv_attn = norm_rows(inputs_f, gain_in)
        normed_in = normed.astype(BF)
        raw = mm(normed_in, wqkv)
        query, key, value, mixed = attention_forward(raw, cosine, sine, width, kv_width)
        hidden_res = inputs_f + mm(mixed, wo)
        normed_two, inv_ffn = norm_rows(hidden_res, gain_mid)
        normed_mid = normed_two.astype(BF)

    with jax.named_scope("ffn_forward"):
        to_column = reordered(width, rows, "zcyx")
        far, y_near, *kept = split_gather(
            mm(normed_mid, to_column).astype(BF),
            (),
            lambda pieces: ffn_forward_beside(pieces, wb, wd),
        )
        near, hid_near, gate_near, up_near = kept
        y_far, pre_far, hid_far = ffn_forward(far, wb, wd)
        y_far, mixed, normed_in = tied(y_far, mixed, normed_in)
        by_side = reordered(width, rows, "cxyz")
        beside = (
            *core_halves(mm(mixed, by_side).astype(BF), c),
            *core_halves(mm(normed_in, by_side).astype(BF), c),
        )
        result, *halves = split_reduce(y_near, y_far.astype(BF), beside)
        mixed_mine, mixed_theirs, normed_mine, normed_theirs = halves
        result = hidden_res + result
        out_act = result.astype(BF)

    with jax.named_scope("loss"):
        mask_f = valid_mask.astype(F32)
        grad_out = (result - teacher.astype(F32)) * mask_f[:, None]
        sums = jnp.stack([jnp.sum(grad_out * grad_out), jnp.sum(mask_f)])
        sums = jnp.broadcast_to(sums[:, None], (2, LANES))

    high = n // 2
    rest = [1 << k for k in range(4, n.bit_length() - 2)]

    with jax.named_scope("ffn_backward"):
        grad_low, sums = tied(grad_out.astype(BF), sums)

        def near_backward(pieces, came):
            value = sums + came
            for mask in rest:
                value = value + swap(value, mask)
            near = ffn_backward_beside(pieces, gate_near, up_near, wb, wd)
            return (value, swap(value, 8), *near)

        d_far, sums, sums_came, m_near, d_near, g_near = split_gather(
            grad_low, (swap(sums, 1),), near_backward
        )
        m_far, g_far = ffn_backward(d_far, pre_far, wb, wd)
        m_far = m_far.astype(BF)
        m_near, m_far, sums, sums_came = tied(m_near, m_far, sums, sums_came)
        sums = sums + sums_came
        g_both = products([(near, g_near), (far, g_far)], BF)
        g_down = products([(hid_near, d_near), (hid_far, d_far)], BF)
        g_both, g_down = sum_to_owners(g_both), sum_to_owners(g_down)

        def later(sums, sums_came):
            sums = sums + sums_came
            return (sums, swap(sums, 2))

        grad_mid, sums, sums_came = split_reduce(m_near, m_far, (sums, swap(sums, high)), later)
        sums = sums + sums_came
        high_part = grad_mid.astype(BF)
        low_part = (grad_mid - high_part.astype(F32)).astype(BF)
        grad_mid = mm_t(high_part, to_column) + mm_t(low_part, to_column)

    with jax.named_scope("attention_backward"):
        grad_gain_mid, grad_res = norm_back(grad_mid, hidden_res, inv_ffn, gain_mid)
        grad_res = grad_out + grad_res
        res_low = grad_res.astype(BF)
        wo_came, sums_came = tied(swap(t_mm(mixed_theirs, res_low).astype(BF), 1), swap(sums, 4))
        sums = sums + sums_came
        loss = sums[0, 0] / (sums[1, 0] * width)
        shape = (2, 2, planes, rows, -1)
        g_wo = [t_mm(mixed_mine, res_low).reshape(shape), wo_came.reshape(shape)]
        wo_moving = plane_step_1(g_wo, bits)
        grad_mixed = mm_t(res_low, wo).astype(BF)
        grad_raw = attention_backward(grad_mixed, query, key, value, cosine, sine)
        *wo_came, grad_raw = tied(*wo_moving, grad_raw)
        g_wo, wo_moving = plane_step_2(g_wo, wo_came, bits)

    with jax.named_scope("q_k_v_weight_gradients"):
        qkv_came = swap(t_mm(normed_theirs, grad_raw).astype(BF), 1)
        g_qkv = t_mm(normed_mine, grad_raw)
        qkv_came, g_qkv, grad_raw, *wo_came = tied(qkv_came, g_qkv, grad_raw, *wo_moving)
        g_wo = plane_step_3(g_wo, wo_came, bits)
        g_qkv = [g_qkv.reshape(shape), qkv_came.reshape(shape)]
        qkv_moving = plane_step_1(g_qkv, bits)

    with jax.named_scope("input_gradient"):
        grad_in = mm_t(grad_raw, wqkv)
        grad_gain_in, grad_tokens = norm_back(grad_in, inputs_f, inv_attn, gain_in)
        input_grad = (grad_res + grad_tokens).astype(BF)
        gains = jnp.stack([grad_gain_in, grad_gain_mid])
        gains_came = swap(gains, 1)

    with jax.named_scope("weight_gradients_to_owners"):
        *qkv_came, gains_came, gains = tied(*qkv_moving, gains_came, gains)
        gains = gains + gains_came
        g_qkv, qkv_moving = plane_step_2(g_qkv, qkv_came, bits)
        *qkv_came, gains_came = tied(*qkv_moving, swap(gains, 8))
        gains = gains + gains_came
        g_qkv = plane_step_3(g_qkv, qkv_came, bits)
        if planes == 4:
            moving = direct([g_qkv], z) + direct([g_wo], z)
        gains_came = swap(gains, high)
        g_both = g_both.reshape(4, rows, 2 * units)
        gains, gains_came, g_both = tied(gains, gains_came, g_both)
        gains = gains + gains_came
        came = [pick(g_both, p ^ r, 0) for r in range(4)]
        gains_came, *moved = tied(swap(gains, 2), *[swap(came[r], r << 1) for r in (1, 2, 3)])
        gains = gains + gains_came
        for mask in rest:
            gains = gains + swap(gains, mask)
        grad_gate, grad_up = spread_columns([came[0]] + moved, p, part)
        gains = gains + swap(gains, 4)
        g_gains = lax.dynamic_slice_in_dim(gains, position * rows, rows, 1)
        if planes == 4:
            g_qkv = owned([g_qkv], moving[:3], z)
            g_wo = owned([g_wo], moving[3:], z)
        else:
            g_qkv, g_wo = z_reduce([g_qkv]), z_reduce([g_wo])
        g_wq = g_qkv[:, :width]
        g_wk = g_qkv[:, width : width + kv_width]
        g_wv = g_qkv[:, width + kv_width :]

    return (
        out_act,
        loss,
        input_grad,
        g_wq,
        g_wk,
        g_wv,
        g_wo,
        grad_gate,
        grad_up,
        g_down.astype(F32),
        g_gains[0],
        g_gains[1],
    )


def solution(mesh):
    wide, flat = P("dp", None), P("dp")
    in_specs = (wide, wide, flat) + (wide,) * 7 + (flat, flat)
    out_specs = (wide, P(), wide) + (wide,) * 7 + (flat, flat)
    return jax.shard_map(body, mesh=mesh, in_specs=in_specs, out_specs=out_specs, check_vma=False)
```

time: 560 us -> 500 us (0.89)
  Pallas kernels: 13.4 us -> 84 us
  starting transfers between devices: 129 us -> 73.6 us
  local copies, waits for them, and re-layouts: 76.2 us -> 49.4 us
  waiting for transfers between devices: 185 us -> 163 us
  matrix products: 84 us -> 64.1 us
  other arithmetic: 57.6 us -> 40.5 us
  between operations: 6.29 us -> 17.9 us
    pallas_call x2 -> x9, Pallas kernels: 11.5 us -> 82.1 us  [the longest x1 16.8 us: attention_backward(): pl.pallas_call(kernel, grid=(count // SEQ, steps), out_shape=jax.ShapeDty...]
    ppermute x25 -> x5, waiting for transfers between devices: 59.2 us -> 6.73 us  [along_z(): lax.ppermute(value, 'dp', [(8 * a + i, 8 * b + i) for a, b in pairs for i...]
    ppermute x25 -> x5, starting transfers between devices: 60 us -> 15 us  [along_z(): lax.ppermute(value, 'dp', [(8 * a + i, 8 * b + i) for a, b in pairs for i...]
    ppermute x64 -> x60, waiting for transfers between devices: 126 us -> 156 us  [swap(): return lax.ppermute(value, 'dp', [(i, i ^ mask) for i in range(n)])]
    convert_element_type x10 -> x2, other arithmetic: 16.9 us -> 2.36 us  [the longest x1 2.11 us: body(): g_down.astype(F32)]
    reshape x5 -> x0, local copies, waits for them, and re-layouts: 14.2 us -> none  [the longest x2 8.51 us: body(): grad_mixed = mm_t(res_low, wo).astype(BF).reshape(grouped)]
    dot_general x26 -> x17, matrix products: 78.3 us -> 64.1 us  [dot(): return lax.dot_general(a, b, (dims, ((), ())), preferred_element_type=F32)]
    ppermute x64 -> x60, starting transfers between devices: 69.1 us -> 58.2 us  [swap(): return lax.ppermute(value, 'dp', [(i, i ^ mask) for i in range(n)])]
  transfers between devices with their start and end apart: 89 -> 68, of which waited for: 40 -> 38; matrix products, arithmetic and copies ran while one was open for 33% -> 23% of each run, Pallas kernels for 2% -> 17%
where the time goes in v6:
time: 500 us; the launch traced here: 493 us
  waiting for transfers between devices  163 us (33%)
  Pallas kernels  84 us (17%)
  starting transfers between devices  73.6 us (15%)
  matrix products  64.1 us (13%)
  local copies, waits for them, and re-layouts  49.4 us (10%)
  other arithmetic  40.5 us (8%)
  between operations  17.9 us (4%)
    ppermute x60, waiting for transfers between devices, swap(): return lax.ppermute(value, 'dp', [(i, i ^ mask) for i in range(n)])  156 us
    dot_general x17, matrix products, dot(): return lax.dot_general(a, b, (dims, ((), ())), preferred_element_type=F32)  64.1 us
    ppermute x60, starting transfers between devices, swap(): return lax.ppermute(value, 'dp', [(i, i ^ mask) for i in range(n)])  58.2 us
    dynamic_update_slice x16, local copies, waits for them, and re-layouts, place(): return lax.dynamic_update_slice(out, piece, where)  18.5 us
    pallas_call x1, Pallas kernels, attention_backward(): pl.pallas_call(kernel, grid=(count // SEQ, steps), out_shape=jax.ShapeDty...  16.8 us
    pallas_call x2, Pallas kernels, products(): pl.pallas_call(kernel, grid=(columns // tile,), out_shape=jax.ShapeDtypeS...  16.3 us
    ppermute x5, starting transfers between devices, along_z(): lax.ppermute(value, 'dp', [(8 * a + i, 8 * b + i) for a, b in pairs for i...  15 us
    pallas_call x1, Pallas kernels, attention_forward(): pl.pallas_call(kernel, grid=(count // SEQ, steps), out_shape=[jax.ShapeDt...  14.9 us
  transfers between devices with their start and end apart: 68, of which 38 were waited for; matrix products, arithmetic and copies ran while one was open for 23% of the time, Pallas kernels for 17%

profile of v6, /device:TPU:0, one launch (start us, length us, event | category | flops | bytes accessed | tf_op | source)
XLA Modules:
  0.0 492.6 jit_solution(2967595007141236787)
XLA Ops:
  8.6 1.9 packed.1
  10.5 5.1 %collective-permute-start = (bf16[48,4736]{1,0:T(8,128)(2,1)}, bf16[48,4736]{1,0:T(8,128)(2,1)S(1)}, u32[]{:S(2)}, u32[]{:S(2)}) collective-permute-start(bf16[48,4736]{1,0:T(8,128)(2,1)} %packed.1), channel_id=1, source_target_pairs={{0,8},{1,9},{2,10},{3,11},{4,12},{5,13},{6,14},{7,15},{8,16},{9,17... | collective-permute-start | bytes 1363976 | tf_op jit(solution)/shard_map/phase_0/ppermute | solution.py:77
  16.9 2.1 column_cuts.1
  22.5 4.5 collective-permute-done.2.refs_1_
  27.1 4.0 collective-permute-done.3.refs_2_
  33.1 6.0 %collective-permute-start.7 = (bf16[48,4736]{1,0:T(8,128)(2,1)S(1)}, bf16[48,4736]{1,0:T(8,128)(2,1)}, u32[]{:S(2)}, u32[]{:S(2)}) collective-permute-start(bf16[48,4736]{1,0:T(8,128)(2,1)S(1)} %copy-done.26), channel_id=1, source_target_pairs={{0,16},{1,17},{2,18},{3,19},{4,20},{5,21},{6,22},{7,23},{24,8},{25... | collective-permute-start | bytes 1363976 | tf_op jit(solution)/shard_map/phase_1/ppermute | solution.py:77
  44.3 2.4 merged.1
  46.8 2.6 collective-permute-done.6
  49.4 2.1 collective-permute-done.8
  60.9 4.6 collective-permute-done.11
  65.5 5.7 %collective-permute-done.10 = bf16[2,48,4736]{2,1,0:T(8,128)(2,1)S(1)} collective-permute-done((bf16[2,48,4736]{2,1,0:T(8,128)(2,1)S(1)}, bf16[2,48,4736]{2,1,0:T(8,128)(2,1)S(1)}, u32[]{:S(2)}, u32[]{:S(2)}) %collective-permute-start.10) | collective-permute-done | bytes 909344 | tf_op jit(solution)/shard_map/phase_2/ppermute | solution.py:40
  77.4 7.2 %collective-permute-done.12 = bf16[48,4736]{1,0:T(8,128)(2,1)} collective-permute-done((bf16[48,4736]{1,0:T(8,128)(2,1)S(1)}, bf16[48,4736]{1,0:T(8,128)(2,1)}, u32[]{:S(2)}, u32[]{:S(2)}) %collective-permute-start.12) | collective-permute-done | bytes 454688 | tf_op jit(solution)/shard_map/phase_3/ppermute | solution.py:40
  88.5 1.8 collective-permute-start.15
  90.7 2.2 bitcast_dynamic-update-slice_fusion.11
  92.9 2.2 bitcast_dynamic-update-slice_fusion.10
  97.3 13.8 %collective-permute-done.15 = bf16[2,48,4736]{2,1,0:T(8,128)(2,1)S(1)} collective-permute-done((bf16[2,48,4736]{2,1,0:T(8,128)(2,1)S(1)}, bf16[2,48,4736]{2,1,0:T(8,128)(2,1)S(1)}, u32[]{:S(2)}, u32[]{:S(2)}) %collective-permute-start.15) | collective-permute-done | bytes 909344 | tf_op jit(solution)/shard_map/phase_4/ppermute | solution.py:40
  117.4 1.8 collective-permute-done.19
  125.1 8.3 %fusion.7.q_raw.k_raw.v_raw = f32[256,3072]{1,0:T(8,128)} fusion(bf16[256,1536]{1,0:T(8,128)(2,1)S(1)} %fusion.36, bf16[1536,4736]{1,0:T(8,128)(2,1)} %bitcast.256), kind=kOutput, calls=%fused_computation.9 | convolution fusion | flops 2415919104 | bytes 13369344 | tf_op jit(solution)/shard_map/attention_forward/dot_general | solution.py:23
  133.5 14.9 %attention_forward.1 = (bf16[256,1536]{1,0:T(8,128)(2,1)}, bf16[256,768]{1,0:T(8,128)(2,1)}, bf16[256,768]{1,0:T(8,128)(2,1)}, bf16[256,1536]{1,0:T(8,128)(2,1)}) custom-call(f32[256,3072]{1,0:T(8,128)} %fusion.7.q_raw.k_raw.v_raw, f32[256,3072]{1,0:T(8,128)} %fusion.7.q_raw.k_raw.v_raw, f32[256,3072]{1,0:T(8,128)} %fusion.7.q_raw.k_raw.v_raw, ...), custom_call_target="tpu_custom_call" | custom-call | flops 1 | bytes 1 | tf_op jit(solution)/shard_map/attention_forward/attention_forward/pallas_call | solution.py:519
  148.7 4.1 multiply_reduce_fusion.3
  153.4 2.1 fusion.28
  156.7 10.1 %collective-permute-done.20 = bf16[128,1536]{1,0:T(8,128)(2,1)S(1)} collective-permute-done((bf16[128,1536]{1,0:T(8,128)(2,1)S(1)}, bf16[128,1536]{1,0:T(8,128)(2,1)S(1)}, u32[]{:S(2)}, u32[]{:S(2)}) %collective-permute-start.20) | collective-permute-done | bytes 393248 | tf_op jit(solution)/shard_map/ffn_forward/ppermute | solution.py:40
  169.2 3.7 w_down_from.1.refs_4_.refs_6_
  172.9 11.1 %ffn_forward_beside.1 = (f32[512,1536]{1,0:T(8,128)}, bf16[512,1536]{1,0:T(8,128)(2,1)S(1)}, bf16[512,1024]{1,0:T(8,128)(2,1)S(1)}, f32[512,1024]{1,0:T(8,128)}, f32[512,1024]{1,0:T(8,128)}) custom-call(bf16[256,1536]{1,0:T(8,128)(2,1)S(1)} %pad_maximum_fusion.10.refs_0_, bf16[256,1536]{1,0:T(8,128)(2,1)S(1)} %pad_maximum_fusion.11.refs_1_, ...), custom_call_target="tpu_custom_call" | custom-call | flops 1 | bytes 1 | tf_op jit(solution)/shard_map/ffn_forward/ffn_forward_beside/pallas_call | solution.py:702
  184.1 1.8 collective-permute-done.22
  188.5 5.7 %fusion.11 = f32[512,2048]{1,0:T(8,128)S(1)} fusion(bf16[512,1536]{1,0:T(8,128)(2,1)S(1)} %constant_dynamic-update-slice_fusion.refs_2_, bf16[1536,3072]{1,0:T(8,128)(2,1)} %all-gather.2.cloned.1.call-done.ref.refs_2_.refs_3_.refs_4_.refs_5_), kind=kOutput, calls=%fused_computation.13 | convolution fusion | flops 3221225472 | bytes 12058624 | tf_op jit(solution)/shard_map/ffn_forward/dot_general | solution.py:23
  197.6 1.8 fusion.158
  202.5 2.0 fusion.30
  205.5 2.0 fusion.29
  208.4 8.5 %collective-permute-done.24 = bf16[256,1536]{1,0:T(8,128)(2,1)S(1)} collective-permute-done((bf16[256,1536]{1,0:T(8,128)(2,1)S(1)}, bf16[256,1536]{1,0:T(8,128)(2,1)S(1)}, u32[]{:S(2)}, u32[]{:S(2)}) %collective-permute-start.24) | collective-permute-done | bytes 786464 | tf_op jit(solution)/shard_map/ffn_forward/ppermute | solution.py:40
  221.4 5.2 %collective-permute-done.26 = bf16[128,1536]{1,0:T(8,128)(2,1)S(1)} collective-permute-done((bf16[128,1536]{1,0:T(8,128)(2,1)S(1)}, bf16[128,1536]{1,0:T(8,128)(2,1)S(1)}, u32[]{:S(2)}, u32[]{:S(2)}) %collective-permute-start.26) | collective-permute-done | bytes 393248 | tf_op jit(solution)/shard_map/ffn_forward/ppermute | solution.py:40
  228.3 2.0 multiply_reduce_fusion.2
  234.3 6.8 %collective-permute-done.28 = bf16[128,1536]{1,0:T(8,128)(2,1)S(1)} collective-permute-done((bf16[128,1536]{1,0:T(8,128)(2,1)S(1)}, bf16[128,1536]{1,0:T(8,128)(2,1)S(1)}, u32[]{:S(2)}, u32[]{:S(2)}) %collective-permute-start.28) | collective-permute-done | bytes 393248 | tf_op jit(solution)/shard_map/ffn_backward/ppermute | solution.py:40
  241.1 2.5 collective-permute-done.29
  246.1 14.7 %ffn_backward_beside.1 = (f32[512,1536]{1,0:T(8,128)}, bf16[512,1536]{1,0:T(8,128)(2,1)S(1)}, bf16[512,2048]{1,0:T(8,128)(2,1)S(1)}) custom-call(bf16[256,1536]{1,0:T(8,128)(2,1)S(1)} %pad_maximum_fusion.12.refs_0_, bf16[256,1536]{1,0:T(8,128)(2,1)S(1)} %pad_maximum_fusion.13.refs_1_, f32[512,1024]{1,0:T(8,128)} %get-tuple-element.209.refs_2_, ...), custom_call_target="tpu_custom_call" | custom-call | flops 1 | bytes 1 | tf_op jit(solution)/shard_map/ffn_backward/ffn_backward_beside/pallas_call | solution.py:767
  261.0 2.5 copy-done.3
  263.5 4.8 multiply_convert_fusion.1
  269.3 3.4 fusion.22
  272.8 1.8 collective-permute-start.34
  276.8 3.0 collective-permute-done.36
  279.7 8.4 %collective-permute-done.34 = bf16[256,1536]{1,0:T(8,128)(2,1)S(1)} collective-permute-done((bf16[256,1536]{1,0:T(8,128)(2,1)S(1)}, bf16[256,1536]{1,0:T(8,128)(2,1)S(1)}, u32[]{:S(2)}, u32[]{:S(2)}) %collective-permute-start.34) | collective-permute-done | bytes 786464 | tf_op jit(solution)/shard_map/ffn_backward/ppermute | solution.py:40
  288.1 2.7 collective-permute-done.35
  295.9 6.5 %products.3 = bf16[1024,1536]{1,0:T(8,128)(2,1)} custom-call(bf16[512,1024]{1,0:T(8,128)(2,1)S(1)} %get-tuple-element.263.refs_0_, bf16[512,1536]{1,0:T(8,128)(2,1)S(1)} %get-tuple-element.264.refs_1_, bf16[512,1024]{1,0:T(8,128)(2,1)S(1)} %multiply_convert_fusion.2.refs_2_, bf16[512,1536]{1,0:T(8,128)(2,1)S(1)} %constant_dynamic-update-slice_fusion.2.refs_3_), custom_call_target="tpu_custom_call" | custom-call | flops 1 | bytes 1 | tf_op jit(solution)/shard_map/ffn_backward/products/pallas_call | solution.py:804
  305.6 2.0 fusion.2
  307.7 3.1 multiply_reduce_fusion
  323.1 4.7 fusion.31.d_ref
  327.8 16.8 %attention_backward.1 = bf16[256,3072]{1,0:T(8,128)(2,1)} custom-call(bf16[256,1536]{1,0:T(8,128)(2,1)} %fusion.31.d_ref, bf16[256,1536]{1,0:T(8,128)(2,1)} %get-tuple-element.236.q_ref, bf16[256,768]{1,0:T(8,128)(2,1)} %get-tuple-element.237.k_ref, bf16[256,768]{1,0:T(8,128)(2,1)} %get-tuple-element.238.v_ref, f32[128,768]{1,0:T(8,128)} %copy.84.cosine, ...), custom_call_target="tpu_custom_call" | custom-call | flops 1 | bytes 1 | tf_op jit(solution)/shard_map/attention_backward/attention_backward/pallas_call | solution.py:590
  344.7 5.1 %convolution_convert_fusion = bf16[768,3072]{1,0:T(8,128)(2,1)} fusion(bf16[256,768]{1,0:T(8,128)(2,1)S(1)} %copy-done.25, bf16[256,3072]{1,0:T(8,128)(2,1)} %attention_backward.1), kind=kOutput, calls=%fused_computation.15 | convolution fusion | flops 1210318848 | bytes 6684672 | tf_op jit(solution)/shard_map/q_k_v_weight_gradients/dot_general | solution.py:23
  352.1 9.9 %products.2 = bf16[1536,2048]{1,0:T(8,128)(2,1)} custom-call(bf16[512,1536]{1,0:T(8,128)(2,1)S(1)} %get-tuple-element.255.refs_0_, bf16[512,2048]{1,0:T(8,128)(2,1)S(1)} %copy-done.1, bf16[512,1536]{1,0:T(8,128)(2,1)S(1)} %constant_dynamic-update-slice_fusion.refs_2_, bf16[512,2048]{1,0:T(8,128)(2,1)} %pad_maximum_fusion.refs_3_), custom_call_target="tpu_custom_call" | custom-call | flops 1 | bytes 1 | tf_op jit(solution)/shard_map/ffn_backward/products/pallas_call | solution.py:804
  367.0 1.9 fusion.70
  369.9 5.1 %fusion.159 = f32[768,3072]{1,0:T(8,128)} fusion(bf16[256,768]{1,0:T(8,128)(2,1)S(1)} %copy-done.27, bf16[256,3072]{1,0:T(8,128)(2,1)S(1)} %copy-done.8), kind=kOutput, calls=%fused_computation.368 | convolution fusion | flops 1207959552 | bytes 11403264 | tf_op jit(solution)/shard_map/q_k_v_weight_gradients/dot_general | solution.py:23
  375.0 2.1 convert_element_type.407
  377.6 8.2 %fusion.43 = (f32[1536]{0:T(1024)S(1)}, f32[256]{0:T(256)S(1)}, f32[256,1536]{1,0:T(8,128)}) fusion(bf16[256,1536]{1,0:T(8,128)(2,1)S(1)} %copy-done.11, f32[256]{0:T(256)S(1)} %copy-done.43, f32[1536]{0:T(1024)S(1)} %convert_reduce_fusion.1, bf16[256,3072]{1,0:T(8,128)(2,1)S(1)} %copy-done.8, bf16[1536,4736]{1,0:T(8,128)(2,1)} %bitcast.259), kind=kOutput, calls=%fused_computation.76 | convolution fusion | flops 2418669824 | bytes 13383680 | tf_op jit(solution)/shard_map/input_gradient/dot_general | solution.py:23
  385.9 5.1 %fusion.149 = (bf16[2,2,2,48,3072]{4,3,2,1,0:T(8,128)(2,1)}, bf16[2,2,2,48,3072]{4,3,2,1,0:T(8,128)(2,1)}) fusion(bf16[2,2,4,48,3072]{4,3,2,1,0:T(8,128)(2,1)} %bitcast.66), kind=kLoop, calls=%fused_computation.358 | loop fusion | bytes 9437184 | tf_op jit(solution)/shard_map/q_k_v_weight_gradients/slice | solution.py:336
  392.2 2.5 convert_add_fusion.1
  396.2 2.1 collective-permute-start.47
  403.7 19.5 %collective-permute-done.48 = bf16[2,2,48,3072]{3,2,1,0:T(8,128)(2,1)S(1)} collective-permute-done((bf16[2,2,48,3072]{3,2,1,0:T(8,128)(2,1)S(1)}, bf16[2,2,48,3072]{3,2,1,0:T(8,128)(2,1)S(1)}, u32[]{:S(2)}, u32[]{:S(2)}) %collective-permute-start.48) | collective-permute-done | bytes 1179680 | tf_op jit(solution)/shard_map/q_k_v_weight_gradients/ppermute | solution.py:40
  426.4 1.8 collective-permute-start.51
  430.7 10.4 %collective-permute-done.51 = bf16[2,48,3072]{2,1,0:T(8,128)(2,1)S(1)} collective-permute-done((bf16[2,48,3072]{2,1,0:T(8,128)(2,1)S(1)}, bf16[2,48,3072]{2,1,0:T(8,128)(2,1)S(1)}, u32[]{:S(2)}, u32[]{:S(2)}) %collective-permute-start.51) | collective-permute-done | bytes 589856 | tf_op jit(solution)/shard_map/weight_gradients_to_owners/ppermute | solution.py:40
  445.2 2.5 collective-permute-start.55
  448.6 6.5 %collective-permute-done.53 = bf16[48,3072]{1,0:T(8,128)(2,1)S(1)} collective-permute-done((bf16[48,3072]{1,0:T(8,128)(2,1)S(1)}, bf16[48,3072]{1,0:T(8,128)(2,1)S(1)}, u32[]{:S(2)}, u32[]{:S(2)}) %collective-permute-start.53) | collective-permute-done | bytes 294944 | tf_op jit(solution)/shard_map/weight_gradients_to_owners/ppermute | solution.py:40
  455.1 14.3 %collective-permute-done.54 = bf16[48,3072]{1,0:T(8,128)(2,1)S(1)} collective-permute-done((bf16[48,3072]{1,0:T(8,128)(2,1)S(1)}, bf16[48,3072]{1,0:T(8,128)(2,1)S(1)}, u32[]{:S(2)}, u32[]{:S(2)}) %collective-permute-start.54) | collective-permute-done | bytes 294944 | tf_op jit(solution)/shard_map/weight_gradients_to_owners/ppermute | solution.py:40
  472.3 2.0 collective-permute-start.63
  476.4 3.6 collective-permute-done.60
  (368 shorter events, 135.1 us)
Async XLA Ops:
  7.2 162.1 %all-gather.2.cloned.1.call-start = ((), (), s32[]{:S(2)}) async-start(), calls=%async_computation.2 | async-start | bytes 10616832 | tf_op jit(solution)/shard_map/ffn_weights/all_gather | solution.py:114
  10.5 20.5 %collective-permute-start = (bf16[48,4736]{1,0:T(8,128)(2,1)}, bf16[48,4736]{1,0:T(8,128)(2,1)S(1)}, u32[]{:S(2)}, u32[]{:S(2)}) collective-permute-start(bf16[48,4736]{1,0:T(8,128)(2,1)} %packed.1), channel_id=1, source_target_pairs={{0,8},{1,9},{2,10},{3,11},{4,12},{5,13},{6,14},{7,15},{8,16},{9,17... | collective-permute-start | bytes 1363976 | tf_op jit(solution)/shard_map/phase_0/ppermute | solution.py:77
  15.6 16.2 %collective-permute-start.1 = (bf16[48,4736]{1,0:T(8,128)(2,1)}, bf16[48,4736]{1,0:T(8,128)(2,1)S(1)}, u32[]{:S(2)}, u32[]{:S(2)}) collective-permute-start(bf16[48,4736]{1,0:T(8,128)(2,1)} %packed.1), channel_id=1, source_target_pairs={{8,0},{9,1},{10,2},{11,3},{12,4},{13,5},{14,6},{15,7},{16,8},{17,9... | collective-permute-start | bytes 1363976 | tf_op jit(solution)/shard_map/phase_0/ppermute | solution.py:77
  19.0 8.0 %collective-permute-start.2 = (bf16[48,2048]{1,0:T(8,128)(2,1)}, bf16[48,2048]{1,0:T(8,128)(2,1)S(1)}, u32[]{:S(2)}, u32[]{:S(2)}) collective-permute-start(bf16[48,2048]{1,0:T(8,128)(2,1)} %get-tuple-element.139), channel_id=1, source_target_pairs={{0,2},{1,3},{2,0},{3,1},{4,6},{5,7},{6,4},{7,5},{8,10},{9,11},{10,... | collective-permute-start | bytes 589832 | tf_op jit(solution)/shard_map/phase_0/ppermute | solution.py:40
  20.5 10.5 %collective-permute-start.3 = (bf16[48,2048]{1,0:T(8,128)(2,1)}, bf16[48,2048]{1,0:T(8,128)(2,1)S(1)}, u32[]{:S(2)}, u32[]{:S(2)}) collective-permute-start(bf16[48,2048]{1,0:T(8,128)(2,1)} %get-tuple-element.140), channel_id=1, source_target_pairs={{0,4},{1,5},{2,6},{3,7},{4,0},{5,1},{6,2},{7,3},{8,12},{9,13},{10,... | collective-permute-start | bytes 589832 | tf_op jit(solution)/shard_map/phase_0/ppermute | solution.py:40
  22.0 9.0 %collective-permute-start.4 = (bf16[48,2048]{1,0:T(8,128)(2,1)}, bf16[48,2048]{1,0:T(8,128)(2,1)S(1)}, u32[]{:S(2)}, u32[]{:S(2)}) collective-permute-start(bf16[48,2048]{1,0:T(8,128)(2,1)} %get-tuple-element.141), channel_id=1, source_target_pairs={{0,6},{1,7},{2,4},{3,5},{4,2},{5,3},{6,0},{7,1},{8,14},{9,15},{10,... | collective-permute-start | bytes 589832 | tf_op jit(solution)/shard_map/phase_0/ppermute | solution.py:40
  31.9 14.9 %collective-permute-start.5 = (bf16[48,4736]{1,0:T(8,128)(2,1)S(1)}, bf16[48,4736]{1,0:T(8,128)(2,1)S(1)}, u32[]{:S(2)}, u32[]{:S(2)}) collective-permute-start(bf16[48,4736]{1,0:T(8,128)(2,1)S(1)} %copy-done.26), channel_id=1, source_target_pairs={{0,2},{1,3},{2,0},{3,1},{4,6},{5,7},{6,4},{7,5},{8,10},{9,11},{10,... | collective-permute-start | bytes 1363976 | tf_op jit(solution)/shard_map/phase_1/ppermute | solution.py:40
  33.1 16.3 %collective-permute-start.7 = (bf16[48,4736]{1,0:T(8,128)(2,1)S(1)}, bf16[48,4736]{1,0:T(8,128)(2,1)}, u32[]{:S(2)}, u32[]{:S(2)}) collective-permute-start(bf16[48,4736]{1,0:T(8,128)(2,1)S(1)} %copy-done.26), channel_id=1, source_target_pairs={{0,16},{1,17},{2,18},{3,19},{4,20},{5,21},{6,22},{7,23},{24,8},{25... | collective-permute-start | bytes 1363976 | tf_op jit(solution)/shard_map/phase_1/ppermute | solution.py:77
  39.1 10.2 %collective-permute-start.6 = (bf16[48,4736]{1,0:T(8,128)(2,1)S(1)}, bf16[48,4736]{1,0:T(8,128)(2,1)}, u32[]{:S(2)}, u32[]{:S(2)}) collective-permute-start(bf16[48,4736]{1,0:T(8,128)(2,1)S(1)} %get-tuple-element.145), channel_id=1, source_target_pairs={{0,4},{1,5},{2,6},{3,7},{4,0},{5,1},{6,2},{7,3},{8,12},{9,13},{10,... | collective-permute-start | bytes 1363976 | tf_op jit(solution)/shard_map/phase_1/ppermute | solution.py:40
  40.0 11.5 %collective-permute-start.8 = (bf16[48,4736]{1,0:T(8,128)(2,1)S(1)}, bf16[48,4736]{1,0:T(8,128)(2,1)}, u32[]{:S(2)}, u32[]{:S(2)}) collective-permute-start(bf16[48,4736]{1,0:T(8,128)(2,1)S(1)} %get-tuple-element.146), channel_id=1, source_target_pairs={{8,0},{9,1},{10,2},{11,3},{12,4},{13,5},{14,6},{15,7},{16,24},{17,... | collective-permute-start | bytes 1363976 | tf_op jit(solution)/shard_map/phase_1/ppermute | solution.py:77
  52.9 18.4 %collective-permute-start.10 = (bf16[2,48,4736]{2,1,0:T(8,128)(2,1)S(1)}, bf16[2,48,4736]{2,1,0:T(8,128)(2,1)S(1)}, u32[]{:S(2)}, u32[]{:S(2)}) collective-permute-start(bf16[2,48,4736]{2,1,0:T(8,128)(2,1)S(1)} %pad_maximum_fusion.7), channel_id=1, source_target_pairs={{0,2},{1,3},{2,0},{3,1},{4,6},{5,7},{6,4},{7,5},{8,10},{9,11},{10,... | collective-permute-start | bytes 2727944 | tf_op jit(solution)/shard_map/phase_2/ppermute | solution.py:40
  53.5 18.0 %collective-permute-start.9 = (bf16[2,48,4736]{2,1,0:T(8,128)(2,1)S(1)}, bf16[2,48,4736]{2,1,0:T(8,128)(2,1)S(1)}, u32[]{:S(2)}, u32[]{:S(2)}) collective-permute-start(bf16[2,48,4736]{2,1,0:T(8,128)(2,1)S(1)} %pad_maximum_fusion.6), channel_id=1, source_target_pairs={{0,4},{1,5},{2,6},{3,7},{4,0},{5,1},{6,2},{7,3},{8,12},{9,13},{10,... | collective-permute-start | bytes 2727944 | tf_op jit(solution)/shard_map/phase_2/ppermute | solution.py:40
  55.0 10.5 %collective-permute-start.11 = (bf16[48,4736]{1,0:T(8,128)(2,1)}, bf16[48,4736]{1,0:T(8,128)(2,1)S(1)}, u32[]{:S(2)}, u32[]{:S(2)}) collective-permute-start(bf16[48,4736]{1,0:T(8,128)(2,1)} %collective-permute-done.7), channel_id=1, source_target_pairs={{8,0},{9,1},{10,2},{11,3},{12,4},{13,5},{14,6},{15,7},{16,24},{17,... | collective-permute-start | bytes 1363976 | tf_op jit(solution)/shard_map/phase_2/ppermute | solution.py:77
  71.6 14.4 %collective-permute-start.14 = (bf16[2,2,48,4736]{3,2,1,0:T(8,128)(2,1)}, bf16[2,2,48,4736]{3,2,1,0:T(8,128)(2,1)}, u32[]{:S(2)}, u32[]{:S(2)}) collective-permute-start(bf16[2,2,48,4736]{3,2,1,0:T(8,128)(2,1)} %pad_maximum_fusion.1), channel_id=1, source_target_pairs={{0,1},{1,0},{2,3},{3,2},{4,5},{5,4},{6,7},{7,6},{8,9},{9,8},{10,11... | collective-permute-start | bytes 5455880 | tf_op jit(solution)/shard_map/phase_3/ppermute | solution.py:40
  71.6 13.0 %collective-permute-start.12 = (bf16[48,4736]{1,0:T(8,128)(2,1)S(1)}, bf16[48,4736]{1,0:T(8,128)(2,1)}, u32[]{:S(2)}, u32[]{:S(2)}) collective-permute-start(bf16[48,4736]{1,0:T(8,128)(2,1)S(1)} %broadcast_select_fusion.1), channel_id=1, source_target_pairs={{0,2},{1,3},{2,0},{3,1},{4,6},{5,7},{6,4},{7,5},{8,10},{9,11},{10,... | collective-permute-start | bytes 1363976 | tf_op jit(solution)/shard_map/phase_3/ppermute | solution.py:40
  73.4 12.6 %collective-permute-start.13 = (bf16[48,4736]{1,0:T(8,128)(2,1)S(1)}, bf16[48,4736]{1,0:T(8,128)(2,1)}, u32[]{:S(2)}, u32[]{:S(2)}) collective-permute-start(bf16[48,4736]{1,0:T(8,128)(2,1)S(1)} %broadcast_select_fusion), channel_id=1, source_target_pairs={{0,4},{1,5},{2,6},{3,7},{4,0},{5,1},{6,2},{7,3},{8,12},{9,13},{10,... | collective-permute-start | bytes 1363976 | tf_op jit(solution)/shard_map/phase_3/ppermute | solution.py:40
  75.1 299.8 %reduce-scatter.5.cloned.1.call-start = ((), (), s32[]{:S(2)}) async-start(), calls=%async_computation.4 | async-start | bytes 3538944 | tf_op jit(solution)/shard_map/ffn_backward/reduce_scatter | solution.py:120
  88.4 24.1 %collective-permute-start.17 = (bf16[2,2,48,4736]{3,2,1,0:T(8,128)(2,1)S(1)}, bf16[2,2,48,4736]{3,2,1,0:T(8,128)(2,1)S(1)}, u32[]{:S(2)}, u32[]{:S(2)}) collective-permute-start(bf16[2,2,48,4736]{3,2,1,0:T(8,128)(2,1)S(1)} %pad_maximum_fusion.2), channel_id=1, source_target_pairs={{0,1},{1,0},{2,3},{3,2},{4,5},{5,4},{6,7},{7,6},{8,9},{9,8},{10,11... | collective-permute-start | bytes 5455880 | tf_op jit(solution)/shard_map/phase_4/ppermute | solution.py:40
  88.5 22.6 %collective-permute-start.15 = (bf16[2,48,4736]{2,1,0:T(8,128)(2,1)S(1)}, bf16[2,48,4736]{2,1,0:T(8,128)(2,1)S(1)}, u32[]{:S(2)}, u32[]{:S(2)}) collective-permute-start(bf16[2,48,4736]{2,1,0:T(8,128)(2,1)S(1)} %pad_maximum_fusion.8), channel_id=1, source_target_pairs={{0,4},{1,5},{2,6},{3,7},{4,0},{5,1},{6,2},{7,3},{8,12},{9,13},{10,... | collective-permute-start | bytes 2727944 | tf_op jit(solution)/shard_map/phase_4/ppermute | solution.py:40
  90.3 22.2 %collective-permute-start.16 = (bf16[2,48,4736]{2,1,0:T(8,128)(2,1)S(1)}, bf16[2,48,4736]{2,1,0:T(8,128)(2,1)S(1)}, u32[]{:S(2)}, u32[]{:S(2)}) collective-permute-start(bf16[2,48,4736]{2,1,0:T(8,128)(2,1)S(1)} %pad_maximum_fusion.9), channel_id=1, source_target_pairs={{0,2},{1,3},{2,0},{3,1},{4,6},{5,7},{6,4},{7,5},{8,10},{9,11},{10,... | collective-permute-start | bytes 2727944 | tf_op jit(solution)/shard_map/phase_4/ppermute | solution.py:40
  112.8 4.6 collective-permute-start.18
  112.8 6.3 %collective-permute-start.19 = (bf16[2,2,48,4736]{3,2,1,0:T(8,128)(2,1)S(1)}, bf16[2,2,48,4736]{3,2,1,0:T(8,128)(2,1)S(1)}, u32[]{:S(2)}, u32[]{:S(2)}) collective-permute-start(bf16[2,2,48,4736]{3,2,1,0:T(8,128)(2,1)S(1)} %pad_maximum_fusion.4), channel_id=1, source_target_pairs={{0,1},{1,0},{2,3},{3,2},{4,5},{5,4},{6,7},{7,6},{8,9},{9,8},{10,11... | collective-permute-start | bytes 5455880 | tf_op jit(solution)/shard_map/phase_5/ppermute | solution.py:40
  155.6 11.2 %collective-permute-start.20 = (bf16[128,1536]{1,0:T(8,128)(2,1)S(1)}, bf16[128,1536]{1,0:T(8,128)(2,1)S(1)}, u32[]{:S(2)}, u32[]{:S(2)}) collective-permute-start(bf16[128,1536]{1,0:T(8,128)(2,1)S(1)} %get-tuple-element.331), channel_id=1, source_target_pairs={{0,2},{1,3},{2,0},{3,1},{4,6},{5,7},{6,4},{7,5},{8,10},{9,11},{10,... | collective-permute-start | bytes 1179656 | tf_op jit(solution)/shard_map/ffn_forward/ppermute | solution.py:40
  156.2 10.9 %collective-permute-start.21 = (bf16[128,1536]{1,0:T(8,128)(2,1)S(1)}, bf16[128,1536]{1,0:T(8,128)(2,1)S(1)}, u32[]{:S(2)}, u32[]{:S(2)}) collective-permute-start(bf16[128,1536]{1,0:T(8,128)(2,1)S(1)} %get-tuple-element.330), channel_id=1, source_target_pairs={{0,4},{1,5},{2,6},{3,7},{4,0},{5,1},{6,2},{7,3},{8,12},{9,13},{10,... | collective-permute-start | bytes 1179656 | tf_op jit(solution)/shard_map/ffn_forward/ppermute | solution.py:40
  167.2 18.7 %collective-permute-start.22 = (bf16[256,1536]{1,0:T(8,128)(2,1)S(1)}, bf16[256,1536]{1,0:T(8,128)(2,1)}, u32[]{:S(2)}, u32[]{:S(2)}) collective-permute-start(bf16[256,1536]{1,0:T(8,128)(2,1)S(1)} %pad_maximum_fusion.10.refs_0_), channel_id=1, source_target_pairs={{0,4},{1,5},{2,6},{3,7},{4,0},{5,1},{6,2},{7,3},{8,12},{9,13},{10,... | collective-permute-start | bytes 2359304 | tf_op jit(solution)/shard_map/ffn_forward/ppermute | solution.py:40
  167.8 18.3 %collective-permute-start.23 = (bf16[256,1536]{1,0:T(8,128)(2,1)S(1)}, bf16[256,1536]{1,0:T(8,128)(2,1)}, u32[]{:S(2)}, u32[]{:S(2)}) collective-permute-start(bf16[256,1536]{1,0:T(8,128)(2,1)S(1)} %pad_maximum_fusion.11.refs_1_), channel_id=1, source_target_pairs={{0,2},{1,3},{2,0},{3,1},{4,6},{5,7},{6,4},{7,5},{8,10},{9,11},{10,... | collective-permute-start | bytes 2359304 | tf_op jit(solution)/shard_map/ffn_forward/ppermute | solution.py:40
  199.5 17.4 %collective-permute-start.24 = (bf16[256,1536]{1,0:T(8,128)(2,1)S(1)}, bf16[256,1536]{1,0:T(8,128)(2,1)S(1)}, u32[]{:S(2)}, u32[]{:S(2)}) collective-permute-start(bf16[256,1536]{1,0:T(8,128)(2,1)S(1)} %get-tuple-element.303), channel_id=1, source_target_pairs={{0,4},{1,5},{2,6},{3,7},{4,0},{5,1},{6,2},{7,3},{8,12},{9,13},{10,... | collective-permute-start | bytes 2359304 | tf_op jit(solution)/shard_map/ffn_forward/ppermute | solution.py:40
  201.1 17.1 %collective-permute-start.25 = (bf16[256,1536]{1,0:T(8,128)(2,1)S(1)}, bf16[256,1536]{1,0:T(8,128)(2,1)S(1)}, u32[]{:S(2)}, u32[]{:S(2)}) collective-permute-start(bf16[256,1536]{1,0:T(8,128)(2,1)S(1)} %get-tuple-element.302), channel_id=1, source_target_pairs={{0,2},{1,3},{2,0},{3,1},{4,6},{5,7},{6,4},{7,5},{8,10},{9,11},{10,... | collective-permute-start | bytes 2359304 | tf_op jit(solution)/shard_map/ffn_forward/ppermute | solution.py:40
  218.7 7.8 %collective-permute-start.26 = (bf16[128,1536]{1,0:T(8,128)(2,1)S(1)}, bf16[128,1536]{1,0:T(8,128)(2,1)S(1)}, u32[]{:S(2)}, u32[]{:S(2)}) collective-permute-start(bf16[128,1536]{1,0:T(8,128)(2,1)S(1)} %slice.495), channel_id=1, source_target_pairs={{0,2},{1,3},{2,0},{3,1},{4,6},{5,7},{6,4},{7,5},{8,10},{9,11},{10,... | collective-permute-start | bytes 1179656 | tf_op jit(solution)/shard_map/ffn_forward/ppermute | solution.py:40
  220.3 7.8 %collective-permute-start.27 = (bf16[128,1536]{1,0:T(8,128)(2,1)S(1)}, bf16[128,1536]{1,0:T(8,128)(2,1)S(1)}, u32[]{:S(2)}, u32[]{:S(2)}) collective-permute-start(bf16[128,1536]{1,0:T(8,128)(2,1)S(1)} %slice.494), channel_id=1, source_target_pairs={{0,4},{1,5},{2,6},{3,7},{4,0},{5,1},{6,2},{7,3},{8,12},{9,13},{10,... | collective-permute-start | bytes 1179656 | tf_op jit(solution)/shard_map/ffn_forward/ppermute | solution.py:40
  232.0 9.1 %collective-permute-start.28 = (bf16[128,1536]{1,0:T(8,128)(2,1)S(1)}, bf16[128,1536]{1,0:T(8,128)(2,1)S(1)}, u32[]{:S(2)}, u32[]{:S(2)}) collective-permute-start(bf16[128,1536]{1,0:T(8,128)(2,1)S(1)} %get-tuple-element.325), channel_id=1, source_target_pairs={{0,2},{1,3},{2,0},{3,1},{4,6},{5,7},{6,4},{7,5},{8,10},{9,11},{10,... | collective-permute-start | bytes 1179656 | tf_op jit(solution)/shard_map/ffn_backward/ppermute | solution.py:40
  232.6 10.9 %collective-permute-start.29 = (bf16[128,1536]{1,0:T(8,128)(2,1)S(1)}, bf16[128,1536]{1,0:T(8,128)(2,1)S(1)}, u32[]{:S(2)}, u32[]{:S(2)}) collective-permute-start(bf16[128,1536]{1,0:T(8,128)(2,1)S(1)} %get-tuple-element.324), channel_id=1, source_target_pairs={{0,4},{1,5},{2,6},{3,7},{4,0},{5,1},{6,2},{7,3},{8,12},{9,13},{10,... | collective-permute-start | bytes 1179656 | tf_op jit(solution)/shard_map/ffn_backward/ppermute | solution.py:40
  243.7 17.1 %collective-permute-start.31 = (bf16[256,1536]{1,0:T(8,128)(2,1)S(1)}, bf16[256,1536]{1,0:T(8,128)(2,1)S(1)}, u32[]{:S(2)}, u32[]{:S(2)}) collective-permute-start(bf16[256,1536]{1,0:T(8,128)(2,1)S(1)} %pad_maximum_fusion.12.refs_0_), channel_id=1, source_target_pairs={{0,4},{1,5},{2,6},{3,7},{4,0},{5,1},{6,2},{7,3},{8,12},{9,13},{10,... | collective-permute-start | bytes 2359304 | tf_op jit(solution)/shard_map/ffn_backward/ppermute | solution.py:40
  243.8 17.1 %collective-permute-start.32 = (bf16[256,1536]{1,0:T(8,128)(2,1)S(1)}, bf16[256,1536]{1,0:T(8,128)(2,1)S(1)}, u32[]{:S(2)}, u32[]{:S(2)}) collective-permute-start(bf16[256,1536]{1,0:T(8,128)(2,1)S(1)} %pad_maximum_fusion.13.refs_1_), channel_id=1, source_target_pairs={{0,2},{1,3},{2,0},{3,1},{4,6},{5,7},{6,4},{7,5},{8,10},{9,11},{10,... | collective-permute-start | bytes 2359304 | tf_op jit(solution)/shard_map/ffn_backward/ppermute | solution.py:40
  245.3 15.5 %collective-permute-start.33 = (f32[2,128]{1,0:T(2,128)S(1)}, f32[2,128]{1,0:T(2,128)S(1)}, u32[]{:S(2)}, u32[]{:S(2)}) collective-permute-start(f32[2,128]{1,0:T(2,128)S(1)} %add.623), channel_id=1, source_target_pairs={{0,8},{1,9},{2,10},{3,11},{4,12},{5,13},{6,14},{7,15},{8,0},{9,1},... | collective-permute-start | bytes 3080 | tf_op jit(solution)/shard_map/ffn_backward/ppermute | solution.py:40
  272.8 15.3 %collective-permute-start.34 = (bf16[256,1536]{1,0:T(8,128)(2,1)S(1)}, bf16[256,1536]{1,0:T(8,128)(2,1)S(1)}, u32[]{:S(2)}, u32[]{:S(2)}) collective-permute-start(bf16[256,1536]{1,0:T(8,128)(2,1)S(1)} %get-tuple-element.301), channel_id=1, source_target_pairs={{0,4},{1,5},{2,6},{3,7},{4,0},{5,1},{6,2},{7,3},{8,12},{9,13},{10,... | collective-permute-start | bytes 2359304 | tf_op jit(solution)/shard_map/ffn_backward/ppermute | solution.py:40
  274.6 16.2 %collective-permute-start.35 = (bf16[256,1536]{1,0:T(8,128)(2,1)S(1)}, bf16[256,1536]{1,0:T(8,128)(2,1)S(1)}, u32[]{:S(2)}, u32[]{:S(2)}) collective-permute-start(bf16[256,1536]{1,0:T(8,128)(2,1)S(1)} %get-tuple-element.300), channel_id=1, source_target_pairs={{0,2},{1,3},{2,0},{3,1},{4,6},{5,7},{6,4},{7,5},{8,10},{9,11},{10,... | collective-permute-start | bytes 2359304 | tf_op jit(solution)/shard_map/ffn_backward/ppermute | solution.py:40
  292.2 10.5 %collective-permute-start.37 = (bf16[128,1536]{1,0:T(8,128)(2,1)}, bf16[128,1536]{1,0:T(8,128)(2,1)}, u32[]{:S(2)}, u32[]{:S(2)}) collective-permute-start(bf16[128,1536]{1,0:T(8,128)(2,1)} %slice.493), channel_id=1, source_target_pairs={{0,2},{1,3},{2,0},{3,1},{4,6},{5,7},{6,4},{7,5},{8,10},{9,11},{10,... | collective-permute-start | bytes 1179656 | tf_op jit(solution)/shard_map/ffn_backward/ppermute | solution.py:40
  293.7 9.1 %collective-permute-start.38 = (bf16[128,1536]{1,0:T(8,128)(2,1)}, bf16[128,1536]{1,0:T(8,128)(2,1)}, u32[]{:S(2)}, u32[]{:S(2)}) collective-permute-start(bf16[128,1536]{1,0:T(8,128)(2,1)} %slice.492), channel_id=1, source_target_pairs={{0,4},{1,5},{2,6},{3,7},{4,0},{5,1},{6,2},{7,3},{8,12},{9,13},{10,... | collective-permute-start | bytes 1179656 | tf_op jit(solution)/shard_map/ffn_backward/ppermute | solution.py:40
  295.1 7.6 %collective-permute-start.39 = (f32[2,128]{1,0:T(2,128)}, f32[2,128]{1,0:T(2,128)}, u32[]{:S(2)}, u32[]{:S(2)}) collective-permute-start(f32[2,128]{1,0:T(2,128)} %add.628), channel_id=1, source_target_pairs={{0,2},{1,3},{2,0},{3,1},{4,6},{5,7},{6,4},{7,5},{8,10},{9,11},{10,... | collective-permute-start | bytes 3080 | tf_op jit(solution)/shard_map/ffn_backward/ppermute | solution.py:40
  302.4 167.2 %reduce-scatter.3.cloned.1.call-start = ((), (), s32[]{:S(2)}) async-start(), calls=%async_computation.3 | async-start | bytes 7077888 | tf_op jit(solution)/shard_map/ffn_backward/reduce_scatter | solution.py:120
  312.6 4.6 collective-permute-start.40
  319.0 25.6 %collective-permute-start.43 = (bf16[2,2,48,1536]{3,2,1,0:T(8,128)(2,1)}, bf16[2,2,48,1536]{3,2,1,0:T(8,128)(2,1)}, u32[]{:S(2)}, u32[]{:S(2)}) collective-permute-start(bf16[2,2,48,1536]{3,2,1,0:T(8,128)(2,1)} %get-tuple-element.287), channel_id=1, source_target_pairs={{0,2},{1,3},{2,0},{3,1},{4,6},{5,7},{6,4},{7,5},{8,10},{9,11},{10,... | collective-permute-start | bytes 1769480 | tf_op jit(solution)/shard_map/attention_backward/ppermute | solution.py:40
  321.8 22.8 %collective-permute-start.42 = (bf16[2,2,48,1536]{3,2,1,0:T(8,128)(2,1)}, bf16[2,2,48,1536]{3,2,1,0:T(8,128)(2,1)}, u32[]{:S(2)}, u32[]{:S(2)}) collective-permute-start(bf16[2,2,48,1536]{3,2,1,0:T(8,128)(2,1)} %get-tuple-element.289), channel_id=1, source_target_pairs={{0,4},{1,5},{2,6},{3,7},{4,0},{5,1},{6,2},{7,3},{8,12},{9,13},{10,... | collective-permute-start | bytes 1769480 | tf_op jit(solution)/shard_map/attention_backward/ppermute | solution.py:40
  349.8 27.8 %collective-permute-start.44 = (bf16[768,3072]{1,0:T(8,128)(2,1)}, bf16[768,3072]{1,0:T(8,128)(2,1)}, u32[]{:S(2)}, u32[]{:S(2)}) collective-permute-start(bf16[768,3072]{1,0:T(8,128)(2,1)} %convolution_convert_fusion), channel_id=1, source_target_pairs={{0,1},{1,0},{2,3},{3,2},{4,5},{5,4},{6,7},{7,6},{8,9},{9,8},{10,11... | collective-permute-start | bytes 14155784 | tf_op jit(solution)/shard_map/q_k_v_weight_gradients/ppermute | solution.py:40
  366.3 10.8 %collective-permute-start.46 = (bf16[2,48,1536]{2,1,0:T(8,128)(2,1)}, bf16[2,48,1536]{2,1,0:T(8,128)(2,1)S(1)}, u32[]{:S(2)}, u32[]{:S(2)}) collective-permute-start(bf16[2,48,1536]{2,1,0:T(8,128)(2,1)} %fusion.71), channel_id=1, source_target_pairs={{0,4},{1,5},{2,6},{3,7},{4,0},{5,1},{6,2},{7,3},{8,12},{9,13},{10,... | collective-permute-start | bytes 884744 | tf_op jit(solution)/shard_map/attention_backward/ppermute | solution.py:40
  368.9 8.7 %collective-permute-start.45 = (bf16[2,48,1536]{2,1,0:T(8,128)(2,1)}, bf16[2,48,1536]{2,1,0:T(8,128)(2,1)S(1)}, u32[]{:S(2)}, u32[]{:S(2)}) collective-permute-start(bf16[2,48,1536]{2,1,0:T(8,128)(2,1)} %fusion.70), channel_id=1, source_target_pairs={{0,2},{1,3},{2,0},{3,1},{4,6},{5,7},{6,4},{7,5},{8,10},{9,11},{10,... | collective-permute-start | bytes 884744 | tf_op jit(solution)/shard_map/attention_backward/ppermute | solution.py:40
  385.8 17.9 %collective-permute-start.49 = (f32[2,1536]{1,0:T(2,128)S(1)}, f32[2,1536]{1,0:T(2,128)S(1)}, u32[]{:S(2)}, u32[]{:S(2)}) collective-permute-start(f32[2,1536]{1,0:T(2,128)S(1)} %pad_maximum_fusion.14), channel_id=1, source_target_pairs={{0,1},{1,0},{2,3},{3,2},{4,5},{5,4},{6,7},{7,6},{8,9},{9,8},{10,11... | collective-permute-start | bytes 36872 | tf_op jit(solution)/shard_map/input_gradient/ppermute | solution.py:40
  394.7 28.4 %collective-permute-start.48 = (bf16[2,2,48,3072]{3,2,1,0:T(8,128)(2,1)S(1)}, bf16[2,2,48,3072]{3,2,1,0:T(8,128)(2,1)S(1)}, u32[]{:S(2)}, u32[]{:S(2)}) collective-permute-start(bf16[2,2,48,3072]{3,2,1,0:T(8,128)(2,1)S(1)} %get-tuple-element.277), channel_id=1, source_target_pairs={{0,2},{1,3},{2,0},{3,1},{4,6},{5,7},{6,4},{7,5},{8,10},{9,11},{10,... | collective-permute-start | bytes 3538952 | tf_op jit(solution)/shard_map/q_k_v_weight_gradients/ppermute | solution.py:40
  396.2 28.4 %collective-permute-start.47 = (bf16[2,2,48,3072]{3,2,1,0:T(8,128)(2,1)S(1)}, bf16[2,2,48,3072]{3,2,1,0:T(8,128)(2,1)S(1)}, u32[]{:S(2)}, u32[]{:S(2)}) collective-permute-start(bf16[2,2,48,3072]{3,2,1,0:T(8,128)(2,1)S(1)} %get-tuple-element.278), channel_id=1, source_target_pairs={{0,4},{1,5},{2,6},{3,7},{4,0},{5,1},{6,2},{7,3},{8,12},{9,13},{10,... | collective-permute-start | bytes 3538952 | tf_op jit(solution)/shard_map/q_k_v_weight_gradients/ppermute | solution.py:40
  400.7 44.5 %collective-permute-start.56 = (bf16[48,1536]{1,0:T(8,128)(2,1)S(1)}, bf16[48,1536]{1,0:T(8,128)(2,1)S(1)}, u32[]{:S(2)}, u32[]{:S(2)}) collective-permute-start(bf16[48,1536]{1,0:T(8,128)(2,1)S(1)} %get-tuple-element.308), channel_id=1, source_target_pairs={{0,24},{1,25},{2,26},{3,27},{4,28},{5,29},{6,30},{7,31},{8,16},{9,... | collective-permute-start | bytes 442376 | tf_op jit(solution)/shard_map/weight_gradients_to_owners/ppermute | solution.py:40
  402.1 45.6 %collective-permute-start.57 = (bf16[48,1536]{1,0:T(8,128)(2,1)S(1)}, bf16[48,1536]{1,0:T(8,128)(2,1)S(1)}, u32[]{:S(2)}, u32[]{:S(2)}) collective-permute-start(bf16[48,1536]{1,0:T(8,128)(2,1)S(1)} %get-tuple-element.309), channel_id=1, source_target_pairs={{0,16},{1,17},{2,18},{3,19},{4,20},{5,21},{6,22},{7,23},{8,24},{9,... | collective-permute-start | bytes 442376 | tf_op jit(solution)/shard_map/weight_gradients_to_owners/ppermute | solution.py:40
  424.6 5.6 %collective-permute-start.52 = (f32[2,1536]{1,0:T(2,128)S(1)}, f32[2,1536]{1,0:T(2,128)S(1)}, u32[]{:S(2)}, u32[]{:S(2)}) collective-permute-start(f32[2,1536]{1,0:T(2,128)S(1)} %add.650), channel_id=1, source_target_pairs={{0,8},{1,9},{2,10},{3,11},{4,12},{5,13},{6,14},{7,15},{8,0},{9,1},... | collective-permute-start | bytes 36872 | tf_op jit(solution)/shard_map/weight_gradients_to_owners/ppermute | solution.py:40
  426.4 14.8 %collective-permute-start.51 = (bf16[2,48,3072]{2,1,0:T(8,128)(2,1)S(1)}, bf16[2,48,3072]{2,1,0:T(8,128)(2,1)S(1)}, u32[]{:S(2)}, u32[]{:S(2)}) collective-permute-start(bf16[2,48,3072]{2,1,0:T(8,128)(2,1)S(1)} %fusion.55), channel_id=1, source_target_pairs={{0,4},{1,5},{2,6},{3,7},{4,0},{5,1},{6,2},{7,3},{8,12},{9,13},{10,... | collective-permute-start | bytes 1769480 | tf_op jit(solution)/shard_map/weight_gradients_to_owners/ppermute | solution.py:40
  428.3 14.3 %collective-permute-start.50 = (bf16[2,48,3072]{2,1,0:T(8,128)(2,1)S(1)}, bf16[2,48,3072]{2,1,0:T(8,128)(2,1)S(1)}, u32[]{:S(2)}, u32[]{:S(2)}) collective-permute-start(bf16[2,48,3072]{2,1,0:T(8,128)(2,1)S(1)} %fusion.54), channel_id=1, source_target_pairs={{0,2},{1,3},{2,0},{3,1},{4,6},{5,7},{6,4},{7,5},{8,10},{9,11},{10,... | collective-permute-start | bytes 1769480 | tf_op jit(solution)/shard_map/weight_gradients_to_owners/ppermute | solution.py:40
  430.2 17.5 %collective-permute-start.58 = (bf16[48,1536]{1,0:T(8,128)(2,1)S(1)}, bf16[48,1536]{1,0:T(8,128)(2,1)S(1)}, u32[]{:S(2)}, u32[]{:S(2)}) collective-permute-start(bf16[48,1536]{1,0:T(8,128)(2,1)S(1)} %get-tuple-element.310), channel_id=1, source_target_pairs={{0,8},{1,9},{2,10},{3,11},{4,12},{5,13},{6,14},{7,15},{8,0},{9,1},... | collective-permute-start | bytes 442376 | tf_op jit(solution)/shard_map/weight_gradients_to_owners/ppermute | solution.py:40
  443.2 11.9 %collective-permute-start.53 = (bf16[48,3072]{1,0:T(8,128)(2,1)S(1)}, bf16[48,3072]{1,0:T(8,128)(2,1)S(1)}, u32[]{:S(2)}, u32[]{:S(2)}) collective-permute-start(bf16[48,3072]{1,0:T(8,128)(2,1)S(1)} %get-tuple-element.295), channel_id=1, source_target_pairs={{0,24},{1,25},{2,26},{3,27},{4,28},{5,29},{6,30},{7,31},{8,16},{9,... | collective-permute-start | bytes 884744 | tf_op jit(solution)/shard_map/weight_gradients_to_owners/ppermute | solution.py:40
  444.7 24.7 %collective-permute-start.54 = (bf16[48,3072]{1,0:T(8,128)(2,1)S(1)}, bf16[48,3072]{1,0:T(8,128)(2,1)S(1)}, u32[]{:S(2)}, u32[]{:S(2)}) collective-permute-start(bf16[48,3072]{1,0:T(8,128)(2,1)S(1)} %get-tuple-element.296), channel_id=1, source_target_pairs={{0,16},{1,17},{2,18},{3,19},{4,20},{5,21},{6,22},{7,23},{8,24},{9,... | collective-permute-start | bytes 884744 | tf_op jit(solution)/shard_map/weight_gradients_to_owners/ppermute | solution.py:40
  445.2 24.2 %collective-permute-start.55 = (bf16[48,3072]{1,0:T(8,128)(2,1)S(1)}, bf16[48,3072]{1,0:T(8,128)(2,1)S(1)}, u32[]{:S(2)}, u32[]{:S(2)}) collective-permute-start(bf16[48,3072]{1,0:T(8,128)(2,1)S(1)} %get-tuple-element.297), channel_id=1, source_target_pairs={{0,8},{1,9},{2,10},{3,11},{4,12},{5,13},{6,14},{7,15},{8,0},{9,1},... | collective-permute-start | bytes 884744 | tf_op jit(solution)/shard_map/weight_gradients_to_owners/ppermute | solution.py:40
  448.5 21.1 %collective-permute-start.59 = (f32[2,1536]{1,0:T(2,128)S(1)}, f32[2,1536]{1,0:T(2,128)S(1)}, u32[]{:S(2)}, u32[]{:S(2)}) collective-permute-start(f32[2,1536]{1,0:T(2,128)S(1)} %add.671), channel_id=1, source_target_pairs={{0,16},{1,17},{2,18},{3,19},{4,20},{5,21},{6,22},{7,23},{8,24},{9,... | collective-permute-start | bytes 36872 | tf_op jit(solution)/shard_map/weight_gradients_to_owners/ppermute | solution.py:40
  470.8 9.2 %collective-permute-start.61 = (bf16[48,2048]{1,0:T(8,128)(2,1)S(1)}, bf16[48,2048]{1,0:T(8,128)(2,1)S(1)}, u32[]{:S(2)}, u32[]{:S(2)}) collective-permute-start(bf16[48,2048]{1,0:T(8,128)(2,1)S(1)} %get-tuple-element.323), channel_id=1, source_target_pairs={{0,2},{1,3},{2,0},{3,1},{4,6},{5,7},{6,4},{7,5},{8,10},{9,11},{10,... | collective-permute-start | bytes 589832 | tf_op jit(solution)/shard_map/weight_gradients_to_owners/ppermute | solution.py:40
  471.4 8.6 %collective-permute-start.62 = (bf16[48,2048]{1,0:T(8,128)(2,1)S(1)}, bf16[48,2048]{1,0:T(8,128)(2,1)S(1)}, u32[]{:S(2)}, u32[]{:S(2)}) collective-permute-start(bf16[48,2048]{1,0:T(8,128)(2,1)S(1)} %get-tuple-element.322), channel_id=1, source_target_pairs={{0,4},{1,5},{2,6},{3,7},{4,0},{5,1},{6,2},{7,3},{8,12},{9,13},{10,... | collective-permute-start | bytes 589832 | tf_op jit(solution)/shard_map/weight_gradients_to_owners/ppermute | solution.py:40
  472.3 8.0 %collective-permute-start.63 = (bf16[48,2048]{1,0:T(8,128)(2,1)S(1)}, bf16[48,2048]{1,0:T(8,128)(2,1)S(1)}, u32[]{:S(2)}, u32[]{:S(2)}) collective-permute-start(bf16[48,2048]{1,0:T(8,128)(2,1)S(1)} %get-tuple-element.321), channel_id=1, source_target_pairs={{0,6},{1,7},{2,4},{3,5},{4,2},{5,3},{6,0},{7,1},{8,14},{9,15},{10,... | collective-permute-start | bytes 589832 | tf_op jit(solution)/shard_map/weight_gradients_to_owners/ppermute | solution.py:40
  474.3 5.6 %collective-permute-start.60 = (f32[2,1536]{1,0:T(2,128)S(1)}, f32[2,1536]{1,0:T(2,128)S(1)}, u32[]{:S(2)}, u32[]{:S(2)}) collective-permute-start(f32[2,1536]{1,0:T(2,128)S(1)} %add.672), channel_id=1, source_target_pairs={{0,2},{1,3},{2,0},{3,1},{4,6},{5,7},{6,4},{7,5},{8,10},{9,11},{10,... | collective-permute-start | bytes 36872 | tf_op jit(solution)/shard_map/weight_gradients_to_owners/ppermute | solution.py:40
  (65 other events, 437.4 us)
Sparse Core Ops, SparseCore 0:
  75.3 87.8 all-gather.1
  302.5 38.8 reduce-scatter.4
  362.2 77.4 reduce-scatter.2

commit v7 on v6

--- a/solution.py
+++ b/solution.py
@@ -287,20 +287,15 @@
 
     with jax.named_scope("phase_0"):
         cuts = column_cuts_kernel(w_gate, w_up, p, 2 * ff_rows)
-        up, down, came_x, came_y, came_xy = tied(
-            along_z(local, up_pairs),
-            along_z(local, down_pairs),
-            swap(cuts[1], 2),
-            swap(cuts[2], 4),
-            swap(cuts[3], 6),
-        )
+        crossing = (swap(cuts[1], 2), swap(cuts[2], 4), swap(cuts[3], 6))
+        up, down = tied(along_z(local, up_pairs), along_z(local, down_pairs))
     with jax.named_scope("phase_1"):
         b = near_side(up, down)
         a, b, passing = tied(local, b, to_pass_on(up, down))
-        a_x, b_y, far, first = tied(
-            swap(a, 2), swap(b, 4), along_z(a, far_pairs), along_z(passing, out_pairs)
+        a_x, b_y, far, first, *crossing = tied(
+            swap(a, 2), swap(b, 4), along_z(a, far_pairs), along_z(passing, out_pairs), *crossing
         )
-        ffn = merged((cuts[0], came_x, came_y, came_xy), w_down, p)
+        ffn = merged((cuts[0], *crossing), w_down, p)
     with jax.named_scope("phase_2"):
         a2, b2, far = tied(in_order(x, a, a_x), in_order(y, b, b_y), far)
         near_1 = jnp.stack([a2, b2])
@@ -331,31 +326,81 @@
     return gathered, ffn
 
 
-def halves(parts):
-    half = parts[0].shape[2] // 2
-    return [part[:, :, :half] for part in parts], [part[:, :, half:] for part in parts]
-
-
-def plane_step_1(parts, place_bits):
-    z, y, x, c = place_bits
-    a, b = halves(parts)
-    return (swap(summed(a, 1 - y, 1).astype(BF), 4), swap(summed(b, 1 - x, 0).astype(BF), 2))
-
-
-def plane_step_2(parts, came, place_bits):
-    z, y, x, c = place_bits
-    a, b = halves(parts)
-    a = [summed(a, y, 1), came[0]]
-    b = [summed(b, x, 0), came[1]]
-    moving = (swap(summed(a, 1 - x, 0).astype(BF), 2), swap(summed(b, 1 - y, 0).astype(BF), 4))
-    return (a, b), moving
-
-
-def plane_step_3(sums, came, place_bits):
-    z, y, x, c = place_bits
-    a = summed(sums[0], x, 0) + came[0].astype(F32)
-    b = summed(sums[1], y, 0) + came[1].astype(F32)
-    return jnp.concatenate([a, b])
+def block_sums(sets, tables, rows, dtype):
+    columns = sets[0][0].shape[1]
+    count = tables[0][0].shape[0]
+    if rows % 16:
+        results = []
+        for arrays, table in zip(sets, tables):
+            blocks = [a.reshape(-1, rows, columns)[t] for a, t in zip(arrays, table)]
+            total = sum(block.astype(F32) for block in blocks)
+            results.append(total.astype(dtype).reshape(count * rows, columns))
+        return results
+    sizes = [len(arrays) for arrays in sets]
+    inputs = [array for arrays in sets for array in arrays]
+    table = jnp.stack([t for group in tables for t in group]).astype(jnp.int32)
+
+    def kernel(table, *refs):
+        at = 0
+        for size, out in zip(sizes, refs[len(inputs) :]):
+            total = refs[at][...].astype(F32)
+            for ref in refs[at + 1 : at + size]:
+                total += ref[...].astype(F32)
+            out[...] = total.astype(dtype)
+            at += size
+
+    def block(k):
+        return pl.BlockSpec((rows, columns), lambda i, table: (table[k, i], 0))
+
+    return pl.pallas_call(
+        kernel,
+        grid_spec=pltpu.PrefetchScalarGridSpec(
+            num_scalar_prefetch=1,
+            grid=(count,),
+            in_specs=[block(k) for k in range(len(inputs))],
+            out_specs=[pl.BlockSpec((rows, columns), lambda i, table: (i, 0))] * len(sets),
+        ),
+        out_shape=[jax.ShapeDtypeStruct((count * rows, columns), dtype)] * len(sets),
+        compiler_params=pltpu.CompilerParams(vmem_limit_bytes=FFN_VMEM),
+        cost_estimate=NO_COST,
+        name="block_sums",
+    )(table, *inputs)
+
+
+class PlaneSum:
+    def __init__(self, parts, rows, place_bits):
+        self.parts, self.rows, self.place_bits = parts, rows, place_bits
+        self.tall = parts[0].shape[0] // 8
+
+    def block(self, x, y, half):
+        return jnp.atleast_1d(4 * x + 2 * y + half)
+
+    def sums(self, a, b, more_a, more_b, at_a, at_b, dtype):
+        a_arrays, b_arrays = [*self.parts, *more_a], [*self.parts, *more_b]
+        a_tables = [a, a] + [jnp.atleast_1d(i) for i in at_a]
+        b_tables = [b, b] + [jnp.atleast_1d(i) for i in at_b]
+        return block_sums([a_arrays, b_arrays], [a_tables, b_tables], self.tall, dtype)
+
+    def step_1(self):
+        z, y, x, c = self.place_bits
+        i = jnp.arange(2)
+        a, b = self.sums(self.block(i, 1 - y, 0), self.block(1 - x, i, 1), [], [], [], [], BF)
+        return (swap(a, 4), swap(b, 2))
+
+    def step_2(self, came):
+        z, y, x, c = self.place_bits
+        self.came = came
+        a, b = self.block(1 - x, y, 0), self.block(x, 1 - y, 1)
+        a, b = self.sums(a, b, [came[0]], [came[1]], [1 - x], [1 - y], BF)
+        return (swap(a, 2), swap(b, 4))
+
+    def step_3(self, came):
+        z, y, x, c = self.place_bits
+        a, b = self.block(x, y, 0), self.block(x, y, 1)
+        more_a, more_b = [self.came[0], came[0]], [self.came[1], came[1]]
+        a, b = self.sums(a, b, more_a, more_b, [x, 0], [y, 0], F32)
+        shape = (self.tall // self.rows, self.rows, -1)
+        return jnp.concatenate([a.reshape(shape), b.reshape(shape)])
 
 
 def reordered(count, rows, order):
@@ -449,26 +494,35 @@
     return value * cosine + other * sine
 
 
+def lanes_of(shape):
+    return lax.broadcasted_iota(jnp.int32, shape, 1)
+
+
 def head_of(value, i):
-    size = value.shape[1]
-    period = 3 * LANES
-    group = value[:, i // 4 * period : (i // 4 + 1) * period]
-    if i % 4:
-        group = pltpu.roll(group, period - i % 4 * HEAD_SIZE, 1)
-    head = group[:, :LANES]
-    lane = lax.broadcasted_iota(jnp.int32, head.shape, 1)
-    return jnp.where(lane < HEAD_SIZE, head, 0.0)
+    start = i * HEAD_SIZE
+    window = start // LANES * LANES
+    offset = start - window
+    size = LANES if offset + HEAD_SIZE <= LANES else 2 * LANES
+    head = value[:, window : window + size]
+    if offset:
+        head = pltpu.roll(head, size - offset, 1)
+    head = head[:, :LANES]
+    return jnp.where(lanes_of(head.shape) < HEAD_SIZE, head, 0.0)
 
 
 def side_by_side(heads):
-    rows = heads[0].shape[0]
-    total = None
-    for i, head in enumerate(heads):
-        wide = jnp.concatenate([head, jnp.zeros((rows, 2 * LANES), head.dtype)], axis=1)
-        if i:
-            wide = pltpu.roll(wide, i * HEAD_SIZE, 1)
-        total = wide if total is None else total + wide
-    return total
+    lane = lanes_of(heads[0].shape)
+    second = pltpu.roll(heads[1], 96, 1)
+    third = pltpu.roll(heads[2], 64, 1)
+    fourth = pltpu.roll(heads[3], 32, 1)
+    return jnp.concatenate(
+        [
+            jnp.where(lane < 96, heads[0], second),
+            jnp.where(lane < 64, second, third),
+            jnp.where(lane < 32, third, fourth),
+        ],
+        axis=1,
+    )
 
 
 def row_softmax(query, key):
@@ -780,6 +834,61 @@
     return tuple(outs)
 
 
+def input_gradient(grad_raw, weights, tokens, inv_scale, gain, grad_res):
+    count, wide = grad_raw.shape
+    width = tokens.shape[1]
+    tile = 2 * FFN_TILE
+    steps = wide // tile
+
+    def kernel(grads, w, tokens, inv_scale, gain, grad_res, out, gain_grad, total):
+        j = pl.program_id(0)
+        part = lax.dot_general(
+            grads[...], w[...], (((1,), (1,)), ((), ())), preferred_element_type=F32
+        )
+
+        @pl.when(j == 0)
+        def _():
+            total[...] = part
+
+        @pl.when(j > 0)
+        def _():
+            total[...] += part
+
+        @pl.when(j == steps - 1)
+        def _():
+            up, field, inv = total[...], tokens[...].astype(F32), inv_scale[...]
+            gain_grad[...] = jnp.sum(up * field * inv, axis=0, keepdims=True)
+            scaled = up * gain[...]
+            mean = jnp.mean(scaled * field, axis=1, keepdims=True)
+            grad = inv * scaled - field * (inv * inv * inv) * mean
+            out[...] = (grad_res[...] + grad).astype(BF)
+
+    return pl.pallas_call(
+        kernel,
+        grid=(steps,),
+        out_shape=[
+            jax.ShapeDtypeStruct((count, width), BF),
+            jax.ShapeDtypeStruct((1, width), F32),
+        ],
+        in_specs=[
+            pl.BlockSpec((count, tile), lambda j: (0, j)),
+            pl.BlockSpec((width, tile), lambda j: (0, j)),
+            whole(tokens),
+            whole(inv_scale),
+            whole(gain),
+            whole(grad_res),
+        ],
+        out_specs=[
+            pl.BlockSpec((count, width), lambda j: (0, 0)),
+            pl.BlockSpec((1, width), lambda j: (0, 0)),
+        ],
+        scratch_shapes=[pltpu.VMEM((count, width), F32)],
+        compiler_params=pltpu.CompilerParams(vmem_limit_bytes=FFN_VMEM),
+        cost_estimate=NO_COST,
+        name="input_gradient",
+    )(grad_raw, weights, tokens, inv_scale, gain, grad_res)
+
+
 def products(pairs, dtype):
     tokens, rows = pairs[0][0].shape
     columns = pairs[0][1].shape[1]
@@ -897,32 +1006,38 @@
     rest = [1 << k for k in range(4, n.bit_length() - 2)]
 
     with jax.named_scope("ffn_backward"):
-        grad_low, sums = tied(grad_out.astype(BF), sums)
-
-        def near_backward(pieces, came):
-            value = sums + came
-            for mask in rest:
-                value = value + swap(value, mask)
-            near = ffn_backward_beside(pieces, gate_near, up_near, wb, wd)
-            return (value, swap(value, 8), *near)
-
-        d_far, sums, sums_came, m_near, d_near, g_near = split_gather(
-            grad_low, (swap(sums, 1),), near_backward
+        def near_backward(pieces, sums):
+            return (
+                sums,
+                swap(sums, 1),
+                *ffn_backward_beside(pieces, gate_near, up_near, wb, wd),
+            )
+
+        d_far, sums, came, m_near, d_near, g_near = split_gather(
+            grad_out.astype(BF), (sums,), near_backward
         )
+        sums = sums + came
+        for mask in rest:
+            sums = sums + swap(sums, mask)
         m_far, g_far = ffn_backward(d_far, pre_far, wb, wd)
-        m_far = m_far.astype(BF)
-        m_near, m_far, sums, sums_came = tied(m_near, m_far, sums, sums_came)
-        sums = sums + sums_came
-        g_both = products([(near, g_near), (far, g_far)], BF)
-        g_down = products([(hid_near, d_near), (hid_far, d_far)], BF)
-        g_both, g_down = sum_to_owners(g_both), sum_to_owners(g_down)
-
-        def later(sums, sums_came):
-            sums = sums + sums_came
-            return (sums, swap(sums, 2))
-
-        grad_mid, sums, sums_came = split_reduce(m_near, m_far, (sums, swap(sums, high)), later)
-        sums = sums + sums_came
+        m_near, m_far, sums = tied(m_near, m_far.astype(BF), sums)
+        beside = (
+            products([(near, g_near), (far, g_far)], BF),
+            sums,
+            swap(sums, 8),
+        )
+
+        owned_both = []
+
+        def later(g_both, sums, came):
+            owned_both.append(sum_to_owners(g_both))
+            sums = sums + came
+            g_down = products([(hid_near, d_near), (hid_far, d_far)], BF)
+            return (g_down, sums, swap(sums, high))
+
+        grad_mid, g_down, sums, came = split_reduce(m_near, m_far, beside, later)
+        g_both = owned_both[0]
+        sums = sums + came
         high_part = grad_mid.astype(BF)
         low_part = (grad_mid - high_part.astype(F32)).astype(BF)
         grad_mid = mm_t(high_part, to_column) + mm_t(low_part, to_column)
@@ -931,45 +1046,52 @@
         grad_gain_mid, grad_res = norm_back(grad_mid, hidden_res, inv_ffn, gain_mid)
         grad_res = grad_out + grad_res
         res_low = grad_res.astype(BF)
-        wo_came, sums_came = tied(swap(t_mm(mixed_theirs, res_low).astype(BF), 1), swap(sums, 4))
-        sums = sums + sums_came
-        loss = sums[0, 0] / (sums[1, 0] * width)
-        shape = (2, 2, planes, rows, -1)
-        g_wo = [t_mm(mixed_mine, res_low).reshape(shape), wo_came.reshape(shape)]
-        wo_moving = plane_step_1(g_wo, bits)
+        wo_came, came = tied(swap(t_mm(mixed_theirs, res_low).astype(BF), 1), swap(sums, 2))
+        sums = sums + came
+        g_wo = PlaneSum([t_mm(mixed_mine, res_low), wo_came], rows, bits)
+        wo_moving = g_wo.step_1()
         grad_mixed = mm_t(res_low, wo).astype(BF)
         grad_raw = attention_backward(grad_mixed, query, key, value, cosine, sine)
         *wo_came, grad_raw = tied(*wo_moving, grad_raw)
-        g_wo, wo_moving = plane_step_2(g_wo, wo_came, bits)
+        wo_moving = g_wo.step_2(wo_came)
 
     with jax.named_scope("q_k_v_weight_gradients"):
         qkv_came = swap(t_mm(normed_theirs, grad_raw).astype(BF), 1)
         g_qkv = t_mm(normed_mine, grad_raw)
-        qkv_came, g_qkv, grad_raw, *wo_came = tied(qkv_came, g_qkv, grad_raw, *wo_moving)
-        g_wo = plane_step_3(g_wo, wo_came, bits)
-        g_qkv = [g_qkv.reshape(shape), qkv_came.reshape(shape)]
-        qkv_moving = plane_step_1(g_qkv, bits)
+        qkv_came, g_qkv, grad_raw, came, g_both, g_down, *wo_came = tied(
+            qkv_came, g_qkv, grad_raw, swap(sums, 4), g_both, g_down, *wo_moving
+        )
+        g_down = sum_to_owners(g_down)
+        sums = sums + came
+        loss = sums[0, 0] / (sums[1, 0] * width)
+        g_qkv = PlaneSum([g_qkv, qkv_came], rows, bits)
+        qkv_moving = g_qkv.step_1()
+        g_wo = g_wo.step_3(wo_came)
+        if planes == 4:
+            wo_moving = direct([g_wo], z)
 
     with jax.named_scope("input_gradient"):
-        grad_in = mm_t(grad_raw, wqkv)
-        grad_gain_in, grad_tokens = norm_back(grad_in, inputs_f, inv_attn, gain_in)
-        input_grad = (grad_res + grad_tokens).astype(BF)
-        gains = jnp.stack([grad_gain_in, grad_gain_mid])
-        gains_came = swap(gains, 1)
+        input_grad, grad_gain_in = input_gradient(
+            grad_raw, gathered, tokens, inv_attn, gain_in[None], grad_res
+        )
+        gains = jnp.concatenate([grad_gain_in, grad_gain_mid[None]])
 
     with jax.named_scope("weight_gradients_to_owners"):
-        *qkv_came, gains_came, gains = tied(*qkv_moving, gains_came, gains)
-        gains = gains + gains_came
-        g_qkv, qkv_moving = plane_step_2(g_qkv, qkv_came, bits)
-        *qkv_came, gains_came = tied(*qkv_moving, swap(gains, 8))
-        gains = gains + gains_came
-        g_qkv = plane_step_3(g_qkv, qkv_came, bits)
         if planes == 4:
-            moving = direct([g_qkv], z) + direct([g_wo], z)
-        gains_came = swap(gains, high)
+            qkv_0, qkv_1, gains, wo_0, wo_1, wo_2 = tied(*qkv_moving, gains, *wo_moving)
+            g_wo = owned([g_wo], (wo_0, wo_1, wo_2), z)
+            qkv_came = (qkv_0, qkv_1)
+        else:
+            *qkv_came, gains = tied(*qkv_moving, gains)
+            g_wo = z_reduce([g_wo])
+        qkv_moving = g_qkv.step_2(qkv_came)
+        for mask in (1, 8, high):
+            gains = gains + swap(gains, mask)
+        *qkv_came, gains, g_both, g_down = tied(*qkv_moving, gains, g_both, g_down)
+        g_qkv = g_qkv.step_3(qkv_came)
+        if planes == 4:
+            moving = direct([g_qkv], z)
         g_both = g_both.reshape(4, rows, 2 * units)
-        gains, gains_came, g_both = tied(gains, gains_came, g_both)
-        gains = gains + gains_came
         came = [pick(g_both, p ^ r, 0) for r in range(4)]
         gains_came, *moved = tied(swap(gains, 2), *[swap(came[r], r << 1) for r in (1, 2, 3)])
         gains = gains + gains_came
@@ -979,10 +1101,9 @@
         gains = gains + swap(gains, 4)
         g_gains = lax.dynamic_slice_in_dim(gains, position * rows, rows, 1)
         if planes == 4:
-            g_qkv = owned([g_qkv], moving[:3], z)
-            g_wo = owned([g_wo], moving[3:], z)
+            g_qkv = owned([g_qkv], moving, z)
         else:
-            g_qkv, g_wo = z_reduce([g_qkv]), z_reduce([g_wo])
+            g_qkv = z_reduce([g_qkv])
         g_wq = g_qkv[:, :width]
         g_wk = g_qkv[:, width : width + kv_width]
         g_wv = g_qkv[:, width + kv_width :]

time: 500 us -> 483 us (0.966)
  Pallas kernels: 84 us -> 113 us
  waiting for transfers between devices: 163 us -> 141 us
  other arithmetic: 40.5 us -> 32.2 us
  local copies, waits for them, and re-layouts: 49.4 us -> 41.4 us
  starting transfers between devices: 73.6 us -> 68.1 us
    pallas_call x0 -> x7, Pallas kernels: none -> 29.4 us  [the longest x6 20.1 us: block_sums(): pl.pallas_call(kernel, grid_spec=pltpu.PrefetchScalarGridSpec(num_scalar_...]
    ppermute x60, waiting for transfers between devices: 156 us -> 131 us  [swap(): return lax.ppermute(value, 'dp', [(i, i ^ mask) for i in range(n)])]
    slice x5 -> x0, local copies, waits for them, and re-layouts: 8.3 us -> none  [the longest x4 6.9 us: halves(): part[:, :, half:]]
    add x12 -> x9, other arithmetic: 9.45 us -> 1.45 us  [the longest x4 1.41 us: body(): sums = sums + came]
    convert_element_type x8 -> x1, other arithmetic: 6.07 us -> 0.08 us  [body(): grad_out.astype(BF)]
    dot_general x17 -> x16, matrix products: 64.1 us -> 61.5 us  [dot(): return lax.dot_general(a, b, (dims, ((), ())), preferred_element_type=F32)]
    unnamed x141 -> x137, local copies, waits for them, and re-layouts: 11.2 us -> 10.9 us
  transfers between devices with their start and end apart: 68 -> 68, of which waited for: 38 -> 36; matrix products, arithmetic and copies ran while one was open for 23% -> 20% of each run, Pallas kernels for 17% -> 23%
where the time goes in v7:
time: 483 us; the launch traced here: 475 us
  waiting for transfers between devices  141 us (29%)
  Pallas kernels  113 us (23%)
  starting transfers between devices  68.1 us (14%)
  matrix products  61.5 us (13%)
  local copies, waits for them, and re-layouts  41.4 us (9%)
  other arithmetic  32.2 us (7%)
  between operations  17.8 us (4%)
    ppermute x60, waiting for transfers between devices, swap(): return lax.ppermute(value, 'dp', [(i, i ^ mask) for i in range(n)])  131 us
    dot_general x16, matrix products, dot(): return lax.dot_general(a, b, (dims, ((), ())), preferred_element_type=F32)  61.5 us
    ppermute x60, starting transfers between devices, swap(): return lax.ppermute(value, 'dp', [(i, i ^ mask) for i in range(n)])  53.8 us
    pallas_call x6, Pallas kernels, block_sums(): pl.pallas_call(kernel, grid_spec=pltpu.PrefetchScalarGridSpec(num_scalar_...  20.1 us
    dynamic_update_slice x16, local copies, waits for them, and re-layouts, place(): return lax.dynamic_update_slice(out, piece, where)  17.3 us
    pallas_call x1, Pallas kernels, attention_backward(): pl.pallas_call(kernel, grid=(count // SEQ, steps), out_shape=jax.ShapeDty...  16.6 us
    pallas_call x2, Pallas kernels, products(): pl.pallas_call(kernel, grid=(columns // tile,), out_shape=jax.ShapeDtypeS...  16.3 us
    pallas_call x1, Pallas kernels, ffn_backward_beside(): pl.pallas_call(kernel, grid=(steps,), out_shape=[m_shape] + [jax.ShapeDty...  14.9 us
  transfers between devices with their start and end apart: 68, of which 36 were waited for; matrix products, arithmetic and copies ran while one was open for 20% of the time, Pallas kernels for 23%

profile of v7, /device:TPU:0, one launch (start us, length us, event | category | flops | bytes accessed | tf_op | source)
XLA Modules:
  0.0 475.2 jit_solution(10317176489715838276)
XLA Ops:
  8.6 1.9 packed.1
  10.5 5.1 %collective-permute-start = (bf16[48,4736]{1,0:T(8,128)(2,1)}, bf16[48,4736]{1,0:T(8,128)(2,1)S(1)}, u32[]{:S(2)}, u32[]{:S(2)}) collective-permute-start(bf16[48,4736]{1,0:T(8,128)(2,1)} %packed.1), channel_id=1, source_target_pairs={{0,8},{1,9},{2,10},{3,11},{4,12},{5,13},{6,14},{7,15},{8,16},{9,17... | collective-permute-start | bytes 1363976 | tf_op jit(solution)/shard_map/phase_0/ppermute | solution.py:77
  16.9 2.1 column_cuts.1
  22.0 3.5 collective-permute-done
  25.5 4.0 collective-permute-done.1
  31.2 5.2 %collective-permute-start.4 = (bf16[48,4736]{1,0:T(8,128)(2,1)S(1)}, bf16[48,4736]{1,0:T(8,128)(2,1)}, u32[]{:S(2)}, u32[]{:S(2)}) collective-permute-start(bf16[48,4736]{1,0:T(8,128)(2,1)S(1)} %copy-done.34), channel_id=1, source_target_pairs={{0,16},{1,17},{2,18},{3,19},{4,20},{5,21},{6,22},{7,23},{24,8},{25... | collective-permute-start | bytes 1363976 | tf_op jit(solution)/shard_map/phase_1/ppermute | solution.py:77
  42.3 6.4 %collective-permute-done.8.refs_3_ = bf16[48,2048]{1,0:T(8,128)(2,1)S(1)} collective-permute-done((bf16[48,2048]{1,0:T(8,128)(2,1)}, bf16[48,2048]{1,0:T(8,128)(2,1)S(1)}, u32[]{:S(2)}, u32[]{:S(2)}) %collective-permute-start.8) | collective-permute-done | bytes 196640 | tf_op jit(solution)/shard_map/phase_0/ppermute | solution.py:40
  48.7 2.5 collective-permute-done.3
  59.1 2.5 merged.1
  63.0 3.1 collective-permute-done.11
  66.1 4.8 %collective-permute-done.10 = bf16[2,48,4736]{2,1,0:T(8,128)(2,1)S(1)} collective-permute-done((bf16[2,48,4736]{2,1,0:T(8,128)(2,1)S(1)}, bf16[2,48,4736]{2,1,0:T(8,128)(2,1)S(1)}, u32[]{:S(2)}, u32[]{:S(2)}) %collective-permute-start.10) | collective-permute-done | bytes 909344 | tf_op jit(solution)/shard_map/phase_2/ppermute | solution.py:40
  72.3 1.8 broadcast_select_fusion
  77.5 2.2 bitcast_dynamic-update-slice_fusion.13
  82.1 5.2 %collective-permute-done.12 = bf16[48,4736]{1,0:T(8,128)(2,1)} collective-permute-done((bf16[48,4736]{1,0:T(8,128)(2,1)}, bf16[48,4736]{1,0:T(8,128)(2,1)}, u32[]{:S(2)}, u32[]{:S(2)}) %collective-permute-start.12) | collective-permute-done | bytes 454688 | tf_op jit(solution)/shard_map/phase_3/ppermute | solution.py:40
  97.9 16.1 %collective-permute-done.15 = bf16[2,48,4736]{2,1,0:T(8,128)(2,1)S(1)} collective-permute-done((bf16[2,48,4736]{2,1,0:T(8,128)(2,1)S(1)}, bf16[2,48,4736]{2,1,0:T(8,128)(2,1)S(1)}, u32[]{:S(2)}, u32[]{:S(2)}) %collective-permute-start.15) | collective-permute-done | bytes 909344 | tf_op jit(solution)/shard_map/phase_4/ppermute | solution.py:40
  120.2 1.8 collective-permute-done.19
  128.0 8.3 %fusion.q_raw.k_raw.v_raw = f32[256,3072]{1,0:T(8,128)} fusion(bf16[256,1536]{1,0:T(8,128)(2,1)S(1)} %fusion.35, bf16[1536,4736]{1,0:T(8,128)(2,1)} %bitcast.204), kind=kOutput, calls=%fused_computation | convolution fusion | flops 2415919104 | bytes 13369344 | tf_op jit(solution)/shard_map/attention_forward/dot_general | solution.py:23
  136.3 14.6 %attention_forward.1 = (bf16[256,1536]{1,0:T(8,128)(2,1)}, bf16[256,768]{1,0:T(8,128)(2,1)}, bf16[256,768]{1,0:T(8,128)(2,1)}, bf16[256,1536]{1,0:T(8,128)(2,1)}) custom-call(f32[256,3072]{1,0:T(8,128)} %fusion.q_raw.k_raw.v_raw, f32[256,3072]{1,0:T(8,128)} %fusion.q_raw.k_raw.v_raw, f32[256,3072]{1,0:T(8,128)} %fusion.q_raw.k_raw.v_raw, ...), custom_call_target="tpu_custom_call" | custom-call | flops 1 | bytes 1 | tf_op jit(solution)/shard_map/attention_forward/attention_forward/pallas_call | solution.py:573
  150.9 4.1 multiply_reduce_fusion.3
  155.0 2.1 fusion.27
  158.3 10.0 %collective-permute-done.20 = bf16[128,1536]{1,0:T(8,128)(2,1)S(1)} collective-permute-done((bf16[128,1536]{1,0:T(8,128)(2,1)S(1)}, bf16[128,1536]{1,0:T(8,128)(2,1)S(1)}, u32[]{:S(2)}, u32[]{:S(2)}) %collective-permute-start.20) | collective-permute-done | bytes 393248 | tf_op jit(solution)/shard_map/ffn_forward/ppermute | solution.py:40
  170.8 3.7 w_down_from.1.refs_4_.refs_6_
  174.4 11.1 %ffn_forward_beside.1 = (f32[512,1536]{1,0:T(8,128)}, bf16[512,1536]{1,0:T(8,128)(2,1)S(1)}, bf16[512,1024]{1,0:T(8,128)(2,1)S(1)}, f32[512,1024]{1,0:T(8,128)}, f32[512,1024]{1,0:T(8,128)}) custom-call(bf16[256,1536]{1,0:T(8,128)(2,1)S(1)} %pad_maximum_fusion.10.refs_0_, bf16[256,1536]{1,0:T(8,128)(2,1)S(1)} %pad_maximum_fusion.11.refs_1_, ...), custom_call_target="tpu_custom_call" | custom-call | flops 1 | bytes 1 | tf_op jit(solution)/shard_map/ffn_forward/ffn_forward_beside/pallas_call | solution.py:756
  189.0 5.7 %fusion.9 = f32[512,2048]{1,0:T(8,128)S(1)} fusion(bf16[512,1536]{1,0:T(8,128)(2,1)S(1)} %constant_dynamic-update-slice_fusion.refs_2_, bf16[1536,3072]{1,0:T(8,128)(2,1)} %all-gather.2.cloned.1.call-done.ref.refs_2_.refs_3_.refs_4_.refs_5_), kind=kOutput, calls=%fused_computation.11 | convolution fusion | flops 3221225472 | bytes 12058624 | tf_op jit(solution)/shard_map/ffn_forward/dot_general | solution.py:23
  202.9 2.0 fusion.29
  206.0 2.0 fusion.28
  208.9 8.5 %collective-permute-done.24 = bf16[256,1536]{1,0:T(8,128)(2,1)S(1)} collective-permute-done((bf16[256,1536]{1,0:T(8,128)(2,1)S(1)}, bf16[256,1536]{1,0:T(8,128)(2,1)S(1)}, u32[]{:S(2)}, u32[]{:S(2)}) %collective-permute-start.24) | collective-permute-done | bytes 786464 | tf_op jit(solution)/shard_map/ffn_forward/ppermute | solution.py:40
  221.3 5.8 %collective-permute-done.26 = bf16[128,1536]{1,0:T(8,128)(2,1)S(1)} collective-permute-done((bf16[128,1536]{1,0:T(8,128)(2,1)S(1)}, bf16[128,1536]{1,0:T(8,128)(2,1)S(1)}, u32[]{:S(2)}, u32[]{:S(2)}) %collective-permute-start.26) | collective-permute-done | bytes 393248 | tf_op jit(solution)/shard_map/ffn_forward/ppermute | solution.py:40
  228.7 2.0 multiply_reduce_fusion.2
  234.2 6.5 %collective-permute-done.28 = bf16[128,1536]{1,0:T(8,128)(2,1)S(1)} collective-permute-done((bf16[128,1536]{1,0:T(8,128)(2,1)S(1)}, bf16[128,1536]{1,0:T(8,128)(2,1)S(1)}, u32[]{:S(2)}, u32[]{:S(2)}) %collective-permute-start.28) | collective-permute-done | bytes 393248 | tf_op jit(solution)/shard_map/ffn_backward/ppermute | solution.py:40
  240.7 1.9 collective-permute-done.29
  244.7 14.9 %ffn_backward_beside.1 = (f32[512,1536]{1,0:T(8,128)}, bf16[512,1536]{1,0:T(8,128)(2,1)S(1)}, bf16[512,2048]{1,0:T(8,128)(2,1)S(1)}) custom-call(bf16[256,1536]{1,0:T(8,128)(2,1)S(1)} %pad_maximum_fusion.12.refs_0_, bf16[256,1536]{1,0:T(8,128)(2,1)S(1)} %pad_maximum_fusion.13.refs_1_, f32[512,1024]{1,0:T(8,128)} %get-tuple-element.224.refs_2_, ...), custom_call_target="tpu_custom_call" | custom-call | flops 1 | bytes 1 | tf_op jit(solution)/shard_map/ffn_backward/ffn_backward_beside/pallas_call | solution.py:821
  259.8 2.3 copy-done.21
  262.1 5.4 %multiply_convert_fusion.1 = (bf16[512,1024]{1,0:T(8,128)(2,1)S(1)}, bf16[512,1024]{1,0:T(8,128)(2,1)S(1)}) fusion(f32[512,2048]{1,0:T(8,128)} %copy-done.28, bf16[512,1536]{1,0:T(8,128)(2,1)S(1)} %constant_dynamic-update-slice_fusion.2.refs_3_, bf16[1024,1536]{1,0:T(8,128)(2,1)S(1)} %copy-done.21), kind=kOutput, calls=%fused_computation.43 | convolution fusion | flops 1617428480 | bytes 11010048 | tf_op jit(solution)/shard_map/ffn_backward/dot_general | solution.py:23
  267.5 3.4 fusion.20
  275.9 9.7 %products.2 = bf16[1536,2048]{1,0:T(8,128)(2,1)} custom-call(bf16[512,1536]{1,0:T(8,128)(2,1)S(1)} %get-tuple-element.236.refs_0_, bf16[512,2048]{1,0:T(8,128)(2,1)S(1)} %get-tuple-element.237.refs_1_, bf16[512,1536]{1,0:T(8,128)(2,1)S(1)} %constant_dynamic-update-slice_fusion.refs_2_, bf16[512,2048]{1,0:T(8,128)(2,1)} %pad_maximum_fusion.refs_3_), custom_call_target="tpu_custom_call" | custom-call | flops 1 | bytes 1 | tf_op jit(solution)/shard_map/ffn_backward/products/pallas_call | solution.py:913
  285.6 6.9 %collective-permute-done.33 = bf16[256,1536]{1,0:T(8,128)(2,1)} collective-permute-done((bf16[256,1536]{1,0:T(8,128)(2,1)}, bf16[256,1536]{1,0:T(8,128)(2,1)}, u32[]{:S(2)}, u32[]{:S(2)}) %collective-permute-start.33) | collective-permute-done | bytes 786464 | tf_op jit(solution)/shard_map/ffn_backward/ppermute | solution.py:40
  294.0 3.0 convert_add_fusion
  299.6 6.6 %products.3 = bf16[1024,1536]{1,0:T(8,128)(2,1)} custom-call(bf16[512,1024]{1,0:T(8,128)(2,1)S(1)} %copy-done.15, bf16[512,1536]{1,0:T(8,128)(2,1)S(1)} %copy-done.13, bf16[512,1024]{1,0:T(8,128)(2,1)S(1)} %multiply_convert_fusion.2.refs_2_, bf16[512,1536]{1,0:T(8,128)(2,1)S(1)} %copy-done.7), custom_call_target="tpu_custom_call" | custom-call | flops 1 | bytes 1 | tf_op jit(solution)/shard_map/ffn_backward/products/pallas_call | solution.py:913
  306.2 2.2 collective-permute-done.36
  312.2 2.0 fusion.4
  314.2 3.1 multiply_reduce_fusion
  318.3 2.3 convolution_convert_fusion.1
  322.6 4.5 fusion.124.refs_0_.refs_2_.refs_3_.refs_4_
  327.6 3.1 block_sums.6
  332.2 4.7 fusion.30.d_ref
  336.9 16.6 %attention_backward.1.grads = bf16[256,3072]{1,0:T(8,128)(2,1)} custom-call(bf16[256,1536]{1,0:T(8,128)(2,1)} %fusion.30.d_ref, bf16[256,1536]{1,0:T(8,128)(2,1)} %get-tuple-element.256.q_ref, bf16[256,768]{1,0:T(8,128)(2,1)} %get-tuple-element.257.k_ref, bf16[256,768]{1,0:T(8,128)(2,1)} %get-tuple-element.258.v_ref, f32[128,768]{1,0:T(8,128)} %copy.82.cosine, ...), custom_call_target="tpu_custom_call" | custom-call | flops 1 | bytes 1 | tf_op jit(solution)/shard_map/attention_backward/attention_backward/pallas_call | solution.py:644
  353.5 5.0 %convolution_convert_fusion = bf16[768,3072]{1,0:T(8,128)(2,1)} fusion(bf16[256,768]{1,0:T(8,128)(2,1)S(1)} %copy-done.31, bf16[256,3072]{1,0:T(8,128)(2,1)} %attention_backward.1.grads), kind=kOutput, calls=%fused_computation.13 | convolution fusion | flops 1210318848 | bytes 6684672 | tf_op jit(solution)/shard_map/q_k_v_weight_gradients/dot_general | solution.py:23
  360.7 2.2 block_sums.7
  364.9 5.1 %fusion.134.refs_0_.refs_2_.refs_3_.refs_4_ = f32[768,3072]{1,0:T(8,128)} fusion(bf16[256,768]{1,0:T(8,128)(2,1)S(1)} %copy-done.35, bf16[256,3072]{1,0:T(8,128)(2,1)S(1)} %copy-done.3), kind=kOutput, calls=%fused_computation.320 | convolution fusion | flops 1207959552 | bytes 11403264 | tf_op jit(solution)/shard_map/q_k_v_weight_gradients/dot_general | solution.py:23
  370.0 2.1 collective-permute-done.45.refs_3_
  373.9 5.1 %block_sums.8 = (bf16[192,3072]{1,0:T(8,128)(2,1)}, bf16[192,3072]{1,0:T(8,128)(2,1)}) custom-call(s32[4,2]{1,0:T(4,128)S(1)} %pad_add_fusion.table, f32[768,3072]{1,0:T(8,128)} %fusion.134.refs_0_.refs_2_.refs_3_.refs_4_, bf16[768,3072]{1,0:T(8,128)(2,1)} %collective-permute-done.43.refs_1_.refs_3_.refs_4_.refs_5_, ...), custom_call_target="tpu_custom_call" | custom-call | flops 1 | bytes 1 | tf_op jit(solution)/shard_map/q_k_v_weight_gradients/block_sums/pallas_call | solution.py:355
  382.6 2.3 block_sums.9
  386.5 3.0 collective-permute-start.51
  389.5 9.3 %input_gradient.1 = (bf16[256,1536]{1,0:T(8,128)(2,1)}, f32[1,1536]{1,0:T(1,128)S(1)}) custom-call(bf16[256,3072]{1,0:T(8,128)(2,1)S(1)} %copy-done.4, bf16[1536,4736]{1,0:T(8,128)(2,1)} %bitcast.207, bf16[256,1536]{1,0:T(8,128)(2,1)S(1)} %copy-done.5, f32[256,1]{1,0:T(8,128)S(1)} %copy.87.inv_scale, f32[1,1536]{1,0:T(1,128)S(1)} %reshape.378.gain, ...), custom_call_target="tpu_custom_call" | custom-call | flops 1 | bytes 1 | tf_op jit(solution)/shard_map/input_gradient/input_gradient/pallas_call | solution.py:866
  398.9 10.4 %collective-permute-done.50 = bf16[48,1536]{1,0:T(8,128)(2,1)S(1)} collective-permute-done((bf16[48,1536]{1,0:T(8,128)(2,1)S(1)}, bf16[48,1536]{1,0:T(8,128)(2,1)S(1)}, u32[]{:S(2)}, u32[]{:S(2)}) %collective-permute-start.50) | collective-permute-done | bytes 147488 | tf_op jit(solution)/shard_map/q_k_v_weight_gradients/ppermute | solution.py:40
  410.1 4.0 block_sums.10
  417.5 2.3 collective-permute-done.55
  422.5 2.0 collective-permute-done.56
  424.5 5.5 %collective-permute-done.52.refs_3_ = bf16[96,3072]{1,0:T(8,128)(2,1)S(1)} collective-permute-done((bf16[96,3072]{1,0:T(8,128)(2,1)}, bf16[96,3072]{1,0:T(8,128)(2,1)S(1)}, u32[]{:S(2)}, u32[]{:S(2)}) %collective-permute-start.52) | collective-permute-done | bytes 589856 | tf_op jit(solution)/shard_map/weight_gradients_to_owners/ppermute | solution.py:40
  436.2 3.4 block_sums.11
  440.0 3.1 collective-permute-start.57
  444.1 1.9 collective-permute-start.59
  451.8 13.8 %collective-permute-done.58 = bf16[48,3072]{1,0:T(8,128)(2,1)S(1)} collective-permute-done((bf16[48,3072]{1,0:T(8,128)(2,1)S(1)}, bf16[48,3072]{1,0:T(8,128)(2,1)S(1)}, u32[]{:S(2)}, u32[]{:S(2)}) %collective-permute-start.58) | collective-permute-done | bytes 294944 | tf_op jit(solution)/shard_map/weight_gradients_to_owners/ppermute | solution.py:40
  (356 shorter events, 129.5 us)
Async XLA Ops:
  7.2 163.6 %all-gather.2.cloned.1.call-start = ((), (), s32[]{:S(2)}) async-start(), calls=%async_computation.2 | async-start | bytes 10616832 | tf_op jit(solution)/shard_map/ffn_weights/all_gather | solution.py:114
  10.5 15.0 %collective-permute-start = (bf16[48,4736]{1,0:T(8,128)(2,1)}, bf16[48,4736]{1,0:T(8,128)(2,1)S(1)}, u32[]{:S(2)}, u32[]{:S(2)}) collective-permute-start(bf16[48,4736]{1,0:T(8,128)(2,1)} %packed.1), channel_id=1, source_target_pairs={{0,8},{1,9},{2,10},{3,11},{4,12},{5,13},{6,14},{7,15},{8,16},{9,17... | collective-permute-start | bytes 1363976 | tf_op jit(solution)/shard_map/phase_0/ppermute | solution.py:77
  15.6 14.0 %collective-permute-start.1 = (bf16[48,4736]{1,0:T(8,128)(2,1)}, bf16[48,4736]{1,0:T(8,128)(2,1)S(1)}, u32[]{:S(2)}, u32[]{:S(2)}) collective-permute-start(bf16[48,4736]{1,0:T(8,128)(2,1)} %packed.1), channel_id=1, source_target_pairs={{8,0},{9,1},{10,2},{11,3},{12,4},{13,5},{14,6},{15,7},{16,8},{17,9... | collective-permute-start | bytes 1363976 | tf_op jit(solution)/shard_map/phase_0/ppermute | solution.py:77
  19.0 19.0 %collective-permute-start.6 = (bf16[48,2048]{1,0:T(8,128)(2,1)}, bf16[48,2048]{1,0:T(8,128)(2,1)S(1)}, u32[]{:S(2)}, u32[]{:S(2)}) collective-permute-start(bf16[48,2048]{1,0:T(8,128)(2,1)} %get-tuple-element.161), channel_id=1, source_target_pairs={{0,2},{1,3},{2,0},{3,1},{4,6},{5,7},{6,4},{7,5},{8,10},{9,11},{10,... | collective-permute-start | bytes 589832 | tf_op jit(solution)/shard_map/phase_0/ppermute | solution.py:40
  20.5 21.2 %collective-permute-start.7 = (bf16[48,2048]{1,0:T(8,128)(2,1)}, bf16[48,2048]{1,0:T(8,128)(2,1)}, u32[]{:S(2)}, u32[]{:S(2)}) collective-permute-start(bf16[48,2048]{1,0:T(8,128)(2,1)} %get-tuple-element.162), channel_id=1, source_target_pairs={{0,4},{1,5},{2,6},{3,7},{4,0},{5,1},{6,2},{7,3},{8,12},{9,13},{10,... | collective-permute-start | bytes 589832 | tf_op jit(solution)/shard_map/phase_0/ppermute | solution.py:40
  29.7 19.0 %collective-permute-start.2 = (bf16[48,4736]{1,0:T(8,128)(2,1)S(1)}, bf16[48,4736]{1,0:T(8,128)(2,1)S(1)}, u32[]{:S(2)}, u32[]{:S(2)}) collective-permute-start(bf16[48,4736]{1,0:T(8,128)(2,1)S(1)} %copy-done.34), channel_id=1, source_target_pairs={{0,2},{1,3},{2,0},{3,1},{4,6},{5,7},{6,4},{7,5},{8,10},{9,11},{10,... | collective-permute-start | bytes 1363976 | tf_op jit(solution)/shard_map/phase_1/ppermute | solution.py:40
  31.2 17.5 %collective-permute-start.4 = (bf16[48,4736]{1,0:T(8,128)(2,1)S(1)}, bf16[48,4736]{1,0:T(8,128)(2,1)}, u32[]{:S(2)}, u32[]{:S(2)}) collective-permute-start(bf16[48,4736]{1,0:T(8,128)(2,1)S(1)} %copy-done.34), channel_id=1, source_target_pairs={{0,16},{1,17},{2,18},{3,19},{4,20},{5,21},{6,22},{7,23},{24,8},{25... | collective-permute-start | bytes 1363976 | tf_op jit(solution)/shard_map/phase_1/ppermute | solution.py:77
  36.5 14.7 %collective-permute-start.3 = (bf16[48,4736]{1,0:T(8,128)(2,1)S(1)}, bf16[48,4736]{1,0:T(8,128)(2,1)}, u32[]{:S(2)}, u32[]{:S(2)}) collective-permute-start(bf16[48,4736]{1,0:T(8,128)(2,1)S(1)} %get-tuple-element.159), channel_id=1, source_target_pairs={{0,4},{1,5},{2,6},{3,7},{4,0},{5,1},{6,2},{7,3},{8,12},{9,13},{10,... | collective-permute-start | bytes 1363976 | tf_op jit(solution)/shard_map/phase_1/ppermute | solution.py:40
  38.0 13.2 %collective-permute-start.5 = (bf16[48,4736]{1,0:T(8,128)(2,1)S(1)}, bf16[48,4736]{1,0:T(8,128)(2,1)S(1)}, u32[]{:S(2)}, u32[]{:S(2)}) collective-permute-start(bf16[48,4736]{1,0:T(8,128)(2,1)S(1)} %get-tuple-element.160), channel_id=1, source_target_pairs={{8,0},{9,1},{10,2},{11,3},{12,4},{13,5},{14,6},{15,7},{16,24},{17,... | collective-permute-start | bytes 1363976 | tf_op jit(solution)/shard_map/phase_1/ppermute | solution.py:77
  41.7 7.0 %collective-permute-start.8 = (bf16[48,2048]{1,0:T(8,128)(2,1)}, bf16[48,2048]{1,0:T(8,128)(2,1)S(1)}, u32[]{:S(2)}, u32[]{:S(2)}) collective-permute-start(bf16[48,2048]{1,0:T(8,128)(2,1)} %get-tuple-element.163), channel_id=1, source_target_pairs={{0,6},{1,7},{2,4},{3,5},{4,2},{5,3},{6,0},{7,1},{8,14},{9,15},{10,... | collective-permute-start | bytes 589832 | tf_op jit(solution)/shard_map/phase_0/ppermute | solution.py:40
  52.9 18.1 %collective-permute-start.10 = (bf16[2,48,4736]{2,1,0:T(8,128)(2,1)S(1)}, bf16[2,48,4736]{2,1,0:T(8,128)(2,1)S(1)}, u32[]{:S(2)}, u32[]{:S(2)}) collective-permute-start(bf16[2,48,4736]{2,1,0:T(8,128)(2,1)S(1)} %pad_maximum_fusion.7), channel_id=1, source_target_pairs={{0,2},{1,3},{2,0},{3,1},{4,6},{5,7},{6,4},{7,5},{8,10},{9,11},{10,... | collective-permute-start | bytes 2727944 | tf_op jit(solution)/shard_map/phase_2/ppermute | solution.py:40
  53.5 18.8 %collective-permute-start.9 = (bf16[2,48,4736]{2,1,0:T(8,128)(2,1)S(1)}, bf16[2,48,4736]{2,1,0:T(8,128)(2,1)}, u32[]{:S(2)}, u32[]{:S(2)}) collective-permute-start(bf16[2,48,4736]{2,1,0:T(8,128)(2,1)S(1)} %pad_maximum_fusion.6), channel_id=1, source_target_pairs={{0,4},{1,5},{2,6},{3,7},{4,0},{5,1},{6,2},{7,3},{8,12},{9,13},{10,... | collective-permute-start | bytes 2727944 | tf_op jit(solution)/shard_map/phase_2/ppermute | solution.py:40
  55.0 11.1 %collective-permute-start.11 = (bf16[48,4736]{1,0:T(8,128)(2,1)}, bf16[48,4736]{1,0:T(8,128)(2,1)}, u32[]{:S(2)}, u32[]{:S(2)}) collective-permute-start(bf16[48,4736]{1,0:T(8,128)(2,1)} %collective-permute-done.4), channel_id=1, source_target_pairs={{8,0},{9,1},{10,2},{11,3},{12,4},{13,5},{14,6},{15,7},{16,24},{17,... | collective-permute-start | bytes 1363976 | tf_op jit(solution)/shard_map/phase_2/ppermute | solution.py:77
  74.2 14.4 %collective-permute-start.14 = (bf16[2,2,48,4736]{3,2,1,0:T(8,128)(2,1)}, bf16[2,2,48,4736]{3,2,1,0:T(8,128)(2,1)S(1)}, u32[]{:S(2)}, u32[]{:S(2)}) collective-permute-start(bf16[2,2,48,4736]{3,2,1,0:T(8,128)(2,1)} %pad_maximum_fusion.1), channel_id=1, source_target_pairs={{0,1},{1,0},{2,3},{3,2},{4,5},{5,4},{6,7},{7,6},{8,9},{9,8},{10,11... | collective-permute-start | bytes 5455880 | tf_op jit(solution)/shard_map/phase_3/ppermute | solution.py:40
  74.2 13.2 %collective-permute-start.12 = (bf16[48,4736]{1,0:T(8,128)(2,1)}, bf16[48,4736]{1,0:T(8,128)(2,1)}, u32[]{:S(2)}, u32[]{:S(2)}) collective-permute-start(bf16[48,4736]{1,0:T(8,128)(2,1)} %broadcast_select_fusion.1), channel_id=1, source_target_pairs={{0,2},{1,3},{2,0},{3,1},{4,6},{5,7},{6,4},{7,5},{8,10},{9,11},{10,... | collective-permute-start | bytes 1363976 | tf_op jit(solution)/shard_map/phase_3/ppermute | solution.py:40
  75.6 12.9 %collective-permute-start.13 = (bf16[48,4736]{1,0:T(8,128)(2,1)}, bf16[48,4736]{1,0:T(8,128)(2,1)}, u32[]{:S(2)}, u32[]{:S(2)}) collective-permute-start(bf16[48,4736]{1,0:T(8,128)(2,1)} %broadcast_select_fusion), channel_id=1, source_target_pairs={{0,4},{1,5},{2,6},{3,7},{4,0},{5,1},{6,2},{7,3},{8,12},{9,13},{10,... | collective-permute-start | bytes 1363976 | tf_op jit(solution)/shard_map/phase_3/ppermute | solution.py:40
  77.4 296.4 %reduce-scatter.3.cloned.1.call-start = ((), (), s32[]{:S(2)}) async-start(), calls=%async_computation.3 | async-start | bytes 7077888 | tf_op jit(solution)/shard_map/ffn_backward/reduce_scatter | solution.py:120
  91.3 24.1 %collective-permute-start.17 = (bf16[2,2,48,4736]{3,2,1,0:T(8,128)(2,1)S(1)}, bf16[2,2,48,4736]{3,2,1,0:T(8,128)(2,1)S(1)}, u32[]{:S(2)}, u32[]{:S(2)}) collective-permute-start(bf16[2,2,48,4736]{3,2,1,0:T(8,128)(2,1)S(1)} %pad_maximum_fusion.2), channel_id=1, source_target_pairs={{0,1},{1,0},{2,3},{3,2},{4,5},{5,4},{6,7},{7,6},{8,9},{9,8},{10,11... | collective-permute-start | bytes 5455880 | tf_op jit(solution)/shard_map/phase_4/ppermute | solution.py:40
  91.4 22.6 %collective-permute-start.15 = (bf16[2,48,4736]{2,1,0:T(8,128)(2,1)S(1)}, bf16[2,48,4736]{2,1,0:T(8,128)(2,1)S(1)}, u32[]{:S(2)}, u32[]{:S(2)}) collective-permute-start(bf16[2,48,4736]{2,1,0:T(8,128)(2,1)S(1)} %pad_maximum_fusion.8), channel_id=1, source_target_pairs={{0,4},{1,5},{2,6},{3,7},{4,0},{5,1},{6,2},{7,3},{8,12},{9,13},{10,... | collective-permute-start | bytes 2727944 | tf_op jit(solution)/shard_map/phase_4/ppermute | solution.py:40
  93.1 22.2 %collective-permute-start.16 = (bf16[2,48,4736]{2,1,0:T(8,128)(2,1)S(1)}, bf16[2,48,4736]{2,1,0:T(8,128)(2,1)S(1)}, u32[]{:S(2)}, u32[]{:S(2)}) collective-permute-start(bf16[2,48,4736]{2,1,0:T(8,128)(2,1)S(1)} %pad_maximum_fusion.9), channel_id=1, source_target_pairs={{0,2},{1,3},{2,0},{3,1},{4,6},{5,7},{6,4},{7,5},{8,10},{9,11},{10,... | collective-permute-start | bytes 2727944 | tf_op jit(solution)/shard_map/phase_4/ppermute | solution.py:40
  115.7 6.3 %collective-permute-start.19 = (bf16[2,2,48,4736]{3,2,1,0:T(8,128)(2,1)S(1)}, bf16[2,2,48,4736]{3,2,1,0:T(8,128)(2,1)S(1)}, u32[]{:S(2)}, u32[]{:S(2)}) collective-permute-start(bf16[2,2,48,4736]{3,2,1,0:T(8,128)(2,1)S(1)} %pad_maximum_fusion.4), channel_id=1, source_target_pairs={{0,1},{1,0},{2,3},{3,2},{4,5},{5,4},{6,7},{7,6},{8,9},{9,8},{10,11... | collective-permute-start | bytes 5455880 | tf_op jit(solution)/shard_map/phase_5/ppermute | solution.py:40
  157.2 11.2 %collective-permute-start.20 = (bf16[128,1536]{1,0:T(8,128)(2,1)S(1)}, bf16[128,1536]{1,0:T(8,128)(2,1)S(1)}, u32[]{:S(2)}, u32[]{:S(2)}) collective-permute-start(bf16[128,1536]{1,0:T(8,128)(2,1)S(1)} %get-tuple-element.347), channel_id=1, source_target_pairs={{0,2},{1,3},{2,0},{3,1},{4,6},{5,7},{6,4},{7,5},{8,10},{9,11},{10,... | collective-permute-start | bytes 1179656 | tf_op jit(solution)/shard_map/ffn_forward/ppermute | solution.py:40
  157.8 10.9 %collective-permute-start.21 = (bf16[128,1536]{1,0:T(8,128)(2,1)S(1)}, bf16[128,1536]{1,0:T(8,128)(2,1)S(1)}, u32[]{:S(2)}, u32[]{:S(2)}) collective-permute-start(bf16[128,1536]{1,0:T(8,128)(2,1)S(1)} %get-tuple-element.346), channel_id=1, source_target_pairs={{0,4},{1,5},{2,6},{3,7},{4,0},{5,1},{6,2},{7,3},{8,12},{9,13},{10,... | collective-permute-start | bytes 1179656 | tf_op jit(solution)/shard_map/ffn_forward/ppermute | solution.py:40
  168.8 18.6 %collective-permute-start.22 = (bf16[256,1536]{1,0:T(8,128)(2,1)S(1)}, bf16[256,1536]{1,0:T(8,128)(2,1)S(1)}, u32[]{:S(2)}, u32[]{:S(2)}) collective-permute-start(bf16[256,1536]{1,0:T(8,128)(2,1)S(1)} %pad_maximum_fusion.10.refs_0_), channel_id=1, source_target_pairs={{0,4},{1,5},{2,6},{3,7},{4,0},{5,1},{6,2},{7,3},{8,12},{9,13},{10,... | collective-permute-start | bytes 2359304 | tf_op jit(solution)/shard_map/ffn_forward/ppermute | solution.py:40
  169.4 18.3 %collective-permute-start.23 = (bf16[256,1536]{1,0:T(8,128)(2,1)S(1)}, bf16[256,1536]{1,0:T(8,128)(2,1)}, u32[]{:S(2)}, u32[]{:S(2)}) collective-permute-start(bf16[256,1536]{1,0:T(8,128)(2,1)S(1)} %pad_maximum_fusion.11.refs_1_), channel_id=1, source_target_pairs={{0,2},{1,3},{2,0},{3,1},{4,6},{5,7},{6,4},{7,5},{8,10},{9,11},{10,... | collective-permute-start | bytes 2359304 | tf_op jit(solution)/shard_map/ffn_forward/ppermute | solution.py:40
  200.0 17.4 %collective-permute-start.24 = (bf16[256,1536]{1,0:T(8,128)(2,1)S(1)}, bf16[256,1536]{1,0:T(8,128)(2,1)S(1)}, u32[]{:S(2)}, u32[]{:S(2)}) collective-permute-start(bf16[256,1536]{1,0:T(8,128)(2,1)S(1)} %get-tuple-element.319), channel_id=1, source_target_pairs={{0,4},{1,5},{2,6},{3,7},{4,0},{5,1},{6,2},{7,3},{8,12},{9,13},{10,... | collective-permute-start | bytes 2359304 | tf_op jit(solution)/shard_map/ffn_forward/ppermute | solution.py:40
  201.6 17.1 %collective-permute-start.25 = (bf16[256,1536]{1,0:T(8,128)(2,1)S(1)}, bf16[256,1536]{1,0:T(8,128)(2,1)S(1)}, u32[]{:S(2)}, u32[]{:S(2)}) collective-permute-start(bf16[256,1536]{1,0:T(8,128)(2,1)S(1)} %get-tuple-element.318), channel_id=1, source_target_pairs={{0,2},{1,3},{2,0},{3,1},{4,6},{5,7},{6,4},{7,5},{8,10},{9,11},{10,... | collective-permute-start | bytes 2359304 | tf_op jit(solution)/shard_map/ffn_forward/ppermute | solution.py:40
  219.3 7.8 %collective-permute-start.26 = (bf16[128,1536]{1,0:T(8,128)(2,1)S(1)}, bf16[128,1536]{1,0:T(8,128)(2,1)S(1)}, u32[]{:S(2)}, u32[]{:S(2)}) collective-permute-start(bf16[128,1536]{1,0:T(8,128)(2,1)S(1)} %slice.449), channel_id=1, source_target_pairs={{0,2},{1,3},{2,0},{3,1},{4,6},{5,7},{6,4},{7,5},{8,10},{9,11},{10,... | collective-permute-start | bytes 1179656 | tf_op jit(solution)/shard_map/ffn_forward/ppermute | solution.py:40
  220.7 7.8 %collective-permute-start.27 = (bf16[128,1536]{1,0:T(8,128)(2,1)S(1)}, bf16[128,1536]{1,0:T(8,128)(2,1)S(1)}, u32[]{:S(2)}, u32[]{:S(2)}) collective-permute-start(bf16[128,1536]{1,0:T(8,128)(2,1)S(1)} %slice.448), channel_id=1, source_target_pairs={{0,4},{1,5},{2,6},{3,7},{4,0},{5,1},{6,2},{7,3},{8,12},{9,13},{10,... | collective-permute-start | bytes 1179656 | tf_op jit(solution)/shard_map/ffn_forward/ppermute | solution.py:40
  230.9 9.8 %collective-permute-start.28 = (bf16[128,1536]{1,0:T(8,128)(2,1)S(1)}, bf16[128,1536]{1,0:T(8,128)(2,1)S(1)}, u32[]{:S(2)}, u32[]{:S(2)}) collective-permute-start(bf16[128,1536]{1,0:T(8,128)(2,1)S(1)} %get-tuple-element.341), channel_id=1, source_target_pairs={{0,2},{1,3},{2,0},{3,1},{4,6},{5,7},{6,4},{7,5},{8,10},{9,11},{10,... | collective-permute-start | bytes 1179656 | tf_op jit(solution)/shard_map/ffn_backward/ppermute | solution.py:40
  231.7 10.9 %collective-permute-start.29 = (bf16[128,1536]{1,0:T(8,128)(2,1)S(1)}, bf16[128,1536]{1,0:T(8,128)(2,1)S(1)}, u32[]{:S(2)}, u32[]{:S(2)}) collective-permute-start(bf16[128,1536]{1,0:T(8,128)(2,1)S(1)} %get-tuple-element.340), channel_id=1, source_target_pairs={{0,4},{1,5},{2,6},{3,7},{4,0},{5,1},{6,2},{7,3},{8,12},{9,13},{10,... | collective-permute-start | bytes 1179656 | tf_op jit(solution)/shard_map/ffn_backward/ppermute | solution.py:40
  242.8 16.9 %collective-permute-start.30 = (bf16[256,1536]{1,0:T(8,128)(2,1)S(1)}, bf16[256,1536]{1,0:T(8,128)(2,1)S(1)}, u32[]{:S(2)}, u32[]{:S(2)}) collective-permute-start(bf16[256,1536]{1,0:T(8,128)(2,1)S(1)} %pad_maximum_fusion.12.refs_0_), channel_id=1, source_target_pairs={{0,4},{1,5},{2,6},{3,7},{4,0},{5,1},{6,2},{7,3},{8,12},{9,13},{10,... | collective-permute-start | bytes 2359304 | tf_op jit(solution)/shard_map/ffn_backward/ppermute | solution.py:40
  243.2 16.5 %collective-permute-start.31 = (bf16[256,1536]{1,0:T(8,128)(2,1)S(1)}, bf16[256,1536]{1,0:T(8,128)(2,1)S(1)}, u32[]{:S(2)}, u32[]{:S(2)}) collective-permute-start(bf16[256,1536]{1,0:T(8,128)(2,1)S(1)} %pad_maximum_fusion.13.refs_1_), channel_id=1, source_target_pairs={{0,2},{1,3},{2,0},{3,1},{4,6},{5,7},{6,4},{7,5},{8,10},{9,11},{10,... | collective-permute-start | bytes 2359304 | tf_op jit(solution)/shard_map/ffn_backward/ppermute | solution.py:40
  244.7 14.9 %collective-permute-start.32 = (f32[2,128]{1,0:T(2,128)S(1)}, f32[2,128]{1,0:T(2,128)S(1)}, u32[]{:S(2)}, u32[]{:S(2)}) collective-permute-start(f32[2,128]{1,0:T(2,128)S(1)} %broadcast_in_dim.50), channel_id=1, source_target_pairs={{0,1},{1,0},{2,3},{3,2},{4,5},{5,4},{6,7},{7,6},{8,9},{9,8},{10,11... | collective-permute-start | bytes 3080 | tf_op jit(solution)/shard_map/ffn_backward/ppermute | solution.py:40
  272.2 20.3 %collective-permute-start.33 = (bf16[256,1536]{1,0:T(8,128)(2,1)}, bf16[256,1536]{1,0:T(8,128)(2,1)}, u32[]{:S(2)}, u32[]{:S(2)}) collective-permute-start(bf16[256,1536]{1,0:T(8,128)(2,1)} %get-tuple-element.317), channel_id=1, source_target_pairs={{0,4},{1,5},{2,6},{3,7},{4,0},{5,1},{6,2},{7,3},{8,12},{9,13},{10,... | collective-permute-start | bytes 2359304 | tf_op jit(solution)/shard_map/ffn_backward/ppermute | solution.py:40
  273.9 20.0 %collective-permute-start.34 = (bf16[256,1536]{1,0:T(8,128)(2,1)}, bf16[256,1536]{1,0:T(8,128)(2,1)}, u32[]{:S(2)}, u32[]{:S(2)}) collective-permute-start(bf16[256,1536]{1,0:T(8,128)(2,1)} %get-tuple-element.316), channel_id=1, source_target_pairs={{0,2},{1,3},{2,0},{3,1},{4,6},{5,7},{6,4},{7,5},{8,10},{9,11},{10,... | collective-permute-start | bytes 2359304 | tf_op jit(solution)/shard_map/ffn_backward/ppermute | solution.py:40
  274.4 11.2 %collective-permute-start.35 = (f32[2,128]{1,0:T(2,128)S(1)}, f32[2,128]{1,0:T(2,128)S(1)}, u32[]{:S(2)}, u32[]{:S(2)}) collective-permute-start(f32[2,128]{1,0:T(2,128)S(1)} %add.558), channel_id=1, source_target_pairs={{0,8},{1,9},{2,10},{3,11},{4,12},{5,13},{6,14},{7,15},{8,0},{9,1},... | collective-permute-start | bytes 3080 | tf_op jit(solution)/shard_map/ffn_backward/ppermute | solution.py:40
  293.9 136.4 %reduce-scatter.5.cloned.1.call-start = ((), (), s32[]{:S(2)}) async-start(), calls=%async_computation.4 | async-start | bytes 3538944 | tf_op jit(solution)/shard_map/q_k_v_weight_gradients/reduce_scatter | solution.py:120
  297.8 10.7 %collective-permute-start.36 = (bf16[128,1536]{1,0:T(8,128)(2,1)}, bf16[128,1536]{1,0:T(8,128)(2,1)}, u32[]{:S(2)}, u32[]{:S(2)}) collective-permute-start(bf16[128,1536]{1,0:T(8,128)(2,1)} %slice.447), channel_id=1, source_target_pairs={{0,2},{1,3},{2,0},{3,1},{4,6},{5,7},{6,4},{7,5},{8,10},{9,11},{10,... | collective-permute-start | bytes 1179656 | tf_op jit(solution)/shard_map/ffn_backward/ppermute | solution.py:40
  299.0 10.7 %collective-permute-start.37 = (bf16[128,1536]{1,0:T(8,128)(2,1)}, bf16[128,1536]{1,0:T(8,128)(2,1)}, u32[]{:S(2)}, u32[]{:S(2)}) collective-permute-start(bf16[128,1536]{1,0:T(8,128)(2,1)} %slice.446), channel_id=1, source_target_pairs={{0,4},{1,5},{2,6},{3,7},{4,0},{5,1},{6,2},{7,3},{8,12},{9,13},{10,... | collective-permute-start | bytes 1179656 | tf_op jit(solution)/shard_map/ffn_backward/ppermute | solution.py:40
  299.4 6.8 %collective-permute-start.38 = (f32[2,128]{1,0:T(2,128)S(1)}, f32[2,128]{1,0:T(2,128)S(1)}, u32[]{:S(2)}, u32[]{:S(2)}) collective-permute-start(f32[2,128]{1,0:T(2,128)S(1)} %add.561), channel_id=1, source_target_pairs={{0,16},{1,17},{2,18},{3,19},{4,20},{5,21},{6,22},{7,23},{8,24},{9,... | collective-permute-start | bytes 3080 | tf_op jit(solution)/shard_map/ffn_backward/ppermute | solution.py:40
  320.6 7.1 %collective-permute-start.39 = (bf16[768,1536]{1,0:T(8,128)(2,1)}, bf16[768,1536]{1,0:T(8,128)(2,1)S(1)}, u32[]{:S(2)}, u32[]{:S(2)}) collective-permute-start(bf16[768,1536]{1,0:T(8,128)(2,1)} %convolution_convert_fusion.1), channel_id=1, source_target_pairs={{0,1},{1,0},{2,3},{3,2},{4,5},{5,4},{6,7},{7,6},{8,9},{9,8},{10,11... | collective-permute-start | bytes 7077896 | tf_op jit(solution)/shard_map/attention_backward/ppermute | solution.py:40
  321.3 5.8 %collective-permute-start.40 = (f32[2,128]{1,0:T(2,128)S(1)}, f32[2,128]{1,0:T(2,128)S(1)}, u32[]{:S(2)}, u32[]{:S(2)}) collective-permute-start(f32[2,128]{1,0:T(2,128)S(1)} %add.562), channel_id=1, source_target_pairs={{0,2},{1,3},{2,0},{3,1},{4,6},{5,7},{6,4},{7,5},{8,10},{9,11},{10,... | collective-permute-start | bytes 3080 | tf_op jit(solution)/shard_map/attention_backward/ppermute | solution.py:40
  330.8 22.7 %collective-permute-start.41 = (bf16[192,1536]{1,0:T(8,128)(2,1)}, bf16[192,1536]{1,0:T(8,128)(2,1)}, u32[]{:S(2)}, u32[]{:S(2)}) collective-permute-start(bf16[192,1536]{1,0:T(8,128)(2,1)} %get-tuple-element.254), channel_id=1, source_target_pairs={{0,4},{1,5},{2,6},{3,7},{4,0},{5,1},{6,2},{7,3},{8,12},{9,13},{10,... | collective-permute-start | bytes 1769480 | tf_op jit(solution)/shard_map/attention_backward/ppermute | solution.py:40
  331.3 22.2 %collective-permute-start.42 = (bf16[192,1536]{1,0:T(8,128)(2,1)}, bf16[192,1536]{1,0:T(8,128)(2,1)}, u32[]{:S(2)}, u32[]{:S(2)}) collective-permute-start(bf16[192,1536]{1,0:T(8,128)(2,1)} %get-tuple-element.255), channel_id=1, source_target_pairs={{0,2},{1,3},{2,0},{3,1},{4,6},{5,7},{6,4},{7,5},{8,10},{9,11},{10,... | collective-permute-start | bytes 1769480 | tf_op jit(solution)/shard_map/attention_backward/ppermute | solution.py:40
  358.5 15.3 %collective-permute-start.43 = (bf16[768,3072]{1,0:T(8,128)(2,1)}, bf16[768,3072]{1,0:T(8,128)(2,1)}, u32[]{:S(2)}, u32[]{:S(2)}) collective-permute-start(bf16[768,3072]{1,0:T(8,128)(2,1)} %convolution_convert_fusion), channel_id=1, source_target_pairs={{0,1},{1,0},{2,3},{3,2},{4,5},{5,4},{6,7},{7,6},{8,9},{9,8},{10,11... | collective-permute-start | bytes 14155784 | tf_op jit(solution)/shard_map/q_k_v_weight_gradients/ppermute | solution.py:40
  359.4 10.5 %collective-permute-start.44 = (f32[2,128]{1,0:T(2,128)S(1)}, f32[2,128]{1,0:T(2,128)S(1)}, u32[]{:S(2)}, u32[]{:S(2)}) collective-permute-start(f32[2,128]{1,0:T(2,128)S(1)} %add.567), channel_id=1, source_target_pairs={{0,4},{1,5},{2,6},{3,7},{4,0},{5,1},{6,2},{7,3},{8,12},{9,13},{10,... | collective-permute-start | bytes 3080 | tf_op jit(solution)/shard_map/q_k_v_weight_gradients/ppermute | solution.py:40
  362.9 9.2 %collective-permute-start.45 = (bf16[96,1536]{1,0:T(8,128)(2,1)S(1)}, bf16[96,1536]{1,0:T(8,128)(2,1)S(1)}, u32[]{:S(2)}, u32[]{:S(2)}) collective-permute-start(bf16[96,1536]{1,0:T(8,128)(2,1)S(1)} %get-tuple-element.265), channel_id=1, source_target_pairs={{0,2},{1,3},{2,0},{3,1},{4,6},{5,7},{6,4},{7,5},{8,10},{9,11},{10,... | collective-permute-start | bytes 884744 | tf_op jit(solution)/shard_map/attention_backward/ppermute | solution.py:40
  364.3 8.9 %collective-permute-start.46 = (bf16[96,1536]{1,0:T(8,128)(2,1)S(1)}, bf16[96,1536]{1,0:T(8,128)(2,1)S(1)}, u32[]{:S(2)}, u32[]{:S(2)}) collective-permute-start(bf16[96,1536]{1,0:T(8,128)(2,1)S(1)} %get-tuple-element.266), channel_id=1, source_target_pairs={{0,4},{1,5},{2,6},{3,7},{4,0},{5,1},{6,2},{7,3},{8,12},{9,13},{10,... | collective-permute-start | bytes 884744 | tf_op jit(solution)/shard_map/attention_backward/ppermute | solution.py:40
  379.0 30.4 %collective-permute-start.47 = (bf16[192,3072]{1,0:T(8,128)(2,1)}, bf16[192,3072]{1,0:T(8,128)(2,1)}, u32[]{:S(2)}, u32[]{:S(2)}) collective-permute-start(bf16[192,3072]{1,0:T(8,128)(2,1)} %get-tuple-element.272), channel_id=1, source_target_pairs={{0,4},{1,5},{2,6},{3,7},{4,0},{5,1},{6,2},{7,3},{8,12},{9,13},{10,... | collective-permute-start | bytes 3538952 | tf_op jit(solution)/shard_map/q_k_v_weight_gradients/ppermute | solution.py:40
  379.2 30.1 %collective-permute-start.48 = (bf16[192,3072]{1,0:T(8,128)(2,1)}, bf16[192,3072]{1,0:T(8,128)(2,1)}, u32[]{:S(2)}, u32[]{:S(2)}) collective-permute-start(bf16[192,3072]{1,0:T(8,128)(2,1)} %get-tuple-element.273), channel_id=1, source_target_pairs={{0,2},{1,3},{2,0},{3,1},{4,6},{5,7},{6,4},{7,5},{8,10},{9,11},{10,... | collective-permute-start | bytes 3538952 | tf_op jit(solution)/shard_map/q_k_v_weight_gradients/ppermute | solution.py:40
  385.1 13.9 %collective-permute-start.49 = (bf16[48,1536]{1,0:T(8,128)(2,1)S(1)}, bf16[48,1536]{1,0:T(8,128)(2,1)S(1)}, u32[]{:S(2)}, u32[]{:S(2)}) collective-permute-start(bf16[48,1536]{1,0:T(8,128)(2,1)S(1)} %get-tuple-element.325), channel_id=1, source_target_pairs={{0,24},{1,25},{2,26},{3,27},{4,28},{5,29},{6,30},{7,31},{8,16},{9,... | collective-permute-start | bytes 442376 | tf_op jit(solution)/shard_map/q_k_v_weight_gradients/ppermute | solution.py:40
  386.3 23.0 %collective-permute-start.50 = (bf16[48,1536]{1,0:T(8,128)(2,1)S(1)}, bf16[48,1536]{1,0:T(8,128)(2,1)S(1)}, u32[]{:S(2)}, u32[]{:S(2)}) collective-permute-start(bf16[48,1536]{1,0:T(8,128)(2,1)S(1)} %get-tuple-element.326), channel_id=1, source_target_pairs={{0,16},{1,17},{2,18},{3,19},{4,20},{5,21},{6,22},{7,23},{8,24},{9,... | collective-permute-start | bytes 442376 | tf_op jit(solution)/shard_map/q_k_v_weight_gradients/ppermute | solution.py:40
  386.5 22.8 %collective-permute-start.51 = (bf16[48,1536]{1,0:T(8,128)(2,1)S(1)}, bf16[48,1536]{1,0:T(8,128)(2,1)S(1)}, u32[]{:S(2)}, u32[]{:S(2)}) collective-permute-start(bf16[48,1536]{1,0:T(8,128)(2,1)S(1)} %get-tuple-element.324), channel_id=1, source_target_pairs={{0,8},{1,9},{2,10},{3,11},{4,12},{5,13},{6,14},{7,15},{8,0},{9,1},... | collective-permute-start | bytes 442376 | tf_op jit(solution)/shard_map/q_k_v_weight_gradients/ppermute | solution.py:40
  410.1 5.5 %collective-permute-start.54 = (f32[2,1536]{1,0:T(2,128)S(1)}, f32[2,1536]{1,0:T(2,128)S(1)}, u32[]{:S(2)}, u32[]{:S(2)}) collective-permute-start(f32[2,1536]{1,0:T(2,128)S(1)} %pad_maximum_fusion.14), channel_id=1, source_target_pairs={{0,1},{1,0},{2,3},{3,2},{4,5},{5,4},{6,7},{7,6},{8,9},{9,8},{10,11... | collective-permute-start | bytes 36872 | tf_op jit(solution)/shard_map/weight_gradients_to_owners/ppermute | solution.py:40
  414.0 15.9 %collective-permute-start.52 = (bf16[96,3072]{1,0:T(8,128)(2,1)}, bf16[96,3072]{1,0:T(8,128)(2,1)S(1)}, u32[]{:S(2)}, u32[]{:S(2)}) collective-permute-start(bf16[96,3072]{1,0:T(8,128)(2,1)} %get-tuple-element.281), channel_id=1, source_target_pairs={{0,2},{1,3},{2,0},{3,1},{4,6},{5,7},{6,4},{7,5},{8,10},{9,11},{10,... | collective-permute-start | bytes 1769480 | tf_op jit(solution)/shard_map/weight_gradients_to_owners/ppermute | solution.py:40
  414.9 15.4 %collective-permute-start.53 = (bf16[96,3072]{1,0:T(8,128)(2,1)S(1)}, bf16[96,3072]{1,0:T(8,128)(2,1)S(1)}, u32[]{:S(2)}, u32[]{:S(2)}) collective-permute-start(bf16[96,3072]{1,0:T(8,128)(2,1)S(1)} %get-tuple-element.282), channel_id=1, source_target_pairs={{0,4},{1,5},{2,6},{3,7},{4,0},{5,1},{6,2},{7,3},{8,12},{9,13},{10,... | collective-permute-start | bytes 1769480 | tf_op jit(solution)/shard_map/weight_gradients_to_owners/ppermute | solution.py:40
  431.5 12.6 %collective-permute-start.61 = (bf16[48,2048]{1,0:T(8,128)(2,1)S(1)}, bf16[48,2048]{1,0:T(8,128)(2,1)S(1)}, u32[]{:S(2)}, u32[]{:S(2)}) collective-permute-start(bf16[48,2048]{1,0:T(8,128)(2,1)S(1)} %get-tuple-element.339), channel_id=1, source_target_pairs={{0,2},{1,3},{2,0},{3,1},{4,6},{5,7},{6,4},{7,5},{8,10},{9,11},{10,... | collective-permute-start | bytes 589832 | tf_op jit(solution)/shard_map/weight_gradients_to_owners/ppermute | solution.py:40
  432.7 13.3 %collective-permute-start.62 = (bf16[48,2048]{1,0:T(8,128)(2,1)S(1)}, bf16[48,2048]{1,0:T(8,128)(2,1)S(1)}, u32[]{:S(2)}, u32[]{:S(2)}) collective-permute-start(bf16[48,2048]{1,0:T(8,128)(2,1)S(1)} %get-tuple-element.338), channel_id=1, source_target_pairs={{0,4},{1,5},{2,6},{3,7},{4,0},{5,1},{6,2},{7,3},{8,12},{9,13},{10,... | collective-permute-start | bytes 589832 | tf_op jit(solution)/shard_map/weight_gradients_to_owners/ppermute | solution.py:40
  433.5 12.6 %collective-permute-start.63 = (bf16[48,2048]{1,0:T(8,128)(2,1)S(1)}, bf16[48,2048]{1,0:T(8,128)(2,1)S(1)}, u32[]{:S(2)}, u32[]{:S(2)}) collective-permute-start(bf16[48,2048]{1,0:T(8,128)(2,1)S(1)} %get-tuple-element.337), channel_id=1, source_target_pairs={{0,6},{1,7},{2,4},{3,5},{4,2},{5,3},{6,0},{7,1},{8,14},{9,15},{10,... | collective-permute-start | bytes 589832 | tf_op jit(solution)/shard_map/weight_gradients_to_owners/ppermute | solution.py:40
  435.1 9.0 %collective-permute-start.60 = (f32[2,1536]{1,0:T(2,128)S(1)}, f32[2,1536]{1,0:T(2,128)S(1)}, u32[]{:S(2)}, u32[]{:S(2)}) collective-permute-start(f32[2,1536]{1,0:T(2,128)S(1)} %add.584), channel_id=1, source_target_pairs={{0,2},{1,3},{2,0},{3,1},{4,6},{5,7},{6,4},{7,5},{8,10},{9,11},{10,... | collective-permute-start | bytes 36872 | tf_op jit(solution)/shard_map/weight_gradients_to_owners/ppermute | solution.py:40
  440.0 11.9 %collective-permute-start.57 = (bf16[48,3072]{1,0:T(8,128)(2,1)S(1)}, bf16[48,3072]{1,0:T(8,128)(2,1)S(1)}, u32[]{:S(2)}, u32[]{:S(2)}) collective-permute-start(bf16[48,3072]{1,0:T(8,128)(2,1)S(1)} %get-tuple-element.313), channel_id=1, source_target_pairs={{0,24},{1,25},{2,26},{3,27},{4,28},{5,29},{6,30},{7,31},{8,16},{9,... | collective-permute-start | bytes 884744 | tf_op jit(solution)/shard_map/weight_gradients_to_owners/ppermute | solution.py:40
  444.1 21.6 %collective-permute-start.58 = (bf16[48,3072]{1,0:T(8,128)(2,1)S(1)}, bf16[48,3072]{1,0:T(8,128)(2,1)S(1)}, u32[]{:S(2)}, u32[]{:S(2)}) collective-permute-start(bf16[48,3072]{1,0:T(8,128)(2,1)S(1)} %get-tuple-element.314), channel_id=1, source_target_pairs={{0,16},{1,17},{2,18},{3,19},{4,20},{5,21},{6,22},{7,23},{8,24},{9,... | collective-permute-start | bytes 884744 | tf_op jit(solution)/shard_map/weight_gradients_to_owners/ppermute | solution.py:40
  444.1 21.6 %collective-permute-start.59 = (bf16[48,3072]{1,0:T(8,128)(2,1)S(1)}, bf16[48,3072]{1,0:T(8,128)(2,1)S(1)}, u32[]{:S(2)}, u32[]{:S(2)}) collective-permute-start(bf16[48,3072]{1,0:T(8,128)(2,1)S(1)} %get-tuple-element.315), channel_id=1, source_target_pairs={{0,8},{1,9},{2,10},{3,11},{4,12},{5,13},{6,14},{7,15},{8,0},{9,1},... | collective-permute-start | bytes 884744 | tf_op jit(solution)/shard_map/weight_gradients_to_owners/ppermute | solution.py:40
  (64 other events, 389.1 us)
Sparse Core Ops, SparseCore 0:
  77.5 87.8 all-gather.1
  294.0 67.0 reduce-scatter.2
  374.0 47.2 reduce-scatter.4

commit v8 on v7

--- a/solution.py
+++ b/solution.py
@@ -154,6 +154,7 @@
         out_shape=jax.ShapeDtypeStruct((tall, columns + side), w_down.dtype),
         in_specs=[pl.BlockSpec(memory_space=pltpu.SMEM)]
         + [pl.BlockSpec(memory_space=pltpu.VMEM)] * 5,
+        compiler_params=pltpu.CompilerParams(vmem_limit_bytes=8 * 2**20),
         cost_estimate=NO_COST,
         name="merged",
     )(p[None], *came, w_down)
@@ -196,6 +197,7 @@
         in_specs=[pl.BlockSpec(memory_space=pl.ANY)],
         out_specs=pl.BlockSpec(memory_space=pltpu.VMEM),
         scratch_shapes=[pltpu.SemaphoreType.DMA((devices, 1 + ff_rows // low))],
+        compiler_params=pltpu.CompilerParams(vmem_limit_bytes=2 * FFN_VMEM),
         cost_estimate=NO_COST,
         name="w_down_from",
     )(whole)
@@ -224,6 +226,7 @@
     return pl.pallas_call(
         kernel,
         out_shape=jax.ShapeDtypeStruct((rows, sum(widths)), pieces[0].dtype),
+        compiler_params=pltpu.CompilerParams(vmem_limit_bytes=8 * 2**20),
         name="packed",
     )(*pieces)
 
@@ -247,6 +250,7 @@
         out_shape=[shape] * 4,
         in_specs=[pl.BlockSpec(memory_space=pltpu.SMEM)]
         + [pl.BlockSpec(memory_space=pltpu.VMEM)] * 2,
+        compiler_params=pltpu.CompilerParams(vmem_limit_bytes=8 * 2**20),
         name="column_cuts",
     )(p[None], w_gate, w_up)
 
@@ -292,13 +296,13 @@
     with jax.named_scope("phase_1"):
         b = near_side(up, down)
         a, b, passing = tied(local, b, to_pass_on(up, down))
-        a_x, b_y, far, first, *crossing = tied(
-            swap(a, 2), swap(b, 4), along_z(a, far_pairs), along_z(passing, out_pairs), *crossing
+        a_x, b_y, far, first = tied(
+            swap(a, 2), swap(b, 4), along_z(a, far_pairs), along_z(passing, out_pairs)
         )
-        ffn = merged((cuts[0], *crossing), w_down, p)
     with jax.named_scope("phase_2"):
         a2, b2, far = tied(in_order(x, a, a_x), in_order(y, b, b_y), far)
         near_1 = jnp.stack([a2, b2])
+        ffn = merged((cuts[0], *tied(*crossing)), w_down, p)
         a_far, b_far, second = tied(swap(a2, 4), swap(b2, 2), along_z(far, out_pairs))
         out = put(out, near_1, z, z_b, y, x, c)
     with jax.named_scope("ffn_weights"):
@@ -326,7 +330,7 @@
     return gathered, ffn
 
 
-def block_sums(sets, tables, rows, dtype):
+def block_sums(sets, tables, rows, dtype, limit):
     columns = sets[0][0].shape[1]
     count = tables[0][0].shape[0]
     if rows % 16:
@@ -361,7 +365,7 @@
             out_specs=[pl.BlockSpec((rows, columns), lambda i, table: (i, 0))] * len(sets),
         ),
         out_shape=[jax.ShapeDtypeStruct((count * rows, columns), dtype)] * len(sets),
-        compiler_params=pltpu.CompilerParams(vmem_limit_bytes=FFN_VMEM),
+        compiler_params=pltpu.CompilerParams(vmem_limit_bytes=limit),
         cost_estimate=NO_COST,
         name="block_sums",
     )(table, *inputs)
@@ -379,7 +383,9 @@
         a_arrays, b_arrays = [*self.parts, *more_a], [*self.parts, *more_b]
         a_tables = [a, a] + [jnp.atleast_1d(i) for i in at_a]
         b_tables = [b, b] + [jnp.atleast_1d(i) for i in at_b]
-        return block_sums([a_arrays, b_arrays], [a_tables, b_tables], self.tall, dtype)
+        small = not more_a and self.parts[0].shape[1] <= 12 * LANES
+        limit = FFN_VMEM if small else 2 * FFN_VMEM
+        return block_sums([a_arrays, b_arrays], [a_tables, b_tables], self.tall, dtype, limit)
 
     def step_1(self):
         z, y, x, c = self.place_bits
@@ -429,13 +435,13 @@
     a_x, b_y, *beside = tied(swap(a, 2), swap(b, 4), *beside)
     a2, b2 = tied(jnp.concatenate([a, a_x]), jnp.concatenate([b, b_y]))
     a_far, b_far, *beside = tied(swap(a2, 4), swap(b2, 2), *then((a2, b2), *beside))
-    return (jnp.concatenate([a_far, b_far]), *beside)
-
-
-def split_reduce(near, low, beside=(), later=lambda *values: values):
-    two = low.shape[0] // 2
+    return ((a_far, b_far), *beside)
+
+
+def split_reduce(near, far, beside=(), later=lambda *values: values):
+    two = far[0].shape[0]
     one = two // 2
-    came_a, came_b, *beside = tied(swap(low[:two], 4), swap(low[two:], 2), *beside)
+    came_a, came_b, *beside = tied(swap(far[0], 4), swap(far[1], 2), *beside)
     a = near[:two] + came_a.astype(F32)
     b = near[two:] + came_b.astype(F32)
     came_a, came_b, *beside = tied(
@@ -587,6 +593,7 @@
             table,
         ],
         out_specs=[block(q_size, 0), block(kv_size, 0), block(kv_size, 0), block(q_size, 0)],
+        compiler_params=pltpu.CompilerParams(vmem_limit_bytes=16 * 2**20),
         cost_estimate=NO_COST,
         name="attention_forward",
     )(raw, raw, raw, cosine, sine)
@@ -647,6 +654,7 @@
         out_shape=jax.ShapeDtypeStruct((count, width + 2 * kv_width), BF),
         in_specs=[block(q_size), block(q_size), block(kv_size), block(kv_size), table, table],
         out_specs=pl.BlockSpec((SEQ, width + 2 * kv_width), lambda s, j: (s, 0)),
+        compiler_params=pltpu.CompilerParams(vmem_limit_bytes=16 * 2**20),
         cost_estimate=NO_COST,
         name="attention_backward",
     )(grad_mixed, q, k, v, cosine, sine)
@@ -685,7 +693,7 @@
 
 
 FFN_TILE = 256
-FFN_VMEM = 48 * 2**20
+FFN_VMEM = 24 * 2**20
 
 
 def tiles_of(w_both, w_down, units):
@@ -883,43 +891,37 @@
             pl.BlockSpec((1, width), lambda j: (0, 0)),
         ],
         scratch_shapes=[pltpu.VMEM((count, width), F32)],
-        compiler_params=pltpu.CompilerParams(vmem_limit_bytes=FFN_VMEM),
+        compiler_params=pltpu.CompilerParams(vmem_limit_bytes=2 * FFN_VMEM),
         cost_estimate=NO_COST,
         name="input_gradient",
     )(grad_raw, weights, tokens, inv_scale, gain, grad_res)
 
 
-def products(pairs, dtype):
-    tokens, rows = pairs[0][0].shape
-    columns = pairs[0][1].shape[1]
+def products(lefts, rights, dtype):
+    rows, columns = lefts[0].shape[1], rights[0].shape[1]
     tile = columns // 4
+    count = len(lefts)
 
     def kernel(*refs):
         total = None
-        for i in range(len(pairs)):
+        for a, b in zip(refs[:count], refs[count : 2 * count]):
             part = lax.dot_general(
-                refs[2 * i][...],
-                refs[2 * i + 1][...],
-                (((0,), (0,)), ((), ())),
-                preferred_element_type=F32,
+                a[...], b[...], (((0,), (0,)), ((), ())), preferred_element_type=F32
             )
             total = part if total is None else total + part
         refs[-1][...] = total.astype(dtype)
 
-    specs = [
-        pl.BlockSpec((tokens, rows), lambda j: (0, 0)),
-        pl.BlockSpec((tokens, tile), lambda j: (0, j)),
-    ]
     return pl.pallas_call(
         kernel,
         grid=(columns // tile,),
         out_shape=jax.ShapeDtypeStruct((rows, columns), dtype),
-        in_specs=specs * len(pairs),
+        in_specs=[whole(left) for left in lefts]
+        + [pl.BlockSpec((right.shape[0], tile), lambda j: (0, j)) for right in rights],
         out_specs=pl.BlockSpec((rows, tile), lambda j: (0, j)),
         compiler_params=pltpu.CompilerParams(vmem_limit_bytes=FFN_VMEM),
         cost_estimate=NO_COST,
         name="products",
-    )(*[array for pair in pairs for array in pair])
+    )(*lefts, *rights)
 
 
 def body(
@@ -949,6 +951,7 @@
     ff = w_gate.shape[1]
     count = tokens.shape[0]
     cosine, sine = rotation_lanes()
+    to_column, by_side = tied(reordered(width, rows, "zcyx"), reordered(width, rows, "cxyz"))
 
     part = 2 * ff_rows
     units = planes * part
@@ -969,7 +972,7 @@
         gain_mid = gathered[:, wide + width + 1].astype(F32)
         inputs_f = tokens.astype(F32)
         normed, inv_attn = norm_rows(inputs_f, gain_in)
-        normed_in = normed.astype(BF)
+        normed_in = tied(normed.astype(BF))[0]
         raw = mm(normed_in, wqkv)
         query, key, value, mixed = attention_forward(raw, cosine, sine, width, kv_width)
         hidden_res = inputs_f + mm(mixed, wo)
@@ -977,21 +980,21 @@
         normed_mid = normed_two.astype(BF)
 
     with jax.named_scope("ffn_forward"):
-        to_column = reordered(width, rows, "zcyx")
         far, y_near, *kept = split_gather(
             mm(normed_mid, to_column).astype(BF),
             (),
             lambda pieces: ffn_forward_beside(pieces, wb, wd),
         )
         near, hid_near, gate_near, up_near = kept
-        y_far, pre_far, hid_far = ffn_forward(far, wb, wd)
-        y_far, mixed, normed_in = tied(y_far, mixed, normed_in)
-        by_side = reordered(width, rows, "cxyz")
+        y_a, pre_a, hid_a = ffn_forward(far[0], wb, wd)
+        y_b, pre_b, hid_b = ffn_forward(far[1], wb, wd)
+        y_a, y_b = y_a.astype(BF), y_b.astype(BF)
+        y_b, mixed, normed_in = tied(y_b, mixed, normed_in)
         beside = (
             *core_halves(mm(mixed, by_side).astype(BF), c),
             *core_halves(mm(normed_in, by_side).astype(BF), c),
         )
-        result, *halves = split_reduce(y_near, y_far.astype(BF), beside)
+        result, *halves = split_reduce(y_near, (y_a, y_b), beside)
         mixed_mine, mixed_theirs, normed_mine, normed_theirs = halves
         result = hidden_res + result
         out_act = result.astype(BF)
@@ -999,45 +1002,42 @@
     with jax.named_scope("loss"):
         mask_f = valid_mask.astype(F32)
         grad_out = (result - teacher.astype(F32)) * mask_f[:, None]
-        sums = jnp.stack([jnp.sum(grad_out * grad_out), jnp.sum(mask_f)])
-        sums = jnp.broadcast_to(sums[:, None], (2, LANES))
 
     high = n // 2
     rest = [1 << k for k in range(4, n.bit_length() - 2)]
 
     with jax.named_scope("ffn_backward"):
-        def near_backward(pieces, sums):
+        def near_backward(pieces, grads):
+            sums = jnp.stack([jnp.sum(grads * grads), jnp.sum(mask_f)])
             return (
-                sums,
-                swap(sums, 1),
+                jnp.broadcast_to(sums[:, None], (2, LANES)),
                 *ffn_backward_beside(pieces, gate_near, up_near, wb, wd),
             )
 
-        d_far, sums, came, m_near, d_near, g_near = split_gather(
-            grad_out.astype(BF), (sums,), near_backward
+        d_far, sums, m_near, d_near, g_near = split_gather(
+            grad_out.astype(BF), (grad_out,), near_backward
         )
+        m_a, g_a = ffn_backward(d_far[0], pre_a, wb, wd)
+        m_b, g_b = ffn_backward(d_far[1], pre_b, wb, wd)
+        m_b, m_near, sums = tied(m_b.astype(BF), m_near, sums)
+        came = swap(sums, 1)
+        beside = (products([near, *far], [g_near, g_a, g_b], BF), sums, came)
+
+        owned_both = []
+
+        def later(g_both, sums, came):
+            owned_both.append(sum_to_owners(g_both))
+            sums = sums + came
+            g_down = products([hid_near, hid_a, hid_b], [d_near, *d_far], BF)
+            return (g_down, sums, swap(sums, 8))
+
+        grad_mid, g_down, sums, came = split_reduce(
+            m_near, (m_a.astype(BF), m_b), beside, later
+        )
+        g_both = owned_both[0]
         sums = sums + came
         for mask in rest:
             sums = sums + swap(sums, mask)
-        m_far, g_far = ffn_backward(d_far, pre_far, wb, wd)
-        m_near, m_far, sums = tied(m_near, m_far.astype(BF), sums)
-        beside = (
-            products([(near, g_near), (far, g_far)], BF),
-            sums,
-            swap(sums, 8),
-        )
-
-        owned_both = []
-
-        def later(g_both, sums, came):
-            owned_both.append(sum_to_owners(g_both))
-            sums = sums + came
-            g_down = products([(hid_near, d_near), (hid_far, d_far)], BF)
-            return (g_down, sums, swap(sums, high))
-
-        grad_mid, g_down, sums, came = split_reduce(m_near, m_far, beside, later)
-        g_both = owned_both[0]
-        sums = sums + came
         high_part = grad_mid.astype(BF)
         low_part = (grad_mid - high_part.astype(F32)).astype(BF)
         grad_mid = mm_t(high_part, to_column) + mm_t(low_part, to_column)
@@ -1046,13 +1046,14 @@
         grad_gain_mid, grad_res = norm_back(grad_mid, hidden_res, inv_ffn, gain_mid)
         grad_res = grad_out + grad_res
         res_low = grad_res.astype(BF)
-        wo_came, came = tied(swap(t_mm(mixed_theirs, res_low).astype(BF), 1), swap(sums, 2))
+        wo_came, came = tied(swap(t_mm(mixed_theirs, res_low).astype(BF), 1), swap(sums, high))
         sums = sums + came
         g_wo = PlaneSum([t_mm(mixed_mine, res_low), wo_came], rows, bits)
         wo_moving = g_wo.step_1()
         grad_mixed = mm_t(res_low, wo).astype(BF)
         grad_raw = attention_backward(grad_mixed, query, key, value, cosine, sine)
-        *wo_came, grad_raw = tied(*wo_moving, grad_raw)
+        *wo_came, grad_raw, sums, came = tied(*wo_moving, grad_raw, sums, swap(sums, 2))
+        sums = sums + came
         wo_moving = g_wo.step_2(wo_came)
 
     with jax.named_scope("q_k_v_weight_gradients"):
@@ -1067,8 +1068,7 @@
         g_qkv = PlaneSum([g_qkv, qkv_came], rows, bits)
         qkv_moving = g_qkv.step_1()
         g_wo = g_wo.step_3(wo_came)
-        if planes == 4:
-            wo_moving = direct([g_wo], z)
+        wo_moving = direct([g_wo], z) if planes == 4 else []
 
     with jax.named_scope("input_gradient"):
         input_grad, grad_gain_in = input_gradient(
@@ -1077,17 +1077,15 @@
         gains = jnp.concatenate([grad_gain_in, grad_gain_mid[None]])
 
     with jax.named_scope("weight_gradients_to_owners"):
-        if planes == 4:
-            qkv_0, qkv_1, gains, wo_0, wo_1, wo_2 = tied(*qkv_moving, gains, *wo_moving)
-            g_wo = owned([g_wo], (wo_0, wo_1, wo_2), z)
-            qkv_came = (qkv_0, qkv_1)
-        else:
-            *qkv_came, gains = tied(*qkv_moving, gains)
-            g_wo = z_reduce([g_wo])
+        *qkv_came, gains = tied(*qkv_moving, gains)
         qkv_moving = g_qkv.step_2(qkv_came)
         for mask in (1, 8, high):
             gains = gains + swap(gains, mask)
-        *qkv_came, gains, g_both, g_down = tied(*qkv_moving, gains, g_both, g_down)
+        qkv_0, qkv_1, gains, g_both, g_down, *wo_came = tied(
+            *qkv_moving, gains, g_both, g_down, *wo_moving
+        )
+        qkv_came = (qkv_0, qkv_1)
+        g_wo = owned([g_wo], wo_came, z) if planes == 4 else z_reduce([g_wo])
         g_qkv = g_qkv.step_3(qkv_came)
         if planes == 4:
             moving = direct([g_qkv], z)

time: 483 us -> 474 us (0.981)
  local copies, waits for them, and re-layouts: 41.4 us -> 59.4 us
  waiting for transfers between devices: 141 us -> 123 us
  Pallas kernels: 113 us -> 95.1 us
  starting transfers between devices: 68.1 us -> 77.9 us
  matrix products: 61.5 us -> 52.6 us
  other arithmetic: 32.2 us -> 40.8 us
    unnamed x137 -> x225, local copies, waits for them, and re-layouts: 10.9 us -> 30.3 us
    ppermute x60, waiting for transfers between devices: 131 us -> 119 us  [swap(): return lax.ppermute(value, 'dp', [(i, i ^ mask) for i in range(n)])]
    dot_general x16 -> x20, matrix products: 61.5 us -> 52.6 us  [dot(): return lax.dot_general(a, b, (dims, ((), ())), preferred_element_type=F32)]
    convert_element_type x1 -> x3, other arithmetic: 0.25 us -> 8.91 us  [the longest x2 8.66 us: reordered(): return (jnp.arange(count)[:, None] == source[None, :]).astype(BF)]
    ppermute x60, starting transfers between devices: 53.8 us -> 62.4 us  [swap(): return lax.ppermute(value, 'dp', [(i, i ^ mask) for i in range(n)])]
    ppermute x5, waiting for transfers between devices: 10.6 us -> 4.35 us  [along_z(): lax.ppermute(value, 'dp', [(8 * a + i, 8 * b + i) for a, b in pairs for i...]
  transfers between devices with their start and end apart: 68 -> 68, of which waited for: 36 -> 30; matrix products, arithmetic and copies ran while one was open for 20% -> 23% of each run, Pallas kernels for 23% -> 20%
where the time goes in v8:
time: 474 us; the launch traced here: 467 us
  waiting for transfers between devices  123 us (26%)
  Pallas kernels  95.1 us (20%)
  starting transfers between devices  77.9 us (16%)
  local copies, waits for them, and re-layouts  59.4 us (13%)
  matrix products  52.6 us (11%)
  other arithmetic  40.8 us (9%)
  between operations  18.3 us (4%)
    ppermute x60, waiting for transfers between devices, swap(): return lax.ppermute(value, 'dp', [(i, i ^ mask) for i in range(n)])  119 us
    ppermute x60, starting transfers between devices, swap(): return lax.ppermute(value, 'dp', [(i, i ^ mask) for i in range(n)])  62.4 us
    dot_general x20, matrix products, dot(): return lax.dot_general(a, b, (dims, ((), ())), preferred_element_type=F32)  52.6 us
    unnamed x225, local copies, waits for them, and re-layouts  30.3 us
    dynamic_update_slice x16, local copies, waits for them, and re-layouts, place(): return lax.dynamic_update_slice(out, piece, where)  19.7 us
    pallas_call x6, Pallas kernels, block_sums(): pl.pallas_call(kernel, grid_spec=pltpu.PrefetchScalarGridSpec(num_scalar_...  17.7 us
    pallas_call x2, Pallas kernels, products(): pl.pallas_call(kernel, grid=(columns // tile,), out_shape=jax.ShapeDtypeS...  15.5 us
    ppermute x5, starting transfers between devices, along_z(): lax.ppermute(value, 'dp', [(8 * a + i, 8 * b + i) for a, b in pairs for i...  15.1 us
  transfers between devices with their start and end apart: 68, of which 30 were waited for; matrix products, arithmetic and copies ran while one was open for 23% of the time, Pallas kernels for 20%

profile of v8, /device:TPU:0, one launch (start us, length us, event | category | flops | bytes accessed | tf_op | source)
XLA Modules:
  0.0 467.3 jit_solution(6397663858117754926)
XLA Ops:
  11.7 5.0 %collective-permute-start = (bf16[48,4736]{1,0:T(8,128)(2,1)S(1)}, bf16[48,4736]{1,0:T(8,128)(2,1)S(1)}, u32[]{:S(2)}, u32[]{:S(2)}) collective-permute-start(bf16[48,4736]{1,0:T(8,128)(2,1)S(1)} %packed.1), channel_id=1, source_target_pairs={{0,8},{1,9},{2,10},{3,11},{4,12},{5,13},{6,14},{7,15},{8,16},{9,17... | collective-permute-start | bytes 1363976 | tf_op jit(solution)/shard_map/phase_0/ppermute | solution.py:77
  23.2 4.3 fusion.2
  27.5 4.3 fusion.3
  33.5 6.3 %collective-permute-start.4 = (bf16[48,4736]{1,0:T(8,128)(2,1)S(1)}, bf16[48,4736]{1,0:T(8,128)(2,1)}, u32[]{:S(2)}, u32[]{:S(2)}) collective-permute-start(bf16[48,4736]{1,0:T(8,128)(2,1)S(1)} %packed.1), channel_id=1, source_target_pairs={{0,16},{1,17},{2,18},{3,19},{4,20},{5,21},{6,22},{7,23},{24,8},{25... | collective-permute-start | bytes 1363976 | tf_op jit(solution)/shard_map/phase_1/ppermute | solution.py:77
  44.4 2.5 collective-permute-start.23
  46.9 4.2 collective-permute-done.23.refs_3_
  52.3 2.6 collective-permute-done.3
  62.0 1.8 broadcast_select_fusion.1
  65.2 4.3 collective-permute-done.8
  69.6 6.4 %collective-permute-done.6 = bf16[2,48,4736]{2,1,0:T(8,128)(2,1)S(1)} collective-permute-done((bf16[2,48,4736]{2,1,0:T(8,128)(2,1)S(1)}, bf16[2,48,4736]{2,1,0:T(8,128)(2,1)S(1)}, u32[]{:S(2)}, u32[]{:S(2)}) %collective-permute-start.6) | collective-permute-done | bytes 909344 | tf_op jit(solution)/shard_map/phase_2/ppermute | solution.py:40
  80.5 2.2 bitcast_dynamic-update-slice_fusion.13
  83.9 7.1 %collective-permute-done.10 = bf16[48,4736]{1,0:T(8,128)(2,1)} collective-permute-done((bf16[48,4736]{1,0:T(8,128)(2,1)}, bf16[48,4736]{1,0:T(8,128)(2,1)}, u32[]{:S(2)}, u32[]{:S(2)}) %collective-permute-start.10) | collective-permute-done | bytes 454688 | tf_op jit(solution)/shard_map/phase_3/ppermute | solution.py:40
  97.2 2.2 bitcast_dynamic-update-slice_fusion.11
  99.3 2.2 bitcast_dynamic-update-slice_fusion.10
  103.7 13.3 %collective-permute-done.12 = bf16[2,48,4736]{2,1,0:T(8,128)(2,1)S(1)} collective-permute-done((bf16[2,48,4736]{2,1,0:T(8,128)(2,1)S(1)}, bf16[2,48,4736]{2,1,0:T(8,128)(2,1)S(1)}, u32[]{:S(2)}, u32[]{:S(2)}) %collective-permute-start.12) | collective-permute-done | bytes 909344 | tf_op jit(solution)/shard_map/phase_4/ppermute | solution.py:40
  122.7 1.8 collective-permute-done.16
  131.3 5.3 %fusion.q_raw.k_raw.v_raw = f32[256,3072]{1,0:T(8,128)S(1)} fusion(bf16[256,1536]{1,0:T(8,128)(2,1)S(1)} %fusion.30, bf16[1536,4736]{1,0:T(8,128)(2,1)} %bitcast.212), kind=kOutput, calls=%fused_computation | convolution fusion | flops 2415919104 | bytes 13369344 | tf_op jit(solution)/shard_map/attention_forward/dot_general | solution.py:23
  136.6 12.6 %attention_forward.1 = (bf16[256,1536]{1,0:T(8,128)(2,1)S(1)}, bf16[256,768]{1,0:T(8,128)(2,1)S(1)}, bf16[256,768]{1,0:T(8,128)(2,1)S(1)}, bf16[256,1536]{1,0:T(8,128)(2,1)S(1)}) custom-call(f32[256,3072]{1,0:T(8,128)S(1)} %fusion.q_raw.k_raw.v_raw, f32[256,3072]{1,0:T(8,128)S(1)} %fusion.q_raw.k_raw.v_raw, f32[256,3072]{1,0:T(8,128)S(1)} %fusion.q_raw.k_raw.v_raw, ...), custom_call_target="tpu_custom_call" | custom-call | flops 1 | bytes 1 | tf_op jit(solution)/shard_map/attention_forward/attention_forward/pallas_call | solution.py:579
  150.8 4.3 multiply_reduce_fusion.3
  159.9 8.6 %collective-permute-done.17 = bf16[128,1536]{1,0:T(8,128)(2,1)S(1)} collective-permute-done((bf16[128,1536]{1,0:T(8,128)(2,1)S(1)}, bf16[128,1536]{1,0:T(8,128)(2,1)S(1)}, u32[]{:S(2)}, u32[]{:S(2)}) %collective-permute-start.17) | collective-permute-done | bytes 393248 | tf_op jit(solution)/shard_map/ffn_forward/ppermute | solution.py:40
  173.1 2.2 w_down_from.1.refs_4_.refs_6_
  175.3 3.7 copy-done.1
  179.0 9.9 %ffn_forward_beside.1 = (f32[512,1536]{1,0:T(8,128)S(1)}, bf16[512,1536]{1,0:T(8,128)(2,1)S(1)}, bf16[512,1024]{1,0:T(8,128)(2,1)S(1)}, f32[512,1024]{1,0:T(8,128)S(1)}, f32[512,1024]{1,0:T(8,128)S(1)}) custom-call(bf16[256,1536]{1,0:T(8,128)(2,1)} %pad_maximum_fusion.11.refs_0_, bf16[256,1536]{1,0:T(8,128)(2,1)} %pad_maximum_fusion.12.refs_1_, ...), custom_call_target="tpu_custom_call" | custom-call | flops 1 | bytes 1 | tf_op jit(solution)/shard_map/ffn_forward/ffn_forward_beside/pallas_call | solution.py:764
  191.0 2.9 fusion.12
  196.1 2.9 fusion.14
  206.1 6.4 %collective-permute-done.25 = bf16[256,1536]{1,0:T(8,128)(2,1)S(1)} collective-permute-done((bf16[256,1536]{1,0:T(8,128)(2,1)S(1)}, bf16[256,1536]{1,0:T(8,128)(2,1)S(1)}, u32[]{:S(2)}, u32[]{:S(2)}) %collective-permute-start.25) | collective-permute-done | bytes 786464 | tf_op jit(solution)/shard_map/ffn_forward/ppermute | solution.py:40
  212.5 4.9 %collective-permute-done.24 = bf16[256,1536]{1,0:T(8,128)(2,1)S(1)} collective-permute-done((bf16[256,1536]{1,0:T(8,128)(2,1)S(1)}, bf16[256,1536]{1,0:T(8,128)(2,1)S(1)}, u32[]{:S(2)}, u32[]{:S(2)}) %collective-permute-start.24) | collective-permute-done | bytes 786464 | tf_op jit(solution)/shard_map/ffn_forward/ppermute | solution.py:40
  220.5 5.4 %collective-permute-done.26 = bf16[128,1536]{1,0:T(8,128)(2,1)S(1)} collective-permute-done((bf16[128,1536]{1,0:T(8,128)(2,1)S(1)}, bf16[128,1536]{1,0:T(8,128)(2,1)S(1)}, u32[]{:S(2)}, u32[]{:S(2)}) %collective-permute-start.26) | collective-permute-done | bytes 393248 | tf_op jit(solution)/shard_map/ffn_forward/ppermute | solution.py:40
  230.6 7.1 %collective-permute-done.28 = bf16[128,1536]{1,0:T(8,128)(2,1)S(1)} collective-permute-done((bf16[128,1536]{1,0:T(8,128)(2,1)S(1)}, bf16[128,1536]{1,0:T(8,128)(2,1)S(1)}, u32[]{:S(2)}, u32[]{:S(2)}) %collective-permute-start.28) | collective-permute-done | bytes 393248 | tf_op jit(solution)/shard_map/ffn_backward/ppermute | solution.py:40
  237.7 2.7 collective-permute-done.29
  243.5 12.4 %ffn_backward_beside.1 = (f32[512,1536]{1,0:T(8,128)S(1)}, bf16[512,1536]{1,0:T(8,128)(2,1)S(1)}, bf16[512,2048]{1,0:T(8,128)(2,1)S(1)}) custom-call(bf16[256,1536]{1,0:T(8,128)(2,1)S(1)} %pad_maximum_fusion.13.refs_0_, bf16[256,1536]{1,0:T(8,128)(2,1)S(1)} %pad_maximum_fusion.14.refs_1_, f32[512,1024]{1,0:T(8,128)S(1)} %get-tuple-element.230.refs_2_, ...), custom_call_target="tpu_custom_call" | custom-call | flops 1 | bytes 1 | tf_op jit(solution)/shard_map/ffn_backward/ffn_backward_beside/pallas_call | solution.py:829
  263.3 2.7 fusion.19
  266.6 2.7 fusion.22
  270.5 9.5 %products.2 = bf16[1536,2048]{1,0:T(8,128)(2,1)S(1)} custom-call(bf16[512,1536]{1,0:T(8,128)(2,1)S(1)} %get-tuple-element.241.refs_0_, bf16[256,1536]{1,0:T(8,128)(2,1)} %collective-permute-done.19.refs_1_, bf16[256,1536]{1,0:T(8,128)(2,1)} %collective-permute-done.20.refs_2_, bf16[512,2048]{1,0:T(8,128)(2,1)S(1)} %get-tuple-element.242.refs_3_, ...), custom_call_target="tpu_custom_call" | custom-call | flops 1 | bytes 1 | tf_op jit(solution)/shard_map/ffn_backward/products/pallas_call | solution.py:914
  280.0 2.6 copy-done.3
  282.7 1.8 copy-done.16
  284.5 1.9 convert_add_fusion.1
  289.8 1.9 collective-permute-start.37
  291.8 6.0 %products.3 = bf16[1024,1536]{1,0:T(8,128)(2,1)S(1)} custom-call(bf16[512,1024]{1,0:T(8,128)(2,1)S(1)} %copy-done.34, bf16[256,1024]{1,0:T(8,128)(2,1)S(1)} %copy-done.30, bf16[256,1024]{1,0:T(8,128)(2,1)S(1)} %copy-done.28, bf16[512,1536]{1,0:T(8,128)(2,1)S(1)} %copy-done.32, bf16[256,1536]{1,0:T(8,128)(2,1)S(1)} %copy-done.38, bf16[256,1536]{1,0:T(8,128)(2,1)S(1)} %copy-done.40), custom_call_target="tpu_custom_call" | custom-call | flops 1 | bytes 1 | tf_op jit(solution)/shard_map/ffn_backward/products/pallas_call | solution.py:914
  302.7 3.9 fusion.32
  306.7 2.3 multiply_reduce_fusion
  310.0 2.2 convolution_convert_fusion.1
  314.1 2.2 fusion.121.refs_0_.refs_2_.refs_3_.refs_4_
  321.8 3.8 fusion.25.d_ref
  325.7 14.3 %attention_backward.1.grads = bf16[256,3072]{1,0:T(8,128)(2,1)S(1)} custom-call(bf16[256,1536]{1,0:T(8,128)(2,1)S(1)} %fusion.25.d_ref, bf16[256,1536]{1,0:T(8,128)(2,1)S(1)} %copy-done.36, bf16[256,768]{1,0:T(8,128)(2,1)S(1)} %copy-done.43, bf16[256,768]{1,0:T(8,128)(2,1)S(1)} %copy-done.45, f32[128,768]{1,0:T(8,128)S(1)} %copy.82.cosine, ...), custom_call_target="tpu_custom_call" | custom-call | flops 1 | bytes 1 | tf_op jit(solution)/shard_map/attention_backward/attention_backward/pallas_call | solution.py:651
  340.1 3.6 convolution_convert_fusion
  346.2 2.1 block_sums.7
  351.0 5.1 %fusion.128.refs_0_.refs_2_.refs_3_.refs_4_ = f32[768,3072]{1,0:T(8,128)} fusion(bf16[256,768]{1,0:T(8,128)(2,1)S(1)} %copy-done.74, bf16[256,3072]{1,0:T(8,128)(2,1)S(1)} %copy-done.8), kind=kOutput, calls=%fused_computation.319 | convolution fusion | flops 1207959552 | bytes 11403264 | tf_op jit(solution)/shard_map/q_k_v_weight_gradients/dot_general | solution.py:23
  356.1 2.0 collective-permute-done.44
  359.7 4.8 %block_sums.8 = (bf16[192,3072]{1,0:T(8,128)(2,1)}, bf16[192,3072]{1,0:T(8,128)(2,1)}) custom-call(s32[4,2]{1,0:T(4,128)S(1)} %pad_add_fusion.table, f32[768,3072]{1,0:T(8,128)} %fusion.128.refs_0_.refs_2_.refs_3_.refs_4_, bf16[768,3072]{1,0:T(8,128)(2,1)} %collective-permute-done.43.refs_1_.refs_3_.refs_4_.refs_5_, ...), custom_call_target="tpu_custom_call" | custom-call | flops 1 | bytes 1 | tf_op jit(solution)/shard_map/q_k_v_weight_gradients/block_sums/pallas_call | solution.py:359
  369.8 9.3 %input_gradient.1 = (bf16[256,1536]{1,0:T(8,128)(2,1)}, f32[1,1536]{1,0:T(1,128)S(1)}) custom-call(bf16[256,3072]{1,0:T(8,128)(2,1)S(1)} %copy-done.9, bf16[1536,4736]{1,0:T(8,128)(2,1)} %bitcast.215, bf16[256,1536]{1,0:T(8,128)(2,1)S(1)} %copy-done.12, f32[256,1]{1,0:T(8,128)S(1)} %copy.87.inv_scale, f32[1,1536]{1,0:T(1,128)S(1)} %reshape.378.gain, ...), custom_call_target="tpu_custom_call" | custom-call | flops 1 | bytes 1 | tf_op jit(solution)/shard_map/input_gradient/input_gradient/pallas_call | solution.py:874
  379.2 12.9 %collective-permute-done.47.refs_2_ = bf16[192,3072]{1,0:T(8,128)(2,1)} collective-permute-done((bf16[192,3072]{1,0:T(8,128)(2,1)}, bf16[192,3072]{1,0:T(8,128)(2,1)}, u32[]{:S(2)}, u32[]{:S(2)}) %collective-permute-start.47) | collective-permute-done | bytes 1179680 | tf_op jit(solution)/shard_map/q_k_v_weight_gradients/ppermute | solution.py:40
  392.6 4.1 block_sums.9
  404.7 2.1 block_sums.10
  407.7 1.9 collective-permute-start.53
  412.3 2.0 collective-permute-start.56
  416.8 1.7 collective-permute-done.54
  418.5 6.7 %collective-permute-done.55 = bf16[48,1536]{1,0:T(8,128)(2,1)S(1)} collective-permute-done((bf16[48,1536]{1,0:T(8,128)(2,1)S(1)}, bf16[48,1536]{1,0:T(8,128)(2,1)S(1)}, u32[]{:S(2)}, u32[]{:S(2)}) %collective-permute-start.55) | collective-permute-done | bytes 147488 | tf_op jit(solution)/shard_map/q_k_v_weight_gradients/ppermute | solution.py:40
  427.0 1.9 collective-permute-start.63
  429.5 3.7 block_sums.11
  433.6 1.8 collective-permute-start.57
  437.2 2.6 collective-permute-start.59
  441.3 2.3 collective-permute-done.64
  445.4 12.3 %collective-permute-done.58 = bf16[48,3072]{1,0:T(8,128)(2,1)S(1)} collective-permute-done((bf16[48,3072]{1,0:T(8,128)(2,1)S(1)}, bf16[48,3072]{1,0:T(8,128)(2,1)S(1)}, u32[]{:S(2)}, u32[]{:S(2)}) %collective-permute-start.58) | collective-permute-done | bytes 294944 | tf_op jit(solution)/shard_map/weight_gradients_to_owners/ppermute | solution.py:40
  (450 shorter events, 146.2 us)
Async XLA Ops:
  7.2 165.9 %all-gather.2.cloned.1.call-start = ((), (), s32[]{:S(2)}) async-start(), calls=%async_computation.2 | async-start | bytes 10616832 | tf_op jit(solution)/shard_map/ffn_weights/all_gather | solution.py:114
  11.7 20.2 %collective-permute-start = (bf16[48,4736]{1,0:T(8,128)(2,1)S(1)}, bf16[48,4736]{1,0:T(8,128)(2,1)S(1)}, u32[]{:S(2)}, u32[]{:S(2)}) collective-permute-start(bf16[48,4736]{1,0:T(8,128)(2,1)S(1)} %packed.1), channel_id=1, source_target_pairs={{0,8},{1,9},{2,10},{3,11},{4,12},{5,13},{6,14},{7,15},{8,16},{9,17... | collective-permute-start | bytes 1363976 | tf_op jit(solution)/shard_map/phase_0/ppermute | solution.py:77
  16.6 15.3 %collective-permute-start.1 = (bf16[48,4736]{1,0:T(8,128)(2,1)S(1)}, bf16[48,4736]{1,0:T(8,128)(2,1)S(1)}, u32[]{:S(2)}, u32[]{:S(2)}) collective-permute-start(bf16[48,4736]{1,0:T(8,128)(2,1)S(1)} %packed.1), channel_id=1, source_target_pairs={{8,0},{9,1},{10,2},{11,3},{12,4},{13,5},{14,6},{15,7},{16,8},{17,9... | collective-permute-start | bytes 1363976 | tf_op jit(solution)/shard_map/phase_0/ppermute | solution.py:77
  20.1 20.3 %collective-permute-start.21 = (bf16[48,2048]{1,0:T(8,128)(2,1)S(1)}, bf16[48,2048]{1,0:T(8,128)(2,1)S(1)}, u32[]{:S(2)}, u32[]{:S(2)}) collective-permute-start(bf16[48,2048]{1,0:T(8,128)(2,1)S(1)} %get-tuple-element.197), channel_id=1, source_target_pairs={{0,2},{1,3},{2,0},{3,1},{4,6},{5,7},{6,4},{7,5},{8,10},{9,11},{10,... | collective-permute-start | bytes 589832 | tf_op jit(solution)/shard_map/phase_0/ppermute | solution.py:40
  21.6 22.7 %collective-permute-start.22 = (bf16[48,2048]{1,0:T(8,128)(2,1)S(1)}, bf16[48,2048]{1,0:T(8,128)(2,1)S(1)}, u32[]{:S(2)}, u32[]{:S(2)}) collective-permute-start(bf16[48,2048]{1,0:T(8,128)(2,1)S(1)} %get-tuple-element.198), channel_id=1, source_target_pairs={{0,4},{1,5},{2,6},{3,7},{4,0},{5,1},{6,2},{7,3},{8,12},{9,13},{10,... | collective-permute-start | bytes 589832 | tf_op jit(solution)/shard_map/phase_0/ppermute | solution.py:40
  33.0 19.3 %collective-permute-start.2 = (bf16[48,4736]{1,0:T(8,128)(2,1)S(1)}, bf16[48,4736]{1,0:T(8,128)(2,1)}, u32[]{:S(2)}, u32[]{:S(2)}) collective-permute-start(bf16[48,4736]{1,0:T(8,128)(2,1)S(1)} %packed.1), channel_id=1, source_target_pairs={{0,2},{1,3},{2,0},{3,1},{4,6},{5,7},{6,4},{7,5},{8,10},{9,11},{10,... | collective-permute-start | bytes 1363976 | tf_op jit(solution)/shard_map/phase_1/ppermute | solution.py:40
  33.5 18.8 %collective-permute-start.4 = (bf16[48,4736]{1,0:T(8,128)(2,1)S(1)}, bf16[48,4736]{1,0:T(8,128)(2,1)}, u32[]{:S(2)}, u32[]{:S(2)}) collective-permute-start(bf16[48,4736]{1,0:T(8,128)(2,1)S(1)} %packed.1), channel_id=1, source_target_pairs={{0,16},{1,17},{2,18},{3,19},{4,20},{5,21},{6,22},{7,23},{24,8},{25... | collective-permute-start | bytes 1363976 | tf_op jit(solution)/shard_map/phase_1/ppermute | solution.py:77
  39.8 15.0 %collective-permute-start.3 = (bf16[48,4736]{1,0:T(8,128)(2,1)}, bf16[48,4736]{1,0:T(8,128)(2,1)}, u32[]{:S(2)}, u32[]{:S(2)}) collective-permute-start(bf16[48,4736]{1,0:T(8,128)(2,1)} %get-tuple-element.162), channel_id=1, source_target_pairs={{0,4},{1,5},{2,6},{3,7},{4,0},{5,1},{6,2},{7,3},{8,12},{9,13},{10,... | collective-permute-start | bytes 1363976 | tf_op jit(solution)/shard_map/phase_1/ppermute | solution.py:40
  40.3 14.5 %collective-permute-start.5 = (bf16[48,4736]{1,0:T(8,128)(2,1)}, bf16[48,4736]{1,0:T(8,128)(2,1)}, u32[]{:S(2)}, u32[]{:S(2)}) collective-permute-start(bf16[48,4736]{1,0:T(8,128)(2,1)} %get-tuple-element.163), channel_id=1, source_target_pairs={{8,0},{9,1},{10,2},{11,3},{12,4},{13,5},{14,6},{15,7},{16,24},{17,... | collective-permute-start | bytes 1363976 | tf_op jit(solution)/shard_map/phase_1/ppermute | solution.py:77
  44.4 6.7 %collective-permute-start.23 = (bf16[48,2048]{1,0:T(8,128)(2,1)S(1)}, bf16[48,2048]{1,0:T(8,128)(2,1)S(1)}, u32[]{:S(2)}, u32[]{:S(2)}) collective-permute-start(bf16[48,2048]{1,0:T(8,128)(2,1)S(1)} %get-tuple-element.199), channel_id=1, source_target_pairs={{0,6},{1,7},{2,4},{3,5},{4,2},{5,3},{6,0},{7,1},{8,14},{9,15},{10,... | collective-permute-start | bytes 589832 | tf_op jit(solution)/shard_map/phase_0/ppermute | solution.py:40
  56.5 19.4 %collective-permute-start.6 = (bf16[2,48,4736]{2,1,0:T(8,128)(2,1)S(1)}, bf16[2,48,4736]{2,1,0:T(8,128)(2,1)S(1)}, u32[]{:S(2)}, u32[]{:S(2)}) collective-permute-start(bf16[2,48,4736]{2,1,0:T(8,128)(2,1)S(1)} %pad_maximum_fusion.7), channel_id=1, source_target_pairs={{0,4},{1,5},{2,6},{3,7},{4,0},{5,1},{6,2},{7,3},{8,12},{9,13},{10,... | collective-permute-start | bytes 2727944 | tf_op jit(solution)/shard_map/phase_2/ppermute | solution.py:40
  57.1 18.9 %collective-permute-start.7 = (bf16[2,48,4736]{2,1,0:T(8,128)(2,1)S(1)}, bf16[2,48,4736]{2,1,0:T(8,128)(2,1)S(1)}, u32[]{:S(2)}, u32[]{:S(2)}) collective-permute-start(bf16[2,48,4736]{2,1,0:T(8,128)(2,1)S(1)} %pad_maximum_fusion.8), channel_id=1, source_target_pairs={{0,2},{1,3},{2,0},{3,1},{4,6},{5,7},{6,4},{7,5},{8,10},{9,11},{10,... | collective-permute-start | bytes 2727944 | tf_op jit(solution)/shard_map/phase_2/ppermute | solution.py:40
  58.6 10.9 %collective-permute-start.8 = (bf16[48,4736]{1,0:T(8,128)(2,1)}, bf16[48,4736]{1,0:T(8,128)(2,1)S(1)}, u32[]{:S(2)}, u32[]{:S(2)}) collective-permute-start(bf16[48,4736]{1,0:T(8,128)(2,1)} %collective-permute-done.4), channel_id=1, source_target_pairs={{8,0},{9,1},{10,2},{11,3},{12,4},{13,5},{14,6},{15,7},{16,24},{17,... | collective-permute-start | bytes 1363976 | tf_op jit(solution)/shard_map/phase_2/ppermute | solution.py:77
  77.9 13.7 %collective-permute-start.11 = (bf16[2,2,48,4736]{3,2,1,0:T(8,128)(2,1)}, bf16[2,2,48,4736]{3,2,1,0:T(8,128)(2,1)}, u32[]{:S(2)}, u32[]{:S(2)}) collective-permute-start(bf16[2,2,48,4736]{3,2,1,0:T(8,128)(2,1)} %pad_maximum_fusion), channel_id=1, source_target_pairs={{0,1},{1,0},{2,3},{3,2},{4,5},{5,4},{6,7},{7,6},{8,9},{9,8},{10,11... | collective-permute-start | bytes 5455880 | tf_op jit(solution)/shard_map/phase_3/ppermute | solution.py:40
  77.9 13.2 %collective-permute-start.10 = (bf16[48,4736]{1,0:T(8,128)(2,1)}, bf16[48,4736]{1,0:T(8,128)(2,1)}, u32[]{:S(2)}, u32[]{:S(2)}) collective-permute-start(bf16[48,4736]{1,0:T(8,128)(2,1)} %broadcast_select_fusion), channel_id=1, source_target_pairs={{0,4},{1,5},{2,6},{3,7},{4,0},{5,1},{6,2},{7,3},{8,12},{9,13},{10,... | collective-permute-start | bytes 1363976 | tf_op jit(solution)/shard_map/phase_3/ppermute | solution.py:40
  78.7 12.9 %collective-permute-start.9 = (bf16[48,4736]{1,0:T(8,128)(2,1)}, bf16[48,4736]{1,0:T(8,128)(2,1)}, u32[]{:S(2)}, u32[]{:S(2)}) collective-permute-start(bf16[48,4736]{1,0:T(8,128)(2,1)} %broadcast_select_fusion.1), channel_id=1, source_target_pairs={{0,2},{1,3},{2,0},{3,1},{4,6},{5,7},{6,4},{7,5},{8,10},{9,11},{10,... | collective-permute-start | bytes 1363976 | tf_op jit(solution)/shard_map/phase_3/ppermute | solution.py:40
  80.3 279.3 %reduce-scatter.3.cloned.1.call-start = ((), (), s32[]{:S(2)}) async-start(), calls=%async_computation.3 | async-start | bytes 7077888 | tf_op jit(solution)/shard_map/ffn_backward/reduce_scatter | solution.py:120
  94.3 23.6 %collective-permute-start.14 = (bf16[2,2,48,4736]{3,2,1,0:T(8,128)(2,1)S(1)}, bf16[2,2,48,4736]{3,2,1,0:T(8,128)(2,1)S(1)}, u32[]{:S(2)}, u32[]{:S(2)}) collective-permute-start(bf16[2,2,48,4736]{3,2,1,0:T(8,128)(2,1)S(1)} %pad_maximum_fusion.1), channel_id=1, source_target_pairs={{0,1},{1,0},{2,3},{3,2},{4,5},{5,4},{6,7},{7,6},{8,9},{9,8},{10,11... | collective-permute-start | bytes 5455880 | tf_op jit(solution)/shard_map/phase_4/ppermute | solution.py:40
  94.4 22.6 %collective-permute-start.12 = (bf16[2,48,4736]{2,1,0:T(8,128)(2,1)S(1)}, bf16[2,48,4736]{2,1,0:T(8,128)(2,1)S(1)}, u32[]{:S(2)}, u32[]{:S(2)}) collective-permute-start(bf16[2,48,4736]{2,1,0:T(8,128)(2,1)S(1)} %pad_maximum_fusion.9), channel_id=1, source_target_pairs={{0,4},{1,5},{2,6},{3,7},{4,0},{5,1},{6,2},{7,3},{8,12},{9,13},{10,... | collective-permute-start | bytes 2727944 | tf_op jit(solution)/shard_map/phase_4/ppermute | solution.py:40
  95.7 22.2 %collective-permute-start.13 = (bf16[2,48,4736]{2,1,0:T(8,128)(2,1)S(1)}, bf16[2,48,4736]{2,1,0:T(8,128)(2,1)S(1)}, u32[]{:S(2)}, u32[]{:S(2)}) collective-permute-start(bf16[2,48,4736]{2,1,0:T(8,128)(2,1)S(1)} %pad_maximum_fusion.10), channel_id=1, source_target_pairs={{0,2},{1,3},{2,0},{3,1},{4,6},{5,7},{6,4},{7,5},{8,10},{9,11},{10,... | collective-permute-start | bytes 2727944 | tf_op jit(solution)/shard_map/phase_4/ppermute | solution.py:40
  118.2 6.3 %collective-permute-start.16 = (bf16[2,2,48,4736]{3,2,1,0:T(8,128)(2,1)S(1)}, bf16[2,2,48,4736]{3,2,1,0:T(8,128)(2,1)S(1)}, u32[]{:S(2)}, u32[]{:S(2)}) collective-permute-start(bf16[2,2,48,4736]{3,2,1,0:T(8,128)(2,1)S(1)} %pad_maximum_fusion.3), channel_id=1, source_target_pairs={{0,1},{1,0},{2,3},{3,2},{4,5},{5,4},{6,7},{7,6},{8,9},{9,8},{10,11... | collective-permute-start | bytes 5455880 | tf_op jit(solution)/shard_map/phase_5/ppermute | solution.py:40
  157.3 11.2 %collective-permute-start.17 = (bf16[128,1536]{1,0:T(8,128)(2,1)S(1)}, bf16[128,1536]{1,0:T(8,128)(2,1)S(1)}, u32[]{:S(2)}, u32[]{:S(2)}) collective-permute-start(bf16[128,1536]{1,0:T(8,128)(2,1)S(1)} %get-tuple-element.351), channel_id=1, source_target_pairs={{0,2},{1,3},{2,0},{3,1},{4,6},{5,7},{6,4},{7,5},{8,10},{9,11},{10,... | collective-permute-start | bytes 1179656 | tf_op jit(solution)/shard_map/ffn_forward/ppermute | solution.py:40
  158.8 10.9 %collective-permute-start.18 = (bf16[128,1536]{1,0:T(8,128)(2,1)S(1)}, bf16[128,1536]{1,0:T(8,128)(2,1)S(1)}, u32[]{:S(2)}, u32[]{:S(2)}) collective-permute-start(bf16[128,1536]{1,0:T(8,128)(2,1)S(1)} %get-tuple-element.350), channel_id=1, source_target_pairs={{0,4},{1,5},{2,6},{3,7},{4,0},{5,1},{6,2},{7,3},{8,12},{9,13},{10,... | collective-permute-start | bytes 1179656 | tf_op jit(solution)/shard_map/ffn_forward/ppermute | solution.py:40
  171.6 18.8 %collective-permute-start.19 = (bf16[256,1536]{1,0:T(8,128)(2,1)}, bf16[256,1536]{1,0:T(8,128)(2,1)}, u32[]{:S(2)}, u32[]{:S(2)}) collective-permute-start(bf16[256,1536]{1,0:T(8,128)(2,1)} %pad_maximum_fusion.11.refs_0_), channel_id=1, source_target_pairs={{0,4},{1,5},{2,6},{3,7},{4,0},{5,1},{6,2},{7,3},{8,12},{9,13},{10,... | collective-permute-start | bytes 2359304 | tf_op jit(solution)/shard_map/ffn_forward/ppermute | solution.py:40
  172.6 18.4 %collective-permute-start.20 = (bf16[256,1536]{1,0:T(8,128)(2,1)}, bf16[256,1536]{1,0:T(8,128)(2,1)}, u32[]{:S(2)}, u32[]{:S(2)}) collective-permute-start(bf16[256,1536]{1,0:T(8,128)(2,1)} %pad_maximum_fusion.12.refs_1_), channel_id=1, source_target_pairs={{0,2},{1,3},{2,0},{3,1},{4,6},{5,7},{6,4},{7,5},{8,10},{9,11},{10,... | collective-permute-start | bytes 2359304 | tf_op jit(solution)/shard_map/ffn_forward/ppermute | solution.py:40
  195.3 17.2 %collective-permute-start.25 = (bf16[256,1536]{1,0:T(8,128)(2,1)S(1)}, bf16[256,1536]{1,0:T(8,128)(2,1)S(1)}, u32[]{:S(2)}, u32[]{:S(2)}) collective-permute-start(bf16[256,1536]{1,0:T(8,128)(2,1)S(1)} %convolution_convert_fusion.2), channel_id=1, source_target_pairs={{0,2},{1,3},{2,0},{3,1},{4,6},{5,7},{6,4},{7,5},{8,10},{9,11},{10,... | collective-permute-start | bytes 2359304 | tf_op jit(solution)/shard_map/ffn_forward/ppermute | solution.py:40
  200.3 17.1 %collective-permute-start.24 = (bf16[256,1536]{1,0:T(8,128)(2,1)S(1)}, bf16[256,1536]{1,0:T(8,128)(2,1)S(1)}, u32[]{:S(2)}, u32[]{:S(2)}) collective-permute-start(bf16[256,1536]{1,0:T(8,128)(2,1)S(1)} %convolution_convert_fusion.3), channel_id=1, source_target_pairs={{0,4},{1,5},{2,6},{3,7},{4,0},{5,1},{6,2},{7,3},{8,12},{9,13},{10,... | collective-permute-start | bytes 2359304 | tf_op jit(solution)/shard_map/ffn_forward/ppermute | solution.py:40
  218.0 7.8 %collective-permute-start.26 = (bf16[128,1536]{1,0:T(8,128)(2,1)S(1)}, bf16[128,1536]{1,0:T(8,128)(2,1)S(1)}, u32[]{:S(2)}, u32[]{:S(2)}) collective-permute-start(bf16[128,1536]{1,0:T(8,128)(2,1)S(1)} %slice.456), channel_id=1, source_target_pairs={{0,2},{1,3},{2,0},{3,1},{4,6},{5,7},{6,4},{7,5},{8,10},{9,11},{10,... | collective-permute-start | bytes 1179656 | tf_op jit(solution)/shard_map/ffn_forward/ppermute | solution.py:40
  219.3 7.8 %collective-permute-start.27 = (bf16[128,1536]{1,0:T(8,128)(2,1)S(1)}, bf16[128,1536]{1,0:T(8,128)(2,1)S(1)}, u32[]{:S(2)}, u32[]{:S(2)}) collective-permute-start(bf16[128,1536]{1,0:T(8,128)(2,1)S(1)} %slice.455), channel_id=1, source_target_pairs={{0,4},{1,5},{2,6},{3,7},{4,0},{5,1},{6,2},{7,3},{8,12},{9,13},{10,... | collective-permute-start | bytes 1179656 | tf_op jit(solution)/shard_map/ffn_forward/ppermute | solution.py:40
  228.6 9.1 %collective-permute-start.28 = (bf16[128,1536]{1,0:T(8,128)(2,1)S(1)}, bf16[128,1536]{1,0:T(8,128)(2,1)S(1)}, u32[]{:S(2)}, u32[]{:S(2)}) collective-permute-start(bf16[128,1536]{1,0:T(8,128)(2,1)S(1)} %get-tuple-element.345), channel_id=1, source_target_pairs={{0,2},{1,3},{2,0},{3,1},{4,6},{5,7},{6,4},{7,5},{8,10},{9,11},{10,... | collective-permute-start | bytes 1179656 | tf_op jit(solution)/shard_map/ffn_backward/ppermute | solution.py:40
  229.5 10.8 %collective-permute-start.29 = (bf16[128,1536]{1,0:T(8,128)(2,1)S(1)}, bf16[128,1536]{1,0:T(8,128)(2,1)S(1)}, u32[]{:S(2)}, u32[]{:S(2)}) collective-permute-start(bf16[128,1536]{1,0:T(8,128)(2,1)S(1)} %get-tuple-element.344), channel_id=1, source_target_pairs={{0,4},{1,5},{2,6},{3,7},{4,0},{5,1},{6,2},{7,3},{8,12},{9,13},{10,... | collective-permute-start | bytes 1179656 | tf_op jit(solution)/shard_map/ffn_backward/ppermute | solution.py:40
  240.5 19.5 %collective-permute-start.30 = (bf16[256,1536]{1,0:T(8,128)(2,1)S(1)}, bf16[256,1536]{1,0:T(8,128)(2,1)S(1)}, u32[]{:S(2)}, u32[]{:S(2)}) collective-permute-start(bf16[256,1536]{1,0:T(8,128)(2,1)S(1)} %pad_maximum_fusion.13.refs_0_), channel_id=1, source_target_pairs={{0,4},{1,5},{2,6},{3,7},{4,0},{5,1},{6,2},{7,3},{8,12},{9,13},{10,... | collective-permute-start | bytes 2359304 | tf_op jit(solution)/shard_map/ffn_backward/ppermute | solution.py:40
  241.5 18.5 %collective-permute-start.31 = (bf16[256,1536]{1,0:T(8,128)(2,1)S(1)}, bf16[256,1536]{1,0:T(8,128)(2,1)S(1)}, u32[]{:S(2)}, u32[]{:S(2)}) collective-permute-start(bf16[256,1536]{1,0:T(8,128)(2,1)S(1)} %pad_maximum_fusion.14.refs_1_), channel_id=1, source_target_pairs={{0,2},{1,3},{2,0},{3,1},{4,6},{5,7},{6,4},{7,5},{8,10},{9,11},{10,... | collective-permute-start | bytes 2359304 | tf_op jit(solution)/shard_map/ffn_backward/ppermute | solution.py:40
  266.0 16.6 %collective-permute-start.33 = (bf16[256,1536]{1,0:T(8,128)(2,1)}, bf16[256,1536]{1,0:T(8,128)(2,1)}, u32[]{:S(2)}, u32[]{:S(2)}) collective-permute-start(bf16[256,1536]{1,0:T(8,128)(2,1)} %fusion.19), channel_id=1, source_target_pairs={{0,2},{1,3},{2,0},{3,1},{4,6},{5,7},{6,4},{7,5},{8,10},{9,11},{10,... | collective-permute-start | bytes 2359304 | tf_op jit(solution)/shard_map/ffn_backward/ppermute | solution.py:40
  269.3 13.3 %collective-permute-start.32 = (bf16[256,1536]{1,0:T(8,128)(2,1)}, bf16[256,1536]{1,0:T(8,128)(2,1)}, u32[]{:S(2)}, u32[]{:S(2)}) collective-permute-start(bf16[256,1536]{1,0:T(8,128)(2,1)} %fusion.22), channel_id=1, source_target_pairs={{0,4},{1,5},{2,6},{3,7},{4,0},{5,1},{6,2},{7,3},{8,12},{9,13},{10,... | collective-permute-start | bytes 2359304 | tf_op jit(solution)/shard_map/ffn_backward/ppermute | solution.py:40
  270.4 12.2 %collective-permute-start.34 = (f32[2,128]{1,0:T(2,128)}, f32[2,128]{1,0:T(2,128)}, u32[]{:S(2)}, u32[]{:S(2)}) collective-permute-start(f32[2,128]{1,0:T(2,128)} %broadcast_in_dim.50), channel_id=1, source_target_pairs={{0,1},{1,0},{2,3},{3,2},{4,5},{5,4},{6,7},{7,6},{8,9},{9,8},{10,11... | collective-permute-start | bytes 3080 | tf_op jit(solution)/shard_map/ffn_backward/ppermute | solution.py:40
  282.7 142.6 %reduce-scatter.5.cloned.1.call-start = ((), (), s32[]{:S(2)}) async-start(), calls=%async_computation.4 | async-start | bytes 3538944 | tf_op jit(solution)/shard_map/q_k_v_weight_gradients/reduce_scatter | solution.py:120
  286.5 12.9 %collective-permute-start.35 = (bf16[128,1536]{1,0:T(8,128)(2,1)S(1)}, bf16[128,1536]{1,0:T(8,128)(2,1)}, u32[]{:S(2)}, u32[]{:S(2)}) collective-permute-start(bf16[128,1536]{1,0:T(8,128)(2,1)S(1)} %slice.454), channel_id=1, source_target_pairs={{0,2},{1,3},{2,0},{3,1},{4,6},{5,7},{6,4},{7,5},{8,10},{9,11},{10,... | collective-permute-start | bytes 1179656 | tf_op jit(solution)/shard_map/ffn_backward/ppermute | solution.py:40
  288.0 11.5 %collective-permute-start.36 = (bf16[128,1536]{1,0:T(8,128)(2,1)S(1)}, bf16[128,1536]{1,0:T(8,128)(2,1)}, u32[]{:S(2)}, u32[]{:S(2)}) collective-permute-start(bf16[128,1536]{1,0:T(8,128)(2,1)S(1)} %slice.453), channel_id=1, source_target_pairs={{0,4},{1,5},{2,6},{3,7},{4,0},{5,1},{6,2},{7,3},{8,12},{9,13},{10,... | collective-permute-start | bytes 1179656 | tf_op jit(solution)/shard_map/ffn_backward/ppermute | solution.py:40
  289.8 9.6 %collective-permute-start.37 = (f32[2,128]{1,0:T(2,128)S(1)}, f32[2,128]{1,0:T(2,128)S(1)}, u32[]{:S(2)}, u32[]{:S(2)}) collective-permute-start(f32[2,128]{1,0:T(2,128)S(1)} %add.526), channel_id=1, source_target_pairs={{0,8},{1,9},{2,10},{3,11},{4,12},{5,13},{6,14},{7,15},{8,0},{9,1},... | collective-permute-start | bytes 3080 | tf_op jit(solution)/shard_map/ffn_backward/ppermute | solution.py:40
  312.2 5.4 %collective-permute-start.38 = (bf16[768,1536]{1,0:T(8,128)(2,1)}, bf16[768,1536]{1,0:T(8,128)(2,1)S(1)}, u32[]{:S(2)}, u32[]{:S(2)}) collective-permute-start(bf16[768,1536]{1,0:T(8,128)(2,1)} %convolution_convert_fusion.1), channel_id=1, source_target_pairs={{0,1},{1,0},{2,3},{3,2},{4,5},{5,4},{6,7},{7,6},{8,9},{9,8},{10,11... | collective-permute-start | bytes 7077896 | tf_op jit(solution)/shard_map/attention_backward/ppermute | solution.py:40
  312.9 4.7 collective-permute-start.39
  318.6 21.5 %collective-permute-start.40 = (bf16[192,1536]{1,0:T(8,128)(2,1)S(1)}, bf16[192,1536]{1,0:T(8,128)(2,1)S(1)}, u32[]{:S(2)}, u32[]{:S(2)}) collective-permute-start(bf16[192,1536]{1,0:T(8,128)(2,1)S(1)} %get-tuple-element.256), channel_id=1, source_target_pairs={{0,4},{1,5},{2,6},{3,7},{4,0},{5,1},{6,2},{7,3},{8,12},{9,13},{10,... | collective-permute-start | bytes 1769480 | tf_op jit(solution)/shard_map/attention_backward/ppermute | solution.py:40
  319.7 20.4 %collective-permute-start.41 = (bf16[192,1536]{1,0:T(8,128)(2,1)S(1)}, bf16[192,1536]{1,0:T(8,128)(2,1)S(1)}, u32[]{:S(2)}, u32[]{:S(2)}) collective-permute-start(bf16[192,1536]{1,0:T(8,128)(2,1)S(1)} %get-tuple-element.257), channel_id=1, source_target_pairs={{0,2},{1,3},{2,0},{3,1},{4,6},{5,7},{6,4},{7,5},{8,10},{9,11},{10,... | collective-permute-start | bytes 1769480 | tf_op jit(solution)/shard_map/attention_backward/ppermute | solution.py:40
  320.3 19.7 %collective-permute-start.42 = (f32[2,128]{1,0:T(2,128)S(1)}, f32[2,128]{1,0:T(2,128)S(1)}, u32[]{:S(2)}, u32[]{:S(2)}) collective-permute-start(f32[2,128]{1,0:T(2,128)S(1)} %add.532), channel_id=1, source_target_pairs={{0,2},{1,3},{2,0},{3,1},{4,6},{5,7},{6,4},{7,5},{8,10},{9,11},{10,... | collective-permute-start | bytes 3080 | tf_op jit(solution)/shard_map/attention_backward/ppermute | solution.py:40
  343.7 15.8 %collective-permute-start.43 = (bf16[768,3072]{1,0:T(8,128)(2,1)}, bf16[768,3072]{1,0:T(8,128)(2,1)}, u32[]{:S(2)}, u32[]{:S(2)}) collective-permute-start(bf16[768,3072]{1,0:T(8,128)(2,1)} %convolution_convert_fusion), channel_id=1, source_target_pairs={{0,1},{1,0},{2,3},{3,2},{4,5},{5,4},{6,7},{7,6},{8,9},{9,8},{10,11... | collective-permute-start | bytes 14155784 | tf_op jit(solution)/shard_map/q_k_v_weight_gradients/ppermute | solution.py:40
  348.3 9.9 %collective-permute-start.45 = (bf16[96,1536]{1,0:T(8,128)(2,1)S(1)}, bf16[96,1536]{1,0:T(8,128)(2,1)S(1)}, u32[]{:S(2)}, u32[]{:S(2)}) collective-permute-start(bf16[96,1536]{1,0:T(8,128)(2,1)S(1)} %get-tuple-element.271), channel_id=1, source_target_pairs={{0,2},{1,3},{2,0},{3,1},{4,6},{5,7},{6,4},{7,5},{8,10},{9,11},{10,... | collective-permute-start | bytes 884744 | tf_op jit(solution)/shard_map/attention_backward/ppermute | solution.py:40
  348.9 10.0 %collective-permute-start.46 = (bf16[96,1536]{1,0:T(8,128)(2,1)S(1)}, bf16[96,1536]{1,0:T(8,128)(2,1)S(1)}, u32[]{:S(2)}, u32[]{:S(2)}) collective-permute-start(bf16[96,1536]{1,0:T(8,128)(2,1)S(1)} %get-tuple-element.272), channel_id=1, source_target_pairs={{0,4},{1,5},{2,6},{3,7},{4,0},{5,1},{6,2},{7,3},{8,12},{9,13},{10,... | collective-permute-start | bytes 884744 | tf_op jit(solution)/shard_map/attention_backward/ppermute | solution.py:40
  349.8 8.4 %collective-permute-start.44 = (f32[2,128]{1,0:T(2,128)S(1)}, f32[2,128]{1,0:T(2,128)S(1)}, u32[]{:S(2)}, u32[]{:S(2)}) collective-permute-start(f32[2,128]{1,0:T(2,128)S(1)} %add.533), channel_id=1, source_target_pairs={{0,4},{1,5},{2,6},{3,7},{4,0},{5,1},{6,2},{7,3},{8,12},{9,13},{10,... | collective-permute-start | bytes 3080 | tf_op jit(solution)/shard_map/q_k_v_weight_gradients/ppermute | solution.py:40
  364.5 27.6 %collective-permute-start.47 = (bf16[192,3072]{1,0:T(8,128)(2,1)}, bf16[192,3072]{1,0:T(8,128)(2,1)}, u32[]{:S(2)}, u32[]{:S(2)}) collective-permute-start(bf16[192,3072]{1,0:T(8,128)(2,1)} %get-tuple-element.278), channel_id=1, source_target_pairs={{0,4},{1,5},{2,6},{3,7},{4,0},{5,1},{6,2},{7,3},{8,12},{9,13},{10,... | collective-permute-start | bytes 3538952 | tf_op jit(solution)/shard_map/q_k_v_weight_gradients/ppermute | solution.py:40
  365.2 27.4 %collective-permute-start.48 = (bf16[192,3072]{1,0:T(8,128)(2,1)}, bf16[192,3072]{1,0:T(8,128)(2,1)}, u32[]{:S(2)}, u32[]{:S(2)}) collective-permute-start(bf16[192,3072]{1,0:T(8,128)(2,1)} %get-tuple-element.279), channel_id=1, source_target_pairs={{0,2},{1,3},{2,0},{3,1},{4,6},{5,7},{6,4},{7,5},{8,10},{9,11},{10,... | collective-permute-start | bytes 3538952 | tf_op jit(solution)/shard_map/q_k_v_weight_gradients/ppermute | solution.py:40
  396.8 28.5 %collective-permute-start.49 = (bf16[96,3072]{1,0:T(8,128)(2,1)}, bf16[96,3072]{1,0:T(8,128)(2,1)}, u32[]{:S(2)}, u32[]{:S(2)}) collective-permute-start(bf16[96,3072]{1,0:T(8,128)(2,1)} %get-tuple-element.283), channel_id=1, source_target_pairs={{0,2},{1,3},{2,0},{3,1},{4,6},{5,7},{6,4},{7,5},{8,10},{9,11},{10,... | collective-permute-start | bytes 1769480 | tf_op jit(solution)/shard_map/weight_gradients_to_owners/ppermute | solution.py:40
  398.2 27.0 %collective-permute-start.50 = (bf16[96,3072]{1,0:T(8,128)(2,1)}, bf16[96,3072]{1,0:T(8,128)(2,1)}, u32[]{:S(2)}, u32[]{:S(2)}) collective-permute-start(bf16[96,3072]{1,0:T(8,128)(2,1)} %get-tuple-element.284), channel_id=1, source_target_pairs={{0,4},{1,5},{2,6},{3,7},{4,0},{5,1},{6,2},{7,3},{8,12},{9,13},{10,... | collective-permute-start | bytes 1769480 | tf_op jit(solution)/shard_map/weight_gradients_to_owners/ppermute | solution.py:40
  400.5 6.3 %collective-permute-start.52 = (f32[2,1536]{1,0:T(2,128)S(1)}, f32[2,1536]{1,0:T(2,128)}, u32[]{:S(2)}, u32[]{:S(2)}) collective-permute-start(f32[2,1536]{1,0:T(2,128)S(1)} %add.540), channel_id=1, source_target_pairs={{0,8},{1,9},{2,10},{3,11},{4,12},{5,13},{6,14},{7,15},{8,0},{9,1},... | collective-permute-start | bytes 36872 | tf_op jit(solution)/shard_map/weight_gradients_to_owners/ppermute | solution.py:40
  409.8 8.7 %collective-permute-start.54 = (bf16[48,1536]{1,0:T(8,128)(2,1)S(1)}, bf16[48,1536]{1,0:T(8,128)(2,1)S(1)}, u32[]{:S(2)}, u32[]{:S(2)}) collective-permute-start(bf16[48,1536]{1,0:T(8,128)(2,1)S(1)} %get-tuple-element.329), channel_id=1, source_target_pairs={{0,24},{1,25},{2,26},{3,27},{4,28},{5,29},{6,30},{7,31},{8,16},{9,... | collective-permute-start | bytes 442376 | tf_op jit(solution)/shard_map/q_k_v_weight_gradients/ppermute | solution.py:40
  411.4 13.8 %collective-permute-start.55 = (bf16[48,1536]{1,0:T(8,128)(2,1)S(1)}, bf16[48,1536]{1,0:T(8,128)(2,1)S(1)}, u32[]{:S(2)}, u32[]{:S(2)}) collective-permute-start(bf16[48,1536]{1,0:T(8,128)(2,1)S(1)} %get-tuple-element.330), channel_id=1, source_target_pairs={{0,16},{1,17},{2,18},{3,19},{4,20},{5,21},{6,22},{7,23},{8,24},{9,... | collective-permute-start | bytes 442376 | tf_op jit(solution)/shard_map/q_k_v_weight_gradients/ppermute | solution.py:40
  412.3 12.9 %collective-permute-start.56 = (bf16[48,1536]{1,0:T(8,128)(2,1)S(1)}, bf16[48,1536]{1,0:T(8,128)(2,1)S(1)}, u32[]{:S(2)}, u32[]{:S(2)}) collective-permute-start(bf16[48,1536]{1,0:T(8,128)(2,1)S(1)} %get-tuple-element.328), channel_id=1, source_target_pairs={{0,8},{1,9},{2,10},{3,11},{4,12},{5,13},{6,14},{7,15},{8,0},{9,1},... | collective-permute-start | bytes 442376 | tf_op jit(solution)/shard_map/q_k_v_weight_gradients/ppermute | solution.py:40
  425.3 11.9 %collective-permute-start.61 = (bf16[48,2048]{1,0:T(8,128)(2,1)S(1)}, bf16[48,2048]{1,0:T(8,128)(2,1)S(1)}, u32[]{:S(2)}, u32[]{:S(2)}) collective-permute-start(bf16[48,2048]{1,0:T(8,128)(2,1)S(1)} %get-tuple-element.343), channel_id=1, source_target_pairs={{0,2},{1,3},{2,0},{3,1},{4,6},{5,7},{6,4},{7,5},{8,10},{9,11},{10,... | collective-permute-start | bytes 589832 | tf_op jit(solution)/shard_map/weight_gradients_to_owners/ppermute | solution.py:40
  426.0 13.8 %collective-permute-start.62 = (bf16[48,2048]{1,0:T(8,128)(2,1)S(1)}, bf16[48,2048]{1,0:T(8,128)(2,1)S(1)}, u32[]{:S(2)}, u32[]{:S(2)}) collective-permute-start(bf16[48,2048]{1,0:T(8,128)(2,1)S(1)} %get-tuple-element.342), channel_id=1, source_target_pairs={{0,4},{1,5},{2,6},{3,7},{4,0},{5,1},{6,2},{7,3},{8,12},{9,13},{10,... | collective-permute-start | bytes 589832 | tf_op jit(solution)/shard_map/weight_gradients_to_owners/ppermute | solution.py:40
  427.0 12.9 %collective-permute-start.63 = (bf16[48,2048]{1,0:T(8,128)(2,1)S(1)}, bf16[48,2048]{1,0:T(8,128)(2,1)S(1)}, u32[]{:S(2)}, u32[]{:S(2)}) collective-permute-start(bf16[48,2048]{1,0:T(8,128)(2,1)S(1)} %get-tuple-element.341), channel_id=1, source_target_pairs={{0,6},{1,7},{2,4},{3,5},{4,2},{5,3},{6,0},{7,1},{8,14},{9,15},{10,... | collective-permute-start | bytes 589832 | tf_op jit(solution)/shard_map/weight_gradients_to_owners/ppermute | solution.py:40
  428.9 8.3 %collective-permute-start.60 = (f32[2,1536]{1,0:T(2,128)S(1)}, f32[2,1536]{1,0:T(2,128)S(1)}, u32[]{:S(2)}, u32[]{:S(2)}) collective-permute-start(f32[2,1536]{1,0:T(2,128)S(1)} %add.542), channel_id=1, source_target_pairs={{0,2},{1,3},{2,0},{3,1},{4,6},{5,7},{6,4},{7,5},{8,10},{9,11},{10,... | collective-permute-start | bytes 36872 | tf_op jit(solution)/shard_map/weight_gradients_to_owners/ppermute | solution.py:40
  433.6 11.8 %collective-permute-start.57 = (bf16[48,3072]{1,0:T(8,128)(2,1)S(1)}, bf16[48,3072]{1,0:T(8,128)(2,1)S(1)}, u32[]{:S(2)}, u32[]{:S(2)}) collective-permute-start(bf16[48,3072]{1,0:T(8,128)(2,1)S(1)} %get-tuple-element.321), channel_id=1, source_target_pairs={{0,24},{1,25},{2,26},{3,27},{4,28},{5,29},{6,30},{7,31},{8,16},{9,... | collective-permute-start | bytes 884744 | tf_op jit(solution)/shard_map/weight_gradients_to_owners/ppermute | solution.py:40
  437.2 20.5 %collective-permute-start.58 = (bf16[48,3072]{1,0:T(8,128)(2,1)S(1)}, bf16[48,3072]{1,0:T(8,128)(2,1)S(1)}, u32[]{:S(2)}, u32[]{:S(2)}) collective-permute-start(bf16[48,3072]{1,0:T(8,128)(2,1)S(1)} %get-tuple-element.322), channel_id=1, source_target_pairs={{0,16},{1,17},{2,18},{3,19},{4,20},{5,21},{6,22},{7,23},{8,24},{9,... | collective-permute-start | bytes 884744 | tf_op jit(solution)/shard_map/weight_gradients_to_owners/ppermute | solution.py:40
  437.2 20.5 %collective-permute-start.59 = (bf16[48,3072]{1,0:T(8,128)(2,1)S(1)}, bf16[48,3072]{1,0:T(8,128)(2,1)S(1)}, u32[]{:S(2)}, u32[]{:S(2)}) collective-permute-start(bf16[48,3072]{1,0:T(8,128)(2,1)S(1)} %get-tuple-element.323), channel_id=1, source_target_pairs={{0,8},{1,9},{2,10},{3,11},{4,12},{5,13},{6,14},{7,15},{8,0},{9,1},... | collective-permute-start | bytes 884744 | tf_op jit(solution)/shard_map/weight_gradients_to_owners/ppermute | solution.py:40
  (109 other events, 713.3 us)
Sparse Core Ops, SparseCore 0:
  80.4 88.5 all-gather.1
  282.8 68.9 reduce-scatter.2
  359.7 39.6 reduce-scatter.4

commit v9 on v8

--- a/solution.py
+++ b/solution.py
@@ -330,103 +330,61 @@
     return gathered, ffn
 
 
-def block_sums(sets, tables, rows, dtype, limit):
-    columns = sets[0][0].shape[1]
-    count = tables[0][0].shape[0]
-    if rows % 16:
-        results = []
-        for arrays, table in zip(sets, tables):
-            blocks = [a.reshape(-1, rows, columns)[t] for a, t in zip(arrays, table)]
-            total = sum(block.astype(F32) for block in blocks)
-            results.append(total.astype(dtype).reshape(count * rows, columns))
-        return results
-    sizes = [len(arrays) for arrays in sets]
-    inputs = [array for arrays in sets for array in arrays]
-    table = jnp.stack([t for group in tables for t in group]).astype(jnp.int32)
-
-    def kernel(table, *refs):
-        at = 0
-        for size, out in zip(sizes, refs[len(inputs) :]):
-            total = refs[at][...].astype(F32)
-            for ref in refs[at + 1 : at + size]:
-                total += ref[...].astype(F32)
-            out[...] = total.astype(dtype)
-            at += size
-
-    def block(k):
-        return pl.BlockSpec((rows, columns), lambda i, table: (table[k, i], 0))
-
-    return pl.pallas_call(
-        kernel,
-        grid_spec=pltpu.PrefetchScalarGridSpec(
-            num_scalar_prefetch=1,
-            grid=(count,),
-            in_specs=[block(k) for k in range(len(inputs))],
-            out_specs=[pl.BlockSpec((rows, columns), lambda i, table: (i, 0))] * len(sets),
-        ),
-        out_shape=[jax.ShapeDtypeStruct((count * rows, columns), dtype)] * len(sets),
-        compiler_params=pltpu.CompilerParams(vmem_limit_bytes=limit),
-        cost_estimate=NO_COST,
-        name="block_sums",
-    )(table, *inputs)
-
-
 class PlaneSum:
-    def __init__(self, parts, rows, place_bits):
-        self.parts, self.rows, self.place_bits = parts, rows, place_bits
-        self.tall = parts[0].shape[0] // 8
-
-    def block(self, x, y, half):
-        return jnp.atleast_1d(4 * x + 2 * y + half)
-
-    def sums(self, a, b, more_a, more_b, at_a, at_b, dtype):
-        a_arrays, b_arrays = [*self.parts, *more_a], [*self.parts, *more_b]
-        a_tables = [a, a] + [jnp.atleast_1d(i) for i in at_a]
-        b_tables = [b, b] + [jnp.atleast_1d(i) for i in at_b]
-        small = not more_a and self.parts[0].shape[1] <= 12 * LANES
-        limit = FFN_VMEM if small else 2 * FFN_VMEM
-        return block_sums([a_arrays, b_arrays], [a_tables, b_tables], self.tall, dtype, limit)
-
-    def step_1(self):
-        z, y, x, c = self.place_bits
-        i = jnp.arange(2)
-        a, b = self.sums(self.block(i, 1 - y, 0), self.block(1 - x, i, 1), [], [], [], [], BF)
-        return (swap(a, 4), swap(b, 2))
+    def __init__(self, left, grads):
+        self.left, self.grads = left, grads
+        self.own = left.shape[1] // 2
+        self.first = self.own // 2
+        self.tall = self.first // 4
+
+    def step_0(self):
+        return swap(t_mm(self.left[:, self.own :], self.grads).astype(BF), 1)
+
+    def step_1(self, came):
+        first, both = self.first, 2 * self.tall
+        sent = t_mm(self.left[:, :first], self.grads) + came[:first].astype(F32)
+        sent = sent.astype(BF)
+        self.rest = t_mm(self.left[:, first : self.own], self.grads) + came[first:].astype(F32)
+        return (swap(sent[:both], 4), swap(sent[both:], 2))
 
     def step_2(self, came):
-        z, y, x, c = self.place_bits
-        self.came = came
-        a, b = self.block(1 - x, y, 0), self.block(x, 1 - y, 1)
-        a, b = self.sums(a, b, [came[0]], [came[1]], [1 - x], [1 - y], BF)
-        return (swap(a, 2), swap(b, 4))
-
-    def step_3(self, came):
-        z, y, x, c = self.place_bits
-        a, b = self.block(x, y, 0), self.block(x, y, 1)
-        more_a, more_b = [self.came[0], came[0]], [self.came[1], came[1]]
-        a, b = self.sums(a, b, more_a, more_b, [x, 0], [y, 0], F32)
-        shape = (self.tall // self.rows, self.rows, -1)
-        return jnp.concatenate([a.reshape(shape), b.reshape(shape)])
-
-
-def reordered(count, rows, order):
+        self.came, tall = came, self.tall
+        a = self.rest[:tall] + came[0][tall:].astype(F32)
+        b = self.rest[tall : 2 * tall] + came[1][tall:].astype(F32)
+        return (swap(a.astype(BF), 2), swap(b.astype(BF), 4))
+
+    def step_3(self, came, rows):
+        tall = self.tall
+        sums = []
+        for i in (0, 1):
+            own = self.rest[(2 + i) * tall : (3 + i) * tall]
+            own = own + self.came[i][:tall].astype(F32) + came[i].astype(F32)
+            sums.append(own.reshape(tall // rows, rows, -1))
+        return jnp.concatenate(sums)
+
+
+def selection(source):
+    return (jnp.arange(source.shape[0])[:, None] == source[None, :]).astype(BF)
+
+
+def column_order(count, rows):
     place_of, row = jnp.arange(count) // rows, jnp.arange(count) % rows
+    z, core, y, x = place_of // 8, place_of // 4 % 2, place_of // 2 % 2, place_of % 2
+    return selection((8 * z + 4 * y + 2 * x + core) * rows + row)
+
+
+def sending_order(count, rows, place_bits):
+    z, y, x, c = place_bits
+    at = jnp.arange(count)
+    group, within = at // (count // 16) % 8, at % (count // 16)
+    upper = jnp.isin(group, jnp.array([2, 3, 5, 7]))
+    x_differs = jnp.isin(group, jnp.array([1, 2, 3, 4]))
+    y_differs = jnp.isin(group, jnp.array([0, 1, 3, 5]))
+    core = c ^ (at // (count // 2))
     planes = count // rows // 8
-    if order == "cxyz":
-        core, chip = place_of // (4 * planes), place_of % (4 * planes)
-        x, y, z = chip // (2 * planes), chip // planes % 2, chip % planes
-    else:
-        z, core, y, x = place_of // 8, place_of // 4 % 2, place_of // 2 % 2, place_of % 2
-    source = (8 * z + 4 * y + 2 * x + core) * rows + row
-    return (jnp.arange(count)[:, None] == source[None, :]).astype(BF)
-
-
-def core_halves(values, c):
-    width = values.shape[1] // 2
-    return (
-        lax.dynamic_slice_in_dim(values, c * width, width, 1),
-        lax.dynamic_slice_in_dim(values, (1 - c) * width, width, 1),
-    )
+    z_of = upper * (planes // 2) + within // rows
+    chip = 4 * z_of + 2 * (y ^ y_differs.astype(jnp.int32)) + (x ^ x_differs.astype(jnp.int32))
+    return selection((2 * chip + core) * rows + within % rows)
 
 
 def split_gather(rows, beside=(), then=lambda pieces, *values: values):
@@ -951,7 +909,7 @@
     ff = w_gate.shape[1]
     count = tokens.shape[0]
     cosine, sine = rotation_lanes()
-    to_column, by_side = tied(reordered(width, rows, "zcyx"), reordered(width, rows, "cxyz"))
+    to_column, to_senders = tied(column_order(width, rows), sending_order(width, rows, bits))
 
     part = 2 * ff_rows
     units = planes * part
@@ -990,12 +948,8 @@
         y_b, pre_b, hid_b = ffn_forward(far[1], wb, wd)
         y_a, y_b = y_a.astype(BF), y_b.astype(BF)
         y_b, mixed, normed_in = tied(y_b, mixed, normed_in)
-        beside = (
-            *core_halves(mm(mixed, by_side).astype(BF), c),
-            *core_halves(mm(normed_in, by_side).astype(BF), c),
-        )
-        result, *halves = split_reduce(y_near, (y_a, y_b), beside)
-        mixed_mine, mixed_theirs, normed_mine, normed_theirs = halves
+        beside = (mm(mixed, to_senders).astype(BF), mm(normed_in, to_senders).astype(BF))
+        result, mixed_sent, normed_sent = split_reduce(y_near, (y_a, y_b), beside)
         result = hidden_res + result
         out_act = result.astype(BF)
 
@@ -1046,10 +1000,10 @@
         grad_gain_mid, grad_res = norm_back(grad_mid, hidden_res, inv_ffn, gain_mid)
         grad_res = grad_out + grad_res
         res_low = grad_res.astype(BF)
-        wo_came, came = tied(swap(t_mm(mixed_theirs, res_low).astype(BF), 1), swap(sums, high))
+        g_wo = PlaneSum(mixed_sent, res_low)
+        wo_came, came = tied(g_wo.step_0(), swap(sums, high))
         sums = sums + came
-        g_wo = PlaneSum([t_mm(mixed_mine, res_low), wo_came], rows, bits)
-        wo_moving = g_wo.step_1()
+        wo_moving = g_wo.step_1(wo_came)
         grad_mixed = mm_t(res_low, wo).astype(BF)
         grad_raw = attention_backward(grad_mixed, query, key, value, cosine, sine)
         *wo_came, grad_raw, sums, came = tied(*wo_moving, grad_raw, sums, swap(sums, 2))
@@ -1057,17 +1011,15 @@
         wo_moving = g_wo.step_2(wo_came)
 
     with jax.named_scope("q_k_v_weight_gradients"):
-        qkv_came = swap(t_mm(normed_theirs, grad_raw).astype(BF), 1)
-        g_qkv = t_mm(normed_mine, grad_raw)
-        qkv_came, g_qkv, grad_raw, came, g_both, g_down, *wo_came = tied(
-            qkv_came, g_qkv, grad_raw, swap(sums, 4), g_both, g_down, *wo_moving
+        g_qkv = PlaneSum(normed_sent, grad_raw)
+        qkv_came, grad_raw, sums, came, g_both, g_down, *wo_came = tied(
+            g_qkv.step_0(), grad_raw, sums, swap(sums, 4), g_both, g_down, *wo_moving
         )
         g_down = sum_to_owners(g_down)
         sums = sums + came
         loss = sums[0, 0] / (sums[1, 0] * width)
-        g_qkv = PlaneSum([g_qkv, qkv_came], rows, bits)
-        qkv_moving = g_qkv.step_1()
-        g_wo = g_wo.step_3(wo_came)
+        qkv_moving = g_qkv.step_1(qkv_came)
+        g_wo = g_wo.step_3(wo_came, rows)
         wo_moving = direct([g_wo], z) if planes == 4 else []
 
     with jax.named_scope("input_gradient"):
@@ -1086,7 +1038,7 @@
         )
         qkv_came = (qkv_0, qkv_1)
         g_wo = owned([g_wo], wo_came, z) if planes == 4 else z_reduce([g_wo])
-        g_qkv = g_qkv.step_3(qkv_came)
+        g_qkv = g_qkv.step_3(qkv_came, rows)
         if planes == 4:
             moving = direct([g_qkv], z)
         g_both = g_both.reshape(4, rows, 2 * units)

time: 474 us -> 457 us (0.964)
  Pallas kernels: 95.1 us -> 76.2 us
  local copies, waits for them, and re-layouts: 59.4 us -> 47.4 us
  waiting for transfers between devices: 123 us -> 135 us
    pallas_call x6 -> x0, Pallas kernels: 17.7 us -> none  [block_sums(): pl.pallas_call(kernel, grid_spec=pltpu.PrefetchScalarGridSpec(num_scalar_...]
    ppermute x60, waiting for transfers between devices: 119 us -> 130 us  [swap(): return lax.ppermute(value, 'dp', [(i, i ^ mask) for i in range(n)])]
    unnamed x225 -> x141, local copies, waits for them, and re-layouts: 30.3 us -> 20.3 us
    convert_element_type x2 -> x5, other arithmetic: 8.66 us -> 12.9 us  [the longest x2 8.56 us: selection(): return (jnp.arange(source.shape[0])[:, None] == source[None, :]).astype(BF)]
    dot_general x20 -> x22, matrix products: 52.6 us -> 51.8 us  [dot(): return lax.dot_general(a, b, (dims, ((), ())), preferred_element_type=F32)]
  transfers between devices with their start and end apart: 68 -> 68, of which waited for: 30 -> 31; matrix products, arithmetic and copies ran while one was open for 23% -> 24% of each run, Pallas kernels for 20% -> 17%
where the time goes in v9:
time: 457 us; the launch traced here: 451 us
  waiting for transfers between devices  135 us (30%)
  starting transfers between devices  77.3 us (17%)
  Pallas kernels  76.2 us (17%)
  matrix products  51.8 us (11%)
  local copies, waits for them, and re-layouts  47.4 us (10%)
  other arithmetic  45.2 us (10%)
  between operations  18.1 us (4%)
    ppermute x60, waiting for transfers between devices, swap(): return lax.ppermute(value, 'dp', [(i, i ^ mask) for i in range(n)])  130 us
    ppermute x60, starting transfers between devices, swap(): return lax.ppermute(value, 'dp', [(i, i ^ mask) for i in range(n)])  61.9 us
    dot_general x22, matrix products, dot(): return lax.dot_general(a, b, (dims, ((), ())), preferred_element_type=F32)  51.8 us
    unnamed x141, local copies, waits for them, and re-layouts  20.3 us
    dynamic_update_slice x16, local copies, waits for them, and re-layouts, place(): return lax.dynamic_update_slice(out, piece, where)  18.6 us
    pallas_call x2, Pallas kernels, products(): pl.pallas_call(kernel, grid=(columns // tile,), out_shape=jax.ShapeDtypeS...  15.5 us
    ppermute x5, starting transfers between devices, along_z(): lax.ppermute(value, 'dp', [(8 * a + i, 8 * b + i) for a, b in pairs for i...  15.1 us
    pallas_call x1, Pallas kernels, attention_backward(): pl.pallas_call(kernel, grid=(count // SEQ, steps), out_shape=jax.ShapeDty...  14.3 us
  transfers between devices with their start and end apart: 68, of which 31 were waited for; matrix products, arithmetic and copies ran while one was open for 24% of the time, Pallas kernels for 17%

profile of v9, /device:TPU:0, one launch (start us, length us, event | category | flops | bytes accessed | tf_op | source)
XLA Modules:
  0.0 450.5 jit_solution(70299118950827294)
XLA Ops:
  11.7 5.0 %collective-permute-start = (bf16[48,4736]{1,0:T(8,128)(2,1)S(1)}, bf16[48,4736]{1,0:T(8,128)(2,1)S(1)}, u32[]{:S(2)}, u32[]{:S(2)}) collective-permute-start(bf16[48,4736]{1,0:T(8,128)(2,1)S(1)} %packed.1), channel_id=1, source_target_pairs={{0,8},{1,9},{2,10},{3,11},{4,12},{5,13},{6,14},{7,15},{8,16},{9,17... | collective-permute-start | bytes 1363976 | tf_op jit(solution)/shard_map/phase_0/ppermute | solution.py:77
  23.4 4.2 fusion.3
  27.6 4.4 fusion.2
  33.6 6.3 %collective-permute-start.4 = (bf16[48,4736]{1,0:T(8,128)(2,1)S(1)}, bf16[48,4736]{1,0:T(8,128)(2,1)}, u32[]{:S(2)}, u32[]{:S(2)}) collective-permute-start(bf16[48,4736]{1,0:T(8,128)(2,1)S(1)} %packed.1), channel_id=1, source_target_pairs={{0,16},{1,17},{2,18},{3,19},{4,20},{5,21},{6,22},{7,23},{24,8},{25... | collective-permute-start | bytes 1363976 | tf_op jit(solution)/shard_map/phase_1/ppermute | solution.py:77
  44.5 2.5 collective-permute-start.23
  47.0 4.2 collective-permute-done.23.refs_3_
  52.4 2.6 collective-permute-done.3
  62.1 1.8 broadcast_select_fusion.1
  65.3 4.4 collective-permute-done.8
  69.7 6.4 %collective-permute-done.6 = bf16[2,48,4736]{2,1,0:T(8,128)(2,1)S(1)} collective-permute-done((bf16[2,48,4736]{2,1,0:T(8,128)(2,1)S(1)}, bf16[2,48,4736]{2,1,0:T(8,128)(2,1)S(1)}, u32[]{:S(2)}, u32[]{:S(2)}) %collective-permute-start.6) | collective-permute-done | bytes 909344 | tf_op jit(solution)/shard_map/phase_2/ppermute | solution.py:40
  82.6 7.5 %collective-permute-done.10 = bf16[48,4736]{1,0:T(8,128)(2,1)} collective-permute-done((bf16[48,4736]{1,0:T(8,128)(2,1)}, bf16[48,4736]{1,0:T(8,128)(2,1)}, u32[]{:S(2)}, u32[]{:S(2)}) %collective-permute-start.10) | collective-permute-done | bytes 454688 | tf_op jit(solution)/shard_map/phase_3/ppermute | solution.py:40
  96.2 2.2 bitcast_dynamic-update-slice_fusion.11
  98.4 2.2 bitcast_dynamic-update-slice_fusion.10
  102.9 14.0 %collective-permute-done.12 = bf16[2,48,4736]{2,1,0:T(8,128)(2,1)S(1)} collective-permute-done((bf16[2,48,4736]{2,1,0:T(8,128)(2,1)S(1)}, bf16[2,48,4736]{2,1,0:T(8,128)(2,1)S(1)}, u32[]{:S(2)}, u32[]{:S(2)}) %collective-permute-start.12) | collective-permute-done | bytes 909344 | tf_op jit(solution)/shard_map/phase_4/ppermute | solution.py:40
  121.7 2.1 collective-permute-done.16
  129.7 5.6 %fusion.q_raw.k_raw.v_raw = f32[256,3072]{1,0:T(8,128)S(1)} fusion(bf16[256,1536]{1,0:T(8,128)(2,1)S(1)} %fusion.31, bf16[1536,4736]{1,0:T(8,128)(2,1)} %bitcast.197), kind=kOutput, calls=%fused_computation | convolution fusion | flops 2415919104 | bytes 13369344 | tf_op jit(solution)/shard_map/attention_forward/dot_general | solution.py:23
  135.3 12.6 %attention_forward.1 = (bf16[256,1536]{1,0:T(8,128)(2,1)S(1)}, bf16[256,768]{1,0:T(8,128)(2,1)S(1)}, bf16[256,768]{1,0:T(8,128)(2,1)S(1)}, bf16[256,1536]{1,0:T(8,128)(2,1)S(1)}) custom-call(f32[256,3072]{1,0:T(8,128)S(1)} %fusion.q_raw.k_raw.v_raw, f32[256,3072]{1,0:T(8,128)S(1)} %fusion.q_raw.k_raw.v_raw, f32[256,3072]{1,0:T(8,128)S(1)} %fusion.q_raw.k_raw.v_raw, ...), custom_call_target="tpu_custom_call" | custom-call | flops 1 | bytes 1 | tf_op jit(solution)/shard_map/attention_forward/attention_forward/pallas_call | solution.py:537
  150.4 4.1 multiply_reduce_fusion.3
  159.3 8.0 %collective-permute-done.17 = bf16[128,1536]{1,0:T(8,128)(2,1)S(1)} collective-permute-done((bf16[128,1536]{1,0:T(8,128)(2,1)S(1)}, bf16[128,1536]{1,0:T(8,128)(2,1)S(1)}, u32[]{:S(2)}, u32[]{:S(2)}) %collective-permute-start.17) | collective-permute-done | bytes 393248 | tf_op jit(solution)/shard_map/ffn_forward/ppermute | solution.py:40
  168.6 1.7 collective-permute-start.19
  170.9 2.2 w_down_from.1.refs_4_.refs_6_
  173.1 2.5 copy-done
  175.5 8.6 %ffn_forward_beside.1 = (f32[512,1536]{1,0:T(8,128)S(1)}, bf16[512,1536]{1,0:T(8,128)(2,1)S(1)}, bf16[512,1024]{1,0:T(8,128)(2,1)S(1)}, f32[512,1024]{1,0:T(8,128)S(1)}, f32[512,1024]{1,0:T(8,128)S(1)}) custom-call(bf16[256,1536]{1,0:T(8,128)(2,1)S(1)} %pad_maximum_fusion.11.refs_0_, bf16[256,1536]{1,0:T(8,128)(2,1)S(1)} %pad_maximum_fusion.12.refs_1_, ...), custom_call_target="tpu_custom_call" | custom-call | flops 1 | bytes 1 | tf_op jit(solution)/shard_map/ffn_forward/ffn_forward_beside/pallas_call | solution.py:722
  184.2 3.0 collective-permute-done.19.refs_1_
  188.6 2.9 fusion.12
  193.6 2.9 fusion.14
  198.3 2.3 convolution_convert_fusion.4
  200.6 2.3 convolution_convert_fusion.5
  202.9 7.2 %collective-permute-done.25 = bf16[256,1536]{1,0:T(8,128)(2,1)S(1)} collective-permute-done((bf16[256,1536]{1,0:T(8,128)(2,1)S(1)}, bf16[256,1536]{1,0:T(8,128)(2,1)S(1)}, u32[]{:S(2)}, u32[]{:S(2)}) %collective-permute-start.25) | collective-permute-done | bytes 786464 | tf_op jit(solution)/shard_map/ffn_forward/ppermute | solution.py:40
  210.2 4.9 %collective-permute-done.24 = bf16[256,1536]{1,0:T(8,128)(2,1)S(1)} collective-permute-done((bf16[256,1536]{1,0:T(8,128)(2,1)S(1)}, bf16[256,1536]{1,0:T(8,128)(2,1)S(1)}, u32[]{:S(2)}, u32[]{:S(2)}) %collective-permute-start.24) | collective-permute-done | bytes 786464 | tf_op jit(solution)/shard_map/ffn_forward/ppermute | solution.py:40
  217.5 6.0 %collective-permute-done.26 = bf16[128,1536]{1,0:T(8,128)(2,1)S(1)} collective-permute-done((bf16[128,1536]{1,0:T(8,128)(2,1)S(1)}, bf16[128,1536]{1,0:T(8,128)(2,1)S(1)}, u32[]{:S(2)}, u32[]{:S(2)}) %collective-permute-start.26) | collective-permute-done | bytes 393248 | tf_op jit(solution)/shard_map/ffn_forward/ppermute | solution.py:40
  227.7 7.9 %collective-permute-done.28 = bf16[128,1536]{1,0:T(8,128)(2,1)S(1)} collective-permute-done((bf16[128,1536]{1,0:T(8,128)(2,1)S(1)}, bf16[128,1536]{1,0:T(8,128)(2,1)S(1)}, u32[]{:S(2)}, u32[]{:S(2)}) %collective-permute-start.28) | collective-permute-done | bytes 393248 | tf_op jit(solution)/shard_map/ffn_backward/ppermute | solution.py:40
  235.6 2.3 collective-permute-done.29
  240.4 12.4 %ffn_backward_beside.1 = (f32[512,1536]{1,0:T(8,128)S(1)}, bf16[512,1536]{1,0:T(8,128)(2,1)S(1)}, bf16[512,2048]{1,0:T(8,128)(2,1)S(1)}) custom-call(bf16[256,1536]{1,0:T(8,128)(2,1)S(1)} %pad_maximum_fusion.13.refs_0_, bf16[256,1536]{1,0:T(8,128)(2,1)S(1)} %pad_maximum_fusion.14.refs_1_, f32[512,1024]{1,0:T(8,128)S(1)} %get-tuple-element.213.refs_2_, ...), custom_call_target="tpu_custom_call" | custom-call | flops 1 | bytes 1 | tf_op jit(solution)/shard_map/ffn_backward/ffn_backward_beside/pallas_call | solution.py:787
  259.6 2.7 fusion.20
  263.0 2.7 fusion.23
  267.5 9.5 %products.2 = bf16[1536,2048]{1,0:T(8,128)(2,1)S(1)} custom-call(bf16[512,1536]{1,0:T(8,128)(2,1)S(1)} %get-tuple-element.224.refs_0_, bf16[256,1536]{1,0:T(8,128)(2,1)} %collective-permute-done.19.refs_1_, bf16[256,1536]{1,0:T(8,128)(2,1)} %collective-permute-done.20.refs_2_, bf16[512,2048]{1,0:T(8,128)(2,1)S(1)} %get-tuple-element.225.refs_3_, ...), custom_call_target="tpu_custom_call" | custom-call | flops 1 | bytes 1 | tf_op jit(solution)/shard_map/ffn_backward/products/pallas_call | solution.py:872
  277.0 2.7 copy-done.1
  279.8 2.9 convert_add_fusion.2
  286.0 2.5 collective-permute-start.37
  288.5 6.0 %products.3 = bf16[1024,1536]{1,0:T(8,128)(2,1)S(1)} custom-call(bf16[512,1024]{1,0:T(8,128)(2,1)S(1)} %copy-done.9, bf16[256,1024]{1,0:T(8,128)(2,1)S(1)} %multiply_convert_fusion.6.refs_1_, bf16[256,1024]{1,0:T(8,128)(2,1)S(1)} %multiply_convert_fusion.5.refs_2_, bf16[512,1536]{1,0:T(8,128)(2,1)S(1)} %copy-done.7, ...), custom_call_target="tpu_custom_call" | custom-call | flops 1 | bytes 1 | tf_op jit(solution)/shard_map/ffn_backward/products/pallas_call | solution.py:872
  299.6 3.9 fusion.37
  303.6 4.2 multiply_reduce_fusion
  311.2 3.8 collective-permute-done.39
  318.1 3.8 fusion.26.d_ref
  322.0 14.3 %attention_backward.1.grads = bf16[256,3072]{1,0:T(8,128)(2,1)S(1)} custom-call(bf16[256,1536]{1,0:T(8,128)(2,1)S(1)} %fusion.26.d_ref, bf16[256,1536]{1,0:T(8,128)(2,1)S(1)} %copy-done.11, bf16[256,768]{1,0:T(8,128)(2,1)S(1)} %copy-done.16, bf16[256,768]{1,0:T(8,128)(2,1)S(1)} %copy-done.18, f32[128,768]{1,0:T(8,128)S(1)} %copy.107.cosine, ...), custom_call_target="tpu_custom_call" | custom-call | flops 1 | bytes 1 | tf_op jit(solution)/shard_map/attention_backward/attention_backward/pallas_call | solution.py:609
  340.7 1.8 collective-permute-start.46
  342.7 7.2 %collective-permute-done.44 = f32[2,128]{1,0:T(2,128)S(1)} collective-permute-done((f32[2,128]{1,0:T(2,128)S(1)}, f32[2,128]{1,0:T(2,128)S(1)}, u32[]{:S(2)}, u32[]{:S(2)}) %collective-permute-start.44) | collective-permute-done | bytes 1056 | tf_op jit(solution)/shard_map/q_k_v_weight_gradients/ppermute | solution.py:40
  350.0 2.6 add_convert_fusion
  354.2 1.7 collective-permute-start.47
  358.9 9.3 %input_gradient.1 = (bf16[256,1536]{1,0:T(8,128)(2,1)}, f32[1,1536]{1,0:T(1,128)S(1)}) custom-call(bf16[256,3072]{1,0:T(8,128)(2,1)S(1)} %attention_backward.1.grads, bf16[1536,4736]{1,0:T(8,128)(2,1)} %bitcast.200, bf16[256,1536]{1,0:T(8,128)(2,1)S(1)} %copy-done.3, f32[256,1]{1,0:T(8,128)S(1)} %copy.111.inv_scale, f32[1,1536]{1,0:T(1,128)S(1)} %reshape.348.gain, ...), custom_call_target="tpu_custom_call" | custom-call | flops 1 | bytes 1 | tf_op jit(solution)/shard_map/input_gradient/input_gradient/pallas_call | solution.py:832
  368.2 2.6 convert_add_fusion
  370.9 10.9 %collective-permute-done.47 = bf16[192,3072]{1,0:T(8,128)(2,1)} collective-permute-done((bf16[192,3072]{1,0:T(8,128)(2,1)}, bf16[192,3072]{1,0:T(8,128)(2,1)}, u32[]{:S(2)}, u32[]{:S(2)}) %collective-permute-start.47) | collective-permute-done | bytes 1179680 | tf_op jit(solution)/shard_map/q_k_v_weight_gradients/ppermute | solution.py:40
  383.3 2.6 fusion.34
  387.5 2.5 collective-permute-start.52
  394.0 2.9 collective-permute-start.54
  400.4 2.4 collective-permute-done.54
  402.8 6.0 %collective-permute-done.55 = bf16[48,1536]{1,0:T(8,128)(2,1)S(1)} collective-permute-done((bf16[48,1536]{1,0:T(8,128)(2,1)}, bf16[48,1536]{1,0:T(8,128)(2,1)S(1)}, u32[]{:S(2)}, u32[]{:S(2)}) %collective-permute-start.55) | collective-permute-done | bytes 147488 | tf_op jit(solution)/shard_map/q_k_v_weight_gradients/ppermute | solution.py:40
  411.1 2.0 collective-permute-start.63
  413.8 2.4 fusion.33
  416.5 2.4 collective-permute-start.57
  421.6 2.0 collective-permute-start.59
  425.0 2.4 collective-permute-done.64
  428.3 12.6 %collective-permute-done.58 = bf16[48,3072]{1,0:T(8,128)(2,1)S(1)} collective-permute-done((bf16[48,3072]{1,0:T(8,128)(2,1)S(1)}, bf16[48,3072]{1,0:T(8,128)(2,1)S(1)}, u32[]{:S(2)}, u32[]{:S(2)}) %collective-permute-start.58) | collective-permute-done | bytes 294944 | tf_op jit(solution)/shard_map/weight_gradients_to_owners/ppermute | solution.py:40
  (361 shorter events, 127.7 us)
Async XLA Ops:
  7.2 163.7 %all-gather.2.cloned.1.call-start = ((), (), s32[]{:S(2)}) async-start(), calls=%async_computation.2 | async-start | bytes 10616832 | tf_op jit(solution)/shard_map/ffn_weights/all_gather | solution.py:114
  11.7 20.3 %collective-permute-start = (bf16[48,4736]{1,0:T(8,128)(2,1)S(1)}, bf16[48,4736]{1,0:T(8,128)(2,1)S(1)}, u32[]{:S(2)}, u32[]{:S(2)}) collective-permute-start(bf16[48,4736]{1,0:T(8,128)(2,1)S(1)} %packed.1), channel_id=1, source_target_pairs={{0,8},{1,9},{2,10},{3,11},{4,12},{5,13},{6,14},{7,15},{8,16},{9,17... | collective-permute-start | bytes 1363976 | tf_op jit(solution)/shard_map/phase_0/ppermute | solution.py:77
  16.7 15.4 %collective-permute-start.1 = (bf16[48,4736]{1,0:T(8,128)(2,1)S(1)}, bf16[48,4736]{1,0:T(8,128)(2,1)S(1)}, u32[]{:S(2)}, u32[]{:S(2)}) collective-permute-start(bf16[48,4736]{1,0:T(8,128)(2,1)S(1)} %packed.1), channel_id=1, source_target_pairs={{8,0},{9,1},{10,2},{11,3},{12,4},{13,5},{14,6},{15,7},{16,8},{17,9... | collective-permute-start | bytes 1363976 | tf_op jit(solution)/shard_map/phase_0/ppermute | solution.py:77
  20.1 20.4 %collective-permute-start.21 = (bf16[48,2048]{1,0:T(8,128)(2,1)S(1)}, bf16[48,2048]{1,0:T(8,128)(2,1)S(1)}, u32[]{:S(2)}, u32[]{:S(2)}) collective-permute-start(bf16[48,2048]{1,0:T(8,128)(2,1)S(1)} %get-tuple-element.181), channel_id=1, source_target_pairs={{0,2},{1,3},{2,0},{3,1},{4,6},{5,7},{6,4},{7,5},{8,10},{9,11},{10,... | collective-permute-start | bytes 589832 | tf_op jit(solution)/shard_map/phase_0/ppermute | solution.py:40
  21.7 22.8 %collective-permute-start.22 = (bf16[48,2048]{1,0:T(8,128)(2,1)S(1)}, bf16[48,2048]{1,0:T(8,128)(2,1)S(1)}, u32[]{:S(2)}, u32[]{:S(2)}) collective-permute-start(bf16[48,2048]{1,0:T(8,128)(2,1)S(1)} %get-tuple-element.182), channel_id=1, source_target_pairs={{0,4},{1,5},{2,6},{3,7},{4,0},{5,1},{6,2},{7,3},{8,12},{9,13},{10,... | collective-permute-start | bytes 589832 | tf_op jit(solution)/shard_map/phase_0/ppermute | solution.py:40
  33.1 19.3 %collective-permute-start.2 = (bf16[48,4736]{1,0:T(8,128)(2,1)S(1)}, bf16[48,4736]{1,0:T(8,128)(2,1)}, u32[]{:S(2)}, u32[]{:S(2)}) collective-permute-start(bf16[48,4736]{1,0:T(8,128)(2,1)S(1)} %packed.1), channel_id=1, source_target_pairs={{0,2},{1,3},{2,0},{3,1},{4,6},{5,7},{6,4},{7,5},{8,10},{9,11},{10,... | collective-permute-start | bytes 1363976 | tf_op jit(solution)/shard_map/phase_1/ppermute | solution.py:40
  33.6 21.3 %collective-permute-start.4 = (bf16[48,4736]{1,0:T(8,128)(2,1)S(1)}, bf16[48,4736]{1,0:T(8,128)(2,1)}, u32[]{:S(2)}, u32[]{:S(2)}) collective-permute-start(bf16[48,4736]{1,0:T(8,128)(2,1)S(1)} %packed.1), channel_id=1, source_target_pairs={{0,16},{1,17},{2,18},{3,19},{4,20},{5,21},{6,22},{7,23},{24,8},{25... | collective-permute-start | bytes 1363976 | tf_op jit(solution)/shard_map/phase_1/ppermute | solution.py:77
  40.0 15.0 %collective-permute-start.3 = (bf16[48,4736]{1,0:T(8,128)(2,1)}, bf16[48,4736]{1,0:T(8,128)(2,1)}, u32[]{:S(2)}, u32[]{:S(2)}) collective-permute-start(bf16[48,4736]{1,0:T(8,128)(2,1)} %get-tuple-element.146), channel_id=1, source_target_pairs={{0,4},{1,5},{2,6},{3,7},{4,0},{5,1},{6,2},{7,3},{8,12},{9,13},{10,... | collective-permute-start | bytes 1363976 | tf_op jit(solution)/shard_map/phase_1/ppermute | solution.py:40
  40.5 14.5 %collective-permute-start.5 = (bf16[48,4736]{1,0:T(8,128)(2,1)}, bf16[48,4736]{1,0:T(8,128)(2,1)}, u32[]{:S(2)}, u32[]{:S(2)}) collective-permute-start(bf16[48,4736]{1,0:T(8,128)(2,1)} %get-tuple-element.147), channel_id=1, source_target_pairs={{8,0},{9,1},{10,2},{11,3},{12,4},{13,5},{14,6},{15,7},{16,24},{17,... | collective-permute-start | bytes 1363976 | tf_op jit(solution)/shard_map/phase_1/ppermute | solution.py:77
  44.5 6.7 %collective-permute-start.23 = (bf16[48,2048]{1,0:T(8,128)(2,1)S(1)}, bf16[48,2048]{1,0:T(8,128)(2,1)S(1)}, u32[]{:S(2)}, u32[]{:S(2)}) collective-permute-start(bf16[48,2048]{1,0:T(8,128)(2,1)S(1)} %get-tuple-element.183), channel_id=1, source_target_pairs={{0,6},{1,7},{2,4},{3,5},{4,2},{5,3},{6,0},{7,1},{8,14},{9,15},{10,... | collective-permute-start | bytes 589832 | tf_op jit(solution)/shard_map/phase_0/ppermute | solution.py:40
  56.7 19.4 %collective-permute-start.6 = (bf16[2,48,4736]{2,1,0:T(8,128)(2,1)S(1)}, bf16[2,48,4736]{2,1,0:T(8,128)(2,1)S(1)}, u32[]{:S(2)}, u32[]{:S(2)}) collective-permute-start(bf16[2,48,4736]{2,1,0:T(8,128)(2,1)S(1)} %pad_maximum_fusion.7), channel_id=1, source_target_pairs={{0,4},{1,5},{2,6},{3,7},{4,0},{5,1},{6,2},{7,3},{8,12},{9,13},{10,... | collective-permute-start | bytes 2727944 | tf_op jit(solution)/shard_map/phase_2/ppermute | solution.py:40
  57.2 18.9 %collective-permute-start.7 = (bf16[2,48,4736]{2,1,0:T(8,128)(2,1)S(1)}, bf16[2,48,4736]{2,1,0:T(8,128)(2,1)S(1)}, u32[]{:S(2)}, u32[]{:S(2)}) collective-permute-start(bf16[2,48,4736]{2,1,0:T(8,128)(2,1)S(1)} %pad_maximum_fusion.8), channel_id=1, source_target_pairs={{0,2},{1,3},{2,0},{3,1},{4,6},{5,7},{6,4},{7,5},{8,10},{9,11},{10,... | collective-permute-start | bytes 2727944 | tf_op jit(solution)/shard_map/phase_2/ppermute | solution.py:40
  58.7 10.9 %collective-permute-start.8 = (bf16[48,4736]{1,0:T(8,128)(2,1)}, bf16[48,4736]{1,0:T(8,128)(2,1)S(1)}, u32[]{:S(2)}, u32[]{:S(2)}) collective-permute-start(bf16[48,4736]{1,0:T(8,128)(2,1)} %collective-permute-done.4), channel_id=1, source_target_pairs={{8,0},{9,1},{10,2},{11,3},{12,4},{13,5},{14,6},{15,7},{16,24},{17,... | collective-permute-start | bytes 1363976 | tf_op jit(solution)/shard_map/phase_2/ppermute | solution.py:77
  77.0 14.6 %collective-permute-start.11 = (bf16[2,2,48,4736]{3,2,1,0:T(8,128)(2,1)}, bf16[2,2,48,4736]{3,2,1,0:T(8,128)(2,1)}, u32[]{:S(2)}, u32[]{:S(2)}) collective-permute-start(bf16[2,2,48,4736]{3,2,1,0:T(8,128)(2,1)} %pad_maximum_fusion), channel_id=1, source_target_pairs={{0,1},{1,0},{2,3},{3,2},{4,5},{5,4},{6,7},{7,6},{8,9},{9,8},{10,11... | collective-permute-start | bytes 5455880 | tf_op jit(solution)/shard_map/phase_3/ppermute | solution.py:40
  77.0 13.2 %collective-permute-start.10 = (bf16[48,4736]{1,0:T(8,128)(2,1)}, bf16[48,4736]{1,0:T(8,128)(2,1)}, u32[]{:S(2)}, u32[]{:S(2)}) collective-permute-start(bf16[48,4736]{1,0:T(8,128)(2,1)} %broadcast_select_fusion), channel_id=1, source_target_pairs={{0,4},{1,5},{2,6},{3,7},{4,0},{5,1},{6,2},{7,3},{8,12},{9,13},{10,... | collective-permute-start | bytes 1363976 | tf_op jit(solution)/shard_map/phase_3/ppermute | solution.py:40
  78.6 12.9 %collective-permute-start.9 = (bf16[48,4736]{1,0:T(8,128)(2,1)}, bf16[48,4736]{1,0:T(8,128)(2,1)}, u32[]{:S(2)}, u32[]{:S(2)}) collective-permute-start(bf16[48,4736]{1,0:T(8,128)(2,1)} %broadcast_select_fusion.1), channel_id=1, source_target_pairs={{0,2},{1,3},{2,0},{3,1},{4,6},{5,7},{6,4},{7,5},{8,10},{9,11},{10,... | collective-permute-start | bytes 1363976 | tf_op jit(solution)/shard_map/phase_3/ppermute | solution.py:40
  80.1 269.9 %reduce-scatter.3.cloned.1.call-start = ((), (), s32[]{:S(2)}) async-start(), calls=%async_computation.3 | async-start | bytes 7077888 | tf_op jit(solution)/shard_map/ffn_backward/reduce_scatter | solution.py:120
  94.2 22.8 %collective-permute-start.14 = (bf16[2,2,48,4736]{3,2,1,0:T(8,128)(2,1)S(1)}, bf16[2,2,48,4736]{3,2,1,0:T(8,128)(2,1)S(1)}, u32[]{:S(2)}, u32[]{:S(2)}) collective-permute-start(bf16[2,2,48,4736]{3,2,1,0:T(8,128)(2,1)S(1)} %pad_maximum_fusion.1), channel_id=1, source_target_pairs={{0,1},{1,0},{2,3},{3,2},{4,5},{5,4},{6,7},{7,6},{8,9},{9,8},{10,11... | collective-permute-start | bytes 5455880 | tf_op jit(solution)/shard_map/phase_4/ppermute | solution.py:40
  94.3 22.6 %collective-permute-start.12 = (bf16[2,48,4736]{2,1,0:T(8,128)(2,1)S(1)}, bf16[2,48,4736]{2,1,0:T(8,128)(2,1)S(1)}, u32[]{:S(2)}, u32[]{:S(2)}) collective-permute-start(bf16[2,48,4736]{2,1,0:T(8,128)(2,1)S(1)} %pad_maximum_fusion.9), channel_id=1, source_target_pairs={{0,4},{1,5},{2,6},{3,7},{4,0},{5,1},{6,2},{7,3},{8,12},{9,13},{10,... | collective-permute-start | bytes 2727944 | tf_op jit(solution)/shard_map/phase_4/ppermute | solution.py:40
  94.7 22.2 %collective-permute-start.13 = (bf16[2,48,4736]{2,1,0:T(8,128)(2,1)S(1)}, bf16[2,48,4736]{2,1,0:T(8,128)(2,1)S(1)}, u32[]{:S(2)}, u32[]{:S(2)}) collective-permute-start(bf16[2,48,4736]{2,1,0:T(8,128)(2,1)S(1)} %pad_maximum_fusion.10), channel_id=1, source_target_pairs={{0,2},{1,3},{2,0},{3,1},{4,6},{5,7},{6,4},{7,5},{8,10},{9,11},{10,... | collective-permute-start | bytes 2727944 | tf_op jit(solution)/shard_map/phase_4/ppermute | solution.py:40
  117.2 6.6 %collective-permute-start.16 = (bf16[2,2,48,4736]{3,2,1,0:T(8,128)(2,1)S(1)}, bf16[2,2,48,4736]{3,2,1,0:T(8,128)(2,1)S(1)}, u32[]{:S(2)}, u32[]{:S(2)}) collective-permute-start(bf16[2,2,48,4736]{3,2,1,0:T(8,128)(2,1)S(1)} %pad_maximum_fusion.3), channel_id=1, source_target_pairs={{0,1},{1,0},{2,3},{3,2},{4,5},{5,4},{6,7},{7,6},{8,9},{9,8},{10,11... | collective-permute-start | bytes 5455880 | tf_op jit(solution)/shard_map/phase_5/ppermute | solution.py:40
  156.1 11.2 %collective-permute-start.17 = (bf16[128,1536]{1,0:T(8,128)(2,1)S(1)}, bf16[128,1536]{1,0:T(8,128)(2,1)S(1)}, u32[]{:S(2)}, u32[]{:S(2)}) collective-permute-start(bf16[128,1536]{1,0:T(8,128)(2,1)S(1)} %get-tuple-element.332), channel_id=1, source_target_pairs={{0,2},{1,3},{2,0},{3,1},{4,6},{5,7},{6,4},{7,5},{8,10},{9,11},{10,... | collective-permute-start | bytes 1179656 | tf_op jit(solution)/shard_map/ffn_forward/ppermute | solution.py:40
  157.6 10.9 %collective-permute-start.18 = (bf16[128,1536]{1,0:T(8,128)(2,1)S(1)}, bf16[128,1536]{1,0:T(8,128)(2,1)S(1)}, u32[]{:S(2)}, u32[]{:S(2)}) collective-permute-start(bf16[128,1536]{1,0:T(8,128)(2,1)S(1)} %get-tuple-element.331), channel_id=1, source_target_pairs={{0,4},{1,5},{2,6},{3,7},{4,0},{5,1},{6,2},{7,3},{8,12},{9,13},{10,... | collective-permute-start | bytes 1179656 | tf_op jit(solution)/shard_map/ffn_forward/ppermute | solution.py:40
  168.6 18.6 %collective-permute-start.19 = (bf16[256,1536]{1,0:T(8,128)(2,1)S(1)}, bf16[256,1536]{1,0:T(8,128)(2,1)}, u32[]{:S(2)}, u32[]{:S(2)}) collective-permute-start(bf16[256,1536]{1,0:T(8,128)(2,1)S(1)} %pad_maximum_fusion.11.refs_0_), channel_id=1, source_target_pairs={{0,4},{1,5},{2,6},{3,7},{4,0},{5,1},{6,2},{7,3},{8,12},{9,13},{10,... | collective-permute-start | bytes 2359304 | tf_op jit(solution)/shard_map/ffn_forward/ppermute | solution.py:40
  170.3 18.3 %collective-permute-start.20 = (bf16[256,1536]{1,0:T(8,128)(2,1)S(1)}, bf16[256,1536]{1,0:T(8,128)(2,1)}, u32[]{:S(2)}, u32[]{:S(2)}) collective-permute-start(bf16[256,1536]{1,0:T(8,128)(2,1)S(1)} %pad_maximum_fusion.12.refs_1_), channel_id=1, source_target_pairs={{0,2},{1,3},{2,0},{3,1},{4,6},{5,7},{6,4},{7,5},{8,10},{9,11},{10,... | collective-permute-start | bytes 2359304 | tf_op jit(solution)/shard_map/ffn_forward/ppermute | solution.py:40
  192.9 17.3 %collective-permute-start.25 = (bf16[256,1536]{1,0:T(8,128)(2,1)S(1)}, bf16[256,1536]{1,0:T(8,128)(2,1)S(1)}, u32[]{:S(2)}, u32[]{:S(2)}) collective-permute-start(bf16[256,1536]{1,0:T(8,128)(2,1)S(1)} %convolution_convert_fusion.2), channel_id=1, source_target_pairs={{0,2},{1,3},{2,0},{3,1},{4,6},{5,7},{6,4},{7,5},{8,10},{9,11},{10,... | collective-permute-start | bytes 2359304 | tf_op jit(solution)/shard_map/ffn_forward/ppermute | solution.py:40
  197.9 17.2 %collective-permute-start.24 = (bf16[256,1536]{1,0:T(8,128)(2,1)S(1)}, bf16[256,1536]{1,0:T(8,128)(2,1)S(1)}, u32[]{:S(2)}, u32[]{:S(2)}) collective-permute-start(bf16[256,1536]{1,0:T(8,128)(2,1)S(1)} %convolution_convert_fusion.3), channel_id=1, source_target_pairs={{0,4},{1,5},{2,6},{3,7},{4,0},{5,1},{6,2},{7,3},{8,12},{9,13},{10,... | collective-permute-start | bytes 2359304 | tf_op jit(solution)/shard_map/ffn_forward/ppermute | solution.py:40
  215.6 7.8 %collective-permute-start.26 = (bf16[128,1536]{1,0:T(8,128)(2,1)S(1)}, bf16[128,1536]{1,0:T(8,128)(2,1)S(1)}, u32[]{:S(2)}, u32[]{:S(2)}) collective-permute-start(bf16[128,1536]{1,0:T(8,128)(2,1)S(1)} %slice.636), channel_id=1, source_target_pairs={{0,2},{1,3},{2,0},{3,1},{4,6},{5,7},{6,4},{7,5},{8,10},{9,11},{10,... | collective-permute-start | bytes 1179656 | tf_op jit(solution)/shard_map/ffn_forward/ppermute | solution.py:40
  216.9 7.8 %collective-permute-start.27 = (bf16[128,1536]{1,0:T(8,128)(2,1)S(1)}, bf16[128,1536]{1,0:T(8,128)(2,1)S(1)}, u32[]{:S(2)}, u32[]{:S(2)}) collective-permute-start(bf16[128,1536]{1,0:T(8,128)(2,1)S(1)} %slice.635), channel_id=1, source_target_pairs={{0,4},{1,5},{2,6},{3,7},{4,0},{5,1},{6,2},{7,3},{8,12},{9,13},{10,... | collective-permute-start | bytes 1179656 | tf_op jit(solution)/shard_map/ffn_forward/ppermute | solution.py:40
  226.2 9.4 %collective-permute-start.28 = (bf16[128,1536]{1,0:T(8,128)(2,1)S(1)}, bf16[128,1536]{1,0:T(8,128)(2,1)S(1)}, u32[]{:S(2)}, u32[]{:S(2)}) collective-permute-start(bf16[128,1536]{1,0:T(8,128)(2,1)S(1)} %get-tuple-element.330), channel_id=1, source_target_pairs={{0,2},{1,3},{2,0},{3,1},{4,6},{5,7},{6,4},{7,5},{8,10},{9,11},{10,... | collective-permute-start | bytes 1179656 | tf_op jit(solution)/shard_map/ffn_backward/ppermute | solution.py:40
  227.2 10.8 %collective-permute-start.29 = (bf16[128,1536]{1,0:T(8,128)(2,1)S(1)}, bf16[128,1536]{1,0:T(8,128)(2,1)S(1)}, u32[]{:S(2)}, u32[]{:S(2)}) collective-permute-start(bf16[128,1536]{1,0:T(8,128)(2,1)S(1)} %get-tuple-element.329), channel_id=1, source_target_pairs={{0,4},{1,5},{2,6},{3,7},{4,0},{5,1},{6,2},{7,3},{8,12},{9,13},{10,... | collective-permute-start | bytes 1179656 | tf_op jit(solution)/shard_map/ffn_backward/ppermute | solution.py:40
  238.1 18.9 %collective-permute-start.30 = (bf16[256,1536]{1,0:T(8,128)(2,1)S(1)}, bf16[256,1536]{1,0:T(8,128)(2,1)S(1)}, u32[]{:S(2)}, u32[]{:S(2)}) collective-permute-start(bf16[256,1536]{1,0:T(8,128)(2,1)S(1)} %pad_maximum_fusion.13.refs_0_), channel_id=1, source_target_pairs={{0,4},{1,5},{2,6},{3,7},{4,0},{5,1},{6,2},{7,3},{8,12},{9,13},{10,... | collective-permute-start | bytes 2359304 | tf_op jit(solution)/shard_map/ffn_backward/ppermute | solution.py:40
  238.5 18.5 %collective-permute-start.31 = (bf16[256,1536]{1,0:T(8,128)(2,1)S(1)}, bf16[256,1536]{1,0:T(8,128)(2,1)S(1)}, u32[]{:S(2)}, u32[]{:S(2)}) collective-permute-start(bf16[256,1536]{1,0:T(8,128)(2,1)S(1)} %pad_maximum_fusion.14.refs_1_), channel_id=1, source_target_pairs={{0,2},{1,3},{2,0},{3,1},{4,6},{5,7},{6,4},{7,5},{8,10},{9,11},{10,... | collective-permute-start | bytes 2359304 | tf_op jit(solution)/shard_map/ffn_backward/ppermute | solution.py:40
  262.3 17.4 %collective-permute-start.33 = (bf16[256,1536]{1,0:T(8,128)(2,1)}, bf16[256,1536]{1,0:T(8,128)(2,1)}, u32[]{:S(2)}, u32[]{:S(2)}) collective-permute-start(bf16[256,1536]{1,0:T(8,128)(2,1)} %fusion.20), channel_id=1, source_target_pairs={{0,2},{1,3},{2,0},{3,1},{4,6},{5,7},{6,4},{7,5},{8,10},{9,11},{10,... | collective-permute-start | bytes 2359304 | tf_op jit(solution)/shard_map/ffn_backward/ppermute | solution.py:40
  265.7 14.0 %collective-permute-start.32 = (bf16[256,1536]{1,0:T(8,128)(2,1)}, bf16[256,1536]{1,0:T(8,128)(2,1)}, u32[]{:S(2)}, u32[]{:S(2)}) collective-permute-start(bf16[256,1536]{1,0:T(8,128)(2,1)} %fusion.23), channel_id=1, source_target_pairs={{0,4},{1,5},{2,6},{3,7},{4,0},{5,1},{6,2},{7,3},{8,12},{9,13},{10,... | collective-permute-start | bytes 2359304 | tf_op jit(solution)/shard_map/ffn_backward/ppermute | solution.py:40
  267.3 12.3 %collective-permute-start.34 = (f32[2,128]{1,0:T(2,128)S(1)}, f32[2,128]{1,0:T(2,128)S(1)}, u32[]{:S(2)}, u32[]{:S(2)}) collective-permute-start(f32[2,128]{1,0:T(2,128)S(1)} %broadcast_in_dim.15), channel_id=1, source_target_pairs={{0,1},{1,0},{2,3},{3,2},{4,5},{5,4},{6,7},{7,6},{8,9},{9,8},{10,11... | collective-permute-start | bytes 3080 | tf_op jit(solution)/shard_map/ffn_backward/ppermute | solution.py:40
  279.7 129.2 %reduce-scatter.5.cloned.1.call-start = ((), (), s32[]{:S(2)}) async-start(), calls=%async_computation.4 | async-start | bytes 3538944 | tf_op jit(solution)/shard_map/q_k_v_weight_gradients/reduce_scatter | solution.py:120
  283.5 12.7 %collective-permute-start.35 = (bf16[128,1536]{1,0:T(8,128)(2,1)}, bf16[128,1536]{1,0:T(8,128)(2,1)}, u32[]{:S(2)}, u32[]{:S(2)}) collective-permute-start(bf16[128,1536]{1,0:T(8,128)(2,1)} %slice.634), channel_id=1, source_target_pairs={{0,2},{1,3},{2,0},{3,1},{4,6},{5,7},{6,4},{7,5},{8,10},{9,11},{10,... | collective-permute-start | bytes 1179656 | tf_op jit(solution)/shard_map/ffn_backward/ppermute | solution.py:40
  285.7 11.6 %collective-permute-start.36 = (bf16[128,1536]{1,0:T(8,128)(2,1)}, bf16[128,1536]{1,0:T(8,128)(2,1)}, u32[]{:S(2)}, u32[]{:S(2)}) collective-permute-start(bf16[128,1536]{1,0:T(8,128)(2,1)} %slice.633), channel_id=1, source_target_pairs={{0,4},{1,5},{2,6},{3,7},{4,0},{5,1},{6,2},{7,3},{8,12},{9,13},{10,... | collective-permute-start | bytes 1179656 | tf_op jit(solution)/shard_map/ffn_backward/ppermute | solution.py:40
  286.0 10.2 %collective-permute-start.37 = (f32[2,128]{1,0:T(2,128)S(1)}, f32[2,128]{1,0:T(2,128)S(1)}, u32[]{:S(2)}, u32[]{:S(2)}) collective-permute-start(f32[2,128]{1,0:T(2,128)S(1)} %add.500), channel_id=1, source_target_pairs={{0,8},{1,9},{2,10},{3,11},{4,12},{5,13},{6,14},{7,15},{8,0},{9,1},... | collective-permute-start | bytes 3080 | tf_op jit(solution)/shard_map/ffn_backward/ppermute | solution.py:40
  310.2 4.8 %collective-permute-start.38 = (bf16[768,1536]{1,0:T(8,128)(2,1)S(1)}, bf16[768,1536]{1,0:T(8,128)(2,1)S(1)}, u32[]{:S(2)}, u32[]{:S(2)}) collective-permute-start(bf16[768,1536]{1,0:T(8,128)(2,1)S(1)} %convolution_convert_fusion.1), channel_id=1, source_target_pairs={{0,1},{1,0},{2,3},{3,2},{4,5},{5,4},{6,7},{7,6},{8,9},{9,8},{10,11... | collective-permute-start | bytes 7077896 | tf_op jit(solution)/shard_map/attention_backward/ppermute | solution.py:40
  310.3 4.7 %collective-permute-start.39 = (f32[2,128]{1,0:T(2,128)S(1)}, f32[2,128]{1,0:T(2,128)S(1)}, u32[]{:S(2)}, u32[]{:S(2)}) collective-permute-start(f32[2,128]{1,0:T(2,128)S(1)} %add.505), channel_id=1, source_target_pairs={{0,16},{1,17},{2,18},{3,19},{4,20},{5,21},{6,22},{7,23},{8,24},{9,... | collective-permute-start | bytes 3080 | tf_op jit(solution)/shard_map/attention_backward/ppermute | solution.py:40
  315.6 20.7 %collective-permute-start.40 = (bf16[192,1536]{1,0:T(8,128)(2,1)S(1)}, bf16[192,1536]{1,0:T(8,128)(2,1)S(1)}, u32[]{:S(2)}, u32[]{:S(2)}) collective-permute-start(bf16[192,1536]{1,0:T(8,128)(2,1)S(1)} %get-tuple-element.315), channel_id=1, source_target_pairs={{0,4},{1,5},{2,6},{3,7},{4,0},{5,1},{6,2},{7,3},{8,12},{9,13},{10,... | collective-permute-start | bytes 1769480 | tf_op jit(solution)/shard_map/attention_backward/ppermute | solution.py:40
  316.0 20.3 %collective-permute-start.41 = (bf16[192,1536]{1,0:T(8,128)(2,1)S(1)}, bf16[192,1536]{1,0:T(8,128)(2,1)S(1)}, u32[]{:S(2)}, u32[]{:S(2)}) collective-permute-start(bf16[192,1536]{1,0:T(8,128)(2,1)S(1)} %get-tuple-element.314), channel_id=1, source_target_pairs={{0,2},{1,3},{2,0},{3,1},{4,6},{5,7},{6,4},{7,5},{8,10},{9,11},{10,... | collective-permute-start | bytes 1769480 | tf_op jit(solution)/shard_map/attention_backward/ppermute | solution.py:40
  316.7 19.6 %collective-permute-start.42 = (f32[2,128]{1,0:T(2,128)S(1)}, f32[2,128]{1,0:T(2,128)S(1)}, u32[]{:S(2)}, u32[]{:S(2)}) collective-permute-start(f32[2,128]{1,0:T(2,128)S(1)} %add.507), channel_id=1, source_target_pairs={{0,2},{1,3},{2,0},{3,1},{4,6},{5,7},{6,4},{7,5},{8,10},{9,11},{10,... | collective-permute-start | bytes 3080 | tf_op jit(solution)/shard_map/attention_backward/ppermute | solution.py:40
  337.8 12.2 %collective-permute-start.43 = (bf16[768,3072]{1,0:T(8,128)(2,1)S(1)}, bf16[768,3072]{1,0:T(8,128)(2,1)}, u32[]{:S(2)}, u32[]{:S(2)}) collective-permute-start(bf16[768,3072]{1,0:T(8,128)(2,1)S(1)} %convolution_convert_fusion), channel_id=1, source_target_pairs={{0,1},{1,0},{2,3},{3,2},{4,5},{5,4},{6,7},{7,6},{8,9},{9,8},{10,11... | collective-permute-start | bytes 14155784 | tf_op jit(solution)/shard_map/q_k_v_weight_gradients/ppermute | solution.py:40
  340.0 10.0 %collective-permute-start.45 = (bf16[96,1536]{1,0:T(8,128)(2,1)S(1)}, bf16[96,1536]{1,0:T(8,128)(2,1)}, u32[]{:S(2)}, u32[]{:S(2)}) collective-permute-start(bf16[96,1536]{1,0:T(8,128)(2,1)S(1)} %get-tuple-element.306), channel_id=1, source_target_pairs={{0,2},{1,3},{2,0},{3,1},{4,6},{5,7},{6,4},{7,5},{8,10},{9,11},{10,... | collective-permute-start | bytes 884744 | tf_op jit(solution)/shard_map/attention_backward/ppermute | solution.py:40
  340.7 9.3 %collective-permute-start.46 = (bf16[96,1536]{1,0:T(8,128)(2,1)S(1)}, bf16[96,1536]{1,0:T(8,128)(2,1)}, u32[]{:S(2)}, u32[]{:S(2)}) collective-permute-start(bf16[96,1536]{1,0:T(8,128)(2,1)S(1)} %get-tuple-element.305), channel_id=1, source_target_pairs={{0,4},{1,5},{2,6},{3,7},{4,0},{5,1},{6,2},{7,3},{8,12},{9,13},{10,... | collective-permute-start | bytes 884744 | tf_op jit(solution)/shard_map/attention_backward/ppermute | solution.py:40
  342.5 7.5 %collective-permute-start.44 = (f32[2,128]{1,0:T(2,128)S(1)}, f32[2,128]{1,0:T(2,128)S(1)}, u32[]{:S(2)}, u32[]{:S(2)}) collective-permute-start(f32[2,128]{1,0:T(2,128)S(1)} %add.508), channel_id=1, source_target_pairs={{0,4},{1,5},{2,6},{3,7},{4,0},{5,1},{6,2},{7,3},{8,12},{9,13},{10,... | collective-permute-start | bytes 3080 | tf_op jit(solution)/shard_map/q_k_v_weight_gradients/ppermute | solution.py:40
  354.2 27.6 %collective-permute-start.47 = (bf16[192,3072]{1,0:T(8,128)(2,1)}, bf16[192,3072]{1,0:T(8,128)(2,1)}, u32[]{:S(2)}, u32[]{:S(2)}) collective-permute-start(bf16[192,3072]{1,0:T(8,128)(2,1)} %get-tuple-element.304), channel_id=1, source_target_pairs={{0,4},{1,5},{2,6},{3,7},{4,0},{5,1},{6,2},{7,3},{8,12},{9,13},{10,... | collective-permute-start | bytes 3538952 | tf_op jit(solution)/shard_map/q_k_v_weight_gradients/ppermute | solution.py:40
  356.0 27.3 %collective-permute-start.48 = (bf16[192,3072]{1,0:T(8,128)(2,1)}, bf16[192,3072]{1,0:T(8,128)(2,1)}, u32[]{:S(2)}, u32[]{:S(2)}) collective-permute-start(bf16[192,3072]{1,0:T(8,128)(2,1)} %get-tuple-element.303), channel_id=1, source_target_pairs={{0,2},{1,3},{2,0},{3,1},{4,6},{5,7},{6,4},{7,5},{8,10},{9,11},{10,... | collective-permute-start | bytes 3538952 | tf_op jit(solution)/shard_map/q_k_v_weight_gradients/ppermute | solution.py:40
  385.9 23.0 %collective-permute-start.49 = (bf16[96,3072]{1,0:T(8,128)(2,1)}, bf16[96,3072]{1,0:T(8,128)(2,1)S(1)}, u32[]{:S(2)}, u32[]{:S(2)}) collective-permute-start(bf16[96,3072]{1,0:T(8,128)(2,1)} %get-tuple-element.288), channel_id=1, source_target_pairs={{0,2},{1,3},{2,0},{3,1},{4,6},{5,7},{6,4},{7,5},{8,10},{9,11},{10,... | collective-permute-start | bytes 1769480 | tf_op jit(solution)/shard_map/weight_gradients_to_owners/ppermute | solution.py:40
  387.2 21.7 %collective-permute-start.50 = (bf16[96,3072]{1,0:T(8,128)(2,1)}, bf16[96,3072]{1,0:T(8,128)(2,1)S(1)}, u32[]{:S(2)}, u32[]{:S(2)}) collective-permute-start(bf16[96,3072]{1,0:T(8,128)(2,1)} %get-tuple-element.287), channel_id=1, source_target_pairs={{0,4},{1,5},{2,6},{3,7},{4,0},{5,1},{6,2},{7,3},{8,12},{9,13},{10,... | collective-permute-start | bytes 1769480 | tf_op jit(solution)/shard_map/weight_gradients_to_owners/ppermute | solution.py:40
  391.7 5.3 %collective-permute-start.53 = (f32[2,1536]{1,0:T(2,128)S(1)}, f32[2,1536]{1,0:T(2,128)S(1)}, u32[]{:S(2)}, u32[]{:S(2)}) collective-permute-start(f32[2,1536]{1,0:T(2,128)S(1)} %add.519), channel_id=1, source_target_pairs={{0,16},{1,17},{2,18},{3,19},{4,20},{5,21},{6,22},{7,23},{8,24},{9,... | collective-permute-start | bytes 36872 | tf_op jit(solution)/shard_map/weight_gradients_to_owners/ppermute | solution.py:40
  394.0 8.8 %collective-permute-start.54 = (bf16[48,1536]{1,0:T(8,128)(2,1)}, bf16[48,1536]{1,0:T(8,128)(2,1)S(1)}, u32[]{:S(2)}, u32[]{:S(2)}) collective-permute-start(bf16[48,1536]{1,0:T(8,128)(2,1)} %get-tuple-element.312), channel_id=1, source_target_pairs={{0,24},{1,25},{2,26},{3,27},{4,28},{5,29},{6,30},{7,31},{8,16},{9,... | collective-permute-start | bytes 442376 | tf_op jit(solution)/shard_map/q_k_v_weight_gradients/ppermute | solution.py:40
  397.0 11.9 %collective-permute-start.55 = (bf16[48,1536]{1,0:T(8,128)(2,1)}, bf16[48,1536]{1,0:T(8,128)(2,1)S(1)}, u32[]{:S(2)}, u32[]{:S(2)}) collective-permute-start(bf16[48,1536]{1,0:T(8,128)(2,1)} %get-tuple-element.313), channel_id=1, source_target_pairs={{0,16},{1,17},{2,18},{3,19},{4,20},{5,21},{6,22},{7,23},{8,24},{9,... | collective-permute-start | bytes 442376 | tf_op jit(solution)/shard_map/q_k_v_weight_gradients/ppermute | solution.py:40
  397.0 11.9 %collective-permute-start.56 = (bf16[48,1536]{1,0:T(8,128)(2,1)}, bf16[48,1536]{1,0:T(8,128)(2,1)}, u32[]{:S(2)}, u32[]{:S(2)}) collective-permute-start(bf16[48,1536]{1,0:T(8,128)(2,1)} %get-tuple-element.311), channel_id=1, source_target_pairs={{0,8},{1,9},{2,10},{3,11},{4,12},{5,13},{6,14},{7,15},{8,0},{9,1},... | collective-permute-start | bytes 442376 | tf_op jit(solution)/shard_map/q_k_v_weight_gradients/ppermute | solution.py:40
  409.6 12.0 %collective-permute-start.61 = (bf16[48,2048]{1,0:T(8,128)(2,1)S(1)}, bf16[48,2048]{1,0:T(8,128)(2,1)S(1)}, u32[]{:S(2)}, u32[]{:S(2)}) collective-permute-start(bf16[48,2048]{1,0:T(8,128)(2,1)S(1)} %get-tuple-element.328), channel_id=1, source_target_pairs={{0,2},{1,3},{2,0},{3,1},{4,6},{5,7},{6,4},{7,5},{8,10},{9,11},{10,... | collective-permute-start | bytes 589832 | tf_op jit(solution)/shard_map/weight_gradients_to_owners/ppermute | solution.py:40
  410.3 13.4 %collective-permute-start.62 = (bf16[48,2048]{1,0:T(8,128)(2,1)S(1)}, bf16[48,2048]{1,0:T(8,128)(2,1)S(1)}, u32[]{:S(2)}, u32[]{:S(2)}) collective-permute-start(bf16[48,2048]{1,0:T(8,128)(2,1)S(1)} %get-tuple-element.327), channel_id=1, source_target_pairs={{0,4},{1,5},{2,6},{3,7},{4,0},{5,1},{6,2},{7,3},{8,12},{9,13},{10,... | collective-permute-start | bytes 589832 | tf_op jit(solution)/shard_map/weight_gradients_to_owners/ppermute | solution.py:40
  411.1 12.5 %collective-permute-start.63 = (bf16[48,2048]{1,0:T(8,128)(2,1)S(1)}, bf16[48,2048]{1,0:T(8,128)(2,1)S(1)}, u32[]{:S(2)}, u32[]{:S(2)}) collective-permute-start(bf16[48,2048]{1,0:T(8,128)(2,1)S(1)} %get-tuple-element.326), channel_id=1, source_target_pairs={{0,6},{1,7},{2,4},{3,5},{4,2},{5,3},{6,0},{7,1},{8,14},{9,15},{10,... | collective-permute-start | bytes 589832 | tf_op jit(solution)/shard_map/weight_gradients_to_owners/ppermute | solution.py:40
  413.1 8.5 %collective-permute-start.60 = (f32[2,1536]{1,0:T(2,128)S(1)}, f32[2,1536]{1,0:T(2,128)S(1)}, u32[]{:S(2)}, u32[]{:S(2)}) collective-permute-start(f32[2,1536]{1,0:T(2,128)S(1)} %add.520), channel_id=1, source_target_pairs={{0,2},{1,3},{2,0},{3,1},{4,6},{5,7},{6,4},{7,5},{8,10},{9,11},{10,... | collective-permute-start | bytes 36872 | tf_op jit(solution)/shard_map/weight_gradients_to_owners/ppermute | solution.py:40
  416.5 11.8 %collective-permute-start.57 = (bf16[48,3072]{1,0:T(8,128)(2,1)S(1)}, bf16[48,3072]{1,0:T(8,128)(2,1)S(1)}, u32[]{:S(2)}, u32[]{:S(2)}) collective-permute-start(bf16[48,3072]{1,0:T(8,128)(2,1)S(1)} %get-tuple-element.298), channel_id=1, source_target_pairs={{0,24},{1,25},{2,26},{3,27},{4,28},{5,29},{6,30},{7,31},{8,16},{9,... | collective-permute-start | bytes 884744 | tf_op jit(solution)/shard_map/weight_gradients_to_owners/ppermute | solution.py:40
  421.6 19.3 %collective-permute-start.58 = (bf16[48,3072]{1,0:T(8,128)(2,1)S(1)}, bf16[48,3072]{1,0:T(8,128)(2,1)S(1)}, u32[]{:S(2)}, u32[]{:S(2)}) collective-permute-start(bf16[48,3072]{1,0:T(8,128)(2,1)S(1)} %get-tuple-element.299), channel_id=1, source_target_pairs={{0,16},{1,17},{2,18},{3,19},{4,20},{5,21},{6,22},{7,23},{8,24},{9,... | collective-permute-start | bytes 884744 | tf_op jit(solution)/shard_map/weight_gradients_to_owners/ppermute | solution.py:40
  421.6 19.3 %collective-permute-start.59 = (bf16[48,3072]{1,0:T(8,128)(2,1)S(1)}, bf16[48,3072]{1,0:T(8,128)(2,1)S(1)}, u32[]{:S(2)}, u32[]{:S(2)}) collective-permute-start(bf16[48,3072]{1,0:T(8,128)(2,1)S(1)} %get-tuple-element.300), channel_id=1, source_target_pairs={{0,8},{1,9},{2,10},{3,11},{4,12},{5,13},{6,14},{7,15},{8,0},{9,1},... | collective-permute-start | bytes 884744 | tf_op jit(solution)/shard_map/weight_gradients_to_owners/ppermute | solution.py:40
  (67 other events, 443.5 us)
Sparse Core Ops, SparseCore 0:
  80.3 88.3 all-gather.1
  279.8 68.7 reduce-scatter.2
  351.0 38.6 reduce-scatter.4

commit v10 on v9

--- a/solution.py
+++ b/solution.py
@@ -303,28 +303,29 @@
         a2, b2, far = tied(in_order(x, a, a_x), in_order(y, b, b_y), far)
         near_1 = jnp.stack([a2, b2])
         ffn = merged((cuts[0], *tied(*crossing)), w_down, p)
-        a_far, b_far, second = tied(swap(a2, 4), swap(b2, 2), along_z(far, out_pairs))
+        a_far, b_far, second, core_1 = tied(
+            swap(a2, 4), swap(b2, 2), along_z(far, out_pairs), swap(near_1, 1)
+        )
         out = put(out, near_1, z, z_b, y, x, c)
     with jax.named_scope("ffn_weights"):
         ffn = along_column(tied(ffn, second)[0])
     with jax.named_scope("phase_3"):
         a, b = jnp.where(end, first, down), jnp.where(end, second, far)
-        a, b, near_1 = tied(a, b, near_1)
-        a_x, b_y, core_1 = tied(swap(a, 2), swap(b, 4), swap(near_1, 1))
-        far_1 = jnp.stack([a_far, b_far])
+        a, b, far_1 = tied(a, b, jnp.stack([a_far, b_far]))
+        a_x, b_y, core_2 = tied(swap(a, 2), swap(b, 4), swap(far_1, 1))
+        out = put(out, core_1, z, z_b, y, x, 1 - c)
         out = put(out, far_1, z, z_b, 1 - y, 1 - x, c)
     with jax.named_scope("phase_4"):
-        a2, b2, far_1 = tied(in_order(x, a, a_x), in_order(y, b, b_y), far_1)
-        a_far, b_far, core_2 = tied(swap(a2, 4), swap(b2, 2), swap(far_1, 1))
-        out = put(out, core_1, z, z_b, y, x, 1 - c)
+        a2, b2 = tied(in_order(x, a, a_x), in_order(y, b, b_y))
         near_2 = jnp.stack([a2, b2])
+        a_far, b_far, core_3 = tied(swap(a2, 4), swap(b2, 2), swap(near_2, 1))
+        out = put(out, core_2, z, z_b, 1 - y, 1 - x, 1 - c)
         out = put(out, near_2, z_c, z_d, y, x, c)
     with jax.named_scope("phase_5"):
-        near_2, far_2 = tied(near_2, jnp.stack([a_far, b_far]))
-        core_3, core_4 = tied(swap(near_2, 1), swap(far_2, 1))
-        out = put(out, core_2, z, z_b, 1 - y, 1 - x, 1 - c)
+        far_2 = jnp.stack([a_far, b_far])
+        core_4 = swap(far_2, 1)
+        out = put(out, core_3, z_c, z_d, y, x, 1 - c)
         out = put(out, far_2, z_c, z_d, 1 - y, 1 - x, c)
-        out = put(out, core_3, z_c, z_d, y, x, 1 - c)
         out = put(out, core_4, z_c, z_d, 1 - y, 1 - x, 1 - c)
         gathered = out.reshape(32 * rows, columns)
     return gathered, ffn
@@ -1001,19 +1002,26 @@
         grad_res = grad_out + grad_res
         res_low = grad_res.astype(BF)
         g_wo = PlaneSum(mixed_sent, res_low)
-        wo_came, came = tied(g_wo.step_0(), swap(sums, high))
+        wo_came, came, grad_mixed = tied(
+            g_wo.step_0(), swap(sums, high), mm_t(res_low, wo).astype(BF)
+        )
         sums = sums + came
         wo_moving = g_wo.step_1(wo_came)
-        grad_mixed = mm_t(res_low, wo).astype(BF)
         grad_raw = attention_backward(grad_mixed, query, key, value, cosine, sine)
         *wo_came, grad_raw, sums, came = tied(*wo_moving, grad_raw, sums, swap(sums, 2))
         sums = sums + came
         wo_moving = g_wo.step_2(wo_came)
 
+    with jax.named_scope("input_gradient"):
+        input_grad, grad_gain_in = input_gradient(
+            grad_raw, gathered, tokens, inv_attn, gain_in[None], grad_res
+        )
+        gains = jnp.concatenate([grad_gain_in, grad_gain_mid[None]])
+
     with jax.named_scope("q_k_v_weight_gradients"):
         g_qkv = PlaneSum(normed_sent, grad_raw)
-        qkv_came, grad_raw, sums, came, g_both, g_down, *wo_came = tied(
-            g_qkv.step_0(), grad_raw, sums, swap(sums, 4), g_both, g_down, *wo_moving
+        qkv_came, gains, sums, came, g_both, g_down, *wo_came = tied(
+            g_qkv.step_0(), gains, sums, swap(sums, 4), g_both, g_down, *wo_moving
         )
         g_down = sum_to_owners(g_down)
         sums = sums + came
@@ -1022,33 +1030,28 @@
         g_wo = g_wo.step_3(wo_came, rows)
         wo_moving = direct([g_wo], z) if planes == 4 else []
 
-    with jax.named_scope("input_gradient"):
-        input_grad, grad_gain_in = input_gradient(
-            grad_raw, gathered, tokens, inv_attn, gain_in[None], grad_res
-        )
-        gains = jnp.concatenate([grad_gain_in, grad_gain_mid[None]])
-
     with jax.named_scope("weight_gradients_to_owners"):
+        for mask in (1, 8, high):
+            gains = gains + swap(gains, mask)
         *qkv_came, gains = tied(*qkv_moving, gains)
         qkv_moving = g_qkv.step_2(qkv_came)
-        for mask in (1, 8, high):
-            gains = gains + swap(gains, mask)
         qkv_0, qkv_1, gains, g_both, g_down, *wo_came = tied(
             *qkv_moving, gains, g_both, g_down, *wo_moving
         )
         qkv_came = (qkv_0, qkv_1)
         g_wo = owned([g_wo], wo_came, z) if planes == 4 else z_reduce([g_wo])
-        g_qkv = g_qkv.step_3(qkv_came, rows)
+        g_qkv, g_both = tied(g_qkv.step_3(qkv_came, rows), g_both)
         if planes == 4:
             moving = direct([g_qkv], z)
+        gains = gains + swap(gains, 2)
+        gains, g_both = tied(gains, g_both)
         g_both = g_both.reshape(4, rows, 2 * units)
         came = [pick(g_both, p ^ r, 0) for r in range(4)]
-        gains_came, *moved = tied(swap(gains, 2), *[swap(came[r], r << 1) for r in (1, 2, 3)])
+        gains_came, *moved = tied(swap(gains, 4), *[swap(came[r], r << 1) for r in (1, 2, 3)])
         gains = gains + gains_came
         for mask in rest:
             gains = gains + swap(gains, mask)
         grad_gate, grad_up = spread_columns([came[0]] + moved, p, part)
-        gains = gains + swap(gains, 4)
         g_gains = lax.dynamic_slice_in_dim(gains, position * rows, rows, 1)
         if planes == 4:
             g_qkv = owned([g_qkv], moving, z)

time: 457 us -> 451 us (0.987)
  waiting for transfers between devices: 135 us -> 128 us
    ppermute x60, waiting for transfers between devices: 130 us -> 113 us  [swap(): return lax.ppermute(value, 'dp', [(i, i ^ mask) for i in range(n)])]
    all_gather x1, waiting for transfers between devices: 0.01 us -> 5.26 us  [along_column(): lax.all_gather(value, 'dp', axis_index_groups=column_groups(True), axis=0...]
    ppermute x5, waiting for transfers between devices: 4.4 us -> 9.63 us  [along_z(): lax.ppermute(value, 'dp', [(8 * a + i, 8 * b + i) for a, b in pairs for i...]
    unnamed x141 -> x143, local copies, waits for them, and re-layouts: 20.3 us -> 19.4 us
  transfers between devices with their start and end apart: 68 -> 68, of which waited for: 31 -> 29; matrix products, arithmetic and copies ran while one was open for 24% -> 24% of each run, Pallas kernels for 17% -> 17%
where the time goes in v10:
time: 451 us; the launch traced here: 444 us
  waiting for transfers between devices  128 us (28%)
  starting transfers between devices  77.1 us (17%)
  Pallas kernels  76.1 us (17%)
  matrix products  54 us (12%)
  local copies, waits for them, and re-layouts  46.5 us (10%)
  other arithmetic  44.1 us (10%)
  between operations  18.2 us (4%)
    ppermute x60, waiting for transfers between devices, swap(): return lax.ppermute(value, 'dp', [(i, i ^ mask) for i in range(n)])  113 us
    ppermute x60, starting transfers between devices, swap(): return lax.ppermute(value, 'dp', [(i, i ^ mask) for i in range(n)])  61.6 us
    dot_general x22, matrix products, dot(): return lax.dot_general(a, b, (dims, ((), ())), preferred_element_type=F32)  54 us
    unnamed x143, local copies, waits for them, and re-layouts  19.4 us
    dynamic_update_slice x16, local copies, waits for them, and re-layouts, place(): return lax.dynamic_update_slice(out, piece, where)  18.6 us
    pallas_call x2, Pallas kernels, products(): pl.pallas_call(kernel, grid=(columns // tile,), out_shape=jax.ShapeDtypeS...  15.5 us
    ppermute x5, starting transfers between devices, along_z(): lax.ppermute(value, 'dp', [(8 * a + i, 8 * b + i) for a, b in pairs for i...  15.3 us
    pallas_call x1, Pallas kernels, attention_backward(): pl.pallas_call(kernel, grid=(count // SEQ, steps), out_shape=jax.ShapeDty...  14.1 us
  transfers between devices with their start and end apart: 68, of which 29 were waited for; matrix products, arithmetic and copies ran while one was open for 24% of the time, Pallas kernels for 17%

profile of v10, /device:TPU:0, one launch (start us, length us, event | category | flops | bytes accessed | tf_op | source)
XLA Modules:
  0.0 443.8 jit_solution(11509171691760778436)
XLA Ops:
  11.7 5.0 %collective-permute-start = (bf16[48,4736]{1,0:T(8,128)(2,1)S(1)}, bf16[48,4736]{1,0:T(8,128)(2,1)S(1)}, u32[]{:S(2)}, u32[]{:S(2)}) collective-permute-start(bf16[48,4736]{1,0:T(8,128)(2,1)S(1)} %packed.1), channel_id=1, source_target_pairs={{0,8},{1,9},{2,10},{3,11},{4,12},{5,13},{6,14},{7,15},{8,16},{9,17... | collective-permute-start | bytes 1363976 | tf_op jit(solution)/shard_map/phase_0/ppermute | solution.py:77
  24.1 4.2 fusion.3
  28.3 4.4 fusion.2
  34.2 6.3 %collective-permute-start.4 = (bf16[48,4736]{1,0:T(8,128)(2,1)S(1)}, bf16[48,4736]{1,0:T(8,128)(2,1)}, u32[]{:S(2)}, u32[]{:S(2)}) collective-permute-start(bf16[48,4736]{1,0:T(8,128)(2,1)S(1)} %packed.1), channel_id=1, source_target_pairs={{0,16},{1,17},{2,18},{3,19},{4,20},{5,21},{6,22},{7,23},{24,8},{25... | collective-permute-start | bytes 1363976 | tf_op jit(solution)/shard_map/phase_1/ppermute | solution.py:77
  45.1 2.5 collective-permute-start.23
  47.6 4.2 collective-permute-done.23.refs_3_
  52.9 2.6 collective-permute-done.3
  63.1 1.8 broadcast_select_fusion.1
  64.9 9.6 %collective-permute-done.8 = bf16[48,4736]{1,0:T(8,128)(2,1)S(1)} collective-permute-done((bf16[48,4736]{1,0:T(8,128)(2,1)}, bf16[48,4736]{1,0:T(8,128)(2,1)S(1)}, u32[]{:S(2)}, u32[]{:S(2)}) %collective-permute-start.8) | collective-permute-done | bytes 454688 | tf_op jit(solution)/shard_map/phase_2/ppermute | solution.py:77
  74.5 2.1 collective-permute-done.6
  79.4 1.7 collective-permute-start.11
  85.4 5.6 %collective-permute-done.10 = bf16[48,4736]{1,0:T(8,128)(2,1)} collective-permute-done((bf16[48,4736]{1,0:T(8,128)(2,1)}, bf16[48,4736]{1,0:T(8,128)(2,1)}, u32[]{:S(2)}, u32[]{:S(2)}) %collective-permute-start.10) | collective-permute-done | bytes 454688 | tf_op jit(solution)/shard_map/phase_3/ppermute | solution.py:40
  94.9 1.7 collective-permute-start.13
  97.5 2.2 bitcast_dynamic-update-slice_fusion.7
  99.7 2.1 bitcast_dynamic-update-slice_fusion.6
  103.9 12.5 %collective-permute-done.13 = bf16[2,48,4736]{2,1,0:T(8,128)(2,1)S(1)} collective-permute-done((bf16[2,48,4736]{2,1,0:T(8,128)(2,1)S(1)}, bf16[2,48,4736]{2,1,0:T(8,128)(2,1)S(1)}, u32[]{:S(2)}, u32[]{:S(2)}) %collective-permute-start.13) | collective-permute-done | bytes 909344 | tf_op jit(solution)/shard_map/phase_4/ppermute | solution.py:40
  126.0 5.6 %fusion.q_raw.k_raw.v_raw = f32[256,3072]{1,0:T(8,128)S(1)} fusion(bf16[256,1536]{1,0:T(8,128)(2,1)S(1)} %fusion.31, bf16[1536,4736]{1,0:T(8,128)(2,1)} %bitcast.199), kind=kOutput, calls=%fused_computation | convolution fusion | flops 2415919104 | bytes 13369344 | tf_op jit(solution)/shard_map/attention_forward/dot_general | solution.py:23
  131.7 12.6 %attention_forward.1 = (bf16[256,1536]{1,0:T(8,128)(2,1)S(1)}, bf16[256,768]{1,0:T(8,128)(2,1)S(1)}, bf16[256,768]{1,0:T(8,128)(2,1)S(1)}, bf16[256,1536]{1,0:T(8,128)(2,1)S(1)}) custom-call(f32[256,3072]{1,0:T(8,128)S(1)} %fusion.q_raw.k_raw.v_raw, f32[256,3072]{1,0:T(8,128)S(1)} %fusion.q_raw.k_raw.v_raw, f32[256,3072]{1,0:T(8,128)S(1)} %fusion.q_raw.k_raw.v_raw, ...), custom_call_target="tpu_custom_call" | custom-call | flops 1 | bytes 1 | tf_op jit(solution)/shard_map/attention_forward/attention_forward/pallas_call | solution.py:538
  146.7 4.1 multiply_reduce_fusion.3
  153.7 10.3 %collective-permute-done.17 = bf16[128,1536]{1,0:T(8,128)(2,1)S(1)} collective-permute-done((bf16[128,1536]{1,0:T(8,128)(2,1)S(1)}, bf16[128,1536]{1,0:T(8,128)(2,1)S(1)}, u32[]{:S(2)}, u32[]{:S(2)}) %collective-permute-start.17) | collective-permute-done | bytes 393248 | tf_op jit(solution)/shard_map/ffn_forward/ppermute | solution.py:40
  166.3 5.3 %all-gather.2.cloned.1.call-done.ref.refs_2_.refs_3_.refs_4_.refs_5_ = bf16[1536,3072]{1,0:T(8,128)(2,1)} async-done(((bf16[192,3072]{1,0:T(8,128)(2,1)}), bf16[1536,3072]{1,0:T(8,128)(2,1)}) %all-gather.2.cloned.1.call-update) | async-done | bytes 9437200 | tf_op jit(solution)/shard_map/ffn_weights/all_gather | solution.py:114
  171.6 2.2 w_down_from.1.refs_4_.refs_6_
  173.8 2.5 copy-done
  176.2 8.6 %ffn_forward_beside.1 = (f32[512,1536]{1,0:T(8,128)S(1)}, bf16[512,1536]{1,0:T(8,128)(2,1)S(1)}, bf16[512,1024]{1,0:T(8,128)(2,1)S(1)}, f32[512,1024]{1,0:T(8,128)S(1)}, f32[512,1024]{1,0:T(8,128)S(1)}) custom-call(bf16[256,1536]{1,0:T(8,128)(2,1)S(1)} %pad_maximum_fusion.12.refs_0_, bf16[256,1536]{1,0:T(8,128)(2,1)S(1)} %pad_maximum_fusion.13.refs_1_, ...), custom_call_target="tpu_custom_call" | custom-call | flops 1 | bytes 1 | tf_op jit(solution)/shard_map/ffn_forward/ffn_forward_beside/pallas_call | solution.py:723
  184.9 3.3 fusion.12
  191.1 2.9 fusion.14
  196.9 2.3 convolution_convert_fusion.4
  199.2 2.3 convolution_convert_fusion.5
  201.5 7.8 %collective-permute-done.25 = bf16[256,1536]{1,0:T(8,128)(2,1)S(1)} collective-permute-done((bf16[256,1536]{1,0:T(8,128)(2,1)S(1)}, bf16[256,1536]{1,0:T(8,128)(2,1)S(1)}, u32[]{:S(2)}, u32[]{:S(2)}) %collective-permute-start.25) | collective-permute-done | bytes 786464 | tf_op jit(solution)/shard_map/ffn_forward/ppermute | solution.py:40
  209.3 5.6 %collective-permute-done.24 = bf16[256,1536]{1,0:T(8,128)(2,1)S(1)} collective-permute-done((bf16[256,1536]{1,0:T(8,128)(2,1)S(1)}, bf16[256,1536]{1,0:T(8,128)(2,1)S(1)}, u32[]{:S(2)}, u32[]{:S(2)}) %collective-permute-start.24) | collective-permute-done | bytes 786464 | tf_op jit(solution)/shard_map/ffn_forward/ppermute | solution.py:40
  217.7 7.9 %collective-permute-done.26 = bf16[128,1536]{1,0:T(8,128)(2,1)S(1)} collective-permute-done((bf16[128,1536]{1,0:T(8,128)(2,1)S(1)}, bf16[128,1536]{1,0:T(8,128)(2,1)S(1)}, u32[]{:S(2)}, u32[]{:S(2)}) %collective-permute-start.26) | collective-permute-done | bytes 393248 | tf_op jit(solution)/shard_map/ffn_forward/ppermute | solution.py:40
  230.5 6.3 %collective-permute-done.28 = bf16[128,1536]{1,0:T(8,128)(2,1)S(1)} collective-permute-done((bf16[128,1536]{1,0:T(8,128)(2,1)S(1)}, bf16[128,1536]{1,0:T(8,128)(2,1)S(1)}, u32[]{:S(2)}, u32[]{:S(2)}) %collective-permute-start.28) | collective-permute-done | bytes 393248 | tf_op jit(solution)/shard_map/ffn_backward/ppermute | solution.py:40
  241.1 12.4 %ffn_backward_beside.1 = (f32[512,1536]{1,0:T(8,128)S(1)}, bf16[512,1536]{1,0:T(8,128)(2,1)S(1)}, bf16[512,2048]{1,0:T(8,128)(2,1)S(1)}) custom-call(bf16[256,1536]{1,0:T(8,128)(2,1)S(1)} %pad_maximum_fusion.14.refs_0_, bf16[256,1536]{1,0:T(8,128)(2,1)S(1)} %pad_maximum_fusion.15.refs_1_, f32[512,1024]{1,0:T(8,128)S(1)} %get-tuple-element.210.refs_2_, ...), custom_call_target="tpu_custom_call" | custom-call | flops 1 | bytes 1 | tf_op jit(solution)/shard_map/ffn_backward/ffn_backward_beside/pallas_call | solution.py:788
  253.5 1.7 copy-done.5
  260.2 2.7 fusion.20
  264.2 2.7 fusion.23
  267.7 9.5 %products.2 = bf16[1536,2048]{1,0:T(8,128)(2,1)S(1)} custom-call(bf16[512,1536]{1,0:T(8,128)(2,1)S(1)} %get-tuple-element.221.refs_0_, bf16[256,1536]{1,0:T(8,128)(2,1)} %collective-permute-done.19.refs_1_, bf16[256,1536]{1,0:T(8,128)(2,1)} %collective-permute-done.20.refs_2_, bf16[512,2048]{1,0:T(8,128)(2,1)S(1)} %get-tuple-element.222.refs_3_, ...), custom_call_target="tpu_custom_call" | custom-call | flops 1 | bytes 1 | tf_op jit(solution)/shard_map/ffn_backward/products/pallas_call | solution.py:873
  277.2 2.7 copy-done.1
  279.8 2.3 collective-permute-done.32
  282.2 2.9 convert_add_fusion.2
  288.5 6.0 %products.3 = bf16[1024,1536]{1,0:T(8,128)(2,1)S(1)} custom-call(bf16[512,1024]{1,0:T(8,128)(2,1)S(1)} %copy-done.9, bf16[256,1024]{1,0:T(8,128)(2,1)S(1)} %multiply_convert_fusion.6.refs_1_, bf16[256,1024]{1,0:T(8,128)(2,1)S(1)} %multiply_convert_fusion.5.refs_2_, bf16[512,1536]{1,0:T(8,128)(2,1)S(1)} %copy-done.7, ...), custom_call_target="tpu_custom_call" | custom-call | flops 1 | bytes 1 | tf_op jit(solution)/shard_map/ffn_backward/products/pallas_call | solution.py:873
  294.5 1.6 copy-done.2
  299.2 3.9 fusion.39
  303.1 4.1 multiply_reduce_fusion
  307.3 1.6 fusion.135
  309.8 1.7 collective-permute-start.39
  311.5 3.8 fusion.26.d_ref
  318.8 14.1 %attention_backward.1.grads = bf16[256,3072]{1,0:T(8,128)(2,1)S(1)} custom-call(bf16[256,1536]{1,0:T(8,128)(2,1)S(1)} %fusion.26.d_ref, bf16[256,1536]{1,0:T(8,128)(2,1)S(1)} %copy-done.11, bf16[256,768]{1,0:T(8,128)(2,1)S(1)} %copy-done.16, bf16[256,768]{1,0:T(8,128)(2,1)S(1)} %copy-done.18, f32[128,768]{1,0:T(8,128)S(1)} %copy.107.cosine, ...), custom_call_target="tpu_custom_call" | custom-call | flops 1 | bytes 1 | tf_op jit(solution)/shard_map/attention_backward/attention_backward/pallas_call | solution.py:610
  333.0 3.6 convolution_convert_fusion
  343.0 9.5 %input_gradient.1 = (bf16[256,1536]{1,0:T(8,128)(2,1)}, f32[1,1536]{1,0:T(1,128)S(1)}) custom-call(bf16[256,3072]{1,0:T(8,128)(2,1)S(1)} %attention_backward.1.grads, bf16[1536,4736]{1,0:T(8,128)(2,1)} %bitcast.202, bf16[256,1536]{1,0:T(8,128)(2,1)S(1)} %copy-done.3, f32[256,1]{1,0:T(8,128)S(1)} %copy.111.inv_scale, f32[1,1536]{1,0:T(1,128)S(1)} %reshape.348.gain, ...), custom_call_target="tpu_custom_call" | custom-call | flops 1 | bytes 1 | tf_op jit(solution)/shard_map/input_gradient/input_gradient/pallas_call | solution.py:833
  353.8 2.5 add_convert_fusion
  362.3 3.1 collective-permute-done.50
  366.7 2.5 convert_add_fusion
  370.8 15.0 %collective-permute-done.47 = bf16[192,3072]{1,0:T(8,128)(2,1)} collective-permute-done((bf16[192,3072]{1,0:T(8,128)(2,1)}, bf16[192,3072]{1,0:T(8,128)(2,1)}, u32[]{:S(2)}, u32[]{:S(2)}) %collective-permute-start.47) | collective-permute-done | bytes 1179680 | tf_op jit(solution)/shard_map/q_k_v_weight_gradients/ppermute | solution.py:40
  391.1 3.1 collective-permute-start.54
  398.0 2.1 collective-permute-done.54
  400.1 5.5 %collective-permute-done.55 = bf16[48,1536]{1,0:T(8,128)(2,1)} collective-permute-done((bf16[48,1536]{1,0:T(8,128)(2,1)}, bf16[48,1536]{1,0:T(8,128)(2,1)}, u32[]{:S(2)}, u32[]{:S(2)}) %collective-permute-start.55) | collective-permute-done | bytes 147488 | tf_op jit(solution)/shard_map/q_k_v_weight_gradients/ppermute | solution.py:40
  406.8 2.4 fusion.36
  409.6 2.1 collective-permute-start.57
  413.7 1.6 collective-permute-start.64
  416.4 1.9 fusion.59
  419.2 2.4 collective-permute-done.61
  421.6 3.1 collective-permute-start.59
  425.8 8.5 %collective-permute-done.58 = bf16[48,3072]{1,0:T(8,128)(2,1)S(1)} collective-permute-done((bf16[48,3072]{1,0:T(8,128)(2,1)S(1)}, bf16[48,3072]{1,0:T(8,128)(2,1)S(1)}, u32[]{:S(2)}, u32[]{:S(2)}) %collective-permute-start.58) | collective-permute-done | bytes 294944 | tf_op jit(solution)/shard_map/weight_gradients_to_owners/ppermute | solution.py:40
  (364 shorter events, 124.9 us)
Async XLA Ops:
  7.2 164.4 %all-gather.2.cloned.1.call-start = ((), (), s32[]{:S(2)}) async-start(), calls=%async_computation.2 | async-start | bytes 10616832 | tf_op jit(solution)/shard_map/ffn_weights/all_gather | solution.py:114
  11.7 21.0 %collective-permute-start = (bf16[48,4736]{1,0:T(8,128)(2,1)S(1)}, bf16[48,4736]{1,0:T(8,128)(2,1)S(1)}, u32[]{:S(2)}, u32[]{:S(2)}) collective-permute-start(bf16[48,4736]{1,0:T(8,128)(2,1)S(1)} %packed.1), channel_id=1, source_target_pairs={{0,8},{1,9},{2,10},{3,11},{4,12},{5,13},{6,14},{7,15},{8,16},{9,17... | collective-permute-start | bytes 1363976 | tf_op jit(solution)/shard_map/phase_0/ppermute | solution.py:77
  16.6 16.0 %collective-permute-start.1 = (bf16[48,4736]{1,0:T(8,128)(2,1)S(1)}, bf16[48,4736]{1,0:T(8,128)(2,1)S(1)}, u32[]{:S(2)}, u32[]{:S(2)}) collective-permute-start(bf16[48,4736]{1,0:T(8,128)(2,1)S(1)} %packed.1), channel_id=1, source_target_pairs={{8,0},{9,1},{10,2},{11,3},{12,4},{13,5},{14,6},{15,7},{16,8},{17,9... | collective-permute-start | bytes 1363976 | tf_op jit(solution)/shard_map/phase_0/ppermute | solution.py:77
  20.1 21.0 %collective-permute-start.21 = (bf16[48,2048]{1,0:T(8,128)(2,1)S(1)}, bf16[48,2048]{1,0:T(8,128)(2,1)S(1)}, u32[]{:S(2)}, u32[]{:S(2)}) collective-permute-start(bf16[48,2048]{1,0:T(8,128)(2,1)S(1)} %get-tuple-element.178), channel_id=1, source_target_pairs={{0,2},{1,3},{2,0},{3,1},{4,6},{5,7},{6,4},{7,5},{8,10},{9,11},{10,... | collective-permute-start | bytes 589832 | tf_op jit(solution)/shard_map/phase_0/ppermute | solution.py:40
  21.6 23.5 %collective-permute-start.22 = (bf16[48,2048]{1,0:T(8,128)(2,1)S(1)}, bf16[48,2048]{1,0:T(8,128)(2,1)S(1)}, u32[]{:S(2)}, u32[]{:S(2)}) collective-permute-start(bf16[48,2048]{1,0:T(8,128)(2,1)S(1)} %get-tuple-element.179), channel_id=1, source_target_pairs={{0,4},{1,5},{2,6},{3,7},{4,0},{5,1},{6,2},{7,3},{8,12},{9,13},{10,... | collective-permute-start | bytes 589832 | tf_op jit(solution)/shard_map/phase_0/ppermute | solution.py:40
  33.7 19.2 %collective-permute-start.2 = (bf16[48,4736]{1,0:T(8,128)(2,1)S(1)}, bf16[48,4736]{1,0:T(8,128)(2,1)}, u32[]{:S(2)}, u32[]{:S(2)}) collective-permute-start(bf16[48,4736]{1,0:T(8,128)(2,1)S(1)} %packed.1), channel_id=1, source_target_pairs={{0,2},{1,3},{2,0},{3,1},{4,6},{5,7},{6,4},{7,5},{8,10},{9,11},{10,... | collective-permute-start | bytes 1363976 | tf_op jit(solution)/shard_map/phase_1/ppermute | solution.py:40
  34.2 21.3 %collective-permute-start.4 = (bf16[48,4736]{1,0:T(8,128)(2,1)S(1)}, bf16[48,4736]{1,0:T(8,128)(2,1)}, u32[]{:S(2)}, u32[]{:S(2)}) collective-permute-start(bf16[48,4736]{1,0:T(8,128)(2,1)S(1)} %packed.1), channel_id=1, source_target_pairs={{0,16},{1,17},{2,18},{3,19},{4,20},{5,21},{6,22},{7,23},{24,8},{25... | collective-permute-start | bytes 1363976 | tf_op jit(solution)/shard_map/phase_1/ppermute | solution.py:77
  40.6 15.0 %collective-permute-start.3 = (bf16[48,4736]{1,0:T(8,128)(2,1)}, bf16[48,4736]{1,0:T(8,128)(2,1)}, u32[]{:S(2)}, u32[]{:S(2)}) collective-permute-start(bf16[48,4736]{1,0:T(8,128)(2,1)} %get-tuple-element.147), channel_id=1, source_target_pairs={{0,4},{1,5},{2,6},{3,7},{4,0},{5,1},{6,2},{7,3},{8,12},{9,13},{10,... | collective-permute-start | bytes 1363976 | tf_op jit(solution)/shard_map/phase_1/ppermute | solution.py:40
  41.1 14.5 %collective-permute-start.5 = (bf16[48,4736]{1,0:T(8,128)(2,1)}, bf16[48,4736]{1,0:T(8,128)(2,1)}, u32[]{:S(2)}, u32[]{:S(2)}) collective-permute-start(bf16[48,4736]{1,0:T(8,128)(2,1)} %get-tuple-element.148), channel_id=1, source_target_pairs={{8,0},{9,1},{10,2},{11,3},{12,4},{13,5},{14,6},{15,7},{16,24},{17,... | collective-permute-start | bytes 1363976 | tf_op jit(solution)/shard_map/phase_1/ppermute | solution.py:77
  45.1 6.7 %collective-permute-start.23 = (bf16[48,2048]{1,0:T(8,128)(2,1)S(1)}, bf16[48,2048]{1,0:T(8,128)(2,1)S(1)}, u32[]{:S(2)}, u32[]{:S(2)}) collective-permute-start(bf16[48,2048]{1,0:T(8,128)(2,1)S(1)} %get-tuple-element.180), channel_id=1, source_target_pairs={{0,6},{1,7},{2,4},{3,5},{4,2},{5,3},{6,0},{7,1},{8,14},{9,15},{10,... | collective-permute-start | bytes 589832 | tf_op jit(solution)/shard_map/phase_0/ppermute | solution.py:40
  57.3 19.4 %collective-permute-start.6 = (bf16[2,48,4736]{2,1,0:T(8,128)(2,1)S(1)}, bf16[2,48,4736]{2,1,0:T(8,128)(2,1)S(1)}, u32[]{:S(2)}, u32[]{:S(2)}) collective-permute-start(bf16[2,48,4736]{2,1,0:T(8,128)(2,1)S(1)} %pad_maximum_fusion.8), channel_id=1, source_target_pairs={{0,4},{1,5},{2,6},{3,7},{4,0},{5,1},{6,2},{7,3},{8,12},{9,13},{10,... | collective-permute-start | bytes 2727944 | tf_op jit(solution)/shard_map/phase_2/ppermute | solution.py:40
  57.8 18.9 %collective-permute-start.7 = (bf16[2,48,4736]{2,1,0:T(8,128)(2,1)S(1)}, bf16[2,48,4736]{2,1,0:T(8,128)(2,1)S(1)}, u32[]{:S(2)}, u32[]{:S(2)}) collective-permute-start(bf16[2,48,4736]{2,1,0:T(8,128)(2,1)S(1)} %pad_maximum_fusion.9), channel_id=1, source_target_pairs={{0,2},{1,3},{2,0},{3,1},{4,6},{5,7},{6,4},{7,5},{8,10},{9,11},{10,... | collective-permute-start | bytes 2727944 | tf_op jit(solution)/shard_map/phase_2/ppermute | solution.py:40
  59.5 17.2 %collective-permute-start.9 = (bf16[2,2,48,4736]{3,2,1,0:T(8,128)(2,1)S(1)}, bf16[2,2,48,4736]{3,2,1,0:T(8,128)(2,1)S(1)}, u32[]{:S(2)}, u32[]{:S(2)}) collective-permute-start(bf16[2,2,48,4736]{3,2,1,0:T(8,128)(2,1)S(1)} %pad_maximum_fusion.1), channel_id=1, source_target_pairs={{0,1},{1,0},{2,3},{3,2},{4,5},{5,4},{6,7},{7,6},{8,9},{9,8},{10,11... | collective-permute-start | bytes 5455880 | tf_op jit(solution)/shard_map/phase_2/ppermute | solution.py:40
  59.6 14.9 %collective-permute-start.8 = (bf16[48,4736]{1,0:T(8,128)(2,1)}, bf16[48,4736]{1,0:T(8,128)(2,1)S(1)}, u32[]{:S(2)}, u32[]{:S(2)}) collective-permute-start(bf16[48,4736]{1,0:T(8,128)(2,1)} %collective-permute-done.4), channel_id=1, source_target_pairs={{8,0},{9,1},{10,2},{11,3},{12,4},{13,5},{14,6},{15,7},{16,24},{17,... | collective-permute-start | bytes 1363976 | tf_op jit(solution)/shard_map/phase_2/ppermute | solution.py:77
  77.8 14.5 %collective-permute-start.12 = (bf16[2,2,48,4736]{3,2,1,0:T(8,128)(2,1)S(1)}, bf16[2,2,48,4736]{3,2,1,0:T(8,128)(2,1)}, u32[]{:S(2)}, u32[]{:S(2)}) collective-permute-start(bf16[2,2,48,4736]{3,2,1,0:T(8,128)(2,1)S(1)} %pad_maximum_fusion.2), channel_id=1, source_target_pairs={{0,1},{1,0},{2,3},{3,2},{4,5},{5,4},{6,7},{7,6},{8,9},{9,8},{10,11... | collective-permute-start | bytes 5455880 | tf_op jit(solution)/shard_map/phase_3/ppermute | solution.py:40
  77.8 13.2 %collective-permute-start.10 = (bf16[48,4736]{1,0:T(8,128)(2,1)}, bf16[48,4736]{1,0:T(8,128)(2,1)}, u32[]{:S(2)}, u32[]{:S(2)}) collective-permute-start(bf16[48,4736]{1,0:T(8,128)(2,1)} %broadcast_select_fusion.1), channel_id=1, source_target_pairs={{0,2},{1,3},{2,0},{3,1},{4,6},{5,7},{6,4},{7,5},{8,10},{9,11},{10,... | collective-permute-start | bytes 1363976 | tf_op jit(solution)/shard_map/phase_3/ppermute | solution.py:40
  79.4 12.8 %collective-permute-start.11 = (bf16[48,4736]{1,0:T(8,128)(2,1)}, bf16[48,4736]{1,0:T(8,128)(2,1)}, u32[]{:S(2)}, u32[]{:S(2)}) collective-permute-start(bf16[48,4736]{1,0:T(8,128)(2,1)} %broadcast_select_fusion), channel_id=1, source_target_pairs={{0,4},{1,5},{2,6},{3,7},{4,0},{5,1},{6,2},{7,3},{8,12},{9,13},{10,... | collective-permute-start | bytes 1363976 | tf_op jit(solution)/shard_map/phase_3/ppermute | solution.py:40
  83.1 269.5 %reduce-scatter.3.cloned.1.call-start = ((), (), s32[]{:S(2)}) async-start(), calls=%async_computation.3 | async-start | bytes 7077888 | tf_op jit(solution)/shard_map/ffn_backward/reduce_scatter | solution.py:120
  94.9 21.5 %collective-permute-start.13 = (bf16[2,48,4736]{2,1,0:T(8,128)(2,1)S(1)}, bf16[2,48,4736]{2,1,0:T(8,128)(2,1)S(1)}, u32[]{:S(2)}, u32[]{:S(2)}) collective-permute-start(bf16[2,48,4736]{2,1,0:T(8,128)(2,1)S(1)} %pad_maximum_fusion.10), channel_id=1, source_target_pairs={{0,4},{1,5},{2,6},{3,7},{4,0},{5,1},{6,2},{7,3},{8,12},{9,13},{10,... | collective-permute-start | bytes 2727944 | tf_op jit(solution)/shard_map/phase_4/ppermute | solution.py:40
  96.6 21.2 %collective-permute-start.14 = (bf16[2,48,4736]{2,1,0:T(8,128)(2,1)S(1)}, bf16[2,48,4736]{2,1,0:T(8,128)(2,1)S(1)}, u32[]{:S(2)}, u32[]{:S(2)}) collective-permute-start(bf16[2,48,4736]{2,1,0:T(8,128)(2,1)S(1)} %pad_maximum_fusion.11), channel_id=1, source_target_pairs={{0,2},{1,3},{2,0},{3,1},{4,6},{5,7},{6,4},{7,5},{8,10},{9,11},{10,... | collective-permute-start | bytes 2727944 | tf_op jit(solution)/shard_map/phase_4/ppermute | solution.py:40
  97.4 20.4 %collective-permute-start.15 = (bf16[2,2,48,4736]{3,2,1,0:T(8,128)(2,1)S(1)}, bf16[2,2,48,4736]{3,2,1,0:T(8,128)(2,1)S(1)}, u32[]{:S(2)}, u32[]{:S(2)}) collective-permute-start(bf16[2,2,48,4736]{3,2,1,0:T(8,128)(2,1)S(1)} %pad_maximum_fusion.3), channel_id=1, source_target_pairs={{0,1},{1,0},{2,3},{3,2},{4,5},{5,4},{6,7},{7,6},{8,9},{9,8},{10,11... | collective-permute-start | bytes 5455880 | tf_op jit(solution)/shard_map/phase_4/ppermute | solution.py:40
  152.4 11.6 %collective-permute-start.17 = (bf16[128,1536]{1,0:T(8,128)(2,1)S(1)}, bf16[128,1536]{1,0:T(8,128)(2,1)S(1)}, u32[]{:S(2)}, u32[]{:S(2)}) collective-permute-start(bf16[128,1536]{1,0:T(8,128)(2,1)S(1)} %get-tuple-element.334), channel_id=1, source_target_pairs={{0,2},{1,3},{2,0},{3,1},{4,6},{5,7},{6,4},{7,5},{8,10},{9,11},{10,... | collective-permute-start | bytes 1179656 | tf_op jit(solution)/shard_map/ffn_forward/ppermute | solution.py:40
  153.2 11.2 %collective-permute-start.18 = (bf16[128,1536]{1,0:T(8,128)(2,1)S(1)}, bf16[128,1536]{1,0:T(8,128)(2,1)S(1)}, u32[]{:S(2)}, u32[]{:S(2)}) collective-permute-start(bf16[128,1536]{1,0:T(8,128)(2,1)S(1)} %get-tuple-element.333), channel_id=1, source_target_pairs={{0,4},{1,5},{2,6},{3,7},{4,0},{5,1},{6,2},{7,3},{8,12},{9,13},{10,... | collective-permute-start | bytes 1179656 | tf_op jit(solution)/shard_map/ffn_forward/ppermute | solution.py:40
  164.5 20.3 %collective-permute-start.19 = (bf16[256,1536]{1,0:T(8,128)(2,1)S(1)}, bf16[256,1536]{1,0:T(8,128)(2,1)}, u32[]{:S(2)}, u32[]{:S(2)}) collective-permute-start(bf16[256,1536]{1,0:T(8,128)(2,1)S(1)} %pad_maximum_fusion.12.refs_0_), channel_id=1, source_target_pairs={{0,4},{1,5},{2,6},{3,7},{4,0},{5,1},{6,2},{7,3},{8,12},{9,13},{10,... | collective-permute-start | bytes 2359304 | tf_op jit(solution)/shard_map/ffn_forward/ppermute | solution.py:40
  165.1 19.8 %collective-permute-start.20 = (bf16[256,1536]{1,0:T(8,128)(2,1)S(1)}, bf16[256,1536]{1,0:T(8,128)(2,1)}, u32[]{:S(2)}, u32[]{:S(2)}) collective-permute-start(bf16[256,1536]{1,0:T(8,128)(2,1)S(1)} %pad_maximum_fusion.13.refs_1_), channel_id=1, source_target_pairs={{0,2},{1,3},{2,0},{3,1},{4,6},{5,7},{6,4},{7,5},{8,10},{9,11},{10,... | collective-permute-start | bytes 2359304 | tf_op jit(solution)/shard_map/ffn_forward/ppermute | solution.py:40
  189.5 19.8 %collective-permute-start.25 = (bf16[256,1536]{1,0:T(8,128)(2,1)S(1)}, bf16[256,1536]{1,0:T(8,128)(2,1)S(1)}, u32[]{:S(2)}, u32[]{:S(2)}) collective-permute-start(bf16[256,1536]{1,0:T(8,128)(2,1)S(1)} %convolution_convert_fusion.2), channel_id=1, source_target_pairs={{0,2},{1,3},{2,0},{3,1},{4,6},{5,7},{6,4},{7,5},{8,10},{9,11},{10,... | collective-permute-start | bytes 2359304 | tf_op jit(solution)/shard_map/ffn_forward/ppermute | solution.py:40
  195.4 19.5 %collective-permute-start.24 = (bf16[256,1536]{1,0:T(8,128)(2,1)S(1)}, bf16[256,1536]{1,0:T(8,128)(2,1)S(1)}, u32[]{:S(2)}, u32[]{:S(2)}) collective-permute-start(bf16[256,1536]{1,0:T(8,128)(2,1)S(1)} %convolution_convert_fusion.3), channel_id=1, source_target_pairs={{0,4},{1,5},{2,6},{3,7},{4,0},{5,1},{6,2},{7,3},{8,12},{9,13},{10,... | collective-permute-start | bytes 2359304 | tf_op jit(solution)/shard_map/ffn_forward/ppermute | solution.py:40
  215.4 10.2 %collective-permute-start.26 = (bf16[128,1536]{1,0:T(8,128)(2,1)S(1)}, bf16[128,1536]{1,0:T(8,128)(2,1)S(1)}, u32[]{:S(2)}, u32[]{:S(2)}) collective-permute-start(bf16[128,1536]{1,0:T(8,128)(2,1)S(1)} %slice.642), channel_id=1, source_target_pairs={{0,2},{1,3},{2,0},{3,1},{4,6},{5,7},{6,4},{7,5},{8,10},{9,11},{10,... | collective-permute-start | bytes 1179656 | tf_op jit(solution)/shard_map/ffn_forward/ppermute | solution.py:40
  216.2 10.0 %collective-permute-start.27 = (bf16[128,1536]{1,0:T(8,128)(2,1)S(1)}, bf16[128,1536]{1,0:T(8,128)(2,1)S(1)}, u32[]{:S(2)}, u32[]{:S(2)}) collective-permute-start(bf16[128,1536]{1,0:T(8,128)(2,1)S(1)} %slice.641), channel_id=1, source_target_pairs={{0,4},{1,5},{2,6},{3,7},{4,0},{5,1},{6,2},{7,3},{8,12},{9,13},{10,... | collective-permute-start | bytes 1179656 | tf_op jit(solution)/shard_map/ffn_forward/ppermute | solution.py:40
  227.7 9.1 %collective-permute-start.28 = (bf16[128,1536]{1,0:T(8,128)(2,1)S(1)}, bf16[128,1536]{1,0:T(8,128)(2,1)S(1)}, u32[]{:S(2)}, u32[]{:S(2)}) collective-permute-start(bf16[128,1536]{1,0:T(8,128)(2,1)S(1)} %get-tuple-element.332), channel_id=1, source_target_pairs={{0,2},{1,3},{2,0},{3,1},{4,6},{5,7},{6,4},{7,5},{8,10},{9,11},{10,... | collective-permute-start | bytes 1179656 | tf_op jit(solution)/shard_map/ffn_backward/ppermute | solution.py:40
  229.0 9.1 %collective-permute-start.29 = (bf16[128,1536]{1,0:T(8,128)(2,1)S(1)}, bf16[128,1536]{1,0:T(8,128)(2,1)S(1)}, u32[]{:S(2)}, u32[]{:S(2)}) collective-permute-start(bf16[128,1536]{1,0:T(8,128)(2,1)S(1)} %get-tuple-element.331), channel_id=1, source_target_pairs={{0,4},{1,5},{2,6},{3,7},{4,0},{5,1},{6,2},{7,3},{8,12},{9,13},{10,... | collective-permute-start | bytes 1179656 | tf_op jit(solution)/shard_map/ffn_backward/ppermute | solution.py:40
  238.2 19.4 %collective-permute-start.30 = (bf16[256,1536]{1,0:T(8,128)(2,1)S(1)}, bf16[256,1536]{1,0:T(8,128)(2,1)S(1)}, u32[]{:S(2)}, u32[]{:S(2)}) collective-permute-start(bf16[256,1536]{1,0:T(8,128)(2,1)S(1)} %pad_maximum_fusion.14.refs_0_), channel_id=1, source_target_pairs={{0,4},{1,5},{2,6},{3,7},{4,0},{5,1},{6,2},{7,3},{8,12},{9,13},{10,... | collective-permute-start | bytes 2359304 | tf_op jit(solution)/shard_map/ffn_backward/ppermute | solution.py:40
  239.8 17.8 %collective-permute-start.31 = (bf16[256,1536]{1,0:T(8,128)(2,1)S(1)}, bf16[256,1536]{1,0:T(8,128)(2,1)S(1)}, u32[]{:S(2)}, u32[]{:S(2)}) collective-permute-start(bf16[256,1536]{1,0:T(8,128)(2,1)S(1)} %pad_maximum_fusion.15.refs_1_), channel_id=1, source_target_pairs={{0,2},{1,3},{2,0},{3,1},{4,6},{5,7},{6,4},{7,5},{8,10},{9,11},{10,... | collective-permute-start | bytes 2359304 | tf_op jit(solution)/shard_map/ffn_backward/ppermute | solution.py:40
  262.9 16.9 %collective-permute-start.33 = (bf16[256,1536]{1,0:T(8,128)(2,1)}, bf16[256,1536]{1,0:T(8,128)(2,1)}, u32[]{:S(2)}, u32[]{:S(2)}) collective-permute-start(bf16[256,1536]{1,0:T(8,128)(2,1)} %fusion.20), channel_id=1, source_target_pairs={{0,2},{1,3},{2,0},{3,1},{4,6},{5,7},{6,4},{7,5},{8,10},{9,11},{10,... | collective-permute-start | bytes 2359304 | tf_op jit(solution)/shard_map/ffn_backward/ppermute | solution.py:40
  267.0 15.2 %collective-permute-start.32 = (bf16[256,1536]{1,0:T(8,128)(2,1)}, bf16[256,1536]{1,0:T(8,128)(2,1)}, u32[]{:S(2)}, u32[]{:S(2)}) collective-permute-start(bf16[256,1536]{1,0:T(8,128)(2,1)} %fusion.23), channel_id=1, source_target_pairs={{0,4},{1,5},{2,6},{3,7},{4,0},{5,1},{6,2},{7,3},{8,12},{9,13},{10,... | collective-permute-start | bytes 2359304 | tf_op jit(solution)/shard_map/ffn_backward/ppermute | solution.py:40
  267.5 12.3 %collective-permute-start.34 = (f32[2,128]{1,0:T(2,128)S(1)}, f32[2,128]{1,0:T(2,128)S(1)}, u32[]{:S(2)}, u32[]{:S(2)}) collective-permute-start(f32[2,128]{1,0:T(2,128)S(1)} %broadcast_in_dim.15), channel_id=1, source_target_pairs={{0,1},{1,0},{2,3},{3,2},{4,5},{5,4},{6,7},{7,6},{8,9},{9,8},{10,11... | collective-permute-start | bytes 3080 | tf_op jit(solution)/shard_map/ffn_backward/ppermute | solution.py:40
  282.2 123.5 %reduce-scatter.5.cloned.1.call-start = ((), (), s32[]{:S(2)}) async-start(), calls=%async_computation.4 | async-start | bytes 3538944 | tf_op jit(solution)/shard_map/q_k_v_weight_gradients/reduce_scatter | solution.py:120
  286.0 10.1 %collective-permute-start.35 = (bf16[128,1536]{1,0:T(8,128)(2,1)}, bf16[128,1536]{1,0:T(8,128)(2,1)}, u32[]{:S(2)}, u32[]{:S(2)}) collective-permute-start(bf16[128,1536]{1,0:T(8,128)(2,1)} %slice.640), channel_id=1, source_target_pairs={{0,2},{1,3},{2,0},{3,1},{4,6},{5,7},{6,4},{7,5},{8,10},{9,11},{10,... | collective-permute-start | bytes 1179656 | tf_op jit(solution)/shard_map/ffn_backward/ppermute | solution.py:40
  287.7 9.1 %collective-permute-start.36 = (bf16[128,1536]{1,0:T(8,128)(2,1)}, bf16[128,1536]{1,0:T(8,128)(2,1)}, u32[]{:S(2)}, u32[]{:S(2)}) collective-permute-start(bf16[128,1536]{1,0:T(8,128)(2,1)} %slice.639), channel_id=1, source_target_pairs={{0,4},{1,5},{2,6},{3,7},{4,0},{5,1},{6,2},{7,3},{8,12},{9,13},{10,... | collective-permute-start | bytes 1179656 | tf_op jit(solution)/shard_map/ffn_backward/ppermute | solution.py:40
  288.4 7.7 %collective-permute-start.37 = (f32[2,128]{1,0:T(2,128)S(1)}, f32[2,128]{1,0:T(2,128)S(1)}, u32[]{:S(2)}, u32[]{:S(2)}) collective-permute-start(f32[2,128]{1,0:T(2,128)S(1)} %add.500), channel_id=1, source_target_pairs={{0,8},{1,9},{2,10},{3,11},{4,12},{5,13},{6,14},{7,15},{8,0},{9,1},... | collective-permute-start | bytes 3080 | tf_op jit(solution)/shard_map/ffn_backward/ppermute | solution.py:40
  309.7 5.6 %collective-permute-start.38 = (bf16[768,1536]{1,0:T(8,128)(2,1)S(1)}, bf16[768,1536]{1,0:T(8,128)(2,1)S(1)}, u32[]{:S(2)}, u32[]{:S(2)}) collective-permute-start(bf16[768,1536]{1,0:T(8,128)(2,1)S(1)} %convolution_convert_fusion.1), channel_id=1, source_target_pairs={{0,1},{1,0},{2,3},{3,2},{4,5},{5,4},{6,7},{7,6},{8,9},{9,8},{10,11... | collective-permute-start | bytes 7077896 | tf_op jit(solution)/shard_map/attention_backward/ppermute | solution.py:40
  309.8 5.5 %collective-permute-start.39 = (f32[2,128]{1,0:T(2,128)S(1)}, f32[2,128]{1,0:T(2,128)S(1)}, u32[]{:S(2)}, u32[]{:S(2)}) collective-permute-start(f32[2,128]{1,0:T(2,128)S(1)} %add.505), channel_id=1, source_target_pairs={{0,16},{1,17},{2,18},{3,19},{4,20},{5,21},{6,22},{7,23},{8,24},{9,... | collective-permute-start | bytes 3080 | tf_op jit(solution)/shard_map/attention_backward/ppermute | solution.py:40
  315.9 17.0 %collective-permute-start.40 = (bf16[192,1536]{1,0:T(8,128)(2,1)S(1)}, bf16[192,1536]{1,0:T(8,128)(2,1)S(1)}, u32[]{:S(2)}, u32[]{:S(2)}) collective-permute-start(bf16[192,1536]{1,0:T(8,128)(2,1)S(1)} %get-tuple-element.317), channel_id=1, source_target_pairs={{0,4},{1,5},{2,6},{3,7},{4,0},{5,1},{6,2},{7,3},{8,12},{9,13},{10,... | collective-permute-start | bytes 1769480 | tf_op jit(solution)/shard_map/attention_backward/ppermute | solution.py:40
  316.8 16.2 %collective-permute-start.41 = (bf16[192,1536]{1,0:T(8,128)(2,1)S(1)}, bf16[192,1536]{1,0:T(8,128)(2,1)S(1)}, u32[]{:S(2)}, u32[]{:S(2)}) collective-permute-start(bf16[192,1536]{1,0:T(8,128)(2,1)S(1)} %get-tuple-element.316), channel_id=1, source_target_pairs={{0,2},{1,3},{2,0},{3,1},{4,6},{5,7},{6,4},{7,5},{8,10},{9,11},{10,... | collective-permute-start | bytes 1769480 | tf_op jit(solution)/shard_map/attention_backward/ppermute | solution.py:40
  318.0 15.0 %collective-permute-start.42 = (f32[2,128]{1,0:T(2,128)S(1)}, f32[2,128]{1,0:T(2,128)S(1)}, u32[]{:S(2)}, u32[]{:S(2)}) collective-permute-start(f32[2,128]{1,0:T(2,128)S(1)} %add.507), channel_id=1, source_target_pairs={{0,2},{1,3},{2,0},{3,1},{4,6},{5,7},{6,4},{7,5},{8,10},{9,11},{10,... | collective-permute-start | bytes 3080 | tf_op jit(solution)/shard_map/attention_backward/ppermute | solution.py:40
  336.6 15.9 %collective-permute-start.43 = (bf16[768,3072]{1,0:T(8,128)(2,1)}, bf16[768,3072]{1,0:T(8,128)(2,1)}, u32[]{:S(2)}, u32[]{:S(2)}) collective-permute-start(bf16[768,3072]{1,0:T(8,128)(2,1)} %convolution_convert_fusion), channel_id=1, source_target_pairs={{0,1},{1,0},{2,3},{3,2},{4,5},{5,4},{6,7},{7,6},{8,9},{9,8},{10,11... | collective-permute-start | bytes 14155784 | tf_op jit(solution)/shard_map/q_k_v_weight_gradients/ppermute | solution.py:40
  338.1 14.4 %collective-permute-start.45 = (bf16[96,1536]{1,0:T(8,128)(2,1)}, bf16[96,1536]{1,0:T(8,128)(2,1)S(1)}, u32[]{:S(2)}, u32[]{:S(2)}) collective-permute-start(bf16[96,1536]{1,0:T(8,128)(2,1)} %get-tuple-element.308), channel_id=1, source_target_pairs={{0,2},{1,3},{2,0},{3,1},{4,6},{5,7},{6,4},{7,5},{8,10},{9,11},{10,... | collective-permute-start | bytes 884744 | tf_op jit(solution)/shard_map/attention_backward/ppermute | solution.py:40
  339.3 13.3 %collective-permute-start.46 = (bf16[96,1536]{1,0:T(8,128)(2,1)S(1)}, bf16[96,1536]{1,0:T(8,128)(2,1)S(1)}, u32[]{:S(2)}, u32[]{:S(2)}) collective-permute-start(bf16[96,1536]{1,0:T(8,128)(2,1)S(1)} %get-tuple-element.307), channel_id=1, source_target_pairs={{0,4},{1,5},{2,6},{3,7},{4,0},{5,1},{6,2},{7,3},{8,12},{9,13},{10,... | collective-permute-start | bytes 884744 | tf_op jit(solution)/shard_map/attention_backward/ppermute | solution.py:40
  340.1 12.4 %collective-permute-start.44 = (f32[2,128]{1,0:T(2,128)S(1)}, f32[2,128]{1,0:T(2,128)S(1)}, u32[]{:S(2)}, u32[]{:S(2)}) collective-permute-start(f32[2,128]{1,0:T(2,128)S(1)} %add.508), channel_id=1, source_target_pairs={{0,4},{1,5},{2,6},{3,7},{4,0},{5,1},{6,2},{7,3},{8,12},{9,13},{10,... | collective-permute-start | bytes 3080 | tf_op jit(solution)/shard_map/q_k_v_weight_gradients/ppermute | solution.py:40
  357.9 27.8 %collective-permute-start.47 = (bf16[192,3072]{1,0:T(8,128)(2,1)}, bf16[192,3072]{1,0:T(8,128)(2,1)}, u32[]{:S(2)}, u32[]{:S(2)}) collective-permute-start(bf16[192,3072]{1,0:T(8,128)(2,1)} %get-tuple-element.306), channel_id=1, source_target_pairs={{0,4},{1,5},{2,6},{3,7},{4,0},{5,1},{6,2},{7,3},{8,12},{9,13},{10,... | collective-permute-start | bytes 3538952 | tf_op jit(solution)/shard_map/q_k_v_weight_gradients/ppermute | solution.py:40
  358.5 27.7 %collective-permute-start.48 = (bf16[192,3072]{1,0:T(8,128)(2,1)}, bf16[192,3072]{1,0:T(8,128)(2,1)}, u32[]{:S(2)}, u32[]{:S(2)}) collective-permute-start(bf16[192,3072]{1,0:T(8,128)(2,1)} %get-tuple-element.305), channel_id=1, source_target_pairs={{0,2},{1,3},{2,0},{3,1},{4,6},{5,7},{6,4},{7,5},{8,10},{9,11},{10,... | collective-permute-start | bytes 3538952 | tf_op jit(solution)/shard_map/q_k_v_weight_gradients/ppermute | solution.py:40
  387.8 17.9 %collective-permute-start.52 = (bf16[96,3072]{1,0:T(8,128)(2,1)S(1)}, bf16[96,3072]{1,0:T(8,128)(2,1)S(1)}, u32[]{:S(2)}, u32[]{:S(2)}) collective-permute-start(bf16[96,3072]{1,0:T(8,128)(2,1)S(1)} %get-tuple-element.290), channel_id=1, source_target_pairs={{0,2},{1,3},{2,0},{3,1},{4,6},{5,7},{6,4},{7,5},{8,10},{9,11},{10,... | collective-permute-start | bytes 1769480 | tf_op jit(solution)/shard_map/weight_gradients_to_owners/ppermute | solution.py:40
  389.2 16.4 %collective-permute-start.53 = (bf16[96,3072]{1,0:T(8,128)(2,1)S(1)}, bf16[96,3072]{1,0:T(8,128)(2,1)S(1)}, u32[]{:S(2)}, u32[]{:S(2)}) collective-permute-start(bf16[96,3072]{1,0:T(8,128)(2,1)S(1)} %get-tuple-element.289), channel_id=1, source_target_pairs={{0,4},{1,5},{2,6},{3,7},{4,0},{5,1},{6,2},{7,3},{8,12},{9,13},{10,... | collective-permute-start | bytes 1769480 | tf_op jit(solution)/shard_map/weight_gradients_to_owners/ppermute | solution.py:40
  391.1 9.0 %collective-permute-start.54 = (bf16[48,1536]{1,0:T(8,128)(2,1)}, bf16[48,1536]{1,0:T(8,128)(2,1)}, u32[]{:S(2)}, u32[]{:S(2)}) collective-permute-start(bf16[48,1536]{1,0:T(8,128)(2,1)} %get-tuple-element.314), channel_id=1, source_target_pairs={{0,24},{1,25},{2,26},{3,27},{4,28},{5,29},{6,30},{7,31},{8,16},{9,... | collective-permute-start | bytes 442376 | tf_op jit(solution)/shard_map/q_k_v_weight_gradients/ppermute | solution.py:40
  394.2 11.4 %collective-permute-start.55 = (bf16[48,1536]{1,0:T(8,128)(2,1)}, bf16[48,1536]{1,0:T(8,128)(2,1)}, u32[]{:S(2)}, u32[]{:S(2)}) collective-permute-start(bf16[48,1536]{1,0:T(8,128)(2,1)} %get-tuple-element.315), channel_id=1, source_target_pairs={{0,16},{1,17},{2,18},{3,19},{4,20},{5,21},{6,22},{7,23},{8,24},{9,... | collective-permute-start | bytes 442376 | tf_op jit(solution)/shard_map/q_k_v_weight_gradients/ppermute | solution.py:40
  394.2 11.4 %collective-permute-start.56 = (bf16[48,1536]{1,0:T(8,128)(2,1)}, bf16[48,1536]{1,0:T(8,128)(2,1)}, u32[]{:S(2)}, u32[]{:S(2)}) collective-permute-start(bf16[48,1536]{1,0:T(8,128)(2,1)} %get-tuple-element.313), channel_id=1, source_target_pairs={{0,8},{1,9},{2,10},{3,11},{4,12},{5,13},{6,14},{7,15},{8,0},{9,1},... | collective-permute-start | bytes 442376 | tf_op jit(solution)/shard_map/q_k_v_weight_gradients/ppermute | solution.py:40
  405.7 6.1 %collective-permute-start.60 = (f32[2,1536]{1,0:T(2,128)S(1)}, f32[2,1536]{1,0:T(2,128)S(1)}, u32[]{:S(2)}, u32[]{:S(2)}) collective-permute-start(f32[2,1536]{1,0:T(2,128)S(1)} %add.517), channel_id=1, source_target_pairs={{0,2},{1,3},{2,0},{3,1},{4,6},{5,7},{6,4},{7,5},{8,10},{9,11},{10,... | collective-permute-start | bytes 36872 | tf_op jit(solution)/shard_map/weight_gradients_to_owners/ppermute | solution.py:40
  409.6 16.2 %collective-permute-start.57 = (bf16[48,3072]{1,0:T(8,128)(2,1)S(1)}, bf16[48,3072]{1,0:T(8,128)(2,1)S(1)}, u32[]{:S(2)}, u32[]{:S(2)}) collective-permute-start(bf16[48,3072]{1,0:T(8,128)(2,1)S(1)} %get-tuple-element.300), channel_id=1, source_target_pairs={{0,24},{1,25},{2,26},{3,27},{4,28},{5,29},{6,30},{7,31},{8,16},{9,... | collective-permute-start | bytes 884744 | tf_op jit(solution)/shard_map/weight_gradients_to_owners/ppermute | solution.py:40
  411.8 9.9 %collective-permute-start.62 = (bf16[48,2048]{1,0:T(8,128)(2,1)S(1)}, bf16[48,2048]{1,0:T(8,128)(2,1)S(1)}, u32[]{:S(2)}, u32[]{:S(2)}) collective-permute-start(bf16[48,2048]{1,0:T(8,128)(2,1)S(1)} %get-tuple-element.330), channel_id=1, source_target_pairs={{0,2},{1,3},{2,0},{3,1},{4,6},{5,7},{6,4},{7,5},{8,10},{9,11},{10,... | collective-permute-start | bytes 589832 | tf_op jit(solution)/shard_map/weight_gradients_to_owners/ppermute | solution.py:40
  412.6 12.1 %collective-permute-start.63 = (bf16[48,2048]{1,0:T(8,128)(2,1)S(1)}, bf16[48,2048]{1,0:T(8,128)(2,1)S(1)}, u32[]{:S(2)}, u32[]{:S(2)}) collective-permute-start(bf16[48,2048]{1,0:T(8,128)(2,1)S(1)} %get-tuple-element.329), channel_id=1, source_target_pairs={{0,4},{1,5},{2,6},{3,7},{4,0},{5,1},{6,2},{7,3},{8,12},{9,13},{10,... | collective-permute-start | bytes 589832 | tf_op jit(solution)/shard_map/weight_gradients_to_owners/ppermute | solution.py:40
  413.7 11.0 %collective-permute-start.64 = (bf16[48,2048]{1,0:T(8,128)(2,1)S(1)}, bf16[48,2048]{1,0:T(8,128)(2,1)S(1)}, u32[]{:S(2)}, u32[]{:S(2)}) collective-permute-start(bf16[48,2048]{1,0:T(8,128)(2,1)S(1)} %get-tuple-element.328), channel_id=1, source_target_pairs={{0,6},{1,7},{2,4},{3,5},{4,2},{5,3},{6,0},{7,1},{8,14},{9,15},{10,... | collective-permute-start | bytes 589832 | tf_op jit(solution)/shard_map/weight_gradients_to_owners/ppermute | solution.py:40
  415.3 6.3 %collective-permute-start.61 = (f32[2,1536]{1,0:T(2,128)S(1)}, f32[2,1536]{1,0:T(2,128)S(1)}, u32[]{:S(2)}, u32[]{:S(2)}) collective-permute-start(f32[2,1536]{1,0:T(2,128)S(1)} %add.538), channel_id=1, source_target_pairs={{0,4},{1,5},{2,6},{3,7},{4,0},{5,1},{6,2},{7,3},{8,12},{9,13},{10,... | collective-permute-start | bytes 36872 | tf_op jit(solution)/shard_map/weight_gradients_to_owners/ppermute | solution.py:40
  421.6 12.6 %collective-permute-start.58 = (bf16[48,3072]{1,0:T(8,128)(2,1)S(1)}, bf16[48,3072]{1,0:T(8,128)(2,1)S(1)}, u32[]{:S(2)}, u32[]{:S(2)}) collective-permute-start(bf16[48,3072]{1,0:T(8,128)(2,1)S(1)} %get-tuple-element.302), channel_id=1, source_target_pairs={{0,16},{1,17},{2,18},{3,19},{4,20},{5,21},{6,22},{7,23},{8,24},{9,... | collective-permute-start | bytes 884744 | tf_op jit(solution)/shard_map/weight_gradients_to_owners/ppermute | solution.py:40
  421.6 12.6 %collective-permute-start.59 = (bf16[48,3072]{1,0:T(8,128)(2,1)S(1)}, bf16[48,3072]{1,0:T(8,128)(2,1)S(1)}, u32[]{:S(2)}, u32[]{:S(2)}) collective-permute-start(bf16[48,3072]{1,0:T(8,128)(2,1)S(1)} %get-tuple-element.301), channel_id=1, source_target_pairs={{0,8},{1,9},{2,10},{3,11},{4,12},{5,13},{6,14},{7,15},{8,0},{9,1},... | collective-permute-start | bytes 884744 | tf_op jit(solution)/shard_map/weight_gradients_to_owners/ppermute | solution.py:40
  (68 other events, 417.0 us)
Sparse Core Ops, SparseCore 0:
  83.2 88.2 all-gather.1
  282.3 67.3 reduce-scatter.2
  352.8 40.2 reduce-scatter.4

commit v11 on v10

--- a/solution.py
+++ b/solution.py
@@ -401,12 +401,14 @@
     two = far[0].shape[0]
     one = two // 2
     came_a, came_b, *beside = tied(swap(far[0], 4), swap(far[1], 2), *beside)
-    a = near[:two] + came_a.astype(F32)
-    b = near[two:] + came_b.astype(F32)
-    came_a, came_b, *beside = tied(
-        swap(a[one:].astype(BF), 2), swap(b[one:].astype(BF), 4), *later(*beside)
+    send_a = near[one:two] + came_a[one:].astype(F32)
+    send_b = near[two + one :] + came_b[one:].astype(F32)
+    own_a, own_b, *beside = tied(
+        swap(send_a.astype(BF), 2), swap(send_b.astype(BF), 4), *later(*beside)
     )
-    own = jnp.concatenate([a[:one] + came_a.astype(F32), b[:one] + came_b.astype(F32)])
+    own_a = near[:one] + came_a[:one].astype(F32) + own_a.astype(F32)
+    own_b = near[two : two + one] + came_b[:one].astype(F32) + own_b.astype(F32)
+    own = jnp.concatenate([own_a, own_b])
     return (own, *beside)
 
 

time: 451 us -> 448 us (level)
    unnamed x143 -> x141, local copies, waits for them, and re-layouts: 19.4 us -> 20 us
where the time goes in v11:
time: 448 us; the launch traced here: 441 us
  waiting for transfers between devices  130 us (29%)
  starting transfers between devices  76.5 us (17%)
  Pallas kernels  76.1 us (17%)
  matrix products  51.6 us (12%)
  local copies, waits for them, and re-layouts  45.3 us (10%)
  other arithmetic  43.7 us (10%)
  between operations  18.1 us (4%)
    ppermute x60, waiting for transfers between devices, swap(): return lax.ppermute(value, 'dp', [(i, i ^ mask) for i in range(n)])  114 us
    ppermute x60, starting transfers between devices, swap(): return lax.ppermute(value, 'dp', [(i, i ^ mask) for i in range(n)])  60.9 us
    dot_general x22, matrix products, dot(): return lax.dot_general(a, b, (dims, ((), ())), preferred_element_type=F32)  51.6 us
    unnamed x141, local copies, waits for them, and re-layouts  20 us
    dynamic_update_slice x16, local copies, waits for them, and re-layouts, place(): return lax.dynamic_update_slice(out, piece, where)  18.5 us
    pallas_call x2, Pallas kernels, products(): pl.pallas_call(kernel, grid=(columns // tile,), out_shape=jax.ShapeDtypeS...  15.4 us
    ppermute x5, starting transfers between devices, along_z(): lax.ppermute(value, 'dp', [(8 * a + i, 8 * b + i) for a, b in pairs for i...  15.3 us
    pallas_call x1, Pallas kernels, attention_backward(): pl.pallas_call(kernel, grid=(count // SEQ, steps), out_shape=jax.ShapeDty...  14.1 us
  transfers between devices with their start and end apart: 68, of which 29 were waited for; matrix products, arithmetic and copies ran while one was open for 24% of the time, Pallas kernels for 17%

profile of v11, /device:TPU:0, one launch (start us, length us, event | category | flops | bytes accessed | tf_op | source)
XLA Modules:
  0.0 440.9 jit_solution(12026394564628892191)
XLA Ops:
  11.7 5.0 %collective-permute-start = (bf16[48,4736]{1,0:T(8,128)(2,1)S(1)}, bf16[48,4736]{1,0:T(8,128)(2,1)S(1)}, u32[]{:S(2)}, u32[]{:S(2)}) collective-permute-start(bf16[48,4736]{1,0:T(8,128)(2,1)S(1)} %packed.1), channel_id=1, source_target_pairs={{0,8},{1,9},{2,10},{3,11},{4,12},{5,13},{6,14},{7,15},{8,16},{9,17... | collective-permute-start | bytes 1363976 | tf_op jit(solution)/shard_map/phase_0/ppermute | solution.py:77
  24.1 4.2 fusion.3
  28.3 4.3 fusion.2
  34.2 6.3 %collective-permute-start.4 = (bf16[48,4736]{1,0:T(8,128)(2,1)S(1)}, bf16[48,4736]{1,0:T(8,128)(2,1)}, u32[]{:S(2)}, u32[]{:S(2)}) collective-permute-start(bf16[48,4736]{1,0:T(8,128)(2,1)S(1)} %packed.1), channel_id=1, source_target_pairs={{0,16},{1,17},{2,18},{3,19},{4,20},{5,21},{6,22},{7,23},{24,8},{25... | collective-permute-start | bytes 1363976 | tf_op jit(solution)/shard_map/phase_1/ppermute | solution.py:77
  45.1 2.5 collective-permute-start.23
  47.6 4.2 collective-permute-done.23.refs_3_
  52.9 2.6 collective-permute-done.3
  63.1 1.8 broadcast_select_fusion.1
  64.9 9.6 %collective-permute-done.8 = bf16[48,4736]{1,0:T(8,128)(2,1)S(1)} collective-permute-done((bf16[48,4736]{1,0:T(8,128)(2,1)}, bf16[48,4736]{1,0:T(8,128)(2,1)S(1)}, u32[]{:S(2)}, u32[]{:S(2)}) %collective-permute-start.8) | collective-permute-done | bytes 454688 | tf_op jit(solution)/shard_map/phase_2/ppermute | solution.py:77
  74.5 2.1 collective-permute-done.6
  79.4 1.7 collective-permute-start.11
  85.4 5.6 %collective-permute-done.10 = bf16[48,4736]{1,0:T(8,128)(2,1)} collective-permute-done((bf16[48,4736]{1,0:T(8,128)(2,1)}, bf16[48,4736]{1,0:T(8,128)(2,1)}, u32[]{:S(2)}, u32[]{:S(2)}) %collective-permute-start.10) | collective-permute-done | bytes 454688 | tf_op jit(solution)/shard_map/phase_3/ppermute | solution.py:40
  94.9 1.7 collective-permute-start.13
  97.5 2.2 bitcast_dynamic-update-slice_fusion.7
  99.7 2.2 bitcast_dynamic-update-slice_fusion.6
  103.8 12.6 %collective-permute-done.13 = bf16[2,48,4736]{2,1,0:T(8,128)(2,1)S(1)} collective-permute-done((bf16[2,48,4736]{2,1,0:T(8,128)(2,1)S(1)}, bf16[2,48,4736]{2,1,0:T(8,128)(2,1)S(1)}, u32[]{:S(2)}, u32[]{:S(2)}) %collective-permute-start.13) | collective-permute-done | bytes 909344 | tf_op jit(solution)/shard_map/phase_4/ppermute | solution.py:40
  126.0 5.6 %fusion.q_raw.k_raw.v_raw = f32[256,3072]{1,0:T(8,128)S(1)} fusion(bf16[256,1536]{1,0:T(8,128)(2,1)S(1)} %fusion.31, bf16[1536,4736]{1,0:T(8,128)(2,1)} %bitcast.199), kind=kOutput, calls=%fused_computation | convolution fusion | flops 2415919104 | bytes 13369344 | tf_op jit(solution)/shard_map/attention_forward/dot_general | solution.py:23
  131.6 12.6 %attention_forward.1 = (bf16[256,1536]{1,0:T(8,128)(2,1)S(1)}, bf16[256,768]{1,0:T(8,128)(2,1)S(1)}, bf16[256,768]{1,0:T(8,128)(2,1)S(1)}, bf16[256,1536]{1,0:T(8,128)(2,1)S(1)}) custom-call(f32[256,3072]{1,0:T(8,128)S(1)} %fusion.q_raw.k_raw.v_raw, f32[256,3072]{1,0:T(8,128)S(1)} %fusion.q_raw.k_raw.v_raw, f32[256,3072]{1,0:T(8,128)S(1)} %fusion.q_raw.k_raw.v_raw, ...), custom_call_target="tpu_custom_call" | custom-call | flops 1 | bytes 1 | tf_op jit(solution)/shard_map/attention_forward/attention_forward/pallas_call | solution.py:540
  146.6 4.1 multiply_reduce_fusion.3
  153.6 10.3 %collective-permute-done.17 = bf16[128,1536]{1,0:T(8,128)(2,1)S(1)} collective-permute-done((bf16[128,1536]{1,0:T(8,128)(2,1)S(1)}, bf16[128,1536]{1,0:T(8,128)(2,1)S(1)}, u32[]{:S(2)}, u32[]{:S(2)}) %collective-permute-start.17) | collective-permute-done | bytes 393248 | tf_op jit(solution)/shard_map/ffn_forward/ppermute | solution.py:40
  166.2 5.4 %all-gather.2.cloned.1.call-done.ref.refs_2_.refs_3_.refs_4_.refs_5_ = bf16[1536,3072]{1,0:T(8,128)(2,1)} async-done(((bf16[192,3072]{1,0:T(8,128)(2,1)}), bf16[1536,3072]{1,0:T(8,128)(2,1)}) %all-gather.2.cloned.1.call-update) | async-done | bytes 9437200 | tf_op jit(solution)/shard_map/ffn_weights/all_gather | solution.py:114
  171.6 2.2 w_down_from.1.refs_4_.refs_6_
  173.8 2.5 copy-done
  176.3 8.6 %ffn_forward_beside.1 = (f32[512,1536]{1,0:T(8,128)S(1)}, bf16[512,1536]{1,0:T(8,128)(2,1)S(1)}, bf16[512,1024]{1,0:T(8,128)(2,1)S(1)}, f32[512,1024]{1,0:T(8,128)S(1)}, f32[512,1024]{1,0:T(8,128)S(1)}) custom-call(bf16[256,1536]{1,0:T(8,128)(2,1)S(1)} %pad_maximum_fusion.12.refs_0_, bf16[256,1536]{1,0:T(8,128)(2,1)S(1)} %pad_maximum_fusion.13.refs_1_, ...), custom_call_target="tpu_custom_call" | custom-call | flops 1 | bytes 1 | tf_op jit(solution)/shard_map/ffn_forward/ffn_forward_beside/pallas_call | solution.py:725
  184.9 3.3 fusion.12
  189.6 1.6 collective-permute-start.25
  191.1 2.9 fusion.14
  196.9 2.3 convolution_convert_fusion.4
  199.2 2.3 convolution_convert_fusion.5
  201.5 7.8 %collective-permute-done.25 = bf16[256,1536]{1,0:T(8,128)(2,1)S(1)} collective-permute-done((bf16[256,1536]{1,0:T(8,128)(2,1)S(1)}, bf16[256,1536]{1,0:T(8,128)(2,1)S(1)}, u32[]{:S(2)}, u32[]{:S(2)}) %collective-permute-start.25) | collective-permute-done | bytes 786464 | tf_op jit(solution)/shard_map/ffn_forward/ppermute | solution.py:40
  209.3 5.6 %collective-permute-done.24 = bf16[256,1536]{1,0:T(8,128)(2,1)S(1)} collective-permute-done((bf16[256,1536]{1,0:T(8,128)(2,1)S(1)}, bf16[256,1536]{1,0:T(8,128)(2,1)S(1)}, u32[]{:S(2)}, u32[]{:S(2)}) %collective-permute-start.24) | collective-permute-done | bytes 786464 | tf_op jit(solution)/shard_map/ffn_forward/ppermute | solution.py:40
  217.3 8.0 %collective-permute-done.26 = bf16[128,1536]{1,0:T(8,128)(2,1)S(1)} collective-permute-done((bf16[128,1536]{1,0:T(8,128)(2,1)S(1)}, bf16[128,1536]{1,0:T(8,128)(2,1)S(1)}, u32[]{:S(2)}, u32[]{:S(2)}) %collective-permute-start.26) | collective-permute-done | bytes 393248 | tf_op jit(solution)/shard_map/ffn_forward/ppermute | solution.py:40
  230.2 6.3 %collective-permute-done.28 = bf16[128,1536]{1,0:T(8,128)(2,1)S(1)} collective-permute-done((bf16[128,1536]{1,0:T(8,128)(2,1)S(1)}, bf16[128,1536]{1,0:T(8,128)(2,1)S(1)}, u32[]{:S(2)}, u32[]{:S(2)}) %collective-permute-start.28) | collective-permute-done | bytes 393248 | tf_op jit(solution)/shard_map/ffn_backward/ppermute | solution.py:40
  240.8 12.4 %ffn_backward_beside.1 = (f32[512,1536]{1,0:T(8,128)S(1)}, bf16[512,1536]{1,0:T(8,128)(2,1)S(1)}, bf16[512,2048]{1,0:T(8,128)(2,1)S(1)}) custom-call(bf16[256,1536]{1,0:T(8,128)(2,1)S(1)} %pad_maximum_fusion.14.refs_0_, bf16[256,1536]{1,0:T(8,128)(2,1)S(1)} %pad_maximum_fusion.15.refs_1_, f32[512,1024]{1,0:T(8,128)S(1)} %get-tuple-element.210.refs_2_, ...), custom_call_target="tpu_custom_call" | custom-call | flops 1 | bytes 1 | tf_op jit(solution)/shard_map/ffn_backward/ffn_backward_beside/pallas_call | solution.py:790
  253.2 1.7 copy-done.5
  260.0 2.7 fusion.23
  263.3 2.7 fusion.20
  267.4 9.5 %products.2 = bf16[1536,2048]{1,0:T(8,128)(2,1)S(1)} custom-call(bf16[512,1536]{1,0:T(8,128)(2,1)S(1)} %get-tuple-element.221.refs_0_, bf16[256,1536]{1,0:T(8,128)(2,1)} %collective-permute-done.19.refs_1_, bf16[256,1536]{1,0:T(8,128)(2,1)} %collective-permute-done.20.refs_2_, bf16[512,2048]{1,0:T(8,128)(2,1)S(1)} %get-tuple-element.222.refs_3_, ...), custom_call_target="tpu_custom_call" | custom-call | flops 1 | bytes 1 | tf_op jit(solution)/shard_map/ffn_backward/products/pallas_call | solution.py:875
  276.9 2.6 copy-done.1
  279.5 1.9 collective-permute-done.33
  281.5 2.8 add_convert_fusion.1
  287.9 5.9 %products.3 = bf16[1024,1536]{1,0:T(8,128)(2,1)S(1)} custom-call(bf16[512,1024]{1,0:T(8,128)(2,1)S(1)} %copy-done.9, bf16[256,1024]{1,0:T(8,128)(2,1)S(1)} %multiply_convert_fusion.6.refs_1_, bf16[256,1024]{1,0:T(8,128)(2,1)S(1)} %multiply_convert_fusion.5.refs_2_, bf16[512,1536]{1,0:T(8,128)(2,1)S(1)} %copy-done.7, ...), custom_call_target="tpu_custom_call" | custom-call | flops 1 | bytes 1 | tf_op jit(solution)/shard_map/ffn_backward/products/pallas_call | solution.py:875
  293.9 1.6 copy-done.2
  295.5 2.3 convert_add_fusion.2
  297.9 4.0 fusion.39
  301.9 1.7 multiply_reduce_fusion
  303.6 1.6 fusion.135
  307.4 3.8 fusion.26.d_ref
  314.7 14.1 %attention_backward.1.grads = bf16[256,3072]{1,0:T(8,128)(2,1)S(1)} custom-call(bf16[256,1536]{1,0:T(8,128)(2,1)S(1)} %fusion.26.d_ref, bf16[256,1536]{1,0:T(8,128)(2,1)S(1)} %copy-done.11, bf16[256,768]{1,0:T(8,128)(2,1)S(1)} %copy-done.16, bf16[256,768]{1,0:T(8,128)(2,1)S(1)} %copy-done.18, f32[128,768]{1,0:T(8,128)S(1)} %copy.107.cosine, ...), custom_call_target="tpu_custom_call" | custom-call | flops 1 | bytes 1 | tf_op jit(solution)/shard_map/attention_backward/attention_backward/pallas_call | solution.py:612
  328.9 3.6 convolution_convert_fusion
  339.1 9.6 %input_gradient.1 = (bf16[256,1536]{1,0:T(8,128)(2,1)}, f32[1,1536]{1,0:T(1,128)S(1)}) custom-call(bf16[256,3072]{1,0:T(8,128)(2,1)S(1)} %attention_backward.1.grads, bf16[1536,4736]{1,0:T(8,128)(2,1)} %bitcast.202, bf16[256,1536]{1,0:T(8,128)(2,1)S(1)} %copy-done.3, f32[256,1]{1,0:T(8,128)S(1)} %copy.111.inv_scale, f32[1,1536]{1,0:T(1,128)S(1)} %reshape.348.gain, ...), custom_call_target="tpu_custom_call" | custom-call | flops 1 | bytes 1 | tf_op jit(solution)/shard_map/input_gradient/input_gradient/pallas_call | solution.py:835
  350.1 2.5 add_convert_fusion
  358.8 2.8 collective-permute-done.50
  362.8 2.5 convert_add_fusion
  366.9 15.1 %collective-permute-done.47 = bf16[192,3072]{1,0:T(8,128)(2,1)} collective-permute-done((bf16[192,3072]{1,0:T(8,128)(2,1)}, bf16[192,3072]{1,0:T(8,128)(2,1)}, u32[]{:S(2)}, u32[]{:S(2)}) %collective-permute-start.47) | collective-permute-done | bytes 1179680 | tf_op jit(solution)/shard_map/q_k_v_weight_gradients/ppermute | solution.py:40
  387.0 2.9 collective-permute-start.54
  393.9 2.0 collective-permute-done.54
  395.9 6.2 %collective-permute-done.55 = bf16[48,1536]{1,0:T(8,128)(2,1)} collective-permute-done((bf16[48,1536]{1,0:T(8,128)(2,1)}, bf16[48,1536]{1,0:T(8,128)(2,1)}, u32[]{:S(2)}, u32[]{:S(2)}) %collective-permute-start.55) | collective-permute-done | bytes 147488 | tf_op jit(solution)/shard_map/q_k_v_weight_gradients/ppermute | solution.py:40
  403.7 2.4 fusion.36
  406.5 1.7 collective-permute-start.57
  413.4 1.9 fusion.59
  416.2 2.8 collective-permute-done.61
  419.0 1.6 collective-permute-start.59
  421.7 9.8 %collective-permute-done.58 = bf16[48,3072]{1,0:T(8,128)(2,1)S(1)} collective-permute-done((bf16[48,3072]{1,0:T(8,128)(2,1)S(1)}, bf16[48,3072]{1,0:T(8,128)(2,1)S(1)}, u32[]{:S(2)}, u32[]{:S(2)}) %collective-permute-start.58) | collective-permute-done | bytes 294944 | tf_op jit(solution)/shard_map/weight_gradients_to_owners/ppermute | solution.py:40
  (357 shorter events, 124.2 us)
Async XLA Ops:
  7.2 164.4 %all-gather.2.cloned.1.call-start = ((), (), s32[]{:S(2)}) async-start(), calls=%async_computation.2 | async-start | bytes 10616832 | tf_op jit(solution)/shard_map/ffn_weights/all_gather | solution.py:114
  11.7 21.0 %collective-permute-start = (bf16[48,4736]{1,0:T(8,128)(2,1)S(1)}, bf16[48,4736]{1,0:T(8,128)(2,1)S(1)}, u32[]{:S(2)}, u32[]{:S(2)}) collective-permute-start(bf16[48,4736]{1,0:T(8,128)(2,1)S(1)} %packed.1), channel_id=1, source_target_pairs={{0,8},{1,9},{2,10},{3,11},{4,12},{5,13},{6,14},{7,15},{8,16},{9,17... | collective-permute-start | bytes 1363976 | tf_op jit(solution)/shard_map/phase_0/ppermute | solution.py:77
  16.6 16.0 %collective-permute-start.1 = (bf16[48,4736]{1,0:T(8,128)(2,1)S(1)}, bf16[48,4736]{1,0:T(8,128)(2,1)S(1)}, u32[]{:S(2)}, u32[]{:S(2)}) collective-permute-start(bf16[48,4736]{1,0:T(8,128)(2,1)S(1)} %packed.1), channel_id=1, source_target_pairs={{8,0},{9,1},{10,2},{11,3},{12,4},{13,5},{14,6},{15,7},{16,8},{17,9... | collective-permute-start | bytes 1363976 | tf_op jit(solution)/shard_map/phase_0/ppermute | solution.py:77
  20.1 21.0 %collective-permute-start.21 = (bf16[48,2048]{1,0:T(8,128)(2,1)S(1)}, bf16[48,2048]{1,0:T(8,128)(2,1)S(1)}, u32[]{:S(2)}, u32[]{:S(2)}) collective-permute-start(bf16[48,2048]{1,0:T(8,128)(2,1)S(1)} %get-tuple-element.178), channel_id=1, source_target_pairs={{0,2},{1,3},{2,0},{3,1},{4,6},{5,7},{6,4},{7,5},{8,10},{9,11},{10,... | collective-permute-start | bytes 589832 | tf_op jit(solution)/shard_map/phase_0/ppermute | solution.py:40
  21.6 23.5 %collective-permute-start.22 = (bf16[48,2048]{1,0:T(8,128)(2,1)S(1)}, bf16[48,2048]{1,0:T(8,128)(2,1)S(1)}, u32[]{:S(2)}, u32[]{:S(2)}) collective-permute-start(bf16[48,2048]{1,0:T(8,128)(2,1)S(1)} %get-tuple-element.179), channel_id=1, source_target_pairs={{0,4},{1,5},{2,6},{3,7},{4,0},{5,1},{6,2},{7,3},{8,12},{9,13},{10,... | collective-permute-start | bytes 589832 | tf_op jit(solution)/shard_map/phase_0/ppermute | solution.py:40
  33.7 19.2 %collective-permute-start.2 = (bf16[48,4736]{1,0:T(8,128)(2,1)S(1)}, bf16[48,4736]{1,0:T(8,128)(2,1)}, u32[]{:S(2)}, u32[]{:S(2)}) collective-permute-start(bf16[48,4736]{1,0:T(8,128)(2,1)S(1)} %packed.1), channel_id=1, source_target_pairs={{0,2},{1,3},{2,0},{3,1},{4,6},{5,7},{6,4},{7,5},{8,10},{9,11},{10,... | collective-permute-start | bytes 1363976 | tf_op jit(solution)/shard_map/phase_1/ppermute | solution.py:40
  34.2 21.3 %collective-permute-start.4 = (bf16[48,4736]{1,0:T(8,128)(2,1)S(1)}, bf16[48,4736]{1,0:T(8,128)(2,1)}, u32[]{:S(2)}, u32[]{:S(2)}) collective-permute-start(bf16[48,4736]{1,0:T(8,128)(2,1)S(1)} %packed.1), channel_id=1, source_target_pairs={{0,16},{1,17},{2,18},{3,19},{4,20},{5,21},{6,22},{7,23},{24,8},{25... | collective-permute-start | bytes 1363976 | tf_op jit(solution)/shard_map/phase_1/ppermute | solution.py:77
  40.6 15.0 %collective-permute-start.3 = (bf16[48,4736]{1,0:T(8,128)(2,1)}, bf16[48,4736]{1,0:T(8,128)(2,1)}, u32[]{:S(2)}, u32[]{:S(2)}) collective-permute-start(bf16[48,4736]{1,0:T(8,128)(2,1)} %get-tuple-element.147), channel_id=1, source_target_pairs={{0,4},{1,5},{2,6},{3,7},{4,0},{5,1},{6,2},{7,3},{8,12},{9,13},{10,... | collective-permute-start | bytes 1363976 | tf_op jit(solution)/shard_map/phase_1/ppermute | solution.py:40
  41.1 14.5 %collective-permute-start.5 = (bf16[48,4736]{1,0:T(8,128)(2,1)}, bf16[48,4736]{1,0:T(8,128)(2,1)}, u32[]{:S(2)}, u32[]{:S(2)}) collective-permute-start(bf16[48,4736]{1,0:T(8,128)(2,1)} %get-tuple-element.148), channel_id=1, source_target_pairs={{8,0},{9,1},{10,2},{11,3},{12,4},{13,5},{14,6},{15,7},{16,24},{17,... | collective-permute-start | bytes 1363976 | tf_op jit(solution)/shard_map/phase_1/ppermute | solution.py:77
  45.1 6.7 %collective-permute-start.23 = (bf16[48,2048]{1,0:T(8,128)(2,1)S(1)}, bf16[48,2048]{1,0:T(8,128)(2,1)S(1)}, u32[]{:S(2)}, u32[]{:S(2)}) collective-permute-start(bf16[48,2048]{1,0:T(8,128)(2,1)S(1)} %get-tuple-element.180), channel_id=1, source_target_pairs={{0,6},{1,7},{2,4},{3,5},{4,2},{5,3},{6,0},{7,1},{8,14},{9,15},{10,... | collective-permute-start | bytes 589832 | tf_op jit(solution)/shard_map/phase_0/ppermute | solution.py:40
  57.3 19.4 %collective-permute-start.6 = (bf16[2,48,4736]{2,1,0:T(8,128)(2,1)S(1)}, bf16[2,48,4736]{2,1,0:T(8,128)(2,1)S(1)}, u32[]{:S(2)}, u32[]{:S(2)}) collective-permute-start(bf16[2,48,4736]{2,1,0:T(8,128)(2,1)S(1)} %pad_maximum_fusion.8), channel_id=1, source_target_pairs={{0,4},{1,5},{2,6},{3,7},{4,0},{5,1},{6,2},{7,3},{8,12},{9,13},{10,... | collective-permute-start | bytes 2727944 | tf_op jit(solution)/shard_map/phase_2/ppermute | solution.py:40
  57.8 18.9 %collective-permute-start.7 = (bf16[2,48,4736]{2,1,0:T(8,128)(2,1)S(1)}, bf16[2,48,4736]{2,1,0:T(8,128)(2,1)S(1)}, u32[]{:S(2)}, u32[]{:S(2)}) collective-permute-start(bf16[2,48,4736]{2,1,0:T(8,128)(2,1)S(1)} %pad_maximum_fusion.9), channel_id=1, source_target_pairs={{0,2},{1,3},{2,0},{3,1},{4,6},{5,7},{6,4},{7,5},{8,10},{9,11},{10,... | collective-permute-start | bytes 2727944 | tf_op jit(solution)/shard_map/phase_2/ppermute | solution.py:40
  59.5 17.2 %collective-permute-start.9 = (bf16[2,2,48,4736]{3,2,1,0:T(8,128)(2,1)S(1)}, bf16[2,2,48,4736]{3,2,1,0:T(8,128)(2,1)S(1)}, u32[]{:S(2)}, u32[]{:S(2)}) collective-permute-start(bf16[2,2,48,4736]{3,2,1,0:T(8,128)(2,1)S(1)} %pad_maximum_fusion.1), channel_id=1, source_target_pairs={{0,1},{1,0},{2,3},{3,2},{4,5},{5,4},{6,7},{7,6},{8,9},{9,8},{10,11... | collective-permute-start | bytes 5455880 | tf_op jit(solution)/shard_map/phase_2/ppermute | solution.py:40
  59.6 14.9 %collective-permute-start.8 = (bf16[48,4736]{1,0:T(8,128)(2,1)}, bf16[48,4736]{1,0:T(8,128)(2,1)S(1)}, u32[]{:S(2)}, u32[]{:S(2)}) collective-permute-start(bf16[48,4736]{1,0:T(8,128)(2,1)} %collective-permute-done.4), channel_id=1, source_target_pairs={{8,0},{9,1},{10,2},{11,3},{12,4},{13,5},{14,6},{15,7},{16,24},{17,... | collective-permute-start | bytes 1363976 | tf_op jit(solution)/shard_map/phase_2/ppermute | solution.py:77
  77.7 14.5 %collective-permute-start.12 = (bf16[2,2,48,4736]{3,2,1,0:T(8,128)(2,1)S(1)}, bf16[2,2,48,4736]{3,2,1,0:T(8,128)(2,1)}, u32[]{:S(2)}, u32[]{:S(2)}) collective-permute-start(bf16[2,2,48,4736]{3,2,1,0:T(8,128)(2,1)S(1)} %pad_maximum_fusion.2), channel_id=1, source_target_pairs={{0,1},{1,0},{2,3},{3,2},{4,5},{5,4},{6,7},{7,6},{8,9},{9,8},{10,11... | collective-permute-start | bytes 5455880 | tf_op jit(solution)/shard_map/phase_3/ppermute | solution.py:40
  77.8 13.2 %collective-permute-start.10 = (bf16[48,4736]{1,0:T(8,128)(2,1)}, bf16[48,4736]{1,0:T(8,128)(2,1)}, u32[]{:S(2)}, u32[]{:S(2)}) collective-permute-start(bf16[48,4736]{1,0:T(8,128)(2,1)} %broadcast_select_fusion.1), channel_id=1, source_target_pairs={{0,2},{1,3},{2,0},{3,1},{4,6},{5,7},{6,4},{7,5},{8,10},{9,11},{10,... | collective-permute-start | bytes 1363976 | tf_op jit(solution)/shard_map/phase_3/ppermute | solution.py:40
  79.4 12.8 %collective-permute-start.11 = (bf16[48,4736]{1,0:T(8,128)(2,1)}, bf16[48,4736]{1,0:T(8,128)(2,1)}, u32[]{:S(2)}, u32[]{:S(2)}) collective-permute-start(bf16[48,4736]{1,0:T(8,128)(2,1)} %broadcast_select_fusion), channel_id=1, source_target_pairs={{0,4},{1,5},{2,6},{3,7},{4,0},{5,1},{6,2},{7,3},{8,12},{9,13},{10,... | collective-permute-start | bytes 1363976 | tf_op jit(solution)/shard_map/phase_3/ppermute | solution.py:40
  83.1 266.3 %reduce-scatter.3.cloned.1.call-start = ((), (), s32[]{:S(2)}) async-start(), calls=%async_computation.3 | async-start | bytes 7077888 | tf_op jit(solution)/shard_map/ffn_backward/reduce_scatter | solution.py:120
  94.9 21.5 %collective-permute-start.13 = (bf16[2,48,4736]{2,1,0:T(8,128)(2,1)S(1)}, bf16[2,48,4736]{2,1,0:T(8,128)(2,1)S(1)}, u32[]{:S(2)}, u32[]{:S(2)}) collective-permute-start(bf16[2,48,4736]{2,1,0:T(8,128)(2,1)S(1)} %pad_maximum_fusion.10), channel_id=1, source_target_pairs={{0,4},{1,5},{2,6},{3,7},{4,0},{5,1},{6,2},{7,3},{8,12},{9,13},{10,... | collective-permute-start | bytes 2727944 | tf_op jit(solution)/shard_map/phase_4/ppermute | solution.py:40
  96.6 21.2 %collective-permute-start.14 = (bf16[2,48,4736]{2,1,0:T(8,128)(2,1)S(1)}, bf16[2,48,4736]{2,1,0:T(8,128)(2,1)S(1)}, u32[]{:S(2)}, u32[]{:S(2)}) collective-permute-start(bf16[2,48,4736]{2,1,0:T(8,128)(2,1)S(1)} %pad_maximum_fusion.11), channel_id=1, source_target_pairs={{0,2},{1,3},{2,0},{3,1},{4,6},{5,7},{6,4},{7,5},{8,10},{9,11},{10,... | collective-permute-start | bytes 2727944 | tf_op jit(solution)/shard_map/phase_4/ppermute | solution.py:40
  97.4 20.4 %collective-permute-start.15 = (bf16[2,2,48,4736]{3,2,1,0:T(8,128)(2,1)S(1)}, bf16[2,2,48,4736]{3,2,1,0:T(8,128)(2,1)S(1)}, u32[]{:S(2)}, u32[]{:S(2)}) collective-permute-start(bf16[2,2,48,4736]{3,2,1,0:T(8,128)(2,1)S(1)} %pad_maximum_fusion.3), channel_id=1, source_target_pairs={{0,1},{1,0},{2,3},{3,2},{4,5},{5,4},{6,7},{7,6},{8,9},{9,8},{10,11... | collective-permute-start | bytes 5455880 | tf_op jit(solution)/shard_map/phase_4/ppermute | solution.py:40
  152.4 11.5 %collective-permute-start.17 = (bf16[128,1536]{1,0:T(8,128)(2,1)S(1)}, bf16[128,1536]{1,0:T(8,128)(2,1)S(1)}, u32[]{:S(2)}, u32[]{:S(2)}) collective-permute-start(bf16[128,1536]{1,0:T(8,128)(2,1)S(1)} %get-tuple-element.338), channel_id=1, source_target_pairs={{0,2},{1,3},{2,0},{3,1},{4,6},{5,7},{6,4},{7,5},{8,10},{9,11},{10,... | collective-permute-start | bytes 1179656 | tf_op jit(solution)/shard_map/ffn_forward/ppermute | solution.py:40
  153.2 11.1 %collective-permute-start.18 = (bf16[128,1536]{1,0:T(8,128)(2,1)S(1)}, bf16[128,1536]{1,0:T(8,128)(2,1)S(1)}, u32[]{:S(2)}, u32[]{:S(2)}) collective-permute-start(bf16[128,1536]{1,0:T(8,128)(2,1)S(1)} %get-tuple-element.337), channel_id=1, source_target_pairs={{0,4},{1,5},{2,6},{3,7},{4,0},{5,1},{6,2},{7,3},{8,12},{9,13},{10,... | collective-permute-start | bytes 1179656 | tf_op jit(solution)/shard_map/ffn_forward/ppermute | solution.py:40
  164.4 20.5 %collective-permute-start.19 = (bf16[256,1536]{1,0:T(8,128)(2,1)S(1)}, bf16[256,1536]{1,0:T(8,128)(2,1)}, u32[]{:S(2)}, u32[]{:S(2)}) collective-permute-start(bf16[256,1536]{1,0:T(8,128)(2,1)S(1)} %pad_maximum_fusion.12.refs_0_), channel_id=1, source_target_pairs={{0,4},{1,5},{2,6},{3,7},{4,0},{5,1},{6,2},{7,3},{8,12},{9,13},{10,... | collective-permute-start | bytes 2359304 | tf_op jit(solution)/shard_map/ffn_forward/ppermute | solution.py:40
  165.0 19.9 %collective-permute-start.20 = (bf16[256,1536]{1,0:T(8,128)(2,1)S(1)}, bf16[256,1536]{1,0:T(8,128)(2,1)}, u32[]{:S(2)}, u32[]{:S(2)}) collective-permute-start(bf16[256,1536]{1,0:T(8,128)(2,1)S(1)} %pad_maximum_fusion.13.refs_1_), channel_id=1, source_target_pairs={{0,2},{1,3},{2,0},{3,1},{4,6},{5,7},{6,4},{7,5},{8,10},{9,11},{10,... | collective-permute-start | bytes 2359304 | tf_op jit(solution)/shard_map/ffn_forward/ppermute | solution.py:40
  189.6 19.8 %collective-permute-start.25 = (bf16[256,1536]{1,0:T(8,128)(2,1)S(1)}, bf16[256,1536]{1,0:T(8,128)(2,1)S(1)}, u32[]{:S(2)}, u32[]{:S(2)}) collective-permute-start(bf16[256,1536]{1,0:T(8,128)(2,1)S(1)} %convolution_convert_fusion.2), channel_id=1, source_target_pairs={{0,2},{1,3},{2,0},{3,1},{4,6},{5,7},{6,4},{7,5},{8,10},{9,11},{10,... | collective-permute-start | bytes 2359304 | tf_op jit(solution)/shard_map/ffn_forward/ppermute | solution.py:40
  195.4 19.5 %collective-permute-start.24 = (bf16[256,1536]{1,0:T(8,128)(2,1)S(1)}, bf16[256,1536]{1,0:T(8,128)(2,1)S(1)}, u32[]{:S(2)}, u32[]{:S(2)}) collective-permute-start(bf16[256,1536]{1,0:T(8,128)(2,1)S(1)} %convolution_convert_fusion.3), channel_id=1, source_target_pairs={{0,4},{1,5},{2,6},{3,7},{4,0},{5,1},{6,2},{7,3},{8,12},{9,13},{10,... | collective-permute-start | bytes 2359304 | tf_op jit(solution)/shard_map/ffn_forward/ppermute | solution.py:40
  215.1 10.2 %collective-permute-start.26 = (bf16[128,1536]{1,0:T(8,128)(2,1)S(1)}, bf16[128,1536]{1,0:T(8,128)(2,1)S(1)}, u32[]{:S(2)}, u32[]{:S(2)}) collective-permute-start(bf16[128,1536]{1,0:T(8,128)(2,1)S(1)} %get-tuple-element.303), channel_id=1, source_target_pairs={{0,2},{1,3},{2,0},{3,1},{4,6},{5,7},{6,4},{7,5},{8,10},{9,11},{10,... | collective-permute-start | bytes 1179656 | tf_op jit(solution)/shard_map/ffn_forward/ppermute | solution.py:40
  215.8 10.0 %collective-permute-start.27 = (bf16[128,1536]{1,0:T(8,128)(2,1)S(1)}, bf16[128,1536]{1,0:T(8,128)(2,1)S(1)}, u32[]{:S(2)}, u32[]{:S(2)}) collective-permute-start(bf16[128,1536]{1,0:T(8,128)(2,1)S(1)} %get-tuple-element.302), channel_id=1, source_target_pairs={{0,4},{1,5},{2,6},{3,7},{4,0},{5,1},{6,2},{7,3},{8,12},{9,13},{10,... | collective-permute-start | bytes 1179656 | tf_op jit(solution)/shard_map/ffn_forward/ppermute | solution.py:40
  227.4 9.1 %collective-permute-start.28 = (bf16[128,1536]{1,0:T(8,128)(2,1)S(1)}, bf16[128,1536]{1,0:T(8,128)(2,1)S(1)}, u32[]{:S(2)}, u32[]{:S(2)}) collective-permute-start(bf16[128,1536]{1,0:T(8,128)(2,1)S(1)} %get-tuple-element.336), channel_id=1, source_target_pairs={{0,2},{1,3},{2,0},{3,1},{4,6},{5,7},{6,4},{7,5},{8,10},{9,11},{10,... | collective-permute-start | bytes 1179656 | tf_op jit(solution)/shard_map/ffn_backward/ppermute | solution.py:40
  228.7 9.1 %collective-permute-start.29 = (bf16[128,1536]{1,0:T(8,128)(2,1)S(1)}, bf16[128,1536]{1,0:T(8,128)(2,1)S(1)}, u32[]{:S(2)}, u32[]{:S(2)}) collective-permute-start(bf16[128,1536]{1,0:T(8,128)(2,1)S(1)} %get-tuple-element.335), channel_id=1, source_target_pairs={{0,4},{1,5},{2,6},{3,7},{4,0},{5,1},{6,2},{7,3},{8,12},{9,13},{10,... | collective-permute-start | bytes 1179656 | tf_op jit(solution)/shard_map/ffn_backward/ppermute | solution.py:40
  237.9 19.4 %collective-permute-start.30 = (bf16[256,1536]{1,0:T(8,128)(2,1)S(1)}, bf16[256,1536]{1,0:T(8,128)(2,1)S(1)}, u32[]{:S(2)}, u32[]{:S(2)}) collective-permute-start(bf16[256,1536]{1,0:T(8,128)(2,1)S(1)} %pad_maximum_fusion.14.refs_0_), channel_id=1, source_target_pairs={{0,4},{1,5},{2,6},{3,7},{4,0},{5,1},{6,2},{7,3},{8,12},{9,13},{10,... | collective-permute-start | bytes 2359304 | tf_op jit(solution)/shard_map/ffn_backward/ppermute | solution.py:40
  239.5 17.8 %collective-permute-start.31 = (bf16[256,1536]{1,0:T(8,128)(2,1)S(1)}, bf16[256,1536]{1,0:T(8,128)(2,1)S(1)}, u32[]{:S(2)}, u32[]{:S(2)}) collective-permute-start(bf16[256,1536]{1,0:T(8,128)(2,1)S(1)} %pad_maximum_fusion.15.refs_1_), channel_id=1, source_target_pairs={{0,2},{1,3},{2,0},{3,1},{4,6},{5,7},{6,4},{7,5},{8,10},{9,11},{10,... | collective-permute-start | bytes 2359304 | tf_op jit(solution)/shard_map/ffn_backward/ppermute | solution.py:40
  262.7 16.9 %collective-permute-start.32 = (bf16[256,1536]{1,0:T(8,128)(2,1)}, bf16[256,1536]{1,0:T(8,128)(2,1)}, u32[]{:S(2)}, u32[]{:S(2)}) collective-permute-start(bf16[256,1536]{1,0:T(8,128)(2,1)} %fusion.23), channel_id=1, source_target_pairs={{0,4},{1,5},{2,6},{3,7},{4,0},{5,1},{6,2},{7,3},{8,12},{9,13},{10,... | collective-permute-start | bytes 2359304 | tf_op jit(solution)/shard_map/ffn_backward/ppermute | solution.py:40
  266.0 15.5 %collective-permute-start.33 = (bf16[256,1536]{1,0:T(8,128)(2,1)}, bf16[256,1536]{1,0:T(8,128)(2,1)}, u32[]{:S(2)}, u32[]{:S(2)}) collective-permute-start(bf16[256,1536]{1,0:T(8,128)(2,1)} %fusion.20), channel_id=1, source_target_pairs={{0,2},{1,3},{2,0},{3,1},{4,6},{5,7},{6,4},{7,5},{8,10},{9,11},{10,... | collective-permute-start | bytes 2359304 | tf_op jit(solution)/shard_map/ffn_backward/ppermute | solution.py:40
  267.2 12.3 %collective-permute-start.34 = (f32[2,128]{1,0:T(2,128)S(1)}, f32[2,128]{1,0:T(2,128)S(1)}, u32[]{:S(2)}, u32[]{:S(2)}) collective-permute-start(f32[2,128]{1,0:T(2,128)S(1)} %broadcast_in_dim.15), channel_id=1, source_target_pairs={{0,1},{1,0},{2,3},{3,2},{4,5},{5,4},{6,7},{7,6},{8,9},{9,8},{10,11... | collective-permute-start | bytes 3080 | tf_op jit(solution)/shard_map/ffn_backward/ppermute | solution.py:40
  281.4 120.8 %reduce-scatter.5.cloned.1.call-start = ((), (), s32[]{:S(2)}) async-start(), calls=%async_computation.4 | async-start | bytes 3538944 | tf_op jit(solution)/shard_map/q_k_v_weight_gradients/reduce_scatter | solution.py:120
  284.3 11.2 %collective-permute-start.35 = (bf16[128,1536]{1,0:T(8,128)(2,1)}, bf16[128,1536]{1,0:T(8,128)(2,1)}, u32[]{:S(2)}, u32[]{:S(2)}) collective-permute-start(bf16[128,1536]{1,0:T(8,128)(2,1)} %get-tuple-element.294), channel_id=1, source_target_pairs={{0,2},{1,3},{2,0},{3,1},{4,6},{5,7},{6,4},{7,5},{8,10},{9,11},{10,... | collective-permute-start | bytes 1179656 | tf_op jit(solution)/shard_map/ffn_backward/ppermute | solution.py:40
  285.3 10.2 %collective-permute-start.36 = (bf16[128,1536]{1,0:T(8,128)(2,1)}, bf16[128,1536]{1,0:T(8,128)(2,1)}, u32[]{:S(2)}, u32[]{:S(2)}) collective-permute-start(bf16[128,1536]{1,0:T(8,128)(2,1)} %get-tuple-element.293), channel_id=1, source_target_pairs={{0,4},{1,5},{2,6},{3,7},{4,0},{5,1},{6,2},{7,3},{8,12},{9,13},{10,... | collective-permute-start | bytes 1179656 | tf_op jit(solution)/shard_map/ffn_backward/ppermute | solution.py:40
  286.8 8.7 %collective-permute-start.37 = (f32[2,128]{1,0:T(2,128)S(1)}, f32[2,128]{1,0:T(2,128)S(1)}, u32[]{:S(2)}, u32[]{:S(2)}) collective-permute-start(f32[2,128]{1,0:T(2,128)S(1)} %add.515), channel_id=1, source_target_pairs={{0,8},{1,9},{2,10},{3,11},{4,12},{5,13},{6,14},{7,15},{8,0},{9,1},... | collective-permute-start | bytes 3080 | tf_op jit(solution)/shard_map/ffn_backward/ppermute | solution.py:40
  306.0 5.3 %collective-permute-start.38 = (bf16[768,1536]{1,0:T(8,128)(2,1)S(1)}, bf16[768,1536]{1,0:T(8,128)(2,1)S(1)}, u32[]{:S(2)}, u32[]{:S(2)}) collective-permute-start(bf16[768,1536]{1,0:T(8,128)(2,1)S(1)} %convolution_convert_fusion.1), channel_id=1, source_target_pairs={{0,1},{1,0},{2,3},{3,2},{4,5},{5,4},{6,7},{7,6},{8,9},{9,8},{10,11... | collective-permute-start | bytes 7077896 | tf_op jit(solution)/shard_map/attention_backward/ppermute | solution.py:40
  311.9 17.0 %collective-permute-start.40 = (bf16[192,1536]{1,0:T(8,128)(2,1)S(1)}, bf16[192,1536]{1,0:T(8,128)(2,1)S(1)}, u32[]{:S(2)}, u32[]{:S(2)}) collective-permute-start(bf16[192,1536]{1,0:T(8,128)(2,1)S(1)} %get-tuple-element.321), channel_id=1, source_target_pairs={{0,4},{1,5},{2,6},{3,7},{4,0},{5,1},{6,2},{7,3},{8,12},{9,13},{10,... | collective-permute-start | bytes 1769480 | tf_op jit(solution)/shard_map/attention_backward/ppermute | solution.py:40
  312.7 16.2 %collective-permute-start.41 = (bf16[192,1536]{1,0:T(8,128)(2,1)S(1)}, bf16[192,1536]{1,0:T(8,128)(2,1)S(1)}, u32[]{:S(2)}, u32[]{:S(2)}) collective-permute-start(bf16[192,1536]{1,0:T(8,128)(2,1)S(1)} %get-tuple-element.320), channel_id=1, source_target_pairs={{0,2},{1,3},{2,0},{3,1},{4,6},{5,7},{6,4},{7,5},{8,10},{9,11},{10,... | collective-permute-start | bytes 1769480 | tf_op jit(solution)/shard_map/attention_backward/ppermute | solution.py:40
  314.1 14.7 %collective-permute-start.42 = (f32[2,128]{1,0:T(2,128)S(1)}, f32[2,128]{1,0:T(2,128)S(1)}, u32[]{:S(2)}, u32[]{:S(2)}) collective-permute-start(f32[2,128]{1,0:T(2,128)S(1)} %add.523), channel_id=1, source_target_pairs={{0,2},{1,3},{2,0},{3,1},{4,6},{5,7},{6,4},{7,5},{8,10},{9,11},{10,... | collective-permute-start | bytes 3080 | tf_op jit(solution)/shard_map/attention_backward/ppermute | solution.py:40
  332.5 16.3 %collective-permute-start.43 = (bf16[768,3072]{1,0:T(8,128)(2,1)}, bf16[768,3072]{1,0:T(8,128)(2,1)}, u32[]{:S(2)}, u32[]{:S(2)}) collective-permute-start(bf16[768,3072]{1,0:T(8,128)(2,1)} %convolution_convert_fusion), channel_id=1, source_target_pairs={{0,1},{1,0},{2,3},{3,2},{4,5},{5,4},{6,7},{7,6},{8,9},{9,8},{10,11... | collective-permute-start | bytes 14155784 | tf_op jit(solution)/shard_map/q_k_v_weight_gradients/ppermute | solution.py:40
  334.0 14.8 %collective-permute-start.45 = (bf16[96,1536]{1,0:T(8,128)(2,1)}, bf16[96,1536]{1,0:T(8,128)(2,1)S(1)}, u32[]{:S(2)}, u32[]{:S(2)}) collective-permute-start(bf16[96,1536]{1,0:T(8,128)(2,1)} %get-tuple-element.312), channel_id=1, source_target_pairs={{0,2},{1,3},{2,0},{3,1},{4,6},{5,7},{6,4},{7,5},{8,10},{9,11},{10,... | collective-permute-start | bytes 884744 | tf_op jit(solution)/shard_map/attention_backward/ppermute | solution.py:40
  335.4 13.3 %collective-permute-start.46 = (bf16[96,1536]{1,0:T(8,128)(2,1)S(1)}, bf16[96,1536]{1,0:T(8,128)(2,1)S(1)}, u32[]{:S(2)}, u32[]{:S(2)}) collective-permute-start(bf16[96,1536]{1,0:T(8,128)(2,1)S(1)} %get-tuple-element.311), channel_id=1, source_target_pairs={{0,4},{1,5},{2,6},{3,7},{4,0},{5,1},{6,2},{7,3},{8,12},{9,13},{10,... | collective-permute-start | bytes 884744 | tf_op jit(solution)/shard_map/attention_backward/ppermute | solution.py:40
  336.4 12.3 %collective-permute-start.44 = (f32[2,128]{1,0:T(2,128)S(1)}, f32[2,128]{1,0:T(2,128)S(1)}, u32[]{:S(2)}, u32[]{:S(2)}) collective-permute-start(f32[2,128]{1,0:T(2,128)S(1)} %add.524), channel_id=1, source_target_pairs={{0,4},{1,5},{2,6},{3,7},{4,0},{5,1},{6,2},{7,3},{8,12},{9,13},{10,... | collective-permute-start | bytes 3080 | tf_op jit(solution)/shard_map/q_k_v_weight_gradients/ppermute | solution.py:40
  354.1 27.8 %collective-permute-start.47 = (bf16[192,3072]{1,0:T(8,128)(2,1)}, bf16[192,3072]{1,0:T(8,128)(2,1)}, u32[]{:S(2)}, u32[]{:S(2)}) collective-permute-start(bf16[192,3072]{1,0:T(8,128)(2,1)} %get-tuple-element.310), channel_id=1, source_target_pairs={{0,4},{1,5},{2,6},{3,7},{4,0},{5,1},{6,2},{7,3},{8,12},{9,13},{10,... | collective-permute-start | bytes 3538952 | tf_op jit(solution)/shard_map/q_k_v_weight_gradients/ppermute | solution.py:40
  355.0 27.5 %collective-permute-start.48 = (bf16[192,3072]{1,0:T(8,128)(2,1)}, bf16[192,3072]{1,0:T(8,128)(2,1)}, u32[]{:S(2)}, u32[]{:S(2)}) collective-permute-start(bf16[192,3072]{1,0:T(8,128)(2,1)} %get-tuple-element.309), channel_id=1, source_target_pairs={{0,2},{1,3},{2,0},{3,1},{4,6},{5,7},{6,4},{7,5},{8,10},{9,11},{10,... | collective-permute-start | bytes 3538952 | tf_op jit(solution)/shard_map/q_k_v_weight_gradients/ppermute | solution.py:40
  361.6 5.2 %collective-permute-start.51 = (f32[2,1536]{1,0:T(2,128)S(1)}, f32[2,1536]{1,0:T(2,128)S(1)}, u32[]{:S(2)}, u32[]{:S(2)}) collective-permute-start(f32[2,1536]{1,0:T(2,128)S(1)} %add.532), channel_id=1, source_target_pairs={{0,16},{1,17},{2,18},{3,19},{4,20},{5,21},{6,22},{7,23},{8,24},{9,... | collective-permute-start | bytes 36872 | tf_op jit(solution)/shard_map/weight_gradients_to_owners/ppermute | solution.py:40
  384.1 18.1 %collective-permute-start.52 = (bf16[96,3072]{1,0:T(8,128)(2,1)S(1)}, bf16[96,3072]{1,0:T(8,128)(2,1)S(1)}, u32[]{:S(2)}, u32[]{:S(2)}) collective-permute-start(bf16[96,3072]{1,0:T(8,128)(2,1)S(1)} %get-tuple-element.290), channel_id=1, source_target_pairs={{0,2},{1,3},{2,0},{3,1},{4,6},{5,7},{6,4},{7,5},{8,10},{9,11},{10,... | collective-permute-start | bytes 1769480 | tf_op jit(solution)/shard_map/weight_gradients_to_owners/ppermute | solution.py:40
  385.1 17.0 %collective-permute-start.53 = (bf16[96,3072]{1,0:T(8,128)(2,1)S(1)}, bf16[96,3072]{1,0:T(8,128)(2,1)S(1)}, u32[]{:S(2)}, u32[]{:S(2)}) collective-permute-start(bf16[96,3072]{1,0:T(8,128)(2,1)S(1)} %get-tuple-element.289), channel_id=1, source_target_pairs={{0,4},{1,5},{2,6},{3,7},{4,0},{5,1},{6,2},{7,3},{8,12},{9,13},{10,... | collective-permute-start | bytes 1769480 | tf_op jit(solution)/shard_map/weight_gradients_to_owners/ppermute | solution.py:40
  387.0 8.9 %collective-permute-start.54 = (bf16[48,1536]{1,0:T(8,128)(2,1)}, bf16[48,1536]{1,0:T(8,128)(2,1)}, u32[]{:S(2)}, u32[]{:S(2)}) collective-permute-start(bf16[48,1536]{1,0:T(8,128)(2,1)} %get-tuple-element.318), channel_id=1, source_target_pairs={{0,24},{1,25},{2,26},{3,27},{4,28},{5,29},{6,30},{7,31},{8,16},{9,... | collective-permute-start | bytes 442376 | tf_op jit(solution)/shard_map/q_k_v_weight_gradients/ppermute | solution.py:40
  389.9 12.3 %collective-permute-start.55 = (bf16[48,1536]{1,0:T(8,128)(2,1)}, bf16[48,1536]{1,0:T(8,128)(2,1)}, u32[]{:S(2)}, u32[]{:S(2)}) collective-permute-start(bf16[48,1536]{1,0:T(8,128)(2,1)} %get-tuple-element.319), channel_id=1, source_target_pairs={{0,16},{1,17},{2,18},{3,19},{4,20},{5,21},{6,22},{7,23},{8,24},{9,... | collective-permute-start | bytes 442376 | tf_op jit(solution)/shard_map/q_k_v_weight_gradients/ppermute | solution.py:40
  389.9 12.3 %collective-permute-start.56 = (bf16[48,1536]{1,0:T(8,128)(2,1)}, bf16[48,1536]{1,0:T(8,128)(2,1)}, u32[]{:S(2)}, u32[]{:S(2)}) collective-permute-start(bf16[48,1536]{1,0:T(8,128)(2,1)} %get-tuple-element.317), channel_id=1, source_target_pairs={{0,8},{1,9},{2,10},{3,11},{4,12},{5,13},{6,14},{7,15},{8,0},{9,1},... | collective-permute-start | bytes 442376 | tf_op jit(solution)/shard_map/q_k_v_weight_gradients/ppermute | solution.py:40
  402.2 6.0 %collective-permute-start.60 = (f32[2,1536]{1,0:T(2,128)S(1)}, f32[2,1536]{1,0:T(2,128)S(1)}, u32[]{:S(2)}, u32[]{:S(2)}) collective-permute-start(f32[2,1536]{1,0:T(2,128)S(1)} %add.533), channel_id=1, source_target_pairs={{0,2},{1,3},{2,0},{3,1},{4,6},{5,7},{6,4},{7,5},{8,10},{9,11},{10,... | collective-permute-start | bytes 36872 | tf_op jit(solution)/shard_map/weight_gradients_to_owners/ppermute | solution.py:40
  406.5 15.2 %collective-permute-start.57 = (bf16[48,3072]{1,0:T(8,128)(2,1)S(1)}, bf16[48,3072]{1,0:T(8,128)(2,1)S(1)}, u32[]{:S(2)}, u32[]{:S(2)}) collective-permute-start(bf16[48,3072]{1,0:T(8,128)(2,1)S(1)} %get-tuple-element.304), channel_id=1, source_target_pairs={{0,24},{1,25},{2,26},{3,27},{4,28},{5,29},{6,30},{7,31},{8,16},{9,... | collective-permute-start | bytes 884744 | tf_op jit(solution)/shard_map/weight_gradients_to_owners/ppermute | solution.py:40
  408.3 10.7 %collective-permute-start.62 = (bf16[48,2048]{1,0:T(8,128)(2,1)S(1)}, bf16[48,2048]{1,0:T(8,128)(2,1)S(1)}, u32[]{:S(2)}, u32[]{:S(2)}) collective-permute-start(bf16[48,2048]{1,0:T(8,128)(2,1)S(1)} %get-tuple-element.334), channel_id=1, source_target_pairs={{0,2},{1,3},{2,0},{3,1},{4,6},{5,7},{6,4},{7,5},{8,10},{9,11},{10,... | collective-permute-start | bytes 589832 | tf_op jit(solution)/shard_map/weight_gradients_to_owners/ppermute | solution.py:40
  409.0 11.6 %collective-permute-start.63 = (bf16[48,2048]{1,0:T(8,128)(2,1)S(1)}, bf16[48,2048]{1,0:T(8,128)(2,1)S(1)}, u32[]{:S(2)}, u32[]{:S(2)}) collective-permute-start(bf16[48,2048]{1,0:T(8,128)(2,1)S(1)} %get-tuple-element.333), channel_id=1, source_target_pairs={{0,4},{1,5},{2,6},{3,7},{4,0},{5,1},{6,2},{7,3},{8,12},{9,13},{10,... | collective-permute-start | bytes 589832 | tf_op jit(solution)/shard_map/weight_gradients_to_owners/ppermute | solution.py:40
  410.4 10.2 %collective-permute-start.64 = (bf16[48,2048]{1,0:T(8,128)(2,1)S(1)}, bf16[48,2048]{1,0:T(8,128)(2,1)S(1)}, u32[]{:S(2)}, u32[]{:S(2)}) collective-permute-start(bf16[48,2048]{1,0:T(8,128)(2,1)S(1)} %get-tuple-element.332), channel_id=1, source_target_pairs={{0,6},{1,7},{2,4},{3,5},{4,2},{5,3},{6,0},{7,1},{8,14},{9,15},{10,... | collective-permute-start | bytes 589832 | tf_op jit(solution)/shard_map/weight_gradients_to_owners/ppermute | solution.py:40
  411.9 7.1 %collective-permute-start.61 = (f32[2,1536]{1,0:T(2,128)S(1)}, f32[2,1536]{1,0:T(2,128)S(1)}, u32[]{:S(2)}, u32[]{:S(2)}) collective-permute-start(f32[2,1536]{1,0:T(2,128)S(1)} %add.554), channel_id=1, source_target_pairs={{0,4},{1,5},{2,6},{3,7},{4,0},{5,1},{6,2},{7,3},{8,12},{9,13},{10,... | collective-permute-start | bytes 36872 | tf_op jit(solution)/shard_map/weight_gradients_to_owners/ppermute | solution.py:40
  419.0 12.4 %collective-permute-start.58 = (bf16[48,3072]{1,0:T(8,128)(2,1)S(1)}, bf16[48,3072]{1,0:T(8,128)(2,1)S(1)}, u32[]{:S(2)}, u32[]{:S(2)}) collective-permute-start(bf16[48,3072]{1,0:T(8,128)(2,1)S(1)} %get-tuple-element.306), channel_id=1, source_target_pairs={{0,16},{1,17},{2,18},{3,19},{4,20},{5,21},{6,22},{7,23},{8,24},{9,... | collective-permute-start | bytes 884744 | tf_op jit(solution)/shard_map/weight_gradients_to_owners/ppermute | solution.py:40
  419.0 12.4 %collective-permute-start.59 = (bf16[48,3072]{1,0:T(8,128)(2,1)S(1)}, bf16[48,3072]{1,0:T(8,128)(2,1)S(1)}, u32[]{:S(2)}, u32[]{:S(2)}) collective-permute-start(bf16[48,3072]{1,0:T(8,128)(2,1)S(1)} %get-tuple-element.305), channel_id=1, source_target_pairs={{0,8},{1,9},{2,10},{3,11},{4,12},{5,13},{6,14},{7,15},{8,0},{9,1},... | collective-permute-start | bytes 884744 | tf_op jit(solution)/shard_map/weight_gradients_to_owners/ppermute | solution.py:40
  (67 other events, 410.5 us)
Sparse Core Ops, SparseCore 0:
  83.2 88.3 all-gather.1
  281.6 67.7 reduce-scatter.2
  351.7 39.5 reduce-scatter.4

commit v12 on v11

--- a/solution.py
+++ b/solution.py
@@ -964,19 +964,16 @@
     rest = [1 << k for k in range(4, n.bit_length() - 2)]
 
     with jax.named_scope("ffn_backward"):
-        def near_backward(pieces, grads):
-            sums = jnp.stack([jnp.sum(grads * grads), jnp.sum(mask_f)])
-            return (
-                jnp.broadcast_to(sums[:, None], (2, LANES)),
-                *ffn_backward_beside(pieces, gate_near, up_near, wb, wd),
-            )
-
-        d_far, sums, m_near, d_near, g_near = split_gather(
-            grad_out.astype(BF), (grad_out,), near_backward
+        d_far, m_near, d_near, g_near = split_gather(
+            grad_out.astype(BF),
+            (),
+            lambda pieces: ffn_backward_beside(pieces, gate_near, up_near, wb, wd),
         )
         m_a, g_a = ffn_backward(d_far[0], pre_a, wb, wd)
         m_b, g_b = ffn_backward(d_far[1], pre_b, wb, wd)
-        m_b, m_near, sums = tied(m_b.astype(BF), m_near, sums)
+        m_b, m_near, grads = tied(m_b.astype(BF), m_near, grad_out)
+        sums = jnp.stack([jnp.sum(grads * grads), jnp.sum(mask_f)])
+        sums = jnp.broadcast_to(sums[:, None], (2, LANES))
         came = swap(sums, 1)
         beside = (products([near, *far], [g_near, g_a, g_b], BF), sums, came)
 
@@ -1037,12 +1034,9 @@
             gains = gains + swap(gains, mask)
         *qkv_came, gains = tied(*qkv_moving, gains)
         qkv_moving = g_qkv.step_2(qkv_came)
-        qkv_0, qkv_1, gains, g_both, g_down, *wo_came = tied(
-            *qkv_moving, gains, g_both, g_down, *wo_moving
-        )
-        qkv_came = (qkv_0, qkv_1)
+        *qkv_came, gains, g_both, g_down = tied(*qkv_moving, gains, g_both, g_down)
+        g_qkv, g_both, *wo_came = tied(g_qkv.step_3(qkv_came, rows), g_both, *wo_moving)
         g_wo = owned([g_wo], wo_came, z) if planes == 4 else z_reduce([g_wo])
-        g_qkv, g_both = tied(g_qkv.step_3(qkv_came, rows), g_both)
         if planes == 4:
             moving = direct([g_qkv], z)
         gains = gains + swap(gains, 2)

time: 448 us -> 443 us (0.989)
    unnamed x141 -> x135, local copies, waits for them, and re-layouts: 20 us -> 20.5 us
  transfers between devices with their start and end apart: 68 -> 68, of which waited for: 29 -> 30; matrix products, arithmetic and copies ran while one was open for 24% -> 23% of each run, Pallas kernels for 17% -> 17%
where the time goes in v12:
time: 443 us; the launch traced here: 436 us
  waiting for transfers between devices  128 us (29%)
  Pallas kernels  76 us (17%)
  starting transfers between devices  75.5 us (17%)
  matrix products  51.7 us (12%)
  local copies, waits for them, and re-layouts  45.9 us (10%)
  other arithmetic  41.3 us (9%)
  between operations  18.1 us (4%)
    ppermute x60, waiting for transfers between devices, swap(): return lax.ppermute(value, 'dp', [(i, i ^ mask) for i in range(n)])  113 us
    ppermute x60, starting transfers between devices, swap(): return lax.ppermute(value, 'dp', [(i, i ^ mask) for i in range(n)])  59.9 us
    dot_general x22, matrix products, dot(): return lax.dot_general(a, b, (dims, ((), ())), preferred_element_type=F32)  51.7 us
    unnamed x135, local copies, waits for them, and re-layouts  20.5 us
    dynamic_update_slice x16, local copies, waits for them, and re-layouts, place(): return lax.dynamic_update_slice(out, piece, where)  18.6 us
    pallas_call x2, Pallas kernels, products(): pl.pallas_call(kernel, grid=(columns // tile,), out_shape=jax.ShapeDtypeS...  15.4 us
    ppermute x5, starting transfers between devices, along_z(): lax.ppermute(value, 'dp', [(8 * a + i, 8 * b + i) for a, b in pairs for i...  15.3 us
    pallas_call x1, Pallas kernels, attention_backward(): pl.pallas_call(kernel, grid=(count // SEQ, steps), out_shape=jax.ShapeDty...  14.1 us
  transfers between devices with their start and end apart: 68, of which 30 were waited for; matrix products, arithmetic and copies ran while one was open for 23% of the time, Pallas kernels for 17%

profile of v12, /device:TPU:0, one launch (start us, length us, event | category | flops | bytes accessed | tf_op | source)
XLA Modules:
  0.0 436.4 jit_solution(8245187187975260428)
XLA Ops:
  11.7 5.0 %collective-permute-start = (bf16[48,4736]{1,0:T(8,128)(2,1)S(1)}, bf16[48,4736]{1,0:T(8,128)(2,1)S(1)}, u32[]{:S(2)}, u32[]{:S(2)}) collective-permute-start(bf16[48,4736]{1,0:T(8,128)(2,1)S(1)} %packed.1), channel_id=1, source_target_pairs={{0,8},{1,9},{2,10},{3,11},{4,12},{5,13},{6,14},{7,15},{8,16},{9,17... | collective-permute-start | bytes 1363976 | tf_op jit(solution)/shard_map/phase_0/ppermute | solution.py:77
  24.1 4.2 fusion.3
  28.3 4.4 fusion.2
  34.2 6.3 %collective-permute-start.4 = (bf16[48,4736]{1,0:T(8,128)(2,1)S(1)}, bf16[48,4736]{1,0:T(8,128)(2,1)}, u32[]{:S(2)}, u32[]{:S(2)}) collective-permute-start(bf16[48,4736]{1,0:T(8,128)(2,1)S(1)} %packed.1), channel_id=1, source_target_pairs={{0,16},{1,17},{2,18},{3,19},{4,20},{5,21},{6,22},{7,23},{24,8},{25... | collective-permute-start | bytes 1363976 | tf_op jit(solution)/shard_map/phase_1/ppermute | solution.py:77
  45.1 2.5 collective-permute-start.23
  47.6 4.2 collective-permute-done.23.refs_3_
  52.9 2.6 collective-permute-done.3
  63.1 1.8 broadcast_select_fusion.1
  64.9 9.6 %collective-permute-done.8 = bf16[48,4736]{1,0:T(8,128)(2,1)S(1)} collective-permute-done((bf16[48,4736]{1,0:T(8,128)(2,1)}, bf16[48,4736]{1,0:T(8,128)(2,1)S(1)}, u32[]{:S(2)}, u32[]{:S(2)}) %collective-permute-start.8) | collective-permute-done | bytes 454688 | tf_op jit(solution)/shard_map/phase_2/ppermute | solution.py:77
  74.5 2.1 collective-permute-done.6
  79.4 1.7 collective-permute-start.11
  85.4 5.6 %collective-permute-done.10 = bf16[48,4736]{1,0:T(8,128)(2,1)} collective-permute-done((bf16[48,4736]{1,0:T(8,128)(2,1)}, bf16[48,4736]{1,0:T(8,128)(2,1)}, u32[]{:S(2)}, u32[]{:S(2)}) %collective-permute-start.10) | collective-permute-done | bytes 454688 | tf_op jit(solution)/shard_map/phase_3/ppermute | solution.py:40
  94.9 1.7 collective-permute-start.13
  97.5 2.2 bitcast_dynamic-update-slice_fusion.7
  99.7 2.1 bitcast_dynamic-update-slice_fusion.6
  103.9 12.5 %collective-permute-done.13 = bf16[2,48,4736]{2,1,0:T(8,128)(2,1)S(1)} collective-permute-done((bf16[2,48,4736]{2,1,0:T(8,128)(2,1)S(1)}, bf16[2,48,4736]{2,1,0:T(8,128)(2,1)S(1)}, u32[]{:S(2)}, u32[]{:S(2)}) %collective-permute-start.13) | collective-permute-done | bytes 909344 | tf_op jit(solution)/shard_map/phase_4/ppermute | solution.py:40
  124.2 1.6 convert_reduce_fusion
  126.0 5.6 %fusion.q_raw.k_raw.v_raw = f32[256,3072]{1,0:T(8,128)S(1)} fusion(bf16[256,1536]{1,0:T(8,128)(2,1)S(1)} %fusion.31, bf16[1536,4736]{1,0:T(8,128)(2,1)} %bitcast.199), kind=kOutput, calls=%fused_computation | convolution fusion | flops 2415919104 | bytes 13369344 | tf_op jit(solution)/shard_map/attention_forward/dot_general | solution.py:23
  131.7 12.6 %attention_forward.1 = (bf16[256,1536]{1,0:T(8,128)(2,1)S(1)}, bf16[256,768]{1,0:T(8,128)(2,1)S(1)}, bf16[256,768]{1,0:T(8,128)(2,1)S(1)}, bf16[256,1536]{1,0:T(8,128)(2,1)S(1)}) custom-call(f32[256,3072]{1,0:T(8,128)S(1)} %fusion.q_raw.k_raw.v_raw, f32[256,3072]{1,0:T(8,128)S(1)} %fusion.q_raw.k_raw.v_raw, f32[256,3072]{1,0:T(8,128)S(1)} %fusion.q_raw.k_raw.v_raw, ...), custom_call_target="tpu_custom_call" | custom-call | flops 1 | bytes 1 | tf_op jit(solution)/shard_map/attention_forward/attention_forward/pallas_call | solution.py:540
  146.7 4.1 multiply_reduce_fusion.3
  153.7 10.3 %collective-permute-done.17 = bf16[128,1536]{1,0:T(8,128)(2,1)S(1)} collective-permute-done((bf16[128,1536]{1,0:T(8,128)(2,1)S(1)}, bf16[128,1536]{1,0:T(8,128)(2,1)S(1)}, u32[]{:S(2)}, u32[]{:S(2)}) %collective-permute-start.17) | collective-permute-done | bytes 393248 | tf_op jit(solution)/shard_map/ffn_forward/ppermute | solution.py:40
  166.3 5.2 %all-gather.2.cloned.1.call-done.ref.refs_2_.refs_3_.refs_4_.refs_5_ = bf16[1536,3072]{1,0:T(8,128)(2,1)} async-done(((bf16[192,3072]{1,0:T(8,128)(2,1)}), bf16[1536,3072]{1,0:T(8,128)(2,1)}) %all-gather.2.cloned.1.call-update) | async-done | bytes 9437200 | tf_op jit(solution)/shard_map/ffn_weights/all_gather | solution.py:114
  171.6 2.2 w_down_from.1.refs_4_.refs_6_
  173.8 2.5 copy-done
  176.2 8.6 %ffn_forward_beside.1 = (f32[512,1536]{1,0:T(8,128)S(1)}, bf16[512,1536]{1,0:T(8,128)(2,1)S(1)}, bf16[512,1024]{1,0:T(8,128)(2,1)S(1)}, f32[512,1024]{1,0:T(8,128)S(1)}, f32[512,1024]{1,0:T(8,128)S(1)}) custom-call(bf16[256,1536]{1,0:T(8,128)(2,1)S(1)} %pad_maximum_fusion.12.refs_0_, bf16[256,1536]{1,0:T(8,128)(2,1)S(1)} %pad_maximum_fusion.13.refs_1_, ...), custom_call_target="tpu_custom_call" | custom-call | flops 1 | bytes 1 | tf_op jit(solution)/shard_map/ffn_forward/ffn_forward_beside/pallas_call | solution.py:725
  184.9 3.3 fusion.12
  191.1 2.9 fusion.14
  196.9 2.3 convolution_convert_fusion.4
  199.2 2.3 convolution_convert_fusion.5
  201.5 7.8 %collective-permute-done.25 = bf16[256,1536]{1,0:T(8,128)(2,1)S(1)} collective-permute-done((bf16[256,1536]{1,0:T(8,128)(2,1)S(1)}, bf16[256,1536]{1,0:T(8,128)(2,1)S(1)}, u32[]{:S(2)}, u32[]{:S(2)}) %collective-permute-start.25) | collective-permute-done | bytes 786464 | tf_op jit(solution)/shard_map/ffn_forward/ppermute | solution.py:40
  209.3 5.6 %collective-permute-done.24 = bf16[256,1536]{1,0:T(8,128)(2,1)S(1)} collective-permute-done((bf16[256,1536]{1,0:T(8,128)(2,1)S(1)}, bf16[256,1536]{1,0:T(8,128)(2,1)S(1)}, u32[]{:S(2)}, u32[]{:S(2)}) %collective-permute-start.24) | collective-permute-done | bytes 786464 | tf_op jit(solution)/shard_map/ffn_forward/ppermute | solution.py:40
  217.3 8.0 %collective-permute-done.26 = bf16[128,1536]{1,0:T(8,128)(2,1)S(1)} collective-permute-done((bf16[128,1536]{1,0:T(8,128)(2,1)S(1)}, bf16[128,1536]{1,0:T(8,128)(2,1)S(1)}, u32[]{:S(2)}, u32[]{:S(2)}) %collective-permute-start.26) | collective-permute-done | bytes 393248 | tf_op jit(solution)/shard_map/ffn_forward/ppermute | solution.py:40
  230.2 6.3 %collective-permute-done.28 = bf16[128,1536]{1,0:T(8,128)(2,1)S(1)} collective-permute-done((bf16[128,1536]{1,0:T(8,128)(2,1)S(1)}, bf16[128,1536]{1,0:T(8,128)(2,1)S(1)}, u32[]{:S(2)}, u32[]{:S(2)}) %collective-permute-start.28) | collective-permute-done | bytes 393248 | tf_op jit(solution)/shard_map/ffn_backward/ppermute | solution.py:40
  240.2 12.4 %ffn_backward_beside.1 = (f32[512,1536]{1,0:T(8,128)S(1)}, bf16[512,1536]{1,0:T(8,128)(2,1)S(1)}, bf16[512,2048]{1,0:T(8,128)(2,1)S(1)}) custom-call(bf16[256,1536]{1,0:T(8,128)(2,1)S(1)} %pad_maximum_fusion.14.refs_0_, bf16[256,1536]{1,0:T(8,128)(2,1)S(1)} %pad_maximum_fusion.15.refs_1_, f32[512,1024]{1,0:T(8,128)S(1)} %get-tuple-element.207.refs_2_, ...), custom_call_target="tpu_custom_call" | custom-call | flops 1 | bytes 1 | tf_op jit(solution)/shard_map/ffn_backward/ffn_backward_beside/pallas_call | solution.py:790
  252.6 1.7 copy-done.5
  257.4 2.7 fusion.23
  261.0 2.7 fusion.20
  267.7 9.5 %products.2 = bf16[1536,2048]{1,0:T(8,128)(2,1)S(1)} custom-call(bf16[512,1536]{1,0:T(8,128)(2,1)S(1)} %get-tuple-element.217.refs_0_, bf16[256,1536]{1,0:T(8,128)(2,1)} %collective-permute-done.19.refs_1_, bf16[256,1536]{1,0:T(8,128)(2,1)} %collective-permute-done.20.refs_2_, bf16[512,2048]{1,0:T(8,128)(2,1)S(1)} %get-tuple-element.218.refs_3_, ...), custom_call_target="tpu_custom_call" | custom-call | flops 1 | bytes 1 | tf_op jit(solution)/shard_map/ffn_backward/products/pallas_call | solution.py:875
  277.2 2.7 copy-done.1
  279.9 2.8 add_convert_fusion.1
  286.3 5.9 %products.3 = bf16[1024,1536]{1,0:T(8,128)(2,1)S(1)} custom-call(bf16[512,1024]{1,0:T(8,128)(2,1)S(1)} %copy-done.9, bf16[256,1024]{1,0:T(8,128)(2,1)S(1)} %multiply_convert_fusion.6.refs_1_, bf16[256,1024]{1,0:T(8,128)(2,1)S(1)} %multiply_convert_fusion.5.refs_2_, bf16[512,1536]{1,0:T(8,128)(2,1)S(1)} %copy-done.7, ...), custom_call_target="tpu_custom_call" | custom-call | flops 1 | bytes 1 | tf_op jit(solution)/shard_map/ffn_backward/products/pallas_call | solution.py:875
  292.3 1.6 copy-done.2
  295.5 2.2 convert_add_fusion.2
  297.8 4.0 fusion.39
  301.8 1.7 multiply_reduce_fusion
  303.5 1.6 fusion.135
  307.0 3.8 fusion.26.d_ref
  314.8 14.1 %attention_backward.1.grads = bf16[256,3072]{1,0:T(8,128)(2,1)S(1)} custom-call(bf16[256,1536]{1,0:T(8,128)(2,1)S(1)} %fusion.26.d_ref, bf16[256,1536]{1,0:T(8,128)(2,1)S(1)} %copy-done.11, bf16[256,768]{1,0:T(8,128)(2,1)S(1)} %copy-done.16, bf16[256,768]{1,0:T(8,128)(2,1)S(1)} %copy-done.18, f32[128,768]{1,0:T(8,128)S(1)} %copy.107.cosine, ...), custom_call_target="tpu_custom_call" | custom-call | flops 1 | bytes 1 | tf_op jit(solution)/shard_map/attention_backward/attention_backward/pallas_call | solution.py:612
  328.9 3.6 convolution_convert_fusion
  338.5 9.5 %input_gradient.1 = (bf16[256,1536]{1,0:T(8,128)(2,1)}, f32[1,1536]{1,0:T(1,128)S(1)}) custom-call(bf16[256,3072]{1,0:T(8,128)(2,1)S(1)} %attention_backward.1.grads, bf16[1536,4736]{1,0:T(8,128)(2,1)} %bitcast.202, bf16[256,1536]{1,0:T(8,128)(2,1)S(1)} %copy-done.3, f32[256,1]{1,0:T(8,128)S(1)} %copy.111.inv_scale, f32[1,1536]{1,0:T(1,128)S(1)} %reshape.348.gain, ...), custom_call_target="tpu_custom_call" | custom-call | flops 1 | bytes 1 | tf_op jit(solution)/shard_map/input_gradient/input_gradient/pallas_call | solution.py:835
  349.3 2.5 add_convert_fusion
  357.1 3.8 collective-permute-done.50
  360.9 1.7 collective-permute-start.51
  362.7 2.5 convert_add_fusion
  366.2 15.0 %collective-permute-done.47 = bf16[192,3072]{1,0:T(8,128)(2,1)} collective-permute-done((bf16[192,3072]{1,0:T(8,128)(2,1)}, bf16[192,3072]{1,0:T(8,128)(2,1)}, u32[]{:S(2)}, u32[]{:S(2)}) %collective-permute-start.47) | collective-permute-done | bytes 1179680 | tf_op jit(solution)/shard_map/q_k_v_weight_gradients/ppermute | solution.py:40
  381.7 1.6 fusion.34
  386.2 1.6 collective-permute-start.54
  388.3 2.3 collective-permute-start.56
  392.5 4.5 %collective-permute-done.52 = bf16[96,3072]{1,0:T(8,128)(2,1)S(1)} collective-permute-done((bf16[96,3072]{1,0:T(8,128)(2,1)S(1)}, bf16[96,3072]{1,0:T(8,128)(2,1)S(1)}, u32[]{:S(2)}, u32[]{:S(2)}) %collective-permute-start.52) | collective-permute-done | bytes 589856 | tf_op jit(solution)/shard_map/weight_gradients_to_owners/ppermute | solution.py:40
  398.7 2.4 fusion.36
  401.5 2.1 collective-permute-start.57
  410.0 5.1 %collective-permute-done.61 = f32[2,1536]{1,0:T(2,128)S(1)} collective-permute-done((f32[2,1536]{1,0:T(2,128)S(1)}, f32[2,1536]{1,0:T(2,128)S(1)}, u32[]{:S(2)}, u32[]{:S(2)}) %collective-permute-start.61) | collective-permute-done | bytes 12320 | tf_op jit(solution)/shard_map/weight_gradients_to_owners/ppermute | solution.py:40
  415.1 2.0 collective-permute-start.59
  418.1 8.8 %collective-permute-done.58 = bf16[48,3072]{1,0:T(8,128)(2,1)S(1)} collective-permute-done((bf16[48,3072]{1,0:T(8,128)(2,1)S(1)}, bf16[48,3072]{1,0:T(8,128)(2,1)S(1)}, u32[]{:S(2)}, u32[]{:S(2)}) %collective-permute-start.58) | collective-permute-done | bytes 294944 | tf_op jit(solution)/shard_map/weight_gradients_to_owners/ppermute | solution.py:40
  (351 shorter events, 120.1 us)
Async XLA Ops:
  7.2 164.4 %all-gather.2.cloned.1.call-start = ((), (), s32[]{:S(2)}) async-start(), calls=%async_computation.2 | async-start | bytes 10616832 | tf_op jit(solution)/shard_map/ffn_weights/all_gather | solution.py:114
  11.7 21.0 %collective-permute-start = (bf16[48,4736]{1,0:T(8,128)(2,1)S(1)}, bf16[48,4736]{1,0:T(8,128)(2,1)S(1)}, u32[]{:S(2)}, u32[]{:S(2)}) collective-permute-start(bf16[48,4736]{1,0:T(8,128)(2,1)S(1)} %packed.1), channel_id=1, source_target_pairs={{0,8},{1,9},{2,10},{3,11},{4,12},{5,13},{6,14},{7,15},{8,16},{9,17... | collective-permute-start | bytes 1363976 | tf_op jit(solution)/shard_map/phase_0/ppermute | solution.py:77
  16.6 16.0 %collective-permute-start.1 = (bf16[48,4736]{1,0:T(8,128)(2,1)S(1)}, bf16[48,4736]{1,0:T(8,128)(2,1)S(1)}, u32[]{:S(2)}, u32[]{:S(2)}) collective-permute-start(bf16[48,4736]{1,0:T(8,128)(2,1)S(1)} %packed.1), channel_id=1, source_target_pairs={{8,0},{9,1},{10,2},{11,3},{12,4},{13,5},{14,6},{15,7},{16,8},{17,9... | collective-permute-start | bytes 1363976 | tf_op jit(solution)/shard_map/phase_0/ppermute | solution.py:77
  20.1 21.0 %collective-permute-start.21 = (bf16[48,2048]{1,0:T(8,128)(2,1)S(1)}, bf16[48,2048]{1,0:T(8,128)(2,1)S(1)}, u32[]{:S(2)}, u32[]{:S(2)}) collective-permute-start(bf16[48,2048]{1,0:T(8,128)(2,1)S(1)} %get-tuple-element.176), channel_id=1, source_target_pairs={{0,2},{1,3},{2,0},{3,1},{4,6},{5,7},{6,4},{7,5},{8,10},{9,11},{10,... | collective-permute-start | bytes 589832 | tf_op jit(solution)/shard_map/phase_0/ppermute | solution.py:40
  21.6 23.5 %collective-permute-start.22 = (bf16[48,2048]{1,0:T(8,128)(2,1)S(1)}, bf16[48,2048]{1,0:T(8,128)(2,1)S(1)}, u32[]{:S(2)}, u32[]{:S(2)}) collective-permute-start(bf16[48,2048]{1,0:T(8,128)(2,1)S(1)} %get-tuple-element.177), channel_id=1, source_target_pairs={{0,4},{1,5},{2,6},{3,7},{4,0},{5,1},{6,2},{7,3},{8,12},{9,13},{10,... | collective-permute-start | bytes 589832 | tf_op jit(solution)/shard_map/phase_0/ppermute | solution.py:40
  33.7 19.2 %collective-permute-start.2 = (bf16[48,4736]{1,0:T(8,128)(2,1)S(1)}, bf16[48,4736]{1,0:T(8,128)(2,1)}, u32[]{:S(2)}, u32[]{:S(2)}) collective-permute-start(bf16[48,4736]{1,0:T(8,128)(2,1)S(1)} %packed.1), channel_id=1, source_target_pairs={{0,2},{1,3},{2,0},{3,1},{4,6},{5,7},{6,4},{7,5},{8,10},{9,11},{10,... | collective-permute-start | bytes 1363976 | tf_op jit(solution)/shard_map/phase_1/ppermute | solution.py:40
  34.2 21.3 %collective-permute-start.4 = (bf16[48,4736]{1,0:T(8,128)(2,1)S(1)}, bf16[48,4736]{1,0:T(8,128)(2,1)}, u32[]{:S(2)}, u32[]{:S(2)}) collective-permute-start(bf16[48,4736]{1,0:T(8,128)(2,1)S(1)} %packed.1), channel_id=1, source_target_pairs={{0,16},{1,17},{2,18},{3,19},{4,20},{5,21},{6,22},{7,23},{24,8},{25... | collective-permute-start | bytes 1363976 | tf_op jit(solution)/shard_map/phase_1/ppermute | solution.py:77
  40.6 15.0 %collective-permute-start.3 = (bf16[48,4736]{1,0:T(8,128)(2,1)}, bf16[48,4736]{1,0:T(8,128)(2,1)}, u32[]{:S(2)}, u32[]{:S(2)}) collective-permute-start(bf16[48,4736]{1,0:T(8,128)(2,1)} %get-tuple-element.145), channel_id=1, source_target_pairs={{0,4},{1,5},{2,6},{3,7},{4,0},{5,1},{6,2},{7,3},{8,12},{9,13},{10,... | collective-permute-start | bytes 1363976 | tf_op jit(solution)/shard_map/phase_1/ppermute | solution.py:40
  41.1 14.5 %collective-permute-start.5 = (bf16[48,4736]{1,0:T(8,128)(2,1)}, bf16[48,4736]{1,0:T(8,128)(2,1)}, u32[]{:S(2)}, u32[]{:S(2)}) collective-permute-start(bf16[48,4736]{1,0:T(8,128)(2,1)} %get-tuple-element.146), channel_id=1, source_target_pairs={{8,0},{9,1},{10,2},{11,3},{12,4},{13,5},{14,6},{15,7},{16,24},{17,... | collective-permute-start | bytes 1363976 | tf_op jit(solution)/shard_map/phase_1/ppermute | solution.py:77
  45.1 6.7 %collective-permute-start.23 = (bf16[48,2048]{1,0:T(8,128)(2,1)S(1)}, bf16[48,2048]{1,0:T(8,128)(2,1)S(1)}, u32[]{:S(2)}, u32[]{:S(2)}) collective-permute-start(bf16[48,2048]{1,0:T(8,128)(2,1)S(1)} %get-tuple-element.178), channel_id=1, source_target_pairs={{0,6},{1,7},{2,4},{3,5},{4,2},{5,3},{6,0},{7,1},{8,14},{9,15},{10,... | collective-permute-start | bytes 589832 | tf_op jit(solution)/shard_map/phase_0/ppermute | solution.py:40
  57.3 19.4 %collective-permute-start.6 = (bf16[2,48,4736]{2,1,0:T(8,128)(2,1)S(1)}, bf16[2,48,4736]{2,1,0:T(8,128)(2,1)S(1)}, u32[]{:S(2)}, u32[]{:S(2)}) collective-permute-start(bf16[2,48,4736]{2,1,0:T(8,128)(2,1)S(1)} %pad_maximum_fusion.8), channel_id=1, source_target_pairs={{0,4},{1,5},{2,6},{3,7},{4,0},{5,1},{6,2},{7,3},{8,12},{9,13},{10,... | collective-permute-start | bytes 2727944 | tf_op jit(solution)/shard_map/phase_2/ppermute | solution.py:40
  57.8 18.9 %collective-permute-start.7 = (bf16[2,48,4736]{2,1,0:T(8,128)(2,1)S(1)}, bf16[2,48,4736]{2,1,0:T(8,128)(2,1)S(1)}, u32[]{:S(2)}, u32[]{:S(2)}) collective-permute-start(bf16[2,48,4736]{2,1,0:T(8,128)(2,1)S(1)} %pad_maximum_fusion.9), channel_id=1, source_target_pairs={{0,2},{1,3},{2,0},{3,1},{4,6},{5,7},{6,4},{7,5},{8,10},{9,11},{10,... | collective-permute-start | bytes 2727944 | tf_op jit(solution)/shard_map/phase_2/ppermute | solution.py:40
  59.5 17.2 %collective-permute-start.9 = (bf16[2,2,48,4736]{3,2,1,0:T(8,128)(2,1)S(1)}, bf16[2,2,48,4736]{3,2,1,0:T(8,128)(2,1)S(1)}, u32[]{:S(2)}, u32[]{:S(2)}) collective-permute-start(bf16[2,2,48,4736]{3,2,1,0:T(8,128)(2,1)S(1)} %pad_maximum_fusion.1), channel_id=1, source_target_pairs={{0,1},{1,0},{2,3},{3,2},{4,5},{5,4},{6,7},{7,6},{8,9},{9,8},{10,11... | collective-permute-start | bytes 5455880 | tf_op jit(solution)/shard_map/phase_2/ppermute | solution.py:40
  59.6 14.9 %collective-permute-start.8 = (bf16[48,4736]{1,0:T(8,128)(2,1)}, bf16[48,4736]{1,0:T(8,128)(2,1)S(1)}, u32[]{:S(2)}, u32[]{:S(2)}) collective-permute-start(bf16[48,4736]{1,0:T(8,128)(2,1)} %collective-permute-done.4), channel_id=1, source_target_pairs={{8,0},{9,1},{10,2},{11,3},{12,4},{13,5},{14,6},{15,7},{16,24},{17,... | collective-permute-start | bytes 1363976 | tf_op jit(solution)/shard_map/phase_2/ppermute | solution.py:77
  77.8 14.5 %collective-permute-start.12 = (bf16[2,2,48,4736]{3,2,1,0:T(8,128)(2,1)S(1)}, bf16[2,2,48,4736]{3,2,1,0:T(8,128)(2,1)}, u32[]{:S(2)}, u32[]{:S(2)}) collective-permute-start(bf16[2,2,48,4736]{3,2,1,0:T(8,128)(2,1)S(1)} %pad_maximum_fusion.2), channel_id=1, source_target_pairs={{0,1},{1,0},{2,3},{3,2},{4,5},{5,4},{6,7},{7,6},{8,9},{9,8},{10,11... | collective-permute-start | bytes 5455880 | tf_op jit(solution)/shard_map/phase_3/ppermute | solution.py:40
  77.8 13.2 %collective-permute-start.10 = (bf16[48,4736]{1,0:T(8,128)(2,1)}, bf16[48,4736]{1,0:T(8,128)(2,1)}, u32[]{:S(2)}, u32[]{:S(2)}) collective-permute-start(bf16[48,4736]{1,0:T(8,128)(2,1)} %broadcast_select_fusion.1), channel_id=1, source_target_pairs={{0,2},{1,3},{2,0},{3,1},{4,6},{5,7},{6,4},{7,5},{8,10},{9,11},{10,... | collective-permute-start | bytes 1363976 | tf_op jit(solution)/shard_map/phase_3/ppermute | solution.py:40
  79.4 12.8 %collective-permute-start.11 = (bf16[48,4736]{1,0:T(8,128)(2,1)}, bf16[48,4736]{1,0:T(8,128)(2,1)}, u32[]{:S(2)}, u32[]{:S(2)}) collective-permute-start(bf16[48,4736]{1,0:T(8,128)(2,1)} %broadcast_select_fusion), channel_id=1, source_target_pairs={{0,4},{1,5},{2,6},{3,7},{4,0},{5,1},{6,2},{7,3},{8,12},{9,13},{10,... | collective-permute-start | bytes 1363976 | tf_op jit(solution)/shard_map/phase_3/ppermute | solution.py:40
  83.1 265.0 %reduce-scatter.3.cloned.1.call-start = ((), (), s32[]{:S(2)}) async-start(), calls=%async_computation.3 | async-start | bytes 7077888 | tf_op jit(solution)/shard_map/ffn_backward/reduce_scatter | solution.py:120
  94.9 21.5 %collective-permute-start.13 = (bf16[2,48,4736]{2,1,0:T(8,128)(2,1)S(1)}, bf16[2,48,4736]{2,1,0:T(8,128)(2,1)S(1)}, u32[]{:S(2)}, u32[]{:S(2)}) collective-permute-start(bf16[2,48,4736]{2,1,0:T(8,128)(2,1)S(1)} %pad_maximum_fusion.10), channel_id=1, source_target_pairs={{0,4},{1,5},{2,6},{3,7},{4,0},{5,1},{6,2},{7,3},{8,12},{9,13},{10,... | collective-permute-start | bytes 2727944 | tf_op jit(solution)/shard_map/phase_4/ppermute | solution.py:40
  96.6 21.2 %collective-permute-start.14 = (bf16[2,48,4736]{2,1,0:T(8,128)(2,1)S(1)}, bf16[2,48,4736]{2,1,0:T(8,128)(2,1)S(1)}, u32[]{:S(2)}, u32[]{:S(2)}) collective-permute-start(bf16[2,48,4736]{2,1,0:T(8,128)(2,1)S(1)} %pad_maximum_fusion.11), channel_id=1, source_target_pairs={{0,2},{1,3},{2,0},{3,1},{4,6},{5,7},{6,4},{7,5},{8,10},{9,11},{10,... | collective-permute-start | bytes 2727944 | tf_op jit(solution)/shard_map/phase_4/ppermute | solution.py:40
  97.4 20.4 %collective-permute-start.15 = (bf16[2,2,48,4736]{3,2,1,0:T(8,128)(2,1)S(1)}, bf16[2,2,48,4736]{3,2,1,0:T(8,128)(2,1)S(1)}, u32[]{:S(2)}, u32[]{:S(2)}) collective-permute-start(bf16[2,2,48,4736]{3,2,1,0:T(8,128)(2,1)S(1)} %pad_maximum_fusion.3), channel_id=1, source_target_pairs={{0,1},{1,0},{2,3},{3,2},{4,5},{5,4},{6,7},{7,6},{8,9},{9,8},{10,11... | collective-permute-start | bytes 5455880 | tf_op jit(solution)/shard_map/phase_4/ppermute | solution.py:40
  152.4 11.6 %collective-permute-start.17 = (bf16[128,1536]{1,0:T(8,128)(2,1)S(1)}, bf16[128,1536]{1,0:T(8,128)(2,1)S(1)}, u32[]{:S(2)}, u32[]{:S(2)}) collective-permute-start(bf16[128,1536]{1,0:T(8,128)(2,1)S(1)} %get-tuple-element.334), channel_id=1, source_target_pairs={{0,2},{1,3},{2,0},{3,1},{4,6},{5,7},{6,4},{7,5},{8,10},{9,11},{10,... | collective-permute-start | bytes 1179656 | tf_op jit(solution)/shard_map/ffn_forward/ppermute | solution.py:40
  153.3 11.1 %collective-permute-start.18 = (bf16[128,1536]{1,0:T(8,128)(2,1)S(1)}, bf16[128,1536]{1,0:T(8,128)(2,1)S(1)}, u32[]{:S(2)}, u32[]{:S(2)}) collective-permute-start(bf16[128,1536]{1,0:T(8,128)(2,1)S(1)} %get-tuple-element.333), channel_id=1, source_target_pairs={{0,4},{1,5},{2,6},{3,7},{4,0},{5,1},{6,2},{7,3},{8,12},{9,13},{10,... | collective-permute-start | bytes 1179656 | tf_op jit(solution)/shard_map/ffn_forward/ppermute | solution.py:40
  164.5 20.4 %collective-permute-start.19 = (bf16[256,1536]{1,0:T(8,128)(2,1)S(1)}, bf16[256,1536]{1,0:T(8,128)(2,1)}, u32[]{:S(2)}, u32[]{:S(2)}) collective-permute-start(bf16[256,1536]{1,0:T(8,128)(2,1)S(1)} %pad_maximum_fusion.12.refs_0_), channel_id=1, source_target_pairs={{0,4},{1,5},{2,6},{3,7},{4,0},{5,1},{6,2},{7,3},{8,12},{9,13},{10,... | collective-permute-start | bytes 2359304 | tf_op jit(solution)/shard_map/ffn_forward/ppermute | solution.py:40
  165.1 19.8 %collective-permute-start.20 = (bf16[256,1536]{1,0:T(8,128)(2,1)S(1)}, bf16[256,1536]{1,0:T(8,128)(2,1)}, u32[]{:S(2)}, u32[]{:S(2)}) collective-permute-start(bf16[256,1536]{1,0:T(8,128)(2,1)S(1)} %pad_maximum_fusion.13.refs_1_), channel_id=1, source_target_pairs={{0,2},{1,3},{2,0},{3,1},{4,6},{5,7},{6,4},{7,5},{8,10},{9,11},{10,... | collective-permute-start | bytes 2359304 | tf_op jit(solution)/shard_map/ffn_forward/ppermute | solution.py:40
  189.5 19.8 %collective-permute-start.25 = (bf16[256,1536]{1,0:T(8,128)(2,1)S(1)}, bf16[256,1536]{1,0:T(8,128)(2,1)S(1)}, u32[]{:S(2)}, u32[]{:S(2)}) collective-permute-start(bf16[256,1536]{1,0:T(8,128)(2,1)S(1)} %convolution_convert_fusion.2), channel_id=1, source_target_pairs={{0,2},{1,3},{2,0},{3,1},{4,6},{5,7},{6,4},{7,5},{8,10},{9,11},{10,... | collective-permute-start | bytes 2359304 | tf_op jit(solution)/shard_map/ffn_forward/ppermute | solution.py:40
  195.4 19.5 %collective-permute-start.24 = (bf16[256,1536]{1,0:T(8,128)(2,1)S(1)}, bf16[256,1536]{1,0:T(8,128)(2,1)S(1)}, u32[]{:S(2)}, u32[]{:S(2)}) collective-permute-start(bf16[256,1536]{1,0:T(8,128)(2,1)S(1)} %convolution_convert_fusion.3), channel_id=1, source_target_pairs={{0,4},{1,5},{2,6},{3,7},{4,0},{5,1},{6,2},{7,3},{8,12},{9,13},{10,... | collective-permute-start | bytes 2359304 | tf_op jit(solution)/shard_map/ffn_forward/ppermute | solution.py:40
  215.1 10.2 %collective-permute-start.26 = (bf16[128,1536]{1,0:T(8,128)(2,1)S(1)}, bf16[128,1536]{1,0:T(8,128)(2,1)S(1)}, u32[]{:S(2)}, u32[]{:S(2)}) collective-permute-start(bf16[128,1536]{1,0:T(8,128)(2,1)S(1)} %get-tuple-element.299), channel_id=1, source_target_pairs={{0,2},{1,3},{2,0},{3,1},{4,6},{5,7},{6,4},{7,5},{8,10},{9,11},{10,... | collective-permute-start | bytes 1179656 | tf_op jit(solution)/shard_map/ffn_forward/ppermute | solution.py:40
  215.8 10.0 %collective-permute-start.27 = (bf16[128,1536]{1,0:T(8,128)(2,1)S(1)}, bf16[128,1536]{1,0:T(8,128)(2,1)S(1)}, u32[]{:S(2)}, u32[]{:S(2)}) collective-permute-start(bf16[128,1536]{1,0:T(8,128)(2,1)S(1)} %get-tuple-element.298), channel_id=1, source_target_pairs={{0,4},{1,5},{2,6},{3,7},{4,0},{5,1},{6,2},{7,3},{8,12},{9,13},{10,... | collective-permute-start | bytes 1179656 | tf_op jit(solution)/shard_map/ffn_forward/ppermute | solution.py:40
  227.4 9.1 %collective-permute-start.28 = (bf16[128,1536]{1,0:T(8,128)(2,1)S(1)}, bf16[128,1536]{1,0:T(8,128)(2,1)S(1)}, u32[]{:S(2)}, u32[]{:S(2)}) collective-permute-start(bf16[128,1536]{1,0:T(8,128)(2,1)S(1)} %get-tuple-element.332), channel_id=1, source_target_pairs={{0,2},{1,3},{2,0},{3,1},{4,6},{5,7},{6,4},{7,5},{8,10},{9,11},{10,... | collective-permute-start | bytes 1179656 | tf_op jit(solution)/shard_map/ffn_backward/ppermute | solution.py:40
  228.7 9.1 %collective-permute-start.29 = (bf16[128,1536]{1,0:T(8,128)(2,1)S(1)}, bf16[128,1536]{1,0:T(8,128)(2,1)S(1)}, u32[]{:S(2)}, u32[]{:S(2)}) collective-permute-start(bf16[128,1536]{1,0:T(8,128)(2,1)S(1)} %get-tuple-element.331), channel_id=1, source_target_pairs={{0,4},{1,5},{2,6},{3,7},{4,0},{5,1},{6,2},{7,3},{8,12},{9,13},{10,... | collective-permute-start | bytes 1179656 | tf_op jit(solution)/shard_map/ffn_backward/ppermute | solution.py:40
  237.9 16.4 %collective-permute-start.30 = (bf16[256,1536]{1,0:T(8,128)(2,1)S(1)}, bf16[256,1536]{1,0:T(8,128)(2,1)S(1)}, u32[]{:S(2)}, u32[]{:S(2)}) collective-permute-start(bf16[256,1536]{1,0:T(8,128)(2,1)S(1)} %pad_maximum_fusion.14.refs_0_), channel_id=1, source_target_pairs={{0,4},{1,5},{2,6},{3,7},{4,0},{5,1},{6,2},{7,3},{8,12},{9,13},{10,... | collective-permute-start | bytes 2359304 | tf_op jit(solution)/shard_map/ffn_backward/ppermute | solution.py:40
  239.5 15.4 %collective-permute-start.31 = (bf16[256,1536]{1,0:T(8,128)(2,1)S(1)}, bf16[256,1536]{1,0:T(8,128)(2,1)S(1)}, u32[]{:S(2)}, u32[]{:S(2)}) collective-permute-start(bf16[256,1536]{1,0:T(8,128)(2,1)S(1)} %pad_maximum_fusion.15.refs_1_), channel_id=1, source_target_pairs={{0,2},{1,3},{2,0},{3,1},{4,6},{5,7},{6,4},{7,5},{8,10},{9,11},{10,... | collective-permute-start | bytes 2359304 | tf_op jit(solution)/shard_map/ffn_backward/ppermute | solution.py:40
  260.1 19.7 %collective-permute-start.32 = (bf16[256,1536]{1,0:T(8,128)(2,1)}, bf16[256,1536]{1,0:T(8,128)(2,1)}, u32[]{:S(2)}, u32[]{:S(2)}) collective-permute-start(bf16[256,1536]{1,0:T(8,128)(2,1)} %fusion.23), channel_id=1, source_target_pairs={{0,4},{1,5},{2,6},{3,7},{4,0},{5,1},{6,2},{7,3},{8,12},{9,13},{10,... | collective-permute-start | bytes 2359304 | tf_op jit(solution)/shard_map/ffn_backward/ppermute | solution.py:40
  263.7 16.2 %collective-permute-start.33 = (bf16[256,1536]{1,0:T(8,128)(2,1)}, bf16[256,1536]{1,0:T(8,128)(2,1)}, u32[]{:S(2)}, u32[]{:S(2)}) collective-permute-start(bf16[256,1536]{1,0:T(8,128)(2,1)} %fusion.20), channel_id=1, source_target_pairs={{0,2},{1,3},{2,0},{3,1},{4,6},{5,7},{6,4},{7,5},{8,10},{9,11},{10,... | collective-permute-start | bytes 2359304 | tf_op jit(solution)/shard_map/ffn_backward/ppermute | solution.py:40
  267.5 12.3 %collective-permute-start.34 = (f32[2,128]{1,0:T(2,128)S(1)}, f32[2,128]{1,0:T(2,128)S(1)}, u32[]{:S(2)}, u32[]{:S(2)}) collective-permute-start(f32[2,128]{1,0:T(2,128)S(1)} %broadcast_in_dim.15), channel_id=1, source_target_pairs={{0,1},{1,0},{2,3},{3,2},{4,5},{5,4},{6,7},{7,6},{8,9},{9,8},{10,11... | collective-permute-start | bytes 3080 | tf_op jit(solution)/shard_map/ffn_backward/ppermute | solution.py:40
  279.8 118.2 %reduce-scatter.5.cloned.1.call-start = ((), (), s32[]{:S(2)}) async-start(), calls=%async_computation.4 | async-start | bytes 3538944 | tf_op jit(solution)/shard_map/q_k_v_weight_gradients/reduce_scatter | solution.py:120
  282.7 11.9 %collective-permute-start.35 = (bf16[128,1536]{1,0:T(8,128)(2,1)}, bf16[128,1536]{1,0:T(8,128)(2,1)}, u32[]{:S(2)}, u32[]{:S(2)}) collective-permute-start(bf16[128,1536]{1,0:T(8,128)(2,1)} %get-tuple-element.290), channel_id=1, source_target_pairs={{0,2},{1,3},{2,0},{3,1},{4,6},{5,7},{6,4},{7,5},{8,10},{9,11},{10,... | collective-permute-start | bytes 1179656 | tf_op jit(solution)/shard_map/ffn_backward/ppermute | solution.py:40
  283.9 11.6 %collective-permute-start.36 = (bf16[128,1536]{1,0:T(8,128)(2,1)}, bf16[128,1536]{1,0:T(8,128)(2,1)}, u32[]{:S(2)}, u32[]{:S(2)}) collective-permute-start(bf16[128,1536]{1,0:T(8,128)(2,1)} %get-tuple-element.289), channel_id=1, source_target_pairs={{0,4},{1,5},{2,6},{3,7},{4,0},{5,1},{6,2},{7,3},{8,12},{9,13},{10,... | collective-permute-start | bytes 1179656 | tf_op jit(solution)/shard_map/ffn_backward/ppermute | solution.py:40
  285.2 8.7 %collective-permute-start.37 = (f32[2,128]{1,0:T(2,128)S(1)}, f32[2,128]{1,0:T(2,128)S(1)}, u32[]{:S(2)}, u32[]{:S(2)}) collective-permute-start(f32[2,128]{1,0:T(2,128)S(1)} %add.515), channel_id=1, source_target_pairs={{0,8},{1,9},{2,10},{3,11},{4,12},{5,13},{6,14},{7,15},{8,0},{9,1},... | collective-permute-start | bytes 3080 | tf_op jit(solution)/shard_map/ffn_backward/ppermute | solution.py:40
  305.9 4.9 %collective-permute-start.38 = (bf16[768,1536]{1,0:T(8,128)(2,1)S(1)}, bf16[768,1536]{1,0:T(8,128)(2,1)S(1)}, u32[]{:S(2)}, u32[]{:S(2)}) collective-permute-start(bf16[768,1536]{1,0:T(8,128)(2,1)S(1)} %convolution_convert_fusion.1), channel_id=1, source_target_pairs={{0,1},{1,0},{2,3},{3,2},{4,5},{5,4},{6,7},{7,6},{8,9},{9,8},{10,11... | collective-permute-start | bytes 7077896 | tf_op jit(solution)/shard_map/attention_backward/ppermute | solution.py:40
  311.4 17.4 %collective-permute-start.40 = (bf16[192,1536]{1,0:T(8,128)(2,1)S(1)}, bf16[192,1536]{1,0:T(8,128)(2,1)S(1)}, u32[]{:S(2)}, u32[]{:S(2)}) collective-permute-start(bf16[192,1536]{1,0:T(8,128)(2,1)S(1)} %get-tuple-element.317), channel_id=1, source_target_pairs={{0,4},{1,5},{2,6},{3,7},{4,0},{5,1},{6,2},{7,3},{8,12},{9,13},{10,... | collective-permute-start | bytes 1769480 | tf_op jit(solution)/shard_map/attention_backward/ppermute | solution.py:40
  312.7 16.2 %collective-permute-start.41 = (bf16[192,1536]{1,0:T(8,128)(2,1)S(1)}, bf16[192,1536]{1,0:T(8,128)(2,1)S(1)}, u32[]{:S(2)}, u32[]{:S(2)}) collective-permute-start(bf16[192,1536]{1,0:T(8,128)(2,1)S(1)} %get-tuple-element.316), channel_id=1, source_target_pairs={{0,2},{1,3},{2,0},{3,1},{4,6},{5,7},{6,4},{7,5},{8,10},{9,11},{10,... | collective-permute-start | bytes 1769480 | tf_op jit(solution)/shard_map/attention_backward/ppermute | solution.py:40
  313.5 15.3 %collective-permute-start.42 = (f32[2,128]{1,0:T(2,128)S(1)}, f32[2,128]{1,0:T(2,128)S(1)}, u32[]{:S(2)}, u32[]{:S(2)}) collective-permute-start(f32[2,128]{1,0:T(2,128)S(1)} %add.523), channel_id=1, source_target_pairs={{0,2},{1,3},{2,0},{3,1},{4,6},{5,7},{6,4},{7,5},{8,10},{9,11},{10,... | collective-permute-start | bytes 3080 | tf_op jit(solution)/shard_map/attention_backward/ppermute | solution.py:40
  332.5 15.6 %collective-permute-start.43 = (bf16[768,3072]{1,0:T(8,128)(2,1)}, bf16[768,3072]{1,0:T(8,128)(2,1)}, u32[]{:S(2)}, u32[]{:S(2)}) collective-permute-start(bf16[768,3072]{1,0:T(8,128)(2,1)} %convolution_convert_fusion), channel_id=1, source_target_pairs={{0,1},{1,0},{2,3},{3,2},{4,5},{5,4},{6,7},{7,6},{8,9},{9,8},{10,11... | collective-permute-start | bytes 14155784 | tf_op jit(solution)/shard_map/q_k_v_weight_gradients/ppermute | solution.py:40
  334.0 14.0 %collective-permute-start.45 = (bf16[96,1536]{1,0:T(8,128)(2,1)}, bf16[96,1536]{1,0:T(8,128)(2,1)S(1)}, u32[]{:S(2)}, u32[]{:S(2)}) collective-permute-start(bf16[96,1536]{1,0:T(8,128)(2,1)} %get-tuple-element.308), channel_id=1, source_target_pairs={{0,2},{1,3},{2,0},{3,1},{4,6},{5,7},{6,4},{7,5},{8,10},{9,11},{10,... | collective-permute-start | bytes 884744 | tf_op jit(solution)/shard_map/attention_backward/ppermute | solution.py:40
  334.8 13.3 %collective-permute-start.46 = (bf16[96,1536]{1,0:T(8,128)(2,1)S(1)}, bf16[96,1536]{1,0:T(8,128)(2,1)S(1)}, u32[]{:S(2)}, u32[]{:S(2)}) collective-permute-start(bf16[96,1536]{1,0:T(8,128)(2,1)S(1)} %get-tuple-element.307), channel_id=1, source_target_pairs={{0,4},{1,5},{2,6},{3,7},{4,0},{5,1},{6,2},{7,3},{8,12},{9,13},{10,... | collective-permute-start | bytes 884744 | tf_op jit(solution)/shard_map/attention_backward/ppermute | solution.py:40
  335.7 12.3 %collective-permute-start.44 = (f32[2,128]{1,0:T(2,128)S(1)}, f32[2,128]{1,0:T(2,128)S(1)}, u32[]{:S(2)}, u32[]{:S(2)}) collective-permute-start(f32[2,128]{1,0:T(2,128)S(1)} %add.524), channel_id=1, source_target_pairs={{0,4},{1,5},{2,6},{3,7},{4,0},{5,1},{6,2},{7,3},{8,12},{9,13},{10,... | collective-permute-start | bytes 3080 | tf_op jit(solution)/shard_map/q_k_v_weight_gradients/ppermute | solution.py:40
  353.3 27.9 %collective-permute-start.47 = (bf16[192,3072]{1,0:T(8,128)(2,1)}, bf16[192,3072]{1,0:T(8,128)(2,1)}, u32[]{:S(2)}, u32[]{:S(2)}) collective-permute-start(bf16[192,3072]{1,0:T(8,128)(2,1)} %get-tuple-element.306), channel_id=1, source_target_pairs={{0,4},{1,5},{2,6},{3,7},{4,0},{5,1},{6,2},{7,3},{8,12},{9,13},{10,... | collective-permute-start | bytes 3538952 | tf_op jit(solution)/shard_map/q_k_v_weight_gradients/ppermute | solution.py:40
  354.1 27.6 %collective-permute-start.48 = (bf16[192,3072]{1,0:T(8,128)(2,1)}, bf16[192,3072]{1,0:T(8,128)(2,1)}, u32[]{:S(2)}, u32[]{:S(2)}) collective-permute-start(bf16[192,3072]{1,0:T(8,128)(2,1)} %get-tuple-element.305), channel_id=1, source_target_pairs={{0,2},{1,3},{2,0},{3,1},{4,6},{5,7},{6,4},{7,5},{8,10},{9,11},{10,... | collective-permute-start | bytes 3538952 | tf_op jit(solution)/shard_map/q_k_v_weight_gradients/ppermute | solution.py:40
  360.9 5.3 %collective-permute-start.51 = (f32[2,1536]{1,0:T(2,128)S(1)}, f32[2,1536]{1,0:T(2,128)S(1)}, u32[]{:S(2)}, u32[]{:S(2)}) collective-permute-start(f32[2,1536]{1,0:T(2,128)S(1)} %add.532), channel_id=1, source_target_pairs={{0,16},{1,17},{2,18},{3,19},{4,20},{5,21},{6,22},{7,23},{8,24},{9,... | collective-permute-start | bytes 36872 | tf_op jit(solution)/shard_map/weight_gradients_to_owners/ppermute | solution.py:40
  383.2 13.7 %collective-permute-start.52 = (bf16[96,3072]{1,0:T(8,128)(2,1)S(1)}, bf16[96,3072]{1,0:T(8,128)(2,1)S(1)}, u32[]{:S(2)}, u32[]{:S(2)}) collective-permute-start(bf16[96,3072]{1,0:T(8,128)(2,1)S(1)} %get-tuple-element.286), channel_id=1, source_target_pairs={{0,2},{1,3},{2,0},{3,1},{4,6},{5,7},{6,4},{7,5},{8,10},{9,11},{10,... | collective-permute-start | bytes 1769480 | tf_op jit(solution)/shard_map/weight_gradients_to_owners/ppermute | solution.py:40
  384.6 13.4 %collective-permute-start.53 = (bf16[96,3072]{1,0:T(8,128)(2,1)S(1)}, bf16[96,3072]{1,0:T(8,128)(2,1)S(1)}, u32[]{:S(2)}, u32[]{:S(2)}) collective-permute-start(bf16[96,3072]{1,0:T(8,128)(2,1)S(1)} %get-tuple-element.285), channel_id=1, source_target_pairs={{0,4},{1,5},{2,6},{3,7},{4,0},{5,1},{6,2},{7,3},{8,12},{9,13},{10,... | collective-permute-start | bytes 1769480 | tf_op jit(solution)/shard_map/weight_gradients_to_owners/ppermute | solution.py:40
  386.2 15.2 %collective-permute-start.54 = (bf16[48,1536]{1,0:T(8,128)(2,1)S(1)}, bf16[48,1536]{1,0:T(8,128)(2,1)S(1)}, u32[]{:S(2)}, u32[]{:S(2)}) collective-permute-start(bf16[48,1536]{1,0:T(8,128)(2,1)S(1)} %get-tuple-element.314), channel_id=1, source_target_pairs={{0,24},{1,25},{2,26},{3,27},{4,28},{5,29},{6,30},{7,31},{8,16},{9,... | collective-permute-start | bytes 442376 | tf_op jit(solution)/shard_map/q_k_v_weight_gradients/ppermute | solution.py:40
  387.8 13.6 %collective-permute-start.55 = (bf16[48,1536]{1,0:T(8,128)(2,1)S(1)}, bf16[48,1536]{1,0:T(8,128)(2,1)S(1)}, u32[]{:S(2)}, u32[]{:S(2)}) collective-permute-start(bf16[48,1536]{1,0:T(8,128)(2,1)S(1)} %get-tuple-element.315), channel_id=1, source_target_pairs={{0,16},{1,17},{2,18},{3,19},{4,20},{5,21},{6,22},{7,23},{8,24},{9,... | collective-permute-start | bytes 442376 | tf_op jit(solution)/shard_map/q_k_v_weight_gradients/ppermute | solution.py:40
  388.3 13.1 %collective-permute-start.56 = (bf16[48,1536]{1,0:T(8,128)(2,1)S(1)}, bf16[48,1536]{1,0:T(8,128)(2,1)S(1)}, u32[]{:S(2)}, u32[]{:S(2)}) collective-permute-start(bf16[48,1536]{1,0:T(8,128)(2,1)S(1)} %get-tuple-element.313), channel_id=1, source_target_pairs={{0,8},{1,9},{2,10},{3,11},{4,12},{5,13},{6,14},{7,15},{8,0},{9,1},... | collective-permute-start | bytes 442376 | tf_op jit(solution)/shard_map/q_k_v_weight_gradients/ppermute | solution.py:40
  398.0 5.6 %collective-permute-start.60 = (f32[2,1536]{1,0:T(2,128)S(1)}, f32[2,1536]{1,0:T(2,128)S(1)}, u32[]{:S(2)}, u32[]{:S(2)}) collective-permute-start(f32[2,1536]{1,0:T(2,128)S(1)} %add.533), channel_id=1, source_target_pairs={{0,2},{1,3},{2,0},{3,1},{4,6},{5,7},{6,4},{7,5},{8,10},{9,11},{10,... | collective-permute-start | bytes 36872 | tf_op jit(solution)/shard_map/weight_gradients_to_owners/ppermute | solution.py:40
  401.5 16.6 %collective-permute-start.57 = (bf16[48,3072]{1,0:T(8,128)(2,1)S(1)}, bf16[48,3072]{1,0:T(8,128)(2,1)S(1)}, u32[]{:S(2)}, u32[]{:S(2)}) collective-permute-start(bf16[48,3072]{1,0:T(8,128)(2,1)S(1)} %get-tuple-element.300), channel_id=1, source_target_pairs={{0,24},{1,25},{2,26},{3,27},{4,28},{5,29},{6,30},{7,31},{8,16},{9,... | collective-permute-start | bytes 884744 | tf_op jit(solution)/shard_map/weight_gradients_to_owners/ppermute | solution.py:40
  403.7 11.4 %collective-permute-start.62 = (bf16[48,2048]{1,0:T(8,128)(2,1)S(1)}, bf16[48,2048]{1,0:T(8,128)(2,1)S(1)}, u32[]{:S(2)}, u32[]{:S(2)}) collective-permute-start(bf16[48,2048]{1,0:T(8,128)(2,1)S(1)} %get-tuple-element.330), channel_id=1, source_target_pairs={{0,2},{1,3},{2,0},{3,1},{4,6},{5,7},{6,4},{7,5},{8,10},{9,11},{10,... | collective-permute-start | bytes 589832 | tf_op jit(solution)/shard_map/weight_gradients_to_owners/ppermute | solution.py:40
  404.9 12.2 %collective-permute-start.63 = (bf16[48,2048]{1,0:T(8,128)(2,1)S(1)}, bf16[48,2048]{1,0:T(8,128)(2,1)S(1)}, u32[]{:S(2)}, u32[]{:S(2)}) collective-permute-start(bf16[48,2048]{1,0:T(8,128)(2,1)S(1)} %get-tuple-element.329), channel_id=1, source_target_pairs={{0,4},{1,5},{2,6},{3,7},{4,0},{5,1},{6,2},{7,3},{8,12},{9,13},{10,... | collective-permute-start | bytes 589832 | tf_op jit(solution)/shard_map/weight_gradients_to_owners/ppermute | solution.py:40
  405.8 11.3 %collective-permute-start.64 = (bf16[48,2048]{1,0:T(8,128)(2,1)S(1)}, bf16[48,2048]{1,0:T(8,128)(2,1)S(1)}, u32[]{:S(2)}, u32[]{:S(2)}) collective-permute-start(bf16[48,2048]{1,0:T(8,128)(2,1)S(1)} %get-tuple-element.328), channel_id=1, source_target_pairs={{0,6},{1,7},{2,4},{3,5},{4,2},{5,3},{6,0},{7,1},{8,14},{9,15},{10,... | collective-permute-start | bytes 589832 | tf_op jit(solution)/shard_map/weight_gradients_to_owners/ppermute | solution.py:40
  407.3 7.8 %collective-permute-start.61 = (f32[2,1536]{1,0:T(2,128)S(1)}, f32[2,1536]{1,0:T(2,128)S(1)}, u32[]{:S(2)}, u32[]{:S(2)}) collective-permute-start(f32[2,1536]{1,0:T(2,128)S(1)} %add.554), channel_id=1, source_target_pairs={{0,4},{1,5},{2,6},{3,7},{4,0},{5,1},{6,2},{7,3},{8,12},{9,13},{10,... | collective-permute-start | bytes 36872 | tf_op jit(solution)/shard_map/weight_gradients_to_owners/ppermute | solution.py:40
  415.1 11.8 %collective-permute-start.58 = (bf16[48,3072]{1,0:T(8,128)(2,1)S(1)}, bf16[48,3072]{1,0:T(8,128)(2,1)S(1)}, u32[]{:S(2)}, u32[]{:S(2)}) collective-permute-start(bf16[48,3072]{1,0:T(8,128)(2,1)S(1)} %get-tuple-element.302), channel_id=1, source_target_pairs={{0,16},{1,17},{2,18},{3,19},{4,20},{5,21},{6,22},{7,23},{8,24},{9,... | collective-permute-start | bytes 884744 | tf_op jit(solution)/shard_map/weight_gradients_to_owners/ppermute | solution.py:40
  415.1 11.8 %collective-permute-start.59 = (bf16[48,3072]{1,0:T(8,128)(2,1)S(1)}, bf16[48,3072]{1,0:T(8,128)(2,1)S(1)}, u32[]{:S(2)}, u32[]{:S(2)}) collective-permute-start(bf16[48,3072]{1,0:T(8,128)(2,1)S(1)} %get-tuple-element.301), channel_id=1, source_target_pairs={{0,8},{1,9},{2,10},{3,11},{4,12},{5,13},{6,14},{7,15},{8,0},{9,1},... | collective-permute-start | bytes 884744 | tf_op jit(solution)/shard_map/weight_gradients_to_owners/ppermute | solution.py:40
  (64 other events, 392.3 us)
Sparse Core Ops, SparseCore 0:
  83.2 88.2 all-gather.1
  280.0 67.9 reduce-scatter.2
  350.3 39.1 reduce-scatter.4
